TPU v7x, 128 devices: a whole 4x4x4 slice. The times are simulated.
128 devices in a mesh: seq: 32 (over z, x, core), head: 4 (over y).
Axes of the slice: x: 4, y: 4, z: 4, core: 2. Of those that a mesh axis runs over, the one named last changes fastest.
Arguments:
- token_ids: int32 [32768], P('seq'), may hold values from 0 to 255
- embedding: bfloat16 [256, 1024], replicated, may hold values from -6 to 6
- fine_norm: float32 [1024], replicated, may hold values from 0.1 to 1.9
- fine_query: bfloat16 [1024, 1024], P(None, 'head'), may hold values from -2 to 2
- fine_key: bfloat16 [1024, 1024], P(None, 'head'), may hold values from -2 to 2
- fine_value: bfloat16 [1024, 1024], P(None, 'head'), may hold values from -0.1875 to 0.1875
- fine_output: bfloat16 [1024, 1024], P('head'), may hold values from -0.1875 to 0.1875
- shorten_weight: bfloat16 [4, 1024, 1024], P(None, 'head'), may hold values from -0.09375 to 0.09375
- coarse_norm: float32 [1024], replicated, may hold values from 0.1 to 1.9
- coarse_query: bfloat16 [1024, 1024], P(None, 'head'), may hold values from -2 to 2
- coarse_key: bfloat16 [1024, 1024], P(None, 'head'), may hold values from -2 to 2
- coarse_value: bfloat16 [1024, 1024], P(None, 'head'), may hold values from -0.1875 to 0.1875
- coarse_output: bfloat16 [1024, 1024], P('head'), may hold values from -0.1875 to 0.1875
- ffn_norm: float32 [1024], replicated, may hold values from 0.1 to 1.9
- ffn_up: bfloat16 [1024, 4096], P(None, 'head'), may hold values from -0.1875 to 0.1875
- ffn_down: bfloat16 [4096, 1024], P('head'), may hold values from -0.09375 to 0.09375
- upsample_weight: bfloat16 [1024, 4, 1024], P(None, None, 'head'), may hold values from -0.1875 to 0.1875
Outputs:
- block_output: bfloat16 [32768, 1024], P('seq', 'head')
All inputs are finite; a program needn't handle non-finite values.
Results may differ from a plain program's by a relative error of at most 0.0102.
Values may be sent and summed in bfloat16 or wider, within the bound.
No kernel may reach another device: no remote copies, remote signals or barrier semaphores. Data moves between devices by JAX's collectives and lax.ppermute only.
A program may use at most 128 MiB of HBM per device.

v0:
```python
import functools
import math

import jax
import jax.numpy as jnp
import numpy as np
from jax import lax
from jax.experimental import pallas as pl
from jax.experimental.pallas import tpu as pltpu
from jax.sharding import Mesh
from jax.sharding import PartitionSpec as P

D = 1024
HEAD_DIM = 64
SHORTEN = 4
WINDOW = 1024
BLOCK = 256
HALO = 16
ROWS = 1024
PAST = WINDOW + BLOCK
KEYS = PAST + ROWS
SHARE = 256
COARSE_ROWS = 256
SEQ = ("z", "x", "core")

epsilon = 1e-06
masked_low = -1e30
q_scale = HEAD_DIM ** (-0.5) * math.log2(math.e)
bf16 = jnp.bfloat16
f32 = jnp.float32


def angle_tables():
    lane = np.arange(128) % 32
    period = 2.0 ** (4 + lane * 14 // 32)
    coarse = (256.0 * np.arange(32)[:, None]) % period[None]
    near = np.arange(256)[:, None] % period[None]
    a = coarse * (2.0 * np.pi / period)[None]
    b = near * (2.0 * np.pi / period)[None]
    return [t.astype(np.float32) for t in (np.cos(a), np.sin(a), np.cos(b), np.sin(b))]


def shift(value, axis, steps, count):
    return lax.ppermute(value, axis, [(i, (i + steps) % count) for i in range(count)])


def later(value, axis, steps, count):
    return lax.ppermute(value, axis, [(i, i + steps) for i in range(count - steps)])


def exchange(block_for, axis, count):
    me = lax.axis_index(axis)
    got = [block_for(me)]
    for s in range(1, count):
        got.append(shift(block_for((me + s) % count), axis, s, count))
    return got


def dot(left, right):
    return jnp.dot(left, right, preferred_element_type=f32)


def dot_t(left, right):
    return lax.dot_general(left, right, (((1,), (1,)), ((), ())), preferred_element_type=f32)


def norm_rows(data, gain):
    power = jnp.mean(data * data, axis=-1, keepdims=True)
    return (data * lax.rsqrt(power + epsilon) * gain).astype(bf16)


def partner(values):
    width = values.shape[1]
    lane = lax.broadcasted_iota(jnp.int32, values.shape, 1)
    ahead = pltpu.roll(values, width - 32, 1)
    behind = pltpu.roll(values, 32, 1)
    return jnp.where(lane % 64 < 32, -ahead, behind)


def halves(table):
    high = table.astype(bf16)
    low = (table - high.astype(f32)).astype(bf16)
    return high, low


def fine_kernel(
    place_ref, ids_ref, emb_ref, gain_ref, wq_ref, wk_ref, wv_ref,
    ca_ref, sa_ref, cb_ref, sb_ref,
    out_ref, q_ref, k_ref, v_ref, tab_ref,
):
    step = pl.program_id(0)
    lowest = jnp.maximum(PAST - place_ref[0] * ROWS, 0)
    head_lane = lax.broadcasted_iota(jnp.int32, (1, SHARE), 1) // HEAD_DIM

    @pl.when(step == 0)
    def _():
        fine_in = norm_rows(emb_ref[...].astype(f32), gain_ref[...])
        tq = dot(fine_in, wq_ref[...]) * q_scale
        tk = dot(fine_in, wk_ref[...])
        for n, table in enumerate((tq, partner(tq), tk, partner(tk))):
            high, low = halves(table)
            tab_ref[2 * n] = high
            tab_ref[2 * n + 1] = low
        tab_ref[8] = dot(fine_in, wv_ref[...]).astype(bf16)
        cb = cb_ref[...]
        sb = sb_ref[...]

        def build(block, _):
            begin = pl.multiple_of(block * BLOCK, BLOCK)
            ids = ids_ref[pl.ds(begin, BLOCK), :]
            levels = lax.broadcasted_iota(jnp.int32, (BLOCK, 256), 1)
            hot = (ids == levels).astype(f32).astype(bf16)
            ca = ca_ref[pl.ds(block, 1), :]
            sa = sa_ref[pl.ds(block, 1), :]
            cosine = ca * cb - sa * sb
            sine = sa * cb + ca * sb
            cosine = jnp.concatenate([cosine, cosine], axis=1)
            sine = jnp.concatenate([sine, sine], axis=1)

            def turned(n):
                plain = dot(hot, tab_ref[n]) + dot(hot, tab_ref[n + 1])
                other = dot(hot, tab_ref[n + 2]) + dot(hot, tab_ref[n + 3])
                return (plain * cosine + other * sine).astype(bf16)

            k_ref[pl.ds(begin, BLOCK), :] = turned(4)
            v_ref[pl.ds(begin, BLOCK), :] = dot(hot, tab_ref[8]).astype(bf16)

            @pl.when(block >= PAST // BLOCK - 1)
            def _():
                at = pl.multiple_of(begin - (PAST - BLOCK), BLOCK)
                q_ref[pl.ds(at, BLOCK), :] = turned(0)

            return 0

        lax.fori_loop(0, KEYS // BLOCK, build, 0)

        halo_q = q_ref[BLOCK - HALO : BLOCK, :]
        stacked = jnp.concatenate(
            [jnp.where(head_lane == h, halo_q, jnp.zeros_like(halo_q)) for h in range(4)], axis=0
        )
        scores = dot_t(stacked, k_ref[0:PAST, :])
        row = lax.broadcasted_iota(jnp.int32, scores.shape, 0) % HALO + (PAST - HALO)
        col = lax.broadcasted_iota(jnp.int32, scores.shape, 1)
        allowed = (col <= row) & (col > row - WINDOW) & (col >= lowest)
        scores = jnp.where(allowed, scores, masked_low)
        top = jnp.max(scores, axis=1, keepdims=True)
        weights = jnp.exp2(scores - top)
        total = jnp.sum(weights, axis=1, keepdims=True)
        mixed = dot(weights.astype(bf16), v_ref[0:PAST, :]) / total
        result = jnp.zeros((HALO, SHARE), f32)
        for h in range(4):
            result = jnp.where(head_lane == h, mixed[h * HALO : (h + 1) * HALO], result)
        out_ref[0:HALO, :] = result.astype(bf16)

    begin = pl.multiple_of((step + 1) * BLOCK, BLOCK)
    keys = k_ref[pl.ds(begin, PAST), :]
    values = v_ref[pl.ds(begin, PAST), :]
    query = q_ref[pl.ds(begin, BLOCK), :]
    row = lax.broadcasted_iota(jnp.int32, (BLOCK, BLOCK), 0)
    col = lax.broadcasted_iota(jnp.int32, (BLOCK, BLOCK), 1)
    biases = [
        jnp.where(begin + t * BLOCK >= lowest, 0.0, masked_low).astype(f32) for t in range(4)
    ]
    first_bias = jnp.where(col > row, 0.0, masked_low) + biases[0]
    last_bias = jnp.where(col <= row, 0.0, masked_low)
    result = jnp.zeros((BLOCK, SHARE), f32)
    for h in range(4):
        scores = dot_t(jnp.where(head_lane == h, query, jnp.zeros_like(query)), keys)
        tiles = [scores[:, t * BLOCK : (t + 1) * BLOCK] for t in range(5)]
        tiles = (
            [tiles[0] + first_bias]
            + [tiles[t] + biases[t] for t in range(1, 4)]
            + [tiles[4] + last_bias]
        )
        peak = tiles[0]
        for t in range(1, 5):
            peak = jnp.maximum(peak, tiles[t])
        top = jnp.max(peak, axis=1, keepdims=True)
        weights = [jnp.exp2(tile - top) for tile in tiles]
        summed = weights[0]
        for t in range(1, 5):
            summed = summed + weights[t]
        total = jnp.sum(summed, axis=1, keepdims=True)
        mixed = dot(jnp.concatenate([w.astype(bf16) for w in weights], axis=1), values)
        result = jnp.where(head_lane == h, mixed / total, result)
    at = pl.multiple_of(HALO + step * BLOCK, HALO)
    out_ref[pl.ds(at, BLOCK), :] = result.astype(bf16)


def vmem():
    return pl.BlockSpec(memory_space=pltpu.VMEM)


def smem():
    return pl.BlockSpec(memory_space=pltpu.SMEM)


def fine_attention(place, ids, embedding, gain, wq, wk, wv, tables):
    return pl.pallas_call(
        fine_kernel,
        grid=(4,),
        out_shape=jax.ShapeDtypeStruct((HALO + ROWS, SHARE), bf16),
        in_specs=[smem()] + [vmem()] * 10,
        out_specs=vmem(),
        scratch_shapes=[
            pltpu.VMEM((BLOCK + ROWS, SHARE), bf16),
            pltpu.VMEM((KEYS, SHARE), bf16),
            pltpu.VMEM((KEYS, SHARE), bf16),
            pltpu.VMEM((9, 256, SHARE), bf16),
        ],
        compiler_params=pltpu.CompilerParams(vmem_limit_bytes=48 << 20),
        name="fine_attention",
    )(place, ids, embedding, gain, wq, wk, wv, *tables)


def coarse_pack_kernel(place_ref, x_ref, wq_ref, wk_ref, wv_ref, ca_ref, sa_ref, cb_ref, sb_ref, out_ref):
    x = x_ref[...]
    place = place_ref[0]
    ca = ca_ref[pl.ds(place, 1), :]
    sa = sa_ref[pl.ds(place, 1), :]
    cb = cb_ref[...]
    sb = sb_ref[...]
    cosine = ca * cb - sa * sb
    sine = sa * cb + ca * sb
    cosine = jnp.concatenate([cosine, cosine], axis=1)
    sine = jnp.concatenate([sine, sine], axis=1)

    def turned(values):
        return values * cosine + partner(values) * sine

    q = turned(dot(x, wq_ref[...])) * q_scale
    k = turned(dot(x, wk_ref[...]))
    v = dot(x, wv_ref[...])
    low_lanes = lax.broadcasted_iota(jnp.int32, (1, 128), 1) < 64
    half = COARSE_ROWS // 2
    for h in range(4):
        pair = (h // 2) * 128
        kp = k[:, pair : pair + 128]
        vp = v[:, pair : pair + 128]
        qp = q[:, pair : pair + 128]
        if h % 2 == 0:
            kv = jnp.where(low_lanes, kp, pltpu.roll(vp, 64, 1))
            qq = jnp.where(low_lanes, qp[:half], pltpu.roll(qp[half:], 64, 1))
        else:
            kv = jnp.where(low_lanes, pltpu.roll(kp, 64, 1), vp)
            qq = jnp.where(low_lanes, pltpu.roll(qp[:half], 64, 1), qp[half:])
        out_ref[h, 0:COARSE_ROWS, :] = kv.astype(bf16)
        out_ref[h, COARSE_ROWS : COARSE_ROWS + half, :] = qq.astype(bf16)


def coarse_pack(place, x, wq, wk, wv, tables):
    return pl.pallas_call(
        coarse_pack_kernel,
        out_shape=jax.ShapeDtypeStruct((4, COARSE_ROWS * 3 // 2, 128), bf16),
        in_specs=[smem()] + [vmem()] * 8,
        out_specs=vmem(),
        compiler_params=pltpu.CompilerParams(vmem_limit_bytes=32 << 20),
        name="coarse_pack",
    )(place, x, wq, wk, wv, *tables)


def coarse_kernel(chunk_ref, q_ref, near_ref, far_ref, out_ref, q_all, top_ref, total_ref, acc_ref):
    half = COARSE_ROWS // 2
    low_lanes = lax.broadcasted_iota(jnp.int32, (1, 128), 1) < 64
    for z in range(4):
        packed = q_ref[z].astype(f32)
        zero = jnp.zeros_like(packed)
        q_all[z * 256 : z * 256 + half, :] = jnp.where(low_lanes, packed, zero).astype(bf16)
        q_all[z * 256 + half : (z + 1) * 256, :] = jnp.where(
            low_lanes, pltpu.roll(packed, 64, 1), zero
        ).astype(bf16)
    row = lax.broadcasted_iota(jnp.int32, (256, 256), 0)
    col = lax.broadcasted_iota(jnp.int32, (256, 256), 1)
    for z in range(4):
        kv = near_ref[0, z]
        at = pl.ds(z * 256, 256)
        scores = jnp.where(col <= row, dot_t(q_all[at, :], kv), masked_low)
        top = jnp.max(scores, axis=1, keepdims=True)
        weights = jnp.exp2(scores - top)
        top_ref[at, :] = jnp.broadcast_to(top, (256, 128))
        total_ref[at, :] = jnp.broadcast_to(jnp.sum(weights, axis=1, keepdims=True), (256, 128))
        acc_ref[at, :] = dot(weights.astype(bf16), kv)

    def absorb(begin, rows, parts):
        at = pl.ds(begin, rows)
        query = q_all[at, :]
        scores = [dot_t(query, kv) for kv in parts]
        peak = scores[0]
        for s in scores[1:]:
            peak = jnp.maximum(peak, s)
        old = top_ref[at, :]
        top = jnp.maximum(old, jnp.max(peak, axis=1, keepdims=True))
        factor = jnp.exp2(old - top)
        both = jnp.concatenate([top, top], axis=1)
        weights = [jnp.exp2(s - both) for s in scores]
        summed = weights[0]
        for w in weights[1:]:
            summed = summed + w
        contrib = dot(weights[0].astype(bf16), parts[0])
        for w, kv in zip(weights[1:], parts[1:]):
            contrib = contrib + dot(w.astype(bf16), kv)
        top_ref[at, :] = top
        total_ref[at, :] = total_ref[at, :] * factor + jnp.sum(summed, axis=1, keepdims=True)
        acc_ref[at, :] = acc_ref[at, :] * factor + contrib

    for s in range(4):
        for z in range(3):
            absorb((z + 1) * 256, (3 - z) * 256, [near_ref[s, z], far_ref[s, z]])

    for s in range(4):
        for n, ref in enumerate((near_ref, far_ref)):
            if s == 0 and n == 0:
                continue

            @pl.when(chunk_ref[2 * s + n] < chunk_ref[0])
            def _(ref=ref, s=s):
                for z in range(4):
                    absorb(z * 256, 256, [ref[s, z]])

    mixed = acc_ref[...] / total_ref[...]
    out_ref[...] = pltpu.roll(mixed, 64, 1)[:, :64].astype(bf16)


def coarse_attention(chunks, q, near, far):
    return pl.pallas_call(
        coarse_kernel,
        out_shape=jax.ShapeDtypeStruct((1024, 64), bf16),
        in_specs=[smem()] + [vmem()] * 3,
        out_specs=vmem(),
        scratch_shapes=[
            pltpu.VMEM((1024, 128), bf16),
            pltpu.VMEM((1024, 128), f32),
            pltpu.VMEM((1024, 128), f32),
            pltpu.VMEM((1024, 128), f32),
        ],
        compiler_params=pltpu.CompilerParams(vmem_limit_bytes=48 << 20),
        name="coarse_attention",
    )(chunks, q, near, far)


def to_shares(values):
    rows = values.shape[0] // 4
    return lax.all_to_all(values.reshape(4, rows, -1), "head", 0, 0)


def everyone(values):
    wide = jnp.broadcast_to(values[None], (4, *values.shape))
    return lax.all_to_all(wide, "head", 0, 0).reshape(-1, values.shape[-1])


def local(
    token_ids, embedding, fine_norm, fine_query, fine_key, fine_value, fine_output,
    shorten_weight, coarse_norm, coarse_query, coarse_key, coarse_value, coarse_output,
    ffn_norm, ffn_up, ffn_down, upsample_weight,
):
    place = lax.axis_index(SEQ).astype(jnp.int32)
    head_place = lax.axis_index("head")
    x_place = lax.axis_index("x").astype(jnp.int32)
    core_place = lax.axis_index("core").astype(jnp.int32)
    tables = [jnp.asarray(t) for t in angle_tables()]
    place_1 = place[None]

    prior = later(token_ids, SEQ, 1, 32)
    before = later(token_ids[ROWS - BLOCK :], SEQ, 2, 32)
    all_ids = jnp.concatenate([before, prior, token_ids])
    outputs = [fine_output] + [shift(fine_output, "head", s, 4) for s in range(1, 4)]

    mixed = fine_attention(
        place_1, all_ids[:, None], embedding, fine_norm[None], fine_query, fine_key, fine_value, tables
    )

    got = exchange(
        lambda d: lax.dynamic_slice_in_dim(mixed, d * 256, 256 + HALO, 0), "head", 4
    )
    own_ids = lax.dynamic_slice_in_dim(
        all_ids, PAST - HALO + head_place * 256, 256 + HALO, 0
    )
    hot = (own_ids[:, None] == jnp.arange(256, dtype=jnp.int32)[None]).astype(bf16)
    start = dot(hot, embedding)
    merged = start
    for part, weight in zip(got, outputs):
        merged = merged + dot(part, weight)
    token = place * ROWS + head_place * 256 - HALO + jnp.arange(256 + HALO, dtype=jnp.int32)
    fine_rows = jnp.where(token[:, None] >= 0, merged, 0.0).astype(bf16)

    by_feature = lax.all_to_all(
        fine_rows.reshape(256 + HALO, 4, SHARE), "head", 1, 0, tiled=False
    )
    flat = by_feature.reshape(4 * (256 + HALO), SHARE)
    m_index = jnp.arange(COARSE_ROWS, dtype=jnp.int32)
    column = jnp.arange(4 * (256 + HALO), dtype=jnp.int32)
    pieces = []
    for r in range(SHORTEN):
        t = 4 * m_index + r - 3
        quarter = jnp.maximum(t, 0) // 256
        source = quarter * (256 + HALO) + HALO + (t - quarter * 256)
        choose = (source[:, None] == column[None]).astype(bf16)
        pieces.append(dot(choose, flat).astype(bf16))
    grouped = jnp.concatenate(pieces, axis=1)
    short_terms = dot(grouped, shorten_weight.reshape(SHORTEN * SHARE, D)).astype(bf16)
    short = jnp.sum(to_shares(short_terms).astype(f32), axis=0).astype(bf16)
    short_f = short.astype(f32)

    coarse_in = everyone(norm_rows(short_f, coarse_norm))
    packed = coarse_pack(place_1, coarse_in, coarse_query, coarse_key, coarse_value, tables)
    turned = lax.all_to_all(packed, "z", 0, 0)
    q = turned[:, COARSE_ROWS:]
    kv = turned[:, :COARSE_ROWS]
    near = jnp.stack([kv] + [shift(kv, "x", s, 4) for s in range(1, 4)])
    far = shift(near, "core", 1, 2)
    steps = jnp.arange(4, dtype=jnp.int32)
    columns_x = (x_place - steps + 4) % 4
    chunks = jnp.stack([2 * columns_x + core_place, 2 * columns_x + 1 - core_place], axis=1).reshape(8)
    attended = coarse_attention(chunks, q, near, far)

    heads_in = lax.all_to_all(attended.reshape(16, 64, 64), ("z", "head"), 0, 0)
    coarse_mixed = (
        heads_in.reshape(4, 4, 64, 64).transpose(2, 1, 0, 3).reshape(64, D)
    )
    coarse_full = lax.all_gather(coarse_output, "head", axis=0, tiled=True)
    first = short_f + dot(coarse_mixed, coarse_full)
    ffn_in = everyone(norm_rows(first, ffn_norm))
    inner = jax.nn.gelu(dot(ffn_in, ffn_up)).astype(bf16)
    partial = dot(inner, ffn_down).astype(bf16)
    second = (first + jnp.sum(to_shares(partial).astype(f32), axis=0)).astype(bf16)
    second_all = everyone(second)
    lifted = dot(second_all, upsample_weight.reshape(D, SHORTEN * SHARE)).reshape(ROWS, SHARE)
    fine = by_feature[:, HALO:].reshape(ROWS, SHARE)
    return (fine.astype(f32) + lifted).astype(bf16)


def solution(mesh):
    split = Mesh(mesh.devices.reshape(4, 4, 2, 4), ("z", "x", "core", "head"))
    return jax.shard_map(
        local,
        mesh=split,
        in_specs=(
            P(SEQ), P(), P(), P(None, "head"), P(None, "head"), P(None, "head"), P("head", None),
            P(None, "head", None), P(), P(None, "head"), P(None, "head"), P(None, "head"),
            P("head", None), P(), P(None, "head"), P("head", None), P(None, None, "head"),
        ),
        out_specs=P(SEQ, "head"),
        check_vma=False,
    )
```

profile of v0, /device:TPU:6, one launch (start us, length us, event | category | flops | bytes accessed | tf_op | source)
XLA Modules:
  0.0 209.2 jit_solution(12381402346354100599)
XLA Ops:
  6.6 3.1 %collective-permute-start.7 = (bf16[256,1024]{1,0:T(8,128)(2,1)}, bf16[256,1024]{1,0:T(8,128)(2,1)}, u32[]{:S(2)}, u32[]{:S(2)}) collective-permute-start(bf16[256,1024]{1,0:T(8,128)(2,1)} %param.27), channel_id=1, source_target_pairs={{0,3},{1,0},{2,1},{3,2},{4,7},{5,4},{6,5},{7,6},{8,11},{9,8},{10,9... | collective-permute-start | bytes 1572872 | tf_op jit(solution)/shard_map/ppermute | solution.py:44
  9.7 0.6 collective-permute-start.5
  10.3 1.0 collective-permute-start.3
  11.3 1.9 collective-permute-start.1
  13.2 0.7 slice.12
  13.9 3.7 %collective-permute-start = (s32[256]{0:T(256)S(1)}, s32[256]{0:T(256)S(1)}, u32[]{:S(2)}, u32[]{:S(2)}) collective-permute-start(s32[256]{0:T(256)S(1)} %slice.12), channel_id=1, source_target_pairs={{0,8},{4,12},{8,16},{12,20},{16,24},{20,28},{24,32},{28,36},{32,40... | collective-permute-start | bytes 3080 | tf_op jit(solution)/shard_map/ppermute | solution.py:48
  17.7 1.6 collective-permute-done
  19.3 0.7 constant_dynamic-update-slice_fusion
  20.0 0.4 broadcast_in_dim.32.ids_ref
  20.5 1.0 copy-done.3
  21.5 1.0 copy-done.4
  22.6 16.0 %fine_attention.1 = bf16[1040,256]{1,0:T(8,128)(2,1)S(1)} custom-call(s32[1]{0:T(128)} %bitcast.place_ref, s32[2304,1]{1,0:T(8,128)S(1)} %broadcast_in_dim.32.ids_ref, bf16[256,1024]{1,0:T(8,128)(2,1)S(1)} %copy-done.1, f32[1,1024]{1,0:T(1,128)S(1)} %bitcast.52, bf16[1024,256]{1,0:T(8,128)(2,1)S(1)} %copy-done.2, bf16[1024,256]{1,0:T(8,128)(2,1)S(1)} %copy-done.3, ...), custom_call_target="tpu_custom_call" | custom-call | tf_op jit(solution)/shard_map/fine_attention/pallas_call | solution.py:199
  38.6 2.3 %collective-permute-start.6 = (bf16[272,256]{1,0:T(8,128)(2,1)S(1)}, bf16[272,256]{1,0:T(8,128)(2,1)S(1)}, u32[]{:S(2)}, u32[]{:S(2)}) collective-permute-start(bf16[272,256]{1,0:T(8,128)(2,1)S(1)} %get-tuple-element.6), channel_id=1, source_target_pairs={{0,3},{1,0},{2,1},{3,2},{4,7},{5,4},{6,5},{7,6},{8,11},{9,8},{10,9... | collective-permute-start | bytes 417800 | tf_op jit(solution)/shard_map/ppermute | solution.py:44
  40.9 1.7 collective-permute-start.4
  42.7 0.4 fusion.37
  43.1 0.3 convolution_add_fusion.1
  43.4 4.2 %collective-permute-done.6 = bf16[272,256]{1,0:T(8,128)(2,1)S(1)} collective-permute-done((bf16[272,256]{1,0:T(8,128)(2,1)S(1)}, bf16[272,256]{1,0:T(8,128)(2,1)S(1)}, u32[]{:S(2)}, u32[]{:S(2)}) %collective-permute-start.6) | collective-permute-done | bytes 139296 | tf_op jit(solution)/shard_map/ppermute | solution.py:44
  47.6 2.2 %collective-permute-start.2 = (bf16[272,256]{1,0:T(8,128)(2,1)S(1)}, bf16[272,256]{1,0:T(8,128)(2,1)S(1)}, u32[]{:S(2)}, u32[]{:S(2)}) collective-permute-start(bf16[272,256]{1,0:T(8,128)(2,1)S(1)} %get-tuple-element.5), channel_id=1, source_target_pairs={{0,1},{1,2},{2,3},{3,0},{4,5},{5,6},{6,7},{7,4},{8,9},{9,10},{10,1... | collective-permute-start | bytes 417800 | tf_op jit(solution)/shard_map/ppermute | solution.py:44
  49.9 1.4 fusion.54
  51.2 1.4 fusion.53
  52.6 2.8 %collective-permute-done.2 = bf16[272,256]{1,0:T(8,128)(2,1)S(1)} collective-permute-done((bf16[272,256]{1,0:T(8,128)(2,1)S(1)}, bf16[272,256]{1,0:T(8,128)(2,1)S(1)}, u32[]{:S(2)}, u32[]{:S(2)}) %collective-permute-start.2) | collective-permute-done | bytes 139296 | tf_op jit(solution)/shard_map/ppermute | solution.py:44
  55.4 1.4 fusion.3
  56.8 0.4 broadcast_in_dim_reshape.3
  57.2 0.9 copy.29
  58.1 3.5 %all-to-all-start = ((bf16[1,272,4,256]{3,1,0,2:T(8,128)(2,1)}), bf16[1,272,4,256]{3,1,0,2:T(8,128)(2,1)S(1)}, u32[]{:S(2)}, u32[]{:S(2)}) async-start(bf16[1,272,4,256]{3,1,0,2:T(8,128)(2,1)} %copy.29), calls=%async_computation | async-start | bytes 1114112 | tf_op jit(solution)/shard_map/all_to_all | solution.py:386
  61.6 9.8 %all-to-all-done = bf16[1,272,4,256]{3,1,0,2:T(8,128)(2,1)S(1)} async-done(((bf16[1,272,4,256]{3,1,0,2:T(8,128)(2,1)}), bf16[1,272,4,256]{3,1,0,2:T(8,128)(2,1)S(1)}, u32[]{:S(2)}, u32[]{:S(2)}) %all-to-all-start) | async-done | bytes 557088 | tf_op jit(solution)/shard_map/all_to_all | solution.py:386
  71.4 0.5 fusion.8
  71.9 0.5 fusion.9
  72.5 0.5 fusion.10
  73.0 0.5 fusion.11
  73.5 1.5 convolution_convert_fusion.1
  75.1 3.6 %all-to-all-start.1 = ((bf16[4,64,1024]{2,1,0:T(8,128)(2,1)}), bf16[4,64,1024]{2,1,0:T(8,128)(2,1)S(1)}, u32[]{:S(2)}, u32[]{:S(2)}) async-start(bf16[4,64,1024]{2,1,0:T(8,128)(2,1)} %bitcast.10), calls=%async_computation.1 | async-start | bytes 1048576 | tf_op jit(solution)/shard_map/all_to_all | solution.py:343
  78.7 0.7 all-gather.2.cloned.1.call-update
  79.4 7.8 %all-to-all-done.1 = bf16[4,64,1024]{2,1,0:T(8,128)(2,1)S(1)} async-done(((bf16[4,64,1024]{2,1,0:T(8,128)(2,1)}), bf16[4,64,1024]{2,1,0:T(8,128)(2,1)S(1)}, u32[]{:S(2)}, u32[]{:S(2)}) %all-to-all-start.1) | async-done | bytes 524320 | tf_op jit(solution)/shard_map/all_to_all | solution.py:343
  87.4 0.1 fusion.38
  87.7 12.6 %all_to_all.50 = bf16[4,64,1024]{2,1,0:T(8,128)(2,1)S(1)} all-to-all(bf16[4,64,1024]{2,1,0:T(8,128)(2,1)S(1)} %broadcast_in_dim.29), channel_id=1, replica_groups=mesh['z'=4,'x'=4,'core'=2,'head'=4] {'head'}, dimensions={0} | all-to-all | bytes 1048576 | tf_op jit(solution)/shard_map/all_to_all | solution.py:348
  100.3 0.8 coarse_pack.1
  101.1 12.6 %all_to_all.51 = bf16[4,384,128]{2,1,0:T(8,128)(2,1)S(1)} all-to-all(bf16[4,384,128]{2,1,0:T(8,128)(2,1)S(1)} %coarse_pack.1), channel_id=1, replica_groups=mesh['z'=4,'x'=4,'core'=2,'head'=4] {'z'}, dimensions={0} | all-to-all | bytes 786432 | tf_op jit(solution)/shard_map/all_to_all | solution.py:406
  113.9 1.7 collective-permute-start.9
  115.7 2.5 %collective-permute-start.8 = (bf16[4,256,128]{2,1,0:T(8,128)(2,1)S(1)}, bf16[4,256,128]{2,1,0:T(8,128)(2,1)S(1)}, u32[]{:S(2)}, u32[]{:S(2)}) collective-permute-start(bf16[4,256,128]{2,1,0:T(8,128)(2,1)S(1)} %get-tuple-element.9), channel_id=1, source_target_pairs={{0,8},{8,16},{16,24},{24,0},{1,9},{9,17},{17,25},{25,1},{2,10},{10... | collective-permute-start | bytes 786440 | tf_op jit(solution)/shard_map/ppermute | solution.py:44
  118.2 6.1 %collective-permute-done.10 = bf16[4,256,128]{2,1,0:T(8,128)(2,1)S(1)} collective-permute-done((bf16[4,256,128]{2,1,0:T(8,128)(2,1)S(1)}, bf16[4,256,128]{2,1,0:T(8,128)(2,1)S(1)}, u32[]{:S(2)}, u32[]{:S(2)}) %collective-permute-start.10) | collective-permute-done | bytes 262176 | tf_op jit(solution)/shard_map/ppermute | solution.py:44
  124.3 0.9 collective-permute-done.8
  125.2 0.1 pad_maximum_fusion.near_ref
  125.6 0.9 slice.17.q_ref
  126.5 1.7 collective-permute-done.11.far_ref
  128.2 12.5 %coarse_attention.1 = bf16[1024,64]{1,0:T(8,128)(2,1)S(1)} custom-call(s32[8]{0:T(128)S(1)} %reshape.228.chunk_ref, bf16[4,128,128]{2,1,0:T(8,128)(2,1)S(1)} %slice.17.q_ref, bf16[4,4,256,128]{3,2,1,0:T(8,128)(2,1)S(1)} %pad_maximum_fusion.near_ref, bf16[4,4,256,128]{3,2,1,0:T(8,128)(2,1)} %collective-permute-done.11.far_ref), custom_call_target="tpu_custom_call" | custom-call | tf_op jit(solution)/shard_map/coarse_attention/pallas_call | solution.py:325
  140.8 0.2 reshape.239
  141.0 11.3 %all_to_all.52 = bf16[16,2,2048]{2,1,0:T(2,128)(2,1)S(1)} all-to-all(bf16[16,2,2048]{2,1,0:T(2,128)(2,1)S(1)} %reshape.239), channel_id=1, replica_groups=mesh['z'=4,'x'=4,'core'=2,'head'=4] {'z','head'}, dimensions={0} | all-to-all | bytes 262144 | tf_op jit(solution)/shard_map/all_to_all | solution.py:416
  152.3 0.2 reshape.240
  152.5 0.2 copy.30
  152.7 0.2 reshape.232
  153.0 2.2 %multiply_reduce_fusion = (f32[64]{0:T(128)S(1)}, f32[64,1024]{1,0:T(8,128)S(1)}) fusion(bf16[64,1024]{1,0:T(8,128)(2,1)S(1)} %reshape.232, bf16[1024,1024]{1,0:T(8,128)(2,1)} %all-gather.2.cloned.1.call-done, bf16[64,1024]{1,0:T(8,128)(2,1)S(1)} %copy-done.17), kind=kOutput, calls=%fused_computation.58 | convolution fusion | flops 134479808 | bytes 2621696 | tf_op jit(solution)/shard_map/dot_general | solution.py:60
  155.3 12.4 %all_to_all.53 = bf16[4,64,1024]{2,1,0:T(8,128)(2,1)S(1)} all-to-all(bf16[4,64,1024]{2,1,0:T(8,128)(2,1)S(1)} %broadcast_in_dim.30), channel_id=1, replica_groups=mesh['z'=4,'x'=4,'core'=2,'head'=4] {'head'}, dimensions={0} | all-to-all | bytes 1048576 | tf_op jit(solution)/shard_map/all_to_all | solution.py:348
  167.8 3.7 %convolution_convert_fusion = bf16[256,1024]{1,0:T(8,128)(2,1)S(1)} fusion(bf16[1024,1024]{1,0:T(8,128)(2,1)} %param.36, bf16[256,1024]{1,0:T(8,128)(2,1)S(1)} %bitcast.62, bf16[1024,1024]{1,0:T(8,128)(2,1)} %param.35), kind=kOutput, calls=%fused_computation.7 | convolution fusion | flops 1076363264 | bytes 5242880 | tf_op jit(solution)/shard_map/dot_general | solution.py:60
  171.5 11.6 %all_to_all.54 = bf16[4,64,1024]{2,1,0:T(8,128)(2,1)S(1)} all-to-all(bf16[4,64,1024]{2,1,0:T(8,128)(2,1)S(1)} %bitcast.63), channel_id=1, replica_groups=mesh['z'=4,'x'=4,'core'=2,'head'=4] {'head'}, dimensions={0} | all-to-all | bytes 1048576 | tf_op jit(solution)/shard_map/all_to_all | solution.py:343
  183.2 0.9 broadcast_in_dim.31
  184.0 3.5 %all-to-all-start.7 = ((bf16[4,64,1024]{2,1,0:T(8,128)(2,1)}), bf16[4,64,1024]{2,1,0:T(8,128)(2,1)S(1)}, u32[]{:S(2)}, u32[]{:S(2)}) async-start(bf16[4,64,1024]{2,1,0:T(8,128)(2,1)} %broadcast_in_dim.31), calls=%async_computation.7 | async-start | bytes 1048576 | tf_op jit(solution)/shard_map/all_to_all | solution.py:348
  187.5 3.5 %copy.31 = bf16[128,8,4,256]{3,1,2,0:T(8,128)(2,1)} copy(bf16[128,8,4,256]{3,2,1,0:T(4,128)(2,1)} %bitcast.60) | data formatting | bytes 4194304
  191.0 0.8 slice.16
  191.9 3.7 %all-to-all-done.7 = bf16[4,64,1024]{2,1,0:T(8,128)(2,1)S(1)} async-done(((bf16[4,64,1024]{2,1,0:T(8,128)(2,1)}), bf16[4,64,1024]{2,1,0:T(8,128)(2,1)S(1)}, u32[]{:S(2)}, u32[]{:S(2)}) %all-to-all-start.7) | async-done | bytes 524320 | tf_op jit(solution)/shard_map/all_to_all | solution.py:348
  195.6 0.8 copy-done.15
  196.4 2.5 %fusion.55 = f32[256,1024]{1,0:T(8,128)S(1)} fusion(bf16[256,1024]{1,0:T(8,128)(2,1)} %bitcast.59, bf16[1024,1024]{1,0:T(8,128)(2,1)} %bitcast.53), kind=kOutput, calls=%fused_computation.101 | convolution fusion | flops 536870912 | bytes 3670016 | tf_op jit(solution)/shard_map/dot_general | solution.py:60
  198.8 1.3 reshape.237
  200.1 2.3 %fusion.20 = bf16[1024,256]{1,0:T(8,128)(2,1)} fusion(f32[1024,256]{1,0:T(8,128)} %reshape.237, bf16[4,256,256]{2,1,0:T(8,128)(2,1)} %slice.16), kind=kLoop, calls=%fused_computation.32 | loop fusion | flops 786432 | bytes 2097152 | tf_op jit(solution)/shard_map/convert_element_type | solution.py:429
  (72 shorter events, 1.2 us)
Async XLA Ops:
  6.5 67.0 %copy-start = (bf16[4,256,1024]{2,1,0:T(8,128)(2,1)S(1)}, bf16[4,256,1024]{2,1,0:T(8,128)(2,1)}, u32[]{:S(2)}) copy-start(bf16[4,256,1024]{2,1,0:T(8,128)(2,1)} %param.28) | copy-start | bytes 6291460
  6.5 13.9 %copy-start.10 = (f32[32,128]{1,0:T(8,128)S(1)}, f32[32,128]{1,0:T(8,128)}, u32[]{:S(2)}) copy-start(f32[32,128]{1,0:T(8,128)} %constant.157.clone.ca_ref) | copy-start | bytes 49156
  6.5 13.9 %copy-start.11 = (f32[32,128]{1,0:T(8,128)S(1)}, f32[32,128]{1,0:T(8,128)}, u32[]{:S(2)}) copy-start(f32[32,128]{1,0:T(8,128)} %constant.158.clone.sa_ref) | copy-start | bytes 49156
  6.5 13.9 %copy-start.5 = (f32[256,128]{1,0:T(8,128)S(1)}, f32[256,128]{1,0:T(8,128)}, u32[]{:S(2)}) copy-start(f32[256,128]{1,0:T(8,128)} %constant.159.clone.cb_ref) | copy-start | bytes 393220
  6.5 13.9 %copy-start.6 = (f32[256,128]{1,0:T(8,128)S(1)}, f32[256,128]{1,0:T(8,128)}, u32[]{:S(2)}) copy-start(f32[256,128]{1,0:T(8,128)} %constant.160.clone.sb_ref) | copy-start | bytes 393220
  6.6 13.9 %copy-start.1 = (bf16[256,1024]{1,0:T(8,128)(2,1)S(1)}, bf16[256,1024]{1,0:T(8,128)(2,1)}, u32[]{:S(2)}) copy-start(bf16[256,1024]{1,0:T(8,128)(2,1)} %emb_ref.1) | copy-start | bytes 1572868
  6.6 13.9 %copy-start.12 = (f32[1024]{0:T(1024)S(1)}, f32[1024]{0:T(1024)}, u32[]{:S(2)}) copy-start(f32[1024]{0:T(1024)} %param.23) | copy-start | bytes 12292
  6.6 13.9 %copy-start.2 = (bf16[1024,256]{1,0:T(8,128)(2,1)S(1)}, bf16[1024,256]{1,0:T(8,128)(2,1)}, u32[]{:S(2)}) copy-start(bf16[1024,256]{1,0:T(8,128)(2,1)} %wq_ref.2) | copy-start | bytes 1572868
  6.6 43.3 %collective-permute-start.7 = (bf16[256,1024]{1,0:T(8,128)(2,1)}, bf16[256,1024]{1,0:T(8,128)(2,1)}, u32[]{:S(2)}, u32[]{:S(2)}) collective-permute-start(bf16[256,1024]{1,0:T(8,128)(2,1)} %param.27), channel_id=1, source_target_pairs={{0,3},{1,0},{2,1},{3,2},{4,7},{5,4},{6,5},{7,6},{8,11},{9,8},{10,9... | collective-permute-start | bytes 1572872 | tf_op jit(solution)/shard_map/ppermute | solution.py:44
  9.7 41.6 %collective-permute-start.5 = (bf16[256,1024]{1,0:T(8,128)(2,1)}, bf16[256,1024]{1,0:T(8,128)(2,1)}, u32[]{:S(2)}, u32[]{:S(2)}) collective-permute-start(bf16[256,1024]{1,0:T(8,128)(2,1)} %param.27), channel_id=1, source_target_pairs={{0,2},{1,3},{2,0},{3,1},{4,6},{5,7},{6,4},{7,5},{8,10},{9,11},{10,... | collective-permute-start | bytes 1572872 | tf_op jit(solution)/shard_map/ppermute | solution.py:44
  10.3 45.1 %collective-permute-start.3 = (bf16[256,1024]{1,0:T(8,128)(2,1)}, bf16[256,1024]{1,0:T(8,128)(2,1)}, u32[]{:S(2)}, u32[]{:S(2)}) collective-permute-start(bf16[256,1024]{1,0:T(8,128)(2,1)} %param.27), channel_id=1, source_target_pairs={{0,1},{1,2},{2,3},{3,0},{4,5},{5,6},{6,7},{7,4},{8,9},{9,10},{10,1... | collective-permute-start | bytes 1572872 | tf_op jit(solution)/shard_map/ppermute | solution.py:44
  11.3 8.1 %collective-permute-start.1 = (s32[1024]{0:T(1024)}, s32[1024]{0:T(1024)S(1)}, u32[]{:S(2)}, u32[]{:S(2)}) collective-permute-start(s32[1024]{0:T(1024)} %param.21), channel_id=1, source_target_pairs={{0,4},{4,8},{8,12},{12,16},{16,20},{20,24},{24,28},{28,32},{32,36}... | collective-permute-start | bytes 12296 | tf_op jit(solution)/shard_map/ppermute | solution.py:48
  13.9 5.5 %collective-permute-start = (s32[256]{0:T(256)S(1)}, s32[256]{0:T(256)S(1)}, u32[]{:S(2)}, u32[]{:S(2)}) collective-permute-start(s32[256]{0:T(256)S(1)} %slice.12), channel_id=1, source_target_pairs={{0,8},{4,12},{8,16},{12,20},{16,24},{20,28},{24,32},{28,36},{32,40... | collective-permute-start | bytes 3080 | tf_op jit(solution)/shard_map/ppermute | solution.py:48
  20.5 1.0 copy-start.3
  21.5 1.0 copy-start.4
  38.5 4.5 %copy-start.19 = (bf16[256,1024]{1,0:T(8,128)(2,1)S(1)}, bf16[256,1024]{1,0:T(8,128)(2,1)}, u32[]{:S(2)}) copy-start(bf16[256,1024]{1,0:T(8,128)(2,1)} %param.27) | copy-start | bytes 1572868
  38.6 9.0 %collective-permute-start.6 = (bf16[272,256]{1,0:T(8,128)(2,1)S(1)}, bf16[272,256]{1,0:T(8,128)(2,1)S(1)}, u32[]{:S(2)}, u32[]{:S(2)}) collective-permute-start(bf16[272,256]{1,0:T(8,128)(2,1)S(1)} %get-tuple-element.6), channel_id=1, source_target_pairs={{0,3},{1,0},{2,1},{3,2},{4,7},{5,4},{6,5},{7,6},{8,11},{9,8},{10,9... | collective-permute-start | bytes 417800 | tf_op jit(solution)/shard_map/ppermute | solution.py:44
  40.9 10.3 %collective-permute-start.4 = (bf16[272,256]{1,0:T(8,128)(2,1)S(1)}, bf16[272,256]{1,0:T(8,128)(2,1)S(1)}, u32[]{:S(2)}, u32[]{:S(2)}) collective-permute-start(bf16[272,256]{1,0:T(8,128)(2,1)S(1)} %get-tuple-element.7), channel_id=1, source_target_pairs={{0,2},{1,3},{2,0},{3,1},{4,6},{5,7},{6,4},{7,5},{8,10},{9,11},{10,... | collective-permute-start | bytes 417800 | tf_op jit(solution)/shard_map/ppermute | solution.py:44
  47.6 7.8 %collective-permute-start.2 = (bf16[272,256]{1,0:T(8,128)(2,1)S(1)}, bf16[272,256]{1,0:T(8,128)(2,1)S(1)}, u32[]{:S(2)}, u32[]{:S(2)}) collective-permute-start(bf16[272,256]{1,0:T(8,128)(2,1)S(1)} %get-tuple-element.5), channel_id=1, source_target_pairs={{0,1},{1,2},{2,3},{3,0},{4,5},{5,6},{6,7},{7,4},{8,9},{9,10},{10,1... | collective-permute-start | bytes 417800 | tf_op jit(solution)/shard_map/ppermute | solution.py:44
  58.1 13.3 %all-to-all-start = ((bf16[1,272,4,256]{3,1,0,2:T(8,128)(2,1)}), bf16[1,272,4,256]{3,1,0,2:T(8,128)(2,1)S(1)}, u32[]{:S(2)}, u32[]{:S(2)}) async-start(bf16[1,272,4,256]{3,1,0,2:T(8,128)(2,1)} %copy.29), calls=%async_computation | async-start | bytes 1114112 | tf_op jit(solution)/shard_map/all_to_all | solution.py:386
  71.4 1.6 copy-start.13
  75.1 12.5 %copy-start.20 = (f32[1024]{0:T(1024)S(1)}, f32[1024]{0:T(1024)}, u32[]{:S(2)}) copy-start(f32[1024]{0:T(1024)} %param.29) | copy-start | bytes 12292
  75.1 12.2 %all-to-all-start.1 = ((bf16[4,64,1024]{2,1,0:T(8,128)(2,1)}), bf16[4,64,1024]{2,1,0:T(8,128)(2,1)S(1)}, u32[]{:S(2)}, u32[]{:S(2)}) async-start(bf16[4,64,1024]{2,1,0:T(8,128)(2,1)} %bitcast.10), calls=%async_computation.1 | async-start | bytes 1048576 | tf_op jit(solution)/shard_map/all_to_all | solution.py:343
  78.7 74.3 %all-gather.2.cloned.1.call-start = ((), (), s32[]{:S(2)}) async-start(), calls=%async_computation.8 | async-start | bytes 2621440 | tf_op jit(solution)/shard_map/all_gather | solution.py:420
  87.3 13.8 %copy-start.16 = (bf16[64,1024]{1,0:T(8,128)(2,1)}, bf16[64,1024]{1,0:T(8,128)(2,1)S(1)}, u32[]{:S(2)}) copy-start(bf16[64,1024]{1,0:T(8,128)(2,1)S(1)} %reduce_sum.39) | copy-start | bytes 393220
  87.3 12.9 %copy-start.7 = (bf16[1024,256]{1,0:T(8,128)(2,1)S(1)}, bf16[1024,256]{1,0:T(8,128)(2,1)}, u32[]{:S(2)}) copy-start(bf16[1024,256]{1,0:T(8,128)(2,1)} %wq_ref.3) | copy-start | bytes 1572868
  87.4 12.9 %copy-start.8 = (bf16[1024,256]{1,0:T(8,128)(2,1)S(1)}, bf16[1024,256]{1,0:T(8,128)(2,1)}, u32[]{:S(2)}) copy-start(bf16[1024,256]{1,0:T(8,128)(2,1)} %wk_ref.3) | copy-start | bytes 1572868
  87.4 12.9 %copy-start.9 = (bf16[1024,256]{1,0:T(8,128)(2,1)S(1)}, bf16[1024,256]{1,0:T(8,128)(2,1)}, u32[]{:S(2)}) copy-start(bf16[1024,256]{1,0:T(8,128)(2,1)} %wv_ref.3) | copy-start | bytes 1572868
  113.8 11.4 %copy-start.18 = (bf16[4,384,128]{2,1,0:T(8,128)(2,1)}, bf16[4,384,128]{2,1,0:T(8,128)(2,1)S(1)}, u32[]{:S(2)}) copy-start(bf16[4,384,128]{2,1,0:T(8,128)(2,1)S(1)} %all_to_all.51) | copy-start | bytes 1179652
  113.8 10.5 %collective-permute-start.10 = (bf16[4,256,128]{2,1,0:T(8,128)(2,1)S(1)}, bf16[4,256,128]{2,1,0:T(8,128)(2,1)S(1)}, u32[]{:S(2)}, u32[]{:S(2)}) collective-permute-start(bf16[4,256,128]{2,1,0:T(8,128)(2,1)S(1)} %get-tuple-element.9), channel_id=1, source_target_pairs={{0,24},{8,0},{16,8},{24,16},{1,25},{9,1},{17,9},{25,17},{2,26},{10... | collective-permute-start | bytes 786440 | tf_op jit(solution)/shard_map/ppermute | solution.py:44
  113.9 10.4 %collective-permute-start.9 = (bf16[4,256,128]{2,1,0:T(8,128)(2,1)S(1)}, bf16[4,256,128]{2,1,0:T(8,128)(2,1)S(1)}, u32[]{:S(2)}, u32[]{:S(2)}) collective-permute-start(bf16[4,256,128]{2,1,0:T(8,128)(2,1)S(1)} %get-tuple-element.9), channel_id=1, source_target_pairs={{0,16},{8,24},{16,0},{24,8},{1,17},{9,25},{17,1},{25,9},{2,18},{10... | collective-permute-start | bytes 786440 | tf_op jit(solution)/shard_map/ppermute | solution.py:44
  115.7 9.6 %collective-permute-start.8 = (bf16[4,256,128]{2,1,0:T(8,128)(2,1)S(1)}, bf16[4,256,128]{2,1,0:T(8,128)(2,1)S(1)}, u32[]{:S(2)}, u32[]{:S(2)}) collective-permute-start(bf16[4,256,128]{2,1,0:T(8,128)(2,1)S(1)} %get-tuple-element.9), channel_id=1, source_target_pairs={{0,8},{8,16},{16,24},{24,0},{1,9},{9,17},{17,25},{25,1},{2,10},{10... | collective-permute-start | bytes 786440 | tf_op jit(solution)/shard_map/ppermute | solution.py:44
  125.3 2.9 %collective-permute-start.11 = (bf16[4,4,256,128]{3,2,1,0:T(8,128)(2,1)S(1)}, bf16[4,4,256,128]{3,2,1,0:T(8,128)(2,1)}, u32[]{:S(2)}, u32[]{:S(2)}) collective-permute-start(bf16[4,4,256,128]{3,2,1,0:T(8,128)(2,1)S(1)} %pad_maximum_fusion.near_ref), channel_id=1, source_target_pairs={{0,4},{4,0},{1,5},{5,1},{2,6},{6,2},{3,7},{7,3},{8,12},{12,8},{9,1... | collective-permute-start | bytes 3145736 | tf_op jit(solution)/shard_map/ppermute | solution.py:44
  140.8 12.2 %copy-start.17 = (bf16[64,1024]{1,0:T(8,128)(2,1)S(1)}, bf16[64,1024]{1,0:T(8,128)(2,1)}, u32[]{:S(2)}) copy-start(bf16[64,1024]{1,0:T(8,128)(2,1)} %copy-done.16) | copy-start | bytes 393220
  152.9 2.3 %copy-start.21 = (f32[1024]{0:T(1024)S(1)}, f32[1024]{0:T(1024)}, u32[]{:S(2)}) copy-start(f32[1024]{0:T(1024)} %param.34) | copy-start | bytes 12292
  184.0 11.5 %all-to-all-start.7 = ((bf16[4,64,1024]{2,1,0:T(8,128)(2,1)}), bf16[4,64,1024]{2,1,0:T(8,128)(2,1)S(1)}, u32[]{:S(2)}, u32[]{:S(2)}) async-start(bf16[4,64,1024]{2,1,0:T(8,128)(2,1)} %broadcast_in_dim.31), calls=%async_computation.7 | async-start | bytes 1048576 | tf_op jit(solution)/shard_map/all_to_all | solution.py:348
  187.5 3.5 %copy-start.14 = (bf16[1,272,4,256]{3,1,0,2:T(8,128)(2,1)S(1)}, bf16[1,272,4,256]{3,1,0,2:T(8,128)(2,1)}, u32[]{:S(2)}) copy-start(bf16[1,272,4,256]{3,1,0,2:T(8,128)(2,1)} %copy-done.13) | copy-start | bytes 1671172
  195.6 0.8 copy-start.15
Sparse Core Ops, SparseCore 0:
  81.2 34.0 all-gather.1
where the time goes:
time: 210 us; the launch traced here: 209 us
  blocking collectives  60.5 us (29%)
  waiting for transfers between devices  39.4 us (19%)
  starting transfers between devices  31.6 us (15%)
  Pallas kernels  29.4 us (14%)
  matrix products  16.7 us (8%)
  local copies, waits for them, and re-layouts  14.6 us (7%)
  between operations  14 us (7%)
  other arithmetic  3.05 us (1%)
    all_to_all x2, blocking collectives, everyone(): return lax.all_to_all(wide, 'head', 0, 0).reshape(-1, values.shape[-1])  25 us
    dot_general x13, matrix products, dot(): return jnp.dot(left, right, preferred_element_type=f32)  16.7 us
    pallas_call x1, Pallas kernels, fine_attention(): pl.pallas_call(fine_kernel, grid=(4,), out_shape=jax.ShapeDtypeStruct((HA...  16 us
    ppermute x10, waiting for transfers between devices, shift(): lax.ppermute(value, axis, [(i, (i + steps) % count) for i in range(count)])  15.7 us
    ppermute x10, starting transfers between devices, shift(): lax.ppermute(value, axis, [(i, (i + steps) % count) for i in range(count)])  15.4 us
    all_to_all x1, blocking collectives, local(): turned = lax.all_to_all(packed, 'z', 0, 0)  12.6 us
    pallas_call x1, Pallas kernels, coarse_attention(): pl.pallas_call(coarse_kernel, out_shape=jax.ShapeDtypeStruct((1024, 64),...  12.5 us
    all_to_all x1, blocking collectives, to_shares(): return lax.all_to_all(values.reshape(4, rows, -1), 'head', 0, 0)  11.6 us
  transfers between devices with their start and end apart: 16, of which 9 were waited for; matrix products, arithmetic and copies ran while one was open for 6% of the time, Pallas kernels for 14%

commit v1 on v0

v1 whole, which is shorter than its diff:
```python
import functools
import math

import jax
import jax.numpy as jnp
import numpy as np
from jax import lax
from jax.experimental import pallas as pl
from jax.experimental.pallas import tpu as pltpu
from jax.sharding import Mesh
from jax.sharding import PartitionSpec as P

D = 1024
HEAD_DIM = 64
SHORTEN = 4
WINDOW = 1024
BLOCK = 256
HALO = 16
ROWS = 1024
PAST = WINDOW + BLOCK
KEYS = PAST + ROWS
SHARE = 256
COARSE_ROWS = 256
SEQ = ("z", "x", "core")

epsilon = 1e-06
masked_low = -1e30
q_scale = HEAD_DIM ** (-0.5) * math.log2(math.e)
bf16 = jnp.bfloat16
f32 = jnp.float32


def angle_tables():
    lane = np.arange(128) % 32
    period = 2.0 ** (4 + lane * 14 // 32)
    coarse = (256.0 * np.arange(32)[:, None]) % period[None]
    near = np.arange(256)[:, None] % period[None]
    a = coarse * (2.0 * np.pi / period)[None]
    b = near * (2.0 * np.pi / period)[None]
    return [t.astype(np.float32) for t in (np.cos(a), np.sin(a), np.cos(b), np.sin(b))]


def shift(value, axis, steps, count):
    return lax.ppermute(value, axis, [(i, (i + steps) % count) for i in range(count)])


def later(value, axis, steps, count):
    return lax.ppermute(value, axis, [(i, i + steps) for i in range(count - steps)])


def exchange(block_for, axis, count):
    me = lax.axis_index(axis)
    got = [block_for(me)]
    for s in range(1, count):
        got.append(shift(block_for((me + s) % count), axis, s, count))
    return got


def dot(left, right):
    return jnp.dot(left, right, preferred_element_type=f32)


def dot_t(left, right):
    return lax.dot_general(left, right, (((1,), (1,)), ((), ())), preferred_element_type=f32)


def norm_rows(data, gain):
    power = jnp.mean(data * data, axis=-1, keepdims=True)
    return (data * lax.rsqrt(power + epsilon) * gain).astype(bf16)


def partner(values):
    width = values.shape[1]
    lane = lax.broadcasted_iota(jnp.int32, values.shape, 1)
    ahead = pltpu.roll(values, width - 32, 1)
    behind = pltpu.roll(values, 32, 1)
    return jnp.where(lane % 64 < 32, -ahead, behind)


def halves(table):
    high = table.astype(bf16)
    low = (table - high.astype(f32)).astype(bf16)
    return high, low


def turn_tables(ca, sa, cb, sb):
    cosine = ca * cb - sa * sb
    sine = sa * cb + ca * sb
    return jnp.concatenate([cosine, cosine], axis=1), jnp.concatenate([sine, sine], axis=1)


def pick(ids, levels=256):
    columns = lax.broadcasted_iota(jnp.int32, (ids.shape[0], levels), 1)
    return (ids == columns).astype(f32).astype(bf16)


def turned_rows(hot, tab_ref, n, cosine, sine):
    plain = dot(hot, tab_ref[n]) + dot(hot, tab_ref[n + 1])
    other = dot(hot, tab_ref[n + 2]) + dot(hot, tab_ref[n + 3])
    return (plain * cosine + other * sine).astype(bf16)


def fine_own_kernel(
    ids_ref, emb_ref, gain_ref, wq_ref, wk_ref, wv_ref, ca_ref, sa_ref, cb_ref, sb_ref,
    tab_ref, q_ref, k_ref, v_ref,
):
    fine_in = norm_rows(emb_ref[...].astype(f32), gain_ref[...])
    tq = dot(fine_in, wq_ref[...]) * q_scale
    tk = dot(fine_in, wk_ref[...])
    for n, table in enumerate((tq, partner(tq), tk, partner(tk))):
        high, low = halves(table)
        tab_ref[2 * n] = high
        tab_ref[2 * n + 1] = low
    tab_ref[8] = dot(fine_in, wv_ref[...]).astype(bf16)
    cb = cb_ref[...]
    sb = sb_ref[...]
    for block in range(ROWS // BLOCK):
        at = slice(block * BLOCK, (block + 1) * BLOCK)
        hot = pick(ids_ref[at, :])
        far = PAST // BLOCK + block
        cosine, sine = turn_tables(ca_ref[far : far + 1, :], sa_ref[far : far + 1, :], cb, sb)
        q_ref[at, :] = turned_rows(hot, tab_ref, 0, cosine, sine)
        k_ref[at, :] = turned_rows(hot, tab_ref, 4, cosine, sine)
        v_ref[at, :] = dot(hot, tab_ref[8]).astype(bf16)


def fine_kernel(
    place_ref, ids_ref, tab_ref, q_ref, k_own_ref, v_own_ref, ca_ref, sa_ref, cb_ref, sb_ref,
    out_ref, k_ref, v_ref,
):
    step = pl.program_id(0)
    lowest = jnp.maximum(PAST - place_ref[0] * ROWS, 0)
    head_lane = lax.broadcasted_iota(jnp.int32, (1, SHARE), 1) // HEAD_DIM

    @pl.when(step == 0)
    def _():
        cb = cb_ref[...]
        sb = sb_ref[...]
        k_ref[PAST:, :] = k_own_ref[...]
        v_ref[PAST:, :] = v_own_ref[...]
        for block in range(PAST // BLOCK):
            at = slice(block * BLOCK, (block + 1) * BLOCK)
            hot = pick(ids_ref[at, :])
            cosine, sine = turn_tables(
                ca_ref[block : block + 1, :], sa_ref[block : block + 1, :], cb, sb
            )
            k_ref[at, :] = turned_rows(hot, tab_ref, 4, cosine, sine)
            v_ref[at, :] = dot(hot, tab_ref[8]).astype(bf16)

        halo_q = turned_rows(
            pick(ids_ref[PAST - HALO : PAST, :]), tab_ref, 0, cosine[-HALO:], sine[-HALO:]
        )
        stacked = jnp.concatenate(
            [jnp.where(head_lane == h, halo_q, jnp.zeros_like(halo_q)) for h in range(4)], axis=0
        )
        scores = dot_t(stacked, k_ref[0:PAST, :])
        row = lax.broadcasted_iota(jnp.int32, scores.shape, 0) % HALO + (PAST - HALO)
        col = lax.broadcasted_iota(jnp.int32, scores.shape, 1)
        allowed = (col <= row) & (col > row - WINDOW) & (col >= lowest)
        scores = jnp.where(allowed, scores, masked_low)
        top = jnp.max(scores, axis=1, keepdims=True)
        weights = jnp.exp2(scores - top)
        total = jnp.sum(weights, axis=1, keepdims=True)
        mixed = dot(weights.astype(bf16), v_ref[0:PAST, :]) / total
        result = jnp.zeros((HALO, SHARE), f32)
        for h in range(4):
            result = jnp.where(head_lane == h, mixed[h * HALO : (h + 1) * HALO], result)
        out_ref[0:HALO, :] = result.astype(bf16)

    begin = pl.multiple_of((step + 1) * BLOCK, BLOCK)
    keys = k_ref[pl.ds(begin, PAST), :]
    values = v_ref[pl.ds(begin, PAST), :]
    query = q_ref[pl.ds(pl.multiple_of(step * BLOCK, BLOCK), BLOCK), :]
    row = lax.broadcasted_iota(jnp.int32, (BLOCK, BLOCK), 0)
    col = lax.broadcasted_iota(jnp.int32, (BLOCK, BLOCK), 1)
    biases = [
        jnp.where(begin + t * BLOCK >= lowest, 0.0, masked_low).astype(f32) for t in range(4)
    ]
    first_bias = jnp.where(col > row, 0.0, masked_low) + biases[0]
    last_bias = jnp.where(col <= row, 0.0, masked_low)
    result = jnp.zeros((BLOCK, SHARE), f32)
    for h in range(4):
        scores = dot_t(jnp.where(head_lane == h, query, jnp.zeros_like(query)), keys)
        tiles = [scores[:, t * BLOCK : (t + 1) * BLOCK] for t in range(5)]
        tiles = (
            [tiles[0] + first_bias]
            + [tiles[t] + biases[t] for t in range(1, 4)]
            + [tiles[4] + last_bias]
        )
        peak = tiles[0]
        for t in range(1, 5):
            peak = jnp.maximum(peak, tiles[t])
        top = jnp.max(peak, axis=1, keepdims=True)
        weights = [jnp.exp2(tile - top) for tile in tiles]
        summed = weights[0]
        for t in range(1, 5):
            summed = summed + weights[t]
        total = jnp.sum(summed, axis=1, keepdims=True)
        mixed = dot(jnp.concatenate([w.astype(bf16) for w in weights], axis=1), values)
        result = jnp.where(head_lane == h, mixed / total, result)
    at = pl.multiple_of(HALO + step * BLOCK, HALO)
    out_ref[pl.ds(at, BLOCK), :] = result.astype(bf16)


def vmem():
    return pl.BlockSpec(memory_space=pltpu.VMEM)


def smem():
    return pl.BlockSpec(memory_space=pltpu.SMEM)


def call(kernel, name, shapes, scalars, arrays, scratch=(), grid=None, limit=48):
    one = not isinstance(shapes, (list, tuple))
    extra = {} if grid is None else {"grid": grid}
    return pl.pallas_call(
        kernel,
        out_shape=shapes,
        in_specs=[smem()] * len(scalars) + [vmem()] * len(arrays),
        out_specs=vmem() if one else [vmem()] * len(shapes),
        scratch_shapes=list(scratch),
        compiler_params=pltpu.CompilerParams(vmem_limit_bytes=limit << 20),
        name=name,
        **extra,
    )(*scalars, *arrays)


def half_lanes(ref, quarter, half):
    begin = pl.multiple_of(quarter * 256 + half * 128, 128)
    return ref[:, pl.ds(begin, 128)]


def fine_rows_kernel(
    where_ref, ids_ref, emb_ref, g0, g1, g2, g3, own_ref, mine_ref, other_ref, out_ref
):
    place, head, core = where_ref[0], where_ref[1], where_ref[2]
    merged = dot(pick(ids_ref[...]), emb_ref[...]) + dot(g0[...], own_ref[...])
    for s, got in ((1, g1), (2, g2), (3, g3)):
        merged += dot(half_lanes(got, 0, core), mine_ref[s - 1])
        merged += dot(half_lanes(got, 0, 1 - core), other_ref[s - 1])
    rows = 256 + HALO
    token = (
        place * ROWS + head * 256 - HALO + lax.broadcasted_iota(jnp.int32, (rows, D), 0)
    )
    fine = jnp.where(token >= 0, merged, 0.0).astype(bf16)
    index = lax.broadcasted_iota(jnp.int32, (256, rows), 0)
    column = lax.broadcasted_iota(jnp.int32, (256, rows), 1)
    source = 4 * (index % 64) + index // 64 + (HALO - 3)
    choose = (source == column).astype(f32).astype(bf16)
    grouped = dot(choose, fine).astype(bf16)
    for d in range(4):
        out_ref[d, 0:256, :] = grouped[:, d * SHARE : (d + 1) * SHARE]
        out_ref[d, 256:rows, :] = fine[256:rows, d * SHARE : (d + 1) * SHARE]


def short_part_kernel(group_ref, w_ref, out_ref):
    total = dot(group_ref[0:64, :], w_ref[0])
    for r in range(1, SHORTEN):
        total += dot(group_ref[r * 64 : (r + 1) * 64, :], w_ref[r])
    out_ref[...] = total.astype(bf16)


def coarse_pack_kernel(
    where_ref, s0, s1, s2, s3, gain_ref, wq_ref, wk_ref, wv_ref, ca_ref, sa_ref, cb_ref, sb_ref,
    out_ref, short_ref,
):
    place, head = where_ref[0], where_ref[1]
    for s, ref in enumerate((s0, s1, s2, s3)):
        begin = pl.multiple_of(lax.rem(head - s + 4, 4) * 64, 64)
        short_ref[pl.ds(begin, 64), :] = ref[...]
    x = norm_rows(short_ref[...].astype(f32), gain_ref[...])
    cosine, sine = turn_tables(
        ca_ref[pl.ds(place, 1), :], sa_ref[pl.ds(place, 1), :], cb_ref[...], sb_ref[...]
    )

    def turned(values):
        return values * cosine + partner(values) * sine

    q = turned(dot(x, wq_ref[...])) * q_scale
    k = turned(dot(x, wk_ref[...]))
    v = dot(x, wv_ref[...])
    low_lanes = lax.broadcasted_iota(jnp.int32, (1, 128), 1) < 64
    half = COARSE_ROWS // 2
    for h in range(4):
        pair = (h // 2) * 128
        kp = k[:, pair : pair + 128]
        vp = v[:, pair : pair + 128]
        qp = q[:, pair : pair + 128]
        if h % 2 == 0:
            kv = jnp.where(low_lanes, kp, pltpu.roll(vp, 64, 1))
            qq = jnp.where(low_lanes, qp[:half], pltpu.roll(qp[half:], 64, 1))
        else:
            kv = jnp.where(low_lanes, pltpu.roll(kp, 64, 1), vp)
            qq = jnp.where(low_lanes, pltpu.roll(qp[:half], 64, 1), qp[half:])
        out_ref[h, 0:COARSE_ROWS, :] = kv.astype(bf16)
        out_ref[h, COARSE_ROWS : COARSE_ROWS + half, :] = qq.astype(bf16)


def absorb(q_ref, top_ref, total_ref, acc_ref, begin, rows, parts):
    at = pl.ds(begin, rows)
    query = q_ref[at, :]
    scores = [dot_t(query, kv) for kv in parts]
    peak = scores[0]
    for s in scores[1:]:
        peak = jnp.maximum(peak, s)
    old = top_ref[at, :]
    top = jnp.maximum(old, jnp.max(peak, axis=1, keepdims=True))
    factor = jnp.exp2(old - top)
    both = jnp.concatenate([top, top], axis=1)
    weights = [jnp.exp2(s - both) for s in scores]
    summed = weights[0]
    for w in weights[1:]:
        summed = summed + w
    contrib = dot(weights[0].astype(bf16), parts[0])
    for w, kv in zip(weights[1:], parts[1:]):
        contrib = contrib + dot(w.astype(bf16), kv)
    top_ref[at, :] = top
    total_ref[at, :] = total_ref[at, :] * factor + jnp.sum(summed, axis=1, keepdims=True)
    acc_ref[at, :] = acc_ref[at, :] * factor + contrib


def coarse_first_kernel(turned_ref, q_ref, top_ref, total_ref, acc_ref):
    half = COARSE_ROWS // 2
    low_lanes = lax.broadcasted_iota(jnp.int32, (1, 128), 1) < 64
    row = lax.broadcasted_iota(jnp.int32, (256, 256), 0)
    col = lax.broadcasted_iota(jnp.int32, (256, 256), 1)
    for z in range(4):
        packed = turned_ref[z, COARSE_ROWS:, :].astype(f32)
        zero = jnp.zeros_like(packed)
        q_ref[z * 256 : z * 256 + half, :] = jnp.where(low_lanes, packed, zero).astype(bf16)
        q_ref[z * 256 + half : (z + 1) * 256, :] = jnp.where(
            low_lanes, pltpu.roll(packed, 64, 1), zero
        ).astype(bf16)
        kv = turned_ref[z, :COARSE_ROWS, :]
        at = pl.ds(z * 256, 256)
        scores = jnp.where(col <= row, dot_t(q_ref[at, :], kv), masked_low)
        top = jnp.max(scores, axis=1, keepdims=True)
        weights = jnp.exp2(scores - top)
        top_ref[at, :] = jnp.broadcast_to(top, (256, 128))
        total_ref[at, :] = jnp.broadcast_to(jnp.sum(weights, axis=1, keepdims=True), (256, 128))
        acc_ref[at, :] = dot(weights.astype(bf16), kv)
    for z in range(3):
        absorb(
            q_ref, top_ref, total_ref, acc_ref, (z + 1) * 256, (3 - z) * 256,
            [turned_ref[z, :COARSE_ROWS, :]],
        )


def absorb_chunks(chunk_ref, first_chunk, refs, state):
    for a in range(0, len(refs), 2):
        for z in range(3):
            absorb(*state, (z + 1) * 256, (3 - z) * 256, [r[z] for r in refs[a : a + 2]])
    for n, ref in enumerate(refs):

        @pl.when(chunk_ref[first_chunk + n] < chunk_ref[0])
        def _(ref=ref):
            for z in range(4):
                absorb(*state, z * 256, 256, [ref[z]])


def coarse_near_kernel(
    chunk_ref, n1, n2, n3, q_ref, top_in, total_in, acc_in, top_ref, total_ref, acc_ref
):
    top_ref[...] = top_in[...]
    total_ref[...] = total_in[...]
    acc_ref[...] = acc_in[...]
    absorb_chunks(chunk_ref, 1, [n1, n2, n3], (q_ref, top_ref, total_ref, acc_ref))


def coarse_far_kernel(
    chunk_ref, far_ref, q_ref, top_in, total_in, acc_in, out_ref, top_ref, total_ref, acc_ref
):
    top_ref[...] = top_in[...]
    total_ref[...] = total_in[...]
    acc_ref[...] = acc_in[...]
    refs = [far_ref.at[s] for s in range(4)]
    absorb_chunks(chunk_ref, 4, refs, (q_ref, top_ref, total_ref, acc_ref))
    mixed = acc_ref[...] / total_ref[...]
    low_lanes = lax.broadcasted_iota(jnp.int32, (1, 128), 1) < 64
    for z in range(4):
        upper = pltpu.roll(mixed[z * 256 : z * 256 + 128], 64, 1)
        lower = mixed[z * 256 + 128 : (z + 1) * 256]
        out_ref[z] = jnp.where(low_lanes, upper, lower).astype(bf16)


def feed_kernel(
    where_ref, heads_ref, own_ref, mine_ref, other_ref, short_ref, gain_ref, up_ref, down_ref,
    part_ref, first_ref, mixed_ref, all_ref,
):
    head, core = where_ref[1], where_ref[2]
    low_lanes = lax.broadcasted_iota(jnp.int32, (1, 128), 1) < 64
    for y in range(4):
        for pair in range(2):
            even = heads_ref[2 * pair * 4 + y].astype(f32)
            odd = heads_ref[(2 * pair + 1) * 4 + y].astype(f32)
            at = slice(y * 256 + pair * 128, y * 256 + (pair + 1) * 128)
            mixed_ref[0:128, at] = jnp.where(low_lanes, even, pltpu.roll(odd, 64, 1)).astype(bf16)
            mixed_ref[128:256, at] = jnp.where(low_lanes, pltpu.roll(even, 64, 1), odd).astype(bf16)
    first = short_ref[...].astype(f32)
    for half in range(2):
        first += dot(half_lanes(mixed_ref, head, half), own_ref[half * 128 : (half + 1) * 128, :])
    for s in range(1, 4):
        source = lax.rem(head - s + 4, 4)
        first += dot(half_lanes(mixed_ref, source, core), mine_ref[s - 1])
        first += dot(half_lanes(mixed_ref, source, 1 - core), other_ref[s - 1])
    all_ref[...] = first
    first_ref[...] = all_ref[pl.ds(pl.multiple_of(head * 64, 64), 64), :]
    feed = norm_rows(first, gain_ref[...])
    inner = jax.nn.gelu(dot(feed, up_ref[...])).astype(bf16)
    part_ref[...] = dot(inner, down_ref[...]).astype(bf16).reshape(4, 64, D)


def final_kernel(where_ref, s0, s1, s2, s3, b0, b1, b2, b3, up_ref, out_ref):
    head = where_ref[1]
    rows = 256 + HALO
    second = jnp.concatenate([ref[...] for ref in (s0, s1, s2, s3)], axis=0)
    lifted = dot(second, up_ref[...])
    index = lax.broadcasted_iota(jnp.int32, (256, rows), 0)
    column = lax.broadcasted_iota(jnp.int32, (256, rows), 1)
    r, m = index // 64, index % 64
    source = jnp.where(r == 0, 192 + m, jnp.where(m == 63, 268 + r, (r - 1) * 64 + m + 1))
    choose = (source == column).astype(f32).astype(bf16)
    index = lax.broadcasted_iota(jnp.int32, (256, 256), 0)
    column = lax.broadcasted_iota(jnp.int32, (256, 256), 1)
    weave = ((index % 4) * 64 + index // 4 == column).astype(f32).astype(bf16)
    for s, block in enumerate((b0, b1, b2, b3)):
        mine = lifted[s * 64 : (s + 1) * 64]
        raised = jnp.concatenate([mine[:, q * SHARE : (q + 1) * SHARE] for q in range(4)], axis=0)
        value = (dot(choose, block[...]) + raised).astype(bf16)
        begin = pl.multiple_of(lax.rem(head - s + 4, 4) * 256, 256)
        out_ref[pl.ds(begin, 256), :] = dot(weave, value).astype(bf16)


def gather_rest(weight, core):
    half = lax.dynamic_slice_in_dim(weight, core * 128, 128, 0)
    mine = jnp.stack([shift(half, "head", s, 4) for s in range(1, 4)])
    return mine, shift(mine, "core", 1, 2)


def local(
    token_ids, embedding, fine_norm, fine_query, fine_key, fine_value, fine_output,
    shorten_weight, coarse_norm, coarse_query, coarse_key, coarse_value, coarse_output,
    ffn_norm, ffn_up, ffn_down, upsample_weight,
):
    place = lax.axis_index(SEQ).astype(jnp.int32)
    head = lax.axis_index("head").astype(jnp.int32)
    x_place = lax.axis_index("x").astype(jnp.int32)
    core = lax.axis_index("core").astype(jnp.int32)
    tables = [jnp.asarray(t) for t in angle_tables()]
    where = jnp.stack([place, head, core])

    prior = later(token_ids, SEQ, 1, 32)
    before = later(token_ids[ROWS - BLOCK :], SEQ, 2, 32)
    share = jax.ShapeDtypeStruct((ROWS, SHARE), bf16)
    tab, q, k_own, v_own = call(
        fine_own_kernel, "fine_own",
        [jax.ShapeDtypeStruct((9, 256, SHARE), bf16), share, share, share], [],
        [token_ids[:, None], embedding, fine_norm[None], fine_query, fine_key, fine_value, *tables],
    )
    past_ids = jnp.concatenate([before, prior])
    past_ids, fine_output_held = lax.optimization_barrier((past_ids, fine_output))
    out_mine, out_other = gather_rest(fine_output_held, core)

    mixed = call(
        fine_kernel, "fine_attention", jax.ShapeDtypeStruct((HALO + ROWS, SHARE), bf16),
        [where], [past_ids[:, None], tab, q, k_own, v_own, *tables],
        [pltpu.VMEM((KEYS, SHARE), bf16), pltpu.VMEM((KEYS, SHARE), bf16)], grid=(4,),
    )

    rows = 256 + HALO
    got = exchange(lambda d: lax.dynamic_slice_in_dim(mixed, d * 256, rows, 0), "head", 4)
    own_ids = lax.dynamic_slice_in_dim(
        jnp.concatenate([past_ids[PAST - HALO :], token_ids]), head * 256, rows, 0
    )
    sends = call(
        fine_rows_kernel, "fine_rows", jax.ShapeDtypeStruct((4, rows, SHARE), bf16),
        [where], [own_ids[:, None], embedding, *got, fine_output, out_mine, out_other],
    )
    blocks = exchange(lambda d: lax.dynamic_index_in_dim(sends, d, 0, keepdims=False), "head", 4)

    terms = []
    for s, block in enumerate(blocks):
        part = call(
            short_part_kernel, "short_part", jax.ShapeDtypeStruct((64, D), bf16), [],
            [block, shorten_weight],
        )
        terms.append(part if s == 0 else shift(part, "head", 4 - s, 4))
    short_own = sum(t.astype(f32) for t in terms).astype(bf16)
    shorts = [short_own] + [shift(short_own, "head", s, 4) for s in range(1, 4)]
    packed, short = call(
        coarse_pack_kernel, "coarse_pack",
        [
            jax.ShapeDtypeStruct((4, COARSE_ROWS * 3 // 2, 128), bf16),
            jax.ShapeDtypeStruct((COARSE_ROWS, D), bf16),
        ],
        [where],
        [*shorts, coarse_norm[None], coarse_query, coarse_key, coarse_value, *tables],
    )

    turned = lax.all_to_all(packed, "z", 0, 0)
    turned, coarse_output_held = lax.optimization_barrier((turned, coarse_output))
    kv = turned[:, :COARSE_ROWS]
    near = [shift(kv, "x", s, 4) for s in range(1, 4)]
    far = shift(jnp.stack([kv, *near]), "core", 1, 2)
    co_mine, co_other = gather_rest(coarse_output_held, core)
    steps = jnp.arange(4, dtype=jnp.int32)
    columns_x = (x_place - steps + 4) % 4
    chunks = jnp.concatenate([2 * columns_x + core, 2 * columns_x + 1 - core])
    wide = jax.ShapeDtypeStruct((1024, 128), f32)
    state = call(
        coarse_first_kernel, "coarse_first",
        [jax.ShapeDtypeStruct((1024, 128), bf16), wide, wide, wide], [], [turned],
    )
    q_all, sums = state[0], state[1:]
    sums = call(coarse_near_kernel, "coarse_near", [wide] * 3, [chunks], [*near, q_all, *sums])
    attended = call(
        coarse_far_kernel, "coarse_far", jax.ShapeDtypeStruct((4, 128, 128), bf16),
        [chunks], [far, q_all, *sums], [pltpu.VMEM((1024, 128), f32)] * 3,
    )

    wide_sends = jnp.broadcast_to(attended[:, None], (4, 4, 128, 128)).reshape(16, 128, 128)
    heads_in = lax.all_to_all(wide_sends, ("z", "head"), 0, 0)
    parts, first_own = call(
        feed_kernel, "feed",
        [jax.ShapeDtypeStruct((4, 64, D), bf16), jax.ShapeDtypeStruct((64, D), f32)],
        [where],
        [heads_in, coarse_output, co_mine, co_other, short, ffn_norm[None], ffn_up, ffn_down],
        [pltpu.VMEM((COARSE_ROWS, D), bf16), pltpu.VMEM((COARSE_ROWS, D), f32)],
    )
    sums = exchange(lambda d: lax.dynamic_index_in_dim(parts, d, 0, keepdims=False), "head", 4)
    second_own = (first_own + sum(t.astype(f32) for t in sums)).astype(bf16)
    seconds = [second_own] + [shift(second_own, "head", s, 4) for s in range(1, 4)]
    return call(
        final_kernel, "final", jax.ShapeDtypeStruct((ROWS, SHARE), bf16),
        [where], [*seconds, *blocks, upsample_weight.reshape(D, SHORTEN * SHARE)],
    )


def solution(mesh):
    split = Mesh(mesh.devices.reshape(4, 4, 2, 4), ("z", "x", "core", "head"))
    return jax.shard_map(
        local,
        mesh=split,
        in_specs=(
            P(SEQ), P(), P(), P(None, "head"), P(None, "head"), P(None, "head"), P("head", None),
            P(None, "head", None), P(), P(None, "head"), P(None, "head"), P(None, "head"),
            P("head", None), P(), P(None, "head"), P("head", None), P(None, None, "head"),
        ),
        out_specs=P(SEQ, "head"),
        check_vma=False,
    )
```

time: 210 us -> 194 us (0.924)
  waiting for transfers between devices: 39.4 us -> 87.8 us
  blocking collectives: 60.5 us -> 12.2 us
  matrix products: 16.7 us -> 0 us
  between operations: 14 us -> 0.63 us
  starting transfers between devices: 31.6 us -> 42.6 us
  Pallas kernels: 29.4 us -> 40.1 us
  local copies, waits for them, and re-layouts: 14.6 us -> 8.93 us
  other arithmetic: 3.05 us -> 0.72 us
    ppermute x10 -> x30, waiting for transfers between devices: 15.7 us -> 73.6 us  [shift(): lax.ppermute(value, axis, [(i, (i + steps) % count) for i in range(count)])]
    all_to_all x4 -> x0, blocking collectives: 47.9 us -> none  [the longest x2 25 us: everyone(): return lax.all_to_all(wide, 'head', 0, 0).reshape(-1, values.shape[-1])]
    ppermute x10 -> x30, starting transfers between devices: 15.4 us -> 33.2 us  [shift(): lax.ppermute(value, axis, [(i, (i + steps) % count) for i in range(count)])]
    dot_general x13 -> x0, matrix products: 16.7 us -> none  [dot(): return jnp.dot(left, right, preferred_element_type=f32)]
    pallas_call x3 -> x13, Pallas kernels: 29.4 us -> 40.1 us  [call(): pl.pallas_call(kernel, out_shape=shapes, in_specs=[smem()] * len(scalars)...]
    all_to_all x3 -> x1, waiting for transfers between devices: 21.3 us -> 12.6 us  [local(): heads_in = lax.all_to_all(wide_sends, ('z', 'head'), 0, 0)]
    all_to_all x3 -> x1, starting transfers between devices: 10.5 us -> 3.57 us  [local(): heads_in = lax.all_to_all(wide_sends, ('z', 'head'), 0, 0)]
    convert_element_type x4 -> x2, other arithmetic: 2.49 us -> 0.16 us  [the longest x1 0.09 us: local(): second_own = (first_own + sum((t.astype(f32) for t in sums))).astype(bf16)]
  transfers between devices with their start and end apart: 16 -> 33, of which waited for: 9 -> 23; matrix products, arithmetic and copies ran while one was open for 6% -> 2% of each run, Pallas kernels for 14% -> 15%
where the time goes in v1:
time: 194 us; the launch traced here: 193 us
  waiting for transfers between devices  87.8 us (45%)
  starting transfers between devices  42.6 us (22%)
  Pallas kernels  40.1 us (21%)
  blocking collectives  12.2 us (6%)
  local copies, waits for them, and re-layouts  8.93 us (5%)
    ppermute x30, waiting for transfers between devices, shift(): lax.ppermute(value, axis, [(i, (i + steps) % count) for i in range(count)])  73.6 us
    pallas_call x13, Pallas kernels, call(): pl.pallas_call(kernel, out_shape=shapes, in_specs=[smem()] * len(scalars)...  40.1 us
    ppermute x30, starting transfers between devices, shift(): lax.ppermute(value, axis, [(i, (i + steps) % count) for i in range(count)])  33.2 us
    all_to_all x1, waiting for transfers between devices, local(): heads_in = lax.all_to_all(wide_sends, ('z', 'head'), 0, 0)  12.6 us
    all_to_all x1, blocking collectives, local(): turned = lax.all_to_all(packed, 'z', 0, 0)  12.2 us
    ppermute x2, starting transfers between devices, later(): lax.ppermute(value, axis, [(i, i + steps) for i in range(count - steps)])  5.78 us
    unnamed x63, local copies, waits for them, and re-layouts  4.79 us
  transfers between devices with their start and end apart: 33, of which 23 were waited for; matrix products, arithmetic and copies ran while one was open for 2% of the time, Pallas kernels for 15%

profile of v1, /device:TPU:6, one launch (start us, length us, event | category | flops | bytes accessed | tf_op | source)
XLA Modules:
  0.0 193.0 jit_solution(8915704923578756172)
XLA Ops:
  0.1 2.1 %collective-permute-start.1 = (s32[1024]{0:T(1024)}, s32[1024]{0:T(1024)S(1)}, u32[]{:S(2)}, u32[]{:S(2)}) collective-permute-start(s32[1024]{0:T(1024)} %param.21), channel_id=1, source_target_pairs={{0,4},{4,8},{8,12},{12,16},{16,20},{20,24},{24,28},{28,32},{32,36}... | collective-permute-start | bytes 12296 | tf_op jit(solution)/shard_map/ppermute | solution.py:48
  2.1 0.7 slice.9
  2.8 3.7 %collective-permute-start = (s32[256]{0:T(256)S(1)}, s32[256]{0:T(256)S(1)}, u32[]{:S(2)}, u32[]{:S(2)}) collective-permute-start(s32[256]{0:T(256)S(1)} %slice.9), channel_id=1, source_target_pairs={{0,8},{4,12},{8,16},{12,20},{16,24},{20,28},{24,32},{28,36},{32,40... | collective-permute-start | bytes 3080 | tf_op jit(solution)/shard_map/ppermute | solution.py:48
  6.6 1.7 collective-permute-done
  8.3 1.0 constant_dynamic-slice_fusion.1
  9.3 3.1 %collective-permute-start.7 = (bf16[128,1024]{1,0:T(8,128)(2,1)S(1)}, bf16[128,1024]{1,0:T(8,128)(2,1)S(1)}, u32[]{:S(2)}, u32[]{:S(2)}) collective-permute-start(bf16[128,1024]{1,0:T(8,128)(2,1)S(1)} %constant_dynamic-slice_fusion.1), channel_id=1, source_target_pairs={{0,3},{1,0},{2,1},{3,2},{4,7},{5,4},{6,5},{7,6},{8,11},{9,8},{10,9... | collective-permute-start | bytes 786440 | tf_op jit(solution)/shard_map/ppermute | solution.py:44
  12.3 0.6 collective-permute-start.6
  13.0 1.0 collective-permute-start.5
  13.9 10.5 %collective-permute-done.7 = bf16[128,1024]{1,0:T(8,128)(2,1)S(1)} collective-permute-done((bf16[128,1024]{1,0:T(8,128)(2,1)S(1)}, bf16[128,1024]{1,0:T(8,128)(2,1)S(1)}, u32[]{:S(2)}, u32[]{:S(2)}) %collective-permute-start.7) | collective-permute-done | bytes 262176 | tf_op jit(solution)/shard_map/ppermute | solution.py:44
  24.5 3.7 %collective-permute-done.5 = bf16[128,1024]{1,0:T(8,128)(2,1)S(1)} collective-permute-done((bf16[128,1024]{1,0:T(8,128)(2,1)S(1)}, bf16[128,1024]{1,0:T(8,128)(2,1)S(1)}, u32[]{:S(2)}, u32[]{:S(2)}) %collective-permute-start.5) | collective-permute-done | bytes 262176 | tf_op jit(solution)/shard_map/ppermute | solution.py:44
  28.8 1.0 copy-done.17
  29.8 1.0 copy-done.18
  30.8 2.1 %fine_own.1 = (bf16[9,256,256]{2,1,0:T(8,128)(2,1)S(1)}, bf16[1024,256]{1,0:T(8,128)(2,1)S(1)}, bf16[1024,256]{1,0:T(8,128)(2,1)S(1)}, bf16[1024,256]{1,0:T(8,128)(2,1)S(1)}) custom-call(s32[1024,1]{1,0:T(8,128)S(1)} %copy.22.ids_ref, bf16[256,1024]{1,0:T(8,128)(2,1)S(1)} %copy-done.2, f32[1,1024]{1,0:T(1,128)S(1)} %bitcast.43, ...), custom_call_target="tpu_custom_call" | custom-call | tf_op jit(solution)/shard_map/fine_own/pallas_call | solution.py:216
  33.3 11.8 %fine_attention.1 = bf16[1040,256]{1,0:T(8,128)(2,1)S(1)} custom-call(s32[3]{0:T(128)S(1)} %pad_add_fusion.1.place_ref.where_ref, s32[1280,1]{1,0:T(8,128)S(1)} %broadcast_in_dim.32.ids_ref, bf16[9,256,256]{2,1,0:T(8,128)(2,1)S(1)} %get-tuple-element.25.tab_ref, bf16[1024,256]{1,0:T(8,128)(2,1)S(1)} %get-tuple-element.26.q_ref, ...), custom_call_target="tpu_custom_call" | custom-call | tf_op jit(solution)/shard_map/fine_attention/pallas_call | solution.py:216
  45.2 0.8 constant_dynamic-slice_fusion.2
  45.9 2.1 %collective-permute-start.3 = (bf16[272,256]{1,0:T(8,128)(2,1)}, bf16[272,256]{1,0:T(8,128)(2,1)S(1)}, u32[]{:S(2)}, u32[]{:S(2)}) collective-permute-start(bf16[272,256]{1,0:T(8,128)(2,1)} %get-tuple-element.48), channel_id=1, source_target_pairs={{0,2},{1,3},{2,0},{3,1},{4,6},{5,7},{6,4},{7,5},{8,10},{9,11},{10,... | collective-permute-start | bytes 417800 | tf_op jit(solution)/shard_map/ppermute | solution.py:44
  48.0 1.2 collective-permute-start.4
  49.5 6.9 %collective-permute-done.2.g1 = bf16[272,256]{1,0:T(8,128)(2,1)S(1)} collective-permute-done((bf16[272,256]{1,0:T(8,128)(2,1)}, bf16[272,256]{1,0:T(8,128)(2,1)S(1)}, u32[]{:S(2)}, u32[]{:S(2)}) %collective-permute-start.2) | collective-permute-done | bytes 139296 | tf_op jit(solution)/shard_map/ppermute | solution.py:44
  56.4 0.6 collective-permute-done.4.g3
  57.0 2.2 %fine_rows.1 = bf16[4,272,256]{2,1,0:T(8,128)(2,1)S(1)} custom-call(s32[3]{0:T(128)S(1)} %pad_add_fusion.1.place_ref.where_ref, s32[272,1]{1,0:T(8,128)S(1)} %broadcast_in_dim.31.ids_ref, bf16[256,1024]{1,0:T(8,128)(2,1)S(1)} %copy-done.2, bf16[272,256]{1,0:T(8,128)(2,1)S(1)} %get-tuple-element.50.g0, bf16[272,256]{1,0:T(8,128)(2,1)S(1)} %collective-permute-done.2.g1, ...), custom_call_target="tpu_custom_call" | custom-call | tf_op jit(solution)/shard_map/fine_rows/pallas_call | solution.py:216
  59.3 2.4 %collective-permute-start.13 = (bf16[272,256]{1,0:T(8,128)(2,1)S(1)}, bf16[272,256]{1,0:T(8,128)(2,1)S(1)}, u32[]{:S(2)}, u32[]{:S(2)}) collective-permute-start(bf16[272,256]{1,0:T(8,128)(2,1)S(1)} %get-tuple-element.44), channel_id=1, source_target_pairs={{0,3},{1,0},{2,1},{3,2},{4,7},{5,4},{6,5},{7,6},{8,11},{9,8},{10,9... | collective-permute-start | bytes 417800 | tf_op jit(solution)/shard_map/ppermute | solution.py:44
  61.7 0.9 collective-permute-start.9
  62.6 4.9 %collective-permute-done.13.group_ref.b3 = bf16[272,256]{1,0:T(8,128)(2,1)S(1)} collective-permute-done((bf16[272,256]{1,0:T(8,128)(2,1)S(1)}, bf16[272,256]{1,0:T(8,128)(2,1)S(1)}, u32[]{:S(2)}, u32[]{:S(2)}) %collective-permute-start.13) | collective-permute-done | bytes 139296 | tf_op jit(solution)/shard_map/ppermute | solution.py:44
  67.6 0.5 short_part.7
  68.1 1.7 collective-permute-done.11.group_ref.b2
  69.8 0.5 short_part.6
  70.3 3.7 %collective-permute-start.12 = (bf16[64,1024]{1,0:T(8,128)(2,1)S(1)}, bf16[64,1024]{1,0:T(8,128)(2,1)S(1)}, u32[]{:S(2)}, u32[]{:S(2)}) collective-permute-start(bf16[64,1024]{1,0:T(8,128)(2,1)S(1)} %short_part.6), channel_id=1, source_target_pairs={{0,2},{1,3},{2,0},{3,1},{4,6},{5,7},{6,4},{7,5},{8,10},{9,11},{10,... | collective-permute-start | bytes 393224 | tf_op jit(solution)/shard_map/ppermute | solution.py:44
  74.0 0.5 short_part.5
  74.7 0.5 short_part.4
  75.3 3.4 %collective-permute-done.12 = bf16[64,1024]{1,0:T(8,128)(2,1)S(1)} collective-permute-done((bf16[64,1024]{1,0:T(8,128)(2,1)S(1)}, bf16[64,1024]{1,0:T(8,128)(2,1)S(1)}, u32[]{:S(2)}, u32[]{:S(2)}) %collective-permute-start.12) | collective-permute-done | bytes 131104 | tf_op jit(solution)/shard_map/ppermute | solution.py:44
  78.7 0.9 collective-permute-done.10
  79.8 3.5 %collective-permute-start.16 = (bf16[64,1024]{1,0:T(8,128)(2,1)S(1)}, bf16[64,1024]{1,0:T(8,128)(2,1)S(1)}, u32[]{:S(2)}, u32[]{:S(2)}) collective-permute-start(bf16[64,1024]{1,0:T(8,128)(2,1)S(1)} %add_convert_fusion.s0), channel_id=1, source_target_pairs={{0,2},{1,3},{2,0},{3,1},{4,6},{5,7},{6,4},{7,5},{8,10},{9,11},{10,... | collective-permute-start | bytes 393224 | tf_op jit(solution)/shard_map/ppermute | solution.py:44
  83.3 4.1 %collective-permute-done.15.s1 = bf16[64,1024]{1,0:T(8,128)(2,1)S(1)} collective-permute-done((bf16[64,1024]{1,0:T(8,128)(2,1)S(1)}, bf16[64,1024]{1,0:T(8,128)(2,1)S(1)}, u32[]{:S(2)}, u32[]{:S(2)}) %collective-permute-start.15) | collective-permute-done | bytes 131104 | tf_op jit(solution)/shard_map/ppermute | solution.py:44
  87.4 1.6 collective-permute-done.16.s2
  89.0 1.6 coarse_pack.1
  90.6 12.2 %all_to_all.10.turned_ref = bf16[4,384,128]{2,1,0:T(8,128)(2,1)S(1)} all-to-all(bf16[4,384,128]{2,1,0:T(8,128)(2,1)S(1)} %get-tuple-element.30), channel_id=1, replica_groups=mesh['z'=4,'x'=4,'core'=2,'head'=4] {'z'}, dimensions={0} | all-to-all | bytes 786432 | tf_op jit(solution)/shard_map/all_to_all | solution.py:500
  102.8 0.7 collective-permute-start.20
  103.6 3.5 %collective-permute-start.19 = (bf16[4,256,128]{2,1,0:T(8,128)(2,1)S(1)}, bf16[4,256,128]{2,1,0:T(8,128)(2,1)S(1)}, u32[]{:S(2)}, u32[]{:S(2)}) collective-permute-start(bf16[4,256,128]{2,1,0:T(8,128)(2,1)S(1)} %get-tuple-element.55), channel_id=1, source_target_pairs={{0,16},{8,24},{16,0},{24,8},{1,17},{9,25},{17,1},{25,9},{2,18},{10... | collective-permute-start | bytes 786440 | tf_op jit(solution)/shard_map/ppermute | solution.py:44
  107.1 5.7 %collective-permute-done.20.n3 = bf16[4,256,128]{2,1,0:T(8,128)(2,1)S(1)} collective-permute-done((bf16[4,256,128]{2,1,0:T(8,128)(2,1)S(1)}, bf16[4,256,128]{2,1,0:T(8,128)(2,1)S(1)}, u32[]{:S(2)}, u32[]{:S(2)}) %collective-permute-start.20) | collective-permute-done | bytes 262176 | tf_op jit(solution)/shard_map/ppermute | solution.py:44
  112.8 2.8 %collective-permute-done.19.n2 = bf16[4,256,128]{2,1,0:T(8,128)(2,1)S(1)} collective-permute-done((bf16[4,256,128]{2,1,0:T(8,128)(2,1)S(1)}, bf16[4,256,128]{2,1,0:T(8,128)(2,1)S(1)}, u32[]{:S(2)}, u32[]{:S(2)}) %collective-permute-start.19) | collective-permute-done | bytes 262176 | tf_op jit(solution)/shard_map/ppermute | solution.py:44
  115.9 1.8 collective-permute-start.24
  117.7 0.9 collective-permute-start.22
  118.7 10.9 %collective-permute-done.24 = bf16[128,1024]{1,0:T(8,128)(2,1)S(1)} collective-permute-done((bf16[128,1024]{1,0:T(8,128)(2,1)S(1)}, bf16[128,1024]{1,0:T(8,128)(2,1)S(1)}, u32[]{:S(2)}, u32[]{:S(2)}) %collective-permute-start.24) | collective-permute-done | bytes 262176 | tf_op jit(solution)/shard_map/ppermute | solution.py:44
  129.6 3.4 %collective-permute-done.22 = bf16[128,1024]{1,0:T(8,128)(2,1)S(1)} collective-permute-done((bf16[128,1024]{1,0:T(8,128)(2,1)S(1)}, bf16[128,1024]{1,0:T(8,128)(2,1)S(1)}, u32[]{:S(2)}, u32[]{:S(2)}) %collective-permute-start.22) | collective-permute-done | bytes 262176 | tf_op jit(solution)/shard_map/ppermute | solution.py:44
  133.2 1.3 coarse_first.1
  134.6 5.6 %coarse_near.1 = (f32[1024,128]{1,0:T(8,128)S(1)}, f32[1024,128]{1,0:T(8,128)S(1)}, f32[1024,128]{1,0:T(8,128)S(1)}) custom-call(s32[8]{0:T(128)S(1)} %pad_add_fusion.2.chunk_ref, bf16[4,256,128]{2,1,0:T(8,128)(2,1)S(1)} %collective-permute-done.18.n1, bf16[4,256,128]{2,1,0:T(8,128)(2,1)S(1)} %collective-permute-done.19.n2, ...), custom_call_target="tpu_custom_call" | custom-call | tf_op jit(solution)/shard_map/coarse_near/pallas_call | solution.py:216
  140.2 5.9 %coarse_far.1 = bf16[4,128,128]{2,1,0:T(8,128)(2,1)S(1)} custom-call(s32[8]{0:T(128)S(1)} %pad_add_fusion.2.chunk_ref, bf16[4,4,256,128]{3,2,1,0:T(8,128)(2,1)S(1)} %collective-permute-done.21.far_ref, bf16[1024,128]{1,0:T(8,128)(2,1)S(1)} %get-tuple-element.32.q_ref, f32[1024,128]{1,0:T(8,128)S(1)} %get-tuple-element.36.top_in, ...), custom_call_target="tpu_custom_call" | custom-call | tf_op jit(solution)/shard_map/coarse_far/pallas_call | solution.py:216
  146.1 0.9 broadcast_in_dim.29
  147.0 3.6 %all-to-all-start.1 = ((bf16[16,128,128]{2,1,0:T(8,128)(2,1)}), bf16[16,128,128]{2,1,0:T(8,128)(2,1)S(1)}, u32[]{:S(2)}, u32[]{:S(2)}) async-start(bf16[16,128,128]{2,1,0:T(8,128)(2,1)} %bitcast.45), calls=%async_computation.1 | async-start | bytes 1048576 | tf_op jit(solution)/shard_map/all_to_all | solution.py:522
  150.6 12.6 %all-to-all-done.1.heads_ref = bf16[16,128,128]{2,1,0:T(8,128)(2,1)S(1)} async-done(((bf16[16,128,128]{2,1,0:T(8,128)(2,1)}), bf16[16,128,128]{2,1,0:T(8,128)(2,1)S(1)}, u32[]{:S(2)}, u32[]{:S(2)}) %all-to-all-start.1) | async-done | bytes 524320 | tf_op jit(solution)/shard_map/all_to_all | solution.py:522
  163.2 1.0 copy-done.4
  164.2 1.0 copy-done.15
  165.3 4.9 %feed.1 = (bf16[4,64,1024]{2,1,0:T(8,128)(2,1)S(1)}, f32[64,1024]{1,0:T(8,128)S(1)}) custom-call(s32[3]{0:T(128)S(1)} %pad_add_fusion.1.place_ref.where_ref, bf16[16,128,128]{2,1,0:T(8,128)(2,1)S(1)} %all-to-all-done.1.heads_ref, bf16[256,1024]{1,0:T(8,128)(2,1)S(1)} %copy-done.4, bf16[3,128,1024]{2,1,0:T(8,128)(2,1)S(1)} %pad_maximum_fusion.2.mine_ref, ...), custom_call_target="tpu_custom_call" | custom-call | tf_op jit(solution)/shard_map/feed/pallas_call | solution.py:216
  170.4 2.6 %collective-permute-start.27 = (bf16[64,1024]{1,0:T(8,128)(2,1)S(1)}, bf16[64,1024]{1,0:T(8,128)(2,1)S(1)}, u32[]{:S(2)}, u32[]{:S(2)}) collective-permute-start(bf16[64,1024]{1,0:T(8,128)(2,1)S(1)} %get-tuple-element.53), channel_id=1, source_target_pairs={{0,2},{1,3},{2,0},{3,1},{4,6},{5,7},{6,4},{7,5},{8,10},{9,11},{10,... | collective-permute-start | bytes 393224 | tf_op jit(solution)/shard_map/ppermute | solution.py:44
  173.0 3.7 %collective-permute-done.28 = bf16[64,1024]{1,0:T(8,128)(2,1)S(1)} collective-permute-done((bf16[64,1024]{1,0:T(8,128)(2,1)S(1)}, bf16[64,1024]{1,0:T(8,128)(2,1)S(1)}, u32[]{:S(2)}, u32[]{:S(2)}) %collective-permute-start.28) | collective-permute-done | bytes 131104 | tf_op jit(solution)/shard_map/ppermute | solution.py:44
  176.7 1.6 collective-permute-done.27
  178.3 2.2 %collective-permute-done.26 = bf16[64,1024]{1,0:T(8,128)(2,1)S(1)} collective-permute-done((bf16[64,1024]{1,0:T(8,128)(2,1)S(1)}, bf16[64,1024]{1,0:T(8,128)(2,1)S(1)}, u32[]{:S(2)}, u32[]{:S(2)}) %collective-permute-start.26) | collective-permute-done | bytes 131104 | tf_op jit(solution)/shard_map/ppermute | solution.py:44
  180.6 0.7 collective-permute-start.29
  181.3 1.7 collective-permute-start.30
  183.0 2.0 %collective-permute-start.31 = (bf16[64,1024]{1,0:T(8,128)(2,1)S(1)}, bf16[64,1024]{1,0:T(8,128)(2,1)S(1)}, u32[]{:S(2)}, u32[]{:S(2)}) collective-permute-start(bf16[64,1024]{1,0:T(8,128)(2,1)S(1)} %fusion.3.s0), channel_id=1, source_target_pairs={{0,3},{1,0},{2,1},{3,2},{4,7},{5,4},{6,5},{7,6},{8,11},{9,8},{10,9... | collective-permute-start | bytes 393224 | tf_op jit(solution)/shard_map/ppermute | solution.py:44
  185.0 0.5 copy.25
  185.5 4.2 %collective-permute-done.29.s1 = bf16[64,1024]{1,0:T(8,128)(2,1)S(1)} collective-permute-done((bf16[64,1024]{1,0:T(8,128)(2,1)S(1)}, bf16[64,1024]{1,0:T(8,128)(2,1)S(1)}, u32[]{:S(2)}, u32[]{:S(2)}) %collective-permute-start.29) | collective-permute-done | bytes 131104 | tf_op jit(solution)/shard_map/ppermute | solution.py:44
  189.7 0.6 collective-permute-done.31.s3
  190.3 2.7 %final.1 = bf16[1024,256]{1,0:T(8,128)(2,1)} custom-call(s32[3]{0:T(128)S(1)} %pad_add_fusion.1.place_ref.where_ref, bf16[64,1024]{1,0:T(8,128)(2,1)S(1)} %fusion.3.s0, bf16[64,1024]{1,0:T(8,128)(2,1)S(1)} %collective-permute-done.29.s1, bf16[64,1024]{1,0:T(8,128)(2,1)S(1)} %collective-permute-done.30.s2, bf16[64,1024]{1,0:T(8,128)(2,1)S(1)} %collective-permute-done.31.s3, ...), custom_call_target="tpu_custom_call" | custom-call | tf_op jit(solution)/shard_map/final/pallas_call | solution.py:216
  (101 shorter events, 2.5 us)
Async XLA Ops:
  0.0 28.7 %copy-start.22 = (f32[32,128]{1,0:T(8,128)S(1)}, f32[32,128]{1,0:T(8,128)}, u32[]{:S(2)}) copy-start(f32[32,128]{1,0:T(8,128)} %constant.102.clone.ca_ref) | copy-start | bytes 49156
  0.0 28.7 %copy-start.24 = (f32[32,128]{1,0:T(8,128)S(1)}, f32[32,128]{1,0:T(8,128)}, u32[]{:S(2)}) copy-start(f32[32,128]{1,0:T(8,128)} %constant.103.clone.sa_ref) | copy-start | bytes 49156
  0.0 28.7 %copy-start.6 = (f32[256,128]{1,0:T(8,128)S(1)}, f32[256,128]{1,0:T(8,128)}, u32[]{:S(2)}) copy-start(f32[256,128]{1,0:T(8,128)} %constant.104.clone.cb_ref) | copy-start | bytes 393220
  0.0 28.7 %copy-start.7 = (f32[256,128]{1,0:T(8,128)S(1)}, f32[256,128]{1,0:T(8,128)}, u32[]{:S(2)}) copy-start(f32[256,128]{1,0:T(8,128)} %constant.105.clone.sb_ref) | copy-start | bytes 393220
  0.0 28.4 %copy-start.30 = (s32[1024]{0:T(1024)S(1)}, s32[1024]{0:T(1024)}, u32[]{:S(2)}) copy-start(s32[1024]{0:T(1024)} %param.21) | copy-start | bytes 12292
  0.0 28.7 %copy-start.2 = (bf16[256,1024]{1,0:T(8,128)(2,1)S(1)}, bf16[256,1024]{1,0:T(8,128)(2,1)}, u32[]{:S(2)}) copy-start(bf16[256,1024]{1,0:T(8,128)(2,1)} %emb_ref.3) | copy-start | bytes 1572868
  0.0 28.7 %copy-start.27 = (f32[1024]{0:T(1024)S(1)}, f32[1024]{0:T(1024)}, u32[]{:S(2)}) copy-start(f32[1024]{0:T(1024)} %param.23) | copy-start | bytes 12292
  0.1 28.7 %copy-start.16 = (bf16[1024,256]{1,0:T(8,128)(2,1)S(1)}, bf16[1024,256]{1,0:T(8,128)(2,1)}, u32[]{:S(2)}) copy-start(bf16[1024,256]{1,0:T(8,128)(2,1)} %wq_ref.2) | copy-start | bytes 1572868
  0.1 8.2 %collective-permute-start.1 = (s32[1024]{0:T(1024)}, s32[1024]{0:T(1024)S(1)}, u32[]{:S(2)}, u32[]{:S(2)}) collective-permute-start(s32[1024]{0:T(1024)} %param.21), channel_id=1, source_target_pairs={{0,4},{4,8},{8,12},{12,16},{16,20},{20,24},{24,28},{28,32},{32,36}... | collective-permute-start | bytes 12296 | tf_op jit(solution)/shard_map/ppermute | solution.py:48
  2.8 5.5 %collective-permute-start = (s32[256]{0:T(256)S(1)}, s32[256]{0:T(256)S(1)}, u32[]{:S(2)}, u32[]{:S(2)}) collective-permute-start(s32[256]{0:T(256)S(1)} %slice.9), channel_id=1, source_target_pairs={{0,8},{4,12},{8,16},{12,20},{16,24},{20,28},{24,32},{28,36},{32,40... | collective-permute-start | bytes 3080 | tf_op jit(solution)/shard_map/ppermute | solution.py:48
  9.3 15.2 %collective-permute-start.7 = (bf16[128,1024]{1,0:T(8,128)(2,1)S(1)}, bf16[128,1024]{1,0:T(8,128)(2,1)S(1)}, u32[]{:S(2)}, u32[]{:S(2)}) collective-permute-start(bf16[128,1024]{1,0:T(8,128)(2,1)S(1)} %constant_dynamic-slice_fusion.1), channel_id=1, source_target_pairs={{0,3},{1,0},{2,1},{3,2},{4,7},{5,4},{6,5},{7,6},{8,11},{9,8},{10,9... | collective-permute-start | bytes 786440 | tf_op jit(solution)/shard_map/ppermute | solution.py:44
  12.3 12.1 %collective-permute-start.6 = (bf16[128,1024]{1,0:T(8,128)(2,1)S(1)}, bf16[128,1024]{1,0:T(8,128)(2,1)S(1)}, u32[]{:S(2)}, u32[]{:S(2)}) collective-permute-start(bf16[128,1024]{1,0:T(8,128)(2,1)S(1)} %constant_dynamic-slice_fusion.1), channel_id=1, source_target_pairs={{0,2},{1,3},{2,0},{3,1},{4,6},{5,7},{6,4},{7,5},{8,10},{9,11},{10,... | collective-permute-start | bytes 786440 | tf_op jit(solution)/shard_map/ppermute | solution.py:44
  13.0 15.2 %collective-permute-start.5 = (bf16[128,1024]{1,0:T(8,128)(2,1)S(1)}, bf16[128,1024]{1,0:T(8,128)(2,1)S(1)}, u32[]{:S(2)}, u32[]{:S(2)}) collective-permute-start(bf16[128,1024]{1,0:T(8,128)(2,1)S(1)} %constant_dynamic-slice_fusion.1), channel_id=1, source_target_pairs={{0,1},{1,2},{2,3},{3,0},{4,5},{5,6},{6,7},{7,4},{8,9},{9,10},{10,1... | collective-permute-start | bytes 786440 | tf_op jit(solution)/shard_map/ppermute | solution.py:44
  28.3 28.7 %collective-permute-start.8 = (bf16[3,128,1024]{2,1,0:T(8,128)(2,1)S(1)}, bf16[3,128,1024]{2,1,0:T(8,128)(2,1)S(1)}, u32[]{:S(2)}, u32[]{:S(2)}) collective-permute-start(bf16[3,128,1024]{2,1,0:T(8,128)(2,1)S(1)} %pad_maximum_fusion.1.mine_ref), channel_id=1, source_target_pairs={{0,4},{4,0},{1,5},{5,1},{2,6},{6,2},{3,7},{7,3},{8,12},{12,8},{9,1... | collective-permute-start | bytes 2359304 | tf_op jit(solution)/shard_map/ppermute | solution.py:44
  28.8 1.0 copy-start.17
  29.8 1.0 copy-start.18
  33.3 23.7 %copy-start.5 = (bf16[256,1024]{1,0:T(8,128)(2,1)S(1)}, bf16[256,1024]{1,0:T(8,128)(2,1)}, u32[]{:S(2)}) copy-start(bf16[256,1024]{1,0:T(8,128)(2,1)} %own_ref.2) | copy-start | bytes 1572868
  45.9 10.4 %collective-permute-start.2 = (bf16[272,256]{1,0:T(8,128)(2,1)}, bf16[272,256]{1,0:T(8,128)(2,1)S(1)}, u32[]{:S(2)}, u32[]{:S(2)}) collective-permute-start(bf16[272,256]{1,0:T(8,128)(2,1)} %get-tuple-element.49), channel_id=1, source_target_pairs={{0,1},{1,2},{2,3},{3,0},{4,5},{5,6},{6,7},{7,4},{8,9},{9,10},{10,1... | collective-permute-start | bytes 417800 | tf_op jit(solution)/shard_map/ppermute | solution.py:44
  45.9 10.4 %collective-permute-start.3 = (bf16[272,256]{1,0:T(8,128)(2,1)}, bf16[272,256]{1,0:T(8,128)(2,1)S(1)}, u32[]{:S(2)}, u32[]{:S(2)}) collective-permute-start(bf16[272,256]{1,0:T(8,128)(2,1)} %get-tuple-element.48), channel_id=1, source_target_pairs={{0,2},{1,3},{2,0},{3,1},{4,6},{5,7},{6,4},{7,5},{8,10},{9,11},{10,... | collective-permute-start | bytes 417800 | tf_op jit(solution)/shard_map/ppermute | solution.py:44
  48.0 9.0 %collective-permute-start.4 = (bf16[272,256]{1,0:T(8,128)(2,1)}, bf16[272,256]{1,0:T(8,128)(2,1)S(1)}, u32[]{:S(2)}, u32[]{:S(2)}) collective-permute-start(bf16[272,256]{1,0:T(8,128)(2,1)} %get-tuple-element.47), channel_id=1, source_target_pairs={{0,3},{1,0},{2,1},{3,2},{4,7},{5,4},{6,5},{7,6},{8,11},{9,8},{10,9... | collective-permute-start | bytes 417800 | tf_op jit(solution)/shard_map/ppermute | solution.py:44
  57.0 10.6 %copy-start = (bf16[4,256,1024]{2,1,0:T(8,128)(2,1)S(1)}, bf16[4,256,1024]{2,1,0:T(8,128)(2,1)}, u32[]{:S(2)}) copy-start(bf16[4,256,1024]{2,1,0:T(8,128)(2,1)} %w_ref.7) | copy-start | bytes 6291460
  59.3 8.3 %collective-permute-start.13 = (bf16[272,256]{1,0:T(8,128)(2,1)S(1)}, bf16[272,256]{1,0:T(8,128)(2,1)S(1)}, u32[]{:S(2)}, u32[]{:S(2)}) collective-permute-start(bf16[272,256]{1,0:T(8,128)(2,1)S(1)} %get-tuple-element.44), channel_id=1, source_target_pairs={{0,3},{1,0},{2,1},{3,2},{4,7},{5,4},{6,5},{7,6},{8,11},{9,8},{10,9... | collective-permute-start | bytes 417800 | tf_op jit(solution)/shard_map/ppermute | solution.py:44
  61.7 8.1 %collective-permute-start.11 = (bf16[272,256]{1,0:T(8,128)(2,1)S(1)}, bf16[272,256]{1,0:T(8,128)(2,1)S(1)}, u32[]{:S(2)}, u32[]{:S(2)}) collective-permute-start(bf16[272,256]{1,0:T(8,128)(2,1)S(1)} %get-tuple-element.45), channel_id=1, source_target_pairs={{0,2},{1,3},{2,0},{3,1},{4,6},{5,7},{6,4},{7,5},{8,10},{9,11},{10,... | collective-permute-start | bytes 417800 | tf_op jit(solution)/shard_map/ppermute | solution.py:44
  61.7 12.3 %collective-permute-start.9 = (bf16[272,256]{1,0:T(8,128)(2,1)S(1)}, bf16[272,256]{1,0:T(8,128)(2,1)S(1)}, u32[]{:S(2)}, u32[]{:S(2)}) collective-permute-start(bf16[272,256]{1,0:T(8,128)(2,1)S(1)} %get-tuple-element.46), channel_id=1, source_target_pairs={{0,1},{1,2},{2,3},{3,0},{4,5},{5,6},{6,7},{7,4},{8,9},{9,10},{10,1... | collective-permute-start | bytes 417800 | tf_op jit(solution)/shard_map/ppermute | solution.py:44
  67.6 2.7 %copy-start.8 = (bf16[272,256]{1,0:T(8,128)(2,1)}, bf16[272,256]{1,0:T(8,128)(2,1)S(1)}, u32[]{:S(2)}) copy-start(bf16[272,256]{1,0:T(8,128)(2,1)S(1)} %collective-permute-done.13.group_ref.b3) | copy-start | bytes 417796
  68.1 7.2 %collective-permute-start.14 = (bf16[64,1024]{1,0:T(8,128)(2,1)S(1)}, bf16[64,1024]{1,0:T(8,128)(2,1)S(1)}, u32[]{:S(2)}, u32[]{:S(2)}) collective-permute-start(bf16[64,1024]{1,0:T(8,128)(2,1)S(1)} %short_part.7), channel_id=1, source_target_pairs={{0,1},{1,2},{2,3},{3,0},{4,5},{5,6},{6,7},{7,4},{8,9},{9,10},{10,1... | collective-permute-start | bytes 393224 | tf_op jit(solution)/shard_map/ppermute | solution.py:44
  69.8 4.7 %copy-start.10 = (bf16[272,256]{1,0:T(8,128)(2,1)}, bf16[272,256]{1,0:T(8,128)(2,1)S(1)}, u32[]{:S(2)}) copy-start(bf16[272,256]{1,0:T(8,128)(2,1)S(1)} %collective-permute-done.11.group_ref.b2) | copy-start | bytes 417796
  70.3 8.4 %collective-permute-start.12 = (bf16[64,1024]{1,0:T(8,128)(2,1)S(1)}, bf16[64,1024]{1,0:T(8,128)(2,1)S(1)}, u32[]{:S(2)}, u32[]{:S(2)}) collective-permute-start(bf16[64,1024]{1,0:T(8,128)(2,1)S(1)} %short_part.6), channel_id=1, source_target_pairs={{0,2},{1,3},{2,0},{3,1},{4,6},{5,7},{6,4},{7,5},{8,10},{9,11},{10,... | collective-permute-start | bytes 393224 | tf_op jit(solution)/shard_map/ppermute | solution.py:44
  74.0 1.1 copy-start.12
  74.5 14.5 %copy-start.19 = (bf16[1024,256]{1,0:T(8,128)(2,1)S(1)}, bf16[1024,256]{1,0:T(8,128)(2,1)}, u32[]{:S(2)}) copy-start(bf16[1024,256]{1,0:T(8,128)(2,1)} %wq_ref.3) | copy-start | bytes 1572868
  74.5 14.5 %copy-start.20 = (bf16[1024,256]{1,0:T(8,128)(2,1)S(1)}, bf16[1024,256]{1,0:T(8,128)(2,1)}, u32[]{:S(2)}) copy-start(bf16[1024,256]{1,0:T(8,128)(2,1)} %wk_ref.3) | copy-start | bytes 1572868
  74.5 14.4 %copy-start.21 = (bf16[1024,256]{1,0:T(8,128)(2,1)S(1)}, bf16[1024,256]{1,0:T(8,128)(2,1)}, u32[]{:S(2)}) copy-start(bf16[1024,256]{1,0:T(8,128)(2,1)} %wv_ref.3) | copy-start | bytes 1572868
  74.5 14.4 %copy-start.23 = (f32[32,128]{1,0:T(8,128)S(1)}, f32[32,128]{1,0:T(8,128)}, u32[]{:S(2)}) copy-start(f32[32,128]{1,0:T(8,128)} %constant.102.clone.ca_ref) | copy-start | bytes 49156
  74.6 14.4 %copy-start.25 = (f32[32,128]{1,0:T(8,128)S(1)}, f32[32,128]{1,0:T(8,128)}, u32[]{:S(2)}) copy-start(f32[32,128]{1,0:T(8,128)} %constant.103.clone.sa_ref) | copy-start | bytes 49156
  74.6 14.4 %copy-start.28 = (f32[1024]{0:T(1024)S(1)}, f32[1024]{0:T(1024)}, u32[]{:S(2)}) copy-start(f32[1024]{0:T(1024)} %param.29) | copy-start | bytes 12292
  74.6 5.0 %collective-permute-start.10 = (bf16[64,1024]{1,0:T(8,128)(2,1)S(1)}, bf16[64,1024]{1,0:T(8,128)(2,1)S(1)}, u32[]{:S(2)}, u32[]{:S(2)}) collective-permute-start(bf16[64,1024]{1,0:T(8,128)(2,1)S(1)} %short_part.5), channel_id=1, source_target_pairs={{0,3},{1,0},{2,1},{3,2},{4,7},{5,4},{6,5},{7,6},{8,11},{9,8},{10,9... | collective-permute-start | bytes 393224 | tf_op jit(solution)/shard_map/ppermute | solution.py:44
  79.7 7.7 %collective-permute-start.15 = (bf16[64,1024]{1,0:T(8,128)(2,1)S(1)}, bf16[64,1024]{1,0:T(8,128)(2,1)S(1)}, u32[]{:S(2)}, u32[]{:S(2)}) collective-permute-start(bf16[64,1024]{1,0:T(8,128)(2,1)S(1)} %add_convert_fusion.s0), channel_id=1, source_target_pairs={{0,1},{1,2},{2,3},{3,0},{4,5},{5,6},{6,7},{7,4},{8,9},{9,10},{10,1... | collective-permute-start | bytes 393224 | tf_op jit(solution)/shard_map/ppermute | solution.py:44
  79.8 9.1 %collective-permute-start.16 = (bf16[64,1024]{1,0:T(8,128)(2,1)S(1)}, bf16[64,1024]{1,0:T(8,128)(2,1)S(1)}, u32[]{:S(2)}, u32[]{:S(2)}) collective-permute-start(bf16[64,1024]{1,0:T(8,128)(2,1)S(1)} %add_convert_fusion.s0), channel_id=1, source_target_pairs={{0,2},{1,3},{2,0},{3,1},{4,6},{5,7},{6,4},{7,5},{8,10},{9,11},{10,... | collective-permute-start | bytes 393224 | tf_op jit(solution)/shard_map/ppermute | solution.py:44
  83.3 5.7 %collective-permute-start.17 = (bf16[64,1024]{1,0:T(8,128)(2,1)S(1)}, bf16[64,1024]{1,0:T(8,128)(2,1)S(1)}, u32[]{:S(2)}, u32[]{:S(2)}) collective-permute-start(bf16[64,1024]{1,0:T(8,128)(2,1)S(1)} %add_convert_fusion.s0), channel_id=1, source_target_pairs={{0,3},{1,0},{2,1},{3,2},{4,7},{5,4},{6,5},{7,6},{8,11},{9,8},{10,9... | collective-permute-start | bytes 393224 | tf_op jit(solution)/shard_map/ppermute | solution.py:44
  90.6 25.3 %copy-start.14 = (bf16[256,1024]{1,0:T(8,128)(2,1)}, bf16[256,1024]{1,0:T(8,128)(2,1)S(1)}, u32[]{:S(2)}) copy-start(bf16[256,1024]{1,0:T(8,128)(2,1)S(1)} %get-tuple-element.40.short_ref) | copy-start | bytes 1572868
  90.6 25.3 %copy-start.3 = (bf16[256,1024]{1,0:T(8,128)(2,1)S(1)}, bf16[256,1024]{1,0:T(8,128)(2,1)}, u32[]{:S(2)}) copy-start(bf16[256,1024]{1,0:T(8,128)(2,1)} %own_ref.3) | copy-start | bytes 1572868
  102.8 10.0 %collective-permute-start.20 = (bf16[4,256,128]{2,1,0:T(8,128)(2,1)S(1)}, bf16[4,256,128]{2,1,0:T(8,128)(2,1)S(1)}, u32[]{:S(2)}, u32[]{:S(2)}) collective-permute-start(bf16[4,256,128]{2,1,0:T(8,128)(2,1)S(1)} %get-tuple-element.55), channel_id=1, source_target_pairs={{0,24},{8,0},{16,8},{24,16},{1,25},{9,1},{17,9},{25,17},{2,26},{10... | collective-permute-start | bytes 786440 | tf_op jit(solution)/shard_map/ppermute | solution.py:44
  103.6 12.1 %collective-permute-start.19 = (bf16[4,256,128]{2,1,0:T(8,128)(2,1)S(1)}, bf16[4,256,128]{2,1,0:T(8,128)(2,1)S(1)}, u32[]{:S(2)}, u32[]{:S(2)}) collective-permute-start(bf16[4,256,128]{2,1,0:T(8,128)(2,1)S(1)} %get-tuple-element.55), channel_id=1, source_target_pairs={{0,16},{8,24},{16,0},{24,8},{1,17},{9,25},{17,1},{25,9},{2,18},{10... | collective-permute-start | bytes 786440 | tf_op jit(solution)/shard_map/ppermute | solution.py:44
  107.1 8.5 %collective-permute-start.18 = (bf16[4,256,128]{2,1,0:T(8,128)(2,1)S(1)}, bf16[4,256,128]{2,1,0:T(8,128)(2,1)S(1)}, u32[]{:S(2)}, u32[]{:S(2)}) collective-permute-start(bf16[4,256,128]{2,1,0:T(8,128)(2,1)S(1)} %get-tuple-element.55), channel_id=1, source_target_pairs={{0,8},{8,16},{16,24},{24,0},{1,9},{9,17},{17,25},{25,1},{2,10},{10... | collective-permute-start | bytes 786440 | tf_op jit(solution)/shard_map/ppermute | solution.py:44
  115.8 24.4 %collective-permute-start.21 = (bf16[4,4,256,128]{3,2,1,0:T(8,128)(2,1)S(1)}, bf16[4,4,256,128]{3,2,1,0:T(8,128)(2,1)S(1)}, u32[]{:S(2)}, u32[]{:S(2)}) collective-permute-start(bf16[4,4,256,128]{3,2,1,0:T(8,128)(2,1)S(1)} %pad_maximum_fusion), channel_id=1, source_target_pairs={{0,4},{4,0},{1,5},{5,1},{2,6},{6,2},{3,7},{7,3},{8,12},{12,8},{9,1... | collective-permute-start | bytes 3145736 | tf_op jit(solution)/shard_map/ppermute | solution.py:44
  115.9 13.7 %collective-permute-start.24 = (bf16[128,1024]{1,0:T(8,128)(2,1)S(1)}, bf16[128,1024]{1,0:T(8,128)(2,1)S(1)}, u32[]{:S(2)}, u32[]{:S(2)}) collective-permute-start(bf16[128,1024]{1,0:T(8,128)(2,1)S(1)} %constant_dynamic-slice_fusion), channel_id=1, source_target_pairs={{0,3},{1,0},{2,1},{3,2},{4,7},{5,4},{6,5},{7,6},{8,11},{9,8},{10,9... | collective-permute-start | bytes 786440 | tf_op jit(solution)/shard_map/ppermute | solution.py:44
  117.7 11.9 %collective-permute-start.23 = (bf16[128,1024]{1,0:T(8,128)(2,1)S(1)}, bf16[128,1024]{1,0:T(8,128)(2,1)S(1)}, u32[]{:S(2)}, u32[]{:S(2)}) collective-permute-start(bf16[128,1024]{1,0:T(8,128)(2,1)S(1)} %constant_dynamic-slice_fusion), channel_id=1, source_target_pairs={{0,2},{1,3},{2,0},{3,1},{4,6},{5,7},{6,4},{7,5},{8,10},{9,11},{10,... | collective-permute-start | bytes 786440 | tf_op jit(solution)/shard_map/ppermute | solution.py:44
  117.7 15.2 %collective-permute-start.22 = (bf16[128,1024]{1,0:T(8,128)(2,1)S(1)}, bf16[128,1024]{1,0:T(8,128)(2,1)S(1)}, u32[]{:S(2)}, u32[]{:S(2)}) collective-permute-start(bf16[128,1024]{1,0:T(8,128)(2,1)S(1)} %constant_dynamic-slice_fusion), channel_id=1, source_target_pairs={{0,1},{1,2},{2,3},{3,0},{4,5},{5,6},{6,7},{7,4},{8,9},{9,10},{10,1... | collective-permute-start | bytes 786440 | tf_op jit(solution)/shard_map/ppermute | solution.py:44
  133.1 17.6 %collective-permute-start.25 = (bf16[3,128,1024]{2,1,0:T(8,128)(2,1)S(1)}, bf16[3,128,1024]{2,1,0:T(8,128)(2,1)}, u32[]{:S(2)}, u32[]{:S(2)}) collective-permute-start(bf16[3,128,1024]{2,1,0:T(8,128)(2,1)S(1)} %pad_maximum_fusion.2.mine_ref), channel_id=1, source_target_pairs={{0,4},{4,0},{1,5},{5,1},{2,6},{6,2},{3,7},{7,3},{8,12},{12,8},{9,1... | collective-permute-start | bytes 2359304 | tf_op jit(solution)/shard_map/ppermute | solution.py:44
  140.2 23.0 %copy-start.1 = (bf16[1024,1024]{1,0:T(8,128)(2,1)S(1)}, bf16[1024,1024]{1,0:T(8,128)(2,1)}, u32[]{:S(2)}) copy-start(bf16[1024,1024]{1,0:T(8,128)(2,1)} %up_ref.1) | copy-start | bytes 6291460
  140.2 23.0 %copy-start.26 = (f32[1024]{0:T(1024)S(1)}, f32[1024]{0:T(1024)}, u32[]{:S(2)}) copy-start(f32[1024]{0:T(1024)} %param.34) | copy-start | bytes 12292
  147.0 16.1 %all-to-all-start.1 = ((bf16[16,128,128]{2,1,0:T(8,128)(2,1)}), bf16[16,128,128]{2,1,0:T(8,128)(2,1)S(1)}, u32[]{:S(2)}, u32[]{:S(2)}) async-start(bf16[16,128,128]{2,1,0:T(8,128)(2,1)} %bitcast.45), calls=%async_computation.1 | async-start | bytes 1048576 | tf_op jit(solution)/shard_map/all_to_all | solution.py:522
  163.2 1.0 copy-start.4
  164.2 1.0 copy-start.15
  165.3 19.7 %copy-start.29 = (bf16[1024,4,256]{2,1,0:T(4,128)(2,1)S(1)}, bf16[1024,4,256]{2,1,0:T(4,128)(2,1)}, u32[]{:S(2)}) copy-start(bf16[1024,4,256]{2,1,0:T(4,128)(2,1)} %param.37) | copy-start | bytes 6291460
  170.3 6.4 %collective-permute-start.28 = (bf16[64,1024]{1,0:T(8,128)(2,1)S(1)}, bf16[64,1024]{1,0:T(8,128)(2,1)S(1)}, u32[]{:S(2)}, u32[]{:S(2)}) collective-permute-start(bf16[64,1024]{1,0:T(8,128)(2,1)S(1)} %get-tuple-element.52), channel_id=1, source_target_pairs={{0,3},{1,0},{2,1},{3,2},{4,7},{5,4},{6,5},{7,6},{8,11},{9,8},{10,9... | collective-permute-start | bytes 393224 | tf_op jit(solution)/shard_map/ppermute | solution.py:44
  170.4 7.9 %collective-permute-start.27 = (bf16[64,1024]{1,0:T(8,128)(2,1)S(1)}, bf16[64,1024]{1,0:T(8,128)(2,1)S(1)}, u32[]{:S(2)}, u32[]{:S(2)}) collective-permute-start(bf16[64,1024]{1,0:T(8,128)(2,1)S(1)} %get-tuple-element.53), channel_id=1, source_target_pairs={{0,2},{1,3},{2,0},{3,1},{4,6},{5,7},{6,4},{7,5},{8,10},{9,11},{10,... | collective-permute-start | bytes 393224 | tf_op jit(solution)/shard_map/ppermute | solution.py:44
  173.0 7.4 %collective-permute-start.26 = (bf16[64,1024]{1,0:T(8,128)(2,1)S(1)}, bf16[64,1024]{1,0:T(8,128)(2,1)S(1)}, u32[]{:S(2)}, u32[]{:S(2)}) collective-permute-start(bf16[64,1024]{1,0:T(8,128)(2,1)S(1)} %get-tuple-element.51), channel_id=1, source_target_pairs={{0,1},{1,2},{2,3},{3,0},{4,5},{5,6},{6,7},{7,4},{8,9},{9,10},{10,1... | collective-permute-start | bytes 393224 | tf_op jit(solution)/shard_map/ppermute | solution.py:44
  180.6 9.2 %collective-permute-start.29 = (bf16[64,1024]{1,0:T(8,128)(2,1)S(1)}, bf16[64,1024]{1,0:T(8,128)(2,1)S(1)}, u32[]{:S(2)}, u32[]{:S(2)}) collective-permute-start(bf16[64,1024]{1,0:T(8,128)(2,1)S(1)} %fusion.3.s0), channel_id=1, source_target_pairs={{0,1},{1,2},{2,3},{3,0},{4,5},{5,6},{6,7},{7,4},{8,9},{9,10},{10,1... | collective-permute-start | bytes 393224 | tf_op jit(solution)/shard_map/ppermute | solution.py:44
  181.3 8.4 %collective-permute-start.30 = (bf16[64,1024]{1,0:T(8,128)(2,1)S(1)}, bf16[64,1024]{1,0:T(8,128)(2,1)S(1)}, u32[]{:S(2)}, u32[]{:S(2)}) collective-permute-start(bf16[64,1024]{1,0:T(8,128)(2,1)S(1)} %fusion.3.s0), channel_id=1, source_target_pairs={{0,2},{1,3},{2,0},{3,1},{4,6},{5,7},{6,4},{7,5},{8,10},{9,11},{10,... | collective-permute-start | bytes 393224 | tf_op jit(solution)/shard_map/ppermute | solution.py:44
  183.0 7.3 %collective-permute-start.31 = (bf16[64,1024]{1,0:T(8,128)(2,1)S(1)}, bf16[64,1024]{1,0:T(8,128)(2,1)S(1)}, u32[]{:S(2)}, u32[]{:S(2)}) collective-permute-start(bf16[64,1024]{1,0:T(8,128)(2,1)S(1)} %fusion.3.s0), channel_id=1, source_target_pairs={{0,3},{1,0},{2,1},{3,2},{4,7},{5,4},{6,5},{7,6},{8,11},{9,8},{10,9... | collective-permute-start | bytes 393224 | tf_op jit(solution)/shard_map/ppermute | solution.py:44
  185.0 5.3 %copy-start.9 = (bf16[272,256]{1,0:T(8,128)(2,1)S(1)}, bf16[272,256]{1,0:T(8,128)(2,1)}, u32[]{:S(2)}) copy-start(bf16[272,256]{1,0:T(8,128)(2,1)} %copy-done.8) | copy-start | bytes 417796
  185.0 5.3 %copy-start.11 = (bf16[272,256]{1,0:T(8,128)(2,1)S(1)}, bf16[272,256]{1,0:T(8,128)(2,1)}, u32[]{:S(2)}) copy-start(bf16[272,256]{1,0:T(8,128)(2,1)} %copy-done.10) | copy-start | bytes 417796
  185.0 5.3 %copy-start.13 = (bf16[272,256]{1,0:T(8,128)(2,1)S(1)}, bf16[272,256]{1,0:T(8,128)(2,1)}, u32[]{:S(2)}) copy-start(bf16[272,256]{1,0:T(8,128)(2,1)} %copy-done.12) | copy-start | bytes 417796

commit v2 on v1

--- a/solution.py
+++ b/solution.py
@@ -101,10 +101,15 @@
 
 
 def fine_own_kernel(
-    ids_ref, emb_ref, gain_ref, wq_ref, wk_ref, wv_ref, ca_ref, sa_ref, cb_ref, sb_ref,
-    tab_ref, q_ref, k_ref, v_ref,
+    ids_ref, emb_ref, gain_ref, ca_ref, sa_ref, cb_ref, sb_ref, wq_hbm, wk_hbm, wv_hbm,
+    tab_ref, q_ref, k_ref, v_ref, w_ref, sems,
 ):
+    copies = begin_copies(
+        [(w, w_ref.at[n]) for n, w in enumerate((wq_hbm, wk_hbm, wv_hbm))], sems
+    )
+    wq_ref, wk_ref, wv_ref = (w_ref.at[n] for n in range(3))
     fine_in = norm_rows(emb_ref[...].astype(f32), gain_ref[...])
+    finish_copies(copies)
     tq = dot(fine_in, wq_ref[...]) * q_scale
     tk = dot(fine_in, wk_ref[...])
     for n, table in enumerate((tq, partner(tq), tk, partner(tk))):
@@ -178,7 +183,9 @@
     ]
     first_bias = jnp.where(col > row, 0.0, masked_low) + biases[0]
     last_bias = jnp.where(col <= row, 0.0, masked_low)
-    result = jnp.zeros((BLOCK, SHARE), f32)
+    ones = jnp.ones((PAST, 128), bf16)
+    low_lanes = lax.broadcasted_iota(jnp.int32, (1, 128), 1) < 64
+    results = []
     for h in range(4):
         scores = dot_t(jnp.where(head_lane == h, query, jnp.zeros_like(query)), keys)
         tiles = [scores[:, t * BLOCK : (t + 1) * BLOCK] for t in range(5)]
@@ -191,13 +198,14 @@
         for t in range(1, 5):
             peak = jnp.maximum(peak, tiles[t])
         top = jnp.max(peak, axis=1, keepdims=True)
-        weights = [jnp.exp2(tile - top) for tile in tiles]
-        summed = weights[0]
-        for t in range(1, 5):
-            summed = summed + weights[t]
-        total = jnp.sum(summed, axis=1, keepdims=True)
-        mixed = dot(jnp.concatenate([w.astype(bf16) for w in weights], axis=1), values)
-        result = jnp.where(head_lane == h, mixed / total, result)
+        weights = [jnp.exp2(tile - top).astype(bf16) for tile in tiles]
+        pair = (h // 2) * 128
+        wide = jnp.concatenate([values[:, pair : pair + 128], ones], axis=1)
+        mixed = dot(jnp.concatenate(weights, axis=1), wide)
+        results.append(mixed[:, :128] / mixed[:, 128:])
+    result = jnp.concatenate(
+        [jnp.where(low_lanes, results[2 * n], results[2 * n + 1]) for n in range(2)], axis=1
+    )
     at = pl.multiple_of(HALO + step * BLOCK, HALO)
     out_ref[pl.ds(at, BLOCK), :] = result.astype(bf16)
 
@@ -210,34 +218,54 @@
     return pl.BlockSpec(memory_space=pltpu.SMEM)
 
 
-def call(kernel, name, shapes, scalars, arrays, scratch=(), grid=None, limit=48):
+def call(kernel, name, shapes, scalars, arrays, scratch=(), grid=None, limit=48, us=2, hbm=()):
     one = not isinstance(shapes, (list, tuple))
     extra = {} if grid is None else {"grid": grid}
     return pl.pallas_call(
         kernel,
         out_shape=shapes,
-        in_specs=[smem()] * len(scalars) + [vmem()] * len(arrays),
+        in_specs=[smem()] * len(scalars)
+        + [vmem()] * len(arrays)
+        + [pl.BlockSpec(memory_space=pl.ANY)] * len(hbm),
         out_specs=vmem() if one else [vmem()] * len(shapes),
         scratch_shapes=list(scratch),
         compiler_params=pltpu.CompilerParams(vmem_limit_bytes=limit << 20),
+        cost_estimate=pl.CostEstimate(
+            flops=us * 10**9, transcendentals=0, bytes_accessed=us * 2 * 10**6
+        ),
         name=name,
         **extra,
-    )(*scalars, *arrays)
-
-
-def half_lanes(ref, quarter, half):
-    begin = pl.multiple_of(quarter * 256 + half * 128, 128)
-    return ref[:, pl.ds(begin, 128)]
+    )(*scalars, *arrays, *hbm)
+
+
+def begin_copies(pairs, sems):
+    copies = [pltpu.make_async_copy(a, b, sems.at[n]) for n, (a, b) in enumerate(pairs)]
+    for copy in copies:
+        copy.start()
+    return copies
+
+
+def finish_copies(copies):
+    for copy in copies:
+        copy.wait()
 
 
 def fine_rows_kernel(
-    where_ref, ids_ref, emb_ref, g0, g1, g2, g3, own_ref, mine_ref, other_ref, out_ref
+    where_ref, ids_ref, emb_ref, g0, g1, g2, g3, own_hbm, mine_hbm, other_hbm, out_ref, w_ref, sems
 ):
     place, head, core = where_ref[0], where_ref[1], where_ref[2]
-    merged = dot(pick(ids_ref[...]), emb_ref[...]) + dot(g0[...], own_ref[...])
-    for s, got in ((1, g1), (2, g2), (3, g3)):
-        merged += dot(half_lanes(got, 0, core), mine_ref[s - 1])
-        merged += dot(half_lanes(got, 0, 1 - core), other_ref[s - 1])
+    copies = begin_copies(
+        [(own_hbm, w_ref.at[0:256])]
+        + [(mine_hbm.at[s - 1], w_ref.at[pl.ds(s * 256 + core * 128, 128)]) for s in range(1, 4)]
+        + [
+            (other_hbm.at[s - 1], w_ref.at[pl.ds(s * 256 + 128 - core * 128, 128)])
+            for s in range(1, 4)
+        ],
+        sems,
+    )
+    merged = dot(pick(ids_ref[...]), emb_ref[...])
+    finish_copies(copies)
+    merged += dot(jnp.concatenate([g0[...], g1[...], g2[...], g3[...]], axis=1), w_ref[...])
     rows = 256 + HALO
     token = (
         place * ROWS + head * 256 - HALO + lax.broadcasted_iota(jnp.int32, (rows, D), 0)
@@ -296,6 +324,10 @@
         out_ref[h, COARSE_ROWS : COARSE_ROWS + half, :] = qq.astype(bf16)
 
 
+def with_ones(kv):
+    return jnp.concatenate([kv, jnp.ones((kv.shape[0], 128), bf16)], axis=1)
+
+
 def absorb(q_ref, top_ref, total_ref, acc_ref, begin, rows, parts):
     at = pl.ds(begin, rows)
     query = q_ref[at, :]
@@ -307,19 +339,15 @@
     top = jnp.maximum(old, jnp.max(peak, axis=1, keepdims=True))
     factor = jnp.exp2(old - top)
     both = jnp.concatenate([top, top], axis=1)
-    weights = [jnp.exp2(s - both) for s in scores]
-    summed = weights[0]
-    for w in weights[1:]:
-        summed = summed + w
-    contrib = dot(weights[0].astype(bf16), parts[0])
-    for w, kv in zip(weights[1:], parts[1:]):
-        contrib = contrib + dot(w.astype(bf16), kv)
+    contrib = dot(jnp.exp2(scores[0] - both).astype(bf16), with_ones(parts[0]))
+    for s, kv in zip(scores[1:], parts[1:]):
+        contrib = contrib + dot(jnp.exp2(s - both).astype(bf16), with_ones(kv))
     top_ref[at, :] = top
-    total_ref[at, :] = total_ref[at, :] * factor + jnp.sum(summed, axis=1, keepdims=True)
-    acc_ref[at, :] = acc_ref[at, :] * factor + contrib
-
-
-def coarse_first_kernel(turned_ref, q_ref, top_ref, total_ref, acc_ref):
+    total_ref[at, :] = total_ref[at, :] * factor + contrib[:, 128:]
+    acc_ref[at, :] = acc_ref[at, :] * factor + contrib[:, :128]
+
+
+def coarse_first_kernel(flag_ref, turned_ref, far_ref, q_ref, top_ref, total_ref, acc_ref):
     half = COARSE_ROWS // 2
     low_lanes = lax.broadcasted_iota(jnp.int32, (1, 128), 1) < 64
     row = lax.broadcasted_iota(jnp.int32, (256, 256), 0)
@@ -335,59 +363,64 @@
         at = pl.ds(z * 256, 256)
         scores = jnp.where(col <= row, dot_t(q_ref[at, :], kv), masked_low)
         top = jnp.max(scores, axis=1, keepdims=True)
-        weights = jnp.exp2(scores - top)
+        contrib = dot(jnp.exp2(scores - top).astype(bf16), with_ones(kv))
         top_ref[at, :] = jnp.broadcast_to(top, (256, 128))
-        total_ref[at, :] = jnp.broadcast_to(jnp.sum(weights, axis=1, keepdims=True), (256, 128))
-        acc_ref[at, :] = dot(weights.astype(bf16), kv)
+        total_ref[at, :] = contrib[:, 128:]
+        acc_ref[at, :] = contrib[:, :128]
+    state = (q_ref, top_ref, total_ref, acc_ref)
     for z in range(3):
         absorb(
-            q_ref, top_ref, total_ref, acc_ref, (z + 1) * 256, (3 - z) * 256,
-            [turned_ref[z, :COARSE_ROWS, :]],
+            *state, (z + 1) * 256, (3 - z) * 256, [turned_ref[z, :COARSE_ROWS, :], far_ref[z]]
         )
 
-
-def absorb_chunks(chunk_ref, first_chunk, refs, state):
-    for a in range(0, len(refs), 2):
-        for z in range(3):
-            absorb(*state, (z + 1) * 256, (3 - z) * 256, [r[z] for r in refs[a : a + 2]])
-    for n, ref in enumerate(refs):
-
-        @pl.when(chunk_ref[first_chunk + n] < chunk_ref[0])
-        def _(ref=ref):
-            for z in range(4):
-                absorb(*state, z * 256, 256, [ref[z]])
-
-
-def coarse_near_kernel(
-    chunk_ref, n1, n2, n3, q_ref, top_in, total_in, acc_in, top_ref, total_ref, acc_ref
-):
+    @pl.when(flag_ref[0] > 0)
+    def _():
+        for z in range(4):
+            absorb(*state, z * 256, 256, [far_ref[z]])
+
+
+def coarse_more_kernel(which, last, flag_ref, *refs):
+    count = 2 * len(which)
+    chunks = refs[:count]
+    q_ref, top_in, total_in, acc_in = refs[count : count + 4]
+    out_ref = refs[count + 4] if last else None
+    top_ref, total_ref, acc_ref = refs[-3:]
     top_ref[...] = top_in[...]
     total_ref[...] = total_in[...]
     acc_ref[...] = acc_in[...]
-    absorb_chunks(chunk_ref, 1, [n1, n2, n3], (q_ref, top_ref, total_ref, acc_ref))
-
-
-def coarse_far_kernel(
-    chunk_ref, far_ref, q_ref, top_in, total_in, acc_in, out_ref, top_ref, total_ref, acc_ref
-):
-    top_ref[...] = top_in[...]
-    total_ref[...] = total_in[...]
-    acc_ref[...] = acc_in[...]
-    refs = [far_ref.at[s] for s in range(4)]
-    absorb_chunks(chunk_ref, 4, refs, (q_ref, top_ref, total_ref, acc_ref))
-    mixed = acc_ref[...] / total_ref[...]
-    low_lanes = lax.broadcasted_iota(jnp.int32, (1, 128), 1) < 64
-    for z in range(4):
-        upper = pltpu.roll(mixed[z * 256 : z * 256 + 128], 64, 1)
-        lower = mixed[z * 256 + 128 : (z + 1) * 256]
-        out_ref[z] = jnp.where(low_lanes, upper, lower).astype(bf16)
+    state = (q_ref, top_ref, total_ref, acc_ref)
+    for n, s in enumerate(which):
+        near, far = chunks[2 * n], chunks[2 * n + 1]
+        for z in range(3):
+            absorb(*state, (z + 1) * 256, (3 - z) * 256, [near[z], far[z]])
+
+        @pl.when(flag_ref[s] > 0)
+        def _(near=near, far=far):
+            for z in range(4):
+                absorb(*state, z * 256, 256, [near[z], far[z]])
+
+    if last:
+        mixed = acc_ref[...] / total_ref[...]
+        low_lanes = lax.broadcasted_iota(jnp.int32, (1, 128), 1) < 64
+        for z in range(4):
+            upper = pltpu.roll(mixed[z * 256 : z * 256 + 128], 64, 1)
+            lower = mixed[z * 256 + 128 : (z + 1) * 256]
+            block = jnp.where(low_lanes, upper, lower).astype(bf16)
+            for y in range(4):
+                out_ref[z * 4 + y] = block
 
 
 def feed_kernel(
-    where_ref, heads_ref, own_ref, mine_ref, other_ref, short_ref, gain_ref, up_ref, down_ref,
-    part_ref, first_ref, mixed_ref, all_ref,
+    where_ref, heads_ref, short_ref, gain_ref, own_hbm, mine_hbm, other_hbm, up_hbm, down_hbm,
+    part_ref, first_ref, mixed_ref, all_ref, co_ref, up_ref, down_ref, sems,
 ):
     head, core = where_ref[1], where_ref[2]
+    pairs = [(own_hbm, co_ref.at[pl.ds(head * 256, 256)])]
+    for s in range(1, 4):
+        source = lax.rem(head - s + 4, 4) * 256
+        pairs.append((mine_hbm.at[s - 1], co_ref.at[pl.ds(source + core * 128, 128)]))
+        pairs.append((other_hbm.at[s - 1], co_ref.at[pl.ds(source + 128 - core * 128, 128)]))
+    copies = begin_copies(pairs + [(up_hbm, up_ref), (down_hbm, down_ref)], sems)
     low_lanes = lax.broadcasted_iota(jnp.int32, (1, 128), 1) < 64
     for y in range(4):
         for pair in range(2):
@@ -396,16 +429,12 @@
             at = slice(y * 256 + pair * 128, y * 256 + (pair + 1) * 128)
             mixed_ref[0:128, at] = jnp.where(low_lanes, even, pltpu.roll(odd, 64, 1)).astype(bf16)
             mixed_ref[128:256, at] = jnp.where(low_lanes, pltpu.roll(even, 64, 1), odd).astype(bf16)
-    first = short_ref[...].astype(f32)
-    for half in range(2):
-        first += dot(half_lanes(mixed_ref, head, half), own_ref[half * 128 : (half + 1) * 128, :])
-    for s in range(1, 4):
-        source = lax.rem(head - s + 4, 4)
-        first += dot(half_lanes(mixed_ref, source, core), mine_ref[s - 1])
-        first += dot(half_lanes(mixed_ref, source, 1 - core), other_ref[s - 1])
+    finish_copies(copies[:7])
+    first = short_ref[...].astype(f32) + dot(mixed_ref[...], co_ref[...])
     all_ref[...] = first
     first_ref[...] = all_ref[pl.ds(pl.multiple_of(head * 64, 64), 64), :]
     feed = norm_rows(first, gain_ref[...])
+    finish_copies(copies[7:])
     inner = jax.nn.gelu(dot(feed, up_ref[...])).astype(bf16)
     part_ref[...] = dot(inner, down_ref[...]).astype(bf16).reshape(4, 64, D)
 
@@ -431,10 +460,13 @@
         out_ref[pl.ds(begin, 256), :] = dot(weave, value).astype(bf16)
 
 
-def gather_rest(weight, core):
+def fetch_rest(weight, core):
     half = lax.dynamic_slice_in_dim(weight, core * 128, 128, 0)
-    mine = jnp.stack([shift(half, "head", s, 4) for s in range(1, 4)])
-    return mine, shift(mine, "core", 1, 2)
+    return [shift(half, "head", s, 4) for s in range(1, 4)]
+
+
+def after(value, gate):
+    return lax.optimization_barrier((value, gate))
 
 
 def local(
@@ -455,17 +487,22 @@
     tab, q, k_own, v_own = call(
         fine_own_kernel, "fine_own",
         [jax.ShapeDtypeStruct((9, 256, SHARE), bf16), share, share, share], [],
-        [token_ids[:, None], embedding, fine_norm[None], fine_query, fine_key, fine_value, *tables],
+        [token_ids[:, None], embedding, fine_norm[None], *tables],
+        [pltpu.VMEM((3, D, SHARE), bf16), pltpu.SemaphoreType.DMA((3,))],
+        hbm=[fine_query, fine_key, fine_value], us=5,
     )
     past_ids = jnp.concatenate([before, prior])
-    past_ids, fine_output_held = lax.optimization_barrier((past_ids, fine_output))
-    out_mine, out_other = gather_rest(fine_output_held, core)
+    fine_output_held, tab = after(fine_output, tab)
+    out_rest = fetch_rest(fine_output_held, core)
 
     mixed = call(
         fine_kernel, "fine_attention", jax.ShapeDtypeStruct((HALO + ROWS, SHARE), bf16),
         [where], [past_ids[:, None], tab, q, k_own, v_own, *tables],
-        [pltpu.VMEM((KEYS, SHARE), bf16), pltpu.VMEM((KEYS, SHARE), bf16)], grid=(4,),
-    )
+        [pltpu.VMEM((KEYS, SHARE), bf16), pltpu.VMEM((KEYS, SHARE), bf16)], grid=(4,), us=12,
+    )
+    out_rest, mixed = after(out_rest, mixed)
+    out_mine = jnp.stack(out_rest)
+    out_other = shift(out_mine, "core", 1, 2)
 
     rows = 256 + HALO
     got = exchange(lambda d: lax.dynamic_slice_in_dim(mixed, d * 256, rows, 0), "head", 4)
@@ -474,7 +511,9 @@
     )
     sends = call(
         fine_rows_kernel, "fine_rows", jax.ShapeDtypeStruct((4, rows, SHARE), bf16),
-        [where], [own_ids[:, None], embedding, *got, fine_output, out_mine, out_other],
+        [where], [own_ids[:, None], embedding, *got],
+        [pltpu.VMEM((D, D), bf16), pltpu.SemaphoreType.DMA((7,))],
+        hbm=[fine_output, out_mine, out_other],
     )
     blocks = exchange(lambda d: lax.dynamic_index_in_dim(sends, d, 0, keepdims=False), "head", 4)
 
@@ -498,34 +537,45 @@
     )
 
     turned = lax.all_to_all(packed, "z", 0, 0)
-    turned, coarse_output_held = lax.optimization_barrier((turned, coarse_output))
+    coarse_output_held, turned = after(coarse_output, turned)
     kv = turned[:, :COARSE_ROWS]
+    far = [shift(kv, "core", 1, 2)]
     near = [shift(kv, "x", s, 4) for s in range(1, 4)]
-    far = shift(jnp.stack([kv, *near]), "core", 1, 2)
-    co_mine, co_other = gather_rest(coarse_output_held, core)
+    far += [shift(part, "core", 1, 2) for part in near]
     steps = jnp.arange(4, dtype=jnp.int32)
-    columns_x = (x_place - steps + 4) % 4
-    chunks = jnp.concatenate([2 * columns_x + core, 2 * columns_x + 1 - core])
+    flags = ((x_place - steps + 4) % 4 < x_place).astype(jnp.int32) + (steps == 0) * core
     wide = jax.ShapeDtypeStruct((1024, 128), f32)
-    state = call(
+    q_all, *sums = call(
         coarse_first_kernel, "coarse_first",
-        [jax.ShapeDtypeStruct((1024, 128), bf16), wide, wide, wide], [], [turned],
-    )
-    q_all, sums = state[0], state[1:]
-    sums = call(coarse_near_kernel, "coarse_near", [wide] * 3, [chunks], [*near, q_all, *sums])
-    attended = call(
-        coarse_far_kernel, "coarse_far", jax.ShapeDtypeStruct((4, 128, 128), bf16),
-        [chunks], [far, q_all, *sums], [pltpu.VMEM((1024, 128), f32)] * 3,
-    )
-
-    wide_sends = jnp.broadcast_to(attended[:, None], (4, 4, 128, 128)).reshape(16, 128, 128)
+        [jax.ShapeDtypeStruct((1024, 128), bf16), wide, wide, wide], [flags], [turned, far[0]],
+        us=3,
+    )
+    co_rest = fetch_rest(coarse_output_held, core)
+    sums = call(
+        functools.partial(coarse_more_kernel, (1, 3), False), "coarse_more", [wide] * 3,
+        [flags], [near[0], far[1], near[2], far[3], q_all, *sums], us=6,
+    )
+    wide_sends = call(
+        functools.partial(coarse_more_kernel, (2,), True), "coarse_last",
+        jax.ShapeDtypeStruct((16, 128, 128), bf16),
+        [flags], [near[1], far[2], q_all, *sums], [pltpu.VMEM((1024, 128), f32)] * 3, us=3,
+    )
+    co_rest, wide_sends = after(co_rest, wide_sends)
+    co_mine = jnp.stack(co_rest)
+    co_other = shift(co_mine, "core", 1, 2)
+
     heads_in = lax.all_to_all(wide_sends, ("z", "head"), 0, 0)
+    square = pltpu.VMEM((D, D), bf16)
     parts, first_own = call(
         feed_kernel, "feed",
         [jax.ShapeDtypeStruct((4, 64, D), bf16), jax.ShapeDtypeStruct((64, D), f32)],
         [where],
-        [heads_in, coarse_output, co_mine, co_other, short, ffn_norm[None], ffn_up, ffn_down],
-        [pltpu.VMEM((COARSE_ROWS, D), bf16), pltpu.VMEM((COARSE_ROWS, D), f32)],
+        [heads_in, short, ffn_norm[None]],
+        [
+            pltpu.VMEM((COARSE_ROWS, D), bf16), pltpu.VMEM((COARSE_ROWS, D), f32),
+            square, square, square, pltpu.SemaphoreType.DMA((9,)),
+        ],
+        hbm=[coarse_output, co_mine, co_other, ffn_up, ffn_down], us=4,
     )
     sums = exchange(lambda d: lax.dynamic_index_in_dim(parts, d, 0, keepdims=False), "head", 4)
     second_own = (first_own + sum(t.astype(f32) for t in sums)).astype(bf16)

time: 194 us -> 176 us (0.907)
  waiting for transfers between devices: 87.8 us -> 44 us
  blocking collectives: 12.2 us -> 27.6 us
  local copies, waits for them, and re-layouts: 8.93 us -> 16.4 us
  starting transfers between devices: 42.6 us -> 47.1 us
  Pallas kernels: 40.1 us -> 37.6 us
    ppermute x30 -> x33, waiting for transfers between devices: 73.6 us -> 42.4 us  [shift(): lax.ppermute(value, axis, [(i, (i + steps) % count) for i in range(count)])]
    all_to_all x0 -> x1, blocking collectives: none -> 15.1 us  [local(): heads_in = lax.all_to_all(wide_sends, ('z', 'head'), 0, 0)]
    all_to_all x1 -> x0, waiting for transfers between devices: 12.6 us -> none  [local(): heads_in = lax.all_to_all(wide_sends, ('z', 'head'), 0, 0)]
    unnamed x63 -> x65, local copies, waits for them, and re-layouts: 4.79 us -> 14.2 us
    ppermute x30 -> x33, starting transfers between devices: 33.2 us -> 41.4 us  [shift(): lax.ppermute(value, axis, [(i, (i + steps) % count) for i in range(count)])]
    all_to_all x1 -> x0, starting transfers between devices: 3.57 us -> none  [local(): heads_in = lax.all_to_all(wide_sends, ('z', 'head'), 0, 0)]
    pallas_call x13, Pallas kernels: 40.1 us -> 37.6 us  [call(): pl.pallas_call(kernel, out_shape=shapes, in_specs=[smem()] * len(scalars)...]
  transfers between devices with their start and end apart: 33 -> 35, of which waited for: 23 -> 17; matrix products, arithmetic and copies ran while one was open for 2% -> 2% of each run, Pallas kernels for 15% -> 16%
where the time goes in v2:
time: 176 us; the launch traced here: 175 us
  starting transfers between devices  47.1 us (27%)
  waiting for transfers between devices  44 us (25%)
  Pallas kernels  37.6 us (21%)
  blocking collectives  27.6 us (16%)
  local copies, waits for them, and re-layouts  16.4 us (9%)
    ppermute x33, waiting for transfers between devices, shift(): lax.ppermute(value, axis, [(i, (i + steps) % count) for i in range(count)])  42.4 us
    ppermute x33, starting transfers between devices, shift(): lax.ppermute(value, axis, [(i, (i + steps) % count) for i in range(count)])  41.4 us
    pallas_call x13, Pallas kernels, call(): pl.pallas_call(kernel, out_shape=shapes, in_specs=[smem()] * len(scalars)...  37.6 us
    all_to_all x1, blocking collectives, local(): heads_in = lax.all_to_all(wide_sends, ('z', 'head'), 0, 0)  15.1 us
    unnamed x65, local copies, waits for them, and re-layouts  14.2 us
    all_to_all x1, blocking collectives, local(): turned = lax.all_to_all(packed, 'z', 0, 0)  12.5 us
    ppermute x2, starting transfers between devices, later(): lax.ppermute(value, axis, [(i, i + steps) for i in range(count - steps)])  5.64 us
  transfers between devices with their start and end apart: 35, of which 17 were waited for; matrix products, arithmetic and copies ran while one was open for 2% of the time, Pallas kernels for 16%

profile of v2, /device:TPU:6, one launch (start us, length us, event | category | flops | bytes accessed | tf_op | source)
XLA Modules:
  0.0 174.8 jit_solution(7026516122860958862)
XLA Ops:
  0.0 1.9 %collective-permute-start = (s32[1024]{0:T(1024)}, s32[1024]{0:T(1024)S(1)}, u32[]{:S(2)}, u32[]{:S(2)}) collective-permute-start(s32[1024]{0:T(1024)} %param.21), channel_id=1, source_target_pairs={{0,4},{4,8},{8,12},{12,16},{16,20},{20,24},{24,28},{28,32},{32,36}... | collective-permute-start | bytes 12296 | tf_op jit(solution)/shard_map/ppermute | solution.py:48
  1.9 0.9 copy.22.ids_ref
  2.8 1.0 copy-done.4
  3.9 1.0 copy-done.5
  4.9 1.0 copy-done.6
  6.0 1.0 copy-done.7
  7.0 0.7 copy-done.12
  7.7 0.9 copy-done.15
  8.6 0.9 copy-done.17
  9.5 0.7 copy-done.20
  10.2 0.7 copy-done.22
  11.0 2.4 %fine_own.1 = (bf16[9,256,256]{2,1,0:T(8,128)(2,1)S(1)}, bf16[1024,256]{1,0:T(8,128)(2,1)S(1)}, bf16[1024,256]{1,0:T(8,128)(2,1)S(1)}, bf16[1024,256]{1,0:T(8,128)(2,1)S(1)}) custom-call(s32[1024,1]{1,0:T(8,128)S(1)} %copy.22.ids_ref, bf16[256,1024]{1,0:T(8,128)(2,1)S(1)} %copy-done.7, f32[1,1024]{1,0:T(1,128)S(1)} %bitcast.33, f32[32,128]{1,0:T(8,128)S(1)} %copy-done.20, ...), custom_call_target="tpu_custom_call" | custom-call | flops 5000000000 | bytes 10000000 | tf_op jit(solution)/shard_map/fine_own/pallas_call | solution.py:224
  13.4 0.8 copy-done.24
  14.2 0.8 copy-done.26
  15.0 0.8 copy-done.28
  15.8 1.6 collective-permute-start.1
  17.5 2.9 %collective-permute-start.2 = (bf16[128,1024]{1,0:T(8,128)(2,1)S(1)}, bf16[128,1024]{1,0:T(8,128)(2,1)}, u32[]{:S(2)}, u32[]{:S(2)}) collective-permute-start(bf16[128,1024]{1,0:T(8,128)(2,1)S(1)} %constant_dynamic-slice_fusion.5), channel_id=1, source_target_pairs={{0,2},{1,3},{2,0},{3,1},{4,6},{5,7},{6,4},{7,5},{8,10},{9,11},{10,... | collective-permute-start | bytes 786440 | tf_op jit(solution)/shard_map/ppermute | solution.py:44
  20.4 1.3 collective-permute-start.3
  21.7 3.7 %collective-permute-start.4 = (s32[256]{0:T(256)S(1)}, s32[256]{0:T(256)S(1)}, u32[]{:S(2)}, u32[]{:S(2)}) collective-permute-start(s32[256]{0:T(256)S(1)} %slice.10), channel_id=1, source_target_pairs={{0,8},{4,12},{8,16},{12,20},{16,24},{20,28},{24,32},{28,36},{32,40... | collective-permute-start | bytes 3080 | tf_op jit(solution)/shard_map/ppermute | solution.py:48
  25.6 1.6 collective-permute-done.4
  27.5 1.0 copy-done.25
  28.5 1.0 copy-done.27
  29.6 1.0 copy-done.29
  30.6 11.7 %fine_attention.1 = bf16[1040,256]{1,0:T(8,128)(2,1)S(1)} custom-call(s32[3]{0:T(128)S(1)} %pad_add_fusion.1.place_ref.where_ref, s32[1280,1]{1,0:T(8,128)S(1)} %broadcast_in_dim.25.ids_ref, bf16[9,256,256]{2,1,0:T(8,128)(2,1)S(1)} %get-tuple-element.34.tab_ref, bf16[1024,256]{1,0:T(8,128)(2,1)S(1)} %copy-done.25, bf16[1024,256]{1,0:T(8,128)(2,1)S(1)} %copy-done.27, ...), custom_call_target="tpu_custom_call" | custom-call | flops 12000000000 | bytes 24000000 | tf_op jit(solution)/shard_map/fine_attention/pallas_call | solution.py:224
  42.3 1.2 pad_maximum_fusion.mine_hbm
  44.0 0.8 constant_dynamic-slice_fusion.1
  44.8 0.7 collective-permute-start.5
  45.5 1.1 collective-permute-start.6
  46.6 1.6 collective-permute-start.7
  48.4 6.5 %collective-permute-done.5.g1 = bf16[272,256]{1,0:T(8,128)(2,1)S(1)} collective-permute-done((bf16[272,256]{1,0:T(8,128)(2,1)}, bf16[272,256]{1,0:T(8,128)(2,1)S(1)}, u32[]{:S(2)}, u32[]{:S(2)}) %collective-permute-start.5) | collective-permute-done | bytes 139296 | tf_op jit(solution)/shard_map/ppermute | solution.py:44
  55.6 2.1 %fine_rows.1 = bf16[4,272,256]{2,1,0:T(8,128)(2,1)S(1)} custom-call(s32[3]{0:T(128)S(1)} %pad_add_fusion.1.place_ref.where_ref, s32[272,1]{1,0:T(8,128)S(1)} %broadcast_in_dim.24.ids_ref, bf16[256,1024]{1,0:T(8,128)(2,1)S(1)} %copy-done.8, bf16[272,256]{1,0:T(8,128)(2,1)S(1)} %get-tuple-element.66.g0, bf16[272,256]{1,0:T(8,128)(2,1)S(1)} %collective-permute-done.5.g1, ...), custom_call_target="tpu_custom_call" | custom-call | flops 2000000000 | bytes 4000000 | tf_op jit(solution)/shard_map/fine_rows/pallas_call | solution.py:224
  58.2 3.6 %collective-permute-start.11 = (bf16[272,256]{1,0:T(8,128)(2,1)S(1)}, bf16[272,256]{1,0:T(8,128)(2,1)S(1)}, u32[]{:S(2)}, u32[]{:S(2)}) collective-permute-start(bf16[272,256]{1,0:T(8,128)(2,1)S(1)} %get-tuple-element.61), channel_id=1, source_target_pairs={{0,2},{1,3},{2,0},{3,1},{4,6},{5,7},{6,4},{7,5},{8,10},{9,11},{10,... | collective-permute-start | bytes 417800 | tf_op jit(solution)/shard_map/ppermute | solution.py:44
  61.7 2.5 %collective-permute-done.9.group_ref.b1 = bf16[272,256]{1,0:T(8,128)(2,1)S(1)} collective-permute-done((bf16[272,256]{1,0:T(8,128)(2,1)S(1)}, bf16[272,256]{1,0:T(8,128)(2,1)S(1)}, u32[]{:S(2)}, u32[]{:S(2)}) %collective-permute-start.9) | collective-permute-done | bytes 139296 | tf_op jit(solution)/shard_map/ppermute | solution.py:44
  64.7 2.9 %collective-permute-start.10 = (bf16[64,1024]{1,0:T(8,128)(2,1)S(1)}, bf16[64,1024]{1,0:T(8,128)(2,1)S(1)}, u32[]{:S(2)}, u32[]{:S(2)}) collective-permute-start(bf16[64,1024]{1,0:T(8,128)(2,1)S(1)} %short_part.5), channel_id=1, source_target_pairs={{0,3},{1,0},{2,1},{3,2},{4,7},{5,4},{6,5},{7,6},{8,11},{9,8},{10,9... | collective-permute-start | bytes 393224 | tf_op jit(solution)/shard_map/ppermute | solution.py:44
  69.8 1.2 collective-permute-start.14
  71.4 0.6 collective-permute-done.10
  72.1 3.9 %collective-permute-done.12 = bf16[64,1024]{1,0:T(8,128)(2,1)S(1)} collective-permute-done((bf16[64,1024]{1,0:T(8,128)(2,1)S(1)}, bf16[64,1024]{1,0:T(8,128)(2,1)S(1)}, u32[]{:S(2)}, u32[]{:S(2)}) %collective-permute-start.12) | collective-permute-done | bytes 131104 | tf_op jit(solution)/shard_map/ppermute | solution.py:44
  76.0 1.3 collective-permute-done.14
  77.5 2.0 %collective-permute-start.16 = (bf16[64,1024]{1,0:T(8,128)(2,1)S(1)}, bf16[64,1024]{1,0:T(8,128)(2,1)S(1)}, u32[]{:S(2)}, u32[]{:S(2)}) collective-permute-start(bf16[64,1024]{1,0:T(8,128)(2,1)S(1)} %add_convert_fusion.s0), channel_id=1, source_target_pairs={{0,2},{1,3},{2,0},{3,1},{4,6},{5,7},{6,4},{7,5},{8,10},{9,11},{10,... | collective-permute-start | bytes 393224 | tf_op jit(solution)/shard_map/ppermute | solution.py:44
  79.5 1.5 collective-permute-start.17
  81.0 4.9 %collective-permute-done.15.s1 = bf16[64,1024]{1,0:T(8,128)(2,1)S(1)} collective-permute-done((bf16[64,1024]{1,0:T(8,128)(2,1)S(1)}, bf16[64,1024]{1,0:T(8,128)(2,1)S(1)}, u32[]{:S(2)}, u32[]{:S(2)}) %collective-permute-start.15) | collective-permute-done | bytes 131104 | tf_op jit(solution)/shard_map/ppermute | solution.py:44
  86.6 1.5 coarse_pack.1
  88.1 12.5 %all_to_all.10.turned_ref = bf16[4,384,128]{2,1,0:T(8,128)(2,1)S(1)} all-to-all(bf16[4,384,128]{2,1,0:T(8,128)(2,1)S(1)} %get-tuple-element.42), channel_id=1, replica_groups=mesh['z'=4,'x'=4,'core'=2,'head'=4] {'z'}, dimensions={0} | all-to-all | bytes 786432 | tf_op jit(solution)/shard_map/all_to_all | solution.py:539
  100.7 2.7 %collective-permute-start.24 = (bf16[4,256,128]{2,1,0:T(8,128)(2,1)S(1)}, bf16[4,256,128]{2,1,0:T(8,128)(2,1)S(1)}, u32[]{:S(2)}, u32[]{:S(2)}) collective-permute-start(bf16[4,256,128]{2,1,0:T(8,128)(2,1)S(1)} %slice.11), channel_id=1, source_target_pairs={{0,8},{8,16},{16,24},{24,0},{1,9},{9,17},{17,25},{25,1},{2,10},{10... | collective-permute-start | bytes 786440 | tf_op jit(solution)/shard_map/ppermute | solution.py:44
  103.4 1.6 collective-permute-start.21
  105.5 3.6 %collective-permute-start.19 = (bf16[128,1024]{1,0:T(8,128)(2,1)S(1)}, bf16[128,1024]{1,0:T(8,128)(2,1)S(1)}, u32[]{:S(2)}, u32[]{:S(2)}) collective-permute-start(bf16[128,1024]{1,0:T(8,128)(2,1)S(1)} %constant_dynamic-slice_fusion), channel_id=1, source_target_pairs={{0,2},{1,3},{2,0},{3,1},{4,6},{5,7},{6,4},{7,5},{8,10},{9,11},{10,... | collective-permute-start | bytes 786440 | tf_op jit(solution)/shard_map/ppermute | solution.py:44
  109.1 6.1 %collective-permute-done.24.refs_0_ = bf16[4,256,128]{2,1,0:T(8,128)(2,1)S(1)} collective-permute-done((bf16[4,256,128]{2,1,0:T(8,128)(2,1)S(1)}, bf16[4,256,128]{2,1,0:T(8,128)(2,1)S(1)}, u32[]{:S(2)}, u32[]{:S(2)}) %collective-permute-start.24) | collective-permute-done | bytes 262176 | tf_op jit(solution)/shard_map/ppermute | solution.py:44
  115.2 3.4 %collective-permute-done.26.refs_2_ = bf16[4,256,128]{2,1,0:T(8,128)(2,1)S(1)} collective-permute-done((bf16[4,256,128]{2,1,0:T(8,128)(2,1)S(1)}, bf16[4,256,128]{2,1,0:T(8,128)(2,1)S(1)}, u32[]{:S(2)}, u32[]{:S(2)}) %collective-permute-start.26) | collective-permute-done | bytes 262176 | tf_op jit(solution)/shard_map/ppermute | solution.py:44
  118.6 2.4 %coarse_first.1 = (bf16[1024,128]{1,0:T(8,128)(2,1)S(1)}, f32[1024,128]{1,0:T(8,128)S(1)}, f32[1024,128]{1,0:T(8,128)S(1)}, f32[1024,128]{1,0:T(8,128)S(1)}) custom-call(s32[4]{0:T(128)S(1)} %fusion.5.flag_ref, bf16[4,384,128]{2,1,0:T(8,128)(2,1)S(1)} %all_to_all.10.turned_ref, bf16[4,256,128]{2,1,0:T(8,128)(2,1)S(1)} %collective-permute-done.23.far_ref), custom_call_target="tpu_custom_call" | custom-call | flops 3000000000 | bytes 6000000 | tf_op jit(solution)/shard_map/coarse_first/pallas_call | solution.py:224
  121.0 2.6 %collective-permute-start.20 = (bf16[128,1024]{1,0:T(8,128)(2,1)S(1)}, bf16[128,1024]{1,0:T(8,128)(2,1)S(1)}, u32[]{:S(2)}, u32[]{:S(2)}) collective-permute-start(bf16[128,1024]{1,0:T(8,128)(2,1)S(1)} %constant_dynamic-slice_fusion), channel_id=1, source_target_pairs={{0,3},{1,0},{2,1},{3,2},{4,7},{5,4},{6,5},{7,6},{8,11},{9,8},{10,9... | collective-permute-start | bytes 786440 | tf_op jit(solution)/shard_map/ppermute | solution.py:44
  123.6 0.9 collective-permute-start.22
  124.5 5.7 %coarse_more.1 = (f32[1024,128]{1,0:T(8,128)S(1)}, f32[1024,128]{1,0:T(8,128)S(1)}, f32[1024,128]{1,0:T(8,128)S(1)}) custom-call(s32[4]{0:T(128)S(1)} %fusion.5.flag_ref, bf16[4,256,128]{2,1,0:T(8,128)(2,1)S(1)} %collective-permute-done.24.refs_0_, bf16[4,256,128]{2,1,0:T(8,128)(2,1)S(1)} %collective-permute-done.25.refs_1_, ...), custom_call_target="tpu_custom_call" | custom-call | flops 6000000000 | bytes 12000000 | tf_op jit(solution)/shard_map/coarse_more/pallas_call | solution.py:224
  130.2 3.0 %coarse_last.1 = bf16[16,128,128]{2,1,0:T(8,128)(2,1)S(1)} custom-call(s32[4]{0:T(128)S(1)} %fusion.5.flag_ref, bf16[4,256,128]{2,1,0:T(8,128)(2,1)S(1)} %collective-permute-done.21.refs_0_, bf16[4,256,128]{2,1,0:T(8,128)(2,1)S(1)} %collective-permute-done.22.refs_1_, bf16[1024,128]{1,0:T(8,128)(2,1)S(1)} %get-tuple-element.45.refs_4_.refs_2_, ...), custom_call_target="tpu_custom_call" | custom-call | flops 3000000000 | bytes 6000000 | tf_op jit(solution)/shard_map/coarse_last/pallas_call | solution.py:224
  133.5 15.1 %all_to_all.11.heads_ref = bf16[16,128,128]{2,1,0:T(8,128)(2,1)S(1)} all-to-all(bf16[16,128,128]{2,1,0:T(8,128)(2,1)S(1)} %coarse_last.1), channel_id=1, replica_groups=mesh['z'=4,'x'=4,'core'=2,'head'=4] {'z','head'}, dimensions={0} | all-to-all | bytes 1048576 | tf_op jit(solution)/shard_map/all_to_all | solution.py:567
  148.6 4.2 %feed.1 = (bf16[4,64,1024]{2,1,0:T(8,128)(2,1)S(1)}, f32[64,1024]{1,0:T(8,128)S(1)}) custom-call(s32[3]{0:T(128)S(1)} %pad_add_fusion.1.place_ref.where_ref, bf16[16,128,128]{2,1,0:T(8,128)(2,1)S(1)} %all_to_all.11.heads_ref, bf16[256,1024]{1,0:T(8,128)(2,1)S(1)} %get-tuple-element.53.short_ref, f32[1,1024]{1,0:T(1,128)S(1)} %bitcast.35, ...), custom_call_target="tpu_custom_call" | custom-call | flops 4000000000 | bytes 8000000 | tf_op jit(solution)/shard_map/feed/pallas_call | solution.py:224
  152.8 0.6 collective-permute-start.29
  153.4 1.4 collective-permute-start.30
  154.8 1.4 collective-permute-start.31
  156.3 5.3 %collective-permute-done.29 = bf16[64,1024]{1,0:T(8,128)(2,1)S(1)} collective-permute-done((bf16[64,1024]{1,0:T(8,128)(2,1)S(1)}, bf16[64,1024]{1,0:T(8,128)(2,1)S(1)}, u32[]{:S(2)}, u32[]{:S(2)}) %collective-permute-start.29) | collective-permute-done | bytes 131104 | tf_op jit(solution)/shard_map/ppermute | solution.py:44
  162.2 1.0 collective-permute-start.32
  163.2 3.2 %collective-permute-start.33 = (bf16[64,1024]{1,0:T(8,128)(2,1)S(1)}, bf16[64,1024]{1,0:T(8,128)(2,1)S(1)}, u32[]{:S(2)}, u32[]{:S(2)}) collective-permute-start(bf16[64,1024]{1,0:T(8,128)(2,1)S(1)} %fusion.3.s0), channel_id=1, source_target_pairs={{0,2},{1,3},{2,0},{3,1},{4,6},{5,7},{6,4},{7,5},{8,10},{9,11},{10,... | collective-permute-start | bytes 393224 | tf_op jit(solution)/shard_map/ppermute | solution.py:44
  167.0 2.0 %collective-permute-done.32.s1 = bf16[64,1024]{1,0:T(8,128)(2,1)S(1)} collective-permute-done((bf16[64,1024]{1,0:T(8,128)(2,1)S(1)}, bf16[64,1024]{1,0:T(8,128)(2,1)S(1)}, u32[]{:S(2)}, u32[]{:S(2)}) %collective-permute-start.32) | collective-permute-done | bytes 131104 | tf_op jit(solution)/shard_map/ppermute | solution.py:44
  169.0 3.2 %collective-permute-done.33.s2 = bf16[64,1024]{1,0:T(8,128)(2,1)S(1)} collective-permute-done((bf16[64,1024]{1,0:T(8,128)(2,1)S(1)}, bf16[64,1024]{1,0:T(8,128)(2,1)S(1)}, u32[]{:S(2)}, u32[]{:S(2)}) %collective-permute-start.33) | collective-permute-done | bytes 131104 | tf_op jit(solution)/shard_map/ppermute | solution.py:44
  172.2 2.7 %final.1 = bf16[1024,256]{1,0:T(8,128)(2,1)} custom-call(s32[3]{0:T(128)S(1)} %pad_add_fusion.1.place_ref.where_ref, bf16[64,1024]{1,0:T(8,128)(2,1)S(1)} %fusion.3.s0, bf16[64,1024]{1,0:T(8,128)(2,1)S(1)} %collective-permute-done.32.s1, bf16[64,1024]{1,0:T(8,128)(2,1)S(1)} %collective-permute-done.33.s2, bf16[64,1024]{1,0:T(8,128)(2,1)S(1)} %collective-permute-done.34.s3, ...), custom_call_target="tpu_custom_call" | custom-call | flops 2000000000 | bytes 4000000 | tf_op jit(solution)/shard_map/final/pallas_call | solution.py:224
  (105 shorter events, 8.2 us)
Async XLA Ops:
  0.0 27.2 %collective-permute-start = (s32[1024]{0:T(1024)}, s32[1024]{0:T(1024)S(1)}, u32[]{:S(2)}, u32[]{:S(2)}) collective-permute-start(s32[1024]{0:T(1024)} %param.21), channel_id=1, source_target_pairs={{0,4},{4,8},{8,12},{12,16},{16,20},{20,24},{24,28},{28,32},{32,36}... | collective-permute-start | bytes 12296 | tf_op jit(solution)/shard_map/ppermute | solution.py:48
  2.8 1.0 copy-start.4
  3.9 1.0 copy-start.5
  4.9 1.0 copy-start.6
  6.0 1.0 copy-start.7
  7.7 0.9 copy-start.15
  8.6 0.9 copy-start.17
  10.9 4.9 %copy-start = (bf16[256,1024]{1,0:T(8,128)(2,1)S(1)}, bf16[256,1024]{1,0:T(8,128)(2,1)}, u32[]{:S(2)}) copy-start(bf16[256,1024]{1,0:T(8,128)(2,1)} %own_hbm.2) | copy-start | bytes 1572868
  10.9 10.8 %copy-start.31 = (s32[1024]{0:T(1024)S(1)}, s32[1024]{0:T(1024)}, u32[]{:S(2)}) copy-start(s32[1024]{0:T(1024)} %param.21) | copy-start | bytes 12292
  10.9 16.5 %copy-start.16 = (f32[256,128]{1,0:T(8,128)S(1)}, f32[256,128]{1,0:T(8,128)}, u32[]{:S(2)}) copy-start(f32[256,128]{1,0:T(8,128)} %constant.104.clone.cb_ref) | copy-start | bytes 393220
  10.9 16.5 %copy-start.18 = (f32[256,128]{1,0:T(8,128)S(1)}, f32[256,128]{1,0:T(8,128)}, u32[]{:S(2)}) copy-start(f32[256,128]{1,0:T(8,128)} %constant.105.clone.sb_ref) | copy-start | bytes 393220
  11.0 16.5 %copy-start.21 = (f32[32,128]{1,0:T(8,128)S(1)}, f32[32,128]{1,0:T(8,128)}, u32[]{:S(2)}) copy-start(f32[32,128]{1,0:T(8,128)} %constant.102.clone.ca_ref) | copy-start | bytes 49156
  11.0 16.5 %copy-start.23 = (f32[32,128]{1,0:T(8,128)S(1)}, f32[32,128]{1,0:T(8,128)}, u32[]{:S(2)}) copy-start(f32[32,128]{1,0:T(8,128)} %constant.103.clone.sa_ref) | copy-start | bytes 49156
  13.4 0.8 copy-start.24
  14.2 0.8 copy-start.26
  15.0 0.8 copy-start.28
  15.8 26.5 %collective-permute-start.1 = (bf16[128,1024]{1,0:T(8,128)(2,1)S(1)}, bf16[128,1024]{1,0:T(8,128)(2,1)}, u32[]{:S(2)}, u32[]{:S(2)}) collective-permute-start(bf16[128,1024]{1,0:T(8,128)(2,1)S(1)} %constant_dynamic-slice_fusion.5), channel_id=1, source_target_pairs={{0,1},{1,2},{2,3},{3,0},{4,5},{5,6},{6,7},{7,4},{8,9},{9,10},{10,1... | collective-permute-start | bytes 786440 | tf_op jit(solution)/shard_map/ppermute | solution.py:44
  17.5 24.8 %collective-permute-start.2 = (bf16[128,1024]{1,0:T(8,128)(2,1)S(1)}, bf16[128,1024]{1,0:T(8,128)(2,1)}, u32[]{:S(2)}, u32[]{:S(2)}) collective-permute-start(bf16[128,1024]{1,0:T(8,128)(2,1)S(1)} %constant_dynamic-slice_fusion.5), channel_id=1, source_target_pairs={{0,2},{1,3},{2,0},{3,1},{4,6},{5,7},{6,4},{7,5},{8,10},{9,11},{10,... | collective-permute-start | bytes 786440 | tf_op jit(solution)/shard_map/ppermute | solution.py:44
  20.4 21.9 %collective-permute-start.3 = (bf16[128,1024]{1,0:T(8,128)(2,1)S(1)}, bf16[128,1024]{1,0:T(8,128)(2,1)}, u32[]{:S(2)}, u32[]{:S(2)}) collective-permute-start(bf16[128,1024]{1,0:T(8,128)(2,1)S(1)} %constant_dynamic-slice_fusion.5), channel_id=1, source_target_pairs={{0,3},{1,0},{2,1},{3,2},{4,7},{5,4},{6,5},{7,6},{8,11},{9,8},{10,9... | collective-permute-start | bytes 786440 | tf_op jit(solution)/shard_map/ppermute | solution.py:44
  21.7 5.5 %collective-permute-start.4 = (s32[256]{0:T(256)S(1)}, s32[256]{0:T(256)S(1)}, u32[]{:S(2)}, u32[]{:S(2)}) collective-permute-start(s32[256]{0:T(256)S(1)} %slice.10), channel_id=1, source_target_pairs={{0,8},{4,12},{8,16},{12,20},{16,24},{20,28},{24,32},{28,36},{32,40... | collective-permute-start | bytes 3080 | tf_op jit(solution)/shard_map/ppermute | solution.py:48
  27.5 1.0 copy-start.25
  28.5 1.0 copy-start.27
  29.6 1.0 copy-start.29
  42.3 13.3 %copy-start.8 = (bf16[256,1024]{1,0:T(8,128)(2,1)S(1)}, bf16[256,1024]{1,0:T(8,128)(2,1)}, u32[]{:S(2)}) copy-start(bf16[256,1024]{1,0:T(8,128)(2,1)} %emb_ref.3) | copy-start | bytes 1572868
  43.6 12.0 %collective-permute-start.8 = (bf16[3,128,1024]{2,1,0:T(8,128)(2,1)S(1)}, bf16[3,128,1024]{2,1,0:T(8,128)(2,1)S(1)}, u32[]{:S(2)}, u32[]{:S(2)}) collective-permute-start(bf16[3,128,1024]{2,1,0:T(8,128)(2,1)S(1)} %pad_maximum_fusion.mine_hbm), channel_id=1, source_target_pairs={{0,4},{4,0},{1,5},{5,1},{2,6},{6,2},{3,7},{7,3},{8,12},{12,8},{9,1... | collective-permute-start | bytes 2359304 | tf_op jit(solution)/shard_map/ppermute | solution.py:44
  44.8 10.1 %collective-permute-start.5 = (bf16[272,256]{1,0:T(8,128)(2,1)}, bf16[272,256]{1,0:T(8,128)(2,1)S(1)}, u32[]{:S(2)}, u32[]{:S(2)}) collective-permute-start(bf16[272,256]{1,0:T(8,128)(2,1)} %get-tuple-element.65), channel_id=1, source_target_pairs={{0,1},{1,2},{2,3},{3,0},{4,5},{5,6},{6,7},{7,4},{8,9},{9,10},{10,1... | collective-permute-start | bytes 417800 | tf_op jit(solution)/shard_map/ppermute | solution.py:44
  45.5 9.5 %collective-permute-start.6 = (bf16[272,256]{1,0:T(8,128)(2,1)}, bf16[272,256]{1,0:T(8,128)(2,1)S(1)}, u32[]{:S(2)}, u32[]{:S(2)}) collective-permute-start(bf16[272,256]{1,0:T(8,128)(2,1)} %get-tuple-element.64), channel_id=1, source_target_pairs={{0,2},{1,3},{2,0},{3,1},{4,6},{5,7},{6,4},{7,5},{8,10},{9,11},{10,... | collective-permute-start | bytes 417800 | tf_op jit(solution)/shard_map/ppermute | solution.py:44
  46.6 9.0 %collective-permute-start.7 = (bf16[272,256]{1,0:T(8,128)(2,1)}, bf16[272,256]{1,0:T(8,128)(2,1)S(1)}, u32[]{:S(2)}, u32[]{:S(2)}) collective-permute-start(bf16[272,256]{1,0:T(8,128)(2,1)} %get-tuple-element.63), channel_id=1, source_target_pairs={{0,3},{1,0},{2,1},{3,2},{4,7},{5,4},{6,5},{7,6},{8,11},{9,8},{10,9... | collective-permute-start | bytes 417800 | tf_op jit(solution)/shard_map/ppermute | solution.py:44
  55.6 8.6 %copy-start.2 = (bf16[4,256,1024]{2,1,0:T(8,128)(2,1)S(1)}, bf16[4,256,1024]{2,1,0:T(8,128)(2,1)}, u32[]{:S(2)}) copy-start(bf16[4,256,1024]{2,1,0:T(8,128)(2,1)} %w_ref.7) | copy-start | bytes 6291460
  57.7 6.4 %collective-permute-start.9 = (bf16[272,256]{1,0:T(8,128)(2,1)S(1)}, bf16[272,256]{1,0:T(8,128)(2,1)S(1)}, u32[]{:S(2)}, u32[]{:S(2)}) collective-permute-start(bf16[272,256]{1,0:T(8,128)(2,1)S(1)} %get-tuple-element.62), channel_id=1, source_target_pairs={{0,1},{1,2},{2,3},{3,0},{4,5},{5,6},{6,7},{7,4},{8,9},{9,10},{10,1... | collective-permute-start | bytes 417800 | tf_op jit(solution)/shard_map/ppermute | solution.py:44
  58.2 9.9 %collective-permute-start.11 = (bf16[272,256]{1,0:T(8,128)(2,1)S(1)}, bf16[272,256]{1,0:T(8,128)(2,1)S(1)}, u32[]{:S(2)}, u32[]{:S(2)}) collective-permute-start(bf16[272,256]{1,0:T(8,128)(2,1)S(1)} %get-tuple-element.61), channel_id=1, source_target_pairs={{0,2},{1,3},{2,0},{3,1},{4,6},{5,7},{6,4},{7,5},{8,10},{9,11},{10,... | collective-permute-start | bytes 417800 | tf_op jit(solution)/shard_map/ppermute | solution.py:44
  61.7 7.5 %collective-permute-start.13 = (bf16[272,256]{1,0:T(8,128)(2,1)S(1)}, bf16[272,256]{1,0:T(8,128)(2,1)S(1)}, u32[]{:S(2)}, u32[]{:S(2)}) collective-permute-start(bf16[272,256]{1,0:T(8,128)(2,1)S(1)} %get-tuple-element.60), channel_id=1, source_target_pairs={{0,3},{1,0},{2,1},{3,2},{4,7},{5,4},{6,5},{7,6},{8,11},{9,8},{10,9... | collective-permute-start | bytes 417800 | tf_op jit(solution)/shard_map/ppermute | solution.py:44
  64.7 7.4 %collective-permute-start.10 = (bf16[64,1024]{1,0:T(8,128)(2,1)S(1)}, bf16[64,1024]{1,0:T(8,128)(2,1)S(1)}, u32[]{:S(2)}, u32[]{:S(2)}) collective-permute-start(bf16[64,1024]{1,0:T(8,128)(2,1)S(1)} %short_part.5), channel_id=1, source_target_pairs={{0,3},{1,0},{2,1},{3,2},{4,7},{5,4},{6,5},{7,6},{8,11},{9,8},{10,9... | collective-permute-start | bytes 393224 | tf_op jit(solution)/shard_map/ppermute | solution.py:44
  68.6 7.4 %collective-permute-start.12 = (bf16[64,1024]{1,0:T(8,128)(2,1)S(1)}, bf16[64,1024]{1,0:T(8,128)(2,1)S(1)}, u32[]{:S(2)}, u32[]{:S(2)}) collective-permute-start(bf16[64,1024]{1,0:T(8,128)(2,1)S(1)} %short_part.6), channel_id=1, source_target_pairs={{0,2},{1,3},{2,0},{3,1},{4,6},{5,7},{6,4},{7,5},{8,10},{9,11},{10,... | collective-permute-start | bytes 393224 | tf_op jit(solution)/shard_map/ppermute | solution.py:44
  69.8 7.6 %collective-permute-start.14 = (bf16[64,1024]{1,0:T(8,128)(2,1)S(1)}, bf16[64,1024]{1,0:T(8,128)(2,1)S(1)}, u32[]{:S(2)}, u32[]{:S(2)}) collective-permute-start(bf16[64,1024]{1,0:T(8,128)(2,1)S(1)} %short_part.7), channel_id=1, source_target_pairs={{0,1},{1,2},{2,3},{3,0},{4,5},{5,6},{6,7},{7,4},{8,9},{9,10},{10,1... | collective-permute-start | bytes 393224 | tf_op jit(solution)/shard_map/ppermute | solution.py:44
  70.9 15.6 %copy-start.9 = (bf16[1024,256]{1,0:T(8,128)(2,1)S(1)}, bf16[1024,256]{1,0:T(8,128)(2,1)}, u32[]{:S(2)}) copy-start(bf16[1024,256]{1,0:T(8,128)(2,1)} %wq_ref.1) | copy-start | bytes 1572868
  70.9 15.6 %copy-start.10 = (bf16[1024,256]{1,0:T(8,128)(2,1)S(1)}, bf16[1024,256]{1,0:T(8,128)(2,1)}, u32[]{:S(2)}) copy-start(bf16[1024,256]{1,0:T(8,128)(2,1)} %wk_ref.1) | copy-start | bytes 1572868
  70.9 15.6 %copy-start.11 = (bf16[1024,256]{1,0:T(8,128)(2,1)S(1)}, bf16[1024,256]{1,0:T(8,128)(2,1)}, u32[]{:S(2)}) copy-start(bf16[1024,256]{1,0:T(8,128)(2,1)} %wv_ref.1) | copy-start | bytes 1572868
  70.9 15.6 %copy-start.13 = (f32[1024]{0:T(1024)S(1)}, f32[1024]{0:T(1024)}, u32[]{:S(2)}) copy-start(f32[1024]{0:T(1024)} %param.29) | copy-start | bytes 12292
  70.9 15.6 %copy-start.19 = (f32[256,128]{1,0:T(8,128)S(1)}, f32[256,128]{1,0:T(8,128)}, u32[]{:S(2)}) copy-start(f32[256,128]{1,0:T(8,128)} %constant.105.clone.sb_ref) | copy-start | bytes 393220
  77.4 8.5 %collective-permute-start.15 = (bf16[64,1024]{1,0:T(8,128)(2,1)S(1)}, bf16[64,1024]{1,0:T(8,128)(2,1)S(1)}, u32[]{:S(2)}, u32[]{:S(2)}) collective-permute-start(bf16[64,1024]{1,0:T(8,128)(2,1)S(1)} %add_convert_fusion.s0), channel_id=1, source_target_pairs={{0,1},{1,2},{2,3},{3,0},{4,5},{5,6},{6,7},{7,4},{8,9},{9,10},{10,1... | collective-permute-start | bytes 393224 | tf_op jit(solution)/shard_map/ppermute | solution.py:44
  77.5 8.4 %collective-permute-start.16 = (bf16[64,1024]{1,0:T(8,128)(2,1)S(1)}, bf16[64,1024]{1,0:T(8,128)(2,1)S(1)}, u32[]{:S(2)}, u32[]{:S(2)}) collective-permute-start(bf16[64,1024]{1,0:T(8,128)(2,1)S(1)} %add_convert_fusion.s0), channel_id=1, source_target_pairs={{0,2},{1,3},{2,0},{3,1},{4,6},{5,7},{6,4},{7,5},{8,10},{9,11},{10,... | collective-permute-start | bytes 393224 | tf_op jit(solution)/shard_map/ppermute | solution.py:44
  79.5 7.0 %collective-permute-start.17 = (bf16[64,1024]{1,0:T(8,128)(2,1)S(1)}, bf16[64,1024]{1,0:T(8,128)(2,1)S(1)}, u32[]{:S(2)}, u32[]{:S(2)}) collective-permute-start(bf16[64,1024]{1,0:T(8,128)(2,1)S(1)} %add_convert_fusion.s0), channel_id=1, source_target_pairs={{0,3},{1,0},{2,1},{3,2},{4,7},{5,4},{6,5},{7,6},{8,11},{9,8},{10,9... | collective-permute-start | bytes 393224 | tf_op jit(solution)/shard_map/ppermute | solution.py:44
  86.6 18.5 %copy-start.1 = (bf16[256,1024]{1,0:T(8,128)(2,1)S(1)}, bf16[256,1024]{1,0:T(8,128)(2,1)}, u32[]{:S(2)}) copy-start(bf16[256,1024]{1,0:T(8,128)(2,1)} %own_hbm.3) | copy-start | bytes 1572868
  100.6 4.9 %collective-permute-start.23 = (bf16[4,256,128]{2,1,0:T(8,128)(2,1)S(1)}, bf16[4,256,128]{2,1,0:T(8,128)(2,1)S(1)}, u32[]{:S(2)}, u32[]{:S(2)}) collective-permute-start(bf16[4,256,128]{2,1,0:T(8,128)(2,1)S(1)} %slice.11), channel_id=1, source_target_pairs={{0,4},{4,0},{1,5},{5,1},{2,6},{6,2},{3,7},{7,3},{8,12},{12,8},{9,1... | collective-permute-start | bytes 786440 | tf_op jit(solution)/shard_map/ppermute | solution.py:44
  100.7 14.5 %collective-permute-start.24 = (bf16[4,256,128]{2,1,0:T(8,128)(2,1)S(1)}, bf16[4,256,128]{2,1,0:T(8,128)(2,1)S(1)}, u32[]{:S(2)}, u32[]{:S(2)}) collective-permute-start(bf16[4,256,128]{2,1,0:T(8,128)(2,1)S(1)} %slice.11), channel_id=1, source_target_pairs={{0,8},{8,16},{16,24},{24,0},{1,9},{9,17},{17,25},{25,1},{2,10},{10... | collective-permute-start | bytes 786440 | tf_op jit(solution)/shard_map/ppermute | solution.py:44
  103.4 15.2 %collective-permute-start.26 = (bf16[4,256,128]{2,1,0:T(8,128)(2,1)S(1)}, bf16[4,256,128]{2,1,0:T(8,128)(2,1)S(1)}, u32[]{:S(2)}, u32[]{:S(2)}) collective-permute-start(bf16[4,256,128]{2,1,0:T(8,128)(2,1)S(1)} %slice.11), channel_id=1, source_target_pairs={{0,24},{8,0},{16,8},{24,16},{1,25},{9,1},{17,9},{25,17},{2,26},{10... | collective-permute-start | bytes 786440 | tf_op jit(solution)/shard_map/ppermute | solution.py:44
  103.4 17.6 %collective-permute-start.21 = (bf16[4,256,128]{2,1,0:T(8,128)(2,1)S(1)}, bf16[4,256,128]{2,1,0:T(8,128)(2,1)S(1)}, u32[]{:S(2)}, u32[]{:S(2)}) collective-permute-start(bf16[4,256,128]{2,1,0:T(8,128)(2,1)S(1)} %slice.11), channel_id=1, source_target_pairs={{0,16},{8,24},{16,0},{24,8},{1,17},{9,25},{17,1},{25,9},{2,18},{10... | collective-permute-start | bytes 786440 | tf_op jit(solution)/shard_map/ppermute | solution.py:44
  105.0 28.2 %collective-permute-start.18 = (bf16[128,1024]{1,0:T(8,128)(2,1)S(1)}, bf16[128,1024]{1,0:T(8,128)(2,1)S(1)}, u32[]{:S(2)}, u32[]{:S(2)}) collective-permute-start(bf16[128,1024]{1,0:T(8,128)(2,1)S(1)} %constant_dynamic-slice_fusion), channel_id=1, source_target_pairs={{0,1},{1,2},{2,3},{3,0},{4,5},{5,6},{6,7},{7,4},{8,9},{9,10},{10,1... | collective-permute-start | bytes 786440 | tf_op jit(solution)/shard_map/ppermute | solution.py:44
  105.5 27.7 %collective-permute-start.19 = (bf16[128,1024]{1,0:T(8,128)(2,1)S(1)}, bf16[128,1024]{1,0:T(8,128)(2,1)S(1)}, u32[]{:S(2)}, u32[]{:S(2)}) collective-permute-start(bf16[128,1024]{1,0:T(8,128)(2,1)S(1)} %constant_dynamic-slice_fusion), channel_id=1, source_target_pairs={{0,2},{1,3},{2,0},{3,1},{4,6},{5,7},{6,4},{7,5},{8,10},{9,11},{10,... | collective-permute-start | bytes 786440 | tf_op jit(solution)/shard_map/ppermute | solution.py:44
  115.2 8.4 %collective-permute-start.25 = (bf16[4,256,128]{2,1,0:T(8,128)(2,1)S(1)}, bf16[4,256,128]{2,1,0:T(8,128)(2,1)S(1)}, u32[]{:S(2)}, u32[]{:S(2)}) collective-permute-start(bf16[4,256,128]{2,1,0:T(8,128)(2,1)S(1)} %collective-permute-done.24.refs_0_), channel_id=1, source_target_pairs={{0,4},{4,0},{1,5},{5,1},{2,6},{6,2},{3,7},{7,3},{8,12},{12,8},{9,1... | collective-permute-start | bytes 786440 | tf_op jit(solution)/shard_map/ppermute | solution.py:44
  118.6 5.9 %collective-permute-start.27 = (bf16[4,256,128]{2,1,0:T(8,128)(2,1)S(1)}, bf16[4,256,128]{2,1,0:T(8,128)(2,1)S(1)}, u32[]{:S(2)}, u32[]{:S(2)}) collective-permute-start(bf16[4,256,128]{2,1,0:T(8,128)(2,1)S(1)} %collective-permute-done.26.refs_2_), channel_id=1, source_target_pairs={{0,4},{4,0},{1,5},{5,1},{2,6},{6,2},{3,7},{7,3},{8,12},{12,8},{9,1... | collective-permute-start | bytes 786440 | tf_op jit(solution)/shard_map/ppermute | solution.py:44
  121.0 12.3 %collective-permute-start.20 = (bf16[128,1024]{1,0:T(8,128)(2,1)S(1)}, bf16[128,1024]{1,0:T(8,128)(2,1)S(1)}, u32[]{:S(2)}, u32[]{:S(2)}) collective-permute-start(bf16[128,1024]{1,0:T(8,128)(2,1)S(1)} %constant_dynamic-slice_fusion), channel_id=1, source_target_pairs={{0,3},{1,0},{2,1},{3,2},{4,7},{5,4},{6,5},{7,6},{8,11},{9,8},{10,9... | collective-permute-start | bytes 786440 | tf_op jit(solution)/shard_map/ppermute | solution.py:44
  123.6 6.6 %collective-permute-start.22 = (bf16[4,256,128]{2,1,0:T(8,128)(2,1)S(1)}, bf16[4,256,128]{2,1,0:T(8,128)(2,1)S(1)}, u32[]{:S(2)}, u32[]{:S(2)}) collective-permute-start(bf16[4,256,128]{2,1,0:T(8,128)(2,1)S(1)} %collective-permute-done.21.refs_0_), channel_id=1, source_target_pairs={{0,4},{4,0},{1,5},{5,1},{2,6},{6,2},{3,7},{7,3},{8,12},{12,8},{9,1... | collective-permute-start | bytes 786440 | tf_op jit(solution)/shard_map/ppermute | solution.py:44
  133.2 15.3 %copy-start.3 = (bf16[1024,1024]{1,0:T(8,128)(2,1)S(1)}, bf16[1024,1024]{1,0:T(8,128)(2,1)}, u32[]{:S(2)}) copy-start(bf16[1024,1024]{1,0:T(8,128)(2,1)} %up_hbm.1) | copy-start | bytes 6291460
  133.2 15.3 %copy-start.14 = (f32[1024]{0:T(1024)S(1)}, f32[1024]{0:T(1024)}, u32[]{:S(2)}) copy-start(f32[1024]{0:T(1024)} %param.34) | copy-start | bytes 12292
  133.4 15.2 %collective-permute-start.28 = (bf16[3,128,1024]{2,1,0:T(8,128)(2,1)S(1)}, bf16[3,128,1024]{2,1,0:T(8,128)(2,1)S(1)}, u32[]{:S(2)}, u32[]{:S(2)}) collective-permute-start(bf16[3,128,1024]{2,1,0:T(8,128)(2,1)S(1)} %pad_maximum_fusion.1.mine_hbm), channel_id=1, source_target_pairs={{0,4},{4,0},{1,5},{5,1},{2,6},{6,2},{3,7},{7,3},{8,12},{12,8},{9,1... | collective-permute-start | bytes 2359304 | tf_op jit(solution)/shard_map/ppermute | solution.py:44
  148.6 17.9 %copy-start.30 = (bf16[1024,4,256]{2,1,0:T(4,128)(2,1)S(1)}, bf16[1024,4,256]{2,1,0:T(4,128)(2,1)}, u32[]{:S(2)}) copy-start(bf16[1024,4,256]{2,1,0:T(4,128)(2,1)} %param.37) | copy-start | bytes 6291460
  152.8 8.7 %collective-permute-start.29 = (bf16[64,1024]{1,0:T(8,128)(2,1)S(1)}, bf16[64,1024]{1,0:T(8,128)(2,1)S(1)}, u32[]{:S(2)}, u32[]{:S(2)}) collective-permute-start(bf16[64,1024]{1,0:T(8,128)(2,1)S(1)} %get-tuple-element.67), channel_id=1, source_target_pairs={{0,1},{1,2},{2,3},{3,0},{4,5},{5,6},{6,7},{7,4},{8,9},{9,10},{10,1... | collective-permute-start | bytes 393224 | tf_op jit(solution)/shard_map/ppermute | solution.py:44
  153.4 8.1 %collective-permute-start.30 = (bf16[64,1024]{1,0:T(8,128)(2,1)S(1)}, bf16[64,1024]{1,0:T(8,128)(2,1)S(1)}, u32[]{:S(2)}, u32[]{:S(2)}) collective-permute-start(bf16[64,1024]{1,0:T(8,128)(2,1)S(1)} %get-tuple-element.69), channel_id=1, source_target_pairs={{0,2},{1,3},{2,0},{3,1},{4,6},{5,7},{6,4},{7,5},{8,10},{9,11},{10,... | collective-permute-start | bytes 393224 | tf_op jit(solution)/shard_map/ppermute | solution.py:44
  154.8 7.3 %collective-permute-start.31 = (bf16[64,1024]{1,0:T(8,128)(2,1)S(1)}, bf16[64,1024]{1,0:T(8,128)(2,1)S(1)}, u32[]{:S(2)}, u32[]{:S(2)}) collective-permute-start(bf16[64,1024]{1,0:T(8,128)(2,1)S(1)} %get-tuple-element.68), channel_id=1, source_target_pairs={{0,3},{1,0},{2,1},{3,2},{4,7},{5,4},{6,5},{7,6},{8,11},{9,8},{10,9... | collective-permute-start | bytes 393224 | tf_op jit(solution)/shard_map/ppermute | solution.py:44
  162.2 6.8 %collective-permute-start.32 = (bf16[64,1024]{1,0:T(8,128)(2,1)S(1)}, bf16[64,1024]{1,0:T(8,128)(2,1)S(1)}, u32[]{:S(2)}, u32[]{:S(2)}) collective-permute-start(bf16[64,1024]{1,0:T(8,128)(2,1)S(1)} %fusion.3.s0), channel_id=1, source_target_pairs={{0,1},{1,2},{2,3},{3,0},{4,5},{5,6},{6,7},{7,4},{8,9},{9,10},{10,1... | collective-permute-start | bytes 393224 | tf_op jit(solution)/shard_map/ppermute | solution.py:44
  163.2 8.9 %collective-permute-start.33 = (bf16[64,1024]{1,0:T(8,128)(2,1)S(1)}, bf16[64,1024]{1,0:T(8,128)(2,1)S(1)}, u32[]{:S(2)}, u32[]{:S(2)}) collective-permute-start(bf16[64,1024]{1,0:T(8,128)(2,1)S(1)} %fusion.3.s0), channel_id=1, source_target_pairs={{0,2},{1,3},{2,0},{3,1},{4,6},{5,7},{6,4},{7,5},{8,10},{9,11},{10,... | collective-permute-start | bytes 393224 | tf_op jit(solution)/shard_map/ppermute | solution.py:44
  166.4 5.8 %collective-permute-start.34 = (bf16[64,1024]{1,0:T(8,128)(2,1)S(1)}, bf16[64,1024]{1,0:T(8,128)(2,1)S(1)}, u32[]{:S(2)}, u32[]{:S(2)}) collective-permute-start(bf16[64,1024]{1,0:T(8,128)(2,1)S(1)} %fusion.3.s0), channel_id=1, source_target_pairs={{0,3},{1,0},{2,1},{3,2},{4,7},{5,4},{6,5},{7,6},{8,11},{9,8},{10,9... | collective-permute-start | bytes 393224 | tf_op jit(solution)/shard_map/ppermute | solution.py:44
  (3 other events, 2.1 us)

commit v3 on v2

--- a/solution.py
+++ b/solution.py
@@ -37,7 +37,8 @@
     near = np.arange(256)[:, None] % period[None]
     a = coarse * (2.0 * np.pi / period)[None]
     b = near * (2.0 * np.pi / period)[None]
-    return [t.astype(np.float32) for t in (np.cos(a), np.sin(a), np.cos(b), np.sin(b))]
+    parts = [np.cos(a), np.sin(a), np.cos(b), np.sin(b)]
+    return np.concatenate(parts, axis=0).astype(np.float32)
 
 
 def shift(value, axis, steps, count):
@@ -83,7 +84,11 @@
     return high, low
 
 
-def turn_tables(ca, sa, cb, sb):
+def turn_tables(turn_ref, far):
+    ca = turn_ref[pl.ds(far, 1), :]
+    sa = turn_ref[pl.ds(32 + far, 1), :]
+    cb = turn_ref[64:320, :]
+    sb = turn_ref[320:576, :]
     cosine = ca * cb - sa * sb
     sine = sa * cb + ca * sb
     return jnp.concatenate([cosine, cosine], axis=1), jnp.concatenate([sine, sine], axis=1)
@@ -100,61 +105,51 @@
     return (plain * cosine + other * sine).astype(bf16)
 
 
-def fine_own_kernel(
-    ids_ref, emb_ref, gain_ref, ca_ref, sa_ref, cb_ref, sb_ref, wq_hbm, wk_hbm, wv_hbm,
-    tab_ref, q_ref, k_ref, v_ref, w_ref, sems,
-):
-    copies = begin_copies(
-        [(w, w_ref.at[n]) for n, w in enumerate((wq_hbm, wk_hbm, wv_hbm))], sems
-    )
-    wq_ref, wk_ref, wv_ref = (w_ref.at[n] for n in range(3))
-    fine_in = norm_rows(emb_ref[...].astype(f32), gain_ref[...])
-    finish_copies(copies)
-    tq = dot(fine_in, wq_ref[...]) * q_scale
-    tk = dot(fine_in, wk_ref[...])
-    for n, table in enumerate((tq, partner(tq), tk, partner(tk))):
-        high, low = halves(table)
-        tab_ref[2 * n] = high
-        tab_ref[2 * n + 1] = low
-    tab_ref[8] = dot(fine_in, wv_ref[...]).astype(bf16)
-    cb = cb_ref[...]
-    sb = sb_ref[...]
-    for block in range(ROWS // BLOCK):
-        at = slice(block * BLOCK, (block + 1) * BLOCK)
-        hot = pick(ids_ref[at, :])
-        far = PAST // BLOCK + block
-        cosine, sine = turn_tables(ca_ref[far : far + 1, :], sa_ref[far : far + 1, :], cb, sb)
-        q_ref[at, :] = turned_rows(hot, tab_ref, 0, cosine, sine)
-        k_ref[at, :] = turned_rows(hot, tab_ref, 4, cosine, sine)
-        v_ref[at, :] = dot(hot, tab_ref[8]).astype(bf16)
-
-
 def fine_kernel(
-    place_ref, ids_ref, tab_ref, q_ref, k_own_ref, v_own_ref, ca_ref, sa_ref, cb_ref, sb_ref,
-    out_ref, k_ref, v_ref,
+    where_ref, ids_ref, gain_ref, turn_hbm, emb_hbm, wq_hbm, wk_hbm, wv_hbm,
+    o0, o1, o2, o3, tab_ref, q_ref, k_ref, v_ref, turn_ref, emb_ref, w_ref, sems,
 ):
     step = pl.program_id(0)
-    lowest = jnp.maximum(PAST - place_ref[0] * ROWS, 0)
+    head = where_ref[1]
+    quarter = lax.rem(head + step, 4)
+    outs = (o0, o1, o2, o3)
+    lowest = jnp.maximum(PAST - where_ref[0] * ROWS, 0)
     head_lane = lax.broadcasted_iota(jnp.int32, (1, SHARE), 1) // HEAD_DIM
 
     @pl.when(step == 0)
     def _():
-        cb = cb_ref[...]
-        sb = sb_ref[...]
-        k_ref[PAST:, :] = k_own_ref[...]
-        v_ref[PAST:, :] = v_own_ref[...]
-        for block in range(PAST // BLOCK):
-            at = slice(block * BLOCK, (block + 1) * BLOCK)
-            hot = pick(ids_ref[at, :])
-            cosine, sine = turn_tables(
-                ca_ref[block : block + 1, :], sa_ref[block : block + 1, :], cb, sb
-            )
-            k_ref[at, :] = turned_rows(hot, tab_ref, 4, cosine, sine)
-            v_ref[at, :] = dot(hot, tab_ref[8]).astype(bf16)
-
-        halo_q = turned_rows(
-            pick(ids_ref[PAST - HALO : PAST, :]), tab_ref, 0, cosine[-HALO:], sine[-HALO:]
-        )
+        pairs = [(emb_hbm, emb_ref), (turn_hbm, turn_ref)]
+        for n, w in enumerate((wq_hbm, wk_hbm, wv_hbm)):
+            for part in range(2):
+                rows = pl.ds(part * 512, 512)
+                pairs.append((w.at[rows], w_ref.at[n, rows]))
+        copies = begin_copies(pairs, sems)
+        finish_copies(copies[:1])
+        fine_in = norm_rows(emb_ref[...].astype(f32), gain_ref[...])
+        finish_copies(copies[1:])
+        tq = dot(fine_in, w_ref[0]) * q_scale
+        tk = dot(fine_in, w_ref[1])
+        for n, table in enumerate((tq, partner(tq), tk, partner(tk))):
+            high, low = halves(table)
+            tab_ref[2 * n] = high
+            tab_ref[2 * n + 1] = low
+        tab_ref[8] = dot(fine_in, w_ref[2]).astype(bf16)
+
+        def build(block, with_q):
+            begin = pl.multiple_of(block * BLOCK, BLOCK)
+            hot = pick(ids_ref[pl.ds(begin, BLOCK), :])
+            cosine, sine = turn_tables(turn_ref, block)
+            k_ref[pl.ds(begin, BLOCK), :] = turned_rows(hot, tab_ref, 4, cosine, sine)
+            v_ref[pl.ds(begin, BLOCK), :] = dot(hot, tab_ref[8]).astype(bf16)
+            if with_q:
+                at = pl.multiple_of(begin - (PAST - BLOCK), BLOCK)
+                q_ref[pl.ds(at, BLOCK), :] = turned_rows(hot, tab_ref, 0, cosine, sine)
+            return 0
+
+        early = PAST // BLOCK - 1
+        lax.fori_loop(0, early, lambda block, _: build(block, False), 0)
+        lax.fori_loop(early, KEYS // BLOCK, lambda block, _: build(block, True), 0)
+        halo_q = q_ref[BLOCK - HALO : BLOCK, :]
         stacked = jnp.concatenate(
             [jnp.where(head_lane == h, halo_q, jnp.zeros_like(halo_q)) for h in range(4)], axis=0
         )
@@ -170,12 +165,16 @@
         result = jnp.zeros((HALO, SHARE), f32)
         for h in range(4):
             result = jnp.where(head_lane == h, mixed[h * HALO : (h + 1) * HALO], result)
-        out_ref[0:HALO, :] = result.astype(bf16)
-
-    begin = pl.multiple_of((step + 1) * BLOCK, BLOCK)
+        for s, out_ref in enumerate(outs):
+
+            @pl.when(lax.rem(head + s, 4) == 0)
+            def _(out_ref=out_ref):
+                out_ref[0:HALO, :] = result.astype(bf16)
+
+    begin = pl.multiple_of((quarter + 1) * BLOCK, BLOCK)
     keys = k_ref[pl.ds(begin, PAST), :]
     values = v_ref[pl.ds(begin, PAST), :]
-    query = q_ref[pl.ds(pl.multiple_of(step * BLOCK, BLOCK), BLOCK), :]
+    query = q_ref[pl.ds(begin, BLOCK), :]
     row = lax.broadcasted_iota(jnp.int32, (BLOCK, BLOCK), 0)
     col = lax.broadcasted_iota(jnp.int32, (BLOCK, BLOCK), 1)
     biases = [
@@ -206,8 +205,16 @@
     result = jnp.concatenate(
         [jnp.where(low_lanes, results[2 * n], results[2 * n + 1]) for n in range(2)], axis=1
     )
-    at = pl.multiple_of(HALO + step * BLOCK, HALO)
-    out_ref[pl.ds(at, BLOCK), :] = result.astype(bf16)
+    result = result.astype(bf16)
+    for s in range(4):
+
+        @pl.when(step == s)
+        def _(s=s):
+            outs[s][HALO:, :] = result
+
+            @pl.when(quarter < 3)
+            def _():
+                outs[(s + 1) % 4][0:HALO, :] = result[BLOCK - HALO :]
 
 
 def vmem():
@@ -218,7 +225,7 @@
     return pl.BlockSpec(memory_space=pltpu.SMEM)
 
 
-def call(kernel, name, shapes, scalars, arrays, scratch=(), grid=None, limit=48, us=2, hbm=()):
+def call(kernel, name, shapes, scalars, arrays, scratch=(), grid=None, limit=16, us=2, hbm=(), free=()):
     one = not isinstance(shapes, (list, tuple))
     extra = {} if grid is None else {"grid": grid}
     return pl.pallas_call(
@@ -226,7 +233,8 @@
         out_shape=shapes,
         in_specs=[smem()] * len(scalars)
         + [vmem()] * len(arrays)
-        + [pl.BlockSpec(memory_space=pl.ANY)] * len(hbm),
+        + [pl.BlockSpec(memory_space=pltpu.HBM)] * len(hbm)
+        + [pl.BlockSpec(memory_space=pl.ANY)] * len(free),
         out_specs=vmem() if one else [vmem()] * len(shapes),
         scratch_shapes=list(scratch),
         compiler_params=pltpu.CompilerParams(vmem_limit_bytes=limit << 20),
@@ -235,7 +243,7 @@
         ),
         name=name,
         **extra,
-    )(*scalars, *arrays, *hbm)
+    )(*scalars, *arrays, *(pltpu.with_memory_space_constraint(a, pltpu.HBM) for a in hbm), *free)
 
 
 def begin_copies(pairs, sems):
@@ -251,18 +259,15 @@
 
 
 def fine_rows_kernel(
-    where_ref, ids_ref, emb_ref, g0, g1, g2, g3, own_hbm, mine_hbm, other_hbm, out_ref, w_ref, sems
+    where_ref, ids_ref, emb_ref, g0, g1, g2, g3, f0, f1, f2, f3, out_ref, w_ref, sems
 ):
-    place, head, core = where_ref[0], where_ref[1], where_ref[2]
-    copies = begin_copies(
-        [(own_hbm, w_ref.at[0:256])]
-        + [(mine_hbm.at[s - 1], w_ref.at[pl.ds(s * 256 + core * 128, 128)]) for s in range(1, 4)]
-        + [
-            (other_hbm.at[s - 1], w_ref.at[pl.ds(s * 256 + 128 - core * 128, 128)])
-            for s in range(1, 4)
-        ],
-        sems,
-    )
+    place, head = where_ref[0], where_ref[1]
+    pairs = []
+    for s, f in enumerate((f0, f1, f2, f3)):
+        for part in range(2):
+            at = pl.ds(part * 128, 128)
+            pairs.append((f.at[at], w_ref.at[pl.ds(s * 256 + part * 128, 128)]))
+    copies = begin_copies(pairs, sems)
     merged = dot(pick(ids_ref[...]), emb_ref[...])
     finish_copies(copies)
     merged += dot(jnp.concatenate([g0[...], g1[...], g2[...], g3[...]], axis=1), w_ref[...])
@@ -289,7 +294,7 @@
 
 
 def coarse_pack_kernel(
-    where_ref, s0, s1, s2, s3, gain_ref, wq_ref, wk_ref, wv_ref, ca_ref, sa_ref, cb_ref, sb_ref,
+    where_ref, s0, s1, s2, s3, gain_ref, wq_ref, wk_ref, wv_ref, turn_ref,
     out_ref, short_ref,
 ):
     place, head = where_ref[0], where_ref[1]
@@ -297,9 +302,7 @@
         begin = pl.multiple_of(lax.rem(head - s + 4, 4) * 64, 64)
         short_ref[pl.ds(begin, 64), :] = ref[...]
     x = norm_rows(short_ref[...].astype(f32), gain_ref[...])
-    cosine, sine = turn_tables(
-        ca_ref[pl.ds(place, 1), :], sa_ref[pl.ds(place, 1), :], cb_ref[...], sb_ref[...]
-    )
+    cosine, sine = turn_tables(turn_ref, place)
 
     def turned(values):
         return values * cosine + partner(values) * sine
@@ -411,16 +414,21 @@
 
 
 def feed_kernel(
-    where_ref, heads_ref, short_ref, gain_ref, own_hbm, mine_hbm, other_hbm, up_hbm, down_hbm,
+    where_ref, heads_ref, short_ref, gain_ref, c0, up_hbm, down_hbm, c1, c2, c3,
     part_ref, first_ref, mixed_ref, all_ref, co_ref, up_ref, down_ref, sems,
 ):
-    head, core = where_ref[1], where_ref[2]
-    pairs = [(own_hbm, co_ref.at[pl.ds(head * 256, 256)])]
-    for s in range(1, 4):
+    head = where_ref[1]
+    pairs = []
+    for s, c in enumerate((c0, c1, c2, c3)):
         source = lax.rem(head - s + 4, 4) * 256
-        pairs.append((mine_hbm.at[s - 1], co_ref.at[pl.ds(source + core * 128, 128)]))
-        pairs.append((other_hbm.at[s - 1], co_ref.at[pl.ds(source + 128 - core * 128, 128)]))
-    copies = begin_copies(pairs + [(up_hbm, up_ref), (down_hbm, down_ref)], sems)
+        for part in range(2):
+            at = pl.ds(part * 128, 128)
+            pairs.append((c.at[at], co_ref.at[pl.ds(source + part * 128, 128)]))
+    for w, w_ref in ((up_hbm, up_ref), (down_hbm, down_ref)):
+        for part in range(4):
+            at = pl.ds(part * 256, 256)
+            pairs.append((w.at[at], w_ref.at[at]))
+    copies = begin_copies(pairs, sems)
     low_lanes = lax.broadcasted_iota(jnp.int32, (1, 128), 1) < 64
     for y in range(4):
         for pair in range(2):
@@ -429,12 +437,12 @@
             at = slice(y * 256 + pair * 128, y * 256 + (pair + 1) * 128)
             mixed_ref[0:128, at] = jnp.where(low_lanes, even, pltpu.roll(odd, 64, 1)).astype(bf16)
             mixed_ref[128:256, at] = jnp.where(low_lanes, pltpu.roll(even, 64, 1), odd).astype(bf16)
-    finish_copies(copies[:7])
+    finish_copies(copies[:8])
     first = short_ref[...].astype(f32) + dot(mixed_ref[...], co_ref[...])
     all_ref[...] = first
     first_ref[...] = all_ref[pl.ds(pl.multiple_of(head * 64, 64), 64), :]
     feed = norm_rows(first, gain_ref[...])
-    finish_copies(copies[7:])
+    finish_copies(copies[8:])
     inner = jax.nn.gelu(dot(feed, up_ref[...])).astype(bf16)
     part_ref[...] = dot(inner, down_ref[...]).astype(bf16).reshape(4, 64, D)
 
@@ -460,9 +468,8 @@
         out_ref[pl.ds(begin, 256), :] = dot(weave, value).astype(bf16)
 
 
-def fetch_rest(weight, core):
-    half = lax.dynamic_slice_in_dim(weight, core * 128, 128, 0)
-    return [shift(half, "head", s, 4) for s in range(1, 4)]
+def fetch_rest(weight):
+    return [shift(weight, "head", s, 4) for s in range(1, 4)]
 
 
 def after(value, gate):
@@ -478,42 +485,40 @@
     head = lax.axis_index("head").astype(jnp.int32)
     x_place = lax.axis_index("x").astype(jnp.int32)
     core = lax.axis_index("core").astype(jnp.int32)
-    tables = [jnp.asarray(t) for t in angle_tables()]
+    tables = jnp.asarray(angle_tables())
     where = jnp.stack([place, head, core])
 
     prior = later(token_ids, SEQ, 1, 32)
-    before = later(token_ids[ROWS - BLOCK :], SEQ, 2, 32)
-    share = jax.ShapeDtypeStruct((ROWS, SHARE), bf16)
-    tab, q, k_own, v_own = call(
-        fine_own_kernel, "fine_own",
-        [jax.ShapeDtypeStruct((9, 256, SHARE), bf16), share, share, share], [],
-        [token_ids[:, None], embedding, fine_norm[None], *tables],
-        [pltpu.VMEM((3, D, SHARE), bf16), pltpu.SemaphoreType.DMA((3,))],
-        hbm=[fine_query, fine_key, fine_value], us=5,
-    )
+    fine_output_held, last_ids = after(fine_output, token_ids[ROWS - BLOCK :])
+    before = later(last_ids, SEQ, 2, 32)
     past_ids = jnp.concatenate([before, prior])
-    fine_output_held, tab = after(fine_output, tab)
-    out_rest = fetch_rest(fine_output_held, core)
-
+    out_rest = fetch_rest(fine_output_held)
+
+    rows = 256 + HALO
+    all_ids = jnp.concatenate([past_ids, token_ids])
     mixed = call(
-        fine_kernel, "fine_attention", jax.ShapeDtypeStruct((HALO + ROWS, SHARE), bf16),
-        [where], [past_ids[:, None], tab, q, k_own, v_own, *tables],
-        [pltpu.VMEM((KEYS, SHARE), bf16), pltpu.VMEM((KEYS, SHARE), bf16)], grid=(4,), us=12,
-    )
-    out_rest, mixed = after(out_rest, mixed)
-    out_mine = jnp.stack(out_rest)
-    out_other = shift(out_mine, "core", 1, 2)
-
-    rows = 256 + HALO
-    got = exchange(lambda d: lax.dynamic_slice_in_dim(mixed, d * 256, rows, 0), "head", 4)
+        fine_kernel, "fine_attention", [jax.ShapeDtypeStruct((rows, SHARE), bf16)] * 4,
+        [where],
+        [all_ids[:, None], fine_norm[None]],
+        [
+            pltpu.VMEM((9, 256, SHARE), bf16), pltpu.VMEM((BLOCK + ROWS, SHARE), bf16),
+            pltpu.VMEM((KEYS, SHARE), bf16), pltpu.VMEM((KEYS, SHARE), bf16),
+            pltpu.VMEM((576, 128), f32), pltpu.VMEM((256, D), bf16),
+            pltpu.VMEM((3, D, SHARE), bf16), pltpu.SemaphoreType.DMA((8,)),
+        ],
+        grid=(4,), us=15, limit=24,
+        hbm=[tables, embedding, fine_query, fine_key, fine_value],
+    )
+
+    got = [mixed[0]] + [shift(mixed[s], "head", s, 4) for s in range(1, 4)]
     own_ids = lax.dynamic_slice_in_dim(
         jnp.concatenate([past_ids[PAST - HALO :], token_ids]), head * 256, rows, 0
     )
     sends = call(
         fine_rows_kernel, "fine_rows", jax.ShapeDtypeStruct((4, rows, SHARE), bf16),
         [where], [own_ids[:, None], embedding, *got],
-        [pltpu.VMEM((D, D), bf16), pltpu.SemaphoreType.DMA((7,))],
-        hbm=[fine_output, out_mine, out_other],
+        [pltpu.VMEM((D, D), bf16), pltpu.SemaphoreType.DMA((8,))],
+        hbm=[fine_output], free=out_rest,
     )
     blocks = exchange(lambda d: lax.dynamic_index_in_dim(sends, d, 0, keepdims=False), "head", 4)
 
@@ -533,7 +538,7 @@
             jax.ShapeDtypeStruct((COARSE_ROWS, D), bf16),
         ],
         [where],
-        [*shorts, coarse_norm[None], coarse_query, coarse_key, coarse_value, *tables],
+        [*shorts, coarse_norm[None], coarse_query, coarse_key, coarse_value, tables],
     )
 
     turned = lax.all_to_all(packed, "z", 0, 0)
@@ -541,29 +546,26 @@
     kv = turned[:, :COARSE_ROWS]
     far = [shift(kv, "core", 1, 2)]
     near = [shift(kv, "x", s, 4) for s in range(1, 4)]
-    far += [shift(part, "core", 1, 2) for part in near]
     steps = jnp.arange(4, dtype=jnp.int32)
     flags = ((x_place - steps + 4) % 4 < x_place).astype(jnp.int32) + (steps == 0) * core
     wide = jax.ShapeDtypeStruct((1024, 128), f32)
     q_all, *sums = call(
         coarse_first_kernel, "coarse_first",
         [jax.ShapeDtypeStruct((1024, 128), bf16), wide, wide, wide], [flags], [turned, far[0]],
-        us=3,
-    )
-    co_rest = fetch_rest(coarse_output_held, core)
+        us=3, limit=24,
+    )
+    co_rest = fetch_rest(coarse_output_held)
+    near_held, q_all = after(near, q_all)
+    far += [shift(part, "core", 1, 2) for part in near_held]
     sums = call(
         functools.partial(coarse_more_kernel, (1, 3), False), "coarse_more", [wide] * 3,
-        [flags], [near[0], far[1], near[2], far[3], q_all, *sums], us=6,
+        [flags], [near[0], far[1], near[2], far[3], q_all, *sums], us=6, limit=24,
     )
     wide_sends = call(
         functools.partial(coarse_more_kernel, (2,), True), "coarse_last",
         jax.ShapeDtypeStruct((16, 128, 128), bf16),
-        [flags], [near[1], far[2], q_all, *sums], [pltpu.VMEM((1024, 128), f32)] * 3, us=3,
-    )
-    co_rest, wide_sends = after(co_rest, wide_sends)
-    co_mine = jnp.stack(co_rest)
-    co_other = shift(co_mine, "core", 1, 2)
-
+        [flags], [near[1], far[2], q_all, *sums], [pltpu.VMEM((1024, 128), f32)] * 3, us=3, limit=24,
+    )
     heads_in = lax.all_to_all(wide_sends, ("z", "head"), 0, 0)
     square = pltpu.VMEM((D, D), bf16)
     parts, first_own = call(
@@ -573,9 +575,9 @@
         [heads_in, short, ffn_norm[None]],
         [
             pltpu.VMEM((COARSE_ROWS, D), bf16), pltpu.VMEM((COARSE_ROWS, D), f32),
-            square, square, square, pltpu.SemaphoreType.DMA((9,)),
+            square, square, square, pltpu.SemaphoreType.DMA((16,)),
         ],
-        hbm=[coarse_output, co_mine, co_other, ffn_up, ffn_down], us=4,
+        hbm=[coarse_output, ffn_up, ffn_down], free=co_rest, us=4, limit=24,
     )
     sums = exchange(lambda d: lax.dynamic_index_in_dim(parts, d, 0, keepdims=False), "head", 4)
     second_own = (first_own + sum(t.astype(f32) for t in sums)).astype(bf16)

time: 176 us -> 171 us (0.972)
  waiting for transfers between devices: 44 us -> 63.2 us
  blocking collectives: 27.6 us -> 13.7 us
  local copies, waits for them, and re-layouts: 16.4 us -> 2.55 us
  Pallas kernels: 37.6 us -> 42.5 us
    all_to_all x1 -> x0, blocking collectives: 15.1 us -> none  [local(): heads_in = lax.all_to_all(wide_sends, ('z', 'head'), 0, 0)]
    ppermute x33 -> x31, waiting for transfers between devices: 42.4 us -> 57.4 us  [shift(): lax.ppermute(value, axis, [(i, (i + steps) % count) for i in range(count)])]
    unnamed x65 -> x23, local copies, waits for them, and re-layouts: 14.2 us -> 1.22 us
    ppermute x33 -> x31, starting transfers between devices: 41.4 us -> 35.8 us  [shift(): lax.ppermute(value, axis, [(i, (i + steps) % count) for i in range(count)])]
    pallas_call x13 -> x12, Pallas kernels: 37.6 us -> 42.5 us  [call(): pl.pallas_call(kernel, out_shape=shapes, in_specs=[smem()] * len(scalars)...]
    all_to_all x0 -> x1, waiting for transfers between devices: none -> 4.17 us  [local(): heads_in = lax.all_to_all(wide_sends, ('z', 'head'), 0, 0)]
    all_to_all x0 -> x1, starting transfers between devices: none -> 4 us  [local(): heads_in = lax.all_to_all(wide_sends, ('z', 'head'), 0, 0)]
  transfers between devices with their start and end apart: 35 -> 34, of which waited for: 17 -> 20; matrix products, arithmetic and copies ran while one was open for 2% -> 2% of each run, Pallas kernels for 16% -> 18%
where the time goes in v3:
time: 171 us; the launch traced here: 169 us
  waiting for transfers between devices  63.2 us (37%)
  starting transfers between devices  45.5 us (27%)
  Pallas kernels  42.5 us (25%)
  blocking collectives  13.7 us (8%)
  local copies, waits for them, and re-layouts  2.55 us (1%)
    ppermute x31, waiting for transfers between devices, shift(): lax.ppermute(value, axis, [(i, (i + steps) % count) for i in range(count)])  57.4 us
    pallas_call x12, Pallas kernels, call(): pl.pallas_call(kernel, out_shape=shapes, in_specs=[smem()] * len(scalars)...  42.5 us
    ppermute x31, starting transfers between devices, shift(): lax.ppermute(value, axis, [(i, (i + steps) % count) for i in range(count)])  35.8 us
    all_to_all x1, blocking collectives, local(): turned = lax.all_to_all(packed, 'z', 0, 0)  13.7 us
    ppermute x2, starting transfers between devices, later(): lax.ppermute(value, axis, [(i, i + steps) for i in range(count - steps)])  5.64 us
    all_to_all x1, waiting for transfers between devices, local(): heads_in = lax.all_to_all(wide_sends, ('z', 'head'), 0, 0)  4.17 us
    all_to_all x1, starting transfers between devices, local(): heads_in = lax.all_to_all(wide_sends, ('z', 'head'), 0, 0)  4 us
  transfers between devices with their start and end apart: 34, of which 20 were waited for; matrix products, arithmetic and copies ran while one was open for 2% of the time, Pallas kernels for 18%

profile of v3, /device:TPU:6, one launch (start us, length us, event | category | flops | bytes accessed | tf_op | source)
XLA Modules:
  0.0 168.9 jit_solution(1217268435297130220)
XLA Ops:
  0.0 1.9 %collective-permute-start = (s32[1024]{0:T(1024)}, s32[1024]{0:T(1024)S(1)}, u32[]{:S(2)}, u32[]{:S(2)}) collective-permute-start(s32[1024]{0:T(1024)} %param.18), channel_id=1, source_target_pairs={{0,4},{4,8},{8,12},{12,16},{16,20},{20,24},{24,28},{28,32},{32,36}... | collective-permute-start | bytes 12296 | tf_op jit(solution)/shard_map/ppermute | solution.py:49
  1.9 0.7 slice.10
  2.6 1.6 collective-permute-start.5
  4.2 2.9 %collective-permute-start.6 = (bf16[256,1024]{1,0:T(8,128)(2,1)}, bf16[256,1024]{1,0:T(8,128)(2,1)S(1)}, u32[]{:S(2)}, u32[]{:S(2)}) collective-permute-start(bf16[256,1024]{1,0:T(8,128)(2,1)} %f0.1), channel_id=1, source_target_pairs={{0,2},{1,3},{2,0},{3,1},{4,6},{5,7},{6,4},{7,5},{8,10},{9,11},{10,... | collective-permute-start | bytes 1572872 | tf_op jit(solution)/shard_map/ppermute | solution.py:45
  7.1 1.3 collective-permute-start.7
  8.4 3.7 %collective-permute-start.1 = (s32[256]{0:T(256)S(1)}, s32[256]{0:T(256)S(1)}, u32[]{:S(2)}, u32[]{:S(2)}) collective-permute-start(s32[256]{0:T(256)S(1)} %slice.10), channel_id=1, source_target_pairs={{0,8},{4,12},{8,16},{12,20},{16,24},{20,28},{24,32},{28,36},{32,40... | collective-permute-start | bytes 3080 | tf_op jit(solution)/shard_map/ppermute | solution.py:49
  12.3 1.6 collective-permute-done.1
  13.9 0.7 pad_add_fusion
  14.6 0.4 broadcast_in_dim.21.ids_ref
  15.0 0.7 copy-done.5
  15.7 16.8 %fine_attention.1 = (bf16[272,256]{1,0:T(8,128)(2,1)S(1)}, bf16[272,256]{1,0:T(8,128)(2,1)S(1)}, bf16[272,256]{1,0:T(8,128)(2,1)S(1)}, bf16[272,256]{1,0:T(8,128)(2,1)S(1)}) custom-call(s32[3]{0:T(128)S(1)} %pad_add_fusion.1.where_ref, s32[2304,1]{1,0:T(8,128)S(1)} %broadcast_in_dim.21.ids_ref, f32[1,1024]{1,0:T(1,128)S(1)} %bitcast.26, ...), custom_call_target="tpu_custom_call" | custom-call | flops 15000000512 | bytes 30000000 | tf_op jit(solution)/shard_map/fine_attention/pallas_call | solution.py:231
  32.5 0.8 collective-permute-start.2
  33.2 0.8 collective-permute-start.3
  34.0 8.5 %collective-permute-done.2.g1 = bf16[272,256]{1,0:T(8,128)(2,1)S(1)} collective-permute-done((bf16[272,256]{1,0:T(8,128)(2,1)S(1)}, bf16[272,256]{1,0:T(8,128)(2,1)S(1)}, u32[]{:S(2)}, u32[]{:S(2)}) %collective-permute-start.2) | collective-permute-done | bytes 139296 | tf_op jit(solution)/shard_map/ppermute | solution.py:45
  42.7 0.1 broadcast_in_dim.20.ids_ref
  42.8 4.8 %collective-permute-done.4.g3 = bf16[272,256]{1,0:T(8,128)(2,1)S(1)} collective-permute-done((bf16[272,256]{1,0:T(8,128)(2,1)S(1)}, bf16[272,256]{1,0:T(8,128)(2,1)S(1)}, u32[]{:S(2)}, u32[]{:S(2)}) %collective-permute-start.4) | collective-permute-done | bytes 139296 | tf_op jit(solution)/shard_map/ppermute | solution.py:45
  47.7 3.0 %fine_rows.1 = bf16[4,272,256]{2,1,0:T(8,128)(2,1)S(1)} custom-call(s32[3]{0:T(128)S(1)} %pad_add_fusion.1.where_ref, s32[272,1]{1,0:T(8,128)S(1)} %broadcast_in_dim.20.ids_ref, bf16[256,1024]{1,0:T(8,128)(2,1)S(1)} %copy-done.1, bf16[272,256]{1,0:T(8,128)(2,1)S(1)} %get-tuple-element.29.g0, bf16[272,256]{1,0:T(8,128)(2,1)S(1)} %collective-permute-done.2.g1, ...), custom_call_target="tpu_custom_call" | custom-call | flops 2000000000 | bytes 4000000 | tf_op jit(solution)/shard_map/fine_rows/pallas_call | solution.py:231
  50.7 0.1 collective-permute-start.10
  50.8 2.2 %collective-permute-start.12 = (bf16[272,256]{1,0:T(8,128)(2,1)S(1)}, bf16[272,256]{1,0:T(8,128)(2,1)S(1)}, u32[]{:S(2)}, u32[]{:S(2)}) collective-permute-start(bf16[272,256]{1,0:T(8,128)(2,1)S(1)} %get-tuple-element.52), channel_id=1, source_target_pairs={{0,3},{1,0},{2,1},{3,2},{4,7},{5,4},{6,5},{7,6},{8,11},{9,8},{10,9... | collective-permute-start | bytes 417800 | tf_op jit(solution)/shard_map/ppermute | solution.py:45
  53.1 4.7 %collective-permute-done.10.group_ref.b2 = bf16[272,256]{1,0:T(8,128)(2,1)S(1)} collective-permute-done((bf16[272,256]{1,0:T(8,128)(2,1)S(1)}, bf16[272,256]{1,0:T(8,128)(2,1)S(1)}, u32[]{:S(2)}, u32[]{:S(2)}) %collective-permute-start.10) | collective-permute-done | bytes 139296 | tf_op jit(solution)/shard_map/ppermute | solution.py:45
  57.7 0.5 short_part.6
  58.2 1.2 collective-permute-start.11
  59.4 0.5 short_part.7
  59.9 1.8 %collective-permute-start.13 = (bf16[64,1024]{1,0:T(8,128)(2,1)S(1)}, bf16[64,1024]{1,0:T(8,128)(2,1)S(1)}, u32[]{:S(2)}, u32[]{:S(2)}) collective-permute-start(bf16[64,1024]{1,0:T(8,128)(2,1)S(1)} %short_part.7), channel_id=1, source_target_pairs={{0,1},{1,2},{2,3},{3,0},{4,5},{5,6},{6,7},{7,4},{8,9},{9,10},{10,1... | collective-permute-start | bytes 393224 | tf_op jit(solution)/shard_map/ppermute | solution.py:45
  61.7 0.5 short_part.5
  62.2 1.5 collective-permute-start.9
  63.8 0.5 short_part.4
  64.2 1.4 collective-permute-done.11
  65.7 1.2 collective-permute-done.13
  66.8 0.4 collective-permute-done.9
  67.3 0.7 collective-permute-start.14
  68.0 3.5 %collective-permute-start.15 = (bf16[64,1024]{1,0:T(8,128)(2,1)S(1)}, bf16[64,1024]{1,0:T(8,128)(2,1)S(1)}, u32[]{:S(2)}, u32[]{:S(2)}) collective-permute-start(bf16[64,1024]{1,0:T(8,128)(2,1)S(1)} %add_convert_fusion.s0), channel_id=1, source_target_pairs={{0,2},{1,3},{2,0},{3,1},{4,6},{5,7},{6,4},{7,5},{8,10},{9,11},{10,... | collective-permute-start | bytes 393224 | tf_op jit(solution)/shard_map/ppermute | solution.py:45
  71.5 2.6 %collective-permute-done.14.s1 = bf16[64,1024]{1,0:T(8,128)(2,1)S(1)} collective-permute-done((bf16[64,1024]{1,0:T(8,128)(2,1)S(1)}, bf16[64,1024]{1,0:T(8,128)(2,1)S(1)}, u32[]{:S(2)}, u32[]{:S(2)}) %collective-permute-start.14) | collective-permute-done | bytes 131104 | tf_op jit(solution)/shard_map/ppermute | solution.py:45
  74.1 1.7 %collective-permute-done.15.s2 = bf16[64,1024]{1,0:T(8,128)(2,1)S(1)} collective-permute-done((bf16[64,1024]{1,0:T(8,128)(2,1)S(1)}, bf16[64,1024]{1,0:T(8,128)(2,1)S(1)}, u32[]{:S(2)}, u32[]{:S(2)}) %collective-permute-start.15) | collective-permute-done | bytes 131104 | tf_op jit(solution)/shard_map/ppermute | solution.py:45
  75.9 0.6 collective-permute-done.16.s3
  76.5 1.6 coarse_pack.1
  78.1 13.7 %all_to_all.10.turned_ref = bf16[4,384,128]{2,1,0:T(8,128)(2,1)S(1)} all-to-all(bf16[4,384,128]{2,1,0:T(8,128)(2,1)S(1)} %get-tuple-element.34), channel_id=1, replica_groups=mesh['z'=4,'x'=4,'core'=2,'head'=4] {'z'}, dimensions={0} | all-to-all | bytes 786432 | tf_op jit(solution)/shard_map/all_to_all | solution.py:544
  92.1 3.5 %collective-permute-start.18 = (bf16[4,256,128]{2,1,0:T(8,128)(2,1)S(1)}, bf16[4,256,128]{2,1,0:T(8,128)(2,1)S(1)}, u32[]{:S(2)}, u32[]{:S(2)}) collective-permute-start(bf16[4,256,128]{2,1,0:T(8,128)(2,1)S(1)} %slice.11), channel_id=1, source_target_pairs={{0,8},{8,16},{16,24},{24,0},{1,9},{9,17},{17,25},{25,1},{2,10},{10... | collective-permute-start | bytes 786440 | tf_op jit(solution)/shard_map/ppermute | solution.py:45
  95.6 0.8 collective-permute-start.19
  96.4 2.4 %coarse_first.1 = (bf16[1024,128]{1,0:T(8,128)(2,1)S(1)}, f32[1024,128]{1,0:T(8,128)S(1)}, f32[1024,128]{1,0:T(8,128)S(1)}, f32[1024,128]{1,0:T(8,128)S(1)}) custom-call(s32[4]{0:T(128)S(1)} %fusion.5.flag_ref, bf16[4,384,128]{2,1,0:T(8,128)(2,1)S(1)} %all_to_all.10.turned_ref, bf16[4,256,128]{2,1,0:T(8,128)(2,1)S(1)} %collective-permute-done.20.far_ref), custom_call_target="tpu_custom_call" | custom-call | flops 3000000000 | bytes 6000000 | tf_op jit(solution)/shard_map/coarse_first/pallas_call | solution.py:231
  98.8 3.9 %collective-permute-done.17.refs_0_ = bf16[4,256,128]{2,1,0:T(8,128)(2,1)S(1)} collective-permute-done((bf16[4,256,128]{2,1,0:T(8,128)(2,1)S(1)}, bf16[4,256,128]{2,1,0:T(8,128)(2,1)S(1)}, u32[]{:S(2)}, u32[]{:S(2)}) %collective-permute-start.17) | collective-permute-done | bytes 262176 | tf_op jit(solution)/shard_map/ppermute | solution.py:45
  102.7 6.0 %collective-permute-done.18.refs_0_ = bf16[4,256,128]{2,1,0:T(8,128)(2,1)S(1)} collective-permute-done((bf16[4,256,128]{2,1,0:T(8,128)(2,1)S(1)}, bf16[4,256,128]{2,1,0:T(8,128)(2,1)S(1)}, u32[]{:S(2)}, u32[]{:S(2)}) %collective-permute-start.18) | collective-permute-done | bytes 262176 | tf_op jit(solution)/shard_map/ppermute | solution.py:45
  108.7 0.5 collective-permute-start.23
  109.2 3.0 %collective-permute-start.25 = (bf16[256,1024]{1,0:T(8,128)(2,1)}, bf16[256,1024]{1,0:T(8,128)(2,1)S(1)}, u32[]{:S(2)}, u32[]{:S(2)}) collective-permute-start(bf16[256,1024]{1,0:T(8,128)(2,1)} %c0.1), channel_id=1, source_target_pairs={{0,2},{1,3},{2,0},{3,1},{4,6},{5,7},{6,4},{7,5},{8,10},{9,11},{10,... | collective-permute-start | bytes 1572872 | tf_op jit(solution)/shard_map/ppermute | solution.py:45
  112.2 1.1 collective-permute-start.26
  113.4 5.5 %coarse_more.1 = (f32[1024,128]{1,0:T(8,128)S(1)}, f32[1024,128]{1,0:T(8,128)S(1)}, f32[1024,128]{1,0:T(8,128)S(1)}) custom-call(s32[4]{0:T(128)S(1)} %fusion.5.flag_ref, bf16[4,256,128]{2,1,0:T(8,128)(2,1)S(1)} %collective-permute-done.18.refs_0_, bf16[4,256,128]{2,1,0:T(8,128)(2,1)S(1)} %collective-permute-done.22.refs_1_, ...), custom_call_target="tpu_custom_call" | custom-call | flops 6000000000 | bytes 12000000 | tf_op jit(solution)/shard_map/coarse_more/pallas_call | solution.py:231
  118.9 4.1 %coarse_last.1 = bf16[16,128,128]{2,1,0:T(8,128)(2,1)} custom-call(s32[4]{0:T(128)S(1)} %fusion.5.flag_ref, bf16[4,256,128]{2,1,0:T(8,128)(2,1)S(1)} %collective-permute-done.17.refs_0_, bf16[4,256,128]{2,1,0:T(8,128)(2,1)S(1)} %collective-permute-done.21.refs_1_, bf16[1024,128]{1,0:T(8,128)(2,1)S(1)} %get-tuple-element.38.refs_4_.refs_2_, ...), custom_call_target="tpu_custom_call" | custom-call | flops 3000000000 | bytes 6000000 | tf_op jit(solution)/shard_map/coarse_last/pallas_call | solution.py:231
  123.0 4.0 %all-to-all-start.1 = ((bf16[16,128,128]{2,1,0:T(8,128)(2,1)}), bf16[16,128,128]{2,1,0:T(8,128)(2,1)S(1)}, u32[]{:S(2)}, u32[]{:S(2)}) async-start(bf16[16,128,128]{2,1,0:T(8,128)(2,1)} %coarse_last.1), calls=%async_computation.1 | async-start | bytes 1048576 | tf_op jit(solution)/shard_map/all_to_all | solution.py:569
  127.0 10.2 %collective-permute-done.24.c1 = bf16[256,1024]{1,0:T(8,128)(2,1)S(1)} collective-permute-done((bf16[256,1024]{1,0:T(8,128)(2,1)}, bf16[256,1024]{1,0:T(8,128)(2,1)S(1)}, u32[]{:S(2)}, u32[]{:S(2)}) %collective-permute-start.24) | collective-permute-done | bytes 524320 | tf_op jit(solution)/shard_map/ppermute | solution.py:45
  137.2 0.4 collective-permute-done.26.c3
  137.6 4.2 %all-to-all-done.1.heads_ref = bf16[16,128,128]{2,1,0:T(8,128)(2,1)S(1)} async-done(((bf16[16,128,128]{2,1,0:T(8,128)(2,1)}), bf16[16,128,128]{2,1,0:T(8,128)(2,1)S(1)}, u32[]{:S(2)}, u32[]{:S(2)}) %all-to-all-start.1) | async-done | bytes 524320 | tf_op jit(solution)/shard_map/all_to_all | solution.py:569
  141.8 4.6 %feed.1 = (bf16[4,64,1024]{2,1,0:T(8,128)(2,1)S(1)}, f32[64,1024]{1,0:T(8,128)S(1)}) custom-call(s32[3]{0:T(128)S(1)} %pad_add_fusion.1.where_ref, bf16[16,128,128]{2,1,0:T(8,128)(2,1)S(1)} %all-to-all-done.1.heads_ref, bf16[256,1024]{1,0:T(8,128)(2,1)S(1)} %get-tuple-element.47.short_ref, f32[1,1024]{1,0:T(1,128)S(1)} %bitcast.28, bf16[256,1024]{1,0:T(8,128)(2,1)} %c0.1, ...), custom_call_target="tpu_custom_call" | custom-call | flops 4000000000 | bytes 8000000 | tf_op jit(solution)/shard_map/feed/pallas_call | solution.py:231
  146.4 1.7 %collective-permute-start.27 = (bf16[64,1024]{1,0:T(8,128)(2,1)S(1)}, bf16[64,1024]{1,0:T(8,128)(2,1)S(1)}, u32[]{:S(2)}, u32[]{:S(2)}) collective-permute-start(bf16[64,1024]{1,0:T(8,128)(2,1)S(1)} %get-tuple-element.55), channel_id=1, source_target_pairs={{0,1},{1,2},{2,3},{3,0},{4,5},{5,6},{6,7},{7,4},{8,9},{9,10},{10,1... | collective-permute-start | bytes 393224 | tf_op jit(solution)/shard_map/ppermute | solution.py:45
  148.2 2.6 %collective-permute-start.28 = (bf16[64,1024]{1,0:T(8,128)(2,1)S(1)}, bf16[64,1024]{1,0:T(8,128)(2,1)S(1)}, u32[]{:S(2)}, u32[]{:S(2)}) collective-permute-start(bf16[64,1024]{1,0:T(8,128)(2,1)S(1)} %get-tuple-element.57), channel_id=1, source_target_pairs={{0,2},{1,3},{2,0},{3,1},{4,6},{5,7},{6,4},{7,5},{8,10},{9,11},{10,... | collective-permute-start | bytes 393224 | tf_op jit(solution)/shard_map/ppermute | solution.py:45
  150.8 0.1 collective-permute-start.29
  151.0 2.1 %collective-permute-done.27 = bf16[64,1024]{1,0:T(8,128)(2,1)S(1)} collective-permute-done((bf16[64,1024]{1,0:T(8,128)(2,1)S(1)}, bf16[64,1024]{1,0:T(8,128)(2,1)S(1)}, u32[]{:S(2)}, u32[]{:S(2)}) %collective-permute-start.27) | collective-permute-done | bytes 131104 | tf_op jit(solution)/shard_map/ppermute | solution.py:45
  153.0 3.6 %collective-permute-done.28 = bf16[64,1024]{1,0:T(8,128)(2,1)S(1)} collective-permute-done((bf16[64,1024]{1,0:T(8,128)(2,1)S(1)}, bf16[64,1024]{1,0:T(8,128)(2,1)S(1)}, u32[]{:S(2)}, u32[]{:S(2)}) %collective-permute-start.28) | collective-permute-done | bytes 131104 | tf_op jit(solution)/shard_map/ppermute | solution.py:45
  156.6 0.1 fusion.3.s0
  156.7 0.4 collective-permute-start.30
  157.2 3.2 %collective-permute-start.31 = (bf16[64,1024]{1,0:T(8,128)(2,1)S(1)}, bf16[64,1024]{1,0:T(8,128)(2,1)S(1)}, u32[]{:S(2)}, u32[]{:S(2)}) collective-permute-start(bf16[64,1024]{1,0:T(8,128)(2,1)S(1)} %fusion.3.s0), channel_id=1, source_target_pairs={{0,2},{1,3},{2,0},{3,1},{4,6},{5,7},{6,4},{7,5},{8,10},{9,11},{10,... | collective-permute-start | bytes 393224 | tf_op jit(solution)/shard_map/ppermute | solution.py:45
  160.4 0.5 copy.21
  160.9 3.2 %collective-permute-done.30.s1 = bf16[64,1024]{1,0:T(8,128)(2,1)S(1)} collective-permute-done((bf16[64,1024]{1,0:T(8,128)(2,1)S(1)}, bf16[64,1024]{1,0:T(8,128)(2,1)S(1)}, u32[]{:S(2)}, u32[]{:S(2)}) %collective-permute-start.30) | collective-permute-done | bytes 131104 | tf_op jit(solution)/shard_map/ppermute | solution.py:45
  164.1 2.0 %collective-permute-done.31.s2 = bf16[64,1024]{1,0:T(8,128)(2,1)S(1)} collective-permute-done((bf16[64,1024]{1,0:T(8,128)(2,1)S(1)}, bf16[64,1024]{1,0:T(8,128)(2,1)S(1)}, u32[]{:S(2)}, u32[]{:S(2)}) %collective-permute-start.31) | collective-permute-done | bytes 131104 | tf_op jit(solution)/shard_map/ppermute | solution.py:45
  166.2 2.7 %final.1 = bf16[1024,256]{1,0:T(8,128)(2,1)} custom-call(s32[3]{0:T(128)S(1)} %pad_add_fusion.1.where_ref, bf16[64,1024]{1,0:T(8,128)(2,1)S(1)} %fusion.3.s0, bf16[64,1024]{1,0:T(8,128)(2,1)S(1)} %collective-permute-done.30.s1, bf16[64,1024]{1,0:T(8,128)(2,1)S(1)} %collective-permute-done.31.s2, bf16[64,1024]{1,0:T(8,128)(2,1)S(1)} %collective-permute-done.32.s3, ...), custom_call_target="tpu_custom_call" | custom-call | flops 2000000000 | bytes 4000000 | tf_op jit(solution)/shard_map/final/pallas_call | solution.py:231
  (53 shorter events, 0.8 us)
Async XLA Ops:
  0.0 13.9 %collective-permute-start = (s32[1024]{0:T(1024)}, s32[1024]{0:T(1024)S(1)}, u32[]{:S(2)}, u32[]{:S(2)}) collective-permute-start(s32[1024]{0:T(1024)} %param.18), channel_id=1, source_target_pairs={{0,4},{4,8},{8,12},{12,16},{16,20},{20,24},{24,28},{28,32},{32,36}... | collective-permute-start | bytes 12296 | tf_op jit(solution)/shard_map/ppermute | solution.py:49
  2.6 45.0 %collective-permute-start.5 = (bf16[256,1024]{1,0:T(8,128)(2,1)}, bf16[256,1024]{1,0:T(8,128)(2,1)S(1)}, u32[]{:S(2)}, u32[]{:S(2)}) collective-permute-start(bf16[256,1024]{1,0:T(8,128)(2,1)} %f0.1), channel_id=1, source_target_pairs={{0,1},{1,2},{2,3},{3,0},{4,5},{5,6},{6,7},{7,4},{8,9},{9,10},{10,1... | collective-permute-start | bytes 1572872 | tf_op jit(solution)/shard_map/ppermute | solution.py:45
  4.2 43.4 %collective-permute-start.6 = (bf16[256,1024]{1,0:T(8,128)(2,1)}, bf16[256,1024]{1,0:T(8,128)(2,1)S(1)}, u32[]{:S(2)}, u32[]{:S(2)}) collective-permute-start(bf16[256,1024]{1,0:T(8,128)(2,1)} %f0.1), channel_id=1, source_target_pairs={{0,2},{1,3},{2,0},{3,1},{4,6},{5,7},{6,4},{7,5},{8,10},{9,11},{10,... | collective-permute-start | bytes 1572872 | tf_op jit(solution)/shard_map/ppermute | solution.py:45
  7.1 40.5 %collective-permute-start.7 = (bf16[256,1024]{1,0:T(8,128)(2,1)}, bf16[256,1024]{1,0:T(8,128)(2,1)S(1)}, u32[]{:S(2)}, u32[]{:S(2)}) collective-permute-start(bf16[256,1024]{1,0:T(8,128)(2,1)} %f0.1), channel_id=1, source_target_pairs={{0,3},{1,0},{2,1},{3,2},{4,7},{5,4},{6,5},{7,6},{8,11},{9,8},{10,9... | collective-permute-start | bytes 1572872 | tf_op jit(solution)/shard_map/ppermute | solution.py:45
  8.4 5.5 %collective-permute-start.1 = (s32[256]{0:T(256)S(1)}, s32[256]{0:T(256)S(1)}, u32[]{:S(2)}, u32[]{:S(2)}) collective-permute-start(s32[256]{0:T(256)S(1)} %slice.10), channel_id=1, source_target_pairs={{0,8},{4,12},{8,16},{12,20},{16,24},{20,28},{24,32},{28,36},{32,40... | collective-permute-start | bytes 3080 | tf_op jit(solution)/shard_map/ppermute | solution.py:49
  15.0 0.7 copy-start.5
  15.6 27.0 %copy-start.10 = (s32[1024]{0:T(1024)S(1)}, s32[1024]{0:T(1024)}, u32[]{:S(2)}) copy-start(s32[1024]{0:T(1024)} %param.18) | copy-start | bytes 12292
  15.6 32.0 %copy-start.1 = (bf16[256,1024]{1,0:T(8,128)(2,1)S(1)}, bf16[256,1024]{1,0:T(8,128)(2,1)}, u32[]{:S(2)}) copy-start(bf16[256,1024]{1,0:T(8,128)(2,1)} %emb_ref.1) | copy-start | bytes 1572868
  32.5 10.1 %collective-permute-start.2 = (bf16[272,256]{1,0:T(8,128)(2,1)S(1)}, bf16[272,256]{1,0:T(8,128)(2,1)S(1)}, u32[]{:S(2)}, u32[]{:S(2)}) collective-permute-start(bf16[272,256]{1,0:T(8,128)(2,1)S(1)} %get-tuple-element.30), channel_id=1, source_target_pairs={{0,1},{1,2},{2,3},{3,0},{4,5},{5,6},{6,7},{7,4},{8,9},{9,10},{10,1... | collective-permute-start | bytes 417800 | tf_op jit(solution)/shard_map/ppermute | solution.py:45
  33.2 9.6 %collective-permute-start.3 = (bf16[272,256]{1,0:T(8,128)(2,1)S(1)}, bf16[272,256]{1,0:T(8,128)(2,1)S(1)}, u32[]{:S(2)}, u32[]{:S(2)}) collective-permute-start(bf16[272,256]{1,0:T(8,128)(2,1)S(1)} %get-tuple-element.31), channel_id=1, source_target_pairs={{0,2},{1,3},{2,0},{3,1},{4,6},{5,7},{6,4},{7,5},{8,10},{9,11},{10,... | collective-permute-start | bytes 417800 | tf_op jit(solution)/shard_map/ppermute | solution.py:45
  42.6 5.1 %collective-permute-start.4 = (bf16[272,256]{1,0:T(8,128)(2,1)S(1)}, bf16[272,256]{1,0:T(8,128)(2,1)S(1)}, u32[]{:S(2)}, u32[]{:S(2)}) collective-permute-start(bf16[272,256]{1,0:T(8,128)(2,1)S(1)} %get-tuple-element.32), channel_id=1, source_target_pairs={{0,3},{1,0},{2,1},{3,2},{4,7},{5,4},{6,5},{7,6},{8,11},{9,8},{10,9... | collective-permute-start | bytes 417800 | tf_op jit(solution)/shard_map/ppermute | solution.py:45
  47.6 10.1 %copy-start = (bf16[4,256,1024]{2,1,0:T(8,128)(2,1)S(1)}, bf16[4,256,1024]{2,1,0:T(8,128)(2,1)}, u32[]{:S(2)}) copy-start(bf16[4,256,1024]{2,1,0:T(8,128)(2,1)} %w_ref.7) | copy-start | bytes 6291460
  50.7 7.0 %collective-permute-start.10 = (bf16[272,256]{1,0:T(8,128)(2,1)S(1)}, bf16[272,256]{1,0:T(8,128)(2,1)S(1)}, u32[]{:S(2)}, u32[]{:S(2)}) collective-permute-start(bf16[272,256]{1,0:T(8,128)(2,1)S(1)} %get-tuple-element.53), channel_id=1, source_target_pairs={{0,2},{1,3},{2,0},{3,1},{4,6},{5,7},{6,4},{7,5},{8,10},{9,11},{10,... | collective-permute-start | bytes 417800 | tf_op jit(solution)/shard_map/ppermute | solution.py:45
  50.8 8.6 %collective-permute-start.12 = (bf16[272,256]{1,0:T(8,128)(2,1)S(1)}, bf16[272,256]{1,0:T(8,128)(2,1)S(1)}, u32[]{:S(2)}, u32[]{:S(2)}) collective-permute-start(bf16[272,256]{1,0:T(8,128)(2,1)S(1)} %get-tuple-element.52), channel_id=1, source_target_pairs={{0,3},{1,0},{2,1},{3,2},{4,7},{5,4},{6,5},{7,6},{8,11},{9,8},{10,9... | collective-permute-start | bytes 417800 | tf_op jit(solution)/shard_map/ppermute | solution.py:45
  53.0 8.7 %collective-permute-start.8 = (bf16[272,256]{1,0:T(8,128)(2,1)S(1)}, bf16[272,256]{1,0:T(8,128)(2,1)S(1)}, u32[]{:S(2)}, u32[]{:S(2)}) collective-permute-start(bf16[272,256]{1,0:T(8,128)(2,1)S(1)} %get-tuple-element.54), channel_id=1, source_target_pairs={{0,1},{1,2},{2,3},{3,0},{4,5},{5,6},{6,7},{7,4},{8,9},{9,10},{10,1... | collective-permute-start | bytes 417800 | tf_op jit(solution)/shard_map/ppermute | solution.py:45
  58.2 7.4 %collective-permute-start.11 = (bf16[64,1024]{1,0:T(8,128)(2,1)S(1)}, bf16[64,1024]{1,0:T(8,128)(2,1)S(1)}, u32[]{:S(2)}, u32[]{:S(2)}) collective-permute-start(bf16[64,1024]{1,0:T(8,128)(2,1)S(1)} %short_part.6), channel_id=1, source_target_pairs={{0,2},{1,3},{2,0},{3,1},{4,6},{5,7},{6,4},{7,5},{8,10},{9,11},{10,... | collective-permute-start | bytes 393224 | tf_op jit(solution)/shard_map/ppermute | solution.py:45
  59.9 7.0 %collective-permute-start.13 = (bf16[64,1024]{1,0:T(8,128)(2,1)S(1)}, bf16[64,1024]{1,0:T(8,128)(2,1)S(1)}, u32[]{:S(2)}, u32[]{:S(2)}) collective-permute-start(bf16[64,1024]{1,0:T(8,128)(2,1)S(1)} %short_part.7), channel_id=1, source_target_pairs={{0,1},{1,2},{2,3},{3,0},{4,5},{5,6},{6,7},{7,4},{8,9},{9,10},{10,1... | collective-permute-start | bytes 393224 | tf_op jit(solution)/shard_map/ppermute | solution.py:45
  62.2 5.0 %collective-permute-start.9 = (bf16[64,1024]{1,0:T(8,128)(2,1)S(1)}, bf16[64,1024]{1,0:T(8,128)(2,1)S(1)}, u32[]{:S(2)}, u32[]{:S(2)}) collective-permute-start(bf16[64,1024]{1,0:T(8,128)(2,1)S(1)} %short_part.5), channel_id=1, source_target_pairs={{0,3},{1,0},{2,1},{3,2},{4,7},{5,4},{6,5},{7,6},{8,11},{9,8},{10,9... | collective-permute-start | bytes 393224 | tf_op jit(solution)/shard_map/ppermute | solution.py:45
  63.7 12.8 %copy-start.2 = (bf16[1024,256]{1,0:T(8,128)(2,1)S(1)}, bf16[1024,256]{1,0:T(8,128)(2,1)}, u32[]{:S(2)}) copy-start(bf16[1024,256]{1,0:T(8,128)(2,1)} %wq_ref.1) | copy-start | bytes 1572868
  63.7 12.8 %copy-start.3 = (bf16[1024,256]{1,0:T(8,128)(2,1)S(1)}, bf16[1024,256]{1,0:T(8,128)(2,1)}, u32[]{:S(2)}) copy-start(bf16[1024,256]{1,0:T(8,128)(2,1)} %wk_ref.1) | copy-start | bytes 1572868
  63.7 12.8 %copy-start.4 = (bf16[1024,256]{1,0:T(8,128)(2,1)S(1)}, bf16[1024,256]{1,0:T(8,128)(2,1)}, u32[]{:S(2)}) copy-start(bf16[1024,256]{1,0:T(8,128)(2,1)} %wv_ref.1) | copy-start | bytes 1572868
  63.7 12.8 %copy-start.6 = (f32[1024]{0:T(1024)S(1)}, f32[1024]{0:T(1024)}, u32[]{:S(2)}) copy-start(f32[1024]{0:T(1024)} %param.26) | copy-start | bytes 12292
  63.7 12.8 %copy-start.8 = (f32[576,128]{1,0:T(8,128)S(1)}, f32[576,128]{1,0:T(8,128)}, u32[]{:S(2)}) copy-start(f32[576,128]{1,0:T(8,128)} %constant.88.clone.turn_hbm.turn_ref) | copy-start | bytes 884740
  67.3 6.8 %collective-permute-start.14 = (bf16[64,1024]{1,0:T(8,128)(2,1)S(1)}, bf16[64,1024]{1,0:T(8,128)(2,1)S(1)}, u32[]{:S(2)}, u32[]{:S(2)}) collective-permute-start(bf16[64,1024]{1,0:T(8,128)(2,1)S(1)} %add_convert_fusion.s0), channel_id=1, source_target_pairs={{0,1},{1,2},{2,3},{3,0},{4,5},{5,6},{6,7},{7,4},{8,9},{9,10},{10,1... | collective-permute-start | bytes 393224 | tf_op jit(solution)/shard_map/ppermute | solution.py:45
  68.0 7.8 %collective-permute-start.15 = (bf16[64,1024]{1,0:T(8,128)(2,1)S(1)}, bf16[64,1024]{1,0:T(8,128)(2,1)S(1)}, u32[]{:S(2)}, u32[]{:S(2)}) collective-permute-start(bf16[64,1024]{1,0:T(8,128)(2,1)S(1)} %add_convert_fusion.s0), channel_id=1, source_target_pairs={{0,2},{1,3},{2,0},{3,1},{4,6},{5,7},{6,4},{7,5},{8,10},{9,11},{10,... | collective-permute-start | bytes 393224 | tf_op jit(solution)/shard_map/ppermute | solution.py:45
  71.5 5.0 %collective-permute-start.16 = (bf16[64,1024]{1,0:T(8,128)(2,1)S(1)}, bf16[64,1024]{1,0:T(8,128)(2,1)S(1)}, u32[]{:S(2)}, u32[]{:S(2)}) collective-permute-start(bf16[64,1024]{1,0:T(8,128)(2,1)S(1)} %add_convert_fusion.s0), channel_id=1, source_target_pairs={{0,3},{1,0},{2,1},{3,2},{4,7},{5,4},{6,5},{7,6},{8,11},{9,8},{10,9... | collective-permute-start | bytes 393224 | tf_op jit(solution)/shard_map/ppermute | solution.py:45
  91.8 4.5 %collective-permute-start.20 = (bf16[4,256,128]{2,1,0:T(8,128)(2,1)S(1)}, bf16[4,256,128]{2,1,0:T(8,128)(2,1)S(1)}, u32[]{:S(2)}, u32[]{:S(2)}) collective-permute-start(bf16[4,256,128]{2,1,0:T(8,128)(2,1)S(1)} %slice.11), channel_id=1, source_target_pairs={{0,4},{4,0},{1,5},{5,1},{2,6},{6,2},{3,7},{7,3},{8,12},{12,8},{9,1... | collective-permute-start | bytes 786440 | tf_op jit(solution)/shard_map/ppermute | solution.py:45
  92.0 10.7 %collective-permute-start.17 = (bf16[4,256,128]{2,1,0:T(8,128)(2,1)S(1)}, bf16[4,256,128]{2,1,0:T(8,128)(2,1)S(1)}, u32[]{:S(2)}, u32[]{:S(2)}) collective-permute-start(bf16[4,256,128]{2,1,0:T(8,128)(2,1)S(1)} %slice.11), channel_id=1, source_target_pairs={{0,16},{8,24},{16,0},{24,8},{1,17},{9,25},{17,1},{25,9},{2,18},{10... | collective-permute-start | bytes 786440 | tf_op jit(solution)/shard_map/ppermute | solution.py:45
  92.1 16.6 %collective-permute-start.18 = (bf16[4,256,128]{2,1,0:T(8,128)(2,1)S(1)}, bf16[4,256,128]{2,1,0:T(8,128)(2,1)S(1)}, u32[]{:S(2)}, u32[]{:S(2)}) collective-permute-start(bf16[4,256,128]{2,1,0:T(8,128)(2,1)S(1)} %slice.11), channel_id=1, source_target_pairs={{0,8},{8,16},{16,24},{24,0},{1,9},{9,17},{17,25},{25,1},{2,10},{10... | collective-permute-start | bytes 786440 | tf_op jit(solution)/shard_map/ppermute | solution.py:45
  95.6 13.1 %collective-permute-start.19 = (bf16[4,256,128]{2,1,0:T(8,128)(2,1)S(1)}, bf16[4,256,128]{2,1,0:T(8,128)(2,1)S(1)}, u32[]{:S(2)}, u32[]{:S(2)}) collective-permute-start(bf16[4,256,128]{2,1,0:T(8,128)(2,1)S(1)} %slice.11), channel_id=1, source_target_pairs={{0,24},{8,0},{16,8},{24,16},{1,25},{9,1},{17,9},{25,17},{2,26},{10... | collective-permute-start | bytes 786440 | tf_op jit(solution)/shard_map/ppermute | solution.py:45
  108.7 4.7 %collective-permute-start.22 = (bf16[4,256,128]{2,1,0:T(8,128)(2,1)S(1)}, bf16[4,256,128]{2,1,0:T(8,128)(2,1)S(1)}, u32[]{:S(2)}, u32[]{:S(2)}) collective-permute-start(bf16[4,256,128]{2,1,0:T(8,128)(2,1)S(1)} %collective-permute-done.18.refs_0_), channel_id=1, source_target_pairs={{0,4},{4,0},{1,5},{5,1},{2,6},{6,2},{3,7},{7,3},{8,12},{12,8},{9,1... | collective-permute-start | bytes 786440 | tf_op jit(solution)/shard_map/ppermute | solution.py:45
  108.7 4.7 %collective-permute-start.23 = (bf16[4,256,128]{2,1,0:T(8,128)(2,1)S(1)}, bf16[4,256,128]{2,1,0:T(8,128)(2,1)S(1)}, u32[]{:S(2)}, u32[]{:S(2)}) collective-permute-start(bf16[4,256,128]{2,1,0:T(8,128)(2,1)S(1)} %collective-permute-done.19.refs_2_), channel_id=1, source_target_pairs={{0,4},{4,0},{1,5},{5,1},{2,6},{6,2},{3,7},{7,3},{8,12},{12,8},{9,1... | collective-permute-start | bytes 786440 | tf_op jit(solution)/shard_map/ppermute | solution.py:45
  109.2 27.9 %collective-permute-start.24 = (bf16[256,1024]{1,0:T(8,128)(2,1)}, bf16[256,1024]{1,0:T(8,128)(2,1)S(1)}, u32[]{:S(2)}, u32[]{:S(2)}) collective-permute-start(bf16[256,1024]{1,0:T(8,128)(2,1)} %c0.1), channel_id=1, source_target_pairs={{0,1},{1,2},{2,3},{3,0},{4,5},{5,6},{6,7},{7,4},{8,9},{9,10},{10,1... | collective-permute-start | bytes 1572872 | tf_op jit(solution)/shard_map/ppermute | solution.py:45
  109.2 27.9 %collective-permute-start.25 = (bf16[256,1024]{1,0:T(8,128)(2,1)}, bf16[256,1024]{1,0:T(8,128)(2,1)S(1)}, u32[]{:S(2)}, u32[]{:S(2)}) collective-permute-start(bf16[256,1024]{1,0:T(8,128)(2,1)} %c0.1), channel_id=1, source_target_pairs={{0,2},{1,3},{2,0},{3,1},{4,6},{5,7},{6,4},{7,5},{8,10},{9,11},{10,... | collective-permute-start | bytes 1572872 | tf_op jit(solution)/shard_map/ppermute | solution.py:45
  112.2 25.4 %collective-permute-start.26 = (bf16[256,1024]{1,0:T(8,128)(2,1)}, bf16[256,1024]{1,0:T(8,128)(2,1)S(1)}, u32[]{:S(2)}, u32[]{:S(2)}) collective-permute-start(bf16[256,1024]{1,0:T(8,128)(2,1)} %c0.1), channel_id=1, source_target_pairs={{0,3},{1,0},{2,1},{3,2},{4,7},{5,4},{6,5},{7,6},{8,11},{9,8},{10,9... | collective-permute-start | bytes 1572872 | tf_op jit(solution)/shard_map/ppermute | solution.py:45
  113.4 5.5 %collective-permute-start.21 = (bf16[4,256,128]{2,1,0:T(8,128)(2,1)S(1)}, bf16[4,256,128]{2,1,0:T(8,128)(2,1)S(1)}, u32[]{:S(2)}, u32[]{:S(2)}) collective-permute-start(bf16[4,256,128]{2,1,0:T(8,128)(2,1)S(1)} %collective-permute-done.17.refs_0_), channel_id=1, source_target_pairs={{0,4},{4,0},{1,5},{5,1},{2,6},{6,2},{3,7},{7,3},{8,12},{12,8},{9,1... | collective-permute-start | bytes 786440 | tf_op jit(solution)/shard_map/ppermute | solution.py:45
  118.9 22.9 %copy-start.7 = (f32[1024]{0:T(1024)S(1)}, f32[1024]{0:T(1024)}, u32[]{:S(2)}) copy-start(f32[1024]{0:T(1024)} %param.31) | copy-start | bytes 12292
  123.0 18.8 %all-to-all-start.1 = ((bf16[16,128,128]{2,1,0:T(8,128)(2,1)}), bf16[16,128,128]{2,1,0:T(8,128)(2,1)S(1)}, u32[]{:S(2)}, u32[]{:S(2)}) async-start(bf16[16,128,128]{2,1,0:T(8,128)(2,1)} %coarse_last.1), calls=%async_computation.1 | async-start | bytes 1048576 | tf_op jit(solution)/shard_map/all_to_all | solution.py:569
  141.8 18.7 %copy-start.9 = (bf16[1024,4,256]{2,1,0:T(4,128)(2,1)S(1)}, bf16[1024,4,256]{2,1,0:T(4,128)(2,1)}, u32[]{:S(2)}) copy-start(bf16[1024,4,256]{2,1,0:T(4,128)(2,1)} %param.34) | copy-start | bytes 6291460
  146.4 6.6 %collective-permute-start.27 = (bf16[64,1024]{1,0:T(8,128)(2,1)S(1)}, bf16[64,1024]{1,0:T(8,128)(2,1)S(1)}, u32[]{:S(2)}, u32[]{:S(2)}) collective-permute-start(bf16[64,1024]{1,0:T(8,128)(2,1)S(1)} %get-tuple-element.55), channel_id=1, source_target_pairs={{0,1},{1,2},{2,3},{3,0},{4,5},{5,6},{6,7},{7,4},{8,9},{9,10},{10,1... | collective-permute-start | bytes 393224 | tf_op jit(solution)/shard_map/ppermute | solution.py:45
  148.2 8.4 %collective-permute-start.28 = (bf16[64,1024]{1,0:T(8,128)(2,1)S(1)}, bf16[64,1024]{1,0:T(8,128)(2,1)S(1)}, u32[]{:S(2)}, u32[]{:S(2)}) collective-permute-start(bf16[64,1024]{1,0:T(8,128)(2,1)S(1)} %get-tuple-element.57), channel_id=1, source_target_pairs={{0,2},{1,3},{2,0},{3,1},{4,6},{5,7},{6,4},{7,5},{8,10},{9,11},{10,... | collective-permute-start | bytes 393224 | tf_op jit(solution)/shard_map/ppermute | solution.py:45
  150.8 5.8 %collective-permute-start.29 = (bf16[64,1024]{1,0:T(8,128)(2,1)S(1)}, bf16[64,1024]{1,0:T(8,128)(2,1)S(1)}, u32[]{:S(2)}, u32[]{:S(2)}) collective-permute-start(bf16[64,1024]{1,0:T(8,128)(2,1)S(1)} %get-tuple-element.56), channel_id=1, source_target_pairs={{0,3},{1,0},{2,1},{3,2},{4,7},{5,4},{6,5},{7,6},{8,11},{9,8},{10,9... | collective-permute-start | bytes 393224 | tf_op jit(solution)/shard_map/ppermute | solution.py:45
  156.7 7.4 %collective-permute-start.30 = (bf16[64,1024]{1,0:T(8,128)(2,1)S(1)}, bf16[64,1024]{1,0:T(8,128)(2,1)S(1)}, u32[]{:S(2)}, u32[]{:S(2)}) collective-permute-start(bf16[64,1024]{1,0:T(8,128)(2,1)S(1)} %fusion.3.s0), channel_id=1, source_target_pairs={{0,1},{1,2},{2,3},{3,0},{4,5},{5,6},{6,7},{7,4},{8,9},{9,10},{10,1... | collective-permute-start | bytes 393224 | tf_op jit(solution)/shard_map/ppermute | solution.py:45
  157.2 8.9 %collective-permute-start.31 = (bf16[64,1024]{1,0:T(8,128)(2,1)S(1)}, bf16[64,1024]{1,0:T(8,128)(2,1)S(1)}, u32[]{:S(2)}, u32[]{:S(2)}) collective-permute-start(bf16[64,1024]{1,0:T(8,128)(2,1)S(1)} %fusion.3.s0), channel_id=1, source_target_pairs={{0,2},{1,3},{2,0},{3,1},{4,6},{5,7},{6,4},{7,5},{8,10},{9,11},{10,... | collective-permute-start | bytes 393224 | tf_op jit(solution)/shard_map/ppermute | solution.py:45
  160.4 5.8 %collective-permute-start.32 = (bf16[64,1024]{1,0:T(8,128)(2,1)S(1)}, bf16[64,1024]{1,0:T(8,128)(2,1)S(1)}, u32[]{:S(2)}, u32[]{:S(2)}) collective-permute-start(bf16[64,1024]{1,0:T(8,128)(2,1)S(1)} %fusion.3.s0), channel_id=1, source_target_pairs={{0,3},{1,0},{2,1},{3,2},{4,7},{5,4},{6,5},{7,6},{8,11},{9,8},{10,9... | collective-permute-start | bytes 393224 | tf_op jit(solution)/shard_map/ppermute | solution.py:45

commit v4 on v3

--- a/solution.py
+++ b/solution.py
@@ -105,9 +105,29 @@
     return (plain * cosine + other * sine).astype(bf16)
 
 
+def fine_tables_kernel(gain_hbm, emb_hbm, wq_hbm, wk_hbm, wv_hbm, tab_hbm, tab_ref, gain_ref, emb_ref, w_ref, sems):
+    pairs = [(emb_hbm, emb_ref), (gain_hbm, gain_ref)]
+    for n, w in enumerate((wq_hbm, wk_hbm, wv_hbm)):
+        for part in range(2):
+            rows = pl.ds(part * 512, 512)
+            pairs.append((w.at[rows], w_ref.at[n, rows]))
+    copies = begin_copies(pairs, sems)
+    finish_copies(copies[:2])
+    fine_in = norm_rows(emb_ref[...].astype(f32), gain_ref[...])
+    finish_copies(copies[2:])
+    tq = dot(fine_in, w_ref[0]) * q_scale
+    tk = dot(fine_in, w_ref[1])
+    for n, table in enumerate((tq, partner(tq), tk, partner(tk))):
+        high, low = halves(table)
+        tab_ref[2 * n] = high
+        tab_ref[2 * n + 1] = low
+    tab_ref[8] = dot(fine_in, w_ref[2]).astype(bf16)
+    finish_copies(begin_copies([(tab_ref.at[n], tab_hbm.at[n]) for n in range(9)], sems))
+
+
 def fine_kernel(
-    where_ref, ids_ref, gain_ref, turn_hbm, emb_hbm, wq_hbm, wk_hbm, wv_hbm,
-    o0, o1, o2, o3, tab_ref, q_ref, k_ref, v_ref, turn_ref, emb_ref, w_ref, sems,
+    where_ref, before_ref, prior_ref, own_ref, tab_hbm, turn_hbm,
+    o0, o1, o2, o3, q_ref, k_ref, v_ref, tab_ref, turn_ref, sems,
 ):
     step = pl.program_id(0)
     head = where_ref[1]
@@ -118,37 +138,30 @@
 
     @pl.when(step == 0)
     def _():
-        pairs = [(emb_hbm, emb_ref), (turn_hbm, turn_ref)]
-        for n, w in enumerate((wq_hbm, wk_hbm, wv_hbm)):
-            for part in range(2):
-                rows = pl.ds(part * 512, 512)
-                pairs.append((w.at[rows], w_ref.at[n, rows]))
-        copies = begin_copies(pairs, sems)
-        finish_copies(copies[:1])
-        fine_in = norm_rows(emb_ref[...].astype(f32), gain_ref[...])
-        finish_copies(copies[1:])
-        tq = dot(fine_in, w_ref[0]) * q_scale
-        tk = dot(fine_in, w_ref[1])
-        for n, table in enumerate((tq, partner(tq), tk, partner(tk))):
-            high, low = halves(table)
-            tab_ref[2 * n] = high
-            tab_ref[2 * n + 1] = low
-        tab_ref[8] = dot(fine_in, w_ref[2]).astype(bf16)
-
-        def build(block, with_q):
+        def build(block, ids, with_q):
             begin = pl.multiple_of(block * BLOCK, BLOCK)
-            hot = pick(ids_ref[pl.ds(begin, BLOCK), :])
+            hot = pick(ids)
             cosine, sine = turn_tables(turn_ref, block)
             k_ref[pl.ds(begin, BLOCK), :] = turned_rows(hot, tab_ref, 4, cosine, sine)
             v_ref[pl.ds(begin, BLOCK), :] = dot(hot, tab_ref[8]).astype(bf16)
             if with_q:
                 at = pl.multiple_of(begin - (PAST - BLOCK), BLOCK)
                 q_ref[pl.ds(at, BLOCK), :] = turned_rows(hot, tab_ref, 0, cosine, sine)
-            return 0
-
-        early = PAST // BLOCK - 1
-        lax.fori_loop(0, early, lambda block, _: build(block, False), 0)
-        lax.fori_loop(early, KEYS // BLOCK, lambda block, _: build(block, True), 0)
+
+        def build_from(ref, first, with_q):
+            def body(n, _):
+                ids = ref[pl.ds(pl.multiple_of(n * BLOCK, BLOCK), BLOCK), :]
+                build(first + n, ids, with_q)
+                return 0
+
+            return body
+
+        pairs = [(tab_hbm.at[n], tab_ref.at[n]) for n in range(9)] + [(turn_hbm, turn_ref)]
+        finish_copies(begin_copies(pairs, sems))
+        build(0, before_ref[...], False)
+        lax.fori_loop(0, 3, build_from(prior_ref, 1, False), 0)
+        build(4, prior_ref[3 * BLOCK :, :], True)
+        lax.fori_loop(0, 4, build_from(own_ref, 5, True), 0)
         halo_q = q_ref[BLOCK - HALO : BLOCK, :]
         stacked = jnp.concatenate(
             [jnp.where(head_lane == h, halo_q, jnp.zeros_like(halo_q)) for h in range(4)], axis=0
@@ -225,7 +238,7 @@
     return pl.BlockSpec(memory_space=pltpu.SMEM)
 
 
-def call(kernel, name, shapes, scalars, arrays, scratch=(), grid=None, limit=16, us=2, hbm=(), free=()):
+def call(kernel, name, shapes, scalars, arrays, scratch=(), grid=None, limit=16, us=2, hbm=(), out_hbm=False):
     one = not isinstance(shapes, (list, tuple))
     extra = {} if grid is None else {"grid": grid}
     return pl.pallas_call(
@@ -233,9 +246,10 @@
         out_shape=shapes,
         in_specs=[smem()] * len(scalars)
         + [vmem()] * len(arrays)
-        + [pl.BlockSpec(memory_space=pltpu.HBM)] * len(hbm)
-        + [pl.BlockSpec(memory_space=pl.ANY)] * len(free),
-        out_specs=vmem() if one else [vmem()] * len(shapes),
+        + [pl.BlockSpec(memory_space=pltpu.HBM)] * len(hbm),
+        out_specs=(pl.BlockSpec(memory_space=pltpu.HBM) if out_hbm else vmem())
+        if one
+        else [vmem()] * len(shapes),
         scratch_shapes=list(scratch),
         compiler_params=pltpu.CompilerParams(vmem_limit_bytes=limit << 20),
         cost_estimate=pl.CostEstimate(
@@ -243,7 +257,7 @@
         ),
         name=name,
         **extra,
-    )(*scalars, *arrays, *(pltpu.with_memory_space_constraint(a, pltpu.HBM) for a in hbm), *free)
+    )(*scalars, *arrays, *(pltpu.with_memory_space_constraint(a, pltpu.HBM) for a in hbm))
 
 
 def begin_copies(pairs, sems):
@@ -259,18 +273,20 @@
 
 
 def fine_rows_kernel(
-    where_ref, ids_ref, emb_ref, g0, g1, g2, g3, f0, f1, f2, f3, out_ref, w_ref, sems
+    where_ref, ids_ref, emb_ref, g0, g1, g2, g3, w_hbm, out_ref, w_ref, got_ref, sems
 ):
     place, head = where_ref[0], where_ref[1]
     pairs = []
-    for s, f in enumerate((f0, f1, f2, f3)):
-        for part in range(2):
-            at = pl.ds(part * 128, 128)
-            pairs.append((f.at[at], w_ref.at[pl.ds(s * 256 + part * 128, 128)]))
+    for part in range(8):
+        at = pl.ds(part * 128, 128)
+        pairs.append((w_hbm.at[at], w_ref.at[at]))
     copies = begin_copies(pairs, sems)
+    for s, got in enumerate((g0, g1, g2, g3)):
+        begin = pl.multiple_of(lax.rem(head - s + 4, 4) * SHARE, SHARE)
+        got_ref[:, pl.ds(begin, SHARE)] = got[...]
     merged = dot(pick(ids_ref[...]), emb_ref[...])
     finish_copies(copies)
-    merged += dot(jnp.concatenate([g0[...], g1[...], g2[...], g3[...]], axis=1), w_ref[...])
+    merged += dot(got_ref[...], w_ref[...])
     rows = 256 + HALO
     token = (
         place * ROWS + head * 256 - HALO + lax.broadcasted_iota(jnp.int32, (rows, D), 0)
@@ -414,17 +430,12 @@
 
 
 def feed_kernel(
-    where_ref, heads_ref, short_ref, gain_ref, c0, up_hbm, down_hbm, c1, c2, c3,
+    where_ref, heads_ref, short_ref, gain_ref, up_hbm, down_hbm, co_hbm,
     part_ref, first_ref, mixed_ref, all_ref, co_ref, up_ref, down_ref, sems,
 ):
     head = where_ref[1]
     pairs = []
-    for s, c in enumerate((c0, c1, c2, c3)):
-        source = lax.rem(head - s + 4, 4) * 256
-        for part in range(2):
-            at = pl.ds(part * 128, 128)
-            pairs.append((c.at[at], co_ref.at[pl.ds(source + part * 128, 128)]))
-    for w, w_ref in ((up_hbm, up_ref), (down_hbm, down_ref)):
+    for w, w_ref in ((co_hbm, co_ref), (up_hbm, up_ref), (down_hbm, down_ref)):
         for part in range(4):
             at = pl.ds(part * 256, 256)
             pairs.append((w.at[at], w_ref.at[at]))
@@ -437,12 +448,12 @@
             at = slice(y * 256 + pair * 128, y * 256 + (pair + 1) * 128)
             mixed_ref[0:128, at] = jnp.where(low_lanes, even, pltpu.roll(odd, 64, 1)).astype(bf16)
             mixed_ref[128:256, at] = jnp.where(low_lanes, pltpu.roll(even, 64, 1), odd).astype(bf16)
-    finish_copies(copies[:8])
+    finish_copies(copies[:4])
     first = short_ref[...].astype(f32) + dot(mixed_ref[...], co_ref[...])
     all_ref[...] = first
     first_ref[...] = all_ref[pl.ds(pl.multiple_of(head * 64, 64), 64), :]
     feed = norm_rows(first, gain_ref[...])
-    finish_copies(copies[8:])
+    finish_copies(copies[4:])
     inner = jax.nn.gelu(dot(feed, up_ref[...])).astype(bf16)
     part_ref[...] = dot(inner, down_ref[...]).astype(bf16).reshape(4, 64, D)
 
@@ -468,8 +479,9 @@
         out_ref[pl.ds(begin, 256), :] = dot(weave, value).astype(bf16)
 
 
-def fetch_rest(weight):
-    return [shift(weight, "head", s, 4) for s in range(1, 4)]
+def fetch_all(weight, core):
+    half = lax.dynamic_slice_in_dim(weight, core * 128, 128, 0)
+    return lax.all_gather(half, ("head", "core"), axis=0, tiled=True)
 
 
 def after(value, gate):
@@ -489,36 +501,44 @@
     where = jnp.stack([place, head, core])
 
     prior = later(token_ids, SEQ, 1, 32)
-    fine_output_held, last_ids = after(fine_output, token_ids[ROWS - BLOCK :])
+    last_ids = token_ids[ROWS - BLOCK :]
     before = later(last_ids, SEQ, 2, 32)
-    past_ids = jnp.concatenate([before, prior])
-    out_rest = fetch_rest(fine_output_held)
-
+    tab = call(
+        fine_tables_kernel, "fine_tables", pltpu.HBM((9, 256, SHARE), bf16), [], [],
+        [
+            pltpu.VMEM((9, 256, SHARE), bf16),
+            pltpu.VMEM((1, D), f32), pltpu.VMEM((256, D), bf16),
+            pltpu.VMEM((3, D, SHARE), bf16), pltpu.SemaphoreType.DMA((9,)),
+        ],
+        us=3, out_hbm=True, hbm=[fine_norm[None], embedding, fine_query, fine_key, fine_value],
+    )
+    fine_output_held, _ = after(fine_output, last_ids)
+    fine_output_all = fetch_all(fine_output_held, core)
     rows = 256 + HALO
-    all_ids = jnp.concatenate([past_ids, token_ids])
     mixed = call(
         fine_kernel, "fine_attention", [jax.ShapeDtypeStruct((rows, SHARE), bf16)] * 4,
-        [where],
-        [all_ids[:, None], fine_norm[None]],
+        [where], [before[:, None], prior[:, None], token_ids[:, None]],
         [
-            pltpu.VMEM((9, 256, SHARE), bf16), pltpu.VMEM((BLOCK + ROWS, SHARE), bf16),
+            pltpu.VMEM((BLOCK + ROWS, SHARE), bf16),
             pltpu.VMEM((KEYS, SHARE), bf16), pltpu.VMEM((KEYS, SHARE), bf16),
-            pltpu.VMEM((576, 128), f32), pltpu.VMEM((256, D), bf16),
-            pltpu.VMEM((3, D, SHARE), bf16), pltpu.SemaphoreType.DMA((8,)),
+            pltpu.VMEM((9, 256, SHARE), bf16), pltpu.VMEM((576, 128), f32),
+            pltpu.SemaphoreType.DMA((10,)),
         ],
-        grid=(4,), us=15, limit=24,
-        hbm=[tables, embedding, fine_query, fine_key, fine_value],
+        grid=(4,), us=12, limit=24, hbm=[tab, tables],
     )
 
     got = [mixed[0]] + [shift(mixed[s], "head", s, 4) for s in range(1, 4)]
     own_ids = lax.dynamic_slice_in_dim(
-        jnp.concatenate([past_ids[PAST - HALO :], token_ids]), head * 256, rows, 0
+        jnp.concatenate([prior[ROWS - HALO :], token_ids]), head * 256, rows, 0
     )
     sends = call(
         fine_rows_kernel, "fine_rows", jax.ShapeDtypeStruct((4, rows, SHARE), bf16),
         [where], [own_ids[:, None], embedding, *got],
-        [pltpu.VMEM((D, D), bf16), pltpu.SemaphoreType.DMA((8,))],
-        hbm=[fine_output], free=out_rest,
+        [
+            pltpu.VMEM((D, D), bf16), pltpu.VMEM((rows, D), bf16),
+            pltpu.SemaphoreType.DMA((8,)),
+        ],
+        hbm=[fine_output_all],
     )
     blocks = exchange(lambda d: lax.dynamic_index_in_dim(sends, d, 0, keepdims=False), "head", 4)
 
@@ -541,8 +561,9 @@
         [*shorts, coarse_norm[None], coarse_query, coarse_key, coarse_value, tables],
     )
 
+    coarse_output_held, packed = after(coarse_output, packed)
+    coarse_output_all = fetch_all(coarse_output_held, core)
     turned = lax.all_to_all(packed, "z", 0, 0)
-    coarse_output_held, turned = after(coarse_output, turned)
     kv = turned[:, :COARSE_ROWS]
     far = [shift(kv, "core", 1, 2)]
     near = [shift(kv, "x", s, 4) for s in range(1, 4)]
@@ -554,7 +575,6 @@
         [jax.ShapeDtypeStruct((1024, 128), bf16), wide, wide, wide], [flags], [turned, far[0]],
         us=3, limit=24,
     )
-    co_rest = fetch_rest(coarse_output_held)
     near_held, q_all = after(near, q_all)
     far += [shift(part, "core", 1, 2) for part in near_held]
     sums = call(
@@ -575,9 +595,9 @@
         [heads_in, short, ffn_norm[None]],
         [
             pltpu.VMEM((COARSE_ROWS, D), bf16), pltpu.VMEM((COARSE_ROWS, D), f32),
-            square, square, square, pltpu.SemaphoreType.DMA((16,)),
+            square, square, square, pltpu.SemaphoreType.DMA((12,)),
         ],
-        hbm=[coarse_output, ffn_up, ffn_down], free=co_rest, us=4, limit=24,
+        hbm=[ffn_up, ffn_down, coarse_output_all], us=4, limit=24,
     )
     sums = exchange(lambda d: lax.dynamic_index_in_dim(parts, d, 0, keepdims=False), "head", 4)
     second_own = (first_own + sum(t.astype(f32) for t in sums)).astype(bf16)

time: 171 us -> 170 us (level)
  waiting for transfers between devices: 63.2 us -> 43.5 us
  blocking collectives: 13.7 us -> 28.4 us
  between operations: 0.32 us -> 13.7 us
  starting transfers between devices: 45.5 us -> 34.8 us
  Pallas kernels: 42.5 us -> 44.8 us
    all_to_all x0 -> x1, blocking collectives: none -> 16.3 us  [local(): heads_in = lax.all_to_all(wide_sends, ('z', 'head'), 0, 0)]
    ppermute x31 -> x25, waiting for transfers between devices: 57.4 us -> 43.5 us  [shift(): lax.ppermute(value, axis, [(i, (i + steps) % count) for i in range(count)])]
    ppermute x31 -> x25, starting transfers between devices: 35.8 us -> 29.1 us  [shift(): lax.ppermute(value, axis, [(i, (i + steps) % count) for i in range(count)])]
    all_to_all x1 -> x0, waiting for transfers between devices: 4.17 us -> none  [local(): heads_in = lax.all_to_all(wide_sends, ('z', 'head'), 0, 0)]
    all_to_all x1 -> x0, starting transfers between devices: 4 us -> none  [local(): heads_in = lax.all_to_all(wide_sends, ('z', 'head'), 0, 0)]
    pallas_call x12 -> x13, Pallas kernels: 42.5 us -> 44.8 us  [call(): pl.pallas_call(kernel, out_shape=shapes, in_specs=[smem()] * len(scalars)...]
  transfers between devices with their start and end apart: 34 -> 29, of which waited for: 20 -> 20; matrix products, arithmetic and copies ran while one was open for 2% -> 1% of each run, Pallas kernels for 18% -> 19%
where the time goes in v4:
time: 170 us; the launch traced here: 169 us
  Pallas kernels  44.8 us (26%)
  waiting for transfers between devices  43.5 us (26%)
  starting transfers between devices  34.8 us (20%)
  blocking collectives  28.4 us (17%)
  between operations  13.7 us (8%)
  local copies, waits for them, and re-layouts  3.9 us (2%)
    pallas_call x13, Pallas kernels, call(): pl.pallas_call(kernel, out_shape=shapes, in_specs=[smem()] * len(scalars)...  44.8 us
    ppermute x25, waiting for transfers between devices, shift(): lax.ppermute(value, axis, [(i, (i + steps) % count) for i in range(count)])  43.5 us
    ppermute x25, starting transfers between devices, shift(): lax.ppermute(value, axis, [(i, (i + steps) % count) for i in range(count)])  29.1 us
    all_to_all x1, blocking collectives, local(): heads_in = lax.all_to_all(wide_sends, ('z', 'head'), 0, 0)  16.3 us
    all_to_all x1, blocking collectives, local(): turned = lax.all_to_all(packed, 'z', 0, 0)  12.1 us
    ppermute x2, starting transfers between devices, later(): lax.ppermute(value, axis, [(i, i + steps) for i in range(count - steps)])  5.66 us
  transfers between devices with their start and end apart: 29, of which 20 were waited for; matrix products, arithmetic and copies ran while one was open for 1% of the time, Pallas kernels for 19%

profile of v4, /device:TPU:6, one launch (start us, length us, event | category | flops | bytes accessed | tf_op | source)
XLA Modules:
  0.0 169.5 jit_solution(9991023428321864117)
XLA Ops:
  6.5 0.7 slice.10
  7.3 0.3 copy-done
  7.6 0.7 constant_dynamic-slice_fusion.1
  8.4 1.9 %collective-permute-start = (s32[1024]{0:T(1024)}, s32[1024]{0:T(1024)S(1)}, u32[]{:S(2)}, u32[]{:S(2)}) collective-permute-start(s32[1024]{0:T(1024)} %param.18), channel_id=1, source_target_pairs={{0,4},{4,8},{8,12},{12,16},{16,20},{20,24},{24,28},{28,32},{32,36}... | collective-permute-start | bytes 12296 | tf_op jit(solution)/shard_map/ppermute | solution.py:49
  10.3 3.7 %collective-permute-start.1 = (s32[256]{0:T(256)S(1)}, s32[256]{0:T(256)S(1)}, u32[]{:S(2)}, u32[]{:S(2)}) collective-permute-start(s32[256]{0:T(256)S(1)} %slice.10), channel_id=1, source_target_pairs={{0,8},{4,12},{8,16},{12,20},{16,24},{20,28},{24,32},{28,36},{32,40... | collective-permute-start | bytes 3080 | tf_op jit(solution)/shard_map/ppermute | solution.py:49
  14.1 3.3 %fine_tables.1.tab_hbm = bf16[9,256,256]{2,1,0:T(8,128)(2,1)} custom-call(f32[1,1024]{1,0:T(1,128)} %bitcast.35, bf16[256,1024]{1,0:T(8,128)(2,1)} %emb_ref.1, bf16[1024,256]{1,0:T(8,128)(2,1)} %wq_hbm.1, bf16[1024,256]{1,0:T(8,128)(2,1)} %wk_hbm.1, bf16[1024,256]{1,0:T(8,128)(2,1)} %wv_hbm.1), custom_call_target="tpu_custom_call" | custom-call | flops 3000000000 | bytes 6000000 | tf_op jit(solution)/shard_map/fine_tables/pallas_call | solution.py:244
  17.5 0.2 copy.21.own_ref
  17.7 0.1 copy.19.before_ref
  17.9 0.2 copy.20.prior_ref
  18.1 16.0 %fine_attention.1 = (bf16[272,256]{1,0:T(8,128)(2,1)S(1)}, bf16[272,256]{1,0:T(8,128)(2,1)S(1)}, bf16[272,256]{1,0:T(8,128)(2,1)S(1)}, bf16[272,256]{1,0:T(8,128)(2,1)S(1)}) custom-call(s32[3]{0:T(128)S(1)} %pad_add_fusion.where_ref, s32[256,1]{1,0:T(8,128)S(1)} %copy.19.before_ref, s32[1024,1]{1,0:T(8,128)S(1)} %copy.20.prior_ref, ...), custom_call_target="tpu_custom_call" | custom-call | flops 12000000000 | bytes 24000000 | tf_op jit(solution)/shard_map/fine_attention/pallas_call | solution.py:244
  34.1 1.7 collective-permute-start.2
  35.8 2.9 %collective-permute-start.3 = (bf16[272,256]{1,0:T(8,128)(2,1)S(1)}, bf16[272,256]{1,0:T(8,128)(2,1)S(1)}, u32[]{:S(2)}, u32[]{:S(2)}) collective-permute-start(bf16[272,256]{1,0:T(8,128)(2,1)S(1)} %get-tuple-element.29), channel_id=1, source_target_pairs={{0,2},{1,3},{2,0},{3,1},{4,6},{5,7},{6,4},{7,5},{8,10},{9,11},{10,... | collective-permute-start | bytes 417800 | tf_op jit(solution)/shard_map/ppermute | solution.py:45
  38.7 1.3 collective-permute-start.4
  40.2 0.1 broadcast_in_dim.28.ids_ref
  40.3 1.3 collective-permute-done.2.g1
  41.6 4.3 %collective-permute-done.3.g2 = bf16[272,256]{1,0:T(8,128)(2,1)S(1)} collective-permute-done((bf16[272,256]{1,0:T(8,128)(2,1)S(1)}, bf16[272,256]{1,0:T(8,128)(2,1)S(1)}, u32[]{:S(2)}, u32[]{:S(2)}) %collective-permute-start.3) | collective-permute-done | bytes 139296 | tf_op jit(solution)/shard_map/ppermute | solution.py:45
  45.9 3.4 %fine_rows.1 = bf16[4,272,256]{2,1,0:T(8,128)(2,1)S(1)} custom-call(s32[3]{0:T(128)S(1)} %pad_add_fusion.where_ref, s32[272,1]{1,0:T(8,128)S(1)} %broadcast_in_dim.28.ids_ref, bf16[256,1024]{1,0:T(8,128)(2,1)S(1)} %copy-done.2, bf16[272,256]{1,0:T(8,128)(2,1)S(1)} %get-tuple-element.27.g0, bf16[272,256]{1,0:T(8,128)(2,1)S(1)} %collective-permute-done.2.g1, ...), custom_call_target="tpu_custom_call" | custom-call | flops 2000000000 | bytes 4000000 | tf_op jit(solution)/shard_map/fine_rows/pallas_call | solution.py:244
  49.4 2.6 %collective-permute-start.9 = (bf16[272,256]{1,0:T(8,128)(2,1)S(1)}, bf16[272,256]{1,0:T(8,128)(2,1)S(1)}, u32[]{:S(2)}, u32[]{:S(2)}) collective-permute-start(bf16[272,256]{1,0:T(8,128)(2,1)S(1)} %get-tuple-element.50), channel_id=1, source_target_pairs={{0,3},{1,0},{2,1},{3,2},{4,7},{5,4},{6,5},{7,6},{8,11},{9,8},{10,9... | collective-permute-start | bytes 417800 | tf_op jit(solution)/shard_map/ppermute | solution.py:45
  52.0 2.5 %collective-permute-start.7 = (bf16[272,256]{1,0:T(8,128)(2,1)S(1)}, bf16[272,256]{1,0:T(8,128)(2,1)S(1)}, u32[]{:S(2)}, u32[]{:S(2)}) collective-permute-start(bf16[272,256]{1,0:T(8,128)(2,1)S(1)} %get-tuple-element.51), channel_id=1, source_target_pairs={{0,2},{1,3},{2,0},{3,1},{4,6},{5,7},{6,4},{7,5},{8,10},{9,11},{10,... | collective-permute-start | bytes 417800 | tf_op jit(solution)/shard_map/ppermute | solution.py:45
  54.5 0.8 collective-permute-done.9.group_ref.b3
  55.3 0.5 short_part.7
  55.8 1.8 %collective-permute-start.10 = (bf16[64,1024]{1,0:T(8,128)(2,1)S(1)}, bf16[64,1024]{1,0:T(8,128)(2,1)S(1)}, u32[]{:S(2)}, u32[]{:S(2)}) collective-permute-start(bf16[64,1024]{1,0:T(8,128)(2,1)S(1)} %short_part.7), channel_id=1, source_target_pairs={{0,1},{1,2},{2,3},{3,0},{4,5},{5,6},{6,7},{7,4},{8,9},{9,10},{10,1... | collective-permute-start | bytes 393224 | tf_op jit(solution)/shard_map/ppermute | solution.py:45
  57.6 4.5 %collective-permute-done.5.group_ref.b1 = bf16[272,256]{1,0:T(8,128)(2,1)S(1)} collective-permute-done((bf16[272,256]{1,0:T(8,128)(2,1)S(1)}, bf16[272,256]{1,0:T(8,128)(2,1)S(1)}, u32[]{:S(2)}, u32[]{:S(2)}) %collective-permute-start.5) | collective-permute-done | bytes 139296 | tf_op jit(solution)/shard_map/ppermute | solution.py:45
  62.2 0.5 short_part.5
  62.7 0.5 short_part.6
  63.2 0.4 collective-permute-start.8
  63.6 0.5 short_part.4
  64.1 0.3 collective-permute-done.10
  64.4 3.3 %collective-permute-done.6 = bf16[64,1024]{1,0:T(8,128)(2,1)S(1)} collective-permute-done((bf16[64,1024]{1,0:T(8,128)(2,1)S(1)}, bf16[64,1024]{1,0:T(8,128)(2,1)S(1)}, u32[]{:S(2)}, u32[]{:S(2)}) %collective-permute-start.6) | collective-permute-done | bytes 131104 | tf_op jit(solution)/shard_map/ppermute | solution.py:45
  67.7 3.0 %collective-permute-done.8 = bf16[64,1024]{1,0:T(8,128)(2,1)S(1)} collective-permute-done((bf16[64,1024]{1,0:T(8,128)(2,1)S(1)}, bf16[64,1024]{1,0:T(8,128)(2,1)S(1)}, u32[]{:S(2)}, u32[]{:S(2)}) %collective-permute-start.8) | collective-permute-done | bytes 131104 | tf_op jit(solution)/shard_map/ppermute | solution.py:45
  70.8 1.4 collective-permute-start.11
  72.2 1.2 collective-permute-start.12
  73.4 1.6 collective-permute-start.13
  75.0 2.1 %collective-permute-done.11.s1 = bf16[64,1024]{1,0:T(8,128)(2,1)S(1)} collective-permute-done((bf16[64,1024]{1,0:T(8,128)(2,1)S(1)}, bf16[64,1024]{1,0:T(8,128)(2,1)S(1)}, u32[]{:S(2)}, u32[]{:S(2)}) %collective-permute-start.11) | collective-permute-done | bytes 131104 | tf_op jit(solution)/shard_map/ppermute | solution.py:45
  77.1 1.6 collective-permute-done.12.s2
  78.7 0.6 collective-permute-done.13.s3
  79.4 1.6 coarse_pack.1
  80.9 0.7 constant_dynamic-slice_fusion
  81.7 12.1 %all_to_all.10.turned_ref = bf16[4,384,128]{2,1,0:T(8,128)(2,1)S(1)} all-to-all(bf16[4,384,128]{2,1,0:T(8,128)(2,1)S(1)} %get-tuple-element.33), channel_id=1, replica_groups=mesh['z'=4,'x'=4,'core'=2,'head'=4] {'z'}, dimensions={0} | all-to-all | bytes 786432 | tf_op jit(solution)/shard_map/all_to_all | solution.py:566
  93.9 1.0 collective-permute-start.14
  94.9 2.2 %collective-permute-start.15 = (bf16[4,256,128]{2,1,0:T(8,128)(2,1)S(1)}, bf16[4,256,128]{2,1,0:T(8,128)(2,1)S(1)}, u32[]{:S(2)}, u32[]{:S(2)}) collective-permute-start(bf16[4,256,128]{2,1,0:T(8,128)(2,1)S(1)} %slice.12), channel_id=1, source_target_pairs={{0,8},{8,16},{16,24},{24,0},{1,9},{9,17},{17,25},{25,1},{2,10},{10... | collective-permute-start | bytes 786440 | tf_op jit(solution)/shard_map/ppermute | solution.py:45
  97.1 2.4 %coarse_first.1 = (bf16[1024,128]{1,0:T(8,128)(2,1)S(1)}, f32[1024,128]{1,0:T(8,128)S(1)}, f32[1024,128]{1,0:T(8,128)S(1)}, f32[1024,128]{1,0:T(8,128)S(1)}) custom-call(s32[4]{0:T(128)S(1)} %fusion.5.flag_ref, bf16[4,384,128]{2,1,0:T(8,128)(2,1)S(1)} %all_to_all.10.turned_ref, bf16[4,256,128]{2,1,0:T(8,128)(2,1)S(1)} %collective-permute-done.17.far_ref), custom_call_target="tpu_custom_call" | custom-call | flops 3000000000 | bytes 6000000 | tf_op jit(solution)/shard_map/coarse_first/pallas_call | solution.py:244
  99.5 5.1 %collective-permute-done.14.refs_0_ = bf16[4,256,128]{2,1,0:T(8,128)(2,1)S(1)} collective-permute-done((bf16[4,256,128]{2,1,0:T(8,128)(2,1)S(1)}, bf16[4,256,128]{2,1,0:T(8,128)(2,1)S(1)}, u32[]{:S(2)}, u32[]{:S(2)}) %collective-permute-start.14) | collective-permute-done | bytes 262176 | tf_op jit(solution)/shard_map/ppermute | solution.py:45
  104.6 3.1 %collective-permute-done.15.refs_0_ = bf16[4,256,128]{2,1,0:T(8,128)(2,1)S(1)} collective-permute-done((bf16[4,256,128]{2,1,0:T(8,128)(2,1)S(1)}, bf16[4,256,128]{2,1,0:T(8,128)(2,1)S(1)}, u32[]{:S(2)}, u32[]{:S(2)}) %collective-permute-start.15) | collective-permute-done | bytes 262176 | tf_op jit(solution)/shard_map/ppermute | solution.py:45
  107.7 2.1 %collective-permute-done.16.refs_2_ = bf16[4,256,128]{2,1,0:T(8,128)(2,1)S(1)} collective-permute-done((bf16[4,256,128]{2,1,0:T(8,128)(2,1)S(1)}, bf16[4,256,128]{2,1,0:T(8,128)(2,1)S(1)}, u32[]{:S(2)}, u32[]{:S(2)}) %collective-permute-start.16) | collective-permute-done | bytes 262176 | tf_op jit(solution)/shard_map/ppermute | solution.py:45
  109.8 0.5 collective-permute-start.20
  110.3 1.0 collective-permute-done.19.refs_1_
  111.3 0.4 collective-permute-done.20.refs_3_
  111.7 5.5 %coarse_more.1 = (f32[1024,128]{1,0:T(8,128)S(1)}, f32[1024,128]{1,0:T(8,128)S(1)}, f32[1024,128]{1,0:T(8,128)S(1)}) custom-call(s32[4]{0:T(128)S(1)} %fusion.5.flag_ref, bf16[4,256,128]{2,1,0:T(8,128)(2,1)S(1)} %collective-permute-done.15.refs_0_, bf16[4,256,128]{2,1,0:T(8,128)(2,1)S(1)} %collective-permute-done.19.refs_1_, ...), custom_call_target="tpu_custom_call" | custom-call | flops 6000000000 | bytes 12000000 | tf_op jit(solution)/shard_map/coarse_more/pallas_call | solution.py:244
  117.2 3.0 %coarse_last.1 = bf16[16,128,128]{2,1,0:T(8,128)(2,1)S(1)} custom-call(s32[4]{0:T(128)S(1)} %fusion.5.flag_ref, bf16[4,256,128]{2,1,0:T(8,128)(2,1)S(1)} %collective-permute-done.14.refs_0_, bf16[4,256,128]{2,1,0:T(8,128)(2,1)S(1)} %collective-permute-done.18.refs_1_, bf16[1024,128]{1,0:T(8,128)(2,1)S(1)} %get-tuple-element.36.refs_4_.refs_2_, ...), custom_call_target="tpu_custom_call" | custom-call | flops 3000000000 | bytes 6000000 | tf_op jit(solution)/shard_map/coarse_last/pallas_call | solution.py:244
  120.2 16.3 %all_to_all.11.heads_ref = bf16[16,128,128]{2,1,0:T(8,128)(2,1)S(1)} all-to-all(bf16[16,128,128]{2,1,0:T(8,128)(2,1)S(1)} %coarse_last.1), channel_id=1, replica_groups=mesh['z'=4,'x'=4,'core'=2,'head'=4] {'z','head'}, dimensions={0} | all-to-all | bytes 1048576 | tf_op jit(solution)/shard_map/all_to_all | solution.py:589
  136.5 5.0 %feed.1 = (bf16[4,64,1024]{2,1,0:T(8,128)(2,1)S(1)}, f32[64,1024]{1,0:T(8,128)S(1)}) custom-call(s32[3]{0:T(128)S(1)} %pad_add_fusion.where_ref, bf16[16,128,128]{2,1,0:T(8,128)(2,1)S(1)} %all_to_all.11.heads_ref, bf16[256,1024]{1,0:T(8,128)(2,1)S(1)} %get-tuple-element.45.short_ref, f32[1,1024]{1,0:T(1,128)S(1)} %bitcast.30, bf16[1024,1024]{1,0:T(8,128)(2,1)} %up_hbm.1, ...), custom_call_target="tpu_custom_call" | custom-call | flops 4000000000 | bytes 8000000 | tf_op jit(solution)/shard_map/feed/pallas_call | solution.py:244
  141.6 0.6 collective-permute-start.21
  142.3 1.4 collective-permute-start.22
  143.7 1.4 collective-permute-start.23
  145.1 4.7 %collective-permute-done.21 = bf16[64,1024]{1,0:T(8,128)(2,1)S(1)} collective-permute-done((bf16[64,1024]{1,0:T(8,128)(2,1)S(1)}, bf16[64,1024]{1,0:T(8,128)(2,1)S(1)}, u32[]{:S(2)}, u32[]{:S(2)}) %collective-permute-start.21) | collective-permute-done | bytes 131104 | tf_op jit(solution)/shard_map/ppermute | solution.py:45
  149.8 0.6 collective-permute-done.23
  150.6 1.1 collective-permute-start.24
  151.7 3.1 %collective-permute-start.25 = (bf16[64,1024]{1,0:T(8,128)(2,1)S(1)}, bf16[64,1024]{1,0:T(8,128)(2,1)S(1)}, u32[]{:S(2)}, u32[]{:S(2)}) collective-permute-start(bf16[64,1024]{1,0:T(8,128)(2,1)S(1)} %fusion.3.s0), channel_id=1, source_target_pairs={{0,2},{1,3},{2,0},{3,1},{4,6},{5,7},{6,4},{7,5},{8,10},{9,11},{10,... | collective-permute-start | bytes 393224 | tf_op jit(solution)/shard_map/ppermute | solution.py:45
  154.7 0.2 collective-permute-start.26
  154.9 0.5 copy.23
  155.4 2.8 %collective-permute-done.24.s1 = bf16[64,1024]{1,0:T(8,128)(2,1)S(1)} collective-permute-done((bf16[64,1024]{1,0:T(8,128)(2,1)S(1)}, bf16[64,1024]{1,0:T(8,128)(2,1)S(1)}, u32[]{:S(2)}, u32[]{:S(2)}) %collective-permute-start.24) | collective-permute-done | bytes 131104 | tf_op jit(solution)/shard_map/ppermute | solution.py:45
  158.2 1.7 %collective-permute-done.25.s2 = bf16[64,1024]{1,0:T(8,128)(2,1)S(1)} collective-permute-done((bf16[64,1024]{1,0:T(8,128)(2,1)S(1)}, bf16[64,1024]{1,0:T(8,128)(2,1)S(1)}, u32[]{:S(2)}, u32[]{:S(2)}) %collective-permute-start.25) | collective-permute-done | bytes 131104 | tf_op jit(solution)/shard_map/ppermute | solution.py:45
  160.0 2.7 %final.1 = bf16[1024,256]{1,0:T(8,128)(2,1)} custom-call(s32[3]{0:T(128)S(1)} %pad_add_fusion.where_ref, bf16[64,1024]{1,0:T(8,128)(2,1)S(1)} %fusion.3.s0, bf16[64,1024]{1,0:T(8,128)(2,1)S(1)} %collective-permute-done.24.s1, bf16[64,1024]{1,0:T(8,128)(2,1)S(1)} %collective-permute-done.25.s2, bf16[64,1024]{1,0:T(8,128)(2,1)S(1)} %collective-permute-done.26.s3, ...), custom_call_target="tpu_custom_call" | custom-call | flops 2000000000 | bytes 4000000 | tf_op jit(solution)/shard_map/final/pallas_call | solution.py:244
  (52 shorter events, 0.9 us)
Async XLA Ops:
  6.5 1.1 copy-start
  6.5 39.4 %all-gather.3.cloned.1.call-start = ((), (), s32[]{:S(2)}) async-start(), calls=%async_computation.2 | async-start | bytes 2359296 | tf_op jit(solution)/shard_map/all_gather | solution.py:484
  8.3 128.2 %all-gather.5.cloned.1.call-start = ((), (), s32[]{:S(2)}) async-start(), calls=%async_computation.3 | async-start | bytes 2359296 | tf_op jit(solution)/shard_map/all_gather | solution.py:484
  8.4 9.5 %collective-permute-start = (s32[1024]{0:T(1024)}, s32[1024]{0:T(1024)S(1)}, u32[]{:S(2)}, u32[]{:S(2)}) collective-permute-start(s32[1024]{0:T(1024)} %param.18), channel_id=1, source_target_pairs={{0,4},{4,8},{8,12},{12,16},{16,20},{20,24},{24,28},{28,32},{32,36}... | collective-permute-start | bytes 12296 | tf_op jit(solution)/shard_map/ppermute | solution.py:49
  10.3 7.4 %collective-permute-start.1 = (s32[256]{0:T(256)S(1)}, s32[256]{0:T(256)S(1)}, u32[]{:S(2)}, u32[]{:S(2)}) collective-permute-start(s32[256]{0:T(256)S(1)} %slice.10), channel_id=1, source_target_pairs={{0,8},{4,12},{8,16},{12,20},{16,24},{20,28},{24,32},{28,36},{32,40... | collective-permute-start | bytes 3080 | tf_op jit(solution)/shard_map/ppermute | solution.py:49
  14.1 3.4 %copy-start.11 = (s32[1024]{0:T(1024)S(1)}, s32[1024]{0:T(1024)}, u32[]{:S(2)}) copy-start(s32[1024]{0:T(1024)} %param.18) | copy-start | bytes 12292
  18.1 27.8 %copy-start.2 = (bf16[256,1024]{1,0:T(8,128)(2,1)S(1)}, bf16[256,1024]{1,0:T(8,128)(2,1)}, u32[]{:S(2)}) copy-start(bf16[256,1024]{1,0:T(8,128)(2,1)} %emb_ref.1) | copy-start | bytes 1572868
  34.1 7.4 %collective-permute-start.2 = (bf16[272,256]{1,0:T(8,128)(2,1)S(1)}, bf16[272,256]{1,0:T(8,128)(2,1)S(1)}, u32[]{:S(2)}, u32[]{:S(2)}) collective-permute-start(bf16[272,256]{1,0:T(8,128)(2,1)S(1)} %get-tuple-element.28), channel_id=1, source_target_pairs={{0,1},{1,2},{2,3},{3,0},{4,5},{5,6},{6,7},{7,4},{8,9},{9,10},{10,1... | collective-permute-start | bytes 417800 | tf_op jit(solution)/shard_map/ppermute | solution.py:45
  35.8 10.1 %collective-permute-start.3 = (bf16[272,256]{1,0:T(8,128)(2,1)S(1)}, bf16[272,256]{1,0:T(8,128)(2,1)S(1)}, u32[]{:S(2)}, u32[]{:S(2)}) collective-permute-start(bf16[272,256]{1,0:T(8,128)(2,1)S(1)} %get-tuple-element.29), channel_id=1, source_target_pairs={{0,2},{1,3},{2,0},{3,1},{4,6},{5,7},{6,4},{7,5},{8,10},{9,11},{10,... | collective-permute-start | bytes 417800 | tf_op jit(solution)/shard_map/ppermute | solution.py:45
  38.7 7.2 %collective-permute-start.4 = (bf16[272,256]{1,0:T(8,128)(2,1)S(1)}, bf16[272,256]{1,0:T(8,128)(2,1)S(1)}, u32[]{:S(2)}, u32[]{:S(2)}) collective-permute-start(bf16[272,256]{1,0:T(8,128)(2,1)S(1)} %get-tuple-element.30), channel_id=1, source_target_pairs={{0,3},{1,0},{2,1},{3,2},{4,7},{5,4},{6,5},{7,6},{8,11},{9,8},{10,9... | collective-permute-start | bytes 417800 | tf_op jit(solution)/shard_map/ppermute | solution.py:45
  45.9 9.4 %copy-start.1 = (bf16[4,256,1024]{2,1,0:T(8,128)(2,1)S(1)}, bf16[4,256,1024]{2,1,0:T(8,128)(2,1)}, u32[]{:S(2)}) copy-start(bf16[4,256,1024]{2,1,0:T(8,128)(2,1)} %w_ref.7) | copy-start | bytes 6291460
  49.4 5.9 %collective-permute-start.9 = (bf16[272,256]{1,0:T(8,128)(2,1)S(1)}, bf16[272,256]{1,0:T(8,128)(2,1)S(1)}, u32[]{:S(2)}, u32[]{:S(2)}) collective-permute-start(bf16[272,256]{1,0:T(8,128)(2,1)S(1)} %get-tuple-element.50), channel_id=1, source_target_pairs={{0,3},{1,0},{2,1},{3,2},{4,7},{5,4},{6,5},{7,6},{8,11},{9,8},{10,9... | collective-permute-start | bytes 417800 | tf_op jit(solution)/shard_map/ppermute | solution.py:45
  52.0 10.1 %collective-permute-start.5 = (bf16[272,256]{1,0:T(8,128)(2,1)S(1)}, bf16[272,256]{1,0:T(8,128)(2,1)S(1)}, u32[]{:S(2)}, u32[]{:S(2)}) collective-permute-start(bf16[272,256]{1,0:T(8,128)(2,1)S(1)} %get-tuple-element.52), channel_id=1, source_target_pairs={{0,1},{1,2},{2,3},{3,0},{4,5},{5,6},{6,7},{7,4},{8,9},{9,10},{10,1... | collective-permute-start | bytes 417800 | tf_op jit(solution)/shard_map/ppermute | solution.py:45
  52.0 10.7 %collective-permute-start.7 = (bf16[272,256]{1,0:T(8,128)(2,1)S(1)}, bf16[272,256]{1,0:T(8,128)(2,1)S(1)}, u32[]{:S(2)}, u32[]{:S(2)}) collective-permute-start(bf16[272,256]{1,0:T(8,128)(2,1)S(1)} %get-tuple-element.51), channel_id=1, source_target_pairs={{0,2},{1,3},{2,0},{3,1},{4,6},{5,7},{6,4},{7,5},{8,10},{9,11},{10,... | collective-permute-start | bytes 417800 | tf_op jit(solution)/shard_map/ppermute | solution.py:45
  55.8 8.6 %collective-permute-start.10 = (bf16[64,1024]{1,0:T(8,128)(2,1)S(1)}, bf16[64,1024]{1,0:T(8,128)(2,1)S(1)}, u32[]{:S(2)}, u32[]{:S(2)}) collective-permute-start(bf16[64,1024]{1,0:T(8,128)(2,1)S(1)} %short_part.7), channel_id=1, source_target_pairs={{0,1},{1,2},{2,3},{3,0},{4,5},{5,6},{6,7},{7,4},{8,9},{9,10},{10,1... | collective-permute-start | bytes 393224 | tf_op jit(solution)/shard_map/ppermute | solution.py:45
  62.7 5.0 %collective-permute-start.6 = (bf16[64,1024]{1,0:T(8,128)(2,1)S(1)}, bf16[64,1024]{1,0:T(8,128)(2,1)S(1)}, u32[]{:S(2)}, u32[]{:S(2)}) collective-permute-start(bf16[64,1024]{1,0:T(8,128)(2,1)S(1)} %short_part.5), channel_id=1, source_target_pairs={{0,3},{1,0},{2,1},{3,2},{4,7},{5,4},{6,5},{7,6},{8,11},{9,8},{10,9... | collective-permute-start | bytes 393224 | tf_op jit(solution)/shard_map/ppermute | solution.py:45
  63.2 7.5 %collective-permute-start.8 = (bf16[64,1024]{1,0:T(8,128)(2,1)S(1)}, bf16[64,1024]{1,0:T(8,128)(2,1)S(1)}, u32[]{:S(2)}, u32[]{:S(2)}) collective-permute-start(bf16[64,1024]{1,0:T(8,128)(2,1)S(1)} %short_part.6), channel_id=1, source_target_pairs={{0,2},{1,3},{2,0},{3,1},{4,6},{5,7},{6,4},{7,5},{8,10},{9,11},{10,... | collective-permute-start | bytes 393224 | tf_op jit(solution)/shard_map/ppermute | solution.py:45
  63.6 15.7 %copy-start.3 = (bf16[1024,256]{1,0:T(8,128)(2,1)S(1)}, bf16[1024,256]{1,0:T(8,128)(2,1)}, u32[]{:S(2)}) copy-start(bf16[1024,256]{1,0:T(8,128)(2,1)} %wq_ref.1) | copy-start | bytes 1572868
  63.6 15.7 %copy-start.4 = (bf16[1024,256]{1,0:T(8,128)(2,1)S(1)}, bf16[1024,256]{1,0:T(8,128)(2,1)}, u32[]{:S(2)}) copy-start(bf16[1024,256]{1,0:T(8,128)(2,1)} %wk_ref.1) | copy-start | bytes 1572868
  63.6 15.7 %copy-start.5 = (bf16[1024,256]{1,0:T(8,128)(2,1)S(1)}, bf16[1024,256]{1,0:T(8,128)(2,1)}, u32[]{:S(2)}) copy-start(bf16[1024,256]{1,0:T(8,128)(2,1)} %wv_ref.1) | copy-start | bytes 1572868
  63.6 15.7 %copy-start.6 = (f32[1024]{0:T(1024)S(1)}, f32[1024]{0:T(1024)}, u32[]{:S(2)}) copy-start(f32[1024]{0:T(1024)} %param.26) | copy-start | bytes 12292
  63.6 15.7 %copy-start.8 = (f32[576,128]{1,0:T(8,128)S(1)}, f32[576,128]{1,0:T(8,128)}, u32[]{:S(2)}) copy-start(f32[576,128]{1,0:T(8,128)} %constant.90.clone.turn_hbm.turn_ref) | copy-start | bytes 884740
  70.8 6.2 %collective-permute-start.11 = (bf16[64,1024]{1,0:T(8,128)(2,1)S(1)}, bf16[64,1024]{1,0:T(8,128)(2,1)S(1)}, u32[]{:S(2)}, u32[]{:S(2)}) collective-permute-start(bf16[64,1024]{1,0:T(8,128)(2,1)S(1)} %add_convert_fusion.s0), channel_id=1, source_target_pairs={{0,1},{1,2},{2,3},{3,0},{4,5},{5,6},{6,7},{7,4},{8,9},{9,10},{10,1... | collective-permute-start | bytes 393224 | tf_op jit(solution)/shard_map/ppermute | solution.py:45
  72.2 6.5 %collective-permute-start.12 = (bf16[64,1024]{1,0:T(8,128)(2,1)S(1)}, bf16[64,1024]{1,0:T(8,128)(2,1)S(1)}, u32[]{:S(2)}, u32[]{:S(2)}) collective-permute-start(bf16[64,1024]{1,0:T(8,128)(2,1)S(1)} %add_convert_fusion.s0), channel_id=1, source_target_pairs={{0,2},{1,3},{2,0},{3,1},{4,6},{5,7},{6,4},{7,5},{8,10},{9,11},{10,... | collective-permute-start | bytes 393224 | tf_op jit(solution)/shard_map/ppermute | solution.py:45
  73.4 5.9 %collective-permute-start.13 = (bf16[64,1024]{1,0:T(8,128)(2,1)S(1)}, bf16[64,1024]{1,0:T(8,128)(2,1)S(1)}, u32[]{:S(2)}, u32[]{:S(2)}) collective-permute-start(bf16[64,1024]{1,0:T(8,128)(2,1)S(1)} %add_convert_fusion.s0), channel_id=1, source_target_pairs={{0,3},{1,0},{2,1},{3,2},{4,7},{5,4},{6,5},{7,6},{8,11},{9,8},{10,9... | collective-permute-start | bytes 393224 | tf_op jit(solution)/shard_map/ppermute | solution.py:45
  79.4 1.6 copy-start.10
  93.8 3.3 %collective-permute-start.17 = (bf16[4,256,128]{2,1,0:T(8,128)(2,1)S(1)}, bf16[4,256,128]{2,1,0:T(8,128)(2,1)S(1)}, u32[]{:S(2)}, u32[]{:S(2)}) collective-permute-start(bf16[4,256,128]{2,1,0:T(8,128)(2,1)S(1)} %slice.12), channel_id=1, source_target_pairs={{0,4},{4,0},{1,5},{5,1},{2,6},{6,2},{3,7},{7,3},{8,12},{12,8},{9,1... | collective-permute-start | bytes 786440 | tf_op jit(solution)/shard_map/ppermute | solution.py:45
  93.9 10.7 %collective-permute-start.14 = (bf16[4,256,128]{2,1,0:T(8,128)(2,1)S(1)}, bf16[4,256,128]{2,1,0:T(8,128)(2,1)S(1)}, u32[]{:S(2)}, u32[]{:S(2)}) collective-permute-start(bf16[4,256,128]{2,1,0:T(8,128)(2,1)S(1)} %slice.12), channel_id=1, source_target_pairs={{0,16},{8,24},{16,0},{24,8},{1,17},{9,25},{17,1},{25,9},{2,18},{10... | collective-permute-start | bytes 786440 | tf_op jit(solution)/shard_map/ppermute | solution.py:45
  94.9 12.8 %collective-permute-start.15 = (bf16[4,256,128]{2,1,0:T(8,128)(2,1)S(1)}, bf16[4,256,128]{2,1,0:T(8,128)(2,1)S(1)}, u32[]{:S(2)}, u32[]{:S(2)}) collective-permute-start(bf16[4,256,128]{2,1,0:T(8,128)(2,1)S(1)} %slice.12), channel_id=1, source_target_pairs={{0,8},{8,16},{16,24},{24,0},{1,9},{9,17},{17,25},{25,1},{2,10},{10... | collective-permute-start | bytes 786440 | tf_op jit(solution)/shard_map/ppermute | solution.py:45
  97.1 12.7 %collective-permute-start.16 = (bf16[4,256,128]{2,1,0:T(8,128)(2,1)S(1)}, bf16[4,256,128]{2,1,0:T(8,128)(2,1)S(1)}, u32[]{:S(2)}, u32[]{:S(2)}) collective-permute-start(bf16[4,256,128]{2,1,0:T(8,128)(2,1)S(1)} %slice.12), channel_id=1, source_target_pairs={{0,24},{8,0},{16,8},{24,16},{1,25},{9,1},{17,9},{25,17},{2,26},{10... | collective-permute-start | bytes 786440 | tf_op jit(solution)/shard_map/ppermute | solution.py:45
  109.8 1.5 collective-permute-start.19
  109.8 1.9 %collective-permute-start.20 = (bf16[4,256,128]{2,1,0:T(8,128)(2,1)S(1)}, bf16[4,256,128]{2,1,0:T(8,128)(2,1)S(1)}, u32[]{:S(2)}, u32[]{:S(2)}) collective-permute-start(bf16[4,256,128]{2,1,0:T(8,128)(2,1)S(1)} %collective-permute-done.16.refs_2_), channel_id=1, source_target_pairs={{0,4},{4,0},{1,5},{5,1},{2,6},{6,2},{3,7},{7,3},{8,12},{12,8},{9,1... | collective-permute-start | bytes 786440 | tf_op jit(solution)/shard_map/ppermute | solution.py:45
  110.3 6.9 %collective-permute-start.18 = (bf16[4,256,128]{2,1,0:T(8,128)(2,1)S(1)}, bf16[4,256,128]{2,1,0:T(8,128)(2,1)S(1)}, u32[]{:S(2)}, u32[]{:S(2)}) collective-permute-start(bf16[4,256,128]{2,1,0:T(8,128)(2,1)S(1)} %collective-permute-done.14.refs_0_), channel_id=1, source_target_pairs={{0,4},{4,0},{1,5},{5,1},{2,6},{6,2},{3,7},{7,3},{8,12},{12,8},{9,1... | collective-permute-start | bytes 786440 | tf_op jit(solution)/shard_map/ppermute | solution.py:45
  117.2 19.4 %copy-start.7 = (f32[1024]{0:T(1024)S(1)}, f32[1024]{0:T(1024)}, u32[]{:S(2)}) copy-start(f32[1024]{0:T(1024)} %param.31) | copy-start | bytes 12292
  136.5 18.4 %copy-start.9 = (bf16[1024,4,256]{2,1,0:T(4,128)(2,1)S(1)}, bf16[1024,4,256]{2,1,0:T(4,128)(2,1)}, u32[]{:S(2)}) copy-start(bf16[1024,4,256]{2,1,0:T(4,128)(2,1)} %param.34) | copy-start | bytes 6291460
  141.6 8.2 %collective-permute-start.21 = (bf16[64,1024]{1,0:T(8,128)(2,1)S(1)}, bf16[64,1024]{1,0:T(8,128)(2,1)S(1)}, u32[]{:S(2)}, u32[]{:S(2)}) collective-permute-start(bf16[64,1024]{1,0:T(8,128)(2,1)S(1)} %get-tuple-element.53), channel_id=1, source_target_pairs={{0,1},{1,2},{2,3},{3,0},{4,5},{5,6},{6,7},{7,4},{8,9},{9,10},{10,1... | collective-permute-start | bytes 393224 | tf_op jit(solution)/shard_map/ppermute | solution.py:45
  142.3 7.6 %collective-permute-start.22 = (bf16[64,1024]{1,0:T(8,128)(2,1)S(1)}, bf16[64,1024]{1,0:T(8,128)(2,1)S(1)}, u32[]{:S(2)}, u32[]{:S(2)}) collective-permute-start(bf16[64,1024]{1,0:T(8,128)(2,1)S(1)} %get-tuple-element.55), channel_id=1, source_target_pairs={{0,2},{1,3},{2,0},{3,1},{4,6},{5,7},{6,4},{7,5},{8,10},{9,11},{10,... | collective-permute-start | bytes 393224 | tf_op jit(solution)/shard_map/ppermute | solution.py:45
  143.7 6.8 %collective-permute-start.23 = (bf16[64,1024]{1,0:T(8,128)(2,1)S(1)}, bf16[64,1024]{1,0:T(8,128)(2,1)S(1)}, u32[]{:S(2)}, u32[]{:S(2)}) collective-permute-start(bf16[64,1024]{1,0:T(8,128)(2,1)S(1)} %get-tuple-element.54), channel_id=1, source_target_pairs={{0,3},{1,0},{2,1},{3,2},{4,7},{5,4},{6,5},{7,6},{8,11},{9,8},{10,9... | collective-permute-start | bytes 393224 | tf_op jit(solution)/shard_map/ppermute | solution.py:45
  150.6 7.7 %collective-permute-start.24 = (bf16[64,1024]{1,0:T(8,128)(2,1)S(1)}, bf16[64,1024]{1,0:T(8,128)(2,1)S(1)}, u32[]{:S(2)}, u32[]{:S(2)}) collective-permute-start(bf16[64,1024]{1,0:T(8,128)(2,1)S(1)} %fusion.3.s0), channel_id=1, source_target_pairs={{0,1},{1,2},{2,3},{3,0},{4,5},{5,6},{6,7},{7,4},{8,9},{9,10},{10,1... | collective-permute-start | bytes 393224 | tf_op jit(solution)/shard_map/ppermute | solution.py:45
  151.7 8.2 %collective-permute-start.25 = (bf16[64,1024]{1,0:T(8,128)(2,1)S(1)}, bf16[64,1024]{1,0:T(8,128)(2,1)S(1)}, u32[]{:S(2)}, u32[]{:S(2)}) collective-permute-start(bf16[64,1024]{1,0:T(8,128)(2,1)S(1)} %fusion.3.s0), channel_id=1, source_target_pairs={{0,2},{1,3},{2,0},{3,1},{4,6},{5,7},{6,4},{7,5},{8,10},{9,11},{10,... | collective-permute-start | bytes 393224 | tf_op jit(solution)/shard_map/ppermute | solution.py:45
  154.7 5.3 %collective-permute-start.26 = (bf16[64,1024]{1,0:T(8,128)(2,1)S(1)}, bf16[64,1024]{1,0:T(8,128)(2,1)S(1)}, u32[]{:S(2)}, u32[]{:S(2)}) collective-permute-start(bf16[64,1024]{1,0:T(8,128)(2,1)S(1)} %fusion.3.s0), channel_id=1, source_target_pairs={{0,3},{1,0},{2,1},{3,2},{4,7},{5,4},{6,5},{7,6},{8,11},{9,8},{10,9... | collective-permute-start | bytes 393224 | tf_op jit(solution)/shard_map/ppermute | solution.py:45
Sparse Core Ops, SparseCore 0:
  9.1 27.4 all-gather.2
  81.8 26.2 all-gather.4

commit v5 on v4

--- a/solution.py
+++ b/solution.py
@@ -100,9 +100,7 @@
 
 
 def turned_rows(hot, tab_ref, n, cosine, sine):
-    plain = dot(hot, tab_ref[n]) + dot(hot, tab_ref[n + 1])
-    other = dot(hot, tab_ref[n + 2]) + dot(hot, tab_ref[n + 3])
-    return (plain * cosine + other * sine).astype(bf16)
+    return (dot(hot, tab_ref[n]) * cosine + dot(hot, tab_ref[n + 1]) * sine).astype(bf16)
 
 
 def fine_tables_kernel(gain_hbm, emb_hbm, wq_hbm, wk_hbm, wv_hbm, tab_hbm, tab_ref, gain_ref, emb_ref, w_ref, sems):
@@ -117,33 +115,36 @@
     finish_copies(copies[2:])
     tq = dot(fine_in, w_ref[0]) * q_scale
     tk = dot(fine_in, w_ref[1])
-    for n, table in enumerate((tq, partner(tq), tk, partner(tk))):
-        high, low = halves(table)
-        tab_ref[2 * n] = high
-        tab_ref[2 * n + 1] = low
-    tab_ref[8] = dot(fine_in, w_ref[2]).astype(bf16)
-    finish_copies(begin_copies([(tab_ref.at[n], tab_hbm.at[n]) for n in range(9)], sems))
+    tables = (tq, partner(tq), tk, partner(tk), dot(fine_in, w_ref[2]))
+    for n, table in enumerate(tables):
+        tab_ref[n] = table.astype(bf16)
+    finish_copies(begin_copies([(tab_ref.at[n], tab_hbm.at[n]) for n in range(5)], sems))
 
 
 def fine_kernel(
     where_ref, before_ref, prior_ref, own_ref, tab_hbm, turn_hbm,
-    o0, o1, o2, o3, q_ref, k_ref, v_ref, tab_ref, turn_ref, sems,
+    out_ref, q_ref, k_ref, v_ref, tab_ref, turn_ref, sems,
 ):
     step = pl.program_id(0)
-    head = where_ref[1]
-    quarter = lax.rem(head + step, 4)
-    outs = (o0, o1, o2, o3)
     lowest = jnp.maximum(PAST - where_ref[0] * ROWS, 0)
     head_lane = lax.broadcasted_iota(jnp.int32, (1, SHARE), 1) // HEAD_DIM
 
     @pl.when(step == 0)
     def _():
+        pairs = [(tab_hbm.at[n], tab_ref.at[n]) for n in range(5)] + [(turn_hbm, turn_ref)]
+        finish_copies(begin_copies(pairs, sems))
+        cosine, sine = turn_tables(turn_ref, 0)
+        oldest = pick(before_ref[...])
+        at = slice(BLOCK - HALO, BLOCK)
+        k_ref[at, :] = turned_rows(oldest, tab_ref, 2, cosine[at], sine[at])
+        v_ref[at, :] = dot(oldest, tab_ref[4]).astype(bf16)
+
         def build(block, ids, with_q):
             begin = pl.multiple_of(block * BLOCK, BLOCK)
             hot = pick(ids)
             cosine, sine = turn_tables(turn_ref, block)
-            k_ref[pl.ds(begin, BLOCK), :] = turned_rows(hot, tab_ref, 4, cosine, sine)
-            v_ref[pl.ds(begin, BLOCK), :] = dot(hot, tab_ref[8]).astype(bf16)
+            k_ref[pl.ds(begin, BLOCK), :] = turned_rows(hot, tab_ref, 2, cosine, sine)
+            v_ref[pl.ds(begin, BLOCK), :] = dot(hot, tab_ref[4]).astype(bf16)
             if with_q:
                 at = pl.multiple_of(begin - (PAST - BLOCK), BLOCK)
                 q_ref[pl.ds(at, BLOCK), :] = turned_rows(hot, tab_ref, 0, cosine, sine)
@@ -156,9 +157,6 @@
 
             return body
 
-        pairs = [(tab_hbm.at[n], tab_ref.at[n]) for n in range(9)] + [(turn_hbm, turn_ref)]
-        finish_copies(begin_copies(pairs, sems))
-        build(0, before_ref[...], False)
         lax.fori_loop(0, 3, build_from(prior_ref, 1, False), 0)
         build(4, prior_ref[3 * BLOCK :, :], True)
         lax.fori_loop(0, 4, build_from(own_ref, 5, True), 0)
@@ -166,25 +164,21 @@
         stacked = jnp.concatenate(
             [jnp.where(head_lane == h, halo_q, jnp.zeros_like(halo_q)) for h in range(4)], axis=0
         )
-        scores = dot_t(stacked, k_ref[0:PAST, :])
+        scores = dot_t(stacked, k_ref[BLOCK - HALO : PAST, :])
         row = lax.broadcasted_iota(jnp.int32, scores.shape, 0) % HALO + (PAST - HALO)
-        col = lax.broadcasted_iota(jnp.int32, scores.shape, 1)
+        col = lax.broadcasted_iota(jnp.int32, scores.shape, 1) + (BLOCK - HALO)
         allowed = (col <= row) & (col > row - WINDOW) & (col >= lowest)
         scores = jnp.where(allowed, scores, masked_low)
         top = jnp.max(scores, axis=1, keepdims=True)
         weights = jnp.exp2(scores - top)
         total = jnp.sum(weights, axis=1, keepdims=True)
-        mixed = dot(weights.astype(bf16), v_ref[0:PAST, :]) / total
+        mixed = dot(weights.astype(bf16), v_ref[BLOCK - HALO : PAST, :]) / total
         result = jnp.zeros((HALO, SHARE), f32)
         for h in range(4):
             result = jnp.where(head_lane == h, mixed[h * HALO : (h + 1) * HALO], result)
-        for s, out_ref in enumerate(outs):
-
-            @pl.when(lax.rem(head + s, 4) == 0)
-            def _(out_ref=out_ref):
-                out_ref[0:HALO, :] = result.astype(bf16)
-
-    begin = pl.multiple_of((quarter + 1) * BLOCK, BLOCK)
+        out_ref[0, 0:HALO, :] = result.astype(bf16)
+
+    begin = pl.multiple_of((step + 1) * BLOCK, BLOCK)
     keys = k_ref[pl.ds(begin, PAST), :]
     values = v_ref[pl.ds(begin, PAST), :]
     query = q_ref[pl.ds(begin, BLOCK), :]
@@ -198,8 +192,15 @@
     ones = jnp.ones((PAST, 128), bf16)
     low_lanes = lax.broadcasted_iota(jnp.int32, (1, 128), 1) < 64
     results = []
+
+    def score(h):
+        return dot_t(jnp.where(head_lane == h, query, jnp.zeros_like(query)), keys)
+
+    ahead = score(0)
     for h in range(4):
-        scores = dot_t(jnp.where(head_lane == h, query, jnp.zeros_like(query)), keys)
+        scores = ahead
+        if h < 3:
+            ahead = score(h + 1)
         tiles = [scores[:, t * BLOCK : (t + 1) * BLOCK] for t in range(5)]
         tiles = (
             [tiles[0] + first_bias]
@@ -219,15 +220,11 @@
         [jnp.where(low_lanes, results[2 * n], results[2 * n + 1]) for n in range(2)], axis=1
     )
     result = result.astype(bf16)
-    for s in range(4):
-
-        @pl.when(step == s)
-        def _(s=s):
-            outs[s][HALO:, :] = result
-
-            @pl.when(quarter < 3)
-            def _():
-                outs[(s + 1) % 4][0:HALO, :] = result[BLOCK - HALO :]
+    out_ref[step, HALO:, :] = result
+
+    @pl.when(step < 3)
+    def _():
+        out_ref[step + 1, 0:HALO, :] = result[BLOCK - HALO :]
 
 
 def vmem():
@@ -273,20 +270,18 @@
 
 
 def fine_rows_kernel(
-    where_ref, ids_ref, emb_ref, g0, g1, g2, g3, w_hbm, out_ref, w_ref, got_ref, sems
+    where_ref, ids_ref, emb_ref, got_ref, own_ref, m1, m2, m3, t1, t2, t3, w_hbm,
+    out_ref, w_ref, sems,
 ):
-    place, head = where_ref[0], where_ref[1]
-    pairs = []
-    for part in range(8):
-        at = pl.ds(part * 128, 128)
-        pairs.append((w_hbm.at[at], w_ref.at[at]))
-    copies = begin_copies(pairs, sems)
-    for s, got in enumerate((g0, g1, g2, g3)):
-        begin = pl.multiple_of(lax.rem(head - s + 4, 4) * SHARE, SHARE)
-        got_ref[:, pl.ds(begin, SHARE)] = got[...]
-    merged = dot(pick(ids_ref[...]), emb_ref[...])
-    finish_copies(copies)
-    merged += dot(got_ref[...], w_ref[...])
+    place, head, core = where_ref[0], where_ref[1], where_ref[2]
+    copies = begin_copies([(w_hbm.at[n], w_ref.at[n]) for n in range(4)], sems)
+    merged = dot(pick(ids_ref[...]), emb_ref[...]) + dot(got_ref[head], own_ref[...])
+    near = pl.ds(pl.multiple_of(core * 128, 128), 128)
+    far = pl.ds(pl.multiple_of(128 - core * 128, 128), 128)
+    for s, mine, other in ((1, m1, t1), (2, m2, t2), (3, m3, t3)):
+        source = lax.rem(head - s + 4, 4)
+        merged += dot(got_ref[source, :, near], mine[...])
+        merged += dot(got_ref[source, :, far], other[...])
     rows = 256 + HALO
     token = (
         place * ROWS + head * 256 - HALO + lax.broadcasted_iota(jnp.int32, (rows, D), 0)
@@ -300,6 +295,7 @@
     for d in range(4):
         out_ref[d, 0:256, :] = grouped[:, d * SHARE : (d + 1) * SHARE]
         out_ref[d, 256:rows, :] = fine[256:rows, d * SHARE : (d + 1) * SHARE]
+    finish_copies(copies)
 
 
 def short_part_kernel(group_ref, w_ref, out_ref):
@@ -430,12 +426,12 @@
 
 
 def feed_kernel(
-    where_ref, heads_ref, short_ref, gain_ref, up_hbm, down_hbm, co_hbm,
+    where_ref, heads_ref, short_ref, gain_ref, own, mine, other, up_hbm, down_hbm,
     part_ref, first_ref, mixed_ref, all_ref, co_ref, up_ref, down_ref, sems,
 ):
     head = where_ref[1]
-    pairs = []
-    for w, w_ref in ((co_hbm, co_ref), (up_hbm, up_ref), (down_hbm, down_ref)):
+    pairs = place_copies(head, where_ref[2], own, mine, other, co_ref)
+    for w, w_ref in ((up_hbm, up_ref), (down_hbm, down_ref)):
         for part in range(4):
             at = pl.ds(part * 256, 256)
             pairs.append((w.at[at], w_ref.at[at]))
@@ -448,12 +444,12 @@
             at = slice(y * 256 + pair * 128, y * 256 + (pair + 1) * 128)
             mixed_ref[0:128, at] = jnp.where(low_lanes, even, pltpu.roll(odd, 64, 1)).astype(bf16)
             mixed_ref[128:256, at] = jnp.where(low_lanes, pltpu.roll(even, 64, 1), odd).astype(bf16)
-    finish_copies(copies[:4])
+    finish_copies(copies[:7])
     first = short_ref[...].astype(f32) + dot(mixed_ref[...], co_ref[...])
     all_ref[...] = first
     first_ref[...] = all_ref[pl.ds(pl.multiple_of(head * 64, 64), 64), :]
     feed = norm_rows(first, gain_ref[...])
-    finish_copies(copies[4:])
+    finish_copies(copies[7:])
     inner = jax.nn.gelu(dot(feed, up_ref[...])).astype(bf16)
     part_ref[...] = dot(inner, down_ref[...]).astype(bf16).reshape(4, 64, D)
 
@@ -479,9 +475,20 @@
         out_ref[pl.ds(begin, 256), :] = dot(weave, value).astype(bf16)
 
 
-def fetch_all(weight, core):
+def fetch_half(weight, core):
     half = lax.dynamic_slice_in_dim(weight, core * 128, 128, 0)
-    return lax.all_gather(half, ("head", "core"), axis=0, tiled=True)
+    return [shift(half, "head", s, 4) for s in range(1, 4)]
+
+
+def place_copies(head, core, own, mine, other, target):
+    pairs = [(own, target.at[pl.ds(pl.multiple_of(head * 256, 256), 256)])]
+    for s in range(1, 4):
+        source = lax.rem(head - s + 4, 4) * 256
+        at = pl.multiple_of(source + core * 128, 128)
+        pairs.append((mine.at[s - 1], target.at[pl.ds(at, 128)]))
+        at = pl.multiple_of(source + 128 - core * 128, 128)
+        pairs.append((other.at[s - 1], target.at[pl.ds(at, 128)]))
+    return pairs
 
 
 def after(value, gate):
@@ -501,44 +508,47 @@
     where = jnp.stack([place, head, core])
 
     prior = later(token_ids, SEQ, 1, 32)
-    last_ids = token_ids[ROWS - BLOCK :]
+    last_ids = token_ids[ROWS - HALO :]
     before = later(last_ids, SEQ, 2, 32)
     tab = call(
-        fine_tables_kernel, "fine_tables", pltpu.HBM((9, 256, SHARE), bf16), [], [],
+        fine_tables_kernel, "fine_tables", pltpu.HBM((5, 256, SHARE), bf16), [], [],
         [
-            pltpu.VMEM((9, 256, SHARE), bf16),
+            pltpu.VMEM((5, 256, SHARE), bf16),
             pltpu.VMEM((1, D), f32), pltpu.VMEM((256, D), bf16),
             pltpu.VMEM((3, D, SHARE), bf16), pltpu.SemaphoreType.DMA((9,)),
         ],
         us=3, out_hbm=True, hbm=[fine_norm[None], embedding, fine_query, fine_key, fine_value],
     )
     fine_output_held, _ = after(fine_output, last_ids)
-    fine_output_all = fetch_all(fine_output_held, core)
+    out_mine = fetch_half(fine_output_held, core)
     rows = 256 + HALO
     mixed = call(
-        fine_kernel, "fine_attention", [jax.ShapeDtypeStruct((rows, SHARE), bf16)] * 4,
+        fine_kernel, "fine_attention", jax.ShapeDtypeStruct((4, rows, SHARE), bf16),
         [where], [before[:, None], prior[:, None], token_ids[:, None]],
         [
             pltpu.VMEM((BLOCK + ROWS, SHARE), bf16),
             pltpu.VMEM((KEYS, SHARE), bf16), pltpu.VMEM((KEYS, SHARE), bf16),
-            pltpu.VMEM((9, 256, SHARE), bf16), pltpu.VMEM((576, 128), f32),
+            pltpu.VMEM((5, 256, SHARE), bf16), pltpu.VMEM((576, 128), f32),
             pltpu.SemaphoreType.DMA((10,)),
         ],
         grid=(4,), us=12, limit=24, hbm=[tab, tables],
     )
 
-    got = [mixed[0]] + [shift(mixed[s], "head", s, 4) for s in range(1, 4)]
+    out_mine, mixed = after(out_mine, mixed)
+    got = lax.all_to_all(mixed, "head", 0, 0)
+    out_other = [shift(part, "core", 1, 2) for part in out_mine]
     own_ids = lax.dynamic_slice_in_dim(
         jnp.concatenate([prior[ROWS - HALO :], token_ids]), head * 256, rows, 0
     )
-    sends = call(
-        fine_rows_kernel, "fine_rows", jax.ShapeDtypeStruct((4, rows, SHARE), bf16),
-        [where], [own_ids[:, None], embedding, *got],
+    sends, shorten_near = call(
+        fine_rows_kernel, "fine_rows",
         [
-            pltpu.VMEM((D, D), bf16), pltpu.VMEM((rows, D), bf16),
-            pltpu.SemaphoreType.DMA((8,)),
+            jax.ShapeDtypeStruct((4, rows, SHARE), bf16),
+            jax.ShapeDtypeStruct((SHORTEN, SHARE, D), bf16),
         ],
-        hbm=[fine_output_all],
+        [where],
+        [own_ids[:, None], embedding, got, fine_output, *out_mine, *out_other],
+        [pltpu.SemaphoreType.DMA((4,))], hbm=[shorten_weight],
     )
     blocks = exchange(lambda d: lax.dynamic_index_in_dim(sends, d, 0, keepdims=False), "head", 4)
 
@@ -546,7 +556,7 @@
     for s, block in enumerate(blocks):
         part = call(
             short_part_kernel, "short_part", jax.ShapeDtypeStruct((64, D), bf16), [],
-            [block, shorten_weight],
+            [block, shorten_near],
         )
         terms.append(part if s == 0 else shift(part, "head", 4 - s, 4))
     short_own = sum(t.astype(f32) for t in terms).astype(bf16)
@@ -561,9 +571,9 @@
         [*shorts, coarse_norm[None], coarse_query, coarse_key, coarse_value, tables],
     )
 
-    coarse_output_held, packed = after(coarse_output, packed)
-    coarse_output_all = fetch_all(coarse_output_held, core)
     turned = lax.all_to_all(packed, "z", 0, 0)
+    coarse_output_held, turned = after(coarse_output, turned)
+    co_mine = fetch_half(coarse_output_held, core)
     kv = turned[:, :COARSE_ROWS]
     far = [shift(kv, "core", 1, 2)]
     near = [shift(kv, "x", s, 4) for s in range(1, 4)]
@@ -586,8 +596,11 @@
         jax.ShapeDtypeStruct((16, 128, 128), bf16),
         [flags], [near[1], far[2], q_all, *sums], [pltpu.VMEM((1024, 128), f32)] * 3, us=3, limit=24,
     )
+    co_mine, wide_sends = after(co_mine, wide_sends)
+    co_mine = jnp.stack(co_mine)
+    co_other = shift(co_mine, "core", 1, 2)
+
     heads_in = lax.all_to_all(wide_sends, ("z", "head"), 0, 0)
-    square = pltpu.VMEM((D, D), bf16)
     parts, first_own = call(
         feed_kernel, "feed",
         [jax.ShapeDtypeStruct((4, 64, D), bf16), jax.ShapeDtypeStruct((64, D), f32)],
@@ -595,9 +608,9 @@
         [heads_in, short, ffn_norm[None]],
         [
             pltpu.VMEM((COARSE_ROWS, D), bf16), pltpu.VMEM((COARSE_ROWS, D), f32),
-            square, square, square, pltpu.SemaphoreType.DMA((12,)),
+            *[pltpu.VMEM((D, D), bf16)] * 3, pltpu.SemaphoreType.DMA((15,)),
         ],
-        hbm=[ffn_up, ffn_down, coarse_output_all], us=4, limit=24,
+        hbm=[coarse_output, co_mine, co_other, ffn_up, ffn_down], us=4, limit=24,
     )
     sums = exchange(lambda d: lax.dynamic_index_in_dim(parts, d, 0, keepdims=False), "head", 4)
     second_own = (first_own + sum(t.astype(f32) for t in sums)).astype(bf16)

time: 170 us -> 168 us (0.988)
  between operations: 13.7 us -> 0.39 us
  starting transfers between devices: 34.8 us -> 42.1 us
  waiting for transfers between devices: 43.5 us -> 49 us
  Pallas kernels: 44.8 us -> 42.8 us
    all_to_all x0 -> x1, waiting for transfers between devices: none -> 8.24 us  [local(): got = lax.all_to_all(mixed, 'head', 0, 0)]
    ppermute x25 -> x32, starting transfers between devices: 29.1 us -> 33 us  [shift(): lax.ppermute(value, axis, [(i, (i + steps) % count) for i in range(count)])]
    all_to_all x0 -> x1, starting transfers between devices: none -> 3.48 us  [local(): got = lax.all_to_all(mixed, 'head', 0, 0)]
    ppermute x25 -> x32, waiting for transfers between devices: 43.5 us -> 40.8 us  [shift(): lax.ppermute(value, axis, [(i, (i + steps) % count) for i in range(count)])]
    pallas_call x13, Pallas kernels: 44.8 us -> 42.8 us  [call(): pl.pallas_call(kernel, out_shape=shapes, in_specs=[smem()] * len(scalars)...]
  transfers between devices with their start and end apart: 29 -> 35, of which waited for: 20 -> 21; matrix products, arithmetic and copies ran while one was open for 1% -> 2% of each run, Pallas kernels for 19% -> 18%
where the time goes in v5:
time: 168 us; the launch traced here: 167 us
  waiting for transfers between devices  49 us (29%)
  Pallas kernels  42.8 us (25%)
  starting transfers between devices  42.1 us (25%)
  blocking collectives  28.7 us (17%)
  local copies, waits for them, and re-layouts  3.98 us (2%)
    pallas_call x13, Pallas kernels, call(): pl.pallas_call(kernel, out_shape=shapes, in_specs=[smem()] * len(scalars)...  42.8 us
    ppermute x32, waiting for transfers between devices, shift(): lax.ppermute(value, axis, [(i, (i + steps) % count) for i in range(count)])  40.8 us
    ppermute x32, starting transfers between devices, shift(): lax.ppermute(value, axis, [(i, (i + steps) % count) for i in range(count)])  33 us
    all_to_all x1, blocking collectives, local(): heads_in = lax.all_to_all(wide_sends, ('z', 'head'), 0, 0)  16.6 us
    all_to_all x1, blocking collectives, local(): turned = lax.all_to_all(packed, 'z', 0, 0)  12.1 us
    all_to_all x1, waiting for transfers between devices, local(): got = lax.all_to_all(mixed, 'head', 0, 0)  8.24 us
    ppermute x2, starting transfers between devices, later(): lax.ppermute(value, axis, [(i, i + steps) for i in range(count - steps)])  5.64 us
    all_to_all x1, starting transfers between devices, local(): got = lax.all_to_all(mixed, 'head', 0, 0)  3.48 us
  transfers between devices with their start and end apart: 35, of which 21 were waited for; matrix products, arithmetic and copies ran while one was open for 2% of the time, Pallas kernels for 18%

profile of v5, /device:TPU:6, one launch (start us, length us, event | category | flops | bytes accessed | tf_op | source)
XLA Modules:
  0.0 167.4 jit_solution(16072006030131653539)
XLA Ops:
  0.0 1.9 %collective-permute-start = (s32[1024]{0:T(1024)}, s32[1024]{0:T(1024)S(1)}, u32[]{:S(2)}, u32[]{:S(2)}) collective-permute-start(s32[1024]{0:T(1024)} %param.18), channel_id=1, source_target_pairs={{0,4},{4,8},{8,12},{12,16},{16,20},{20,24},{24,28},{28,32},{32,36}... | collective-permute-start | bytes 12296 | tf_op jit(solution)/shard_map/ppermute | solution.py:49
  1.9 0.8 slice.10
  2.7 3.7 %collective-permute-start.4 = (s32[16]{0:T(128)S(1)}, s32[16]{0:T(128)S(1)}, u32[]{:S(2)}, u32[]{:S(2)}) collective-permute-start(s32[16]{0:T(128)S(1)} %slice.10), channel_id=1, source_target_pairs={{0,8},{4,12},{8,16},{12,20},{16,24},{20,28},{24,32},{28,36},{32,40... | collective-permute-start | bytes 200 | tf_op jit(solution)/shard_map/ppermute | solution.py:49
  6.4 1.0 constant_dynamic-slice_fusion.1
  7.4 1.6 collective-permute-start.1
  9.0 2.9 %collective-permute-start.2 = (bf16[128,1024]{1,0:T(8,128)(2,1)S(1)}, bf16[128,1024]{1,0:T(8,128)(2,1)S(1)}, u32[]{:S(2)}, u32[]{:S(2)}) collective-permute-start(bf16[128,1024]{1,0:T(8,128)(2,1)S(1)} %constant_dynamic-slice_fusion.1), channel_id=1, source_target_pairs={{0,2},{1,3},{2,0},{3,1},{4,6},{5,7},{6,4},{7,5},{8,10},{9,11},{10,... | collective-permute-start | bytes 786440 | tf_op jit(solution)/shard_map/ppermute | solution.py:45
  11.9 1.3 collective-permute-start.3
  13.3 3.2 %fine_tables.1.tab_hbm = bf16[5,256,256]{2,1,0:T(8,128)(2,1)} custom-call(f32[1,1024]{1,0:T(1,128)} %bitcast.41, bf16[256,1024]{1,0:T(8,128)(2,1)} %emb_ref.1, bf16[1024,256]{1,0:T(8,128)(2,1)} %wq_hbm.1, bf16[1024,256]{1,0:T(8,128)(2,1)} %wk_hbm.1, bf16[1024,256]{1,0:T(8,128)(2,1)} %wv_hbm.1), custom_call_target="tpu_custom_call" | custom-call | flops 3000000000 | bytes 6000000 | tf_op jit(solution)/shard_map/fine_tables/pallas_call | solution.py:241
  17.1 14.5 %fine_attention.1 = bf16[4,272,256]{2,1,0:T(8,128)(2,1)} custom-call(s32[3]{0:T(128)S(1)} %pad_add_fusion.where_ref, s32[16,1]{1,0:T(8,128)S(1)} %copy.20.before_ref, s32[1024,1]{1,0:T(8,128)S(1)} %copy.21.prior_ref, s32[1024,1]{1,0:T(8,128)S(1)} %copy.22.own_ref, bf16[5,256,256]{2,1,0:T(8,128)(2,1)} %fine_tables.1.tab_hbm, ...), custom_call_target="tpu_custom_call" | custom-call | flops 12000000000 | bytes 24000000 | tf_op jit(solution)/shard_map/fine_attention/pallas_call | solution.py:241
  31.6 3.5 %all-to-all-start = ((bf16[4,272,256]{2,1,0:T(8,128)(2,1)}), bf16[4,272,256]{2,1,0:T(8,128)(2,1)S(1)}, u32[]{:S(2)}, u32[]{:S(2)}) async-start(bf16[4,272,256]{2,1,0:T(8,128)(2,1)} %fine_attention.1), calls=%async_computation | async-start | bytes 1114112 | tf_op jit(solution)/shard_map/all_to_all | solution.py:538
  35.1 0.6 collective-permute-start.5
  35.8 0.4 collective-permute-start.7
  36.5 0.4 collective-permute-done.5.t1
  36.8 0.4 collective-permute-done.6.t2
  37.2 0.4 collective-permute-done.7.t3
  37.6 8.2 %all-to-all-done.got_ref = bf16[4,272,256]{2,1,0:T(8,128)(2,1)S(1)} async-done(((bf16[4,272,256]{2,1,0:T(8,128)(2,1)}), bf16[4,272,256]{2,1,0:T(8,128)(2,1)S(1)}, u32[]{:S(2)}, u32[]{:S(2)}) %all-to-all-start) | async-done | bytes 557088 | tf_op jit(solution)/shard_map/all_to_all | solution.py:538
  45.8 2.8 %fine_rows.1 = (bf16[4,272,256]{2,1,0:T(8,128)(2,1)S(1)}, bf16[4,256,1024]{2,1,0:T(8,128)(2,1)S(1)}) custom-call(s32[3]{0:T(128)S(1)} %pad_add_fusion.where_ref, s32[272,1]{1,0:T(8,128)S(1)} %broadcast_in_dim.28.ids_ref, bf16[256,1024]{1,0:T(8,128)(2,1)S(1)} %copy-done.1, bf16[4,272,256]{2,1,0:T(8,128)(2,1)S(1)} %all-to-all-done.got_ref, ...), custom_call_target="tpu_custom_call" | custom-call | flops 2000000000 | bytes 4000000 | tf_op jit(solution)/shard_map/fine_rows/pallas_call | solution.py:241
  48.7 0.6 collective-permute-start.8
  49.4 2.1 %collective-permute-start.10 = (bf16[272,256]{1,0:T(8,128)(2,1)S(1)}, bf16[272,256]{1,0:T(8,128)(2,1)S(1)}, u32[]{:S(2)}, u32[]{:S(2)}) collective-permute-start(bf16[272,256]{1,0:T(8,128)(2,1)S(1)} %get-tuple-element.63), channel_id=1, source_target_pairs={{0,2},{1,3},{2,0},{3,1},{4,6},{5,7},{6,4},{7,5},{8,10},{9,11},{10,... | collective-permute-start | bytes 417800 | tf_op jit(solution)/shard_map/ppermute | solution.py:45
  51.5 0.7 collective-permute-start.12
  52.2 6.1 %collective-permute-done.8.group_ref.b1 = bf16[272,256]{1,0:T(8,128)(2,1)S(1)} collective-permute-done((bf16[272,256]{1,0:T(8,128)(2,1)S(1)}, bf16[272,256]{1,0:T(8,128)(2,1)S(1)}, u32[]{:S(2)}, u32[]{:S(2)}) %collective-permute-start.8) | collective-permute-done | bytes 139296 | tf_op jit(solution)/shard_map/ppermute | solution.py:45
  58.3 0.5 short_part.5
  58.9 0.5 short_part.6
  59.4 0.4 collective-permute-start.11
  59.7 0.5 short_part.7
  60.2 1.9 %collective-permute-start.13 = (bf16[64,1024]{1,0:T(8,128)(2,1)S(1)}, bf16[64,1024]{1,0:T(8,128)(2,1)S(1)}, u32[]{:S(2)}, u32[]{:S(2)}) collective-permute-start(bf16[64,1024]{1,0:T(8,128)(2,1)S(1)} %short_part.7), channel_id=1, source_target_pairs={{0,1},{1,2},{2,3},{3,0},{4,5},{5,6},{6,7},{7,4},{8,9},{9,10},{10,1... | collective-permute-start | bytes 393224 | tf_op jit(solution)/shard_map/ppermute | solution.py:45
  62.1 0.5 short_part.4
  62.6 1.2 collective-permute-done.9
  63.8 2.8 %collective-permute-done.11 = bf16[64,1024]{1,0:T(8,128)(2,1)S(1)} collective-permute-done((bf16[64,1024]{1,0:T(8,128)(2,1)S(1)}, bf16[64,1024]{1,0:T(8,128)(2,1)S(1)}, u32[]{:S(2)}, u32[]{:S(2)}) %collective-permute-start.11) | collective-permute-done | bytes 131104 | tf_op jit(solution)/shard_map/ppermute | solution.py:45
  66.6 1.4 collective-permute-done.13
  68.1 3.8 %collective-permute-start.15 = (bf16[64,1024]{1,0:T(8,128)(2,1)S(1)}, bf16[64,1024]{1,0:T(8,128)(2,1)S(1)}, u32[]{:S(2)}, u32[]{:S(2)}) collective-permute-start(bf16[64,1024]{1,0:T(8,128)(2,1)S(1)} %add_convert_fusion.s0), channel_id=1, source_target_pairs={{0,2},{1,3},{2,0},{3,1},{4,6},{5,7},{6,4},{7,5},{8,10},{9,11},{10,... | collective-permute-start | bytes 393224 | tf_op jit(solution)/shard_map/ppermute | solution.py:45
  72.1 2.2 %collective-permute-done.14.s1 = bf16[64,1024]{1,0:T(8,128)(2,1)S(1)} collective-permute-done((bf16[64,1024]{1,0:T(8,128)(2,1)S(1)}, bf16[64,1024]{1,0:T(8,128)(2,1)S(1)}, u32[]{:S(2)}, u32[]{:S(2)}) %collective-permute-start.14) | collective-permute-done | bytes 131104 | tf_op jit(solution)/shard_map/ppermute | solution.py:45
  74.3 2.0 %collective-permute-done.15.s2 = bf16[64,1024]{1,0:T(8,128)(2,1)S(1)} collective-permute-done((bf16[64,1024]{1,0:T(8,128)(2,1)S(1)}, bf16[64,1024]{1,0:T(8,128)(2,1)S(1)}, u32[]{:S(2)}, u32[]{:S(2)}) %collective-permute-start.15) | collective-permute-done | bytes 131104 | tf_op jit(solution)/shard_map/ppermute | solution.py:45
  76.3 0.6 collective-permute-done.16.s3
  77.0 1.6 coarse_pack.1
  78.5 12.1 %all_to_all.15.turned_ref = bf16[4,384,128]{2,1,0:T(8,128)(2,1)S(1)} all-to-all(bf16[4,384,128]{2,1,0:T(8,128)(2,1)S(1)} %get-tuple-element.40), channel_id=1, replica_groups=mesh['z'=4,'x'=4,'core'=2,'head'=4] {'z'}, dimensions={0} | all-to-all | bytes 786432 | tf_op jit(solution)/shard_map/all_to_all | solution.py:574
  90.7 1.3 collective-permute-start.20
  92.0 2.0 %collective-permute-start.21 = (bf16[4,256,128]{2,1,0:T(8,128)(2,1)S(1)}, bf16[4,256,128]{2,1,0:T(8,128)(2,1)S(1)}, u32[]{:S(2)}, u32[]{:S(2)}) collective-permute-start(bf16[4,256,128]{2,1,0:T(8,128)(2,1)S(1)} %slice.11), channel_id=1, source_target_pairs={{0,8},{8,16},{16,24},{24,0},{1,9},{9,17},{17,25},{25,1},{2,10},{10... | collective-permute-start | bytes 786440 | tf_op jit(solution)/shard_map/ppermute | solution.py:45
  94.1 2.4 %coarse_first.1 = (bf16[1024,128]{1,0:T(8,128)(2,1)S(1)}, f32[1024,128]{1,0:T(8,128)S(1)}, f32[1024,128]{1,0:T(8,128)S(1)}, f32[1024,128]{1,0:T(8,128)S(1)}) custom-call(s32[4]{0:T(128)S(1)} %fusion.5.flag_ref, bf16[4,384,128]{2,1,0:T(8,128)(2,1)S(1)} %all_to_all.15.turned_ref, bf16[4,256,128]{2,1,0:T(8,128)(2,1)S(1)} %collective-permute-done.23.far_ref), custom_call_target="tpu_custom_call" | custom-call | flops 3000000000 | bytes 6000000 | tf_op jit(solution)/shard_map/coarse_first/pallas_call | solution.py:241
  96.5 4.9 %collective-permute-done.20.refs_0_ = bf16[4,256,128]{2,1,0:T(8,128)(2,1)S(1)} collective-permute-done((bf16[4,256,128]{2,1,0:T(8,128)(2,1)S(1)}, bf16[4,256,128]{2,1,0:T(8,128)(2,1)S(1)}, u32[]{:S(2)}, u32[]{:S(2)}) %collective-permute-start.20) | collective-permute-done | bytes 262176 | tf_op jit(solution)/shard_map/ppermute | solution.py:45
  101.4 3.1 %collective-permute-done.21.refs_0_ = bf16[4,256,128]{2,1,0:T(8,128)(2,1)S(1)} collective-permute-done((bf16[4,256,128]{2,1,0:T(8,128)(2,1)S(1)}, bf16[4,256,128]{2,1,0:T(8,128)(2,1)S(1)}, u32[]{:S(2)}, u32[]{:S(2)}) %collective-permute-start.21) | collective-permute-done | bytes 262176 | tf_op jit(solution)/shard_map/ppermute | solution.py:45
  104.6 2.0 %collective-permute-done.22.refs_2_ = bf16[4,256,128]{2,1,0:T(8,128)(2,1)S(1)} collective-permute-done((bf16[4,256,128]{2,1,0:T(8,128)(2,1)S(1)}, bf16[4,256,128]{2,1,0:T(8,128)(2,1)S(1)}, u32[]{:S(2)}, u32[]{:S(2)}) %collective-permute-start.22) | collective-permute-done | bytes 262176 | tf_op jit(solution)/shard_map/ppermute | solution.py:45
  106.6 0.5 collective-permute-start.26
  107.1 0.4 collective-permute-start.17
  107.6 3.4 %collective-permute-start.18 = (bf16[128,1024]{1,0:T(8,128)(2,1)S(1)}, bf16[128,1024]{1,0:T(8,128)(2,1)S(1)}, u32[]{:S(2)}, u32[]{:S(2)}) collective-permute-start(bf16[128,1024]{1,0:T(8,128)(2,1)S(1)} %constant_dynamic-slice_fusion), channel_id=1, source_target_pairs={{0,2},{1,3},{2,0},{3,1},{4,6},{5,7},{6,4},{7,5},{8,10},{9,11},{10,... | collective-permute-start | bytes 786440 | tf_op jit(solution)/shard_map/ppermute | solution.py:45
  111.0 0.3 collective-permute-start.19
  111.4 5.5 %coarse_more.1 = (f32[1024,128]{1,0:T(8,128)S(1)}, f32[1024,128]{1,0:T(8,128)S(1)}, f32[1024,128]{1,0:T(8,128)S(1)}) custom-call(s32[4]{0:T(128)S(1)} %fusion.5.flag_ref, bf16[4,256,128]{2,1,0:T(8,128)(2,1)S(1)} %collective-permute-done.21.refs_0_, bf16[4,256,128]{2,1,0:T(8,128)(2,1)S(1)} %collective-permute-done.25.refs_1_, ...), custom_call_target="tpu_custom_call" | custom-call | flops 6000000000 | bytes 12000000 | tf_op jit(solution)/shard_map/coarse_more/pallas_call | solution.py:241
  116.9 3.3 %coarse_last.1 = bf16[16,128,128]{2,1,0:T(8,128)(2,1)S(1)} custom-call(s32[4]{0:T(128)S(1)} %fusion.5.flag_ref, bf16[4,256,128]{2,1,0:T(8,128)(2,1)S(1)} %collective-permute-done.20.refs_0_, bf16[4,256,128]{2,1,0:T(8,128)(2,1)S(1)} %collective-permute-done.24.refs_1_, bf16[1024,128]{1,0:T(8,128)(2,1)S(1)} %get-tuple-element.45.refs_4_.refs_2_, ...), custom_call_target="tpu_custom_call" | custom-call | flops 3000000000 | bytes 6000000 | tf_op jit(solution)/shard_map/coarse_last/pallas_call | solution.py:241
  120.2 2.6 %collective-permute-done.18 = bf16[128,1024]{1,0:T(8,128)(2,1)S(1)} collective-permute-done((bf16[128,1024]{1,0:T(8,128)(2,1)S(1)}, bf16[128,1024]{1,0:T(8,128)(2,1)S(1)}, u32[]{:S(2)}, u32[]{:S(2)}) %collective-permute-start.18) | collective-permute-done | bytes 262176 | tf_op jit(solution)/shard_map/ppermute | solution.py:45
  123.1 16.6 %all_to_all.16.heads_ref = bf16[16,128,128]{2,1,0:T(8,128)(2,1)S(1)} all-to-all(bf16[16,128,128]{2,1,0:T(8,128)(2,1)S(1)} %coarse_last.1), channel_id=1, replica_groups=mesh['z'=4,'x'=4,'core'=2,'head'=4] {'z','head'}, dimensions={0} | all-to-all | bytes 1048576 | tf_op jit(solution)/shard_map/all_to_all | solution.py:603
  139.7 0.9 copy-done.12
  140.6 5.0 %feed.1 = (bf16[4,64,1024]{2,1,0:T(8,128)(2,1)S(1)}, f32[64,1024]{1,0:T(8,128)S(1)}) custom-call(s32[3]{0:T(128)S(1)} %pad_add_fusion.where_ref, bf16[16,128,128]{2,1,0:T(8,128)(2,1)S(1)} %all_to_all.16.heads_ref, bf16[256,1024]{1,0:T(8,128)(2,1)S(1)} %get-tuple-element.55.short_ref, f32[1,1024]{1,0:T(1,128)S(1)} %bitcast.33, bf16[256,1024]{1,0:T(8,128)(2,1)} %own.1, ...), custom_call_target="tpu_custom_call" | custom-call | flops 4000000000 | bytes 8000000 | tf_op jit(solution)/shard_map/feed/pallas_call | solution.py:241
  145.6 0.6 collective-permute-start.28
  146.3 1.4 collective-permute-start.29
  147.7 1.5 collective-permute-start.30
  149.2 5.0 %collective-permute-done.28 = bf16[64,1024]{1,0:T(8,128)(2,1)S(1)} collective-permute-done((bf16[64,1024]{1,0:T(8,128)(2,1)S(1)}, bf16[64,1024]{1,0:T(8,128)(2,1)S(1)}, u32[]{:S(2)}, u32[]{:S(2)}) %collective-permute-start.28) | collective-permute-done | bytes 131104 | tf_op jit(solution)/shard_map/ppermute | solution.py:45
  154.2 0.6 collective-permute-done.30
  154.9 1.2 collective-permute-start.31
  156.1 3.0 %collective-permute-start.32 = (bf16[64,1024]{1,0:T(8,128)(2,1)S(1)}, bf16[64,1024]{1,0:T(8,128)(2,1)S(1)}, u32[]{:S(2)}, u32[]{:S(2)}) collective-permute-start(bf16[64,1024]{1,0:T(8,128)(2,1)S(1)} %fusion.3.s0), channel_id=1, source_target_pairs={{0,2},{1,3},{2,0},{3,1},{4,6},{5,7},{6,4},{7,5},{8,10},{9,11},{10,... | collective-permute-start | bytes 393224 | tf_op jit(solution)/shard_map/ppermute | solution.py:45
  159.1 0.3 collective-permute-start.33
  159.4 0.5 copy.24
  159.9 2.2 %collective-permute-done.31.s1 = bf16[64,1024]{1,0:T(8,128)(2,1)S(1)} collective-permute-done((bf16[64,1024]{1,0:T(8,128)(2,1)S(1)}, bf16[64,1024]{1,0:T(8,128)(2,1)S(1)}, u32[]{:S(2)}, u32[]{:S(2)}) %collective-permute-start.31) | collective-permute-done | bytes 131104 | tf_op jit(solution)/shard_map/ppermute | solution.py:45
  162.1 2.5 %collective-permute-done.32.s2 = bf16[64,1024]{1,0:T(8,128)(2,1)S(1)} collective-permute-done((bf16[64,1024]{1,0:T(8,128)(2,1)S(1)}, bf16[64,1024]{1,0:T(8,128)(2,1)S(1)}, u32[]{:S(2)}, u32[]{:S(2)}) %collective-permute-start.32) | collective-permute-done | bytes 131104 | tf_op jit(solution)/shard_map/ppermute | solution.py:45
  164.7 2.7 %final.1 = bf16[1024,256]{1,0:T(8,128)(2,1)} custom-call(s32[3]{0:T(128)S(1)} %pad_add_fusion.where_ref, bf16[64,1024]{1,0:T(8,128)(2,1)S(1)} %fusion.3.s0, bf16[64,1024]{1,0:T(8,128)(2,1)S(1)} %collective-permute-done.31.s1, bf16[64,1024]{1,0:T(8,128)(2,1)S(1)} %collective-permute-done.32.s2, bf16[64,1024]{1,0:T(8,128)(2,1)S(1)} %collective-permute-done.33.s3, ...), custom_call_target="tpu_custom_call" | custom-call | flops 2000000000 | bytes 4000000 | tf_op jit(solution)/shard_map/final/pallas_call | solution.py:241
  (65 shorter events, 2.1 us)
Async XLA Ops:
  0.0 16.9 %collective-permute-start = (s32[1024]{0:T(1024)}, s32[1024]{0:T(1024)S(1)}, u32[]{:S(2)}, u32[]{:S(2)}) collective-permute-start(s32[1024]{0:T(1024)} %param.18), channel_id=1, source_target_pairs={{0,4},{4,8},{8,12},{12,16},{16,20},{20,24},{24,28},{28,32},{32,36}... | collective-permute-start | bytes 12296 | tf_op jit(solution)/shard_map/ppermute | solution.py:49
  2.7 14.1 %collective-permute-start.4 = (s32[16]{0:T(128)S(1)}, s32[16]{0:T(128)S(1)}, u32[]{:S(2)}, u32[]{:S(2)}) collective-permute-start(s32[16]{0:T(128)S(1)} %slice.10), channel_id=1, source_target_pairs={{0,8},{4,12},{8,16},{12,20},{16,24},{20,28},{24,32},{28,36},{32,40... | collective-permute-start | bytes 200 | tf_op jit(solution)/shard_map/ppermute | solution.py:49
  7.4 24.2 %collective-permute-start.1 = (bf16[128,1024]{1,0:T(8,128)(2,1)S(1)}, bf16[128,1024]{1,0:T(8,128)(2,1)S(1)}, u32[]{:S(2)}, u32[]{:S(2)}) collective-permute-start(bf16[128,1024]{1,0:T(8,128)(2,1)S(1)} %constant_dynamic-slice_fusion.1), channel_id=1, source_target_pairs={{0,1},{1,2},{2,3},{3,0},{4,5},{5,6},{6,7},{7,4},{8,9},{9,10},{10,1... | collective-permute-start | bytes 786440 | tf_op jit(solution)/shard_map/ppermute | solution.py:45
  9.0 22.6 %collective-permute-start.2 = (bf16[128,1024]{1,0:T(8,128)(2,1)S(1)}, bf16[128,1024]{1,0:T(8,128)(2,1)S(1)}, u32[]{:S(2)}, u32[]{:S(2)}) collective-permute-start(bf16[128,1024]{1,0:T(8,128)(2,1)S(1)} %constant_dynamic-slice_fusion.1), channel_id=1, source_target_pairs={{0,2},{1,3},{2,0},{3,1},{4,6},{5,7},{6,4},{7,5},{8,10},{9,11},{10,... | collective-permute-start | bytes 786440 | tf_op jit(solution)/shard_map/ppermute | solution.py:45
  11.9 19.7 %collective-permute-start.3 = (bf16[128,1024]{1,0:T(8,128)(2,1)S(1)}, bf16[128,1024]{1,0:T(8,128)(2,1)S(1)}, u32[]{:S(2)}, u32[]{:S(2)}) collective-permute-start(bf16[128,1024]{1,0:T(8,128)(2,1)S(1)} %constant_dynamic-slice_fusion.1), channel_id=1, source_target_pairs={{0,3},{1,0},{2,1},{3,2},{4,7},{5,4},{6,5},{7,6},{8,11},{9,8},{10,9... | collective-permute-start | bytes 786440 | tf_op jit(solution)/shard_map/ppermute | solution.py:45
  13.3 3.2 %copy-start.11 = (s32[1024]{0:T(1024)S(1)}, s32[1024]{0:T(1024)}, u32[]{:S(2)}) copy-start(s32[1024]{0:T(1024)} %param.18) | copy-start | bytes 12292
  17.1 28.8 %copy-start = (bf16[256,1024]{1,0:T(8,128)(2,1)S(1)}, bf16[256,1024]{1,0:T(8,128)(2,1)}, u32[]{:S(2)}) copy-start(bf16[256,1024]{1,0:T(8,128)(2,1)} %own_ref.1) | copy-start | bytes 1572868
  17.1 28.7 %copy-start.1 = (bf16[256,1024]{1,0:T(8,128)(2,1)S(1)}, bf16[256,1024]{1,0:T(8,128)(2,1)}, u32[]{:S(2)}) copy-start(bf16[256,1024]{1,0:T(8,128)(2,1)} %emb_ref.1) | copy-start | bytes 1572868
  31.6 14.2 %all-to-all-start = ((bf16[4,272,256]{2,1,0:T(8,128)(2,1)}), bf16[4,272,256]{2,1,0:T(8,128)(2,1)S(1)}, u32[]{:S(2)}, u32[]{:S(2)}) async-start(bf16[4,272,256]{2,1,0:T(8,128)(2,1)} %fine_attention.1), calls=%async_computation | async-start | bytes 1114112 | tf_op jit(solution)/shard_map/all_to_all | solution.py:538
  35.1 1.7 %collective-permute-start.5 = (bf16[128,1024]{1,0:T(8,128)(2,1)S(1)}, bf16[128,1024]{1,0:T(8,128)(2,1)S(1)}, u32[]{:S(2)}, u32[]{:S(2)}) collective-permute-start(bf16[128,1024]{1,0:T(8,128)(2,1)S(1)} %collective-permute-done.1.m1), channel_id=1, source_target_pairs={{0,4},{4,0},{1,5},{5,1},{2,6},{6,2},{3,7},{7,3},{8,12},{12,8},{9,1... | collective-permute-start | bytes 786440 | tf_op jit(solution)/shard_map/ppermute | solution.py:45
  35.7 1.5 collective-permute-start.6
  35.8 1.8 %collective-permute-start.7 = (bf16[128,1024]{1,0:T(8,128)(2,1)S(1)}, bf16[128,1024]{1,0:T(8,128)(2,1)S(1)}, u32[]{:S(2)}, u32[]{:S(2)}) collective-permute-start(bf16[128,1024]{1,0:T(8,128)(2,1)S(1)} %collective-permute-done.3.m3), channel_id=1, source_target_pairs={{0,4},{4,0},{1,5},{5,1},{2,6},{6,2},{3,7},{7,3},{8,12},{12,8},{9,1... | collective-permute-start | bytes 786440 | tf_op jit(solution)/shard_map/ppermute | solution.py:45
  48.7 9.5 %collective-permute-start.8 = (bf16[272,256]{1,0:T(8,128)(2,1)S(1)}, bf16[272,256]{1,0:T(8,128)(2,1)S(1)}, u32[]{:S(2)}, u32[]{:S(2)}) collective-permute-start(bf16[272,256]{1,0:T(8,128)(2,1)S(1)} %get-tuple-element.64), channel_id=1, source_target_pairs={{0,1},{1,2},{2,3},{3,0},{4,5},{5,6},{6,7},{7,4},{8,9},{9,10},{10,1... | collective-permute-start | bytes 417800 | tf_op jit(solution)/shard_map/ppermute | solution.py:45
  49.4 9.5 %collective-permute-start.10 = (bf16[272,256]{1,0:T(8,128)(2,1)S(1)}, bf16[272,256]{1,0:T(8,128)(2,1)S(1)}, u32[]{:S(2)}, u32[]{:S(2)}) collective-permute-start(bf16[272,256]{1,0:T(8,128)(2,1)S(1)} %get-tuple-element.63), channel_id=1, source_target_pairs={{0,2},{1,3},{2,0},{3,1},{4,6},{5,7},{6,4},{7,5},{8,10},{9,11},{10,... | collective-permute-start | bytes 417800 | tf_op jit(solution)/shard_map/ppermute | solution.py:45
  51.5 8.3 %collective-permute-start.12 = (bf16[272,256]{1,0:T(8,128)(2,1)S(1)}, bf16[272,256]{1,0:T(8,128)(2,1)S(1)}, u32[]{:S(2)}, u32[]{:S(2)}) collective-permute-start(bf16[272,256]{1,0:T(8,128)(2,1)S(1)} %get-tuple-element.62), channel_id=1, source_target_pairs={{0,3},{1,0},{2,1},{3,2},{4,7},{5,4},{6,5},{7,6},{8,11},{9,8},{10,9... | collective-permute-start | bytes 417800 | tf_op jit(solution)/shard_map/ppermute | solution.py:45
  58.8 5.0 %collective-permute-start.9 = (bf16[64,1024]{1,0:T(8,128)(2,1)S(1)}, bf16[64,1024]{1,0:T(8,128)(2,1)S(1)}, u32[]{:S(2)}, u32[]{:S(2)}) collective-permute-start(bf16[64,1024]{1,0:T(8,128)(2,1)S(1)} %short_part.5), channel_id=1, source_target_pairs={{0,3},{1,0},{2,1},{3,2},{4,7},{5,4},{6,5},{7,6},{8,11},{9,8},{10,9... | collective-permute-start | bytes 393224 | tf_op jit(solution)/shard_map/ppermute | solution.py:45
  59.4 7.2 %collective-permute-start.11 = (bf16[64,1024]{1,0:T(8,128)(2,1)S(1)}, bf16[64,1024]{1,0:T(8,128)(2,1)S(1)}, u32[]{:S(2)}, u32[]{:S(2)}) collective-permute-start(bf16[64,1024]{1,0:T(8,128)(2,1)S(1)} %short_part.6), channel_id=1, source_target_pairs={{0,2},{1,3},{2,0},{3,1},{4,6},{5,7},{6,4},{7,5},{8,10},{9,11},{10,... | collective-permute-start | bytes 393224 | tf_op jit(solution)/shard_map/ppermute | solution.py:45
  60.2 7.8 %collective-permute-start.13 = (bf16[64,1024]{1,0:T(8,128)(2,1)S(1)}, bf16[64,1024]{1,0:T(8,128)(2,1)S(1)}, u32[]{:S(2)}, u32[]{:S(2)}) collective-permute-start(bf16[64,1024]{1,0:T(8,128)(2,1)S(1)} %short_part.7), channel_id=1, source_target_pairs={{0,1},{1,2},{2,3},{3,0},{4,5},{5,6},{6,7},{7,4},{8,9},{9,10},{10,1... | collective-permute-start | bytes 393224 | tf_op jit(solution)/shard_map/ppermute | solution.py:45
  62.1 14.8 %copy-start.2 = (bf16[1024,256]{1,0:T(8,128)(2,1)S(1)}, bf16[1024,256]{1,0:T(8,128)(2,1)}, u32[]{:S(2)}) copy-start(bf16[1024,256]{1,0:T(8,128)(2,1)} %wq_ref.1) | copy-start | bytes 1572868
  62.1 14.8 %copy-start.3 = (bf16[1024,256]{1,0:T(8,128)(2,1)S(1)}, bf16[1024,256]{1,0:T(8,128)(2,1)}, u32[]{:S(2)}) copy-start(bf16[1024,256]{1,0:T(8,128)(2,1)} %wk_ref.1) | copy-start | bytes 1572868
  62.1 14.8 %copy-start.4 = (bf16[1024,256]{1,0:T(8,128)(2,1)S(1)}, bf16[1024,256]{1,0:T(8,128)(2,1)}, u32[]{:S(2)}) copy-start(bf16[1024,256]{1,0:T(8,128)(2,1)} %wv_ref.1) | copy-start | bytes 1572868
  62.1 14.8 %copy-start.5 = (f32[1024]{0:T(1024)S(1)}, f32[1024]{0:T(1024)}, u32[]{:S(2)}) copy-start(f32[1024]{0:T(1024)} %param.26) | copy-start | bytes 12292
  62.1 14.8 %copy-start.7 = (f32[576,128]{1,0:T(8,128)S(1)}, f32[576,128]{1,0:T(8,128)}, u32[]{:S(2)}) copy-start(f32[576,128]{1,0:T(8,128)} %constant.90.clone.turn_hbm.turn_ref) | copy-start | bytes 884740
  68.1 6.2 %collective-permute-start.14 = (bf16[64,1024]{1,0:T(8,128)(2,1)S(1)}, bf16[64,1024]{1,0:T(8,128)(2,1)S(1)}, u32[]{:S(2)}, u32[]{:S(2)}) collective-permute-start(bf16[64,1024]{1,0:T(8,128)(2,1)S(1)} %add_convert_fusion.s0), channel_id=1, source_target_pairs={{0,1},{1,2},{2,3},{3,0},{4,5},{5,6},{6,7},{7,4},{8,9},{9,10},{10,1... | collective-permute-start | bytes 393224 | tf_op jit(solution)/shard_map/ppermute | solution.py:45
  68.1 8.2 %collective-permute-start.15 = (bf16[64,1024]{1,0:T(8,128)(2,1)S(1)}, bf16[64,1024]{1,0:T(8,128)(2,1)S(1)}, u32[]{:S(2)}, u32[]{:S(2)}) collective-permute-start(bf16[64,1024]{1,0:T(8,128)(2,1)S(1)} %add_convert_fusion.s0), channel_id=1, source_target_pairs={{0,2},{1,3},{2,0},{3,1},{4,6},{5,7},{6,4},{7,5},{8,10},{9,11},{10,... | collective-permute-start | bytes 393224 | tf_op jit(solution)/shard_map/ppermute | solution.py:45
  72.0 5.0 %collective-permute-start.16 = (bf16[64,1024]{1,0:T(8,128)(2,1)S(1)}, bf16[64,1024]{1,0:T(8,128)(2,1)S(1)}, u32[]{:S(2)}, u32[]{:S(2)}) collective-permute-start(bf16[64,1024]{1,0:T(8,128)(2,1)S(1)} %add_convert_fusion.s0), channel_id=1, source_target_pairs={{0,3},{1,0},{2,1},{3,2},{4,7},{5,4},{6,5},{7,6},{8,11},{9,8},{10,9... | collective-permute-start | bytes 393224 | tf_op jit(solution)/shard_map/ppermute | solution.py:45
  90.6 3.5 %collective-permute-start.23 = (bf16[4,256,128]{2,1,0:T(8,128)(2,1)S(1)}, bf16[4,256,128]{2,1,0:T(8,128)(2,1)S(1)}, u32[]{:S(2)}, u32[]{:S(2)}) collective-permute-start(bf16[4,256,128]{2,1,0:T(8,128)(2,1)S(1)} %slice.11), channel_id=1, source_target_pairs={{0,4},{4,0},{1,5},{5,1},{2,6},{6,2},{3,7},{7,3},{8,12},{12,8},{9,1... | collective-permute-start | bytes 786440 | tf_op jit(solution)/shard_map/ppermute | solution.py:45
  90.7 16.4 %copy-start.10 = (bf16[256,1024]{1,0:T(8,128)(2,1)S(1)}, bf16[256,1024]{1,0:T(8,128)(2,1)}, u32[]{:S(2)}) copy-start(bf16[256,1024]{1,0:T(8,128)(2,1)} %own.1) | copy-start | bytes 1572868
  90.7 10.7 %collective-permute-start.20 = (bf16[4,256,128]{2,1,0:T(8,128)(2,1)S(1)}, bf16[4,256,128]{2,1,0:T(8,128)(2,1)S(1)}, u32[]{:S(2)}, u32[]{:S(2)}) collective-permute-start(bf16[4,256,128]{2,1,0:T(8,128)(2,1)S(1)} %slice.11), channel_id=1, source_target_pairs={{0,16},{8,24},{16,0},{24,8},{1,17},{9,25},{17,1},{25,9},{2,18},{10... | collective-permute-start | bytes 786440 | tf_op jit(solution)/shard_map/ppermute | solution.py:45
  92.0 12.6 %collective-permute-start.21 = (bf16[4,256,128]{2,1,0:T(8,128)(2,1)S(1)}, bf16[4,256,128]{2,1,0:T(8,128)(2,1)S(1)}, u32[]{:S(2)}, u32[]{:S(2)}) collective-permute-start(bf16[4,256,128]{2,1,0:T(8,128)(2,1)S(1)} %slice.11), channel_id=1, source_target_pairs={{0,8},{8,16},{16,24},{24,0},{1,9},{9,17},{17,25},{25,1},{2,10},{10... | collective-permute-start | bytes 786440 | tf_op jit(solution)/shard_map/ppermute | solution.py:45
  94.0 12.6 %collective-permute-start.22 = (bf16[4,256,128]{2,1,0:T(8,128)(2,1)S(1)}, bf16[4,256,128]{2,1,0:T(8,128)(2,1)S(1)}, u32[]{:S(2)}, u32[]{:S(2)}) collective-permute-start(bf16[4,256,128]{2,1,0:T(8,128)(2,1)S(1)} %slice.11), channel_id=1, source_target_pairs={{0,24},{8,0},{16,8},{24,16},{1,25},{9,1},{17,9},{25,17},{2,26},{10... | collective-permute-start | bytes 786440 | tf_op jit(solution)/shard_map/ppermute | solution.py:45
  106.6 4.7 %collective-permute-start.25 = (bf16[4,256,128]{2,1,0:T(8,128)(2,1)S(1)}, bf16[4,256,128]{2,1,0:T(8,128)(2,1)S(1)}, u32[]{:S(2)}, u32[]{:S(2)}) collective-permute-start(bf16[4,256,128]{2,1,0:T(8,128)(2,1)S(1)} %collective-permute-done.21.refs_0_), channel_id=1, source_target_pairs={{0,4},{4,0},{1,5},{5,1},{2,6},{6,2},{3,7},{7,3},{8,12},{12,8},{9,1... | collective-permute-start | bytes 786440 | tf_op jit(solution)/shard_map/ppermute | solution.py:45
  106.6 4.7 %collective-permute-start.26 = (bf16[4,256,128]{2,1,0:T(8,128)(2,1)S(1)}, bf16[4,256,128]{2,1,0:T(8,128)(2,1)S(1)}, u32[]{:S(2)}, u32[]{:S(2)}) collective-permute-start(bf16[4,256,128]{2,1,0:T(8,128)(2,1)S(1)} %collective-permute-done.22.refs_2_), channel_id=1, source_target_pairs={{0,4},{4,0},{1,5},{5,1},{2,6},{6,2},{3,7},{7,3},{8,12},{12,8},{9,1... | collective-permute-start | bytes 786440 | tf_op jit(solution)/shard_map/ppermute | solution.py:45
  107.1 13.0 %collective-permute-start.17 = (bf16[128,1024]{1,0:T(8,128)(2,1)S(1)}, bf16[128,1024]{1,0:T(8,128)(2,1)S(1)}, u32[]{:S(2)}, u32[]{:S(2)}) collective-permute-start(bf16[128,1024]{1,0:T(8,128)(2,1)S(1)} %constant_dynamic-slice_fusion), channel_id=1, source_target_pairs={{0,1},{1,2},{2,3},{3,0},{4,5},{5,6},{6,7},{7,4},{8,9},{9,10},{10,1... | collective-permute-start | bytes 786440 | tf_op jit(solution)/shard_map/ppermute | solution.py:45
  107.6 15.2 %collective-permute-start.18 = (bf16[128,1024]{1,0:T(8,128)(2,1)S(1)}, bf16[128,1024]{1,0:T(8,128)(2,1)S(1)}, u32[]{:S(2)}, u32[]{:S(2)}) collective-permute-start(bf16[128,1024]{1,0:T(8,128)(2,1)S(1)} %constant_dynamic-slice_fusion), channel_id=1, source_target_pairs={{0,2},{1,3},{2,0},{3,1},{4,6},{5,7},{6,4},{7,5},{8,10},{9,11},{10,... | collective-permute-start | bytes 786440 | tf_op jit(solution)/shard_map/ppermute | solution.py:45
  111.0 11.9 %collective-permute-start.19 = (bf16[128,1024]{1,0:T(8,128)(2,1)S(1)}, bf16[128,1024]{1,0:T(8,128)(2,1)S(1)}, u32[]{:S(2)}, u32[]{:S(2)}) collective-permute-start(bf16[128,1024]{1,0:T(8,128)(2,1)S(1)} %constant_dynamic-slice_fusion), channel_id=1, source_target_pairs={{0,3},{1,0},{2,1},{3,2},{4,7},{5,4},{6,5},{7,6},{8,11},{9,8},{10,9... | collective-permute-start | bytes 786440 | tf_op jit(solution)/shard_map/ppermute | solution.py:45
  111.4 5.5 %collective-permute-start.24 = (bf16[4,256,128]{2,1,0:T(8,128)(2,1)S(1)}, bf16[4,256,128]{2,1,0:T(8,128)(2,1)S(1)}, u32[]{:S(2)}, u32[]{:S(2)}) collective-permute-start(bf16[4,256,128]{2,1,0:T(8,128)(2,1)S(1)} %collective-permute-done.20.refs_0_), channel_id=1, source_target_pairs={{0,4},{4,0},{1,5},{5,1},{2,6},{6,2},{3,7},{7,3},{8,12},{12,8},{9,1... | collective-permute-start | bytes 786440 | tf_op jit(solution)/shard_map/ppermute | solution.py:45
  120.2 20.4 %copy-start.6 = (f32[1024]{0:T(1024)S(1)}, f32[1024]{0:T(1024)}, u32[]{:S(2)}) copy-start(f32[1024]{0:T(1024)} %param.31) | copy-start | bytes 12292
  123.0 16.7 %copy-start.9 = (bf16[3,128,1024]{2,1,0:T(8,128)(2,1)}, bf16[3,128,1024]{2,1,0:T(8,128)(2,1)S(1)}, u32[]{:S(2)}) copy-start(bf16[3,128,1024]{2,1,0:T(8,128)(2,1)S(1)} %pad_maximum_fusion.mine) | copy-start | bytes 2359300
  123.0 16.7 %collective-permute-start.27 = (bf16[3,128,1024]{2,1,0:T(8,128)(2,1)S(1)}, bf16[3,128,1024]{2,1,0:T(8,128)(2,1)S(1)}, u32[]{:S(2)}, u32[]{:S(2)}) collective-permute-start(bf16[3,128,1024]{2,1,0:T(8,128)(2,1)S(1)} %pad_maximum_fusion.mine), channel_id=1, source_target_pairs={{0,4},{4,0},{1,5},{5,1},{2,6},{6,2},{3,7},{7,3},{8,12},{12,8},{9,1... | collective-permute-start | bytes 2359304 | tf_op jit(solution)/shard_map/ppermute | solution.py:45
  139.7 0.9 copy-start.12
  140.6 18.8 %copy-start.8 = (bf16[1024,4,256]{2,1,0:T(4,128)(2,1)S(1)}, bf16[1024,4,256]{2,1,0:T(4,128)(2,1)}, u32[]{:S(2)}) copy-start(bf16[1024,4,256]{2,1,0:T(4,128)(2,1)} %param.34) | copy-start | bytes 6291460
  145.6 8.6 %collective-permute-start.28 = (bf16[64,1024]{1,0:T(8,128)(2,1)S(1)}, bf16[64,1024]{1,0:T(8,128)(2,1)S(1)}, u32[]{:S(2)}, u32[]{:S(2)}) collective-permute-start(bf16[64,1024]{1,0:T(8,128)(2,1)S(1)} %get-tuple-element.65), channel_id=1, source_target_pairs={{0,1},{1,2},{2,3},{3,0},{4,5},{5,6},{6,7},{7,4},{8,9},{9,10},{10,1... | collective-permute-start | bytes 393224 | tf_op jit(solution)/shard_map/ppermute | solution.py:45
  146.3 7.9 %collective-permute-start.29 = (bf16[64,1024]{1,0:T(8,128)(2,1)S(1)}, bf16[64,1024]{1,0:T(8,128)(2,1)S(1)}, u32[]{:S(2)}, u32[]{:S(2)}) collective-permute-start(bf16[64,1024]{1,0:T(8,128)(2,1)S(1)} %get-tuple-element.67), channel_id=1, source_target_pairs={{0,2},{1,3},{2,0},{3,1},{4,6},{5,7},{6,4},{7,5},{8,10},{9,11},{10,... | collective-permute-start | bytes 393224 | tf_op jit(solution)/shard_map/ppermute | solution.py:45
  147.7 7.1 %collective-permute-start.30 = (bf16[64,1024]{1,0:T(8,128)(2,1)S(1)}, bf16[64,1024]{1,0:T(8,128)(2,1)S(1)}, u32[]{:S(2)}, u32[]{:S(2)}) collective-permute-start(bf16[64,1024]{1,0:T(8,128)(2,1)S(1)} %get-tuple-element.66), channel_id=1, source_target_pairs={{0,3},{1,0},{2,1},{3,2},{4,7},{5,4},{6,5},{7,6},{8,11},{9,8},{10,9... | collective-permute-start | bytes 393224 | tf_op jit(solution)/shard_map/ppermute | solution.py:45
  154.9 7.2 %collective-permute-start.31 = (bf16[64,1024]{1,0:T(8,128)(2,1)S(1)}, bf16[64,1024]{1,0:T(8,128)(2,1)S(1)}, u32[]{:S(2)}, u32[]{:S(2)}) collective-permute-start(bf16[64,1024]{1,0:T(8,128)(2,1)S(1)} %fusion.3.s0), channel_id=1, source_target_pairs={{0,1},{1,2},{2,3},{3,0},{4,5},{5,6},{6,7},{7,4},{8,9},{9,10},{10,1... | collective-permute-start | bytes 393224 | tf_op jit(solution)/shard_map/ppermute | solution.py:45
  156.1 8.5 %collective-permute-start.32 = (bf16[64,1024]{1,0:T(8,128)(2,1)S(1)}, bf16[64,1024]{1,0:T(8,128)(2,1)S(1)}, u32[]{:S(2)}, u32[]{:S(2)}) collective-permute-start(bf16[64,1024]{1,0:T(8,128)(2,1)S(1)} %fusion.3.s0), channel_id=1, source_target_pairs={{0,2},{1,3},{2,0},{3,1},{4,6},{5,7},{6,4},{7,5},{8,10},{9,11},{10,... | collective-permute-start | bytes 393224 | tf_op jit(solution)/shard_map/ppermute | solution.py:45
  159.1 5.6 %collective-permute-start.33 = (bf16[64,1024]{1,0:T(8,128)(2,1)S(1)}, bf16[64,1024]{1,0:T(8,128)(2,1)S(1)}, u32[]{:S(2)}, u32[]{:S(2)}) collective-permute-start(bf16[64,1024]{1,0:T(8,128)(2,1)S(1)} %fusion.3.s0), channel_id=1, source_target_pairs={{0,3},{1,0},{2,1},{3,2},{4,7},{5,4},{6,5},{7,6},{8,11},{9,8},{10,9... | collective-permute-start | bytes 393224 | tf_op jit(solution)/shard_map/ppermute | solution.py:45

commit v6 on v5

--- a/solution.py
+++ b/solution.py
@@ -235,7 +235,12 @@
     return pl.BlockSpec(memory_space=pltpu.SMEM)
 
 
-def call(kernel, name, shapes, scalars, arrays, scratch=(), grid=None, limit=16, us=2, hbm=(), out_hbm=False):
+def space(shape):
+    plain = isinstance(shape, jax.ShapeDtypeStruct)
+    return vmem() if plain else pl.BlockSpec(memory_space=pltpu.HBM)
+
+
+def call(kernel, name, shapes, scalars, arrays, scratch=(), grid=None, limit=16, us=2, hbm=(), free=()):
     one = not isinstance(shapes, (list, tuple))
     extra = {} if grid is None else {"grid": grid}
     return pl.pallas_call(
@@ -243,10 +248,9 @@
         out_shape=shapes,
         in_specs=[smem()] * len(scalars)
         + [vmem()] * len(arrays)
-        + [pl.BlockSpec(memory_space=pltpu.HBM)] * len(hbm),
-        out_specs=(pl.BlockSpec(memory_space=pltpu.HBM) if out_hbm else vmem())
-        if one
-        else [vmem()] * len(shapes),
+        + [pl.BlockSpec(memory_space=pltpu.HBM)] * len(hbm)
+        + [pl.BlockSpec(memory_space=pl.ANY)] * len(free),
+        out_specs=space(shapes) if one else [space(shape) for shape in shapes],
         scratch_shapes=list(scratch),
         compiler_params=pltpu.CompilerParams(vmem_limit_bytes=limit << 20),
         cost_estimate=pl.CostEstimate(
@@ -254,7 +258,7 @@
         ),
         name=name,
         **extra,
-    )(*scalars, *arrays, *(pltpu.with_memory_space_constraint(a, pltpu.HBM) for a in hbm))
+    )(*scalars, *arrays, *(pltpu.with_memory_space_constraint(a, pltpu.HBM) for a in hbm), *free)
 
 
 def begin_copies(pairs, sems):
@@ -270,18 +274,18 @@
 
 
 def fine_rows_kernel(
-    where_ref, ids_ref, emb_ref, got_ref, own_ref, m1, m2, m3, t1, t2, t3, w_hbm,
+    where_ref, ids_ref, emb_ref, got_ref, own_ref, m1, m2, t1, t2, w_hbm,
     out_ref, w_ref, sems,
 ):
     place, head, core = where_ref[0], where_ref[1], where_ref[2]
     copies = begin_copies([(w_hbm.at[n], w_ref.at[n]) for n in range(4)], sems)
     merged = dot(pick(ids_ref[...]), emb_ref[...]) + dot(got_ref[head], own_ref[...])
-    near = pl.ds(pl.multiple_of(core * 128, 128), 128)
-    far = pl.ds(pl.multiple_of(128 - core * 128, 128), 128)
-    for s, mine, other in ((1, m1, t1), (2, m2, t2), (3, m3, t3)):
-        source = lax.rem(head - s + 4, 4)
-        merged += dot(got_ref[source, :, near], mine[...])
-        merged += dot(got_ref[source, :, far], other[...])
+    near, far, apart = sources(head, core)
+    merged += dot(got_ref[near], m1[...]) + dot(got_ref[far], t1[...])
+    at = pl.ds(pl.multiple_of(core * 128, 128), 128)
+    merged += dot(got_ref[apart, :, at], m2[...])
+    at = pl.ds(pl.multiple_of(128 - core * 128, 128), 128)
+    merged += dot(got_ref[apart, :, at], t2[...])
     rows = 256 + HALO
     token = (
         place * ROWS + head * 256 - HALO + lax.broadcasted_iota(jnp.int32, (rows, D), 0)
@@ -396,10 +400,22 @@
 
 def coarse_more_kernel(which, last, flag_ref, *refs):
     count = 2 * len(which)
+    sems = refs[-1]
+    refs = refs[:-1]
     chunks = refs[:count]
     q_ref, top_in, total_in, acc_in = refs[count : count + 4]
-    out_ref = refs[count + 4] if last else None
+    refs = refs[count + 4 :]
     top_ref, total_ref, acc_ref = refs[-3:]
+    if last:
+        own, m1, m2, t1, t2, target, out_ref = refs[:-3]
+        pairs = place_copies(flag_ref[4], flag_ref[5], own, (m1, m2), (t1, t2), target)
+    else:
+        pairs = []
+        for a, b in zip(refs[:2], refs[2:4]):
+            for part in range(4):
+                at = pl.ds(part * 256, 256)
+                pairs.append((a.at[at], b.at[at]))
+    copies = begin_copies(pairs, sems)
     top_ref[...] = top_in[...]
     total_ref[...] = total_in[...]
     acc_ref[...] = acc_in[...]
@@ -423,19 +439,14 @@
             block = jnp.where(low_lanes, upper, lower).astype(bf16)
             for y in range(4):
                 out_ref[z * 4 + y] = block
+    finish_copies(copies)
 
 
 def feed_kernel(
-    where_ref, heads_ref, short_ref, gain_ref, own, mine, other, up_hbm, down_hbm,
-    part_ref, first_ref, mixed_ref, all_ref, co_ref, up_ref, down_ref, sems,
+    where_ref, heads_ref, short_ref, gain_ref, co_ref, up_ref, down_ref,
+    part_ref, first_ref, mixed_ref, all_ref,
 ):
     head = where_ref[1]
-    pairs = place_copies(head, where_ref[2], own, mine, other, co_ref)
-    for w, w_ref in ((up_hbm, up_ref), (down_hbm, down_ref)):
-        for part in range(4):
-            at = pl.ds(part * 256, 256)
-            pairs.append((w.at[at], w_ref.at[at]))
-    copies = begin_copies(pairs, sems)
     low_lanes = lax.broadcasted_iota(jnp.int32, (1, 128), 1) < 64
     for y in range(4):
         for pair in range(2):
@@ -444,12 +455,10 @@
             at = slice(y * 256 + pair * 128, y * 256 + (pair + 1) * 128)
             mixed_ref[0:128, at] = jnp.where(low_lanes, even, pltpu.roll(odd, 64, 1)).astype(bf16)
             mixed_ref[128:256, at] = jnp.where(low_lanes, pltpu.roll(even, 64, 1), odd).astype(bf16)
-    finish_copies(copies[:7])
     first = short_ref[...].astype(f32) + dot(mixed_ref[...], co_ref[...])
     all_ref[...] = first
     first_ref[...] = all_ref[pl.ds(pl.multiple_of(head * 64, 64), 64), :]
     feed = norm_rows(first, gain_ref[...])
-    finish_copies(copies[7:])
     inner = jax.nn.gelu(dot(feed, up_ref[...])).astype(bf16)
     part_ref[...] = dot(inner, down_ref[...]).astype(bf16).reshape(4, 64, D)
 
@@ -475,20 +484,35 @@
         out_ref[pl.ds(begin, 256), :] = dot(weave, value).astype(bf16)
 
 
-def fetch_half(weight, core):
-    half = lax.dynamic_slice_in_dim(weight, core * 128, 128, 0)
-    return [shift(half, "head", s, 4) for s in range(1, 4)]
+def fetch_rest(weight, core):
+    pairs = []
+    for c, step in ((0, 1), (1, 3)):
+        pairs += [(4 * c + y, 4 * c + (y + step) % 4) for y in range(4)]
+    whole = lax.ppermute(weight, ("core", "head"), pairs)
+    half = shift(lax.dynamic_slice_in_dim(weight, core * 128, 128, 0), "head", 2, 4)
+    return [whole, half]
+
+
+def swap_cores(parts):
+    return [shift(part, "core", 1, 2) for part in parts]
+
+
+def sources(head, core):
+    mine = lax.rem(head + 3 - 2 * core, 4)
+    other = lax.rem(head + 1 + 2 * core, 4)
+    return mine, other, lax.rem(head + 2, 4)
 
 
 def place_copies(head, core, own, mine, other, target):
-    pairs = [(own, target.at[pl.ds(pl.multiple_of(head * 256, 256), 256)])]
-    for s in range(1, 4):
-        source = lax.rem(head - s + 4, 4) * 256
-        at = pl.multiple_of(source + core * 128, 128)
-        pairs.append((mine.at[s - 1], target.at[pl.ds(at, 128)]))
-        at = pl.multiple_of(source + 128 - core * 128, 128)
-        pairs.append((other.at[s - 1], target.at[pl.ds(at, 128)]))
-    return pairs
+    near, far, apart = sources(head, core)
+    halves_at = apart * 256
+    return [
+        (own, target.at[pl.ds(pl.multiple_of(head * 256, 256), 256)]),
+        (mine[0], target.at[pl.ds(pl.multiple_of(near * 256, 256), 256)]),
+        (other[0], target.at[pl.ds(pl.multiple_of(far * 256, 256), 256)]),
+        (mine[1], target.at[pl.ds(pl.multiple_of(halves_at + core * 128, 128), 128)]),
+        (other[1], target.at[pl.ds(pl.multiple_of(halves_at + 128 - core * 128, 128), 128)]),
+    ]
 
 
 def after(value, gate):
@@ -508,8 +532,7 @@
     where = jnp.stack([place, head, core])
 
     prior = later(token_ids, SEQ, 1, 32)
-    last_ids = token_ids[ROWS - HALO :]
-    before = later(last_ids, SEQ, 2, 32)
+    before = later(token_ids, SEQ, 2, 32)[ROWS - HALO :]
     tab = call(
         fine_tables_kernel, "fine_tables", pltpu.HBM((5, 256, SHARE), bf16), [], [],
         [
@@ -517,14 +540,15 @@
             pltpu.VMEM((1, D), f32), pltpu.VMEM((256, D), bf16),
             pltpu.VMEM((3, D, SHARE), bf16), pltpu.SemaphoreType.DMA((9,)),
         ],
-        us=3, out_hbm=True, hbm=[fine_norm[None], embedding, fine_query, fine_key, fine_value],
-    )
-    fine_output_held, _ = after(fine_output, last_ids)
-    out_mine = fetch_half(fine_output_held, core)
+        us=3, hbm=[fine_norm[None], embedding, fine_query, fine_key, fine_value],
+    )
+    own_ids_column = token_ids[:, None]
+    fine_output_held, own_ids_column = after(fine_output, own_ids_column)
+    out_mine = fetch_rest(fine_output_held, core)
     rows = 256 + HALO
     mixed = call(
         fine_kernel, "fine_attention", jax.ShapeDtypeStruct((4, rows, SHARE), bf16),
-        [where], [before[:, None], prior[:, None], token_ids[:, None]],
+        [where], [before[:, None], prior[:, None], own_ids_column],
         [
             pltpu.VMEM((BLOCK + ROWS, SHARE), bf16),
             pltpu.VMEM((KEYS, SHARE), bf16), pltpu.VMEM((KEYS, SHARE), bf16),
@@ -536,7 +560,7 @@
 
     out_mine, mixed = after(out_mine, mixed)
     got = lax.all_to_all(mixed, "head", 0, 0)
-    out_other = [shift(part, "core", 1, 2) for part in out_mine]
+    out_other = swap_cores(out_mine)
     own_ids = lax.dynamic_slice_in_dim(
         jnp.concatenate([prior[ROWS - HALO :], token_ids]), head * 256, rows, 0
     )
@@ -571,46 +595,49 @@
         [*shorts, coarse_norm[None], coarse_query, coarse_key, coarse_value, tables],
     )
 
+    coarse_output_held, packed = after(coarse_output, packed)
+    co_mine = fetch_rest(coarse_output_held, core)
     turned = lax.all_to_all(packed, "z", 0, 0)
-    coarse_output_held, turned = after(coarse_output, turned)
-    co_mine = fetch_half(coarse_output_held, core)
     kv = turned[:, :COARSE_ROWS]
     far = [shift(kv, "core", 1, 2)]
     near = [shift(kv, "x", s, 4) for s in range(1, 4)]
     steps = jnp.arange(4, dtype=jnp.int32)
     flags = ((x_place - steps + 4) % 4 < x_place).astype(jnp.int32) + (steps == 0) * core
+    flags = jnp.concatenate([flags, where[1:]])
     wide = jax.ShapeDtypeStruct((1024, 128), f32)
     q_all, *sums = call(
         coarse_first_kernel, "coarse_first",
         [jax.ShapeDtypeStruct((1024, 128), bf16), wide, wide, wide], [flags], [turned, far[0]],
         us=3, limit=24,
     )
-    near_held, q_all = after(near, q_all)
+    near_held, co_held, q_all = lax.optimization_barrier((near, co_mine, q_all))
     far += [shift(part, "core", 1, 2) for part in near_held]
-    sums = call(
-        functools.partial(coarse_more_kernel, (1, 3), False), "coarse_more", [wide] * 3,
-        [flags], [near[0], far[1], near[2], far[3], q_all, *sums], us=6, limit=24,
-    )
-    wide_sends = call(
+    co_other = swap_cores(co_held)
+    square = jax.ShapeDtypeStruct((D, D), bf16)
+    up_near, down_near, *sums = call(
+        functools.partial(coarse_more_kernel, (1, 3), False), "coarse_more",
+        [square, square, wide, wide, wide],
+        [flags], [near[0], far[1], near[2], far[3], q_all, *sums],
+        [pltpu.SemaphoreType.DMA((8,))], us=6, limit=24, hbm=[ffn_up, ffn_down],
+    )
+    output_near, wide_sends = call(
         functools.partial(coarse_more_kernel, (2,), True), "coarse_last",
-        jax.ShapeDtypeStruct((16, 128, 128), bf16),
-        [flags], [near[1], far[2], q_all, *sums], [pltpu.VMEM((1024, 128), f32)] * 3, us=3, limit=24,
-    )
-    co_mine, wide_sends = after(co_mine, wide_sends)
-    co_mine = jnp.stack(co_mine)
-    co_other = shift(co_mine, "core", 1, 2)
+        [square, jax.ShapeDtypeStruct((16, 128, 128), bf16)],
+        [flags], [near[1], far[2], q_all, *sums],
+        [pltpu.VMEM((1024, 128), f32)] * 3 + [pltpu.SemaphoreType.DMA((5,))],
+        us=3, limit=24, hbm=[coarse_output], free=[*co_mine, *co_other],
+    )
 
     heads_in = lax.all_to_all(wide_sends, ("z", "head"), 0, 0)
     parts, first_own = call(
         feed_kernel, "feed",
         [jax.ShapeDtypeStruct((4, 64, D), bf16), jax.ShapeDtypeStruct((64, D), f32)],
         [where],
-        [heads_in, short, ffn_norm[None]],
+        [heads_in, short, ffn_norm[None], output_near, up_near, down_near],
         [
             pltpu.VMEM((COARSE_ROWS, D), bf16), pltpu.VMEM((COARSE_ROWS, D), f32),
-            *[pltpu.VMEM((D, D), bf16)] * 3, pltpu.SemaphoreType.DMA((15,)),
         ],
-        hbm=[coarse_output, co_mine, co_other, ffn_up, ffn_down], us=4, limit=24,
+        us=4,
     )
     sums = exchange(lambda d: lax.dynamic_index_in_dim(parts, d, 0, keepdims=False), "head", 4)
     second_own = (first_own + sum(t.astype(f32) for t in sums)).astype(bf16)

time: 168 us -> 157 us (0.935)
  blocking collectives: 28.7 us -> 15.6 us
  waiting for transfers between devices: 49 us -> 52.5 us
  starting transfers between devices: 42.1 us -> 44.4 us
    all_to_all x1 -> x0, blocking collectives: 12.1 us -> none  [local(): turned = lax.all_to_all(packed, 'z', 0, 0)]
    all_to_all x0 -> x1, waiting for transfers between devices: none -> 6.99 us  [local(): turned = lax.all_to_all(packed, 'z', 0, 0)]
    ppermute x32 -> x28, starting transfers between devices: 33 us -> 27.8 us  [shift(): lax.ppermute(value, axis, [(i, (i + steps) % count) for i in range(count)])]
    all_to_all x0 -> x1, starting transfers between devices: none -> 4.84 us  [local(): turned = lax.all_to_all(packed, 'z', 0, 0)]
    ppermute x32 -> x28, waiting for transfers between devices: 40.8 us -> 36.9 us  [shift(): lax.ppermute(value, axis, [(i, (i + steps) % count) for i in range(count)])]
    ppermute x0 -> x2, starting transfers between devices: none -> 2.03 us  [fetch_rest(): whole = lax.ppermute(weight, ('core', 'head'), pairs)]
  transfers between devices with their start and end apart: 35 -> 34, of which waited for: 21 -> 21; matrix products, arithmetic and copies ran while one was open for 2% -> 2% of each run, Pallas kernels for 18% -> 18%
where the time goes in v6:
time: 157 us
  waiting for transfers between devices  52.5 us (33%)
  starting transfers between devices  44.4 us (28%)
  Pallas kernels  41.2 us (26%)
  blocking collectives  15.6 us (10%)
  local copies, waits for them, and re-layouts  2.43 us (2%)
    pallas_call x13, Pallas kernels, call(): pl.pallas_call(kernel, out_shape=shapes, in_specs=[smem()] * len(scalars)...  41.2 us
    ppermute x28, waiting for transfers between devices, shift(): lax.ppermute(value, axis, [(i, (i + steps) % count) for i in range(count)])  36.9 us
    ppermute x28, starting transfers between devices, shift(): lax.ppermute(value, axis, [(i, (i + steps) % count) for i in range(count)])  27.8 us
    all_to_all x1, blocking collectives, local(): heads_in = lax.all_to_all(wide_sends, ('z', 'head'), 0, 0)  15.6 us
    all_to_all x1, waiting for transfers between devices, local(): got = lax.all_to_all(mixed, 'head', 0, 0)  8.6 us
    all_to_all x1, waiting for transfers between devices, local(): turned = lax.all_to_all(packed, 'z', 0, 0)  6.99 us
    ppermute x2, starting transfers between devices, later(): lax.ppermute(value, axis, [(i, i + steps) for i in range(count - steps)])  5.65 us
    all_to_all x1, starting transfers between devices, local(): turned = lax.all_to_all(packed, 'z', 0, 0)  4.84 us
  transfers between devices with their start and end apart: 34, of which 21 were waited for; matrix products, arithmetic and copies ran while one was open for 2% of the time, Pallas kernels for 18%

profile of v6, /device:TPU:6, one launch (start us, length us, event | category | flops | bytes accessed | tf_op | source)
XLA Modules:
  0.0 156.9 jit_solution(6745182826004541058)
XLA Ops:
  0.0 1.9 %collective-permute-start = (s32[1024]{0:T(1024)}, s32[1024]{0:T(1024)S(1)}, u32[]{:S(2)}, u32[]{:S(2)}) collective-permute-start(s32[1024]{0:T(1024)} %param.18), channel_id=1, source_target_pairs={{0,4},{4,8},{8,12},{12,16},{16,20},{20,24},{24,28},{28,32},{32,36}... | collective-permute-start | bytes 12296 | tf_op jit(solution)/shard_map/ppermute | solution.py:49
  1.9 3.7 %collective-permute-start.3 = (s32[1024]{0:T(1024)}, s32[1024]{0:T(1024)S(1)}, u32[]{:S(2)}, u32[]{:S(2)}) collective-permute-start(s32[1024]{0:T(1024)} %param.18), channel_id=1, source_target_pairs={{0,8},{4,12},{8,16},{12,20},{16,24},{20,28},{24,32},{28,36},{32,40... | collective-permute-start | bytes 12296 | tf_op jit(solution)/shard_map/ppermute | solution.py:49
  5.7 1.6 %collective-permute-start.1 = (bf16[256,1024]{1,0:T(8,128)(2,1)}, bf16[256,1024]{1,0:T(8,128)(2,1)S(1)}, u32[]{:S(2)}, u32[]{:S(2)}) collective-permute-start(bf16[256,1024]{1,0:T(8,128)(2,1)} %own_ref.1), channel_id=1, source_target_pairs={{0,1},{1,2},{2,3},{3,0},{4,7},{5,4},{6,5},{7,6},{8,9},{9,10},{10,1... | collective-permute-start | bytes 1572872 | tf_op jit(solution)/shard_map/ppermute | solution.py:491
  7.3 1.0 constant_dynamic-slice_fusion.1
  8.3 3.0 %collective-permute-start.2 = (bf16[128,1024]{1,0:T(8,128)(2,1)S(1)}, bf16[128,1024]{1,0:T(8,128)(2,1)S(1)}, u32[]{:S(2)}, u32[]{:S(2)}) collective-permute-start(bf16[128,1024]{1,0:T(8,128)(2,1)S(1)} %constant_dynamic-slice_fusion.1), channel_id=1, source_target_pairs={{0,2},{1,3},{2,0},{3,1},{4,6},{5,7},{6,4},{7,5},{8,10},{9,11},{10,... | collective-permute-start | bytes 786440 | tf_op jit(solution)/shard_map/ppermute | solution.py:45
  11.3 3.1 %fine_tables.1.tab_hbm = bf16[5,256,256]{2,1,0:T(8,128)(2,1)} custom-call(f32[1,1024]{1,0:T(1,128)} %bitcast.35, bf16[256,1024]{1,0:T(8,128)(2,1)} %emb_ref.1, bf16[1024,256]{1,0:T(8,128)(2,1)} %wq_hbm.1, bf16[1024,256]{1,0:T(8,128)(2,1)} %wk_hbm.1, bf16[1024,256]{1,0:T(8,128)(2,1)} %wv_hbm.1), custom_call_target="tpu_custom_call" | custom-call | flops 3000000000 | bytes 6000000 | tf_op jit(solution)/shard_map/fine_tables/pallas_call | solution.py:246
  14.5 0.2 copy.22.own_ref
  14.8 0.2 copy.21.prior_ref
  15.2 14.5 %fine_attention.1 = bf16[4,272,256]{2,1,0:T(8,128)(2,1)} custom-call(s32[3]{0:T(128)S(1)} %pad_add_fusion.where_ref, s32[16,1]{1,0:T(8,128)S(1)} %copy.20.before_ref, s32[1024,1]{1,0:T(8,128)S(1)} %copy.21.prior_ref, s32[1024,1]{1,0:T(8,128)S(1)} %copy.22.own_ref, bf16[5,256,256]{2,1,0:T(8,128)(2,1)} %fine_tables.1.tab_hbm, ...), custom_call_target="tpu_custom_call" | custom-call | flops 12000000000 | bytes 24000000 | tf_op jit(solution)/shard_map/fine_attention/pallas_call | solution.py:246
  29.8 4.1 %all-to-all-start = ((bf16[4,272,256]{2,1,0:T(8,128)(2,1)}), bf16[4,272,256]{2,1,0:T(8,128)(2,1)S(1)}, u32[]{:S(2)}, u32[]{:S(2)}) async-start(bf16[4,272,256]{2,1,0:T(8,128)(2,1)} %fine_attention.1), calls=%async_computation | async-start | bytes 1114112 | tf_op jit(solution)/shard_map/all_to_all | solution.py:562
  34.1 1.3 collective-permute-done.5.t2
  35.4 8.6 %all-to-all-done.got_ref = bf16[4,272,256]{2,1,0:T(8,128)(2,1)S(1)} async-done(((bf16[4,272,256]{2,1,0:T(8,128)(2,1)}), bf16[4,272,256]{2,1,0:T(8,128)(2,1)S(1)}, u32[]{:S(2)}, u32[]{:S(2)}) %all-to-all-start) | async-done | bytes 557088 | tf_op jit(solution)/shard_map/all_to_all | solution.py:562
  44.0 2.5 %fine_rows.1 = (bf16[4,272,256]{2,1,0:T(8,128)(2,1)S(1)}, bf16[4,256,1024]{2,1,0:T(8,128)(2,1)S(1)}) custom-call(s32[3]{0:T(128)S(1)} %pad_add_fusion.where_ref, s32[272,1]{1,0:T(8,128)S(1)} %broadcast_in_dim.28.ids_ref, bf16[256,1024]{1,0:T(8,128)(2,1)S(1)} %copy-done.1, bf16[4,272,256]{2,1,0:T(8,128)(2,1)S(1)} %all-to-all-done.got_ref, ...), custom_call_target="tpu_custom_call" | custom-call | flops 2000000000 | bytes 4000000 | tf_op jit(solution)/shard_map/fine_rows/pallas_call | solution.py:246
  46.6 0.6 collective-permute-start.6
  47.2 2.1 %collective-permute-start.8 = (bf16[272,256]{1,0:T(8,128)(2,1)S(1)}, bf16[272,256]{1,0:T(8,128)(2,1)S(1)}, u32[]{:S(2)}, u32[]{:S(2)}) collective-permute-start(bf16[272,256]{1,0:T(8,128)(2,1)S(1)} %get-tuple-element.67), channel_id=1, source_target_pairs={{0,2},{1,3},{2,0},{3,1},{4,6},{5,7},{6,4},{7,5},{8,10},{9,11},{10,... | collective-permute-start | bytes 417800 | tf_op jit(solution)/shard_map/ppermute | solution.py:45
  49.3 0.7 collective-permute-start.10
  50.0 5.4 %collective-permute-done.6.group_ref.b1 = bf16[272,256]{1,0:T(8,128)(2,1)S(1)} collective-permute-done((bf16[272,256]{1,0:T(8,128)(2,1)S(1)}, bf16[272,256]{1,0:T(8,128)(2,1)S(1)}, u32[]{:S(2)}, u32[]{:S(2)}) %collective-permute-start.6) | collective-permute-done | bytes 139296 | tf_op jit(solution)/shard_map/ppermute | solution.py:45
  55.4 0.5 short_part.5
  56.0 0.5 short_part.6
  56.5 0.6 collective-permute-start.9
  57.2 0.5 short_part.7
  57.6 1.6 %collective-permute-start.11 = (bf16[64,1024]{1,0:T(8,128)(2,1)S(1)}, bf16[64,1024]{1,0:T(8,128)(2,1)S(1)}, u32[]{:S(2)}, u32[]{:S(2)}) collective-permute-start(bf16[64,1024]{1,0:T(8,128)(2,1)S(1)} %short_part.7), channel_id=1, source_target_pairs={{0,1},{1,2},{2,3},{3,0},{4,5},{5,6},{6,7},{7,4},{8,9},{9,10},{10,1... | collective-permute-start | bytes 393224 | tf_op jit(solution)/shard_map/ppermute | solution.py:45
  59.3 0.5 short_part.4
  59.8 1.2 collective-permute-done.7
  61.0 2.5 %collective-permute-done.9 = bf16[64,1024]{1,0:T(8,128)(2,1)S(1)} collective-permute-done((bf16[64,1024]{1,0:T(8,128)(2,1)S(1)}, bf16[64,1024]{1,0:T(8,128)(2,1)S(1)}, u32[]{:S(2)}, u32[]{:S(2)}) %collective-permute-start.9) | collective-permute-done | bytes 131104 | tf_op jit(solution)/shard_map/ppermute | solution.py:45
  63.4 1.6 %collective-permute-done.11 = bf16[64,1024]{1,0:T(8,128)(2,1)S(1)} collective-permute-done((bf16[64,1024]{1,0:T(8,128)(2,1)S(1)}, bf16[64,1024]{1,0:T(8,128)(2,1)S(1)}, u32[]{:S(2)}, u32[]{:S(2)}) %collective-permute-start.11) | collective-permute-done | bytes 131104 | tf_op jit(solution)/shard_map/ppermute | solution.py:45
  65.2 4.3 %collective-permute-start.13 = (bf16[64,1024]{1,0:T(8,128)(2,1)S(1)}, bf16[64,1024]{1,0:T(8,128)(2,1)S(1)}, u32[]{:S(2)}, u32[]{:S(2)}) collective-permute-start(bf16[64,1024]{1,0:T(8,128)(2,1)S(1)} %add_convert_fusion.s0), channel_id=1, source_target_pairs={{0,2},{1,3},{2,0},{3,1},{4,6},{5,7},{6,4},{7,5},{8,10},{9,11},{10,... | collective-permute-start | bytes 393224 | tf_op jit(solution)/shard_map/ppermute | solution.py:45
  69.5 0.1 collective-permute-start.14
  69.6 1.7 %collective-permute-done.12.s1 = bf16[64,1024]{1,0:T(8,128)(2,1)S(1)} collective-permute-done((bf16[64,1024]{1,0:T(8,128)(2,1)S(1)}, bf16[64,1024]{1,0:T(8,128)(2,1)S(1)}, u32[]{:S(2)}, u32[]{:S(2)}) %collective-permute-start.12) | collective-permute-done | bytes 131104 | tf_op jit(solution)/shard_map/ppermute | solution.py:45
  71.4 2.5 %collective-permute-done.13.s2 = bf16[64,1024]{1,0:T(8,128)(2,1)S(1)} collective-permute-done((bf16[64,1024]{1,0:T(8,128)(2,1)S(1)}, bf16[64,1024]{1,0:T(8,128)(2,1)S(1)}, u32[]{:S(2)}, u32[]{:S(2)}) %collective-permute-start.13) | collective-permute-done | bytes 131104 | tf_op jit(solution)/shard_map/ppermute | solution.py:45
  73.8 0.6 collective-permute-done.14.s3
  74.5 2.3 %coarse_pack.1 = (bf16[4,384,128]{2,1,0:T(8,128)(2,1)}, bf16[256,1024]{1,0:T(8,128)(2,1)S(1)}) custom-call(s32[3]{0:T(128)S(1)} %pad_add_fusion.where_ref, bf16[64,1024]{1,0:T(8,128)(2,1)S(1)} %add_convert_fusion.s0, bf16[64,1024]{1,0:T(8,128)(2,1)S(1)} %collective-permute-done.12.s1, bf16[64,1024]{1,0:T(8,128)(2,1)S(1)} %collective-permute-done.13.s2, ...), custom_call_target="tpu_custom_call" | custom-call | flops 2000000000 | bytes 4000000 | tf_op jit(solution)/shard_map/coarse_pack/pallas_call | solution.py:246
  76.8 4.8 %all-to-all-start.1 = ((bf16[4,384,128]{2,1,0:T(8,128)(2,1)}), bf16[4,384,128]{2,1,0:T(8,128)(2,1)S(1)}, u32[]{:S(2)}, u32[]{:S(2)}) async-start(bf16[4,384,128]{2,1,0:T(8,128)(2,1)} %get-tuple-element.43), calls=%async_computation.1 | async-start | bytes 786432 | tf_op jit(solution)/shard_map/all_to_all | solution.py:600
  81.6 0.4 collective-permute-start.18
  82.0 7.0 %all-to-all-done.1.turned_ref = bf16[4,384,128]{2,1,0:T(8,128)(2,1)S(1)} async-done(((bf16[4,384,128]{2,1,0:T(8,128)(2,1)}), bf16[4,384,128]{2,1,0:T(8,128)(2,1)S(1)}, u32[]{:S(2)}, u32[]{:S(2)}) %all-to-all-start.1) | async-done | bytes 393248 | tf_op jit(solution)/shard_map/all_to_all | solution.py:600
  89.2 1.6 %collective-permute-start.19 = (bf16[128,1024]{1,0:T(8,128)(2,1)S(1)}, bf16[128,1024]{1,0:T(8,128)(2,1)S(1)}, u32[]{:S(2)}, u32[]{:S(2)}) collective-permute-start(bf16[128,1024]{1,0:T(8,128)(2,1)S(1)} %constant_dynamic-slice_fusion), channel_id=1, source_target_pairs={{0,2},{1,3},{2,0},{3,1},{4,6},{5,7},{6,4},{7,5},{8,10},{9,11},{10,... | collective-permute-start | bytes 786440 | tf_op jit(solution)/shard_map/ppermute | solution.py:45
  90.8 1.9 %collective-permute-start.15 = (bf16[4,256,128]{2,1,0:T(8,128)(2,1)S(1)}, bf16[4,256,128]{2,1,0:T(8,128)(2,1)S(1)}, u32[]{:S(2)}, u32[]{:S(2)}) collective-permute-start(bf16[4,256,128]{2,1,0:T(8,128)(2,1)S(1)} %slice.14), channel_id=1, source_target_pairs={{0,16},{8,24},{16,0},{24,8},{1,17},{9,25},{17,1},{25,9},{2,18},{10... | collective-permute-start | bytes 786440 | tf_op jit(solution)/shard_map/ppermute | solution.py:45
  92.7 1.8 %collective-permute-start.16 = (bf16[4,256,128]{2,1,0:T(8,128)(2,1)S(1)}, bf16[4,256,128]{2,1,0:T(8,128)(2,1)S(1)}, u32[]{:S(2)}, u32[]{:S(2)}) collective-permute-start(bf16[4,256,128]{2,1,0:T(8,128)(2,1)S(1)} %slice.14), channel_id=1, source_target_pairs={{0,8},{8,16},{16,24},{24,0},{1,9},{9,17},{17,25},{25,1},{2,10},{10... | collective-permute-start | bytes 786440 | tf_op jit(solution)/shard_map/ppermute | solution.py:45
  94.5 0.2 collective-permute-start.17
  94.7 2.3 %coarse_first.1 = (bf16[1024,128]{1,0:T(8,128)(2,1)S(1)}, f32[1024,128]{1,0:T(8,128)S(1)}, f32[1024,128]{1,0:T(8,128)S(1)}, f32[1024,128]{1,0:T(8,128)S(1)}) custom-call(s32[6]{0:T(128)S(1)} %pad_add_fusion.1.flag_ref, bf16[4,384,128]{2,1,0:T(8,128)(2,1)S(1)} %all-to-all-done.1.turned_ref, bf16[4,256,128]{2,1,0:T(8,128)(2,1)S(1)} %collective-permute-done.20.far_ref), custom_call_target="tpu_custom_call" | custom-call | flops 3000000000 | bytes 6000000 | tf_op jit(solution)/shard_map/coarse_first/pallas_call | solution.py:246
  97.1 2.5 %collective-permute-done.19.refs_8_ = bf16[128,1024]{1,0:T(8,128)(2,1)S(1)} collective-permute-done((bf16[128,1024]{1,0:T(8,128)(2,1)S(1)}, bf16[128,1024]{1,0:T(8,128)(2,1)S(1)}, u32[]{:S(2)}, u32[]{:S(2)}) %collective-permute-start.19) | collective-permute-done | bytes 262176 | tf_op jit(solution)/shard_map/ppermute | solution.py:45
  99.5 2.0 %collective-permute-done.15.refs_0_ = bf16[4,256,128]{2,1,0:T(8,128)(2,1)S(1)} collective-permute-done((bf16[4,256,128]{2,1,0:T(8,128)(2,1)S(1)}, bf16[4,256,128]{2,1,0:T(8,128)(2,1)S(1)}, u32[]{:S(2)}, u32[]{:S(2)}) %collective-permute-start.15) | collective-permute-done | bytes 262176 | tf_op jit(solution)/shard_map/ppermute | solution.py:45
  101.5 2.8 %collective-permute-done.16.refs_0_ = bf16[4,256,128]{2,1,0:T(8,128)(2,1)S(1)} collective-permute-done((bf16[4,256,128]{2,1,0:T(8,128)(2,1)S(1)}, bf16[4,256,128]{2,1,0:T(8,128)(2,1)S(1)}, u32[]{:S(2)}, u32[]{:S(2)}) %collective-permute-start.16) | collective-permute-done | bytes 262176 | tf_op jit(solution)/shard_map/ppermute | solution.py:45
  104.4 2.0 %collective-permute-done.17.refs_2_ = bf16[4,256,128]{2,1,0:T(8,128)(2,1)S(1)} collective-permute-done((bf16[4,256,128]{2,1,0:T(8,128)(2,1)S(1)}, bf16[4,256,128]{2,1,0:T(8,128)(2,1)S(1)}, u32[]{:S(2)}, u32[]{:S(2)}) %collective-permute-start.17) | collective-permute-done | bytes 262176 | tf_op jit(solution)/shard_map/ppermute | solution.py:45
  106.4 0.5 collective-permute-start.23
  106.9 0.5 collective-permute-start.21
  107.4 0.5 collective-permute-done.22.refs_1_
  107.9 0.4 collective-permute-done.23.refs_3_
  108.3 5.7 %coarse_more.1 = (bf16[1024,1024]{1,0:T(8,128)(2,1)S(1)}, bf16[1024,1024]{1,0:T(8,128)(2,1)S(1)}, f32[1024,128]{1,0:T(8,128)S(1)}, f32[1024,128]{1,0:T(8,128)S(1)}, f32[1024,128]{1,0:T(8,128)S(1)}) custom-call(s32[6]{0:T(128)S(1)} %pad_add_fusion.1.flag_ref, bf16[4,256,128]{2,1,0:T(8,128)(2,1)S(1)} %collective-permute-done.16.refs_0_, ...), custom_call_target="tpu_custom_call" | custom-call | flops 6000000000 | bytes 12000000 | tf_op jit(solution)/shard_map/coarse_more/pallas_call | solution.py:246
  114.1 3.2 %coarse_last.1 = (bf16[1024,1024]{1,0:T(8,128)(2,1)S(1)}, bf16[16,128,128]{2,1,0:T(8,128)(2,1)S(1)}) custom-call(s32[6]{0:T(128)S(1)} %pad_add_fusion.1.flag_ref, bf16[4,256,128]{2,1,0:T(8,128)(2,1)S(1)} %collective-permute-done.15.refs_0_, bf16[4,256,128]{2,1,0:T(8,128)(2,1)S(1)} %collective-permute-done.21.refs_1_, ...), custom_call_target="tpu_custom_call" | custom-call | flops 3000000000 | bytes 6000000 | tf_op jit(solution)/shard_map/coarse_last/pallas_call | solution.py:246
  117.3 15.6 %all_to_all.15.heads_ref = bf16[16,128,128]{2,1,0:T(8,128)(2,1)S(1)} all-to-all(bf16[16,128,128]{2,1,0:T(8,128)(2,1)S(1)} %get-tuple-element.58), channel_id=1, replica_groups=mesh['z'=4,'x'=4,'core'=2,'head'=4] {'z','head'}, dimensions={0} | all-to-all | bytes 1048576 | tf_op jit(solution)/shard_map/all_to_all | solution.py:631
  133.0 2.9 %feed.1 = (bf16[4,64,1024]{2,1,0:T(8,128)(2,1)S(1)}, f32[64,1024]{1,0:T(8,128)S(1)}) custom-call(s32[3]{0:T(128)S(1)} %pad_add_fusion.where_ref, bf16[16,128,128]{2,1,0:T(8,128)(2,1)S(1)} %all_to_all.15.heads_ref, bf16[256,1024]{1,0:T(8,128)(2,1)S(1)} %get-tuple-element.59.short_ref, f32[1,1024]{1,0:T(1,128)S(1)} %bitcast.31, ...), custom_call_target="tpu_custom_call" | custom-call | flops 4000000000 | bytes 8000000 | tf_op jit(solution)/shard_map/feed/pallas_call | solution.py:246
  135.9 0.6 collective-permute-start.26
  136.5 1.4 collective-permute-start.27
  137.9 1.5 collective-permute-start.28
  139.4 4.7 %collective-permute-done.26 = bf16[64,1024]{1,0:T(8,128)(2,1)S(1)} collective-permute-done((bf16[64,1024]{1,0:T(8,128)(2,1)S(1)}, bf16[64,1024]{1,0:T(8,128)(2,1)S(1)}, u32[]{:S(2)}, u32[]{:S(2)}) %collective-permute-start.26) | collective-permute-done | bytes 131104 | tf_op jit(solution)/shard_map/ppermute | solution.py:45
  144.1 0.6 collective-permute-done.28
  144.8 1.1 collective-permute-start.29
  146.0 3.0 %collective-permute-start.30 = (bf16[64,1024]{1,0:T(8,128)(2,1)S(1)}, bf16[64,1024]{1,0:T(8,128)(2,1)S(1)}, u32[]{:S(2)}, u32[]{:S(2)}) collective-permute-start(bf16[64,1024]{1,0:T(8,128)(2,1)S(1)} %fusion.3.s0), channel_id=1, source_target_pairs={{0,2},{1,3},{2,0},{3,1},{4,6},{5,7},{6,4},{7,5},{8,10},{9,11},{10,... | collective-permute-start | bytes 393224 | tf_op jit(solution)/shard_map/ppermute | solution.py:45
  149.0 0.2 collective-permute-start.31
  149.2 0.5 copy.24
  149.7 2.8 %collective-permute-done.29.s1 = bf16[64,1024]{1,0:T(8,128)(2,1)S(1)} collective-permute-done((bf16[64,1024]{1,0:T(8,128)(2,1)S(1)}, bf16[64,1024]{1,0:T(8,128)(2,1)S(1)}, u32[]{:S(2)}, u32[]{:S(2)}) %collective-permute-start.29) | collective-permute-done | bytes 131104 | tf_op jit(solution)/shard_map/ppermute | solution.py:45
  152.5 1.7 %collective-permute-done.30.s2 = bf16[64,1024]{1,0:T(8,128)(2,1)S(1)} collective-permute-done((bf16[64,1024]{1,0:T(8,128)(2,1)S(1)}, bf16[64,1024]{1,0:T(8,128)(2,1)S(1)}, u32[]{:S(2)}, u32[]{:S(2)}) %collective-permute-start.30) | collective-permute-done | bytes 131104 | tf_op jit(solution)/shard_map/ppermute | solution.py:45
  154.3 2.7 %final.1 = bf16[1024,256]{1,0:T(8,128)(2,1)} custom-call(s32[3]{0:T(128)S(1)} %pad_add_fusion.where_ref, bf16[64,1024]{1,0:T(8,128)(2,1)S(1)} %fusion.3.s0, bf16[64,1024]{1,0:T(8,128)(2,1)S(1)} %collective-permute-done.29.s1, bf16[64,1024]{1,0:T(8,128)(2,1)S(1)} %collective-permute-done.30.s2, bf16[64,1024]{1,0:T(8,128)(2,1)S(1)} %collective-permute-done.31.s3, ...), custom_call_target="tpu_custom_call" | custom-call | flops 2000000000 | bytes 4000000 | tf_op jit(solution)/shard_map/final/pallas_call | solution.py:246
  (58 shorter events, 1.4 us)
Async XLA Ops:
  0.0 14.8 %collective-permute-start = (s32[1024]{0:T(1024)}, s32[1024]{0:T(1024)S(1)}, u32[]{:S(2)}, u32[]{:S(2)}) collective-permute-start(s32[1024]{0:T(1024)} %param.18), channel_id=1, source_target_pairs={{0,4},{4,8},{8,12},{12,16},{16,20},{20,24},{24,28},{28,32},{32,36}... | collective-permute-start | bytes 12296 | tf_op jit(solution)/shard_map/ppermute | solution.py:49
  1.9 13.1 %collective-permute-start.3 = (s32[1024]{0:T(1024)}, s32[1024]{0:T(1024)S(1)}, u32[]{:S(2)}, u32[]{:S(2)}) collective-permute-start(s32[1024]{0:T(1024)} %param.18), channel_id=1, source_target_pairs={{0,8},{4,12},{8,16},{12,20},{16,24},{20,28},{24,32},{28,36},{32,40... | collective-permute-start | bytes 12296 | tf_op jit(solution)/shard_map/ppermute | solution.py:49
  5.7 24.0 %collective-permute-start.1 = (bf16[256,1024]{1,0:T(8,128)(2,1)}, bf16[256,1024]{1,0:T(8,128)(2,1)S(1)}, u32[]{:S(2)}, u32[]{:S(2)}) collective-permute-start(bf16[256,1024]{1,0:T(8,128)(2,1)} %own_ref.1), channel_id=1, source_target_pairs={{0,1},{1,2},{2,3},{3,0},{4,7},{5,4},{6,5},{7,6},{8,9},{9,10},{10,1... | collective-permute-start | bytes 1572872 | tf_op jit(solution)/shard_map/ppermute | solution.py:491
  8.3 21.3 %collective-permute-start.2 = (bf16[128,1024]{1,0:T(8,128)(2,1)S(1)}, bf16[128,1024]{1,0:T(8,128)(2,1)S(1)}, u32[]{:S(2)}, u32[]{:S(2)}) collective-permute-start(bf16[128,1024]{1,0:T(8,128)(2,1)S(1)} %constant_dynamic-slice_fusion.1), channel_id=1, source_target_pairs={{0,2},{1,3},{2,0},{3,1},{4,6},{5,7},{6,4},{7,5},{8,10},{9,11},{10,... | collective-permute-start | bytes 786440 | tf_op jit(solution)/shard_map/ppermute | solution.py:45
  11.3 3.2 %copy-start.10 = (s32[1024]{0:T(1024)S(1)}, s32[1024]{0:T(1024)}, u32[]{:S(2)}) copy-start(s32[1024]{0:T(1024)} %param.18) | copy-start | bytes 12292
  15.2 28.8 %copy-start = (bf16[256,1024]{1,0:T(8,128)(2,1)S(1)}, bf16[256,1024]{1,0:T(8,128)(2,1)}, u32[]{:S(2)}) copy-start(bf16[256,1024]{1,0:T(8,128)(2,1)} %own_ref.1) | copy-start | bytes 1572868
  15.2 28.8 %copy-start.1 = (bf16[256,1024]{1,0:T(8,128)(2,1)S(1)}, bf16[256,1024]{1,0:T(8,128)(2,1)}, u32[]{:S(2)}) copy-start(bf16[256,1024]{1,0:T(8,128)(2,1)} %emb_ref.1) | copy-start | bytes 1572868
  29.7 14.3 %collective-permute-start.4 = (bf16[256,1024]{1,0:T(8,128)(2,1)S(1)}, bf16[256,1024]{1,0:T(8,128)(2,1)S(1)}, u32[]{:S(2)}, u32[]{:S(2)}) collective-permute-start(bf16[256,1024]{1,0:T(8,128)(2,1)S(1)} %collective-permute-done.1.m1), channel_id=1, source_target_pairs={{0,4},{4,0},{1,5},{5,1},{2,6},{6,2},{3,7},{7,3},{8,12},{12,8},{9,1... | collective-permute-start | bytes 1572872 | tf_op jit(solution)/shard_map/ppermute | solution.py:45
  29.8 14.2 %all-to-all-start = ((bf16[4,272,256]{2,1,0:T(8,128)(2,1)}), bf16[4,272,256]{2,1,0:T(8,128)(2,1)S(1)}, u32[]{:S(2)}, u32[]{:S(2)}) async-start(bf16[4,272,256]{2,1,0:T(8,128)(2,1)} %fine_attention.1), calls=%async_computation | async-start | bytes 1114112 | tf_op jit(solution)/shard_map/all_to_all | solution.py:562
  33.8 1.5 collective-permute-start.5
  46.6 8.8 %collective-permute-start.6 = (bf16[272,256]{1,0:T(8,128)(2,1)S(1)}, bf16[272,256]{1,0:T(8,128)(2,1)S(1)}, u32[]{:S(2)}, u32[]{:S(2)}) collective-permute-start(bf16[272,256]{1,0:T(8,128)(2,1)S(1)} %get-tuple-element.68), channel_id=1, source_target_pairs={{0,1},{1,2},{2,3},{3,0},{4,5},{5,6},{6,7},{7,4},{8,9},{9,10},{10,1... | collective-permute-start | bytes 417800 | tf_op jit(solution)/shard_map/ppermute | solution.py:45
  47.2 8.8 %collective-permute-start.8 = (bf16[272,256]{1,0:T(8,128)(2,1)S(1)}, bf16[272,256]{1,0:T(8,128)(2,1)S(1)}, u32[]{:S(2)}, u32[]{:S(2)}) collective-permute-start(bf16[272,256]{1,0:T(8,128)(2,1)S(1)} %get-tuple-element.67), channel_id=1, source_target_pairs={{0,2},{1,3},{2,0},{3,1},{4,6},{5,7},{6,4},{7,5},{8,10},{9,11},{10,... | collective-permute-start | bytes 417800 | tf_op jit(solution)/shard_map/ppermute | solution.py:45
  49.3 7.9 %collective-permute-start.10 = (bf16[272,256]{1,0:T(8,128)(2,1)S(1)}, bf16[272,256]{1,0:T(8,128)(2,1)S(1)}, u32[]{:S(2)}, u32[]{:S(2)}) collective-permute-start(bf16[272,256]{1,0:T(8,128)(2,1)S(1)} %get-tuple-element.66), channel_id=1, source_target_pairs={{0,3},{1,0},{2,1},{3,2},{4,7},{5,4},{6,5},{7,6},{8,11},{9,8},{10,9... | collective-permute-start | bytes 417800 | tf_op jit(solution)/shard_map/ppermute | solution.py:45
  55.9 5.0 %collective-permute-start.7 = (bf16[64,1024]{1,0:T(8,128)(2,1)S(1)}, bf16[64,1024]{1,0:T(8,128)(2,1)S(1)}, u32[]{:S(2)}, u32[]{:S(2)}) collective-permute-start(bf16[64,1024]{1,0:T(8,128)(2,1)S(1)} %short_part.5), channel_id=1, source_target_pairs={{0,3},{1,0},{2,1},{3,2},{4,7},{5,4},{6,5},{7,6},{8,11},{9,8},{10,9... | collective-permute-start | bytes 393224 | tf_op jit(solution)/shard_map/ppermute | solution.py:45
  56.5 6.9 %collective-permute-start.9 = (bf16[64,1024]{1,0:T(8,128)(2,1)S(1)}, bf16[64,1024]{1,0:T(8,128)(2,1)S(1)}, u32[]{:S(2)}, u32[]{:S(2)}) collective-permute-start(bf16[64,1024]{1,0:T(8,128)(2,1)S(1)} %short_part.6), channel_id=1, source_target_pairs={{0,2},{1,3},{2,0},{3,1},{4,6},{5,7},{6,4},{7,5},{8,10},{9,11},{10,... | collective-permute-start | bytes 393224 | tf_op jit(solution)/shard_map/ppermute | solution.py:45
  57.6 7.4 %collective-permute-start.11 = (bf16[64,1024]{1,0:T(8,128)(2,1)S(1)}, bf16[64,1024]{1,0:T(8,128)(2,1)S(1)}, u32[]{:S(2)}, u32[]{:S(2)}) collective-permute-start(bf16[64,1024]{1,0:T(8,128)(2,1)S(1)} %short_part.7), channel_id=1, source_target_pairs={{0,1},{1,2},{2,3},{3,0},{4,5},{5,6},{6,7},{7,4},{8,9},{9,10},{10,1... | collective-permute-start | bytes 393224 | tf_op jit(solution)/shard_map/ppermute | solution.py:45
  59.3 15.2 %copy-start.2 = (bf16[1024,256]{1,0:T(8,128)(2,1)S(1)}, bf16[1024,256]{1,0:T(8,128)(2,1)}, u32[]{:S(2)}) copy-start(bf16[1024,256]{1,0:T(8,128)(2,1)} %wq_ref.1) | copy-start | bytes 1572868
  59.3 15.2 %copy-start.3 = (bf16[1024,256]{1,0:T(8,128)(2,1)S(1)}, bf16[1024,256]{1,0:T(8,128)(2,1)}, u32[]{:S(2)}) copy-start(bf16[1024,256]{1,0:T(8,128)(2,1)} %wk_ref.1) | copy-start | bytes 1572868
  59.3 15.2 %copy-start.4 = (bf16[1024,256]{1,0:T(8,128)(2,1)S(1)}, bf16[1024,256]{1,0:T(8,128)(2,1)}, u32[]{:S(2)}) copy-start(bf16[1024,256]{1,0:T(8,128)(2,1)} %wv_ref.1) | copy-start | bytes 1572868
  59.3 15.2 %copy-start.5 = (f32[1024]{0:T(1024)S(1)}, f32[1024]{0:T(1024)}, u32[]{:S(2)}) copy-start(f32[1024]{0:T(1024)} %param.26) | copy-start | bytes 12292
  59.3 15.2 %copy-start.7 = (f32[576,128]{1,0:T(8,128)S(1)}, f32[576,128]{1,0:T(8,128)}, u32[]{:S(2)}) copy-start(f32[576,128]{1,0:T(8,128)} %constant.90.clone.turn_hbm.turn_ref) | copy-start | bytes 884740
  65.1 6.2 %collective-permute-start.12 = (bf16[64,1024]{1,0:T(8,128)(2,1)S(1)}, bf16[64,1024]{1,0:T(8,128)(2,1)S(1)}, u32[]{:S(2)}, u32[]{:S(2)}) collective-permute-start(bf16[64,1024]{1,0:T(8,128)(2,1)S(1)} %add_convert_fusion.s0), channel_id=1, source_target_pairs={{0,1},{1,2},{2,3},{3,0},{4,5},{5,6},{6,7},{7,4},{8,9},{9,10},{10,1... | collective-permute-start | bytes 393224 | tf_op jit(solution)/shard_map/ppermute | solution.py:45
  65.2 8.6 %collective-permute-start.13 = (bf16[64,1024]{1,0:T(8,128)(2,1)S(1)}, bf16[64,1024]{1,0:T(8,128)(2,1)S(1)}, u32[]{:S(2)}, u32[]{:S(2)}) collective-permute-start(bf16[64,1024]{1,0:T(8,128)(2,1)S(1)} %add_convert_fusion.s0), channel_id=1, source_target_pairs={{0,2},{1,3},{2,0},{3,1},{4,6},{5,7},{6,4},{7,5},{8,10},{9,11},{10,... | collective-permute-start | bytes 393224 | tf_op jit(solution)/shard_map/ppermute | solution.py:45
  69.5 5.0 %collective-permute-start.14 = (bf16[64,1024]{1,0:T(8,128)(2,1)S(1)}, bf16[64,1024]{1,0:T(8,128)(2,1)S(1)}, u32[]{:S(2)}, u32[]{:S(2)}) collective-permute-start(bf16[64,1024]{1,0:T(8,128)(2,1)S(1)} %add_convert_fusion.s0), channel_id=1, source_target_pairs={{0,3},{1,0},{2,1},{3,2},{4,7},{5,4},{6,5},{7,6},{8,11},{9,8},{10,9... | collective-permute-start | bytes 393224 | tf_op jit(solution)/shard_map/ppermute | solution.py:45
  74.5 7.2 %copy-start.9 = (bf16[256,1024]{1,0:T(8,128)(2,1)S(1)}, bf16[256,1024]{1,0:T(8,128)(2,1)}, u32[]{:S(2)}) copy-start(bf16[256,1024]{1,0:T(8,128)(2,1)} %refs_6_.1) | copy-start | bytes 1572868
  76.8 12.2 %all-to-all-start.1 = ((bf16[4,384,128]{2,1,0:T(8,128)(2,1)}), bf16[4,384,128]{2,1,0:T(8,128)(2,1)S(1)}, u32[]{:S(2)}, u32[]{:S(2)}) async-start(bf16[4,384,128]{2,1,0:T(8,128)(2,1)} %get-tuple-element.43), calls=%async_computation.1 | async-start | bytes 786432 | tf_op jit(solution)/shard_map/all_to_all | solution.py:600
  81.6 17.9 %collective-permute-start.18 = (bf16[256,1024]{1,0:T(8,128)(2,1)S(1)}, bf16[256,1024]{1,0:T(8,128)(2,1)S(1)}, u32[]{:S(2)}, u32[]{:S(2)}) collective-permute-start(bf16[256,1024]{1,0:T(8,128)(2,1)S(1)} %copy-done.9), channel_id=1, source_target_pairs={{0,1},{1,2},{2,3},{3,0},{4,7},{5,4},{6,5},{7,6},{8,9},{9,10},{10,1... | collective-permute-start | bytes 1572872 | tf_op jit(solution)/shard_map/ppermute | solution.py:491
  89.0 5.5 %collective-permute-start.20 = (bf16[4,256,128]{2,1,0:T(8,128)(2,1)S(1)}, bf16[4,256,128]{2,1,0:T(8,128)(2,1)S(1)}, u32[]{:S(2)}, u32[]{:S(2)}) collective-permute-start(bf16[4,256,128]{2,1,0:T(8,128)(2,1)S(1)} %slice.14), channel_id=1, source_target_pairs={{0,4},{4,0},{1,5},{5,1},{2,6},{6,2},{3,7},{7,3},{8,12},{12,8},{9,1... | collective-permute-start | bytes 786440 | tf_op jit(solution)/shard_map/ppermute | solution.py:45
  89.2 10.3 %collective-permute-start.19 = (bf16[128,1024]{1,0:T(8,128)(2,1)S(1)}, bf16[128,1024]{1,0:T(8,128)(2,1)S(1)}, u32[]{:S(2)}, u32[]{:S(2)}) collective-permute-start(bf16[128,1024]{1,0:T(8,128)(2,1)S(1)} %constant_dynamic-slice_fusion), channel_id=1, source_target_pairs={{0,2},{1,3},{2,0},{3,1},{4,6},{5,7},{6,4},{7,5},{8,10},{9,11},{10,... | collective-permute-start | bytes 786440 | tf_op jit(solution)/shard_map/ppermute | solution.py:45
  90.8 10.7 %collective-permute-start.15 = (bf16[4,256,128]{2,1,0:T(8,128)(2,1)S(1)}, bf16[4,256,128]{2,1,0:T(8,128)(2,1)S(1)}, u32[]{:S(2)}, u32[]{:S(2)}) collective-permute-start(bf16[4,256,128]{2,1,0:T(8,128)(2,1)S(1)} %slice.14), channel_id=1, source_target_pairs={{0,16},{8,24},{16,0},{24,8},{1,17},{9,25},{17,1},{25,9},{2,18},{10... | collective-permute-start | bytes 786440 | tf_op jit(solution)/shard_map/ppermute | solution.py:45
  92.7 11.7 %collective-permute-start.16 = (bf16[4,256,128]{2,1,0:T(8,128)(2,1)S(1)}, bf16[4,256,128]{2,1,0:T(8,128)(2,1)S(1)}, u32[]{:S(2)}, u32[]{:S(2)}) collective-permute-start(bf16[4,256,128]{2,1,0:T(8,128)(2,1)S(1)} %slice.14), channel_id=1, source_target_pairs={{0,8},{8,16},{16,24},{24,0},{1,9},{9,17},{17,25},{25,1},{2,10},{10... | collective-permute-start | bytes 786440 | tf_op jit(solution)/shard_map/ppermute | solution.py:45
  94.5 11.9 %collective-permute-start.17 = (bf16[4,256,128]{2,1,0:T(8,128)(2,1)S(1)}, bf16[4,256,128]{2,1,0:T(8,128)(2,1)S(1)}, u32[]{:S(2)}, u32[]{:S(2)}) collective-permute-start(bf16[4,256,128]{2,1,0:T(8,128)(2,1)S(1)} %slice.14), channel_id=1, source_target_pairs={{0,24},{8,0},{16,8},{24,16},{1,25},{9,1},{17,9},{25,17},{2,26},{10... | collective-permute-start | bytes 786440 | tf_op jit(solution)/shard_map/ppermute | solution.py:45
  106.4 1.5 collective-permute-start.22
  106.4 1.9 %collective-permute-start.23 = (bf16[4,256,128]{2,1,0:T(8,128)(2,1)S(1)}, bf16[4,256,128]{2,1,0:T(8,128)(2,1)S(1)}, u32[]{:S(2)}, u32[]{:S(2)}) collective-permute-start(bf16[4,256,128]{2,1,0:T(8,128)(2,1)S(1)} %collective-permute-done.17.refs_2_), channel_id=1, source_target_pairs={{0,4},{4,0},{1,5},{5,1},{2,6},{6,2},{3,7},{7,3},{8,12},{12,8},{9,1... | collective-permute-start | bytes 786440 | tf_op jit(solution)/shard_map/ppermute | solution.py:45
  106.9 7.2 %collective-permute-start.24 = (bf16[256,1024]{1,0:T(8,128)(2,1)S(1)}, bf16[256,1024]{1,0:T(8,128)(2,1)S(1)}, u32[]{:S(2)}, u32[]{:S(2)}) collective-permute-start(bf16[256,1024]{1,0:T(8,128)(2,1)S(1)} %collective-permute-done.18.refs_7_), channel_id=1, source_target_pairs={{0,4},{4,0},{1,5},{5,1},{2,6},{6,2},{3,7},{7,3},{8,12},{12,8},{9,1... | collective-permute-start | bytes 1572872 | tf_op jit(solution)/shard_map/ppermute | solution.py:45
  106.9 7.1 %collective-permute-start.21 = (bf16[4,256,128]{2,1,0:T(8,128)(2,1)S(1)}, bf16[4,256,128]{2,1,0:T(8,128)(2,1)S(1)}, u32[]{:S(2)}, u32[]{:S(2)}) collective-permute-start(bf16[4,256,128]{2,1,0:T(8,128)(2,1)S(1)} %collective-permute-done.15.refs_0_), channel_id=1, source_target_pairs={{0,4},{4,0},{1,5},{5,1},{2,6},{6,2},{3,7},{7,3},{8,12},{12,8},{9,1... | collective-permute-start | bytes 786440 | tf_op jit(solution)/shard_map/ppermute | solution.py:45
  107.4 6.7 %collective-permute-start.25 = (bf16[128,1024]{1,0:T(8,128)(2,1)S(1)}, bf16[128,1024]{1,0:T(8,128)(2,1)S(1)}, u32[]{:S(2)}, u32[]{:S(2)}) collective-permute-start(bf16[128,1024]{1,0:T(8,128)(2,1)S(1)} %collective-permute-done.19.refs_8_), channel_id=1, source_target_pairs={{0,4},{4,0},{1,5},{5,1},{2,6},{6,2},{3,7},{7,3},{8,12},{12,8},{9,1... | collective-permute-start | bytes 786440 | tf_op jit(solution)/shard_map/ppermute | solution.py:45
  114.1 18.9 %copy-start.6 = (f32[1024]{0:T(1024)S(1)}, f32[1024]{0:T(1024)}, u32[]{:S(2)}) copy-start(f32[1024]{0:T(1024)} %param.31) | copy-start | bytes 12292
  133.0 16.2 %copy-start.8 = (bf16[1024,4,256]{2,1,0:T(4,128)(2,1)S(1)}, bf16[1024,4,256]{2,1,0:T(4,128)(2,1)}, u32[]{:S(2)}) copy-start(bf16[1024,4,256]{2,1,0:T(4,128)(2,1)} %param.34) | copy-start | bytes 6291460
  135.9 8.2 %collective-permute-start.26 = (bf16[64,1024]{1,0:T(8,128)(2,1)S(1)}, bf16[64,1024]{1,0:T(8,128)(2,1)S(1)}, u32[]{:S(2)}, u32[]{:S(2)}) collective-permute-start(bf16[64,1024]{1,0:T(8,128)(2,1)S(1)} %get-tuple-element.69), channel_id=1, source_target_pairs={{0,1},{1,2},{2,3},{3,0},{4,5},{5,6},{6,7},{7,4},{8,9},{9,10},{10,1... | collective-permute-start | bytes 393224 | tf_op jit(solution)/shard_map/ppermute | solution.py:45
  136.5 7.6 %collective-permute-start.27 = (bf16[64,1024]{1,0:T(8,128)(2,1)S(1)}, bf16[64,1024]{1,0:T(8,128)(2,1)S(1)}, u32[]{:S(2)}, u32[]{:S(2)}) collective-permute-start(bf16[64,1024]{1,0:T(8,128)(2,1)S(1)} %get-tuple-element.71), channel_id=1, source_target_pairs={{0,2},{1,3},{2,0},{3,1},{4,6},{5,7},{6,4},{7,5},{8,10},{9,11},{10,... | collective-permute-start | bytes 393224 | tf_op jit(solution)/shard_map/ppermute | solution.py:45
  137.9 6.8 %collective-permute-start.28 = (bf16[64,1024]{1,0:T(8,128)(2,1)S(1)}, bf16[64,1024]{1,0:T(8,128)(2,1)S(1)}, u32[]{:S(2)}, u32[]{:S(2)}) collective-permute-start(bf16[64,1024]{1,0:T(8,128)(2,1)S(1)} %get-tuple-element.70), channel_id=1, source_target_pairs={{0,3},{1,0},{2,1},{3,2},{4,7},{5,4},{6,5},{7,6},{8,11},{9,8},{10,9... | collective-permute-start | bytes 393224 | tf_op jit(solution)/shard_map/ppermute | solution.py:45
  144.8 7.7 %collective-permute-start.29 = (bf16[64,1024]{1,0:T(8,128)(2,1)S(1)}, bf16[64,1024]{1,0:T(8,128)(2,1)S(1)}, u32[]{:S(2)}, u32[]{:S(2)}) collective-permute-start(bf16[64,1024]{1,0:T(8,128)(2,1)S(1)} %fusion.3.s0), channel_id=1, source_target_pairs={{0,1},{1,2},{2,3},{3,0},{4,5},{5,6},{6,7},{7,4},{8,9},{9,10},{10,1... | collective-permute-start | bytes 393224 | tf_op jit(solution)/shard_map/ppermute | solution.py:45
  146.0 8.2 %collective-permute-start.30 = (bf16[64,1024]{1,0:T(8,128)(2,1)S(1)}, bf16[64,1024]{1,0:T(8,128)(2,1)S(1)}, u32[]{:S(2)}, u32[]{:S(2)}) collective-permute-start(bf16[64,1024]{1,0:T(8,128)(2,1)S(1)} %fusion.3.s0), channel_id=1, source_target_pairs={{0,2},{1,3},{2,0},{3,1},{4,6},{5,7},{6,4},{7,5},{8,10},{9,11},{10,... | collective-permute-start | bytes 393224 | tf_op jit(solution)/shard_map/ppermute | solution.py:45
  149.0 5.3 %collective-permute-start.31 = (bf16[64,1024]{1,0:T(8,128)(2,1)S(1)}, bf16[64,1024]{1,0:T(8,128)(2,1)S(1)}, u32[]{:S(2)}, u32[]{:S(2)}) collective-permute-start(bf16[64,1024]{1,0:T(8,128)(2,1)S(1)} %fusion.3.s0), channel_id=1, source_target_pairs={{0,3},{1,0},{2,1},{3,2},{4,7},{5,4},{6,5},{7,6},{8,11},{9,8},{10,9... | collective-permute-start | bytes 393224 | tf_op jit(solution)/shard_map/ppermute | solution.py:45

commit v7 on v6

--- a/solution.py
+++ b/solution.py
@@ -123,9 +123,12 @@
 
 def fine_kernel(
     where_ref, before_ref, prior_ref, own_ref, tab_hbm, turn_hbm,
-    out_ref, q_ref, k_ref, v_ref, tab_ref, turn_ref, sems,
+    o0, o1, o2, o3, q_ref, k_ref, v_ref, tab_ref, turn_ref, sems,
 ):
     step = pl.program_id(0)
+    head = where_ref[1]
+    quarter = lax.rem(head + step, 4)
+    outs = (o0, o1, o2, o3)
     lowest = jnp.maximum(PAST - where_ref[0] * ROWS, 0)
     head_lane = lax.broadcasted_iota(jnp.int32, (1, SHARE), 1) // HEAD_DIM
 
@@ -176,9 +179,13 @@
         result = jnp.zeros((HALO, SHARE), f32)
         for h in range(4):
             result = jnp.where(head_lane == h, mixed[h * HALO : (h + 1) * HALO], result)
-        out_ref[0, 0:HALO, :] = result.astype(bf16)
-
-    begin = pl.multiple_of((step + 1) * BLOCK, BLOCK)
+        for s, out_ref in enumerate(outs):
+
+            @pl.when(lax.rem(head + s, 4) == 0)
+            def _(out_ref=out_ref):
+                out_ref[0:HALO, :] = result.astype(bf16)
+
+    begin = pl.multiple_of((quarter + 1) * BLOCK, BLOCK)
     keys = k_ref[pl.ds(begin, PAST), :]
     values = v_ref[pl.ds(begin, PAST), :]
     query = q_ref[pl.ds(begin, BLOCK), :]
@@ -220,11 +227,15 @@
         [jnp.where(low_lanes, results[2 * n], results[2 * n + 1]) for n in range(2)], axis=1
     )
     result = result.astype(bf16)
-    out_ref[step, HALO:, :] = result
-
-    @pl.when(step < 3)
-    def _():
-        out_ref[step + 1, 0:HALO, :] = result[BLOCK - HALO :]
+    for s in range(4):
+
+        @pl.when(step == s)
+        def _(s=s):
+            outs[s][HALO:, :] = result
+
+            @pl.when(quarter < 3)
+            def _():
+                outs[(s + 1) % 4][0:HALO, :] = result[BLOCK - HALO :]
 
 
 def vmem():
@@ -274,18 +285,19 @@
 
 
 def fine_rows_kernel(
-    where_ref, ids_ref, emb_ref, got_ref, own_ref, m1, m2, t1, t2, w_hbm,
+    where_ref, ids_ref, emb_ref, g0, g1, g2, g3, own_ref, m1, m2, t1, t2, w_hbm,
     out_ref, w_ref, sems,
 ):
     place, head, core = where_ref[0], where_ref[1], where_ref[2]
     copies = begin_copies([(w_hbm.at[n], w_ref.at[n]) for n in range(4)], sems)
-    merged = dot(pick(ids_ref[...]), emb_ref[...]) + dot(got_ref[head], own_ref[...])
-    near, far, apart = sources(head, core)
-    merged += dot(got_ref[near], m1[...]) + dot(got_ref[far], t1[...])
+    merged = dot(pick(ids_ref[...]), emb_ref[...]) + dot(g0[...], own_ref[...])
+    near = jnp.where(core == 0, g1[...], g3[...])
+    far = jnp.where(core == 0, g3[...], g1[...])
+    merged += dot(near, m1[...]) + dot(far, t1[...])
     at = pl.ds(pl.multiple_of(core * 128, 128), 128)
-    merged += dot(got_ref[apart, :, at], m2[...])
+    merged += dot(g2[:, at], m2[...])
     at = pl.ds(pl.multiple_of(128 - core * 128, 128), 128)
-    merged += dot(got_ref[apart, :, at], t2[...])
+    merged += dot(g2[:, at], t2[...])
     rows = 256 + HALO
     token = (
         place * ROWS + head * 256 - HALO + lax.broadcasted_iota(jnp.int32, (rows, D), 0)
@@ -366,7 +378,7 @@
     acc_ref[at, :] = acc_ref[at, :] * factor + contrib[:, :128]
 
 
-def coarse_first_kernel(flag_ref, turned_ref, far_ref, q_ref, top_ref, total_ref, acc_ref):
+def coarse_first_kernel(turned_ref, q_ref, top_ref, total_ref, acc_ref):
     half = COARSE_ROWS // 2
     low_lanes = lax.broadcasted_iota(jnp.int32, (1, 128), 1) < 64
     row = lax.broadcasted_iota(jnp.int32, (256, 256), 0)
@@ -388,9 +400,18 @@
         acc_ref[at, :] = contrib[:, :128]
     state = (q_ref, top_ref, total_ref, acc_ref)
     for z in range(3):
-        absorb(
-            *state, (z + 1) * 256, (3 - z) * 256, [turned_ref[z, :COARSE_ROWS, :], far_ref[z]]
-        )
+        absorb(*state, (z + 1) * 256, (3 - z) * 256, [turned_ref[z, :COARSE_ROWS, :]])
+
+
+def coarse_far_kernel(
+    flag_ref, far_ref, q_ref, top_in, total_in, acc_in, top_ref, total_ref, acc_ref
+):
+    top_ref[...] = top_in[...]
+    total_ref[...] = total_in[...]
+    acc_ref[...] = acc_in[...]
+    state = (q_ref, top_ref, total_ref, acc_ref)
+    for z in range(3):
+        absorb(*state, (z + 1) * 256, (3 - z) * 256, [far_ref[z]])
 
     @pl.when(flag_ref[0] > 0)
     def _():
@@ -532,7 +553,8 @@
     where = jnp.stack([place, head, core])
 
     prior = later(token_ids, SEQ, 1, 32)
-    before = later(token_ids, SEQ, 2, 32)[ROWS - HALO :]
+    before = later(prior, SEQ, 1, 32)[ROWS - HALO :]
+    norm_held, prior = after(fine_norm, prior)
     tab = call(
         fine_tables_kernel, "fine_tables", pltpu.HBM((5, 256, SHARE), bf16), [], [],
         [
@@ -540,14 +562,14 @@
             pltpu.VMEM((1, D), f32), pltpu.VMEM((256, D), bf16),
             pltpu.VMEM((3, D, SHARE), bf16), pltpu.SemaphoreType.DMA((9,)),
         ],
-        us=3, hbm=[fine_norm[None], embedding, fine_query, fine_key, fine_value],
+        us=3, hbm=[norm_held[None], embedding, fine_query, fine_key, fine_value],
     )
     own_ids_column = token_ids[:, None]
     fine_output_held, own_ids_column = after(fine_output, own_ids_column)
     out_mine = fetch_rest(fine_output_held, core)
     rows = 256 + HALO
     mixed = call(
-        fine_kernel, "fine_attention", jax.ShapeDtypeStruct((4, rows, SHARE), bf16),
+        fine_kernel, "fine_attention", [jax.ShapeDtypeStruct((rows, SHARE), bf16)] * 4,
         [where], [before[:, None], prior[:, None], own_ids_column],
         [
             pltpu.VMEM((BLOCK + ROWS, SHARE), bf16),
@@ -559,7 +581,7 @@
     )
 
     out_mine, mixed = after(out_mine, mixed)
-    got = lax.all_to_all(mixed, "head", 0, 0)
+    got = [mixed[0]] + [shift(mixed[s], "head", s, 4) for s in range(1, 4)]
     out_other = swap_cores(out_mine)
     own_ids = lax.dynamic_slice_in_dim(
         jnp.concatenate([prior[ROWS - HALO :], token_ids]), head * 256, rows, 0
@@ -571,7 +593,7 @@
             jax.ShapeDtypeStruct((SHORTEN, SHARE, D), bf16),
         ],
         [where],
-        [own_ids[:, None], embedding, got, fine_output, *out_mine, *out_other],
+        [own_ids[:, None], embedding, *got, fine_output, *out_mine, *out_other],
         [pltpu.SemaphoreType.DMA((4,))], hbm=[shorten_weight],
     )
     blocks = exchange(lambda d: lax.dynamic_index_in_dim(sends, d, 0, keepdims=False), "head", 4)
@@ -598,6 +620,7 @@
     coarse_output_held, packed = after(coarse_output, packed)
     co_mine = fetch_rest(coarse_output_held, core)
     turned = lax.all_to_all(packed, "z", 0, 0)
+    co_mine[1], turned = after(co_mine[1], turned)
     kv = turned[:, :COARSE_ROWS]
     far = [shift(kv, "core", 1, 2)]
     near = [shift(kv, "x", s, 4) for s in range(1, 4)]
@@ -607,10 +630,14 @@
     wide = jax.ShapeDtypeStruct((1024, 128), f32)
     q_all, *sums = call(
         coarse_first_kernel, "coarse_first",
-        [jax.ShapeDtypeStruct((1024, 128), bf16), wide, wide, wide], [flags], [turned, far[0]],
-        us=3, limit=24,
-    )
-    near_held, co_held, q_all = lax.optimization_barrier((near, co_mine, q_all))
+        [jax.ShapeDtypeStruct((1024, 128), bf16), wide, wide, wide], [], [turned],
+        us=2, limit=24,
+    )
+    sums = call(
+        coarse_far_kernel, "coarse_far", [wide, wide, wide], [flags], [far[0], q_all, *sums],
+        us=2, limit=24,
+    )
+    near_held, co_held, sums = lax.optimization_barrier((near, co_mine, sums))
     far += [shift(part, "core", 1, 2) for part in near_held]
     co_other = swap_cores(co_held)
     square = jax.ShapeDtypeStruct((D, D), bf16)

time: 157 us -> 163 us (1.038)
  blocking collectives: 15.6 us -> 21.1 us
  waiting for transfers between devices: 52.5 us -> 47.3 us
  local copies, waits for them, and re-layouts: 2.43 us -> 5.37 us
  starting transfers between devices: 44.4 us -> 47.3 us
    ppermute x28 -> x31, waiting for transfers between devices: 36.9 us -> 47.3 us  [shift(): lax.ppermute(value, axis, [(i, (i + steps) % count) for i in range(count)])]
    all_to_all x1 -> x0, waiting for transfers between devices: 8.6 us -> none  [local(): got = lax.all_to_all(mixed, 'head', 0, 0)]
    all_to_all x1, waiting for transfers between devices: 6.99 us -> 0.01 us  [local(): turned = lax.all_to_all(packed, 'z', 0, 0)]
    ppermute x28 -> x31, starting transfers between devices: 27.8 us -> 34.1 us  [shift(): lax.ppermute(value, axis, [(i, (i + steps) % count) for i in range(count)])]
    all_to_all x1, blocking collectives: 15.6 us -> 21.1 us  [local(): heads_in = lax.all_to_all(wide_sends, ('z', 'head'), 0, 0)]
    all_to_all x1 -> x0, starting transfers between devices: 4.08 us -> none  [local(): got = lax.all_to_all(mixed, 'head', 0, 0)]
    ppermute x2, starting transfers between devices: 2.03 us -> 4 us  [fetch_rest(): whole = lax.ppermute(weight, ('core', 'head'), pairs)]
    pallas_call x13 -> x14, Pallas kernels: 41.2 us -> 41.2 us  [call(): pl.pallas_call(kernel, out_shape=shapes, in_specs=[smem()] * len(scalars)...]
  transfers between devices with their start and end apart: 34 -> 36, of which waited for: 21 -> 20; matrix products, arithmetic and copies ran while one was open for 2% -> 2% of each run, Pallas kernels for 18% -> 17%
where the time goes in v7:
time: 163 us
  starting transfers between devices  47.3 us (29%)
  waiting for transfers between devices  47.3 us (29%)
  Pallas kernels  41.2 us (25%)
  blocking collectives  21.1 us (13%)
  local copies, waits for them, and re-layouts  5.37 us (3%)
    ppermute x31, waiting for transfers between devices, shift(): lax.ppermute(value, axis, [(i, (i + steps) % count) for i in range(count)])  47.3 us
    pallas_call x14, Pallas kernels, call(): pl.pallas_call(kernel, out_shape=shapes, in_specs=[smem()] * len(scalars)...  41.2 us
    ppermute x31, starting transfers between devices, shift(): lax.ppermute(value, axis, [(i, (i + steps) % count) for i in range(count)])  34.1 us
    all_to_all x1, blocking collectives, local(): heads_in = lax.all_to_all(wide_sends, ('z', 'head'), 0, 0)  21.1 us
    all_to_all x1, starting transfers between devices, local(): turned = lax.all_to_all(packed, 'z', 0, 0)  4.87 us
    ppermute x2, starting transfers between devices, later(): lax.ppermute(value, axis, [(i, i + steps) for i in range(count - steps)])  4.36 us
    ppermute x2, starting transfers between devices, fetch_rest(): whole = lax.ppermute(weight, ('core', 'head'), pairs)  4 us
  transfers between devices with their start and end apart: 36, of which 20 were waited for; matrix products, arithmetic and copies ran while one was open for 2% of the time, Pallas kernels for 17%

profile of v7, /device:TPU:6, one launch (start us, length us, event | category | flops | bytes accessed | tf_op | source)
XLA Modules:
  0.0 163.1 jit_solution(7804299030082697544)
XLA Ops:
  0.0 1.9 %collective-permute-start = (s32[1024]{0:T(1024)}, s32[1024]{0:T(1024)S(1)}, u32[]{:S(2)}, u32[]{:S(2)}) collective-permute-start(s32[1024]{0:T(1024)} %param.18), channel_id=1, source_target_pairs={{0,4},{4,8},{8,12},{12,16},{16,20},{20,24},{24,28},{28,32},{32,36}... | collective-permute-start | bytes 12296 | tf_op jit(solution)/shard_map/ppermute | solution.py:49
  1.9 1.6 %collective-permute-start.1 = (bf16[256,1024]{1,0:T(8,128)(2,1)}, bf16[256,1024]{1,0:T(8,128)(2,1)S(1)}, u32[]{:S(2)}, u32[]{:S(2)}) collective-permute-start(bf16[256,1024]{1,0:T(8,128)(2,1)} %own_ref.1), channel_id=1, source_target_pairs={{0,1},{1,2},{2,3},{3,0},{4,7},{5,4},{6,5},{7,6},{8,9},{9,10},{10,1... | collective-permute-start | bytes 1572872 | tf_op jit(solution)/shard_map/ppermute | solution.py:512
  3.6 1.7 %constant_dynamic-slice_fusion.1 = bf16[128,1024]{1,0:T(8,128)(2,1)} fusion(bf16[256,1024]{1,0:T(8,128)(2,1)} %own_ref.1, s32[]{:T(128)S(6)} %select_n.54), kind=kLoop, calls=%fused_computation.16 | loop fusion | bytes 524292 | tf_op jit(solution)/shard_map/dynamic_slice | solution.py:513
  5.3 2.9 %collective-permute-start.2 = (bf16[128,1024]{1,0:T(8,128)(2,1)}, bf16[128,1024]{1,0:T(8,128)(2,1)S(1)}, u32[]{:S(2)}, u32[]{:S(2)}) collective-permute-start(bf16[128,1024]{1,0:T(8,128)(2,1)} %constant_dynamic-slice_fusion.1), channel_id=1, source_target_pairs={{0,2},{1,3},{2,0},{3,1},{4,6},{5,7},{6,4},{7,5},{8,10},{9,11},{10,... | collective-permute-start | bytes 786440 | tf_op jit(solution)/shard_map/ppermute | solution.py:45
  8.2 0.9 copy.22.own_ref
  9.2 2.5 %collective-permute-start.3 = (s32[1024]{0:T(1024)S(1)}, s32[1024]{0:T(1024)S(1)}, u32[]{:S(2)}, u32[]{:S(2)}) collective-permute-start(s32[1024]{0:T(1024)S(1)} %collective-permute-done), channel_id=1, source_target_pairs={{0,4},{4,8},{8,12},{12,16},{16,20},{20,24},{24,28},{28,32},{32,36}... | collective-permute-start | bytes 12296 | tf_op jit(solution)/shard_map/ppermute | solution.py:49
  11.6 3.1 %fine_tables.1.tab_hbm = bf16[5,256,256]{2,1,0:T(8,128)(2,1)} custom-call(f32[1,1024]{1,0:T(1,128)} %bitcast.35, bf16[256,1024]{1,0:T(8,128)(2,1)} %emb_ref.1, bf16[1024,256]{1,0:T(8,128)(2,1)} %wq_hbm.1, bf16[1024,256]{1,0:T(8,128)(2,1)} %wk_hbm.1, bf16[1024,256]{1,0:T(8,128)(2,1)} %wv_hbm.1), custom_call_target="tpu_custom_call" | custom-call | flops 3000000000 | bytes 6000000 | tf_op jit(solution)/shard_map/fine_tables/pallas_call | solution.py:257
  15.2 13.8 %fine_attention.1 = (bf16[272,256]{1,0:T(8,128)(2,1)S(1)}, bf16[272,256]{1,0:T(8,128)(2,1)S(1)}, bf16[272,256]{1,0:T(8,128)(2,1)S(1)}, bf16[272,256]{1,0:T(8,128)(2,1)S(1)}) custom-call(s32[3]{0:T(128)S(1)} %pad_add_fusion.where_ref, s32[16,1]{1,0:T(8,128)S(1)} %copy.20.before_ref, s32[1024,1]{1,0:T(8,128)S(1)} %copy.21.prior_ref, ...), custom_call_target="tpu_custom_call" | custom-call | flops 12000000000 | bytes 24000000 | tf_op jit(solution)/shard_map/fine_attention/pallas_call | solution.py:257
  28.9 0.7 copy-done.8
  29.6 1.4 collective-permute-start.7
  31.1 2.8 %collective-permute-start.5 = (bf16[272,256]{1,0:T(8,128)(2,1)S(1)}, bf16[272,256]{1,0:T(8,128)(2,1)S(1)}, u32[]{:S(2)}, u32[]{:S(2)}) collective-permute-start(bf16[272,256]{1,0:T(8,128)(2,1)S(1)} %get-tuple-element.61), channel_id=1, source_target_pairs={{0,2},{1,3},{2,0},{3,1},{4,6},{5,7},{6,4},{7,5},{8,10},{9,11},{10,... | collective-permute-start | bytes 417800 | tf_op jit(solution)/shard_map/ppermute | solution.py:45
  33.9 1.7 %collective-permute-start.6 = (bf16[272,256]{1,0:T(8,128)(2,1)S(1)}, bf16[272,256]{1,0:T(8,128)(2,1)}, u32[]{:S(2)}, u32[]{:S(2)}) collective-permute-start(bf16[272,256]{1,0:T(8,128)(2,1)S(1)} %get-tuple-element.62), channel_id=1, source_target_pairs={{0,3},{1,0},{2,1},{3,2},{4,7},{5,4},{6,5},{7,6},{8,11},{9,8},{10,9... | collective-permute-start | bytes 417800 | tf_op jit(solution)/shard_map/ppermute | solution.py:45
  35.9 5.4 %collective-permute-done.4.g1 = bf16[272,256]{1,0:T(8,128)(2,1)S(1)} collective-permute-done((bf16[272,256]{1,0:T(8,128)(2,1)S(1)}, bf16[272,256]{1,0:T(8,128)(2,1)S(1)}, u32[]{:S(2)}, u32[]{:S(2)}) %collective-permute-start.4) | collective-permute-done | bytes 139296 | tf_op jit(solution)/shard_map/ppermute | solution.py:45
  41.3 0.7 collective-permute-done.6.g3
  42.1 0.9 copy-done.9
  43.0 3.0 %fine_rows.1 = (bf16[4,272,256]{2,1,0:T(8,128)(2,1)S(1)}, bf16[4,256,1024]{2,1,0:T(8,128)(2,1)S(1)}) custom-call(s32[3]{0:T(128)S(1)} %pad_add_fusion.where_ref, s32[272,1]{1,0:T(8,128)S(1)} %broadcast_in_dim.28.ids_ref, bf16[256,1024]{1,0:T(8,128)(2,1)S(1)} %copy-done.1, bf16[272,256]{1,0:T(8,128)(2,1)S(1)} %copy-done.9, ...), custom_call_target="tpu_custom_call" | custom-call | flops 2000000000 | bytes 4000000 | tf_op jit(solution)/shard_map/fine_rows/pallas_call | solution.py:257
  46.0 1.0 collective-permute-start.9
  47.0 3.2 %collective-permute-start.11 = (bf16[272,256]{1,0:T(8,128)(2,1)S(1)}, bf16[272,256]{1,0:T(8,128)(2,1)S(1)}, u32[]{:S(2)}, u32[]{:S(2)}) collective-permute-start(bf16[272,256]{1,0:T(8,128)(2,1)S(1)} %get-tuple-element.99), channel_id=1, source_target_pairs={{0,2},{1,3},{2,0},{3,1},{4,6},{5,7},{6,4},{7,5},{8,10},{9,11},{10,... | collective-permute-start | bytes 417800 | tf_op jit(solution)/shard_map/ppermute | solution.py:45
  50.2 2.4 %collective-permute-done.9.group_ref.b1 = bf16[272,256]{1,0:T(8,128)(2,1)S(1)} collective-permute-done((bf16[272,256]{1,0:T(8,128)(2,1)S(1)}, bf16[272,256]{1,0:T(8,128)(2,1)S(1)}, u32[]{:S(2)}, u32[]{:S(2)}) %collective-permute-start.9) | collective-permute-done | bytes 139296 | tf_op jit(solution)/shard_map/ppermute | solution.py:45
  52.6 0.5 short_part.5
  53.1 2.8 %collective-permute-start.10 = (bf16[64,1024]{1,0:T(8,128)(2,1)S(1)}, bf16[64,1024]{1,0:T(8,128)(2,1)S(1)}, u32[]{:S(2)}, u32[]{:S(2)}) collective-permute-start(bf16[64,1024]{1,0:T(8,128)(2,1)S(1)} %short_part.5), channel_id=1, source_target_pairs={{0,3},{1,0},{2,1},{3,2},{4,7},{5,4},{6,5},{7,6},{8,11},{9,8},{10,9... | collective-permute-start | bytes 393224 | tf_op jit(solution)/shard_map/ppermute | solution.py:45
  55.8 0.9 collective-permute-done.11.group_ref.b2
  56.8 0.5 short_part.6
  57.2 0.4 collective-permute-start.12
  57.6 0.5 short_part.7
  58.1 0.9 collective-permute-start.14
  59.0 0.5 short_part.4
  59.5 1.7 %collective-permute-done.10 = bf16[64,1024]{1,0:T(8,128)(2,1)S(1)} collective-permute-done((bf16[64,1024]{1,0:T(8,128)(2,1)S(1)}, bf16[64,1024]{1,0:T(8,128)(2,1)S(1)}, u32[]{:S(2)}, u32[]{:S(2)}) %collective-permute-start.10) | collective-permute-done | bytes 131104 | tf_op jit(solution)/shard_map/ppermute | solution.py:45
  61.2 3.7 %collective-permute-done.12 = bf16[64,1024]{1,0:T(8,128)(2,1)S(1)} collective-permute-done((bf16[64,1024]{1,0:T(8,128)(2,1)S(1)}, bf16[64,1024]{1,0:T(8,128)(2,1)S(1)}, u32[]{:S(2)}, u32[]{:S(2)}) %collective-permute-start.12) | collective-permute-done | bytes 131104 | tf_op jit(solution)/shard_map/ppermute | solution.py:45
  64.8 1.4 collective-permute-done.14
  66.3 2.0 %collective-permute-start.16 = (bf16[64,1024]{1,0:T(8,128)(2,1)S(1)}, bf16[64,1024]{1,0:T(8,128)(2,1)S(1)}, u32[]{:S(2)}, u32[]{:S(2)}) collective-permute-start(bf16[64,1024]{1,0:T(8,128)(2,1)S(1)} %add_convert_fusion.s0), channel_id=1, source_target_pairs={{0,2},{1,3},{2,0},{3,1},{4,6},{5,7},{6,4},{7,5},{8,10},{9,11},{10,... | collective-permute-start | bytes 393224 | tf_op jit(solution)/shard_map/ppermute | solution.py:45
  68.4 1.5 collective-permute-start.17
  69.8 5.3 %collective-permute-done.15.s1 = bf16[64,1024]{1,0:T(8,128)(2,1)S(1)} collective-permute-done((bf16[64,1024]{1,0:T(8,128)(2,1)S(1)}, bf16[64,1024]{1,0:T(8,128)(2,1)S(1)}, u32[]{:S(2)}, u32[]{:S(2)}) %collective-permute-start.15) | collective-permute-done | bytes 131104 | tf_op jit(solution)/shard_map/ppermute | solution.py:45
  75.1 0.6 collective-permute-done.17.s3
  75.7 2.3 %coarse_pack.1 = (bf16[4,384,128]{2,1,0:T(8,128)(2,1)}, bf16[256,1024]{1,0:T(8,128)(2,1)S(1)}) custom-call(s32[3]{0:T(128)S(1)} %pad_add_fusion.where_ref, bf16[64,1024]{1,0:T(8,128)(2,1)S(1)} %add_convert_fusion.s0, bf16[64,1024]{1,0:T(8,128)(2,1)S(1)} %collective-permute-done.15.s1, bf16[64,1024]{1,0:T(8,128)(2,1)S(1)} %collective-permute-done.16.s2, ...), custom_call_target="tpu_custom_call" | custom-call | flops 2000000000 | bytes 4000000 | tf_op jit(solution)/shard_map/coarse_pack/pallas_call | solution.py:257
  78.0 4.9 %all-to-all-start = ((bf16[4,384,128]{2,1,0:T(8,128)(2,1)}), bf16[4,384,128]{2,1,0:T(8,128)(2,1)S(1)}, u32[]{:S(2)}, u32[]{:S(2)}) async-start(bf16[4,384,128]{2,1,0:T(8,128)(2,1)} %get-tuple-element.69), calls=%async_computation | async-start | bytes 786432 | tf_op jit(solution)/shard_map/all_to_all | solution.py:622
  82.9 0.9 collective-permute-start.18
  83.9 2.4 %collective-permute-start.22 = (bf16[256,1024]{1,0:T(8,128)(2,1)S(1)}, bf16[256,1024]{1,0:T(8,128)(2,1)S(1)}, u32[]{:S(2)}, u32[]{:S(2)}) collective-permute-start(bf16[256,1024]{1,0:T(8,128)(2,1)S(1)} %copy-done.11), channel_id=1, source_target_pairs={{0,1},{1,2},{2,3},{3,0},{4,7},{5,4},{6,5},{7,6},{8,9},{9,10},{10,1... | collective-permute-start | bytes 1572872 | tf_op jit(solution)/shard_map/ppermute | solution.py:512
  86.2 4.8 %collective-permute-done.18.refs_8_ = bf16[128,1024]{1,0:T(8,128)(2,1)S(1)} collective-permute-done((bf16[128,1024]{1,0:T(8,128)(2,1)S(1)}, bf16[128,1024]{1,0:T(8,128)(2,1)S(1)}, u32[]{:S(2)}, u32[]{:S(2)}) %collective-permute-start.18) | collective-permute-done | bytes 262176 | tf_op jit(solution)/shard_map/ppermute | solution.py:45
  91.2 1.5 collective-permute-start.19
  92.7 1.8 %collective-permute-start.20 = (bf16[4,256,128]{2,1,0:T(8,128)(2,1)S(1)}, bf16[4,256,128]{2,1,0:T(8,128)(2,1)S(1)}, u32[]{:S(2)}, u32[]{:S(2)}) collective-permute-start(bf16[4,256,128]{2,1,0:T(8,128)(2,1)S(1)} %slice.13), channel_id=1, source_target_pairs={{0,8},{8,16},{16,24},{24,0},{1,9},{9,17},{17,25},{25,1},{2,10},{10... | collective-permute-start | bytes 786440 | tf_op jit(solution)/shard_map/ppermute | solution.py:45
  94.8 1.2 coarse_first.1
  95.9 1.4 coarse_far.1
  97.3 4.6 %collective-permute-done.19.refs_0_ = bf16[4,256,128]{2,1,0:T(8,128)(2,1)S(1)} collective-permute-done((bf16[4,256,128]{2,1,0:T(8,128)(2,1)S(1)}, bf16[4,256,128]{2,1,0:T(8,128)(2,1)S(1)}, u32[]{:S(2)}, u32[]{:S(2)}) %collective-permute-start.19) | collective-permute-done | bytes 262176 | tf_op jit(solution)/shard_map/ppermute | solution.py:45
  101.9 3.4 %collective-permute-done.20.refs_0_ = bf16[4,256,128]{2,1,0:T(8,128)(2,1)S(1)} collective-permute-done((bf16[4,256,128]{2,1,0:T(8,128)(2,1)S(1)}, bf16[4,256,128]{2,1,0:T(8,128)(2,1)S(1)}, u32[]{:S(2)}, u32[]{:S(2)}) %collective-permute-start.20) | collective-permute-done | bytes 262176 | tf_op jit(solution)/shard_map/ppermute | solution.py:45
  105.2 1.8 %collective-permute-done.21.refs_2_ = bf16[4,256,128]{2,1,0:T(8,128)(2,1)S(1)} collective-permute-done((bf16[4,256,128]{2,1,0:T(8,128)(2,1)S(1)}, bf16[4,256,128]{2,1,0:T(8,128)(2,1)S(1)}, u32[]{:S(2)}, u32[]{:S(2)}) %collective-permute-start.21) | collective-permute-done | bytes 262176 | tf_op jit(solution)/shard_map/ppermute | solution.py:45
  107.1 0.5 collective-permute-start.26
  107.6 0.5 collective-permute-start.24
  108.1 0.5 collective-permute-done.25.refs_1_
  109.0 5.8 %coarse_more.1 = (bf16[1024,1024]{1,0:T(8,128)(2,1)S(1)}, bf16[1024,1024]{1,0:T(8,128)(2,1)S(1)}, f32[1024,128]{1,0:T(8,128)S(1)}, f32[1024,128]{1,0:T(8,128)S(1)}, f32[1024,128]{1,0:T(8,128)S(1)}) custom-call(s32[6]{0:T(128)S(1)} %pad_add_fusion.1.flag_ref, bf16[4,256,128]{2,1,0:T(8,128)(2,1)S(1)} %collective-permute-done.20.refs_0_, ...), custom_call_target="tpu_custom_call" | custom-call | flops 6000000000 | bytes 12000000 | tf_op jit(solution)/shard_map/coarse_more/pallas_call | solution.py:257
  114.8 3.2 %coarse_last.1 = (bf16[1024,1024]{1,0:T(8,128)(2,1)S(1)}, bf16[16,128,128]{2,1,0:T(8,128)(2,1)S(1)}) custom-call(s32[6]{0:T(128)S(1)} %pad_add_fusion.1.flag_ref, bf16[4,256,128]{2,1,0:T(8,128)(2,1)S(1)} %collective-permute-done.19.refs_0_, bf16[4,256,128]{2,1,0:T(8,128)(2,1)S(1)} %collective-permute-done.24.refs_1_, ...), custom_call_target="tpu_custom_call" | custom-call | flops 3000000000 | bytes 6000000 | tf_op jit(solution)/shard_map/coarse_last/pallas_call | solution.py:257
  118.0 21.1 %all_to_all.10.heads_ref = bf16[16,128,128]{2,1,0:T(8,128)(2,1)S(1)} all-to-all(bf16[16,128,128]{2,1,0:T(8,128)(2,1)S(1)} %get-tuple-element.90), channel_id=1, replica_groups=mesh['z'=4,'x'=4,'core'=2,'head'=4] {'z','head'}, dimensions={0} | all-to-all | bytes 1048576 | tf_op jit(solution)/shard_map/all_to_all | solution.py:658
  139.1 2.9 %feed.1 = (bf16[4,64,1024]{2,1,0:T(8,128)(2,1)S(1)}, f32[64,1024]{1,0:T(8,128)S(1)}) custom-call(s32[3]{0:T(128)S(1)} %pad_add_fusion.where_ref, bf16[16,128,128]{2,1,0:T(8,128)(2,1)S(1)} %all_to_all.10.heads_ref, bf16[256,1024]{1,0:T(8,128)(2,1)S(1)} %get-tuple-element.91.short_ref, f32[1,1024]{1,0:T(1,128)S(1)} %bitcast.31, ...), custom_call_target="tpu_custom_call" | custom-call | flops 4000000000 | bytes 8000000 | tf_op jit(solution)/shard_map/feed/pallas_call | solution.py:257
  142.0 0.6 collective-permute-start.29
  142.6 1.4 collective-permute-start.30
  144.1 1.5 collective-permute-start.31
  145.5 4.7 %collective-permute-done.29 = bf16[64,1024]{1,0:T(8,128)(2,1)S(1)} collective-permute-done((bf16[64,1024]{1,0:T(8,128)(2,1)S(1)}, bf16[64,1024]{1,0:T(8,128)(2,1)S(1)}, u32[]{:S(2)}, u32[]{:S(2)}) %collective-permute-start.29) | collective-permute-done | bytes 131104 | tf_op jit(solution)/shard_map/ppermute | solution.py:45
  150.2 0.6 collective-permute-done.31
  150.9 1.1 collective-permute-start.32
  152.1 3.0 %collective-permute-start.33 = (bf16[64,1024]{1,0:T(8,128)(2,1)S(1)}, bf16[64,1024]{1,0:T(8,128)(2,1)S(1)}, u32[]{:S(2)}, u32[]{:S(2)}) collective-permute-start(bf16[64,1024]{1,0:T(8,128)(2,1)S(1)} %fusion.3.s0), channel_id=1, source_target_pairs={{0,2},{1,3},{2,0},{3,1},{4,6},{5,7},{6,4},{7,5},{8,10},{9,11},{10,... | collective-permute-start | bytes 393224 | tf_op jit(solution)/shard_map/ppermute | solution.py:45
  155.3 0.5 copy.24
  155.8 2.8 %collective-permute-done.32.s1 = bf16[64,1024]{1,0:T(8,128)(2,1)S(1)} collective-permute-done((bf16[64,1024]{1,0:T(8,128)(2,1)S(1)}, bf16[64,1024]{1,0:T(8,128)(2,1)S(1)}, u32[]{:S(2)}, u32[]{:S(2)}) %collective-permute-start.32) | collective-permute-done | bytes 131104 | tf_op jit(solution)/shard_map/ppermute | solution.py:45
  158.6 1.7 %collective-permute-done.33.s2 = bf16[64,1024]{1,0:T(8,128)(2,1)S(1)} collective-permute-done((bf16[64,1024]{1,0:T(8,128)(2,1)S(1)}, bf16[64,1024]{1,0:T(8,128)(2,1)S(1)}, u32[]{:S(2)}, u32[]{:S(2)}) %collective-permute-start.33) | collective-permute-done | bytes 131104 | tf_op jit(solution)/shard_map/ppermute | solution.py:45
  160.4 2.7 %final.1 = bf16[1024,256]{1,0:T(8,128)(2,1)} custom-call(s32[3]{0:T(128)S(1)} %pad_add_fusion.where_ref, bf16[64,1024]{1,0:T(8,128)(2,1)S(1)} %fusion.3.s0, bf16[64,1024]{1,0:T(8,128)(2,1)S(1)} %collective-permute-done.32.s1, bf16[64,1024]{1,0:T(8,128)(2,1)S(1)} %collective-permute-done.33.s2, bf16[64,1024]{1,0:T(8,128)(2,1)S(1)} %collective-permute-done.34.s3, ...), custom_call_target="tpu_custom_call" | custom-call | flops 2000000000 | bytes 4000000 | tf_op jit(solution)/shard_map/final/pallas_call | solution.py:257
  (67 shorter events, 2.4 us)
Async XLA Ops:
  0.0 9.2 %collective-permute-start = (s32[1024]{0:T(1024)}, s32[1024]{0:T(1024)S(1)}, u32[]{:S(2)}, u32[]{:S(2)}) collective-permute-start(s32[1024]{0:T(1024)} %param.18), channel_id=1, source_target_pairs={{0,4},{4,8},{8,12},{12,16},{16,20},{20,24},{24,28},{28,32},{32,36}... | collective-permute-start | bytes 12296 | tf_op jit(solution)/shard_map/ppermute | solution.py:49
  1.9 27.7 %collective-permute-start.1 = (bf16[256,1024]{1,0:T(8,128)(2,1)}, bf16[256,1024]{1,0:T(8,128)(2,1)S(1)}, u32[]{:S(2)}, u32[]{:S(2)}) collective-permute-start(bf16[256,1024]{1,0:T(8,128)(2,1)} %own_ref.1), channel_id=1, source_target_pairs={{0,1},{1,2},{2,3},{3,0},{4,7},{5,4},{6,5},{7,6},{8,9},{9,10},{10,1... | collective-permute-start | bytes 1572872 | tf_op jit(solution)/shard_map/ppermute | solution.py:512
  5.3 24.3 %collective-permute-start.2 = (bf16[128,1024]{1,0:T(8,128)(2,1)}, bf16[128,1024]{1,0:T(8,128)(2,1)S(1)}, u32[]{:S(2)}, u32[]{:S(2)}) collective-permute-start(bf16[128,1024]{1,0:T(8,128)(2,1)} %constant_dynamic-slice_fusion.1), channel_id=1, source_target_pairs={{0,2},{1,3},{2,0},{3,1},{4,6},{5,7},{6,4},{7,5},{8,10},{9,11},{10,... | collective-permute-start | bytes 786440 | tf_op jit(solution)/shard_map/ppermute | solution.py:45
  9.2 5.8 %collective-permute-start.3 = (s32[1024]{0:T(1024)S(1)}, s32[1024]{0:T(1024)S(1)}, u32[]{:S(2)}, u32[]{:S(2)}) collective-permute-start(s32[1024]{0:T(1024)S(1)} %collective-permute-done), channel_id=1, source_target_pairs={{0,4},{4,8},{8,12},{12,16},{16,20},{20,24},{24,28},{28,32},{32,36}... | collective-permute-start | bytes 12296 | tf_op jit(solution)/shard_map/ppermute | solution.py:49
  15.2 20.5 %copy-start.12 = (s32[1024]{0:T(1024)S(1)}, s32[1024]{0:T(1024)}, u32[]{:S(2)}) copy-start(s32[1024]{0:T(1024)} %param.18) | copy-start | bytes 12292
  15.2 26.9 %copy-start = (bf16[256,1024]{1,0:T(8,128)(2,1)S(1)}, bf16[256,1024]{1,0:T(8,128)(2,1)}, u32[]{:S(2)}) copy-start(bf16[256,1024]{1,0:T(8,128)(2,1)} %own_ref.1) | copy-start | bytes 1572868
  15.2 26.9 %copy-start.1 = (bf16[256,1024]{1,0:T(8,128)(2,1)S(1)}, bf16[256,1024]{1,0:T(8,128)(2,1)}, u32[]{:S(2)}) copy-start(bf16[256,1024]{1,0:T(8,128)(2,1)} %emb_ref.1) | copy-start | bytes 1572868
  28.9 0.7 copy-start.8
  29.6 12.4 %collective-permute-start.7 = (bf16[256,1024]{1,0:T(8,128)(2,1)S(1)}, bf16[256,1024]{1,0:T(8,128)(2,1)S(1)}, u32[]{:S(2)}, u32[]{:S(2)}) collective-permute-start(bf16[256,1024]{1,0:T(8,128)(2,1)S(1)} %collective-permute-done.1.m1), channel_id=1, source_target_pairs={{0,4},{4,0},{1,5},{5,1},{2,6},{6,2},{3,7},{7,3},{8,12},{12,8},{9,1... | collective-permute-start | bytes 1572872 | tf_op jit(solution)/shard_map/ppermute | solution.py:45
  31.0 11.0 %collective-permute-start.8 = (bf16[128,1024]{1,0:T(8,128)(2,1)S(1)}, bf16[128,1024]{1,0:T(8,128)(2,1)S(1)}, u32[]{:S(2)}, u32[]{:S(2)}) collective-permute-start(bf16[128,1024]{1,0:T(8,128)(2,1)S(1)} %collective-permute-done.2.m2), channel_id=1, source_target_pairs={{0,4},{4,0},{1,5},{5,1},{2,6},{6,2},{3,7},{7,3},{8,12},{12,8},{9,1... | collective-permute-start | bytes 786440 | tf_op jit(solution)/shard_map/ppermute | solution.py:45
  31.1 10.2 %collective-permute-start.4 = (bf16[272,256]{1,0:T(8,128)(2,1)S(1)}, bf16[272,256]{1,0:T(8,128)(2,1)S(1)}, u32[]{:S(2)}, u32[]{:S(2)}) collective-permute-start(bf16[272,256]{1,0:T(8,128)(2,1)S(1)} %get-tuple-element.60), channel_id=1, source_target_pairs={{0,1},{1,2},{2,3},{3,0},{4,5},{5,6},{6,7},{7,4},{8,9},{9,10},{10,1... | collective-permute-start | bytes 417800 | tf_op jit(solution)/shard_map/ppermute | solution.py:45
  31.1 10.2 %collective-permute-start.5 = (bf16[272,256]{1,0:T(8,128)(2,1)S(1)}, bf16[272,256]{1,0:T(8,128)(2,1)S(1)}, u32[]{:S(2)}, u32[]{:S(2)}) collective-permute-start(bf16[272,256]{1,0:T(8,128)(2,1)S(1)} %get-tuple-element.61), channel_id=1, source_target_pairs={{0,2},{1,3},{2,0},{3,1},{4,6},{5,7},{6,4},{7,5},{8,10},{9,11},{10,... | collective-permute-start | bytes 417800 | tf_op jit(solution)/shard_map/ppermute | solution.py:45
  33.9 8.1 %collective-permute-start.6 = (bf16[272,256]{1,0:T(8,128)(2,1)S(1)}, bf16[272,256]{1,0:T(8,128)(2,1)}, u32[]{:S(2)}, u32[]{:S(2)}) collective-permute-start(bf16[272,256]{1,0:T(8,128)(2,1)S(1)} %get-tuple-element.62), channel_id=1, source_target_pairs={{0,3},{1,0},{2,1},{3,2},{4,7},{5,4},{6,5},{7,6},{8,11},{9,8},{10,9... | collective-permute-start | bytes 417800 | tf_op jit(solution)/shard_map/ppermute | solution.py:45
  42.0 0.9 copy-start.9
  46.0 6.6 %collective-permute-start.9 = (bf16[272,256]{1,0:T(8,128)(2,1)S(1)}, bf16[272,256]{1,0:T(8,128)(2,1)S(1)}, u32[]{:S(2)}, u32[]{:S(2)}) collective-permute-start(bf16[272,256]{1,0:T(8,128)(2,1)S(1)} %get-tuple-element.100), channel_id=1, source_target_pairs={{0,1},{1,2},{2,3},{3,0},{4,5},{5,6},{6,7},{7,4},{8,9},{9,10},{10,1... | collective-permute-start | bytes 417800 | tf_op jit(solution)/shard_map/ppermute | solution.py:45
  47.0 9.8 %collective-permute-start.11 = (bf16[272,256]{1,0:T(8,128)(2,1)S(1)}, bf16[272,256]{1,0:T(8,128)(2,1)S(1)}, u32[]{:S(2)}, u32[]{:S(2)}) collective-permute-start(bf16[272,256]{1,0:T(8,128)(2,1)S(1)} %get-tuple-element.99), channel_id=1, source_target_pairs={{0,2},{1,3},{2,0},{3,1},{4,6},{5,7},{6,4},{7,5},{8,10},{9,11},{10,... | collective-permute-start | bytes 417800 | tf_op jit(solution)/shard_map/ppermute | solution.py:45
  50.2 7.4 %collective-permute-start.13 = (bf16[272,256]{1,0:T(8,128)(2,1)S(1)}, bf16[272,256]{1,0:T(8,128)(2,1)S(1)}, u32[]{:S(2)}, u32[]{:S(2)}) collective-permute-start(bf16[272,256]{1,0:T(8,128)(2,1)S(1)} %get-tuple-element.98), channel_id=1, source_target_pairs={{0,3},{1,0},{2,1},{3,2},{4,7},{5,4},{6,5},{7,6},{8,11},{9,8},{10,9... | collective-permute-start | bytes 417800 | tf_op jit(solution)/shard_map/ppermute | solution.py:45
  53.1 8.1 %collective-permute-start.10 = (bf16[64,1024]{1,0:T(8,128)(2,1)S(1)}, bf16[64,1024]{1,0:T(8,128)(2,1)S(1)}, u32[]{:S(2)}, u32[]{:S(2)}) collective-permute-start(bf16[64,1024]{1,0:T(8,128)(2,1)S(1)} %short_part.5), channel_id=1, source_target_pairs={{0,3},{1,0},{2,1},{3,2},{4,7},{5,4},{6,5},{7,6},{8,11},{9,8},{10,9... | collective-permute-start | bytes 393224 | tf_op jit(solution)/shard_map/ppermute | solution.py:45
  57.2 7.6 %collective-permute-start.12 = (bf16[64,1024]{1,0:T(8,128)(2,1)S(1)}, bf16[64,1024]{1,0:T(8,128)(2,1)S(1)}, u32[]{:S(2)}, u32[]{:S(2)}) collective-permute-start(bf16[64,1024]{1,0:T(8,128)(2,1)S(1)} %short_part.6), channel_id=1, source_target_pairs={{0,2},{1,3},{2,0},{3,1},{4,6},{5,7},{6,4},{7,5},{8,10},{9,11},{10,... | collective-permute-start | bytes 393224 | tf_op jit(solution)/shard_map/ppermute | solution.py:45
  58.1 8.1 %collective-permute-start.14 = (bf16[64,1024]{1,0:T(8,128)(2,1)S(1)}, bf16[64,1024]{1,0:T(8,128)(2,1)S(1)}, u32[]{:S(2)}, u32[]{:S(2)}) collective-permute-start(bf16[64,1024]{1,0:T(8,128)(2,1)S(1)} %short_part.7), channel_id=1, source_target_pairs={{0,1},{1,2},{2,3},{3,0},{4,5},{5,6},{6,7},{7,4},{8,9},{9,10},{10,1... | collective-permute-start | bytes 393224 | tf_op jit(solution)/shard_map/ppermute | solution.py:45
  59.0 16.7 %copy-start.2 = (bf16[1024,256]{1,0:T(8,128)(2,1)S(1)}, bf16[1024,256]{1,0:T(8,128)(2,1)}, u32[]{:S(2)}) copy-start(bf16[1024,256]{1,0:T(8,128)(2,1)} %wq_ref.1) | copy-start | bytes 1572868
  59.0 16.7 %copy-start.3 = (bf16[1024,256]{1,0:T(8,128)(2,1)S(1)}, bf16[1024,256]{1,0:T(8,128)(2,1)}, u32[]{:S(2)}) copy-start(bf16[1024,256]{1,0:T(8,128)(2,1)} %wk_ref.1) | copy-start | bytes 1572868
  59.0 16.7 %copy-start.4 = (bf16[1024,256]{1,0:T(8,128)(2,1)S(1)}, bf16[1024,256]{1,0:T(8,128)(2,1)}, u32[]{:S(2)}) copy-start(bf16[1024,256]{1,0:T(8,128)(2,1)} %wv_ref.1) | copy-start | bytes 1572868
  59.0 16.7 %copy-start.5 = (f32[1024]{0:T(1024)S(1)}, f32[1024]{0:T(1024)}, u32[]{:S(2)}) copy-start(f32[1024]{0:T(1024)} %param.26) | copy-start | bytes 12292
  59.0 16.7 %copy-start.7 = (f32[576,128]{1,0:T(8,128)S(1)}, f32[576,128]{1,0:T(8,128)}, u32[]{:S(2)}) copy-start(f32[576,128]{1,0:T(8,128)} %constant.90.clone.turn_hbm.turn_ref) | copy-start | bytes 884740
  66.3 8.8 %collective-permute-start.15 = (bf16[64,1024]{1,0:T(8,128)(2,1)S(1)}, bf16[64,1024]{1,0:T(8,128)(2,1)S(1)}, u32[]{:S(2)}, u32[]{:S(2)}) collective-permute-start(bf16[64,1024]{1,0:T(8,128)(2,1)S(1)} %add_convert_fusion.s0), channel_id=1, source_target_pairs={{0,1},{1,2},{2,3},{3,0},{4,5},{5,6},{6,7},{7,4},{8,9},{9,10},{10,1... | collective-permute-start | bytes 393224 | tf_op jit(solution)/shard_map/ppermute | solution.py:45
  66.3 8.7 %collective-permute-start.16 = (bf16[64,1024]{1,0:T(8,128)(2,1)S(1)}, bf16[64,1024]{1,0:T(8,128)(2,1)S(1)}, u32[]{:S(2)}, u32[]{:S(2)}) collective-permute-start(bf16[64,1024]{1,0:T(8,128)(2,1)S(1)} %add_convert_fusion.s0), channel_id=1, source_target_pairs={{0,2},{1,3},{2,0},{3,1},{4,6},{5,7},{6,4},{7,5},{8,10},{9,11},{10,... | collective-permute-start | bytes 393224 | tf_op jit(solution)/shard_map/ppermute | solution.py:45
  68.4 7.3 %collective-permute-start.17 = (bf16[64,1024]{1,0:T(8,128)(2,1)S(1)}, bf16[64,1024]{1,0:T(8,128)(2,1)S(1)}, u32[]{:S(2)}, u32[]{:S(2)}) collective-permute-start(bf16[64,1024]{1,0:T(8,128)(2,1)S(1)} %add_convert_fusion.s0), channel_id=1, source_target_pairs={{0,3},{1,0},{2,1},{3,2},{4,7},{5,4},{6,5},{7,6},{8,11},{9,8},{10,9... | collective-permute-start | bytes 393224 | tf_op jit(solution)/shard_map/ppermute | solution.py:45
  75.7 7.2 %copy-start.11 = (bf16[256,1024]{1,0:T(8,128)(2,1)S(1)}, bf16[256,1024]{1,0:T(8,128)(2,1)}, u32[]{:S(2)}) copy-start(bf16[256,1024]{1,0:T(8,128)(2,1)} %refs_6_.1) | copy-start | bytes 1572868
  78.0 13.0 %all-to-all-start = ((bf16[4,384,128]{2,1,0:T(8,128)(2,1)}), bf16[4,384,128]{2,1,0:T(8,128)(2,1)S(1)}, u32[]{:S(2)}, u32[]{:S(2)}) async-start(bf16[4,384,128]{2,1,0:T(8,128)(2,1)} %get-tuple-element.69), calls=%async_computation | async-start | bytes 786432 | tf_op jit(solution)/shard_map/all_to_all | solution.py:622
  82.9 8.1 %collective-permute-start.18 = (bf16[128,1024]{1,0:T(8,128)(2,1)S(1)}, bf16[128,1024]{1,0:T(8,128)(2,1)S(1)}, u32[]{:S(2)}, u32[]{:S(2)}) collective-permute-start(bf16[128,1024]{1,0:T(8,128)(2,1)S(1)} %constant_dynamic-slice_fusion), channel_id=1, source_target_pairs={{0,2},{1,3},{2,0},{3,1},{4,6},{5,7},{6,4},{7,5},{8,10},{9,11},{10,... | collective-permute-start | bytes 786440 | tf_op jit(solution)/shard_map/ppermute | solution.py:45
  83.9 13.5 %collective-permute-start.22 = (bf16[256,1024]{1,0:T(8,128)(2,1)S(1)}, bf16[256,1024]{1,0:T(8,128)(2,1)S(1)}, u32[]{:S(2)}, u32[]{:S(2)}) collective-permute-start(bf16[256,1024]{1,0:T(8,128)(2,1)S(1)} %copy-done.11), channel_id=1, source_target_pairs={{0,1},{1,2},{2,3},{3,0},{4,7},{5,4},{6,5},{7,6},{8,9},{9,10},{10,1... | collective-permute-start | bytes 1572872 | tf_op jit(solution)/shard_map/ppermute | solution.py:512
  91.0 4.9 %collective-permute-start.23 = (bf16[4,256,128]{2,1,0:T(8,128)(2,1)S(1)}, bf16[4,256,128]{2,1,0:T(8,128)(2,1)S(1)}, u32[]{:S(2)}, u32[]{:S(2)}) collective-permute-start(bf16[4,256,128]{2,1,0:T(8,128)(2,1)S(1)} %slice.13), channel_id=1, source_target_pairs={{0,4},{4,0},{1,5},{5,1},{2,6},{6,2},{3,7},{7,3},{8,12},{12,8},{9,1... | collective-permute-start | bytes 786440 | tf_op jit(solution)/shard_map/ppermute | solution.py:45
  91.2 10.7 %collective-permute-start.19 = (bf16[4,256,128]{2,1,0:T(8,128)(2,1)S(1)}, bf16[4,256,128]{2,1,0:T(8,128)(2,1)S(1)}, u32[]{:S(2)}, u32[]{:S(2)}) collective-permute-start(bf16[4,256,128]{2,1,0:T(8,128)(2,1)S(1)} %slice.13), channel_id=1, source_target_pairs={{0,16},{8,24},{16,0},{24,8},{1,17},{9,25},{17,1},{25,9},{2,18},{10... | collective-permute-start | bytes 786440 | tf_op jit(solution)/shard_map/ppermute | solution.py:45
  92.7 12.5 %collective-permute-start.20 = (bf16[4,256,128]{2,1,0:T(8,128)(2,1)S(1)}, bf16[4,256,128]{2,1,0:T(8,128)(2,1)S(1)}, u32[]{:S(2)}, u32[]{:S(2)}) collective-permute-start(bf16[4,256,128]{2,1,0:T(8,128)(2,1)S(1)} %slice.13), channel_id=1, source_target_pairs={{0,8},{8,16},{16,24},{24,0},{1,9},{9,17},{17,25},{25,1},{2,10},{10... | collective-permute-start | bytes 786440 | tf_op jit(solution)/shard_map/ppermute | solution.py:45
  94.5 12.5 %collective-permute-start.21 = (bf16[4,256,128]{2,1,0:T(8,128)(2,1)S(1)}, bf16[4,256,128]{2,1,0:T(8,128)(2,1)S(1)}, u32[]{:S(2)}, u32[]{:S(2)}) collective-permute-start(bf16[4,256,128]{2,1,0:T(8,128)(2,1)S(1)} %slice.13), channel_id=1, source_target_pairs={{0,24},{8,0},{16,8},{24,16},{1,25},{9,1},{17,9},{25,17},{2,26},{10... | collective-permute-start | bytes 786440 | tf_op jit(solution)/shard_map/ppermute | solution.py:45
  107.0 1.5 collective-permute-start.25
  107.1 1.9 %collective-permute-start.26 = (bf16[4,256,128]{2,1,0:T(8,128)(2,1)S(1)}, bf16[4,256,128]{2,1,0:T(8,128)(2,1)S(1)}, u32[]{:S(2)}, u32[]{:S(2)}) collective-permute-start(bf16[4,256,128]{2,1,0:T(8,128)(2,1)S(1)} %collective-permute-done.21.refs_2_), channel_id=1, source_target_pairs={{0,4},{4,0},{1,5},{5,1},{2,6},{6,2},{3,7},{7,3},{8,12},{12,8},{9,1... | collective-permute-start | bytes 786440 | tf_op jit(solution)/shard_map/ppermute | solution.py:45
  107.6 7.2 %collective-permute-start.27 = (bf16[256,1024]{1,0:T(8,128)(2,1)S(1)}, bf16[256,1024]{1,0:T(8,128)(2,1)S(1)}, u32[]{:S(2)}, u32[]{:S(2)}) collective-permute-start(bf16[256,1024]{1,0:T(8,128)(2,1)S(1)} %collective-permute-done.22.refs_7_), channel_id=1, source_target_pairs={{0,4},{4,0},{1,5},{5,1},{2,6},{6,2},{3,7},{7,3},{8,12},{12,8},{9,1... | collective-permute-start | bytes 1572872 | tf_op jit(solution)/shard_map/ppermute | solution.py:45
  107.6 7.2 %collective-permute-start.24 = (bf16[4,256,128]{2,1,0:T(8,128)(2,1)S(1)}, bf16[4,256,128]{2,1,0:T(8,128)(2,1)S(1)}, u32[]{:S(2)}, u32[]{:S(2)}) collective-permute-start(bf16[4,256,128]{2,1,0:T(8,128)(2,1)S(1)} %collective-permute-done.19.refs_0_), channel_id=1, source_target_pairs={{0,4},{4,0},{1,5},{5,1},{2,6},{6,2},{3,7},{7,3},{8,12},{12,8},{9,1... | collective-permute-start | bytes 786440 | tf_op jit(solution)/shard_map/ppermute | solution.py:45
  108.1 6.7 %collective-permute-start.28 = (bf16[128,1024]{1,0:T(8,128)(2,1)S(1)}, bf16[128,1024]{1,0:T(8,128)(2,1)S(1)}, u32[]{:S(2)}, u32[]{:S(2)}) collective-permute-start(bf16[128,1024]{1,0:T(8,128)(2,1)S(1)} %collective-permute-done.18.refs_8_), channel_id=1, source_target_pairs={{0,4},{4,0},{1,5},{5,1},{2,6},{6,2},{3,7},{7,3},{8,12},{12,8},{9,1... | collective-permute-start | bytes 786440 | tf_op jit(solution)/shard_map/ppermute | solution.py:45
  114.8 24.3 %copy-start.6 = (f32[1024]{0:T(1024)S(1)}, f32[1024]{0:T(1024)}, u32[]{:S(2)}) copy-start(f32[1024]{0:T(1024)} %param.31) | copy-start | bytes 12292
  139.1 16.2 %copy-start.10 = (bf16[1024,4,256]{2,1,0:T(4,128)(2,1)S(1)}, bf16[1024,4,256]{2,1,0:T(4,128)(2,1)}, u32[]{:S(2)}) copy-start(bf16[1024,4,256]{2,1,0:T(4,128)(2,1)} %param.34) | copy-start | bytes 6291460
  142.0 8.2 %collective-permute-start.29 = (bf16[64,1024]{1,0:T(8,128)(2,1)S(1)}, bf16[64,1024]{1,0:T(8,128)(2,1)S(1)}, u32[]{:S(2)}, u32[]{:S(2)}) collective-permute-start(bf16[64,1024]{1,0:T(8,128)(2,1)S(1)} %get-tuple-element.101), channel_id=1, source_target_pairs={{0,1},{1,2},{2,3},{3,0},{4,5},{5,6},{6,7},{7,4},{8,9},{9,10},{10,1... | collective-permute-start | bytes 393224 | tf_op jit(solution)/shard_map/ppermute | solution.py:45
  142.6 7.6 %collective-permute-start.30 = (bf16[64,1024]{1,0:T(8,128)(2,1)S(1)}, bf16[64,1024]{1,0:T(8,128)(2,1)S(1)}, u32[]{:S(2)}, u32[]{:S(2)}) collective-permute-start(bf16[64,1024]{1,0:T(8,128)(2,1)S(1)} %get-tuple-element.103), channel_id=1, source_target_pairs={{0,2},{1,3},{2,0},{3,1},{4,6},{5,7},{6,4},{7,5},{8,10},{9,11},{10,... | collective-permute-start | bytes 393224 | tf_op jit(solution)/shard_map/ppermute | solution.py:45
  144.1 6.8 %collective-permute-start.31 = (bf16[64,1024]{1,0:T(8,128)(2,1)S(1)}, bf16[64,1024]{1,0:T(8,128)(2,1)S(1)}, u32[]{:S(2)}, u32[]{:S(2)}) collective-permute-start(bf16[64,1024]{1,0:T(8,128)(2,1)S(1)} %get-tuple-element.102), channel_id=1, source_target_pairs={{0,3},{1,0},{2,1},{3,2},{4,7},{5,4},{6,5},{7,6},{8,11},{9,8},{10,9... | collective-permute-start | bytes 393224 | tf_op jit(solution)/shard_map/ppermute | solution.py:45
  150.9 7.7 %collective-permute-start.32 = (bf16[64,1024]{1,0:T(8,128)(2,1)S(1)}, bf16[64,1024]{1,0:T(8,128)(2,1)S(1)}, u32[]{:S(2)}, u32[]{:S(2)}) collective-permute-start(bf16[64,1024]{1,0:T(8,128)(2,1)S(1)} %fusion.3.s0), channel_id=1, source_target_pairs={{0,1},{1,2},{2,3},{3,0},{4,5},{5,6},{6,7},{7,4},{8,9},{9,10},{10,1... | collective-permute-start | bytes 393224 | tf_op jit(solution)/shard_map/ppermute | solution.py:45
  152.1 8.2 %collective-permute-start.33 = (bf16[64,1024]{1,0:T(8,128)(2,1)S(1)}, bf16[64,1024]{1,0:T(8,128)(2,1)S(1)}, u32[]{:S(2)}, u32[]{:S(2)}) collective-permute-start(bf16[64,1024]{1,0:T(8,128)(2,1)S(1)} %fusion.3.s0), channel_id=1, source_target_pairs={{0,2},{1,3},{2,0},{3,1},{4,6},{5,7},{6,4},{7,5},{8,10},{9,11},{10,... | collective-permute-start | bytes 393224 | tf_op jit(solution)/shard_map/ppermute | solution.py:45
  155.1 5.3 %collective-permute-start.34 = (bf16[64,1024]{1,0:T(8,128)(2,1)S(1)}, bf16[64,1024]{1,0:T(8,128)(2,1)S(1)}, u32[]{:S(2)}, u32[]{:S(2)}) collective-permute-start(bf16[64,1024]{1,0:T(8,128)(2,1)S(1)} %fusion.3.s0), channel_id=1, source_target_pairs={{0,3},{1,0},{2,1},{3,2},{4,7},{5,4},{6,5},{7,6},{8,11},{9,8},{10,9... | collective-permute-start | bytes 393224 | tf_op jit(solution)/shard_map/ppermute | solution.py:45

commit v8 on v6

--- a/solution.py
+++ b/solution.py
@@ -157,9 +157,11 @@
 
             return body
 
-        lax.fori_loop(0, 3, build_from(prior_ref, 1, False), 0)
+        for n in range(3):
+            build(1 + n, prior_ref[n * BLOCK : (n + 1) * BLOCK, :], False)
         build(4, prior_ref[3 * BLOCK :, :], True)
-        lax.fori_loop(0, 4, build_from(own_ref, 5, True), 0)
+        for n in range(4):
+            build(5 + n, own_ref[n * BLOCK : (n + 1) * BLOCK, :], True)
         halo_q = q_ref[BLOCK - HALO : BLOCK, :]
         stacked = jnp.concatenate(
             [jnp.where(head_lane == h, halo_q, jnp.zeros_like(halo_q)) for h in range(4)], axis=0
@@ -347,23 +349,32 @@
     return jnp.concatenate([kv, jnp.ones((kv.shape[0], 128), bf16)], axis=1)
 
 
-def absorb(q_ref, top_ref, total_ref, acc_ref, begin, rows, parts):
-    at = pl.ds(begin, rows)
-    query = q_ref[at, :]
-    scores = [dot_t(query, kv) for kv in parts]
-    peak = scores[0]
-    for s in scores[1:]:
-        peak = jnp.maximum(peak, s)
-    old = top_ref[at, :]
-    top = jnp.maximum(old, jnp.max(peak, axis=1, keepdims=True))
-    factor = jnp.exp2(old - top)
-    both = jnp.concatenate([top, top], axis=1)
-    contrib = dot(jnp.exp2(scores[0] - both).astype(bf16), with_ones(parts[0]))
-    for s, kv in zip(scores[1:], parts[1:]):
-        contrib = contrib + dot(jnp.exp2(s - both).astype(bf16), with_ones(kv))
-    top_ref[at, :] = top
-    total_ref[at, :] = total_ref[at, :] * factor + contrib[:, 128:]
-    acc_ref[at, :] = acc_ref[at, :] * factor + contrib[:, :128]
+def absorb(state, jobs):
+    q_ref, top_ref, total_ref, acc_ref = state
+
+    def score(job):
+        query = q_ref[pl.ds(job[0], job[1]), :]
+        return [dot_t(query, kv) for kv in job[2]]
+
+    ahead = score(jobs[0])
+    for n, (begin, rows, parts) in enumerate(jobs):
+        scores = ahead
+        if n + 1 < len(jobs):
+            ahead = score(jobs[n + 1])
+        at = pl.ds(begin, rows)
+        peak = scores[0]
+        for s in scores[1:]:
+            peak = jnp.maximum(peak, s)
+        old = top_ref[at, :]
+        top = jnp.maximum(old, jnp.max(peak, axis=1, keepdims=True))
+        factor = jnp.exp2(old - top)
+        both = jnp.concatenate([top, top], axis=1)
+        contrib = dot(jnp.exp2(scores[0] - both).astype(bf16), with_ones(parts[0]))
+        for s, kv in zip(scores[1:], parts[1:]):
+            contrib = contrib + dot(jnp.exp2(s - both).astype(bf16), with_ones(kv))
+        top_ref[at, :] = top
+        total_ref[at, :] = total_ref[at, :] * factor + contrib[:, 128:]
+        acc_ref[at, :] = acc_ref[at, :] * factor + contrib[:, :128]
 
 
 def coarse_first_kernel(flag_ref, turned_ref, far_ref, q_ref, top_ref, total_ref, acc_ref):
@@ -387,15 +398,17 @@
         total_ref[at, :] = contrib[:, 128:]
         acc_ref[at, :] = contrib[:, :128]
     state = (q_ref, top_ref, total_ref, acc_ref)
-    for z in range(3):
-        absorb(
-            *state, (z + 1) * 256, (3 - z) * 256, [turned_ref[z, :COARSE_ROWS, :], far_ref[z]]
-        )
+    absorb(
+        state,
+        [
+            ((z + 1) * 256, (3 - z) * 256, [turned_ref[z, :COARSE_ROWS, :], far_ref[z]])
+            for z in range(3)
+        ],
+    )
 
     @pl.when(flag_ref[0] > 0)
     def _():
-        for z in range(4):
-            absorb(*state, z * 256, 256, [far_ref[z]])
+        absorb(state, [(z * 256, 256, [far_ref[z]]) for z in range(4)])
 
 
 def coarse_more_kernel(which, last, flag_ref, *refs):
@@ -420,15 +433,20 @@
     total_ref[...] = total_in[...]
     acc_ref[...] = acc_in[...]
     state = (q_ref, top_ref, total_ref, acc_ref)
-    for n, s in enumerate(which):
-        near, far = chunks[2 * n], chunks[2 * n + 1]
-        for z in range(3):
-            absorb(*state, (z + 1) * 256, (3 - z) * 256, [near[z], far[z]])
+    pairs_of = [(chunks[2 * n], chunks[2 * n + 1]) for n in range(len(which))]
+    absorb(
+        state,
+        [
+            ((z + 1) * 256, (3 - z) * 256, [near[z], far[z]])
+            for near, far in pairs_of
+            for z in range(3)
+        ],
+    )
+    for s, (near, far) in zip(which, pairs_of):
 
         @pl.when(flag_ref[s] > 0)
         def _(near=near, far=far):
-            for z in range(4):
-                absorb(*state, z * 256, 256, [near[z], far[z]])
+            absorb(state, [(z * 256, 256, [near[z], far[z]]) for z in range(4)])
 
     if last:
         mixed = acc_ref[...] / total_ref[...]

time: 157 us -> 155 us (0.987)
  Pallas kernels: 41.2 us -> 38.3 us
    pallas_call x13, Pallas kernels: 41.2 us -> 38.3 us  [call(): pl.pallas_call(kernel, out_shape=shapes, in_specs=[smem()] * len(scalars)...]
  transfers between devices with their start and end apart: 34 -> 34, of which waited for: 21 -> 21; matrix products, arithmetic and copies ran while one was open for 2% -> 2% of each run, Pallas kernels for 18% -> 16%
where the time goes in v8:
time: 155 us; the launch traced here: 154 us
  waiting for transfers between devices  52.7 us (34%)
  starting transfers between devices  44.4 us (29%)
  Pallas kernels  38.3 us (25%)
  blocking collectives  15.6 us (10%)
  local copies, waits for them, and re-layouts  2.43 us (2%)
    pallas_call x13, Pallas kernels, call(): pl.pallas_call(kernel, out_shape=shapes, in_specs=[smem()] * len(scalars)...  38.3 us
    ppermute x28, waiting for transfers between devices, shift(): lax.ppermute(value, axis, [(i, (i + steps) % count) for i in range(count)])  37.1 us
    ppermute x28, starting transfers between devices, shift(): lax.ppermute(value, axis, [(i, (i + steps) % count) for i in range(count)])  27.8 us
    all_to_all x1, blocking collectives, local(): heads_in = lax.all_to_all(wide_sends, ('z', 'head'), 0, 0)  15.6 us
    all_to_all x1, waiting for transfers between devices, local(): got = lax.all_to_all(mixed, 'head', 0, 0)  8.6 us
    all_to_all x1, waiting for transfers between devices, local(): turned = lax.all_to_all(packed, 'z', 0, 0)  6.99 us
    ppermute x2, starting transfers between devices, later(): lax.ppermute(value, axis, [(i, i + steps) for i in range(count - steps)])  5.65 us
    all_to_all x1, starting transfers between devices, local(): turned = lax.all_to_all(packed, 'z', 0, 0)  4.85 us
  transfers between devices with their start and end apart: 34, of which 21 were waited for; matrix products, arithmetic and copies ran while one was open for 2% of the time, Pallas kernels for 16%

profile of v8, /device:TPU:6, one launch (start us, length us, event | category | flops | bytes accessed | tf_op | source)
XLA Modules:
  0.0 154.2 jit_solution(8935580307667888301)
XLA Ops:
  0.0 1.9 %collective-permute-start = (s32[1024]{0:T(1024)}, s32[1024]{0:T(1024)S(1)}, u32[]{:S(2)}, u32[]{:S(2)}) collective-permute-start(s32[1024]{0:T(1024)} %param.18), channel_id=1, source_target_pairs={{0,4},{4,8},{8,12},{12,16},{16,20},{20,24},{24,28},{28,32},{32,36}... | collective-permute-start | bytes 12296 | tf_op jit(solution)/shard_map/ppermute | solution.py:49
  1.9 3.7 %collective-permute-start.3 = (s32[1024]{0:T(1024)}, s32[1024]{0:T(1024)S(1)}, u32[]{:S(2)}, u32[]{:S(2)}) collective-permute-start(s32[1024]{0:T(1024)} %param.18), channel_id=1, source_target_pairs={{0,8},{4,12},{8,16},{12,20},{16,24},{20,28},{24,32},{28,36},{32,40... | collective-permute-start | bytes 12296 | tf_op jit(solution)/shard_map/ppermute | solution.py:49
  5.7 1.6 %collective-permute-start.1 = (bf16[256,1024]{1,0:T(8,128)(2,1)}, bf16[256,1024]{1,0:T(8,128)(2,1)S(1)}, u32[]{:S(2)}, u32[]{:S(2)}) collective-permute-start(bf16[256,1024]{1,0:T(8,128)(2,1)} %own_ref.1), channel_id=1, source_target_pairs={{0,1},{1,2},{2,3},{3,0},{4,7},{5,4},{6,5},{7,6},{8,9},{9,10},{10,1... | collective-permute-start | bytes 1572872 | tf_op jit(solution)/shard_map/ppermute | solution.py:509
  7.3 1.0 constant_dynamic-slice_fusion.1
  8.3 3.0 %collective-permute-start.2 = (bf16[128,1024]{1,0:T(8,128)(2,1)S(1)}, bf16[128,1024]{1,0:T(8,128)(2,1)S(1)}, u32[]{:S(2)}, u32[]{:S(2)}) collective-permute-start(bf16[128,1024]{1,0:T(8,128)(2,1)S(1)} %constant_dynamic-slice_fusion.1), channel_id=1, source_target_pairs={{0,2},{1,3},{2,0},{3,1},{4,6},{5,7},{6,4},{7,5},{8,10},{9,11},{10,... | collective-permute-start | bytes 786440 | tf_op jit(solution)/shard_map/ppermute | solution.py:45
  11.3 3.1 %fine_tables.1.tab_hbm = bf16[5,256,256]{2,1,0:T(8,128)(2,1)} custom-call(f32[1,1024]{1,0:T(1,128)} %bitcast.35, bf16[256,1024]{1,0:T(8,128)(2,1)} %emb_ref.1, bf16[1024,256]{1,0:T(8,128)(2,1)} %wq_hbm.1, bf16[1024,256]{1,0:T(8,128)(2,1)} %wk_hbm.1, bf16[1024,256]{1,0:T(8,128)(2,1)} %wv_hbm.1), custom_call_target="tpu_custom_call" | custom-call | flops 3000000000 | bytes 6000000 | tf_op jit(solution)/shard_map/fine_tables/pallas_call | solution.py:248
  14.5 0.2 copy.22.own_ref
  14.8 0.2 copy.21.prior_ref
  15.2 12.7 %fine_attention.1 = bf16[4,272,256]{2,1,0:T(8,128)(2,1)} custom-call(s32[3]{0:T(128)S(1)} %pad_add_fusion.where_ref, s32[16,1]{1,0:T(8,128)S(1)} %copy.20.before_ref, s32[1024,1]{1,0:T(8,128)S(1)} %copy.21.prior_ref, s32[1024,1]{1,0:T(8,128)S(1)} %copy.22.own_ref, bf16[5,256,256]{2,1,0:T(8,128)(2,1)} %fine_tables.1.tab_hbm, ...), custom_call_target="tpu_custom_call" | custom-call | flops 12000000000 | bytes 24000000 | tf_op jit(solution)/shard_map/fine_attention/pallas_call | solution.py:248
  28.0 4.1 %all-to-all-start = ((bf16[4,272,256]{2,1,0:T(8,128)(2,1)}), bf16[4,272,256]{2,1,0:T(8,128)(2,1)S(1)}, u32[]{:S(2)}, u32[]{:S(2)}) async-start(bf16[4,272,256]{2,1,0:T(8,128)(2,1)} %fine_attention.1), calls=%async_computation | async-start | bytes 1114112 | tf_op jit(solution)/shard_map/all_to_all | solution.py:580
  32.4 1.3 collective-permute-done.5.t2
  33.6 8.6 %all-to-all-done.got_ref = bf16[4,272,256]{2,1,0:T(8,128)(2,1)S(1)} async-done(((bf16[4,272,256]{2,1,0:T(8,128)(2,1)}), bf16[4,272,256]{2,1,0:T(8,128)(2,1)S(1)}, u32[]{:S(2)}, u32[]{:S(2)}) %all-to-all-start) | async-done | bytes 557088 | tf_op jit(solution)/shard_map/all_to_all | solution.py:580
  42.2 2.5 %fine_rows.1 = (bf16[4,272,256]{2,1,0:T(8,128)(2,1)S(1)}, bf16[4,256,1024]{2,1,0:T(8,128)(2,1)S(1)}) custom-call(s32[3]{0:T(128)S(1)} %pad_add_fusion.where_ref, s32[272,1]{1,0:T(8,128)S(1)} %broadcast_in_dim.28.ids_ref, bf16[256,1024]{1,0:T(8,128)(2,1)S(1)} %copy-done.1, bf16[4,272,256]{2,1,0:T(8,128)(2,1)S(1)} %all-to-all-done.got_ref, ...), custom_call_target="tpu_custom_call" | custom-call | flops 2000000000 | bytes 4000000 | tf_op jit(solution)/shard_map/fine_rows/pallas_call | solution.py:248
  44.9 0.6 collective-permute-start.6
  45.5 2.1 %collective-permute-start.8 = (bf16[272,256]{1,0:T(8,128)(2,1)S(1)}, bf16[272,256]{1,0:T(8,128)(2,1)S(1)}, u32[]{:S(2)}, u32[]{:S(2)}) collective-permute-start(bf16[272,256]{1,0:T(8,128)(2,1)S(1)} %get-tuple-element.67), channel_id=1, source_target_pairs={{0,2},{1,3},{2,0},{3,1},{4,6},{5,7},{6,4},{7,5},{8,10},{9,11},{10,... | collective-permute-start | bytes 417800 | tf_op jit(solution)/shard_map/ppermute | solution.py:45
  47.6 0.7 collective-permute-start.10
  48.3 5.4 %collective-permute-done.6.group_ref.b1 = bf16[272,256]{1,0:T(8,128)(2,1)S(1)} collective-permute-done((bf16[272,256]{1,0:T(8,128)(2,1)S(1)}, bf16[272,256]{1,0:T(8,128)(2,1)S(1)}, u32[]{:S(2)}, u32[]{:S(2)}) %collective-permute-start.6) | collective-permute-done | bytes 139296 | tf_op jit(solution)/shard_map/ppermute | solution.py:45
  53.7 0.5 short_part.5
  54.3 0.5 short_part.6
  54.8 0.6 collective-permute-start.9
  55.4 0.5 short_part.7
  55.9 1.6 %collective-permute-start.11 = (bf16[64,1024]{1,0:T(8,128)(2,1)S(1)}, bf16[64,1024]{1,0:T(8,128)(2,1)S(1)}, u32[]{:S(2)}, u32[]{:S(2)}) collective-permute-start(bf16[64,1024]{1,0:T(8,128)(2,1)S(1)} %short_part.7), channel_id=1, source_target_pairs={{0,1},{1,2},{2,3},{3,0},{4,5},{5,6},{6,7},{7,4},{8,9},{9,10},{10,1... | collective-permute-start | bytes 393224 | tf_op jit(solution)/shard_map/ppermute | solution.py:45
  57.6 0.5 short_part.4
  58.1 1.2 collective-permute-done.7
  59.2 2.5 %collective-permute-done.9 = bf16[64,1024]{1,0:T(8,128)(2,1)S(1)} collective-permute-done((bf16[64,1024]{1,0:T(8,128)(2,1)S(1)}, bf16[64,1024]{1,0:T(8,128)(2,1)S(1)}, u32[]{:S(2)}, u32[]{:S(2)}) %collective-permute-start.9) | collective-permute-done | bytes 131104 | tf_op jit(solution)/shard_map/ppermute | solution.py:45
  61.7 1.6 %collective-permute-done.11 = bf16[64,1024]{1,0:T(8,128)(2,1)S(1)} collective-permute-done((bf16[64,1024]{1,0:T(8,128)(2,1)S(1)}, bf16[64,1024]{1,0:T(8,128)(2,1)S(1)}, u32[]{:S(2)}, u32[]{:S(2)}) %collective-permute-start.11) | collective-permute-done | bytes 131104 | tf_op jit(solution)/shard_map/ppermute | solution.py:45
  63.5 4.3 %collective-permute-start.13 = (bf16[64,1024]{1,0:T(8,128)(2,1)S(1)}, bf16[64,1024]{1,0:T(8,128)(2,1)S(1)}, u32[]{:S(2)}, u32[]{:S(2)}) collective-permute-start(bf16[64,1024]{1,0:T(8,128)(2,1)S(1)} %add_convert_fusion.s0), channel_id=1, source_target_pairs={{0,2},{1,3},{2,0},{3,1},{4,6},{5,7},{6,4},{7,5},{8,10},{9,11},{10,... | collective-permute-start | bytes 393224 | tf_op jit(solution)/shard_map/ppermute | solution.py:45
  67.7 0.1 collective-permute-start.14
  67.9 1.7 %collective-permute-done.12.s1 = bf16[64,1024]{1,0:T(8,128)(2,1)S(1)} collective-permute-done((bf16[64,1024]{1,0:T(8,128)(2,1)S(1)}, bf16[64,1024]{1,0:T(8,128)(2,1)S(1)}, u32[]{:S(2)}, u32[]{:S(2)}) %collective-permute-start.12) | collective-permute-done | bytes 131104 | tf_op jit(solution)/shard_map/ppermute | solution.py:45
  69.6 2.4 %collective-permute-done.13.s2 = bf16[64,1024]{1,0:T(8,128)(2,1)S(1)} collective-permute-done((bf16[64,1024]{1,0:T(8,128)(2,1)S(1)}, bf16[64,1024]{1,0:T(8,128)(2,1)S(1)}, u32[]{:S(2)}, u32[]{:S(2)}) %collective-permute-start.13) | collective-permute-done | bytes 131104 | tf_op jit(solution)/shard_map/ppermute | solution.py:45
  72.1 0.6 collective-permute-done.14.s3
  72.7 2.3 %coarse_pack.1 = (bf16[4,384,128]{2,1,0:T(8,128)(2,1)}, bf16[256,1024]{1,0:T(8,128)(2,1)S(1)}) custom-call(s32[3]{0:T(128)S(1)} %pad_add_fusion.where_ref, bf16[64,1024]{1,0:T(8,128)(2,1)S(1)} %add_convert_fusion.s0, bf16[64,1024]{1,0:T(8,128)(2,1)S(1)} %collective-permute-done.12.s1, bf16[64,1024]{1,0:T(8,128)(2,1)S(1)} %collective-permute-done.13.s2, ...), custom_call_target="tpu_custom_call" | custom-call | flops 2000000000 | bytes 4000000 | tf_op jit(solution)/shard_map/coarse_pack/pallas_call | solution.py:248
  75.0 4.9 %all-to-all-start.1 = ((bf16[4,384,128]{2,1,0:T(8,128)(2,1)}), bf16[4,384,128]{2,1,0:T(8,128)(2,1)S(1)}, u32[]{:S(2)}, u32[]{:S(2)}) async-start(bf16[4,384,128]{2,1,0:T(8,128)(2,1)} %get-tuple-element.43), calls=%async_computation.1 | async-start | bytes 786432 | tf_op jit(solution)/shard_map/all_to_all | solution.py:618
  79.9 0.4 collective-permute-start.18
  80.3 7.0 %all-to-all-done.1.turned_ref = bf16[4,384,128]{2,1,0:T(8,128)(2,1)S(1)} async-done(((bf16[4,384,128]{2,1,0:T(8,128)(2,1)}), bf16[4,384,128]{2,1,0:T(8,128)(2,1)S(1)}, u32[]{:S(2)}, u32[]{:S(2)}) %all-to-all-start.1) | async-done | bytes 393248 | tf_op jit(solution)/shard_map/all_to_all | solution.py:618
  87.5 1.6 %collective-permute-start.19 = (bf16[128,1024]{1,0:T(8,128)(2,1)S(1)}, bf16[128,1024]{1,0:T(8,128)(2,1)S(1)}, u32[]{:S(2)}, u32[]{:S(2)}) collective-permute-start(bf16[128,1024]{1,0:T(8,128)(2,1)S(1)} %constant_dynamic-slice_fusion), channel_id=1, source_target_pairs={{0,2},{1,3},{2,0},{3,1},{4,6},{5,7},{6,4},{7,5},{8,10},{9,11},{10,... | collective-permute-start | bytes 786440 | tf_op jit(solution)/shard_map/ppermute | solution.py:45
  89.1 1.8 %collective-permute-start.15 = (bf16[4,256,128]{2,1,0:T(8,128)(2,1)S(1)}, bf16[4,256,128]{2,1,0:T(8,128)(2,1)S(1)}, u32[]{:S(2)}, u32[]{:S(2)}) collective-permute-start(bf16[4,256,128]{2,1,0:T(8,128)(2,1)S(1)} %slice.14), channel_id=1, source_target_pairs={{0,16},{8,24},{16,0},{24,8},{1,17},{9,25},{17,1},{25,9},{2,18},{10... | collective-permute-start | bytes 786440 | tf_op jit(solution)/shard_map/ppermute | solution.py:45
  91.0 1.8 %collective-permute-start.16 = (bf16[4,256,128]{2,1,0:T(8,128)(2,1)S(1)}, bf16[4,256,128]{2,1,0:T(8,128)(2,1)S(1)}, u32[]{:S(2)}, u32[]{:S(2)}) collective-permute-start(bf16[4,256,128]{2,1,0:T(8,128)(2,1)S(1)} %slice.14), channel_id=1, source_target_pairs={{0,8},{8,16},{16,24},{24,0},{1,9},{9,17},{17,25},{25,1},{2,10},{10... | collective-permute-start | bytes 786440 | tf_op jit(solution)/shard_map/ppermute | solution.py:45
  92.8 0.2 collective-permute-start.17
  93.0 2.1 %coarse_first.1 = (bf16[1024,128]{1,0:T(8,128)(2,1)S(1)}, f32[1024,128]{1,0:T(8,128)S(1)}, f32[1024,128]{1,0:T(8,128)S(1)}, f32[1024,128]{1,0:T(8,128)S(1)}) custom-call(s32[6]{0:T(128)S(1)} %pad_add_fusion.1.flag_ref, bf16[4,384,128]{2,1,0:T(8,128)(2,1)S(1)} %all-to-all-done.1.turned_ref, bf16[4,256,128]{2,1,0:T(8,128)(2,1)S(1)} %collective-permute-done.20.far_ref), custom_call_target="tpu_custom_call" | custom-call | flops 3000000000 | bytes 6000000 | tf_op jit(solution)/shard_map/coarse_first/pallas_call | solution.py:248
  95.1 2.7 %collective-permute-done.19.refs_8_ = bf16[128,1024]{1,0:T(8,128)(2,1)S(1)} collective-permute-done((bf16[128,1024]{1,0:T(8,128)(2,1)S(1)}, bf16[128,1024]{1,0:T(8,128)(2,1)S(1)}, u32[]{:S(2)}, u32[]{:S(2)}) %collective-permute-start.19) | collective-permute-done | bytes 262176 | tf_op jit(solution)/shard_map/ppermute | solution.py:45
  97.8 2.0 %collective-permute-done.15.refs_0_ = bf16[4,256,128]{2,1,0:T(8,128)(2,1)S(1)} collective-permute-done((bf16[4,256,128]{2,1,0:T(8,128)(2,1)S(1)}, bf16[4,256,128]{2,1,0:T(8,128)(2,1)S(1)}, u32[]{:S(2)}, u32[]{:S(2)}) %collective-permute-start.15) | collective-permute-done | bytes 262176 | tf_op jit(solution)/shard_map/ppermute | solution.py:45
  99.8 2.9 %collective-permute-done.16.refs_0_ = bf16[4,256,128]{2,1,0:T(8,128)(2,1)S(1)} collective-permute-done((bf16[4,256,128]{2,1,0:T(8,128)(2,1)S(1)}, bf16[4,256,128]{2,1,0:T(8,128)(2,1)S(1)}, u32[]{:S(2)}, u32[]{:S(2)}) %collective-permute-start.16) | collective-permute-done | bytes 262176 | tf_op jit(solution)/shard_map/ppermute | solution.py:45
  102.7 2.0 %collective-permute-done.17.refs_2_ = bf16[4,256,128]{2,1,0:T(8,128)(2,1)S(1)} collective-permute-done((bf16[4,256,128]{2,1,0:T(8,128)(2,1)S(1)}, bf16[4,256,128]{2,1,0:T(8,128)(2,1)S(1)}, u32[]{:S(2)}, u32[]{:S(2)}) %collective-permute-start.17) | collective-permute-done | bytes 262176 | tf_op jit(solution)/shard_map/ppermute | solution.py:45
  104.7 0.5 collective-permute-start.23
  105.2 0.5 collective-permute-start.21
  105.7 0.5 collective-permute-done.22.refs_1_
  106.2 0.4 collective-permute-done.23.refs_3_
  106.6 4.8 %coarse_more.1 = (bf16[1024,1024]{1,0:T(8,128)(2,1)S(1)}, bf16[1024,1024]{1,0:T(8,128)(2,1)S(1)}, f32[1024,128]{1,0:T(8,128)S(1)}, f32[1024,128]{1,0:T(8,128)S(1)}, f32[1024,128]{1,0:T(8,128)S(1)}) custom-call(s32[6]{0:T(128)S(1)} %pad_add_fusion.1.flag_ref, bf16[4,256,128]{2,1,0:T(8,128)(2,1)S(1)} %collective-permute-done.16.refs_0_, ...), custom_call_target="tpu_custom_call" | custom-call | flops 6000000000 | bytes 12000000 | tf_op jit(solution)/shard_map/coarse_more/pallas_call | solution.py:248
  111.5 3.2 %coarse_last.1 = (bf16[1024,1024]{1,0:T(8,128)(2,1)S(1)}, bf16[16,128,128]{2,1,0:T(8,128)(2,1)S(1)}) custom-call(s32[6]{0:T(128)S(1)} %pad_add_fusion.1.flag_ref, bf16[4,256,128]{2,1,0:T(8,128)(2,1)S(1)} %collective-permute-done.15.refs_0_, bf16[4,256,128]{2,1,0:T(8,128)(2,1)S(1)} %collective-permute-done.21.refs_1_, ...), custom_call_target="tpu_custom_call" | custom-call | flops 3000000000 | bytes 6000000 | tf_op jit(solution)/shard_map/coarse_last/pallas_call | solution.py:248
  114.7 15.6 %all_to_all.15.heads_ref = bf16[16,128,128]{2,1,0:T(8,128)(2,1)S(1)} all-to-all(bf16[16,128,128]{2,1,0:T(8,128)(2,1)S(1)} %get-tuple-element.58), channel_id=1, replica_groups=mesh['z'=4,'x'=4,'core'=2,'head'=4] {'z','head'}, dimensions={0} | all-to-all | bytes 1048576 | tf_op jit(solution)/shard_map/all_to_all | solution.py:649
  130.3 2.9 %feed.1 = (bf16[4,64,1024]{2,1,0:T(8,128)(2,1)S(1)}, f32[64,1024]{1,0:T(8,128)S(1)}) custom-call(s32[3]{0:T(128)S(1)} %pad_add_fusion.where_ref, bf16[16,128,128]{2,1,0:T(8,128)(2,1)S(1)} %all_to_all.15.heads_ref, bf16[256,1024]{1,0:T(8,128)(2,1)S(1)} %get-tuple-element.59.short_ref, f32[1,1024]{1,0:T(1,128)S(1)} %bitcast.31, ...), custom_call_target="tpu_custom_call" | custom-call | flops 4000000000 | bytes 8000000 | tf_op jit(solution)/shard_map/feed/pallas_call | solution.py:248
  133.2 0.6 collective-permute-start.26
  133.9 1.4 collective-permute-start.27
  135.3 1.5 collective-permute-start.28
  136.7 4.7 %collective-permute-done.26 = bf16[64,1024]{1,0:T(8,128)(2,1)S(1)} collective-permute-done((bf16[64,1024]{1,0:T(8,128)(2,1)S(1)}, bf16[64,1024]{1,0:T(8,128)(2,1)S(1)}, u32[]{:S(2)}, u32[]{:S(2)}) %collective-permute-start.26) | collective-permute-done | bytes 131104 | tf_op jit(solution)/shard_map/ppermute | solution.py:45
  141.4 0.6 collective-permute-done.28
  142.1 1.1 collective-permute-start.29
  143.3 3.0 %collective-permute-start.30 = (bf16[64,1024]{1,0:T(8,128)(2,1)S(1)}, bf16[64,1024]{1,0:T(8,128)(2,1)S(1)}, u32[]{:S(2)}, u32[]{:S(2)}) collective-permute-start(bf16[64,1024]{1,0:T(8,128)(2,1)S(1)} %fusion.3.s0), channel_id=1, source_target_pairs={{0,2},{1,3},{2,0},{3,1},{4,6},{5,7},{6,4},{7,5},{8,10},{9,11},{10,... | collective-permute-start | bytes 393224 | tf_op jit(solution)/shard_map/ppermute | solution.py:45
  146.3 0.2 collective-permute-start.31
  146.5 0.5 copy.24
  147.0 2.8 %collective-permute-done.29.s1 = bf16[64,1024]{1,0:T(8,128)(2,1)S(1)} collective-permute-done((bf16[64,1024]{1,0:T(8,128)(2,1)S(1)}, bf16[64,1024]{1,0:T(8,128)(2,1)S(1)}, u32[]{:S(2)}, u32[]{:S(2)}) %collective-permute-start.29) | collective-permute-done | bytes 131104 | tf_op jit(solution)/shard_map/ppermute | solution.py:45
  149.8 1.7 %collective-permute-done.30.s2 = bf16[64,1024]{1,0:T(8,128)(2,1)S(1)} collective-permute-done((bf16[64,1024]{1,0:T(8,128)(2,1)S(1)}, bf16[64,1024]{1,0:T(8,128)(2,1)S(1)}, u32[]{:S(2)}, u32[]{:S(2)}) %collective-permute-start.30) | collective-permute-done | bytes 131104 | tf_op jit(solution)/shard_map/ppermute | solution.py:45
  151.5 2.7 %final.1 = bf16[1024,256]{1,0:T(8,128)(2,1)} custom-call(s32[3]{0:T(128)S(1)} %pad_add_fusion.where_ref, bf16[64,1024]{1,0:T(8,128)(2,1)S(1)} %fusion.3.s0, bf16[64,1024]{1,0:T(8,128)(2,1)S(1)} %collective-permute-done.29.s1, bf16[64,1024]{1,0:T(8,128)(2,1)S(1)} %collective-permute-done.30.s2, bf16[64,1024]{1,0:T(8,128)(2,1)S(1)} %collective-permute-done.31.s3, ...), custom_call_target="tpu_custom_call" | custom-call | flops 2000000000 | bytes 4000000 | tf_op jit(solution)/shard_map/final/pallas_call | solution.py:248
  (58 shorter events, 1.4 us)
Async XLA Ops:
  0.0 14.8 %collective-permute-start = (s32[1024]{0:T(1024)}, s32[1024]{0:T(1024)S(1)}, u32[]{:S(2)}, u32[]{:S(2)}) collective-permute-start(s32[1024]{0:T(1024)} %param.18), channel_id=1, source_target_pairs={{0,4},{4,8},{8,12},{12,16},{16,20},{20,24},{24,28},{28,32},{32,36}... | collective-permute-start | bytes 12296 | tf_op jit(solution)/shard_map/ppermute | solution.py:49
  1.9 13.1 %collective-permute-start.3 = (s32[1024]{0:T(1024)}, s32[1024]{0:T(1024)S(1)}, u32[]{:S(2)}, u32[]{:S(2)}) collective-permute-start(s32[1024]{0:T(1024)} %param.18), channel_id=1, source_target_pairs={{0,8},{4,12},{8,16},{12,20},{16,24},{20,28},{24,32},{28,36},{32,40... | collective-permute-start | bytes 12296 | tf_op jit(solution)/shard_map/ppermute | solution.py:49
  5.7 22.2 %collective-permute-start.1 = (bf16[256,1024]{1,0:T(8,128)(2,1)}, bf16[256,1024]{1,0:T(8,128)(2,1)S(1)}, u32[]{:S(2)}, u32[]{:S(2)}) collective-permute-start(bf16[256,1024]{1,0:T(8,128)(2,1)} %own_ref.1), channel_id=1, source_target_pairs={{0,1},{1,2},{2,3},{3,0},{4,7},{5,4},{6,5},{7,6},{8,9},{9,10},{10,1... | collective-permute-start | bytes 1572872 | tf_op jit(solution)/shard_map/ppermute | solution.py:509
  8.3 19.6 %collective-permute-start.2 = (bf16[128,1024]{1,0:T(8,128)(2,1)S(1)}, bf16[128,1024]{1,0:T(8,128)(2,1)S(1)}, u32[]{:S(2)}, u32[]{:S(2)}) collective-permute-start(bf16[128,1024]{1,0:T(8,128)(2,1)S(1)} %constant_dynamic-slice_fusion.1), channel_id=1, source_target_pairs={{0,2},{1,3},{2,0},{3,1},{4,6},{5,7},{6,4},{7,5},{8,10},{9,11},{10,... | collective-permute-start | bytes 786440 | tf_op jit(solution)/shard_map/ppermute | solution.py:45
  11.3 3.2 %copy-start.10 = (s32[1024]{0:T(1024)S(1)}, s32[1024]{0:T(1024)}, u32[]{:S(2)}) copy-start(s32[1024]{0:T(1024)} %param.18) | copy-start | bytes 12292
  15.2 27.1 %copy-start = (bf16[256,1024]{1,0:T(8,128)(2,1)S(1)}, bf16[256,1024]{1,0:T(8,128)(2,1)}, u32[]{:S(2)}) copy-start(bf16[256,1024]{1,0:T(8,128)(2,1)} %own_ref.1) | copy-start | bytes 1572868
  15.2 27.1 %copy-start.1 = (bf16[256,1024]{1,0:T(8,128)(2,1)S(1)}, bf16[256,1024]{1,0:T(8,128)(2,1)}, u32[]{:S(2)}) copy-start(bf16[256,1024]{1,0:T(8,128)(2,1)} %emb_ref.1) | copy-start | bytes 1572868
  27.9 14.3 %collective-permute-start.4 = (bf16[256,1024]{1,0:T(8,128)(2,1)S(1)}, bf16[256,1024]{1,0:T(8,128)(2,1)S(1)}, u32[]{:S(2)}, u32[]{:S(2)}) collective-permute-start(bf16[256,1024]{1,0:T(8,128)(2,1)S(1)} %collective-permute-done.1.m1), channel_id=1, source_target_pairs={{0,4},{4,0},{1,5},{5,1},{2,6},{6,2},{3,7},{7,3},{8,12},{12,8},{9,1... | collective-permute-start | bytes 1572872 | tf_op jit(solution)/shard_map/ppermute | solution.py:45
  28.0 14.2 %all-to-all-start = ((bf16[4,272,256]{2,1,0:T(8,128)(2,1)}), bf16[4,272,256]{2,1,0:T(8,128)(2,1)S(1)}, u32[]{:S(2)}, u32[]{:S(2)}) async-start(bf16[4,272,256]{2,1,0:T(8,128)(2,1)} %fine_attention.1), calls=%async_computation | async-start | bytes 1114112 | tf_op jit(solution)/shard_map/all_to_all | solution.py:580
  32.1 1.5 collective-permute-start.5
  44.9 8.8 %collective-permute-start.6 = (bf16[272,256]{1,0:T(8,128)(2,1)S(1)}, bf16[272,256]{1,0:T(8,128)(2,1)S(1)}, u32[]{:S(2)}, u32[]{:S(2)}) collective-permute-start(bf16[272,256]{1,0:T(8,128)(2,1)S(1)} %get-tuple-element.68), channel_id=1, source_target_pairs={{0,1},{1,2},{2,3},{3,0},{4,5},{5,6},{6,7},{7,4},{8,9},{9,10},{10,1... | collective-permute-start | bytes 417800 | tf_op jit(solution)/shard_map/ppermute | solution.py:45
  45.5 8.8 %collective-permute-start.8 = (bf16[272,256]{1,0:T(8,128)(2,1)S(1)}, bf16[272,256]{1,0:T(8,128)(2,1)S(1)}, u32[]{:S(2)}, u32[]{:S(2)}) collective-permute-start(bf16[272,256]{1,0:T(8,128)(2,1)S(1)} %get-tuple-element.67), channel_id=1, source_target_pairs={{0,2},{1,3},{2,0},{3,1},{4,6},{5,7},{6,4},{7,5},{8,10},{9,11},{10,... | collective-permute-start | bytes 417800 | tf_op jit(solution)/shard_map/ppermute | solution.py:45
  47.6 7.9 %collective-permute-start.10 = (bf16[272,256]{1,0:T(8,128)(2,1)S(1)}, bf16[272,256]{1,0:T(8,128)(2,1)S(1)}, u32[]{:S(2)}, u32[]{:S(2)}) collective-permute-start(bf16[272,256]{1,0:T(8,128)(2,1)S(1)} %get-tuple-element.66), channel_id=1, source_target_pairs={{0,3},{1,0},{2,1},{3,2},{4,7},{5,4},{6,5},{7,6},{8,11},{9,8},{10,9... | collective-permute-start | bytes 417800 | tf_op jit(solution)/shard_map/ppermute | solution.py:45
  54.2 5.0 %collective-permute-start.7 = (bf16[64,1024]{1,0:T(8,128)(2,1)S(1)}, bf16[64,1024]{1,0:T(8,128)(2,1)S(1)}, u32[]{:S(2)}, u32[]{:S(2)}) collective-permute-start(bf16[64,1024]{1,0:T(8,128)(2,1)S(1)} %short_part.5), channel_id=1, source_target_pairs={{0,3},{1,0},{2,1},{3,2},{4,7},{5,4},{6,5},{7,6},{8,11},{9,8},{10,9... | collective-permute-start | bytes 393224 | tf_op jit(solution)/shard_map/ppermute | solution.py:45
  54.8 7.0 %collective-permute-start.9 = (bf16[64,1024]{1,0:T(8,128)(2,1)S(1)}, bf16[64,1024]{1,0:T(8,128)(2,1)S(1)}, u32[]{:S(2)}, u32[]{:S(2)}) collective-permute-start(bf16[64,1024]{1,0:T(8,128)(2,1)S(1)} %short_part.6), channel_id=1, source_target_pairs={{0,2},{1,3},{2,0},{3,1},{4,6},{5,7},{6,4},{7,5},{8,10},{9,11},{10,... | collective-permute-start | bytes 393224 | tf_op jit(solution)/shard_map/ppermute | solution.py:45
  55.9 7.4 %collective-permute-start.11 = (bf16[64,1024]{1,0:T(8,128)(2,1)S(1)}, bf16[64,1024]{1,0:T(8,128)(2,1)S(1)}, u32[]{:S(2)}, u32[]{:S(2)}) collective-permute-start(bf16[64,1024]{1,0:T(8,128)(2,1)S(1)} %short_part.7), channel_id=1, source_target_pairs={{0,1},{1,2},{2,3},{3,0},{4,5},{5,6},{6,7},{7,4},{8,9},{9,10},{10,1... | collective-permute-start | bytes 393224 | tf_op jit(solution)/shard_map/ppermute | solution.py:45
  57.5 15.2 %copy-start.2 = (bf16[1024,256]{1,0:T(8,128)(2,1)S(1)}, bf16[1024,256]{1,0:T(8,128)(2,1)}, u32[]{:S(2)}) copy-start(bf16[1024,256]{1,0:T(8,128)(2,1)} %wq_ref.1) | copy-start | bytes 1572868
  57.5 15.2 %copy-start.3 = (bf16[1024,256]{1,0:T(8,128)(2,1)S(1)}, bf16[1024,256]{1,0:T(8,128)(2,1)}, u32[]{:S(2)}) copy-start(bf16[1024,256]{1,0:T(8,128)(2,1)} %wk_ref.1) | copy-start | bytes 1572868
  57.5 15.2 %copy-start.4 = (bf16[1024,256]{1,0:T(8,128)(2,1)S(1)}, bf16[1024,256]{1,0:T(8,128)(2,1)}, u32[]{:S(2)}) copy-start(bf16[1024,256]{1,0:T(8,128)(2,1)} %wv_ref.1) | copy-start | bytes 1572868
  57.6 15.2 %copy-start.5 = (f32[1024]{0:T(1024)S(1)}, f32[1024]{0:T(1024)}, u32[]{:S(2)}) copy-start(f32[1024]{0:T(1024)} %param.26) | copy-start | bytes 12292
  57.6 15.2 %copy-start.7 = (f32[576,128]{1,0:T(8,128)S(1)}, f32[576,128]{1,0:T(8,128)}, u32[]{:S(2)}) copy-start(f32[576,128]{1,0:T(8,128)} %constant.90.clone.turn_hbm.turn_ref) | copy-start | bytes 884740
  63.4 6.2 %collective-permute-start.12 = (bf16[64,1024]{1,0:T(8,128)(2,1)S(1)}, bf16[64,1024]{1,0:T(8,128)(2,1)S(1)}, u32[]{:S(2)}, u32[]{:S(2)}) collective-permute-start(bf16[64,1024]{1,0:T(8,128)(2,1)S(1)} %add_convert_fusion.s0), channel_id=1, source_target_pairs={{0,1},{1,2},{2,3},{3,0},{4,5},{5,6},{6,7},{7,4},{8,9},{9,10},{10,1... | collective-permute-start | bytes 393224 | tf_op jit(solution)/shard_map/ppermute | solution.py:45
  63.5 8.6 %collective-permute-start.13 = (bf16[64,1024]{1,0:T(8,128)(2,1)S(1)}, bf16[64,1024]{1,0:T(8,128)(2,1)S(1)}, u32[]{:S(2)}, u32[]{:S(2)}) collective-permute-start(bf16[64,1024]{1,0:T(8,128)(2,1)S(1)} %add_convert_fusion.s0), channel_id=1, source_target_pairs={{0,2},{1,3},{2,0},{3,1},{4,6},{5,7},{6,4},{7,5},{8,10},{9,11},{10,... | collective-permute-start | bytes 393224 | tf_op jit(solution)/shard_map/ppermute | solution.py:45
  67.7 5.0 %collective-permute-start.14 = (bf16[64,1024]{1,0:T(8,128)(2,1)S(1)}, bf16[64,1024]{1,0:T(8,128)(2,1)S(1)}, u32[]{:S(2)}, u32[]{:S(2)}) collective-permute-start(bf16[64,1024]{1,0:T(8,128)(2,1)S(1)} %add_convert_fusion.s0), channel_id=1, source_target_pairs={{0,3},{1,0},{2,1},{3,2},{4,7},{5,4},{6,5},{7,6},{8,11},{9,8},{10,9... | collective-permute-start | bytes 393224 | tf_op jit(solution)/shard_map/ppermute | solution.py:45
  72.7 7.2 %copy-start.9 = (bf16[256,1024]{1,0:T(8,128)(2,1)S(1)}, bf16[256,1024]{1,0:T(8,128)(2,1)}, u32[]{:S(2)}) copy-start(bf16[256,1024]{1,0:T(8,128)(2,1)} %refs_6_.1) | copy-start | bytes 1572868
  75.0 12.2 %all-to-all-start.1 = ((bf16[4,384,128]{2,1,0:T(8,128)(2,1)}), bf16[4,384,128]{2,1,0:T(8,128)(2,1)S(1)}, u32[]{:S(2)}, u32[]{:S(2)}) async-start(bf16[4,384,128]{2,1,0:T(8,128)(2,1)} %get-tuple-element.43), calls=%async_computation.1 | async-start | bytes 786432 | tf_op jit(solution)/shard_map/all_to_all | solution.py:618
  79.9 17.9 %collective-permute-start.18 = (bf16[256,1024]{1,0:T(8,128)(2,1)S(1)}, bf16[256,1024]{1,0:T(8,128)(2,1)S(1)}, u32[]{:S(2)}, u32[]{:S(2)}) collective-permute-start(bf16[256,1024]{1,0:T(8,128)(2,1)S(1)} %copy-done.9), channel_id=1, source_target_pairs={{0,1},{1,2},{2,3},{3,0},{4,7},{5,4},{6,5},{7,6},{8,9},{9,10},{10,1... | collective-permute-start | bytes 1572872 | tf_op jit(solution)/shard_map/ppermute | solution.py:509
  87.3 5.5 %collective-permute-start.20 = (bf16[4,256,128]{2,1,0:T(8,128)(2,1)S(1)}, bf16[4,256,128]{2,1,0:T(8,128)(2,1)S(1)}, u32[]{:S(2)}, u32[]{:S(2)}) collective-permute-start(bf16[4,256,128]{2,1,0:T(8,128)(2,1)S(1)} %slice.14), channel_id=1, source_target_pairs={{0,4},{4,0},{1,5},{5,1},{2,6},{6,2},{3,7},{7,3},{8,12},{12,8},{9,1... | collective-permute-start | bytes 786440 | tf_op jit(solution)/shard_map/ppermute | solution.py:45
  87.5 10.3 %collective-permute-start.19 = (bf16[128,1024]{1,0:T(8,128)(2,1)S(1)}, bf16[128,1024]{1,0:T(8,128)(2,1)S(1)}, u32[]{:S(2)}, u32[]{:S(2)}) collective-permute-start(bf16[128,1024]{1,0:T(8,128)(2,1)S(1)} %constant_dynamic-slice_fusion), channel_id=1, source_target_pairs={{0,2},{1,3},{2,0},{3,1},{4,6},{5,7},{6,4},{7,5},{8,10},{9,11},{10,... | collective-permute-start | bytes 786440 | tf_op jit(solution)/shard_map/ppermute | solution.py:45
  89.1 10.7 %collective-permute-start.15 = (bf16[4,256,128]{2,1,0:T(8,128)(2,1)S(1)}, bf16[4,256,128]{2,1,0:T(8,128)(2,1)S(1)}, u32[]{:S(2)}, u32[]{:S(2)}) collective-permute-start(bf16[4,256,128]{2,1,0:T(8,128)(2,1)S(1)} %slice.14), channel_id=1, source_target_pairs={{0,16},{8,24},{16,0},{24,8},{1,17},{9,25},{17,1},{25,9},{2,18},{10... | collective-permute-start | bytes 786440 | tf_op jit(solution)/shard_map/ppermute | solution.py:45
  91.0 11.7 %collective-permute-start.16 = (bf16[4,256,128]{2,1,0:T(8,128)(2,1)S(1)}, bf16[4,256,128]{2,1,0:T(8,128)(2,1)S(1)}, u32[]{:S(2)}, u32[]{:S(2)}) collective-permute-start(bf16[4,256,128]{2,1,0:T(8,128)(2,1)S(1)} %slice.14), channel_id=1, source_target_pairs={{0,8},{8,16},{16,24},{24,0},{1,9},{9,17},{17,25},{25,1},{2,10},{10... | collective-permute-start | bytes 786440 | tf_op jit(solution)/shard_map/ppermute | solution.py:45
  92.8 11.9 %collective-permute-start.17 = (bf16[4,256,128]{2,1,0:T(8,128)(2,1)S(1)}, bf16[4,256,128]{2,1,0:T(8,128)(2,1)S(1)}, u32[]{:S(2)}, u32[]{:S(2)}) collective-permute-start(bf16[4,256,128]{2,1,0:T(8,128)(2,1)S(1)} %slice.14), channel_id=1, source_target_pairs={{0,24},{8,0},{16,8},{24,16},{1,25},{9,1},{17,9},{25,17},{2,26},{10... | collective-permute-start | bytes 786440 | tf_op jit(solution)/shard_map/ppermute | solution.py:45
  104.7 1.5 collective-permute-start.22
  104.7 1.9 %collective-permute-start.23 = (bf16[4,256,128]{2,1,0:T(8,128)(2,1)S(1)}, bf16[4,256,128]{2,1,0:T(8,128)(2,1)S(1)}, u32[]{:S(2)}, u32[]{:S(2)}) collective-permute-start(bf16[4,256,128]{2,1,0:T(8,128)(2,1)S(1)} %collective-permute-done.17.refs_2_), channel_id=1, source_target_pairs={{0,4},{4,0},{1,5},{5,1},{2,6},{6,2},{3,7},{7,3},{8,12},{12,8},{9,1... | collective-permute-start | bytes 786440 | tf_op jit(solution)/shard_map/ppermute | solution.py:45
  105.2 6.3 %collective-permute-start.24 = (bf16[256,1024]{1,0:T(8,128)(2,1)S(1)}, bf16[256,1024]{1,0:T(8,128)(2,1)S(1)}, u32[]{:S(2)}, u32[]{:S(2)}) collective-permute-start(bf16[256,1024]{1,0:T(8,128)(2,1)S(1)} %collective-permute-done.18.refs_7_), channel_id=1, source_target_pairs={{0,4},{4,0},{1,5},{5,1},{2,6},{6,2},{3,7},{7,3},{8,12},{12,8},{9,1... | collective-permute-start | bytes 1572872 | tf_op jit(solution)/shard_map/ppermute | solution.py:45
  105.2 6.2 %collective-permute-start.21 = (bf16[4,256,128]{2,1,0:T(8,128)(2,1)S(1)}, bf16[4,256,128]{2,1,0:T(8,128)(2,1)S(1)}, u32[]{:S(2)}, u32[]{:S(2)}) collective-permute-start(bf16[4,256,128]{2,1,0:T(8,128)(2,1)S(1)} %collective-permute-done.15.refs_0_), channel_id=1, source_target_pairs={{0,4},{4,0},{1,5},{5,1},{2,6},{6,2},{3,7},{7,3},{8,12},{12,8},{9,1... | collective-permute-start | bytes 786440 | tf_op jit(solution)/shard_map/ppermute | solution.py:45
  105.7 5.7 %collective-permute-start.25 = (bf16[128,1024]{1,0:T(8,128)(2,1)S(1)}, bf16[128,1024]{1,0:T(8,128)(2,1)S(1)}, u32[]{:S(2)}, u32[]{:S(2)}) collective-permute-start(bf16[128,1024]{1,0:T(8,128)(2,1)S(1)} %collective-permute-done.19.refs_8_), channel_id=1, source_target_pairs={{0,4},{4,0},{1,5},{5,1},{2,6},{6,2},{3,7},{7,3},{8,12},{12,8},{9,1... | collective-permute-start | bytes 786440 | tf_op jit(solution)/shard_map/ppermute | solution.py:45
  111.4 18.8 %copy-start.6 = (f32[1024]{0:T(1024)S(1)}, f32[1024]{0:T(1024)}, u32[]{:S(2)}) copy-start(f32[1024]{0:T(1024)} %param.31) | copy-start | bytes 12292
  130.3 16.2 %copy-start.8 = (bf16[1024,4,256]{2,1,0:T(4,128)(2,1)S(1)}, bf16[1024,4,256]{2,1,0:T(4,128)(2,1)}, u32[]{:S(2)}) copy-start(bf16[1024,4,256]{2,1,0:T(4,128)(2,1)} %param.34) | copy-start | bytes 6291460
  133.2 8.2 %collective-permute-start.26 = (bf16[64,1024]{1,0:T(8,128)(2,1)S(1)}, bf16[64,1024]{1,0:T(8,128)(2,1)S(1)}, u32[]{:S(2)}, u32[]{:S(2)}) collective-permute-start(bf16[64,1024]{1,0:T(8,128)(2,1)S(1)} %get-tuple-element.69), channel_id=1, source_target_pairs={{0,1},{1,2},{2,3},{3,0},{4,5},{5,6},{6,7},{7,4},{8,9},{9,10},{10,1... | collective-permute-start | bytes 393224 | tf_op jit(solution)/shard_map/ppermute | solution.py:45
  133.9 7.6 %collective-permute-start.27 = (bf16[64,1024]{1,0:T(8,128)(2,1)S(1)}, bf16[64,1024]{1,0:T(8,128)(2,1)S(1)}, u32[]{:S(2)}, u32[]{:S(2)}) collective-permute-start(bf16[64,1024]{1,0:T(8,128)(2,1)S(1)} %get-tuple-element.71), channel_id=1, source_target_pairs={{0,2},{1,3},{2,0},{3,1},{4,6},{5,7},{6,4},{7,5},{8,10},{9,11},{10,... | collective-permute-start | bytes 393224 | tf_op jit(solution)/shard_map/ppermute | solution.py:45
  135.3 6.8 %collective-permute-start.28 = (bf16[64,1024]{1,0:T(8,128)(2,1)S(1)}, bf16[64,1024]{1,0:T(8,128)(2,1)S(1)}, u32[]{:S(2)}, u32[]{:S(2)}) collective-permute-start(bf16[64,1024]{1,0:T(8,128)(2,1)S(1)} %get-tuple-element.70), channel_id=1, source_target_pairs={{0,3},{1,0},{2,1},{3,2},{4,7},{5,4},{6,5},{7,6},{8,11},{9,8},{10,9... | collective-permute-start | bytes 393224 | tf_op jit(solution)/shard_map/ppermute | solution.py:45
  142.1 7.7 %collective-permute-start.29 = (bf16[64,1024]{1,0:T(8,128)(2,1)S(1)}, bf16[64,1024]{1,0:T(8,128)(2,1)S(1)}, u32[]{:S(2)}, u32[]{:S(2)}) collective-permute-start(bf16[64,1024]{1,0:T(8,128)(2,1)S(1)} %fusion.3.s0), channel_id=1, source_target_pairs={{0,1},{1,2},{2,3},{3,0},{4,5},{5,6},{6,7},{7,4},{8,9},{9,10},{10,1... | collective-permute-start | bytes 393224 | tf_op jit(solution)/shard_map/ppermute | solution.py:45
  143.3 8.2 %collective-permute-start.30 = (bf16[64,1024]{1,0:T(8,128)(2,1)S(1)}, bf16[64,1024]{1,0:T(8,128)(2,1)S(1)}, u32[]{:S(2)}, u32[]{:S(2)}) collective-permute-start(bf16[64,1024]{1,0:T(8,128)(2,1)S(1)} %fusion.3.s0), channel_id=1, source_target_pairs={{0,2},{1,3},{2,0},{3,1},{4,6},{5,7},{6,4},{7,5},{8,10},{9,11},{10,... | collective-permute-start | bytes 393224 | tf_op jit(solution)/shard_map/ppermute | solution.py:45
  146.3 5.2 %collective-permute-start.31 = (bf16[64,1024]{1,0:T(8,128)(2,1)S(1)}, bf16[64,1024]{1,0:T(8,128)(2,1)S(1)}, u32[]{:S(2)}, u32[]{:S(2)}) collective-permute-start(bf16[64,1024]{1,0:T(8,128)(2,1)S(1)} %fusion.3.s0), channel_id=1, source_target_pairs={{0,3},{1,0},{2,1},{3,2},{4,7},{5,4},{6,5},{7,6},{8,11},{9,8},{10,9... | collective-permute-start | bytes 393224 | tf_op jit(solution)/shard_map/ppermute | solution.py:45

commit v9 on v8

--- a/solution.py
+++ b/solution.py
@@ -103,22 +103,28 @@
     return (dot(hot, tab_ref[n]) * cosine + dot(hot, tab_ref[n + 1]) * sine).astype(bf16)
 
 
-def fine_tables_kernel(gain_hbm, emb_hbm, wq_hbm, wk_hbm, wv_hbm, tab_hbm, tab_ref, gain_ref, emb_ref, w_ref, sems):
+def fine_tables_kernel(
+    where_ref, gain_hbm, emb_hbm, wq_hbm, wk_hbm, wv_hbm, fo_hbm,
+    tab_hbm, fo_half, tab_ref, gain_ref, emb_ref, w_ref, sems,
+):
     pairs = [(emb_hbm, emb_ref), (gain_hbm, gain_ref)]
     for n, w in enumerate((wq_hbm, wk_hbm, wv_hbm)):
         for part in range(2):
             rows = pl.ds(part * 512, 512)
             pairs.append((w.at[rows], w_ref.at[n, rows]))
+    half = pl.ds(pl.multiple_of(where_ref[2] * 128, 128), 128)
+    pairs.append((fo_hbm.at[half], fo_half))
     copies = begin_copies(pairs, sems)
     finish_copies(copies[:2])
     fine_in = norm_rows(emb_ref[...].astype(f32), gain_ref[...])
-    finish_copies(copies[2:])
+    finish_copies(copies[2:8])
     tq = dot(fine_in, w_ref[0]) * q_scale
     tk = dot(fine_in, w_ref[1])
     tables = (tq, partner(tq), tk, partner(tk), dot(fine_in, w_ref[2]))
     for n, table in enumerate(tables):
         tab_ref[n] = table.astype(bf16)
     finish_copies(begin_copies([(tab_ref.at[n], tab_hbm.at[n]) for n in range(5)], sems))
+    finish_copies(copies[8:])
 
 
 def fine_kernel(
@@ -180,53 +186,54 @@
             result = jnp.where(head_lane == h, mixed[h * HALO : (h + 1) * HALO], result)
         out_ref[0, 0:HALO, :] = result.astype(bf16)
 
-    begin = pl.multiple_of((step + 1) * BLOCK, BLOCK)
-    keys = k_ref[pl.ds(begin, PAST), :]
-    values = v_ref[pl.ds(begin, PAST), :]
-    query = q_ref[pl.ds(begin, BLOCK), :]
-    row = lax.broadcasted_iota(jnp.int32, (BLOCK, BLOCK), 0)
-    col = lax.broadcasted_iota(jnp.int32, (BLOCK, BLOCK), 1)
-    biases = [
-        jnp.where(begin + t * BLOCK >= lowest, 0.0, masked_low).astype(f32) for t in range(4)
-    ]
-    first_bias = jnp.where(col > row, 0.0, masked_low) + biases[0]
-    last_bias = jnp.where(col <= row, 0.0, masked_low)
-    ones = jnp.ones((PAST, 128), bf16)
-    low_lanes = lax.broadcasted_iota(jnp.int32, (1, 128), 1) < 64
-    results = []
-
-    def score(h):
-        return dot_t(jnp.where(head_lane == h, query, jnp.zeros_like(query)), keys)
-
-    ahead = score(0)
-    for h in range(4):
-        scores = ahead
-        if h < 3:
-            ahead = score(h + 1)
-        tiles = [scores[:, t * BLOCK : (t + 1) * BLOCK] for t in range(5)]
-        tiles = (
-            [tiles[0] + first_bias]
-            + [tiles[t] + biases[t] for t in range(1, 4)]
-            + [tiles[4] + last_bias]
+    for late in range(2):
+        place = 2 * step + late
+        begin = pl.multiple_of((place + 1) * BLOCK, BLOCK)
+        keys = k_ref[pl.ds(begin, PAST), :]
+        values = v_ref[pl.ds(begin, PAST), :]
+        query = q_ref[pl.ds(begin, BLOCK), :]
+        row = lax.broadcasted_iota(jnp.int32, (BLOCK, BLOCK), 0)
+        col = lax.broadcasted_iota(jnp.int32, (BLOCK, BLOCK), 1)
+        biases = [
+            jnp.where(begin + t * BLOCK >= lowest, 0.0, masked_low).astype(f32) for t in range(4)
+        ]
+        inside = col <= row
+        ones = jnp.ones((PAST, 128), bf16)
+        low_lanes = lax.broadcasted_iota(jnp.int32, (1, 128), 1) < 64
+        results = []
+
+        def score(h):
+            return dot_t(jnp.where(head_lane == h, query, jnp.zeros_like(query)), keys)
+
+        ahead = score(0)
+        for h in range(4):
+            scores = ahead
+            if h < 3:
+                ahead = score(h + 1)
+            tiles = [scores[:, t * BLOCK : (t + 1) * BLOCK] for t in range(5)]
+            edge = jnp.where(inside, tiles[4], tiles[0] + biases[0])
+            middle = [tiles[t] + biases[t] for t in range(1, 4)]
+            peak = edge
+            for tile in middle:
+                peak = jnp.maximum(peak, tile)
+            top = jnp.max(peak, axis=1, keepdims=True)
+            edge = jnp.exp2(edge - top).astype(bf16)
+            none = jnp.zeros_like(edge)
+            weights = [jnp.exp2(tile - top).astype(bf16) for tile in middle]
+            weights = [jnp.where(inside, none, edge), *weights, jnp.where(inside, edge, none)]
+            pair = (h // 2) * 128
+            wide = jnp.concatenate([values[:, pair : pair + 128], ones], axis=1)
+            mixed = dot(jnp.concatenate(weights, axis=1), wide)
+            results.append(mixed[:, :128] / mixed[:, 128:])
+        result = jnp.concatenate(
+            [jnp.where(low_lanes, results[2 * n], results[2 * n + 1]) for n in range(2)], axis=1
         )
-        peak = tiles[0]
-        for t in range(1, 5):
-            peak = jnp.maximum(peak, tiles[t])
-        top = jnp.max(peak, axis=1, keepdims=True)
-        weights = [jnp.exp2(tile - top).astype(bf16) for tile in tiles]
-        pair = (h // 2) * 128
-        wide = jnp.concatenate([values[:, pair : pair + 128], ones], axis=1)
-        mixed = dot(jnp.concatenate(weights, axis=1), wide)
-        results.append(mixed[:, :128] / mixed[:, 128:])
-    result = jnp.concatenate(
-        [jnp.where(low_lanes, results[2 * n], results[2 * n + 1]) for n in range(2)], axis=1
-    )
-    result = result.astype(bf16)
-    out_ref[step, HALO:, :] = result
-
-    @pl.when(step < 3)
-    def _():
-        out_ref[step + 1, 0:HALO, :] = result[BLOCK - HALO :]
+        result = result.astype(bf16)
+        out_ref[place, HALO:, :] = result
+
+        @pl.when(place < 3)
+        def _():
+            out_ref[place + 1, 0:HALO, :] = result[BLOCK - HALO :]
 
 
 def vmem():
@@ -502,13 +509,12 @@
         out_ref[pl.ds(begin, 256), :] = dot(weave, value).astype(bf16)
 
 
-def fetch_rest(weight, core):
+def fetch_rest(weight, half):
     pairs = []
     for c, step in ((0, 1), (1, 3)):
         pairs += [(4 * c + y, 4 * c + (y + step) % 4) for y in range(4)]
     whole = lax.ppermute(weight, ("core", "head"), pairs)
-    half = shift(lax.dynamic_slice_in_dim(weight, core * 128, 128, 0), "head", 2, 4)
-    return [whole, half]
+    return [whole, shift(half, "head", 2, 4)]
 
 
 def swap_cores(parts):
@@ -551,18 +557,22 @@
 
     prior = later(token_ids, SEQ, 1, 32)
     before = later(token_ids, SEQ, 2, 32)[ROWS - HALO :]
-    tab = call(
-        fine_tables_kernel, "fine_tables", pltpu.HBM((5, 256, SHARE), bf16), [], [],
+    tab, fo_half = call(
+        fine_tables_kernel, "fine_tables",
+        [pltpu.HBM((5, 256, SHARE), bf16), pltpu.HBM((128, D), bf16)], [where], [],
         [
             pltpu.VMEM((5, 256, SHARE), bf16),
             pltpu.VMEM((1, D), f32), pltpu.VMEM((256, D), bf16),
             pltpu.VMEM((3, D, SHARE), bf16), pltpu.SemaphoreType.DMA((9,)),
         ],
-        us=3, hbm=[fine_norm[None], embedding, fine_query, fine_key, fine_value],
+        us=3, hbm=[
+            fine_norm[None], embedding, fine_query, fine_key, fine_value,
+            fine_output,
+        ],
     )
     own_ids_column = token_ids[:, None]
     fine_output_held, own_ids_column = after(fine_output, own_ids_column)
-    out_mine = fetch_rest(fine_output_held, core)
+    out_mine = fetch_rest(fine_output_held, fo_half)
     rows = 256 + HALO
     mixed = call(
         fine_kernel, "fine_attention", jax.ShapeDtypeStruct((4, rows, SHARE), bf16),
@@ -573,7 +583,7 @@
             pltpu.VMEM((5, 256, SHARE), bf16), pltpu.VMEM((576, 128), f32),
             pltpu.SemaphoreType.DMA((10,)),
         ],
-        grid=(4,), us=12, limit=24, hbm=[tab, tables],
+        grid=(2,), us=12, limit=24, hbm=[tab, tables],
     )
 
     out_mine, mixed = after(out_mine, mixed)
@@ -614,7 +624,8 @@
     )
 
     coarse_output_held, packed = after(coarse_output, packed)
-    co_mine = fetch_rest(coarse_output_held, core)
+    co_half = lax.dynamic_slice_in_dim(coarse_output_held, core * 128, 128, 0)
+    co_mine = fetch_rest(coarse_output_held, co_half)
     turned = lax.all_to_all(packed, "z", 0, 0)
     kv = turned[:, :COARSE_ROWS]
     far = [shift(kv, "core", 1, 2)]

time: 155 us -> 161 us (1.039)
  Pallas kernels: 38.3 us -> 44.5 us
    pallas_call x13, Pallas kernels: 38.3 us -> 44.5 us  [call(): pl.pallas_call(kernel, out_shape=shapes, in_specs=[smem()] * len(scalars)...]
  transfers between devices with their start and end apart: 34 -> 34, of which waited for: 21 -> 21; matrix products, arithmetic and copies ran while one was open for 2% -> 2% of each run, Pallas kernels for 16% -> 19%
where the time goes in v9:
time: 161 us
  waiting for transfers between devices  53.2 us (33%)
  Pallas kernels  44.5 us (28%)
  starting transfers between devices  44.3 us (28%)
  blocking collectives  15.6 us (10%)
  local copies, waits for them, and re-layouts  2.38 us (1%)
    pallas_call x13, Pallas kernels, call(): pl.pallas_call(kernel, out_shape=shapes, in_specs=[smem()] * len(scalars)...  44.5 us
    ppermute x28, waiting for transfers between devices, shift(): lax.ppermute(value, axis, [(i, (i + steps) % count) for i in range(count)])  37.5 us
    ppermute x28, starting transfers between devices, shift(): lax.ppermute(value, axis, [(i, (i + steps) % count) for i in range(count)])  29.2 us
    all_to_all x1, blocking collectives, local(): heads_in = lax.all_to_all(wide_sends, ('z', 'head'), 0, 0)  15.6 us
    all_to_all x1, waiting for transfers between devices, local(): got = lax.all_to_all(mixed, 'head', 0, 0)  8.65 us
    all_to_all x1, waiting for transfers between devices, local(): turned = lax.all_to_all(packed, 'z', 0, 0)  7.01 us
    ppermute x2, starting transfers between devices, later(): lax.ppermute(value, axis, [(i, i + steps) for i in range(count - steps)])  5.65 us
    all_to_all x1, starting transfers between devices, local(): turned = lax.all_to_all(packed, 'z', 0, 0)  4.85 us
  transfers between devices with their start and end apart: 34, of which 21 were waited for; matrix products, arithmetic and copies ran while one was open for 2% of the time, Pallas kernels for 19%

profile of v9, /device:TPU:6, one launch (start us, length us, event | category | flops | bytes accessed | tf_op | source)
XLA Modules:
  0.0 160.8 jit_solution(17547810122893572455)
XLA Ops:
  0.0 1.9 %collective-permute-start = (s32[1024]{0:T(1024)}, s32[1024]{0:T(1024)S(1)}, u32[]{:S(2)}, u32[]{:S(2)}) collective-permute-start(s32[1024]{0:T(1024)} %param.18), channel_id=1, source_target_pairs={{0,4},{4,8},{8,12},{12,16},{16,20},{20,24},{24,28},{28,32},{32,36}... | collective-permute-start | bytes 12296 | tf_op jit(solution)/shard_map/ppermute | solution.py:49
  1.9 3.7 %collective-permute-start.3 = (s32[1024]{0:T(1024)}, s32[1024]{0:T(1024)S(1)}, u32[]{:S(2)}, u32[]{:S(2)}) collective-permute-start(s32[1024]{0:T(1024)} %param.18), channel_id=1, source_target_pairs={{0,8},{4,12},{8,16},{12,20},{16,24},{20,28},{24,32},{28,36},{32,40... | collective-permute-start | bytes 12296 | tf_op jit(solution)/shard_map/ppermute | solution.py:49
  5.8 9.7 %fine_tables.1 = (bf16[5,256,256]{2,1,0:T(8,128)(2,1)}, bf16[128,1024]{1,0:T(8,128)(2,1)}) custom-call(s32[3]{0:T(128)S(1)} %pad_add_fusion.where_ref, f32[1,1024]{1,0:T(1,128)} %bitcast.35, bf16[256,1024]{1,0:T(8,128)(2,1)} %emb_ref.1, bf16[1024,256]{1,0:T(8,128)(2,1)} %wq_hbm.1, bf16[1024,256]{1,0:T(8,128)(2,1)} %wk_hbm.1, bf16[1024,256]{1,0:T(8,128)(2,1)} %wv_hbm.1, ...), custom_call_target="tpu_custom_call" | custom-call | flops 3000000000 | bytes 6000000 | tf_op jit(solution)/shard_map/fine_tables/pallas_call | solution.py:255
  15.4 3.3 %collective-permute-start.2 = (bf16[128,1024]{1,0:T(8,128)(2,1)}, bf16[128,1024]{1,0:T(8,128)(2,1)S(1)}, u32[]{:S(2)}, u32[]{:S(2)}) collective-permute-start(bf16[128,1024]{1,0:T(8,128)(2,1)} %get-tuple-element.38), channel_id=1, source_target_pairs={{0,2},{1,3},{2,0},{3,1},{4,6},{5,7},{6,4},{7,5},{8,10},{9,11},{10,... | collective-permute-start | bytes 786440 | tf_op jit(solution)/shard_map/ppermute | solution.py:45
  18.7 0.7 collective-permute-start.1
  19.4 0.2 copy.22.own_ref
  19.6 0.2 copy.21.prior_ref
  20.0 12.3 %fine_attention.1 = bf16[4,272,256]{2,1,0:T(8,128)(2,1)} custom-call(s32[3]{0:T(128)S(1)} %pad_add_fusion.where_ref, s32[16,1]{1,0:T(8,128)S(1)} %copy.20.before_ref, s32[1024,1]{1,0:T(8,128)S(1)} %copy.21.prior_ref, s32[1024,1]{1,0:T(8,128)S(1)} %copy.22.own_ref, bf16[5,256,256]{2,1,0:T(8,128)(2,1)} %get-tuple-element.40.tab_hbm, ...), custom_call_target="tpu_custom_call" | custom-call | flops 12000000000 | bytes 24000000 | tf_op jit(solution)/shard_map/fine_attention/pallas_call | solution.py:255
  32.4 1.2 collective-permute-start.4
  33.6 3.5 %all-to-all-start = ((bf16[4,272,256]{2,1,0:T(8,128)(2,1)}), bf16[4,272,256]{2,1,0:T(8,128)(2,1)S(1)}, u32[]{:S(2)}, u32[]{:S(2)}) async-start(bf16[4,272,256]{2,1,0:T(8,128)(2,1)} %fine_attention.1), calls=%async_computation | async-start | bytes 1114112 | tf_op jit(solution)/shard_map/all_to_all | solution.py:590
  37.5 1.2 collective-permute-done.5.t2
  38.7 8.6 %all-to-all-done.got_ref = bf16[4,272,256]{2,1,0:T(8,128)(2,1)S(1)} async-done(((bf16[4,272,256]{2,1,0:T(8,128)(2,1)}), bf16[4,272,256]{2,1,0:T(8,128)(2,1)S(1)}, u32[]{:S(2)}, u32[]{:S(2)}) %all-to-all-start) | async-done | bytes 557088 | tf_op jit(solution)/shard_map/all_to_all | solution.py:590
  47.4 2.6 %fine_rows.1 = (bf16[4,272,256]{2,1,0:T(8,128)(2,1)S(1)}, bf16[4,256,1024]{2,1,0:T(8,128)(2,1)S(1)}) custom-call(s32[3]{0:T(128)S(1)} %pad_add_fusion.where_ref, s32[272,1]{1,0:T(8,128)S(1)} %broadcast_in_dim.28.ids_ref, bf16[256,1024]{1,0:T(8,128)(2,1)S(1)} %copy-done, bf16[4,272,256]{2,1,0:T(8,128)(2,1)S(1)} %all-to-all-done.got_ref, ...), custom_call_target="tpu_custom_call" | custom-call | flops 2000000000 | bytes 4000000 | tf_op jit(solution)/shard_map/fine_rows/pallas_call | solution.py:255
  50.0 0.7 collective-permute-start.6
  50.6 2.1 %collective-permute-start.8 = (bf16[272,256]{1,0:T(8,128)(2,1)S(1)}, bf16[272,256]{1,0:T(8,128)(2,1)S(1)}, u32[]{:S(2)}, u32[]{:S(2)}) collective-permute-start(bf16[272,256]{1,0:T(8,128)(2,1)S(1)} %get-tuple-element.71), channel_id=1, source_target_pairs={{0,2},{1,3},{2,0},{3,1},{4,6},{5,7},{6,4},{7,5},{8,10},{9,11},{10,... | collective-permute-start | bytes 417800 | tf_op jit(solution)/shard_map/ppermute | solution.py:45
  52.7 0.7 collective-permute-start.10
  53.4 5.6 %collective-permute-done.6.group_ref.b1 = bf16[272,256]{1,0:T(8,128)(2,1)S(1)} collective-permute-done((bf16[272,256]{1,0:T(8,128)(2,1)S(1)}, bf16[272,256]{1,0:T(8,128)(2,1)S(1)}, u32[]{:S(2)}, u32[]{:S(2)}) %collective-permute-start.6) | collective-permute-done | bytes 139296 | tf_op jit(solution)/shard_map/ppermute | solution.py:45
  59.0 0.5 short_part.5
  59.6 0.5 short_part.6
  60.1 0.7 collective-permute-start.9
  60.8 0.5 short_part.7
  61.2 1.8 %collective-permute-start.11 = (bf16[64,1024]{1,0:T(8,128)(2,1)S(1)}, bf16[64,1024]{1,0:T(8,128)(2,1)S(1)}, u32[]{:S(2)}, u32[]{:S(2)}) collective-permute-start(bf16[64,1024]{1,0:T(8,128)(2,1)S(1)} %short_part.7), channel_id=1, source_target_pairs={{0,1},{1,2},{2,3},{3,0},{4,5},{5,6},{6,7},{7,4},{8,9},{9,10},{10,1... | collective-permute-start | bytes 393224 | tf_op jit(solution)/shard_map/ppermute | solution.py:45
  63.1 0.5 short_part.4
  63.6 1.0 collective-permute-done.7
  64.5 2.6 %collective-permute-done.9 = bf16[64,1024]{1,0:T(8,128)(2,1)S(1)} collective-permute-done((bf16[64,1024]{1,0:T(8,128)(2,1)S(1)}, bf16[64,1024]{1,0:T(8,128)(2,1)S(1)}, u32[]{:S(2)}, u32[]{:S(2)}) %collective-permute-start.9) | collective-permute-done | bytes 131104 | tf_op jit(solution)/shard_map/ppermute | solution.py:45
  67.1 1.4 collective-permute-done.11
  68.6 0.2 collective-permute-start.12
  68.8 4.5 %collective-permute-start.13 = (bf16[64,1024]{1,0:T(8,128)(2,1)S(1)}, bf16[64,1024]{1,0:T(8,128)(2,1)S(1)}, u32[]{:S(2)}, u32[]{:S(2)}) collective-permute-start(bf16[64,1024]{1,0:T(8,128)(2,1)S(1)} %add_convert_fusion.s0), channel_id=1, source_target_pairs={{0,2},{1,3},{2,0},{3,1},{4,6},{5,7},{6,4},{7,5},{8,10},{9,11},{10,... | collective-permute-start | bytes 393224 | tf_op jit(solution)/shard_map/ppermute | solution.py:45
  73.5 1.4 collective-permute-done.12.s1
  74.9 2.8 %collective-permute-done.13.s2 = bf16[64,1024]{1,0:T(8,128)(2,1)S(1)} collective-permute-done((bf16[64,1024]{1,0:T(8,128)(2,1)S(1)}, bf16[64,1024]{1,0:T(8,128)(2,1)S(1)}, u32[]{:S(2)}, u32[]{:S(2)}) %collective-permute-start.13) | collective-permute-done | bytes 131104 | tf_op jit(solution)/shard_map/ppermute | solution.py:45
  77.7 0.6 collective-permute-done.14.s3
  78.3 2.3 %coarse_pack.1 = (bf16[4,384,128]{2,1,0:T(8,128)(2,1)}, bf16[256,1024]{1,0:T(8,128)(2,1)S(1)}) custom-call(s32[3]{0:T(128)S(1)} %pad_add_fusion.where_ref, bf16[64,1024]{1,0:T(8,128)(2,1)S(1)} %add_convert_fusion.s0, bf16[64,1024]{1,0:T(8,128)(2,1)S(1)} %collective-permute-done.12.s1, bf16[64,1024]{1,0:T(8,128)(2,1)S(1)} %collective-permute-done.13.s2, ...), custom_call_target="tpu_custom_call" | custom-call | flops 2000000000 | bytes 4000000 | tf_op jit(solution)/shard_map/coarse_pack/pallas_call | solution.py:255
  80.6 4.8 %all-to-all-start.1 = ((bf16[4,384,128]{2,1,0:T(8,128)(2,1)}), bf16[4,384,128]{2,1,0:T(8,128)(2,1)S(1)}, u32[]{:S(2)}, u32[]{:S(2)}) async-start(bf16[4,384,128]{2,1,0:T(8,128)(2,1)} %get-tuple-element.47), calls=%async_computation.1 | async-start | bytes 786432 | tf_op jit(solution)/shard_map/all_to_all | solution.py:629
  85.5 0.4 collective-permute-start.18
  85.9 7.0 %all-to-all-done.1.turned_ref = bf16[4,384,128]{2,1,0:T(8,128)(2,1)S(1)} async-done(((bf16[4,384,128]{2,1,0:T(8,128)(2,1)}), bf16[4,384,128]{2,1,0:T(8,128)(2,1)S(1)}, u32[]{:S(2)}, u32[]{:S(2)}) %all-to-all-start.1) | async-done | bytes 393248 | tf_op jit(solution)/shard_map/all_to_all | solution.py:629
  93.1 1.0 constant_dynamic-slice_fusion
  94.1 1.6 collective-permute-start.19
  95.6 1.2 collective-permute-start.15
  96.9 2.0 %collective-permute-start.16 = (bf16[4,256,128]{2,1,0:T(8,128)(2,1)S(1)}, bf16[4,256,128]{2,1,0:T(8,128)(2,1)S(1)}, u32[]{:S(2)}, u32[]{:S(2)}) collective-permute-start(bf16[4,256,128]{2,1,0:T(8,128)(2,1)S(1)} %slice.14), channel_id=1, source_target_pairs={{0,8},{8,16},{16,24},{24,0},{1,9},{9,17},{17,25},{25,1},{2,10},{10... | collective-permute-start | bytes 786440 | tf_op jit(solution)/shard_map/ppermute | solution.py:45
  98.9 2.1 %coarse_first.1 = (bf16[1024,128]{1,0:T(8,128)(2,1)S(1)}, f32[1024,128]{1,0:T(8,128)S(1)}, f32[1024,128]{1,0:T(8,128)S(1)}, f32[1024,128]{1,0:T(8,128)S(1)}) custom-call(s32[6]{0:T(128)S(1)} %pad_add_fusion.1.flag_ref, bf16[4,384,128]{2,1,0:T(8,128)(2,1)S(1)} %all-to-all-done.1.turned_ref, bf16[4,256,128]{2,1,0:T(8,128)(2,1)S(1)} %collective-permute-done.20.far_ref), custom_call_target="tpu_custom_call" | custom-call | flops 3000000000 | bytes 6000000 | tf_op jit(solution)/shard_map/coarse_first/pallas_call | solution.py:255
  101.0 3.3 %collective-permute-done.19.refs_8_ = bf16[128,1024]{1,0:T(8,128)(2,1)S(1)} collective-permute-done((bf16[128,1024]{1,0:T(8,128)(2,1)S(1)}, bf16[128,1024]{1,0:T(8,128)(2,1)S(1)}, u32[]{:S(2)}, u32[]{:S(2)}) %collective-permute-start.19) | collective-permute-done | bytes 262176 | tf_op jit(solution)/shard_map/ppermute | solution.py:45
  104.3 2.0 %collective-permute-done.15.refs_0_ = bf16[4,256,128]{2,1,0:T(8,128)(2,1)S(1)} collective-permute-done((bf16[4,256,128]{2,1,0:T(8,128)(2,1)S(1)}, bf16[4,256,128]{2,1,0:T(8,128)(2,1)S(1)}, u32[]{:S(2)}, u32[]{:S(2)}) %collective-permute-start.15) | collective-permute-done | bytes 262176 | tf_op jit(solution)/shard_map/ppermute | solution.py:45
  106.3 2.8 %collective-permute-done.16.refs_0_ = bf16[4,256,128]{2,1,0:T(8,128)(2,1)S(1)} collective-permute-done((bf16[4,256,128]{2,1,0:T(8,128)(2,1)S(1)}, bf16[4,256,128]{2,1,0:T(8,128)(2,1)S(1)}, u32[]{:S(2)}, u32[]{:S(2)}) %collective-permute-start.16) | collective-permute-done | bytes 262176 | tf_op jit(solution)/shard_map/ppermute | solution.py:45
  109.2 2.0 %collective-permute-done.17.refs_2_ = bf16[4,256,128]{2,1,0:T(8,128)(2,1)S(1)} collective-permute-done((bf16[4,256,128]{2,1,0:T(8,128)(2,1)S(1)}, bf16[4,256,128]{2,1,0:T(8,128)(2,1)S(1)}, u32[]{:S(2)}, u32[]{:S(2)}) %collective-permute-start.17) | collective-permute-done | bytes 262176 | tf_op jit(solution)/shard_map/ppermute | solution.py:45
  111.2 0.5 collective-permute-start.23
  111.7 0.5 collective-permute-start.21
  112.2 0.5 collective-permute-done.22.refs_1_
  112.7 0.4 collective-permute-done.23.refs_3_
  113.1 5.0 %coarse_more.1 = (bf16[1024,1024]{1,0:T(8,128)(2,1)S(1)}, bf16[1024,1024]{1,0:T(8,128)(2,1)S(1)}, f32[1024,128]{1,0:T(8,128)S(1)}, f32[1024,128]{1,0:T(8,128)S(1)}, f32[1024,128]{1,0:T(8,128)S(1)}) custom-call(s32[6]{0:T(128)S(1)} %pad_add_fusion.1.flag_ref, bf16[4,256,128]{2,1,0:T(8,128)(2,1)S(1)} %collective-permute-done.16.refs_0_, ...), custom_call_target="tpu_custom_call" | custom-call | flops 6000000000 | bytes 12000000 | tf_op jit(solution)/shard_map/coarse_more/pallas_call | solution.py:255
  118.2 3.0 %coarse_last.1 = (bf16[1024,1024]{1,0:T(8,128)(2,1)S(1)}, bf16[16,128,128]{2,1,0:T(8,128)(2,1)S(1)}) custom-call(s32[6]{0:T(128)S(1)} %pad_add_fusion.1.flag_ref, bf16[4,256,128]{2,1,0:T(8,128)(2,1)S(1)} %collective-permute-done.15.refs_0_, bf16[4,256,128]{2,1,0:T(8,128)(2,1)S(1)} %collective-permute-done.21.refs_1_, ...), custom_call_target="tpu_custom_call" | custom-call | flops 3000000000 | bytes 6000000 | tf_op jit(solution)/shard_map/coarse_last/pallas_call | solution.py:255
  121.2 15.6 %all_to_all.15.heads_ref = bf16[16,128,128]{2,1,0:T(8,128)(2,1)S(1)} all-to-all(bf16[16,128,128]{2,1,0:T(8,128)(2,1)S(1)} %get-tuple-element.62), channel_id=1, replica_groups=mesh['z'=4,'x'=4,'core'=2,'head'=4] {'z','head'}, dimensions={0} | all-to-all | bytes 1048576 | tf_op jit(solution)/shard_map/all_to_all | solution.py:660
  136.8 2.9 %feed.1 = (bf16[4,64,1024]{2,1,0:T(8,128)(2,1)S(1)}, f32[64,1024]{1,0:T(8,128)S(1)}) custom-call(s32[3]{0:T(128)S(1)} %pad_add_fusion.where_ref, bf16[16,128,128]{2,1,0:T(8,128)(2,1)S(1)} %all_to_all.15.heads_ref, bf16[256,1024]{1,0:T(8,128)(2,1)S(1)} %get-tuple-element.63.short_ref, f32[1,1024]{1,0:T(1,128)S(1)} %bitcast.31, ...), custom_call_target="tpu_custom_call" | custom-call | flops 4000000000 | bytes 8000000 | tf_op jit(solution)/shard_map/feed/pallas_call | solution.py:255
  139.8 0.6 collective-permute-start.26
  140.4 1.4 collective-permute-start.27
  141.8 1.5 collective-permute-start.28
  143.3 4.7 %collective-permute-done.26 = bf16[64,1024]{1,0:T(8,128)(2,1)S(1)} collective-permute-done((bf16[64,1024]{1,0:T(8,128)(2,1)S(1)}, bf16[64,1024]{1,0:T(8,128)(2,1)S(1)}, u32[]{:S(2)}, u32[]{:S(2)}) %collective-permute-start.26) | collective-permute-done | bytes 131104 | tf_op jit(solution)/shard_map/ppermute | solution.py:45
  148.0 0.6 collective-permute-done.28
  148.7 1.1 collective-permute-start.29
  149.8 3.1 %collective-permute-start.30 = (bf16[64,1024]{1,0:T(8,128)(2,1)S(1)}, bf16[64,1024]{1,0:T(8,128)(2,1)S(1)}, u32[]{:S(2)}, u32[]{:S(2)}) collective-permute-start(bf16[64,1024]{1,0:T(8,128)(2,1)S(1)} %fusion.3.s0), channel_id=1, source_target_pairs={{0,2},{1,3},{2,0},{3,1},{4,6},{5,7},{6,4},{7,5},{8,10},{9,11},{10,... | collective-permute-start | bytes 393224 | tf_op jit(solution)/shard_map/ppermute | solution.py:45
  152.8 0.2 collective-permute-start.31
  153.0 0.5 copy.24
  153.5 2.8 %collective-permute-done.29.s1 = bf16[64,1024]{1,0:T(8,128)(2,1)S(1)} collective-permute-done((bf16[64,1024]{1,0:T(8,128)(2,1)S(1)}, bf16[64,1024]{1,0:T(8,128)(2,1)S(1)}, u32[]{:S(2)}, u32[]{:S(2)}) %collective-permute-start.29) | collective-permute-done | bytes 131104 | tf_op jit(solution)/shard_map/ppermute | solution.py:45
  156.3 1.7 %collective-permute-done.30.s2 = bf16[64,1024]{1,0:T(8,128)(2,1)S(1)} collective-permute-done((bf16[64,1024]{1,0:T(8,128)(2,1)S(1)}, bf16[64,1024]{1,0:T(8,128)(2,1)S(1)}, u32[]{:S(2)}, u32[]{:S(2)}) %collective-permute-start.30) | collective-permute-done | bytes 131104 | tf_op jit(solution)/shard_map/ppermute | solution.py:45
  158.1 2.7 %final.1 = bf16[1024,256]{1,0:T(8,128)(2,1)} custom-call(s32[3]{0:T(128)S(1)} %pad_add_fusion.where_ref, bf16[64,1024]{1,0:T(8,128)(2,1)S(1)} %fusion.3.s0, bf16[64,1024]{1,0:T(8,128)(2,1)S(1)} %collective-permute-done.29.s1, bf16[64,1024]{1,0:T(8,128)(2,1)S(1)} %collective-permute-done.30.s2, bf16[64,1024]{1,0:T(8,128)(2,1)S(1)} %collective-permute-done.31.s3, ...), custom_call_target="tpu_custom_call" | custom-call | flops 2000000000 | bytes 4000000 | tf_op jit(solution)/shard_map/final/pallas_call | solution.py:255
  (55 shorter events, 1.5 us)
Async XLA Ops:
  0.0 19.6 %collective-permute-start = (s32[1024]{0:T(1024)}, s32[1024]{0:T(1024)S(1)}, u32[]{:S(2)}, u32[]{:S(2)}) collective-permute-start(s32[1024]{0:T(1024)} %param.18), channel_id=1, source_target_pairs={{0,4},{4,8},{8,12},{12,16},{16,20},{20,24},{24,28},{28,32},{32,36}... | collective-permute-start | bytes 12296 | tf_op jit(solution)/shard_map/ppermute | solution.py:49
  1.9 18.0 %collective-permute-start.3 = (s32[1024]{0:T(1024)}, s32[1024]{0:T(1024)S(1)}, u32[]{:S(2)}, u32[]{:S(2)}) collective-permute-start(s32[1024]{0:T(1024)} %param.18), channel_id=1, source_target_pairs={{0,8},{4,12},{8,16},{12,20},{16,24},{20,28},{24,32},{28,36},{32,40... | collective-permute-start | bytes 12296 | tf_op jit(solution)/shard_map/ppermute | solution.py:49
  5.8 13.0 %copy-start.1 = (bf16[256,1024]{1,0:T(8,128)(2,1)S(1)}, bf16[256,1024]{1,0:T(8,128)(2,1)}, u32[]{:S(2)}) copy-start(bf16[256,1024]{1,0:T(8,128)(2,1)} %own_ref.1) | copy-start | bytes 1572868
  5.8 13.6 %copy-start.9 = (s32[1024]{0:T(1024)S(1)}, s32[1024]{0:T(1024)}, u32[]{:S(2)}) copy-start(s32[1024]{0:T(1024)} %param.18) | copy-start | bytes 12292
  15.4 17.0 %collective-permute-start.2 = (bf16[128,1024]{1,0:T(8,128)(2,1)}, bf16[128,1024]{1,0:T(8,128)(2,1)S(1)}, u32[]{:S(2)}, u32[]{:S(2)}) collective-permute-start(bf16[128,1024]{1,0:T(8,128)(2,1)} %get-tuple-element.38), channel_id=1, source_target_pairs={{0,2},{1,3},{2,0},{3,1},{4,6},{5,7},{6,4},{7,5},{8,10},{9,11},{10,... | collective-permute-start | bytes 786440 | tf_op jit(solution)/shard_map/ppermute | solution.py:45
  18.7 13.7 %collective-permute-start.1 = (bf16[256,1024]{1,0:T(8,128)(2,1)S(1)}, bf16[256,1024]{1,0:T(8,128)(2,1)S(1)}, u32[]{:S(2)}, u32[]{:S(2)}) collective-permute-start(bf16[256,1024]{1,0:T(8,128)(2,1)S(1)} %copy-done.1), channel_id=1, source_target_pairs={{0,1},{1,2},{2,3},{3,0},{4,7},{5,4},{6,5},{7,6},{8,9},{9,10},{10,1... | collective-permute-start | bytes 1572872 | tf_op jit(solution)/shard_map/ppermute | solution.py:516
  20.0 27.3 %copy-start = (bf16[256,1024]{1,0:T(8,128)(2,1)S(1)}, bf16[256,1024]{1,0:T(8,128)(2,1)}, u32[]{:S(2)}) copy-start(bf16[256,1024]{1,0:T(8,128)(2,1)} %emb_ref.1) | copy-start | bytes 1572868
  32.4 15.0 %collective-permute-start.4 = (bf16[256,1024]{1,0:T(8,128)(2,1)S(1)}, bf16[256,1024]{1,0:T(8,128)(2,1)S(1)}, u32[]{:S(2)}, u32[]{:S(2)}) collective-permute-start(bf16[256,1024]{1,0:T(8,128)(2,1)S(1)} %collective-permute-done.1.m1), channel_id=1, source_target_pairs={{0,4},{4,0},{1,5},{5,1},{2,6},{6,2},{3,7},{7,3},{8,12},{12,8},{9,1... | collective-permute-start | bytes 1572872 | tf_op jit(solution)/shard_map/ppermute | solution.py:45
  33.6 13.7 %all-to-all-start = ((bf16[4,272,256]{2,1,0:T(8,128)(2,1)}), bf16[4,272,256]{2,1,0:T(8,128)(2,1)S(1)}, u32[]{:S(2)}, u32[]{:S(2)}) async-start(bf16[4,272,256]{2,1,0:T(8,128)(2,1)} %fine_attention.1), calls=%async_computation | async-start | bytes 1114112 | tf_op jit(solution)/shard_map/all_to_all | solution.py:590
  37.1 1.6 %collective-permute-start.5 = (bf16[128,1024]{1,0:T(8,128)(2,1)S(1)}, bf16[128,1024]{1,0:T(8,128)(2,1)S(1)}, u32[]{:S(2)}, u32[]{:S(2)}) collective-permute-start(bf16[128,1024]{1,0:T(8,128)(2,1)S(1)} %collective-permute-done.2.m2), channel_id=1, source_target_pairs={{0,4},{4,0},{1,5},{5,1},{2,6},{6,2},{3,7},{7,3},{8,12},{12,8},{9,1... | collective-permute-start | bytes 786440 | tf_op jit(solution)/shard_map/ppermute | solution.py:45
  50.0 9.0 %collective-permute-start.6 = (bf16[272,256]{1,0:T(8,128)(2,1)S(1)}, bf16[272,256]{1,0:T(8,128)(2,1)S(1)}, u32[]{:S(2)}, u32[]{:S(2)}) collective-permute-start(bf16[272,256]{1,0:T(8,128)(2,1)S(1)} %get-tuple-element.72), channel_id=1, source_target_pairs={{0,1},{1,2},{2,3},{3,0},{4,5},{5,6},{6,7},{7,4},{8,9},{9,10},{10,1... | collective-permute-start | bytes 417800 | tf_op jit(solution)/shard_map/ppermute | solution.py:45
  50.6 8.9 %collective-permute-start.8 = (bf16[272,256]{1,0:T(8,128)(2,1)S(1)}, bf16[272,256]{1,0:T(8,128)(2,1)S(1)}, u32[]{:S(2)}, u32[]{:S(2)}) collective-permute-start(bf16[272,256]{1,0:T(8,128)(2,1)S(1)} %get-tuple-element.71), channel_id=1, source_target_pairs={{0,2},{1,3},{2,0},{3,1},{4,6},{5,7},{6,4},{7,5},{8,10},{9,11},{10,... | collective-permute-start | bytes 417800 | tf_op jit(solution)/shard_map/ppermute | solution.py:45
  52.7 8.1 %collective-permute-start.10 = (bf16[272,256]{1,0:T(8,128)(2,1)S(1)}, bf16[272,256]{1,0:T(8,128)(2,1)S(1)}, u32[]{:S(2)}, u32[]{:S(2)}) collective-permute-start(bf16[272,256]{1,0:T(8,128)(2,1)S(1)} %get-tuple-element.70), channel_id=1, source_target_pairs={{0,3},{1,0},{2,1},{3,2},{4,7},{5,4},{6,5},{7,6},{8,11},{9,8},{10,9... | collective-permute-start | bytes 417800 | tf_op jit(solution)/shard_map/ppermute | solution.py:45
  59.5 5.0 %collective-permute-start.7 = (bf16[64,1024]{1,0:T(8,128)(2,1)S(1)}, bf16[64,1024]{1,0:T(8,128)(2,1)S(1)}, u32[]{:S(2)}, u32[]{:S(2)}) collective-permute-start(bf16[64,1024]{1,0:T(8,128)(2,1)S(1)} %short_part.5), channel_id=1, source_target_pairs={{0,3},{1,0},{2,1},{3,2},{4,7},{5,4},{6,5},{7,6},{8,11},{9,8},{10,9... | collective-permute-start | bytes 393224 | tf_op jit(solution)/shard_map/ppermute | solution.py:45
  60.1 7.0 %collective-permute-start.9 = (bf16[64,1024]{1,0:T(8,128)(2,1)S(1)}, bf16[64,1024]{1,0:T(8,128)(2,1)S(1)}, u32[]{:S(2)}, u32[]{:S(2)}) collective-permute-start(bf16[64,1024]{1,0:T(8,128)(2,1)S(1)} %short_part.6), channel_id=1, source_target_pairs={{0,2},{1,3},{2,0},{3,1},{4,6},{5,7},{6,4},{7,5},{8,10},{9,11},{10,... | collective-permute-start | bytes 393224 | tf_op jit(solution)/shard_map/ppermute | solution.py:45
  61.2 7.3 %collective-permute-start.11 = (bf16[64,1024]{1,0:T(8,128)(2,1)S(1)}, bf16[64,1024]{1,0:T(8,128)(2,1)S(1)}, u32[]{:S(2)}, u32[]{:S(2)}) collective-permute-start(bf16[64,1024]{1,0:T(8,128)(2,1)S(1)} %short_part.7), channel_id=1, source_target_pairs={{0,1},{1,2},{2,3},{3,0},{4,5},{5,6},{6,7},{7,4},{8,9},{9,10},{10,1... | collective-permute-start | bytes 393224 | tf_op jit(solution)/shard_map/ppermute | solution.py:45
  63.0 15.3 %copy-start.2 = (bf16[1024,256]{1,0:T(8,128)(2,1)S(1)}, bf16[1024,256]{1,0:T(8,128)(2,1)}, u32[]{:S(2)}) copy-start(bf16[1024,256]{1,0:T(8,128)(2,1)} %wq_ref.1) | copy-start | bytes 1572868
  63.0 15.3 %copy-start.3 = (bf16[1024,256]{1,0:T(8,128)(2,1)S(1)}, bf16[1024,256]{1,0:T(8,128)(2,1)}, u32[]{:S(2)}) copy-start(bf16[1024,256]{1,0:T(8,128)(2,1)} %wk_ref.1) | copy-start | bytes 1572868
  63.0 15.3 %copy-start.4 = (bf16[1024,256]{1,0:T(8,128)(2,1)S(1)}, bf16[1024,256]{1,0:T(8,128)(2,1)}, u32[]{:S(2)}) copy-start(bf16[1024,256]{1,0:T(8,128)(2,1)} %wv_ref.1) | copy-start | bytes 1572868
  63.0 15.3 %copy-start.5 = (f32[1024]{0:T(1024)S(1)}, f32[1024]{0:T(1024)}, u32[]{:S(2)}) copy-start(f32[1024]{0:T(1024)} %param.26) | copy-start | bytes 12292
  63.1 15.3 %copy-start.7 = (f32[576,128]{1,0:T(8,128)S(1)}, f32[576,128]{1,0:T(8,128)}, u32[]{:S(2)}) copy-start(f32[576,128]{1,0:T(8,128)} %constant.90.clone.turn_hbm.turn_ref) | copy-start | bytes 884740
  68.6 6.2 %collective-permute-start.12 = (bf16[64,1024]{1,0:T(8,128)(2,1)S(1)}, bf16[64,1024]{1,0:T(8,128)(2,1)S(1)}, u32[]{:S(2)}, u32[]{:S(2)}) collective-permute-start(bf16[64,1024]{1,0:T(8,128)(2,1)S(1)} %add_convert_fusion.s0), channel_id=1, source_target_pairs={{0,1},{1,2},{2,3},{3,0},{4,5},{5,6},{6,7},{7,4},{8,9},{9,10},{10,1... | collective-permute-start | bytes 393224 | tf_op jit(solution)/shard_map/ppermute | solution.py:45
  68.8 8.9 %collective-permute-start.13 = (bf16[64,1024]{1,0:T(8,128)(2,1)S(1)}, bf16[64,1024]{1,0:T(8,128)(2,1)S(1)}, u32[]{:S(2)}, u32[]{:S(2)}) collective-permute-start(bf16[64,1024]{1,0:T(8,128)(2,1)S(1)} %add_convert_fusion.s0), channel_id=1, source_target_pairs={{0,2},{1,3},{2,0},{3,1},{4,6},{5,7},{6,4},{7,5},{8,10},{9,11},{10,... | collective-permute-start | bytes 393224 | tf_op jit(solution)/shard_map/ppermute | solution.py:45
  73.3 5.0 %collective-permute-start.14 = (bf16[64,1024]{1,0:T(8,128)(2,1)S(1)}, bf16[64,1024]{1,0:T(8,128)(2,1)S(1)}, u32[]{:S(2)}, u32[]{:S(2)}) collective-permute-start(bf16[64,1024]{1,0:T(8,128)(2,1)S(1)} %add_convert_fusion.s0), channel_id=1, source_target_pairs={{0,3},{1,0},{2,1},{3,2},{4,7},{5,4},{6,5},{7,6},{8,11},{9,8},{10,9... | collective-permute-start | bytes 393224 | tf_op jit(solution)/shard_map/ppermute | solution.py:45
  80.6 12.2 %all-to-all-start.1 = ((bf16[4,384,128]{2,1,0:T(8,128)(2,1)}), bf16[4,384,128]{2,1,0:T(8,128)(2,1)S(1)}, u32[]{:S(2)}, u32[]{:S(2)}) async-start(bf16[4,384,128]{2,1,0:T(8,128)(2,1)} %get-tuple-element.47), calls=%async_computation.1 | async-start | bytes 786432 | tf_op jit(solution)/shard_map/all_to_all | solution.py:629
  85.5 18.9 %collective-permute-start.18 = (bf16[256,1024]{1,0:T(8,128)(2,1)}, bf16[256,1024]{1,0:T(8,128)(2,1)S(1)}, u32[]{:S(2)}, u32[]{:S(2)}) collective-permute-start(bf16[256,1024]{1,0:T(8,128)(2,1)} %refs_6_.1), channel_id=1, source_target_pairs={{0,1},{1,2},{2,3},{3,0},{4,7},{5,4},{6,5},{7,6},{8,9},{9,10},{10,1... | collective-permute-start | bytes 1572872 | tf_op jit(solution)/shard_map/ppermute | solution.py:516
  92.9 6.0 %collective-permute-start.20 = (bf16[4,256,128]{2,1,0:T(8,128)(2,1)S(1)}, bf16[4,256,128]{2,1,0:T(8,128)(2,1)S(1)}, u32[]{:S(2)}, u32[]{:S(2)}) collective-permute-start(bf16[4,256,128]{2,1,0:T(8,128)(2,1)S(1)} %slice.14), channel_id=1, source_target_pairs={{0,4},{4,0},{1,5},{5,1},{2,6},{6,2},{3,7},{7,3},{8,12},{12,8},{9,1... | collective-permute-start | bytes 786440 | tf_op jit(solution)/shard_map/ppermute | solution.py:45
  94.1 10.3 %collective-permute-start.19 = (bf16[128,1024]{1,0:T(8,128)(2,1)S(1)}, bf16[128,1024]{1,0:T(8,128)(2,1)S(1)}, u32[]{:S(2)}, u32[]{:S(2)}) collective-permute-start(bf16[128,1024]{1,0:T(8,128)(2,1)S(1)} %constant_dynamic-slice_fusion), channel_id=1, source_target_pairs={{0,2},{1,3},{2,0},{3,1},{4,6},{5,7},{6,4},{7,5},{8,10},{9,11},{10,... | collective-permute-start | bytes 786440 | tf_op jit(solution)/shard_map/ppermute | solution.py:45
  95.6 10.7 %collective-permute-start.15 = (bf16[4,256,128]{2,1,0:T(8,128)(2,1)S(1)}, bf16[4,256,128]{2,1,0:T(8,128)(2,1)S(1)}, u32[]{:S(2)}, u32[]{:S(2)}) collective-permute-start(bf16[4,256,128]{2,1,0:T(8,128)(2,1)S(1)} %slice.14), channel_id=1, source_target_pairs={{0,16},{8,24},{16,0},{24,8},{1,17},{9,25},{17,1},{25,9},{2,18},{10... | collective-permute-start | bytes 786440 | tf_op jit(solution)/shard_map/ppermute | solution.py:45
  96.9 12.3 %collective-permute-start.16 = (bf16[4,256,128]{2,1,0:T(8,128)(2,1)S(1)}, bf16[4,256,128]{2,1,0:T(8,128)(2,1)S(1)}, u32[]{:S(2)}, u32[]{:S(2)}) collective-permute-start(bf16[4,256,128]{2,1,0:T(8,128)(2,1)S(1)} %slice.14), channel_id=1, source_target_pairs={{0,8},{8,16},{16,24},{24,0},{1,9},{9,17},{17,25},{25,1},{2,10},{10... | collective-permute-start | bytes 786440 | tf_op jit(solution)/shard_map/ppermute | solution.py:45
  98.9 12.3 %collective-permute-start.17 = (bf16[4,256,128]{2,1,0:T(8,128)(2,1)S(1)}, bf16[4,256,128]{2,1,0:T(8,128)(2,1)S(1)}, u32[]{:S(2)}, u32[]{:S(2)}) collective-permute-start(bf16[4,256,128]{2,1,0:T(8,128)(2,1)S(1)} %slice.14), channel_id=1, source_target_pairs={{0,24},{8,0},{16,8},{24,16},{1,25},{9,1},{17,9},{25,17},{2,26},{10... | collective-permute-start | bytes 786440 | tf_op jit(solution)/shard_map/ppermute | solution.py:45
  111.2 1.5 collective-permute-start.22
  111.2 1.9 %collective-permute-start.23 = (bf16[4,256,128]{2,1,0:T(8,128)(2,1)S(1)}, bf16[4,256,128]{2,1,0:T(8,128)(2,1)S(1)}, u32[]{:S(2)}, u32[]{:S(2)}) collective-permute-start(bf16[4,256,128]{2,1,0:T(8,128)(2,1)S(1)} %collective-permute-done.17.refs_2_), channel_id=1, source_target_pairs={{0,4},{4,0},{1,5},{5,1},{2,6},{6,2},{3,7},{7,3},{8,12},{12,8},{9,1... | collective-permute-start | bytes 786440 | tf_op jit(solution)/shard_map/ppermute | solution.py:45
  111.7 6.5 %collective-permute-start.24 = (bf16[256,1024]{1,0:T(8,128)(2,1)S(1)}, bf16[256,1024]{1,0:T(8,128)(2,1)S(1)}, u32[]{:S(2)}, u32[]{:S(2)}) collective-permute-start(bf16[256,1024]{1,0:T(8,128)(2,1)S(1)} %collective-permute-done.18.refs_7_), channel_id=1, source_target_pairs={{0,4},{4,0},{1,5},{5,1},{2,6},{6,2},{3,7},{7,3},{8,12},{12,8},{9,1... | collective-permute-start | bytes 1572872 | tf_op jit(solution)/shard_map/ppermute | solution.py:45
  111.7 6.4 %collective-permute-start.21 = (bf16[4,256,128]{2,1,0:T(8,128)(2,1)S(1)}, bf16[4,256,128]{2,1,0:T(8,128)(2,1)S(1)}, u32[]{:S(2)}, u32[]{:S(2)}) collective-permute-start(bf16[4,256,128]{2,1,0:T(8,128)(2,1)S(1)} %collective-permute-done.15.refs_0_), channel_id=1, source_target_pairs={{0,4},{4,0},{1,5},{5,1},{2,6},{6,2},{3,7},{7,3},{8,12},{12,8},{9,1... | collective-permute-start | bytes 786440 | tf_op jit(solution)/shard_map/ppermute | solution.py:45
  112.2 6.0 %collective-permute-start.25 = (bf16[128,1024]{1,0:T(8,128)(2,1)S(1)}, bf16[128,1024]{1,0:T(8,128)(2,1)S(1)}, u32[]{:S(2)}, u32[]{:S(2)}) collective-permute-start(bf16[128,1024]{1,0:T(8,128)(2,1)S(1)} %collective-permute-done.19.refs_8_), channel_id=1, source_target_pairs={{0,4},{4,0},{1,5},{5,1},{2,6},{6,2},{3,7},{7,3},{8,12},{12,8},{9,1... | collective-permute-start | bytes 786440 | tf_op jit(solution)/shard_map/ppermute | solution.py:45
  118.2 18.6 %copy-start.6 = (f32[1024]{0:T(1024)S(1)}, f32[1024]{0:T(1024)}, u32[]{:S(2)}) copy-start(f32[1024]{0:T(1024)} %param.31) | copy-start | bytes 12292
  136.8 16.2 %copy-start.8 = (bf16[1024,4,256]{2,1,0:T(4,128)(2,1)S(1)}, bf16[1024,4,256]{2,1,0:T(4,128)(2,1)}, u32[]{:S(2)}) copy-start(bf16[1024,4,256]{2,1,0:T(4,128)(2,1)} %param.34) | copy-start | bytes 6291460
  139.8 8.2 %collective-permute-start.26 = (bf16[64,1024]{1,0:T(8,128)(2,1)S(1)}, bf16[64,1024]{1,0:T(8,128)(2,1)S(1)}, u32[]{:S(2)}, u32[]{:S(2)}) collective-permute-start(bf16[64,1024]{1,0:T(8,128)(2,1)S(1)} %get-tuple-element.73), channel_id=1, source_target_pairs={{0,1},{1,2},{2,3},{3,0},{4,5},{5,6},{6,7},{7,4},{8,9},{9,10},{10,1... | collective-permute-start | bytes 393224 | tf_op jit(solution)/shard_map/ppermute | solution.py:45
  140.4 7.6 %collective-permute-start.27 = (bf16[64,1024]{1,0:T(8,128)(2,1)S(1)}, bf16[64,1024]{1,0:T(8,128)(2,1)S(1)}, u32[]{:S(2)}, u32[]{:S(2)}) collective-permute-start(bf16[64,1024]{1,0:T(8,128)(2,1)S(1)} %get-tuple-element.75), channel_id=1, source_target_pairs={{0,2},{1,3},{2,0},{3,1},{4,6},{5,7},{6,4},{7,5},{8,10},{9,11},{10,... | collective-permute-start | bytes 393224 | tf_op jit(solution)/shard_map/ppermute | solution.py:45
  141.8 6.8 %collective-permute-start.28 = (bf16[64,1024]{1,0:T(8,128)(2,1)S(1)}, bf16[64,1024]{1,0:T(8,128)(2,1)S(1)}, u32[]{:S(2)}, u32[]{:S(2)}) collective-permute-start(bf16[64,1024]{1,0:T(8,128)(2,1)S(1)} %get-tuple-element.74), channel_id=1, source_target_pairs={{0,3},{1,0},{2,1},{3,2},{4,7},{5,4},{6,5},{7,6},{8,11},{9,8},{10,9... | collective-permute-start | bytes 393224 | tf_op jit(solution)/shard_map/ppermute | solution.py:45
  148.7 7.7 %collective-permute-start.29 = (bf16[64,1024]{1,0:T(8,128)(2,1)S(1)}, bf16[64,1024]{1,0:T(8,128)(2,1)S(1)}, u32[]{:S(2)}, u32[]{:S(2)}) collective-permute-start(bf16[64,1024]{1,0:T(8,128)(2,1)S(1)} %fusion.3.s0), channel_id=1, source_target_pairs={{0,1},{1,2},{2,3},{3,0},{4,5},{5,6},{6,7},{7,4},{8,9},{9,10},{10,1... | collective-permute-start | bytes 393224 | tf_op jit(solution)/shard_map/ppermute | solution.py:45
  149.8 8.3 %collective-permute-start.30 = (bf16[64,1024]{1,0:T(8,128)(2,1)S(1)}, bf16[64,1024]{1,0:T(8,128)(2,1)S(1)}, u32[]{:S(2)}, u32[]{:S(2)}) collective-permute-start(bf16[64,1024]{1,0:T(8,128)(2,1)S(1)} %fusion.3.s0), channel_id=1, source_target_pairs={{0,2},{1,3},{2,0},{3,1},{4,6},{5,7},{6,4},{7,5},{8,10},{9,11},{10,... | collective-permute-start | bytes 393224 | tf_op jit(solution)/shard_map/ppermute | solution.py:45
  152.8 5.3 %collective-permute-start.31 = (bf16[64,1024]{1,0:T(8,128)(2,1)S(1)}, bf16[64,1024]{1,0:T(8,128)(2,1)S(1)}, u32[]{:S(2)}, u32[]{:S(2)}) collective-permute-start(bf16[64,1024]{1,0:T(8,128)(2,1)S(1)} %fusion.3.s0), channel_id=1, source_target_pairs={{0,3},{1,0},{2,1},{3,2},{4,7},{5,4},{6,5},{7,6},{8,11},{9,8},{10,9... | collective-permute-start | bytes 393224 | tf_op jit(solution)/shard_map/ppermute | solution.py:45

commit v10 on v9

--- a/solution.py
+++ b/solution.py
@@ -105,7 +105,7 @@
 
 def fine_tables_kernel(
     where_ref, gain_hbm, emb_hbm, wq_hbm, wk_hbm, wv_hbm, fo_hbm,
-    tab_hbm, fo_half, tab_ref, gain_ref, emb_ref, w_ref, sems,
+    tab_hbm, fo_half, tab_ref, gain_ref, emb_ref, w_ref, half_ref, sems,
 ):
     pairs = [(emb_hbm, emb_ref), (gain_hbm, gain_ref)]
     for n, w in enumerate((wq_hbm, wk_hbm, wv_hbm)):
@@ -113,18 +113,21 @@
             rows = pl.ds(part * 512, 512)
             pairs.append((w.at[rows], w_ref.at[n, rows]))
     half = pl.ds(pl.multiple_of(where_ref[2] * 128, 128), 128)
-    pairs.append((fo_hbm.at[half], fo_half))
+    pairs.append((fo_hbm.at[half], half_ref))
     copies = begin_copies(pairs, sems)
     finish_copies(copies[:2])
     fine_in = norm_rows(emb_ref[...].astype(f32), gain_ref[...])
     finish_copies(copies[2:8])
+    finish_copies(copies[8:])
+    out = pltpu.make_async_copy(half_ref, fo_half, sems.at[9])
+    out.start()
     tq = dot(fine_in, w_ref[0]) * q_scale
     tk = dot(fine_in, w_ref[1])
     tables = (tq, partner(tq), tk, partner(tk), dot(fine_in, w_ref[2]))
     for n, table in enumerate(tables):
         tab_ref[n] = table.astype(bf16)
     finish_copies(begin_copies([(tab_ref.at[n], tab_hbm.at[n]) for n in range(5)], sems))
-    finish_copies(copies[8:])
+    out.wait()
 
 
 def fine_kernel(
@@ -563,7 +566,8 @@
         [
             pltpu.VMEM((5, 256, SHARE), bf16),
             pltpu.VMEM((1, D), f32), pltpu.VMEM((256, D), bf16),
-            pltpu.VMEM((3, D, SHARE), bf16), pltpu.SemaphoreType.DMA((9,)),
+            pltpu.VMEM((3, D, SHARE), bf16), pltpu.VMEM((128, D), bf16),
+            pltpu.SemaphoreType.DMA((10,)),
         ],
         us=3, hbm=[
             fine_norm[None], embedding, fine_query, fine_key, fine_value,

time: 161 us -> 155 us (0.963)
  Pallas kernels: 44.5 us -> 38.5 us
    pallas_call x13, Pallas kernels: 44.5 us -> 38.5 us  [call(): pl.pallas_call(kernel, out_shape=shapes, in_specs=[smem()] * len(scalars)...]
  transfers between devices with their start and end apart: 34 -> 34, of which waited for: 21 -> 21; matrix products, arithmetic and copies ran while one was open for 2% -> 2% of each run, Pallas kernels for 19% -> 16%
where the time goes in v10:
time: 155 us
  waiting for transfers between devices  53.2 us (34%)
  starting transfers between devices  44.3 us (29%)
  Pallas kernels  38.5 us (25%)
  blocking collectives  15.6 us (10%)
  local copies, waits for them, and re-layouts  2.38 us (2%)
    pallas_call x13, Pallas kernels, call(): pl.pallas_call(kernel, out_shape=shapes, in_specs=[smem()] * len(scalars)...  38.5 us
    ppermute x28, waiting for transfers between devices, shift(): lax.ppermute(value, axis, [(i, (i + steps) % count) for i in range(count)])  37.5 us
    ppermute x28, starting transfers between devices, shift(): lax.ppermute(value, axis, [(i, (i + steps) % count) for i in range(count)])  29.2 us
    all_to_all x1, blocking collectives, local(): heads_in = lax.all_to_all(wide_sends, ('z', 'head'), 0, 0)  15.6 us
    all_to_all x1, waiting for transfers between devices, local(): got = lax.all_to_all(mixed, 'head', 0, 0)  8.65 us
    all_to_all x1, waiting for transfers between devices, local(): turned = lax.all_to_all(packed, 'z', 0, 0)  7.01 us
    ppermute x2, starting transfers between devices, later(): lax.ppermute(value, axis, [(i, i + steps) for i in range(count - steps)])  5.65 us
    all_to_all x1, starting transfers between devices, local(): turned = lax.all_to_all(packed, 'z', 0, 0)  4.86 us
  transfers between devices with their start and end apart: 34, of which 21 were waited for; matrix products, arithmetic and copies ran while one was open for 2% of the time, Pallas kernels for 16%

profile of v10, /device:TPU:6, one launch (start us, length us, event | category | flops | bytes accessed | tf_op | source)
XLA Modules:
  0.0 154.8 jit_solution(946255053856716104)
XLA Ops:
  0.0 1.9 %collective-permute-start = (s32[1024]{0:T(1024)}, s32[1024]{0:T(1024)S(1)}, u32[]{:S(2)}, u32[]{:S(2)}) collective-permute-start(s32[1024]{0:T(1024)} %param.18), channel_id=1, source_target_pairs={{0,4},{4,8},{8,12},{12,16},{16,20},{20,24},{24,28},{28,32},{32,36}... | collective-permute-start | bytes 12296 | tf_op jit(solution)/shard_map/ppermute | solution.py:49
  1.9 3.7 %collective-permute-start.3 = (s32[1024]{0:T(1024)}, s32[1024]{0:T(1024)S(1)}, u32[]{:S(2)}, u32[]{:S(2)}) collective-permute-start(s32[1024]{0:T(1024)} %param.18), channel_id=1, source_target_pairs={{0,8},{4,12},{8,16},{12,20},{16,24},{20,28},{24,32},{28,36},{32,40... | collective-permute-start | bytes 12296 | tf_op jit(solution)/shard_map/ppermute | solution.py:49
  5.8 3.7 %fine_tables.1 = (bf16[5,256,256]{2,1,0:T(8,128)(2,1)}, bf16[128,1024]{1,0:T(8,128)(2,1)}) custom-call(s32[3]{0:T(128)S(1)} %pad_add_fusion.where_ref, f32[1,1024]{1,0:T(1,128)} %bitcast.35, bf16[256,1024]{1,0:T(8,128)(2,1)} %emb_ref.1, bf16[1024,256]{1,0:T(8,128)(2,1)} %wq_hbm.1, bf16[1024,256]{1,0:T(8,128)(2,1)} %wk_hbm.1, bf16[1024,256]{1,0:T(8,128)(2,1)} %wv_hbm.1, ...), custom_call_target="tpu_custom_call" | custom-call | flops 3000000000 | bytes 6000000 | tf_op jit(solution)/shard_map/fine_tables/pallas_call | solution.py:258
  9.5 3.3 %collective-permute-start.2 = (bf16[128,1024]{1,0:T(8,128)(2,1)}, bf16[128,1024]{1,0:T(8,128)(2,1)S(1)}, u32[]{:S(2)}, u32[]{:S(2)}) collective-permute-start(bf16[128,1024]{1,0:T(8,128)(2,1)} %get-tuple-element.38), channel_id=1, source_target_pairs={{0,2},{1,3},{2,0},{3,1},{4,6},{5,7},{6,4},{7,5},{8,10},{9,11},{10,... | collective-permute-start | bytes 786440 | tf_op jit(solution)/shard_map/ppermute | solution.py:45
  12.8 0.7 collective-permute-start.1
  13.5 0.2 copy.22.own_ref
  13.7 0.2 copy.21.prior_ref
  14.1 12.3 %fine_attention.1 = bf16[4,272,256]{2,1,0:T(8,128)(2,1)} custom-call(s32[3]{0:T(128)S(1)} %pad_add_fusion.where_ref, s32[16,1]{1,0:T(8,128)S(1)} %copy.20.before_ref, s32[1024,1]{1,0:T(8,128)S(1)} %copy.21.prior_ref, s32[1024,1]{1,0:T(8,128)S(1)} %copy.22.own_ref, bf16[5,256,256]{2,1,0:T(8,128)(2,1)} %get-tuple-element.40.tab_hbm, ...), custom_call_target="tpu_custom_call" | custom-call | flops 12000000000 | bytes 24000000 | tf_op jit(solution)/shard_map/fine_attention/pallas_call | solution.py:258
  26.5 1.2 collective-permute-start.4
  27.7 3.5 %all-to-all-start = ((bf16[4,272,256]{2,1,0:T(8,128)(2,1)}), bf16[4,272,256]{2,1,0:T(8,128)(2,1)S(1)}, u32[]{:S(2)}, u32[]{:S(2)}) async-start(bf16[4,272,256]{2,1,0:T(8,128)(2,1)} %fine_attention.1), calls=%async_computation | async-start | bytes 1114112 | tf_op jit(solution)/shard_map/all_to_all | solution.py:594
  31.6 1.2 collective-permute-done.5.t2
  32.8 8.6 %all-to-all-done.got_ref = bf16[4,272,256]{2,1,0:T(8,128)(2,1)S(1)} async-done(((bf16[4,272,256]{2,1,0:T(8,128)(2,1)}), bf16[4,272,256]{2,1,0:T(8,128)(2,1)S(1)}, u32[]{:S(2)}, u32[]{:S(2)}) %all-to-all-start) | async-done | bytes 557088 | tf_op jit(solution)/shard_map/all_to_all | solution.py:594
  41.4 2.6 %fine_rows.1 = (bf16[4,272,256]{2,1,0:T(8,128)(2,1)S(1)}, bf16[4,256,1024]{2,1,0:T(8,128)(2,1)S(1)}) custom-call(s32[3]{0:T(128)S(1)} %pad_add_fusion.where_ref, s32[272,1]{1,0:T(8,128)S(1)} %broadcast_in_dim.28.ids_ref, bf16[256,1024]{1,0:T(8,128)(2,1)S(1)} %copy-done, bf16[4,272,256]{2,1,0:T(8,128)(2,1)S(1)} %all-to-all-done.got_ref, ...), custom_call_target="tpu_custom_call" | custom-call | flops 2000000000 | bytes 4000000 | tf_op jit(solution)/shard_map/fine_rows/pallas_call | solution.py:258
  44.1 0.7 collective-permute-start.6
  44.7 2.1 %collective-permute-start.8 = (bf16[272,256]{1,0:T(8,128)(2,1)S(1)}, bf16[272,256]{1,0:T(8,128)(2,1)S(1)}, u32[]{:S(2)}, u32[]{:S(2)}) collective-permute-start(bf16[272,256]{1,0:T(8,128)(2,1)S(1)} %get-tuple-element.71), channel_id=1, source_target_pairs={{0,2},{1,3},{2,0},{3,1},{4,6},{5,7},{6,4},{7,5},{8,10},{9,11},{10,... | collective-permute-start | bytes 417800 | tf_op jit(solution)/shard_map/ppermute | solution.py:45
  46.8 0.7 collective-permute-start.10
  47.5 5.6 %collective-permute-done.6.group_ref.b1 = bf16[272,256]{1,0:T(8,128)(2,1)S(1)} collective-permute-done((bf16[272,256]{1,0:T(8,128)(2,1)S(1)}, bf16[272,256]{1,0:T(8,128)(2,1)S(1)}, u32[]{:S(2)}, u32[]{:S(2)}) %collective-permute-start.6) | collective-permute-done | bytes 139296 | tf_op jit(solution)/shard_map/ppermute | solution.py:45
  53.1 0.5 short_part.5
  53.7 0.5 short_part.6
  54.1 0.7 collective-permute-start.9
  54.8 0.5 short_part.7
  55.3 1.8 %collective-permute-start.11 = (bf16[64,1024]{1,0:T(8,128)(2,1)S(1)}, bf16[64,1024]{1,0:T(8,128)(2,1)S(1)}, u32[]{:S(2)}, u32[]{:S(2)}) collective-permute-start(bf16[64,1024]{1,0:T(8,128)(2,1)S(1)} %short_part.7), channel_id=1, source_target_pairs={{0,1},{1,2},{2,3},{3,0},{4,5},{5,6},{6,7},{7,4},{8,9},{9,10},{10,1... | collective-permute-start | bytes 393224 | tf_op jit(solution)/shard_map/ppermute | solution.py:45
  57.1 0.5 short_part.4
  57.6 1.0 collective-permute-done.7
  58.6 2.6 %collective-permute-done.9 = bf16[64,1024]{1,0:T(8,128)(2,1)S(1)} collective-permute-done((bf16[64,1024]{1,0:T(8,128)(2,1)S(1)}, bf16[64,1024]{1,0:T(8,128)(2,1)S(1)}, u32[]{:S(2)}, u32[]{:S(2)}) %collective-permute-start.9) | collective-permute-done | bytes 131104 | tf_op jit(solution)/shard_map/ppermute | solution.py:45
  61.2 1.4 collective-permute-done.11
  62.7 0.2 collective-permute-start.12
  62.8 4.5 %collective-permute-start.13 = (bf16[64,1024]{1,0:T(8,128)(2,1)S(1)}, bf16[64,1024]{1,0:T(8,128)(2,1)S(1)}, u32[]{:S(2)}, u32[]{:S(2)}) collective-permute-start(bf16[64,1024]{1,0:T(8,128)(2,1)S(1)} %add_convert_fusion.s0), channel_id=1, source_target_pairs={{0,2},{1,3},{2,0},{3,1},{4,6},{5,7},{6,4},{7,5},{8,10},{9,11},{10,... | collective-permute-start | bytes 393224 | tf_op jit(solution)/shard_map/ppermute | solution.py:45
  67.5 1.4 collective-permute-done.12.s1
  68.9 2.8 %collective-permute-done.13.s2 = bf16[64,1024]{1,0:T(8,128)(2,1)S(1)} collective-permute-done((bf16[64,1024]{1,0:T(8,128)(2,1)S(1)}, bf16[64,1024]{1,0:T(8,128)(2,1)S(1)}, u32[]{:S(2)}, u32[]{:S(2)}) %collective-permute-start.13) | collective-permute-done | bytes 131104 | tf_op jit(solution)/shard_map/ppermute | solution.py:45
  71.7 0.6 collective-permute-done.14.s3
  72.4 2.3 %coarse_pack.1 = (bf16[4,384,128]{2,1,0:T(8,128)(2,1)}, bf16[256,1024]{1,0:T(8,128)(2,1)S(1)}) custom-call(s32[3]{0:T(128)S(1)} %pad_add_fusion.where_ref, bf16[64,1024]{1,0:T(8,128)(2,1)S(1)} %add_convert_fusion.s0, bf16[64,1024]{1,0:T(8,128)(2,1)S(1)} %collective-permute-done.12.s1, bf16[64,1024]{1,0:T(8,128)(2,1)S(1)} %collective-permute-done.13.s2, ...), custom_call_target="tpu_custom_call" | custom-call | flops 2000000000 | bytes 4000000 | tf_op jit(solution)/shard_map/coarse_pack/pallas_call | solution.py:258
  74.7 4.9 %all-to-all-start.1 = ((bf16[4,384,128]{2,1,0:T(8,128)(2,1)}), bf16[4,384,128]{2,1,0:T(8,128)(2,1)S(1)}, u32[]{:S(2)}, u32[]{:S(2)}) async-start(bf16[4,384,128]{2,1,0:T(8,128)(2,1)} %get-tuple-element.47), calls=%async_computation.1 | async-start | bytes 786432 | tf_op jit(solution)/shard_map/all_to_all | solution.py:633
  79.6 0.4 collective-permute-start.18
  79.9 7.0 %all-to-all-done.1.turned_ref = bf16[4,384,128]{2,1,0:T(8,128)(2,1)S(1)} async-done(((bf16[4,384,128]{2,1,0:T(8,128)(2,1)}), bf16[4,384,128]{2,1,0:T(8,128)(2,1)S(1)}, u32[]{:S(2)}, u32[]{:S(2)}) %all-to-all-start.1) | async-done | bytes 393248 | tf_op jit(solution)/shard_map/all_to_all | solution.py:633
  87.2 1.0 constant_dynamic-slice_fusion
  88.1 1.6 %collective-permute-start.19 = (bf16[128,1024]{1,0:T(8,128)(2,1)S(1)}, bf16[128,1024]{1,0:T(8,128)(2,1)S(1)}, u32[]{:S(2)}, u32[]{:S(2)}) collective-permute-start(bf16[128,1024]{1,0:T(8,128)(2,1)S(1)} %constant_dynamic-slice_fusion), channel_id=1, source_target_pairs={{0,2},{1,3},{2,0},{3,1},{4,6},{5,7},{6,4},{7,5},{8,10},{9,11},{10,... | collective-permute-start | bytes 786440 | tf_op jit(solution)/shard_map/ppermute | solution.py:45
  89.7 1.2 collective-permute-start.15
  90.9 2.0 %collective-permute-start.16 = (bf16[4,256,128]{2,1,0:T(8,128)(2,1)S(1)}, bf16[4,256,128]{2,1,0:T(8,128)(2,1)S(1)}, u32[]{:S(2)}, u32[]{:S(2)}) collective-permute-start(bf16[4,256,128]{2,1,0:T(8,128)(2,1)S(1)} %slice.14), channel_id=1, source_target_pairs={{0,8},{8,16},{16,24},{24,0},{1,9},{9,17},{17,25},{25,1},{2,10},{10... | collective-permute-start | bytes 786440 | tf_op jit(solution)/shard_map/ppermute | solution.py:45
  93.0 2.1 %coarse_first.1 = (bf16[1024,128]{1,0:T(8,128)(2,1)S(1)}, f32[1024,128]{1,0:T(8,128)S(1)}, f32[1024,128]{1,0:T(8,128)S(1)}, f32[1024,128]{1,0:T(8,128)S(1)}) custom-call(s32[6]{0:T(128)S(1)} %pad_add_fusion.1.flag_ref, bf16[4,384,128]{2,1,0:T(8,128)(2,1)S(1)} %all-to-all-done.1.turned_ref, bf16[4,256,128]{2,1,0:T(8,128)(2,1)S(1)} %collective-permute-done.20.far_ref), custom_call_target="tpu_custom_call" | custom-call | flops 3000000000 | bytes 6000000 | tf_op jit(solution)/shard_map/coarse_first/pallas_call | solution.py:258
  95.1 3.3 %collective-permute-done.19.refs_8_ = bf16[128,1024]{1,0:T(8,128)(2,1)S(1)} collective-permute-done((bf16[128,1024]{1,0:T(8,128)(2,1)S(1)}, bf16[128,1024]{1,0:T(8,128)(2,1)S(1)}, u32[]{:S(2)}, u32[]{:S(2)}) %collective-permute-start.19) | collective-permute-done | bytes 262176 | tf_op jit(solution)/shard_map/ppermute | solution.py:45
  98.4 2.0 %collective-permute-done.15.refs_0_ = bf16[4,256,128]{2,1,0:T(8,128)(2,1)S(1)} collective-permute-done((bf16[4,256,128]{2,1,0:T(8,128)(2,1)S(1)}, bf16[4,256,128]{2,1,0:T(8,128)(2,1)S(1)}, u32[]{:S(2)}, u32[]{:S(2)}) %collective-permute-start.15) | collective-permute-done | bytes 262176 | tf_op jit(solution)/shard_map/ppermute | solution.py:45
  100.4 2.8 %collective-permute-done.16.refs_0_ = bf16[4,256,128]{2,1,0:T(8,128)(2,1)S(1)} collective-permute-done((bf16[4,256,128]{2,1,0:T(8,128)(2,1)S(1)}, bf16[4,256,128]{2,1,0:T(8,128)(2,1)S(1)}, u32[]{:S(2)}, u32[]{:S(2)}) %collective-permute-start.16) | collective-permute-done | bytes 262176 | tf_op jit(solution)/shard_map/ppermute | solution.py:45
  103.2 2.0 %collective-permute-done.17.refs_2_ = bf16[4,256,128]{2,1,0:T(8,128)(2,1)S(1)} collective-permute-done((bf16[4,256,128]{2,1,0:T(8,128)(2,1)S(1)}, bf16[4,256,128]{2,1,0:T(8,128)(2,1)S(1)}, u32[]{:S(2)}, u32[]{:S(2)}) %collective-permute-start.17) | collective-permute-done | bytes 262176 | tf_op jit(solution)/shard_map/ppermute | solution.py:45
  105.3 0.5 collective-permute-start.23
  105.8 0.5 collective-permute-start.21
  106.3 0.5 collective-permute-done.22.refs_1_
  106.8 0.4 collective-permute-done.23.refs_3_
  107.2 5.0 %coarse_more.1 = (bf16[1024,1024]{1,0:T(8,128)(2,1)S(1)}, bf16[1024,1024]{1,0:T(8,128)(2,1)S(1)}, f32[1024,128]{1,0:T(8,128)S(1)}, f32[1024,128]{1,0:T(8,128)S(1)}, f32[1024,128]{1,0:T(8,128)S(1)}) custom-call(s32[6]{0:T(128)S(1)} %pad_add_fusion.1.flag_ref, bf16[4,256,128]{2,1,0:T(8,128)(2,1)S(1)} %collective-permute-done.16.refs_0_, ...), custom_call_target="tpu_custom_call" | custom-call | flops 6000000000 | bytes 12000000 | tf_op jit(solution)/shard_map/coarse_more/pallas_call | solution.py:258
  112.3 3.0 %coarse_last.1 = (bf16[1024,1024]{1,0:T(8,128)(2,1)S(1)}, bf16[16,128,128]{2,1,0:T(8,128)(2,1)S(1)}) custom-call(s32[6]{0:T(128)S(1)} %pad_add_fusion.1.flag_ref, bf16[4,256,128]{2,1,0:T(8,128)(2,1)S(1)} %collective-permute-done.15.refs_0_, bf16[4,256,128]{2,1,0:T(8,128)(2,1)S(1)} %collective-permute-done.21.refs_1_, ...), custom_call_target="tpu_custom_call" | custom-call | flops 3000000000 | bytes 6000000 | tf_op jit(solution)/shard_map/coarse_last/pallas_call | solution.py:258
  115.2 15.6 %all_to_all.15.heads_ref = bf16[16,128,128]{2,1,0:T(8,128)(2,1)S(1)} all-to-all(bf16[16,128,128]{2,1,0:T(8,128)(2,1)S(1)} %get-tuple-element.62), channel_id=1, replica_groups=mesh['z'=4,'x'=4,'core'=2,'head'=4] {'z','head'}, dimensions={0} | all-to-all | bytes 1048576 | tf_op jit(solution)/shard_map/all_to_all | solution.py:664
  130.9 2.9 %feed.1 = (bf16[4,64,1024]{2,1,0:T(8,128)(2,1)S(1)}, f32[64,1024]{1,0:T(8,128)S(1)}) custom-call(s32[3]{0:T(128)S(1)} %pad_add_fusion.where_ref, bf16[16,128,128]{2,1,0:T(8,128)(2,1)S(1)} %all_to_all.15.heads_ref, bf16[256,1024]{1,0:T(8,128)(2,1)S(1)} %get-tuple-element.63.short_ref, f32[1,1024]{1,0:T(1,128)S(1)} %bitcast.31, ...), custom_call_target="tpu_custom_call" | custom-call | flops 4000000000 | bytes 8000000 | tf_op jit(solution)/shard_map/feed/pallas_call | solution.py:258
  133.8 0.6 collective-permute-start.26
  134.5 1.4 collective-permute-start.27
  135.9 1.5 collective-permute-start.28
  137.3 4.7 %collective-permute-done.26 = bf16[64,1024]{1,0:T(8,128)(2,1)S(1)} collective-permute-done((bf16[64,1024]{1,0:T(8,128)(2,1)S(1)}, bf16[64,1024]{1,0:T(8,128)(2,1)S(1)}, u32[]{:S(2)}, u32[]{:S(2)}) %collective-permute-start.26) | collective-permute-done | bytes 131104 | tf_op jit(solution)/shard_map/ppermute | solution.py:45
  142.0 0.6 collective-permute-done.28
  142.7 1.1 collective-permute-start.29
  143.8 3.1 %collective-permute-start.30 = (bf16[64,1024]{1,0:T(8,128)(2,1)S(1)}, bf16[64,1024]{1,0:T(8,128)(2,1)S(1)}, u32[]{:S(2)}, u32[]{:S(2)}) collective-permute-start(bf16[64,1024]{1,0:T(8,128)(2,1)S(1)} %fusion.3.s0), channel_id=1, source_target_pairs={{0,2},{1,3},{2,0},{3,1},{4,6},{5,7},{6,4},{7,5},{8,10},{9,11},{10,... | collective-permute-start | bytes 393224 | tf_op jit(solution)/shard_map/ppermute | solution.py:45
  146.9 0.2 collective-permute-start.31
  147.1 0.5 copy.24
  147.6 2.8 %collective-permute-done.29.s1 = bf16[64,1024]{1,0:T(8,128)(2,1)S(1)} collective-permute-done((bf16[64,1024]{1,0:T(8,128)(2,1)S(1)}, bf16[64,1024]{1,0:T(8,128)(2,1)S(1)}, u32[]{:S(2)}, u32[]{:S(2)}) %collective-permute-start.29) | collective-permute-done | bytes 131104 | tf_op jit(solution)/shard_map/ppermute | solution.py:45
  150.4 1.7 %collective-permute-done.30.s2 = bf16[64,1024]{1,0:T(8,128)(2,1)S(1)} collective-permute-done((bf16[64,1024]{1,0:T(8,128)(2,1)S(1)}, bf16[64,1024]{1,0:T(8,128)(2,1)S(1)}, u32[]{:S(2)}, u32[]{:S(2)}) %collective-permute-start.30) | collective-permute-done | bytes 131104 | tf_op jit(solution)/shard_map/ppermute | solution.py:45
  152.2 2.7 %final.1 = bf16[1024,256]{1,0:T(8,128)(2,1)} custom-call(s32[3]{0:T(128)S(1)} %pad_add_fusion.where_ref, bf16[64,1024]{1,0:T(8,128)(2,1)S(1)} %fusion.3.s0, bf16[64,1024]{1,0:T(8,128)(2,1)S(1)} %collective-permute-done.29.s1, bf16[64,1024]{1,0:T(8,128)(2,1)S(1)} %collective-permute-done.30.s2, bf16[64,1024]{1,0:T(8,128)(2,1)S(1)} %collective-permute-done.31.s3, ...), custom_call_target="tpu_custom_call" | custom-call | flops 2000000000 | bytes 4000000 | tf_op jit(solution)/shard_map/final/pallas_call | solution.py:258
  (55 shorter events, 1.5 us)
Async XLA Ops:
  0.0 13.7 %collective-permute-start = (s32[1024]{0:T(1024)}, s32[1024]{0:T(1024)S(1)}, u32[]{:S(2)}, u32[]{:S(2)}) collective-permute-start(s32[1024]{0:T(1024)} %param.18), channel_id=1, source_target_pairs={{0,4},{4,8},{8,12},{12,16},{16,20},{20,24},{24,28},{28,32},{32,36}... | collective-permute-start | bytes 12296 | tf_op jit(solution)/shard_map/ppermute | solution.py:49
  1.9 12.0 %collective-permute-start.3 = (s32[1024]{0:T(1024)}, s32[1024]{0:T(1024)S(1)}, u32[]{:S(2)}, u32[]{:S(2)}) collective-permute-start(s32[1024]{0:T(1024)} %param.18), channel_id=1, source_target_pairs={{0,8},{4,12},{8,16},{12,20},{16,24},{20,28},{24,32},{28,36},{32,40... | collective-permute-start | bytes 12296 | tf_op jit(solution)/shard_map/ppermute | solution.py:49
  5.8 7.0 %copy-start.1 = (bf16[256,1024]{1,0:T(8,128)(2,1)S(1)}, bf16[256,1024]{1,0:T(8,128)(2,1)}, u32[]{:S(2)}) copy-start(bf16[256,1024]{1,0:T(8,128)(2,1)} %own_ref.1) | copy-start | bytes 1572868
  5.8 7.7 %copy-start.9 = (s32[1024]{0:T(1024)S(1)}, s32[1024]{0:T(1024)}, u32[]{:S(2)}) copy-start(s32[1024]{0:T(1024)} %param.18) | copy-start | bytes 12292
  9.5 17.0 %collective-permute-start.2 = (bf16[128,1024]{1,0:T(8,128)(2,1)}, bf16[128,1024]{1,0:T(8,128)(2,1)S(1)}, u32[]{:S(2)}, u32[]{:S(2)}) collective-permute-start(bf16[128,1024]{1,0:T(8,128)(2,1)} %get-tuple-element.38), channel_id=1, source_target_pairs={{0,2},{1,3},{2,0},{3,1},{4,6},{5,7},{6,4},{7,5},{8,10},{9,11},{10,... | collective-permute-start | bytes 786440 | tf_op jit(solution)/shard_map/ppermute | solution.py:45
  12.8 13.7 %collective-permute-start.1 = (bf16[256,1024]{1,0:T(8,128)(2,1)S(1)}, bf16[256,1024]{1,0:T(8,128)(2,1)S(1)}, u32[]{:S(2)}, u32[]{:S(2)}) collective-permute-start(bf16[256,1024]{1,0:T(8,128)(2,1)S(1)} %copy-done.1), channel_id=1, source_target_pairs={{0,1},{1,2},{2,3},{3,0},{4,7},{5,4},{6,5},{7,6},{8,9},{9,10},{10,1... | collective-permute-start | bytes 1572872 | tf_op jit(solution)/shard_map/ppermute | solution.py:519
  14.1 27.3 %copy-start = (bf16[256,1024]{1,0:T(8,128)(2,1)S(1)}, bf16[256,1024]{1,0:T(8,128)(2,1)}, u32[]{:S(2)}) copy-start(bf16[256,1024]{1,0:T(8,128)(2,1)} %emb_ref.1) | copy-start | bytes 1572868
  26.5 15.0 %collective-permute-start.4 = (bf16[256,1024]{1,0:T(8,128)(2,1)S(1)}, bf16[256,1024]{1,0:T(8,128)(2,1)S(1)}, u32[]{:S(2)}, u32[]{:S(2)}) collective-permute-start(bf16[256,1024]{1,0:T(8,128)(2,1)S(1)} %collective-permute-done.1.m1), channel_id=1, source_target_pairs={{0,4},{4,0},{1,5},{5,1},{2,6},{6,2},{3,7},{7,3},{8,12},{12,8},{9,1... | collective-permute-start | bytes 1572872 | tf_op jit(solution)/shard_map/ppermute | solution.py:45
  27.7 13.7 %all-to-all-start = ((bf16[4,272,256]{2,1,0:T(8,128)(2,1)}), bf16[4,272,256]{2,1,0:T(8,128)(2,1)S(1)}, u32[]{:S(2)}, u32[]{:S(2)}) async-start(bf16[4,272,256]{2,1,0:T(8,128)(2,1)} %fine_attention.1), calls=%async_computation | async-start | bytes 1114112 | tf_op jit(solution)/shard_map/all_to_all | solution.py:594
  31.2 1.6 %collective-permute-start.5 = (bf16[128,1024]{1,0:T(8,128)(2,1)S(1)}, bf16[128,1024]{1,0:T(8,128)(2,1)S(1)}, u32[]{:S(2)}, u32[]{:S(2)}) collective-permute-start(bf16[128,1024]{1,0:T(8,128)(2,1)S(1)} %collective-permute-done.2.m2), channel_id=1, source_target_pairs={{0,4},{4,0},{1,5},{5,1},{2,6},{6,2},{3,7},{7,3},{8,12},{12,8},{9,1... | collective-permute-start | bytes 786440 | tf_op jit(solution)/shard_map/ppermute | solution.py:45
  44.1 9.0 %collective-permute-start.6 = (bf16[272,256]{1,0:T(8,128)(2,1)S(1)}, bf16[272,256]{1,0:T(8,128)(2,1)S(1)}, u32[]{:S(2)}, u32[]{:S(2)}) collective-permute-start(bf16[272,256]{1,0:T(8,128)(2,1)S(1)} %get-tuple-element.72), channel_id=1, source_target_pairs={{0,1},{1,2},{2,3},{3,0},{4,5},{5,6},{6,7},{7,4},{8,9},{9,10},{10,1... | collective-permute-start | bytes 417800 | tf_op jit(solution)/shard_map/ppermute | solution.py:45
  44.7 8.9 %collective-permute-start.8 = (bf16[272,256]{1,0:T(8,128)(2,1)S(1)}, bf16[272,256]{1,0:T(8,128)(2,1)S(1)}, u32[]{:S(2)}, u32[]{:S(2)}) collective-permute-start(bf16[272,256]{1,0:T(8,128)(2,1)S(1)} %get-tuple-element.71), channel_id=1, source_target_pairs={{0,2},{1,3},{2,0},{3,1},{4,6},{5,7},{6,4},{7,5},{8,10},{9,11},{10,... | collective-permute-start | bytes 417800 | tf_op jit(solution)/shard_map/ppermute | solution.py:45
  46.8 8.1 %collective-permute-start.10 = (bf16[272,256]{1,0:T(8,128)(2,1)S(1)}, bf16[272,256]{1,0:T(8,128)(2,1)S(1)}, u32[]{:S(2)}, u32[]{:S(2)}) collective-permute-start(bf16[272,256]{1,0:T(8,128)(2,1)S(1)} %get-tuple-element.70), channel_id=1, source_target_pairs={{0,3},{1,0},{2,1},{3,2},{4,7},{5,4},{6,5},{7,6},{8,11},{9,8},{10,9... | collective-permute-start | bytes 417800 | tf_op jit(solution)/shard_map/ppermute | solution.py:45
  53.6 5.0 %collective-permute-start.7 = (bf16[64,1024]{1,0:T(8,128)(2,1)S(1)}, bf16[64,1024]{1,0:T(8,128)(2,1)S(1)}, u32[]{:S(2)}, u32[]{:S(2)}) collective-permute-start(bf16[64,1024]{1,0:T(8,128)(2,1)S(1)} %short_part.5), channel_id=1, source_target_pairs={{0,3},{1,0},{2,1},{3,2},{4,7},{5,4},{6,5},{7,6},{8,11},{9,8},{10,9... | collective-permute-start | bytes 393224 | tf_op jit(solution)/shard_map/ppermute | solution.py:45
  54.1 7.0 %collective-permute-start.9 = (bf16[64,1024]{1,0:T(8,128)(2,1)S(1)}, bf16[64,1024]{1,0:T(8,128)(2,1)S(1)}, u32[]{:S(2)}, u32[]{:S(2)}) collective-permute-start(bf16[64,1024]{1,0:T(8,128)(2,1)S(1)} %short_part.6), channel_id=1, source_target_pairs={{0,2},{1,3},{2,0},{3,1},{4,6},{5,7},{6,4},{7,5},{8,10},{9,11},{10,... | collective-permute-start | bytes 393224 | tf_op jit(solution)/shard_map/ppermute | solution.py:45
  55.3 7.3 %collective-permute-start.11 = (bf16[64,1024]{1,0:T(8,128)(2,1)S(1)}, bf16[64,1024]{1,0:T(8,128)(2,1)S(1)}, u32[]{:S(2)}, u32[]{:S(2)}) collective-permute-start(bf16[64,1024]{1,0:T(8,128)(2,1)S(1)} %short_part.7), channel_id=1, source_target_pairs={{0,1},{1,2},{2,3},{3,0},{4,5},{5,6},{6,7},{7,4},{8,9},{9,10},{10,1... | collective-permute-start | bytes 393224 | tf_op jit(solution)/shard_map/ppermute | solution.py:45
  57.1 15.3 %copy-start.2 = (bf16[1024,256]{1,0:T(8,128)(2,1)S(1)}, bf16[1024,256]{1,0:T(8,128)(2,1)}, u32[]{:S(2)}) copy-start(bf16[1024,256]{1,0:T(8,128)(2,1)} %wq_ref.1) | copy-start | bytes 1572868
  57.1 15.3 %copy-start.3 = (bf16[1024,256]{1,0:T(8,128)(2,1)S(1)}, bf16[1024,256]{1,0:T(8,128)(2,1)}, u32[]{:S(2)}) copy-start(bf16[1024,256]{1,0:T(8,128)(2,1)} %wk_ref.1) | copy-start | bytes 1572868
  57.1 15.3 %copy-start.4 = (bf16[1024,256]{1,0:T(8,128)(2,1)S(1)}, bf16[1024,256]{1,0:T(8,128)(2,1)}, u32[]{:S(2)}) copy-start(bf16[1024,256]{1,0:T(8,128)(2,1)} %wv_ref.1) | copy-start | bytes 1572868
  57.1 15.3 %copy-start.5 = (f32[1024]{0:T(1024)S(1)}, f32[1024]{0:T(1024)}, u32[]{:S(2)}) copy-start(f32[1024]{0:T(1024)} %param.26) | copy-start | bytes 12292
  57.1 15.3 %copy-start.7 = (f32[576,128]{1,0:T(8,128)S(1)}, f32[576,128]{1,0:T(8,128)}, u32[]{:S(2)}) copy-start(f32[576,128]{1,0:T(8,128)} %constant.90.clone.turn_hbm.turn_ref) | copy-start | bytes 884740
  62.7 6.2 %collective-permute-start.12 = (bf16[64,1024]{1,0:T(8,128)(2,1)S(1)}, bf16[64,1024]{1,0:T(8,128)(2,1)S(1)}, u32[]{:S(2)}, u32[]{:S(2)}) collective-permute-start(bf16[64,1024]{1,0:T(8,128)(2,1)S(1)} %add_convert_fusion.s0), channel_id=1, source_target_pairs={{0,1},{1,2},{2,3},{3,0},{4,5},{5,6},{6,7},{7,4},{8,9},{9,10},{10,1... | collective-permute-start | bytes 393224 | tf_op jit(solution)/shard_map/ppermute | solution.py:45
  62.8 8.9 %collective-permute-start.13 = (bf16[64,1024]{1,0:T(8,128)(2,1)S(1)}, bf16[64,1024]{1,0:T(8,128)(2,1)S(1)}, u32[]{:S(2)}, u32[]{:S(2)}) collective-permute-start(bf16[64,1024]{1,0:T(8,128)(2,1)S(1)} %add_convert_fusion.s0), channel_id=1, source_target_pairs={{0,2},{1,3},{2,0},{3,1},{4,6},{5,7},{6,4},{7,5},{8,10},{9,11},{10,... | collective-permute-start | bytes 393224 | tf_op jit(solution)/shard_map/ppermute | solution.py:45
  67.4 5.0 %collective-permute-start.14 = (bf16[64,1024]{1,0:T(8,128)(2,1)S(1)}, bf16[64,1024]{1,0:T(8,128)(2,1)S(1)}, u32[]{:S(2)}, u32[]{:S(2)}) collective-permute-start(bf16[64,1024]{1,0:T(8,128)(2,1)S(1)} %add_convert_fusion.s0), channel_id=1, source_target_pairs={{0,3},{1,0},{2,1},{3,2},{4,7},{5,4},{6,5},{7,6},{8,11},{9,8},{10,9... | collective-permute-start | bytes 393224 | tf_op jit(solution)/shard_map/ppermute | solution.py:45
  74.7 12.2 %all-to-all-start.1 = ((bf16[4,384,128]{2,1,0:T(8,128)(2,1)}), bf16[4,384,128]{2,1,0:T(8,128)(2,1)S(1)}, u32[]{:S(2)}, u32[]{:S(2)}) async-start(bf16[4,384,128]{2,1,0:T(8,128)(2,1)} %get-tuple-element.47), calls=%async_computation.1 | async-start | bytes 786432 | tf_op jit(solution)/shard_map/all_to_all | solution.py:633
  79.6 18.9 %collective-permute-start.18 = (bf16[256,1024]{1,0:T(8,128)(2,1)}, bf16[256,1024]{1,0:T(8,128)(2,1)S(1)}, u32[]{:S(2)}, u32[]{:S(2)}) collective-permute-start(bf16[256,1024]{1,0:T(8,128)(2,1)} %refs_6_.1), channel_id=1, source_target_pairs={{0,1},{1,2},{2,3},{3,0},{4,7},{5,4},{6,5},{7,6},{8,9},{9,10},{10,1... | collective-permute-start | bytes 1572872 | tf_op jit(solution)/shard_map/ppermute | solution.py:519
  87.0 6.0 %collective-permute-start.20 = (bf16[4,256,128]{2,1,0:T(8,128)(2,1)S(1)}, bf16[4,256,128]{2,1,0:T(8,128)(2,1)S(1)}, u32[]{:S(2)}, u32[]{:S(2)}) collective-permute-start(bf16[4,256,128]{2,1,0:T(8,128)(2,1)S(1)} %slice.14), channel_id=1, source_target_pairs={{0,4},{4,0},{1,5},{5,1},{2,6},{6,2},{3,7},{7,3},{8,12},{12,8},{9,1... | collective-permute-start | bytes 786440 | tf_op jit(solution)/shard_map/ppermute | solution.py:45
  88.1 10.3 %collective-permute-start.19 = (bf16[128,1024]{1,0:T(8,128)(2,1)S(1)}, bf16[128,1024]{1,0:T(8,128)(2,1)S(1)}, u32[]{:S(2)}, u32[]{:S(2)}) collective-permute-start(bf16[128,1024]{1,0:T(8,128)(2,1)S(1)} %constant_dynamic-slice_fusion), channel_id=1, source_target_pairs={{0,2},{1,3},{2,0},{3,1},{4,6},{5,7},{6,4},{7,5},{8,10},{9,11},{10,... | collective-permute-start | bytes 786440 | tf_op jit(solution)/shard_map/ppermute | solution.py:45
  89.7 10.7 %collective-permute-start.15 = (bf16[4,256,128]{2,1,0:T(8,128)(2,1)S(1)}, bf16[4,256,128]{2,1,0:T(8,128)(2,1)S(1)}, u32[]{:S(2)}, u32[]{:S(2)}) collective-permute-start(bf16[4,256,128]{2,1,0:T(8,128)(2,1)S(1)} %slice.14), channel_id=1, source_target_pairs={{0,16},{8,24},{16,0},{24,8},{1,17},{9,25},{17,1},{25,9},{2,18},{10... | collective-permute-start | bytes 786440 | tf_op jit(solution)/shard_map/ppermute | solution.py:45
  90.9 12.3 %collective-permute-start.16 = (bf16[4,256,128]{2,1,0:T(8,128)(2,1)S(1)}, bf16[4,256,128]{2,1,0:T(8,128)(2,1)S(1)}, u32[]{:S(2)}, u32[]{:S(2)}) collective-permute-start(bf16[4,256,128]{2,1,0:T(8,128)(2,1)S(1)} %slice.14), channel_id=1, source_target_pairs={{0,8},{8,16},{16,24},{24,0},{1,9},{9,17},{17,25},{25,1},{2,10},{10... | collective-permute-start | bytes 786440 | tf_op jit(solution)/shard_map/ppermute | solution.py:45
  92.9 12.3 %collective-permute-start.17 = (bf16[4,256,128]{2,1,0:T(8,128)(2,1)S(1)}, bf16[4,256,128]{2,1,0:T(8,128)(2,1)S(1)}, u32[]{:S(2)}, u32[]{:S(2)}) collective-permute-start(bf16[4,256,128]{2,1,0:T(8,128)(2,1)S(1)} %slice.14), channel_id=1, source_target_pairs={{0,24},{8,0},{16,8},{24,16},{1,25},{9,1},{17,9},{25,17},{2,26},{10... | collective-permute-start | bytes 786440 | tf_op jit(solution)/shard_map/ppermute | solution.py:45
  105.3 1.5 collective-permute-start.22
  105.3 1.9 %collective-permute-start.23 = (bf16[4,256,128]{2,1,0:T(8,128)(2,1)S(1)}, bf16[4,256,128]{2,1,0:T(8,128)(2,1)S(1)}, u32[]{:S(2)}, u32[]{:S(2)}) collective-permute-start(bf16[4,256,128]{2,1,0:T(8,128)(2,1)S(1)} %collective-permute-done.17.refs_2_), channel_id=1, source_target_pairs={{0,4},{4,0},{1,5},{5,1},{2,6},{6,2},{3,7},{7,3},{8,12},{12,8},{9,1... | collective-permute-start | bytes 786440 | tf_op jit(solution)/shard_map/ppermute | solution.py:45
  105.8 6.5 %collective-permute-start.24 = (bf16[256,1024]{1,0:T(8,128)(2,1)S(1)}, bf16[256,1024]{1,0:T(8,128)(2,1)S(1)}, u32[]{:S(2)}, u32[]{:S(2)}) collective-permute-start(bf16[256,1024]{1,0:T(8,128)(2,1)S(1)} %collective-permute-done.18.refs_7_), channel_id=1, source_target_pairs={{0,4},{4,0},{1,5},{5,1},{2,6},{6,2},{3,7},{7,3},{8,12},{12,8},{9,1... | collective-permute-start | bytes 1572872 | tf_op jit(solution)/shard_map/ppermute | solution.py:45
  105.8 6.4 %collective-permute-start.21 = (bf16[4,256,128]{2,1,0:T(8,128)(2,1)S(1)}, bf16[4,256,128]{2,1,0:T(8,128)(2,1)S(1)}, u32[]{:S(2)}, u32[]{:S(2)}) collective-permute-start(bf16[4,256,128]{2,1,0:T(8,128)(2,1)S(1)} %collective-permute-done.15.refs_0_), channel_id=1, source_target_pairs={{0,4},{4,0},{1,5},{5,1},{2,6},{6,2},{3,7},{7,3},{8,12},{12,8},{9,1... | collective-permute-start | bytes 786440 | tf_op jit(solution)/shard_map/ppermute | solution.py:45
  106.3 6.0 %collective-permute-start.25 = (bf16[128,1024]{1,0:T(8,128)(2,1)S(1)}, bf16[128,1024]{1,0:T(8,128)(2,1)S(1)}, u32[]{:S(2)}, u32[]{:S(2)}) collective-permute-start(bf16[128,1024]{1,0:T(8,128)(2,1)S(1)} %collective-permute-done.19.refs_8_), channel_id=1, source_target_pairs={{0,4},{4,0},{1,5},{5,1},{2,6},{6,2},{3,7},{7,3},{8,12},{12,8},{9,1... | collective-permute-start | bytes 786440 | tf_op jit(solution)/shard_map/ppermute | solution.py:45
  112.2 18.6 %copy-start.6 = (f32[1024]{0:T(1024)S(1)}, f32[1024]{0:T(1024)}, u32[]{:S(2)}) copy-start(f32[1024]{0:T(1024)} %param.31) | copy-start | bytes 12292
  130.9 16.2 %copy-start.8 = (bf16[1024,4,256]{2,1,0:T(4,128)(2,1)S(1)}, bf16[1024,4,256]{2,1,0:T(4,128)(2,1)}, u32[]{:S(2)}) copy-start(bf16[1024,4,256]{2,1,0:T(4,128)(2,1)} %param.34) | copy-start | bytes 6291460
  133.8 8.2 %collective-permute-start.26 = (bf16[64,1024]{1,0:T(8,128)(2,1)S(1)}, bf16[64,1024]{1,0:T(8,128)(2,1)S(1)}, u32[]{:S(2)}, u32[]{:S(2)}) collective-permute-start(bf16[64,1024]{1,0:T(8,128)(2,1)S(1)} %get-tuple-element.73), channel_id=1, source_target_pairs={{0,1},{1,2},{2,3},{3,0},{4,5},{5,6},{6,7},{7,4},{8,9},{9,10},{10,1... | collective-permute-start | bytes 393224 | tf_op jit(solution)/shard_map/ppermute | solution.py:45
  134.5 7.6 %collective-permute-start.27 = (bf16[64,1024]{1,0:T(8,128)(2,1)S(1)}, bf16[64,1024]{1,0:T(8,128)(2,1)S(1)}, u32[]{:S(2)}, u32[]{:S(2)}) collective-permute-start(bf16[64,1024]{1,0:T(8,128)(2,1)S(1)} %get-tuple-element.75), channel_id=1, source_target_pairs={{0,2},{1,3},{2,0},{3,1},{4,6},{5,7},{6,4},{7,5},{8,10},{9,11},{10,... | collective-permute-start | bytes 393224 | tf_op jit(solution)/shard_map/ppermute | solution.py:45
  135.9 6.8 %collective-permute-start.28 = (bf16[64,1024]{1,0:T(8,128)(2,1)S(1)}, bf16[64,1024]{1,0:T(8,128)(2,1)S(1)}, u32[]{:S(2)}, u32[]{:S(2)}) collective-permute-start(bf16[64,1024]{1,0:T(8,128)(2,1)S(1)} %get-tuple-element.74), channel_id=1, source_target_pairs={{0,3},{1,0},{2,1},{3,2},{4,7},{5,4},{6,5},{7,6},{8,11},{9,8},{10,9... | collective-permute-start | bytes 393224 | tf_op jit(solution)/shard_map/ppermute | solution.py:45
  142.7 7.7 %collective-permute-start.29 = (bf16[64,1024]{1,0:T(8,128)(2,1)S(1)}, bf16[64,1024]{1,0:T(8,128)(2,1)S(1)}, u32[]{:S(2)}, u32[]{:S(2)}) collective-permute-start(bf16[64,1024]{1,0:T(8,128)(2,1)S(1)} %fusion.3.s0), channel_id=1, source_target_pairs={{0,1},{1,2},{2,3},{3,0},{4,5},{5,6},{6,7},{7,4},{8,9},{9,10},{10,1... | collective-permute-start | bytes 393224 | tf_op jit(solution)/shard_map/ppermute | solution.py:45
  143.8 8.3 %collective-permute-start.30 = (bf16[64,1024]{1,0:T(8,128)(2,1)S(1)}, bf16[64,1024]{1,0:T(8,128)(2,1)S(1)}, u32[]{:S(2)}, u32[]{:S(2)}) collective-permute-start(bf16[64,1024]{1,0:T(8,128)(2,1)S(1)} %fusion.3.s0), channel_id=1, source_target_pairs={{0,2},{1,3},{2,0},{3,1},{4,6},{5,7},{6,4},{7,5},{8,10},{9,11},{10,... | collective-permute-start | bytes 393224 | tf_op jit(solution)/shard_map/ppermute | solution.py:45
  146.9 5.3 %collective-permute-start.31 = (bf16[64,1024]{1,0:T(8,128)(2,1)S(1)}, bf16[64,1024]{1,0:T(8,128)(2,1)S(1)}, u32[]{:S(2)}, u32[]{:S(2)}) collective-permute-start(bf16[64,1024]{1,0:T(8,128)(2,1)S(1)} %fusion.3.s0), channel_id=1, source_target_pairs={{0,3},{1,0},{2,1},{3,2},{4,7},{5,4},{6,5},{7,6},{8,11},{9,8},{10,9... | collective-permute-start | bytes 393224 | tf_op jit(solution)/shard_map/ppermute | solution.py:45

commit v11 on v9

--- a/solution.py
+++ b/solution.py
@@ -103,35 +103,32 @@
     return (dot(hot, tab_ref[n]) * cosine + dot(hot, tab_ref[n + 1]) * sine).astype(bf16)
 
 
-def fine_tables_kernel(
-    where_ref, gain_hbm, emb_hbm, wq_hbm, wk_hbm, wv_hbm, fo_hbm,
-    tab_hbm, fo_half, tab_ref, gain_ref, emb_ref, w_ref, sems,
-):
+def fine_tables_kernel(gain_hbm, emb_hbm, wq_hbm, wk_hbm, wv_hbm, tab_hbm, tab_ref, gain_ref, emb_ref, w_ref, sems):
     pairs = [(emb_hbm, emb_ref), (gain_hbm, gain_ref)]
     for n, w in enumerate((wq_hbm, wk_hbm, wv_hbm)):
         for part in range(2):
             rows = pl.ds(part * 512, 512)
             pairs.append((w.at[rows], w_ref.at[n, rows]))
-    half = pl.ds(pl.multiple_of(where_ref[2] * 128, 128), 128)
-    pairs.append((fo_hbm.at[half], fo_half))
     copies = begin_copies(pairs, sems)
     finish_copies(copies[:2])
     fine_in = norm_rows(emb_ref[...].astype(f32), gain_ref[...])
-    finish_copies(copies[2:8])
+    finish_copies(copies[2:])
     tq = dot(fine_in, w_ref[0]) * q_scale
     tk = dot(fine_in, w_ref[1])
     tables = (tq, partner(tq), tk, partner(tk), dot(fine_in, w_ref[2]))
     for n, table in enumerate(tables):
         tab_ref[n] = table.astype(bf16)
     finish_copies(begin_copies([(tab_ref.at[n], tab_hbm.at[n]) for n in range(5)], sems))
-    finish_copies(copies[8:])
 
 
 def fine_kernel(
     where_ref, before_ref, prior_ref, own_ref, tab_hbm, turn_hbm,
-    out_ref, q_ref, k_ref, v_ref, tab_ref, turn_ref, sems,
+    own_hbm, o1, o2, o3, q_ref, k_ref, v_ref, tab_ref, turn_ref, block_ref, sems,
 ):
     step = pl.program_id(0)
+    head = where_ref[1]
+    outs = (block_ref, o1, o2, o3)
+    turns = ((3, 0), (1, 2))
     lowest = jnp.maximum(PAST - where_ref[0] * ROWS, 0)
     head_lane = lax.broadcasted_iota(jnp.int32, (1, SHARE), 1) // HEAD_DIM
 
@@ -184,10 +181,15 @@
         result = jnp.zeros((HALO, SHARE), f32)
         for h in range(4):
             result = jnp.where(head_lane == h, mixed[h * HALO : (h + 1) * HALO], result)
-        out_ref[0, 0:HALO, :] = result.astype(bf16)
+        for s, out_ref in enumerate(outs):
+
+            @pl.when(lax.rem(head + s, 4) == 0)
+            def _(out_ref=out_ref):
+                out_ref[0:HALO, :] = result.astype(bf16)
 
     for late in range(2):
-        place = 2 * step + late
+        turn = jnp.where(step == 0, turns[0][late], turns[1][late])
+        place = lax.rem(head + turn, 4)
         begin = pl.multiple_of((place + 1) * BLOCK, BLOCK)
         keys = k_ref[pl.ds(begin, PAST), :]
         values = v_ref[pl.ds(begin, PAST), :]
@@ -229,11 +231,24 @@
             [jnp.where(low_lanes, results[2 * n], results[2 * n + 1]) for n in range(2)], axis=1
         )
         result = result.astype(bf16)
-        out_ref[place, HALO:, :] = result
-
-        @pl.when(place < 3)
-        def _():
-            out_ref[place + 1, 0:HALO, :] = result[BLOCK - HALO :]
+        for n in range(2):
+
+            @pl.when(step == n)
+            def _(n=n, late=late, result=result, place=place):
+                turn = turns[n][late]
+                outs[turn][HALO:, :] = result
+
+                @pl.when(place < 3)
+                def _():
+                    outs[(turn + 1) % 4][0:HALO, :] = result[BLOCK - HALO :]
+
+    @pl.when(step == 0)
+    def _():
+        pltpu.make_async_copy(block_ref, own_hbm, sems.at[9]).start()
+
+    @pl.when(step == 1)
+    def _():
+        pltpu.make_async_copy(block_ref, own_hbm, sems.at[9]).wait()
 
 
 def vmem():
@@ -283,18 +298,23 @@
 
 
 def fine_rows_kernel(
-    where_ref, ids_ref, emb_ref, got_ref, own_ref, m1, m2, t1, t2, w_hbm,
-    out_ref, w_ref, sems,
+    where_ref, ids_ref, emb_ref, g1, g2, g3, own_ref, m1, m2, t1, t2, w_hbm, block_hbm,
+    out_ref, w_ref, block_ref, sems,
 ):
     place, head, core = where_ref[0], where_ref[1], where_ref[2]
-    copies = begin_copies([(w_hbm.at[n], w_ref.at[n]) for n in range(4)], sems)
-    merged = dot(pick(ids_ref[...]), emb_ref[...]) + dot(got_ref[head], own_ref[...])
-    near, far, apart = sources(head, core)
-    merged += dot(got_ref[near], m1[...]) + dot(got_ref[far], t1[...])
+    copies = begin_copies(
+        [(block_hbm, block_ref)] + [(w_hbm.at[n], w_ref.at[n]) for n in range(4)], sems
+    )
+    merged = dot(pick(ids_ref[...]), emb_ref[...])
+    near = jnp.where(core == 0, g1[...], g3[...])
+    far = jnp.where(core == 0, g3[...], g1[...])
+    merged += dot(near, m1[...]) + dot(far, t1[...])
     at = pl.ds(pl.multiple_of(core * 128, 128), 128)
-    merged += dot(got_ref[apart, :, at], m2[...])
+    merged += dot(g2[:, at], m2[...])
     at = pl.ds(pl.multiple_of(128 - core * 128, 128), 128)
-    merged += dot(got_ref[apart, :, at], t2[...])
+    merged += dot(g2[:, at], t2[...])
+    finish_copies(copies[:1])
+    merged += dot(block_ref[...], own_ref[...])
     rows = 256 + HALO
     token = (
         place * ROWS + head * 256 - HALO + lax.broadcasted_iota(jnp.int32, (rows, D), 0)
@@ -308,7 +328,7 @@
     for d in range(4):
         out_ref[d, 0:256, :] = grouped[:, d * SHARE : (d + 1) * SHARE]
         out_ref[d, 256:rows, :] = fine[256:rows, d * SHARE : (d + 1) * SHARE]
-    finish_copies(copies)
+    finish_copies(copies[1:])
 
 
 def short_part_kernel(group_ref, w_ref, out_ref):
@@ -509,12 +529,13 @@
         out_ref[pl.ds(begin, 256), :] = dot(weave, value).astype(bf16)
 
 
-def fetch_rest(weight, half):
+def fetch_rest(weight, core):
     pairs = []
     for c, step in ((0, 1), (1, 3)):
         pairs += [(4 * c + y, 4 * c + (y + step) % 4) for y in range(4)]
     whole = lax.ppermute(weight, ("core", "head"), pairs)
-    return [whole, shift(half, "head", 2, 4)]
+    half = shift(lax.dynamic_slice_in_dim(weight, core * 128, 128, 0), "head", 2, 4)
+    return [whole, half]
 
 
 def swap_cores(parts):
@@ -557,37 +578,34 @@
 
     prior = later(token_ids, SEQ, 1, 32)
     before = later(token_ids, SEQ, 2, 32)[ROWS - HALO :]
-    tab, fo_half = call(
-        fine_tables_kernel, "fine_tables",
-        [pltpu.HBM((5, 256, SHARE), bf16), pltpu.HBM((128, D), bf16)], [where], [],
+    tab = call(
+        fine_tables_kernel, "fine_tables", pltpu.HBM((5, 256, SHARE), bf16), [], [],
         [
             pltpu.VMEM((5, 256, SHARE), bf16),
             pltpu.VMEM((1, D), f32), pltpu.VMEM((256, D), bf16),
             pltpu.VMEM((3, D, SHARE), bf16), pltpu.SemaphoreType.DMA((9,)),
         ],
-        us=3, hbm=[
-            fine_norm[None], embedding, fine_query, fine_key, fine_value,
-            fine_output,
-        ],
+        us=3, hbm=[fine_norm[None], embedding, fine_query, fine_key, fine_value],
     )
     own_ids_column = token_ids[:, None]
     fine_output_held, own_ids_column = after(fine_output, own_ids_column)
-    out_mine = fetch_rest(fine_output_held, fo_half)
+    out_mine = fetch_rest(fine_output_held, core)
     rows = 256 + HALO
     mixed = call(
-        fine_kernel, "fine_attention", jax.ShapeDtypeStruct((4, rows, SHARE), bf16),
+        fine_kernel, "fine_attention",
+        [pltpu.HBM((rows, SHARE), bf16)] + [jax.ShapeDtypeStruct((rows, SHARE), bf16)] * 3,
         [where], [before[:, None], prior[:, None], own_ids_column],
         [
             pltpu.VMEM((BLOCK + ROWS, SHARE), bf16),
             pltpu.VMEM((KEYS, SHARE), bf16), pltpu.VMEM((KEYS, SHARE), bf16),
             pltpu.VMEM((5, 256, SHARE), bf16), pltpu.VMEM((576, 128), f32),
-            pltpu.SemaphoreType.DMA((10,)),
+            pltpu.VMEM((rows, SHARE), bf16), pltpu.SemaphoreType.DMA((10,)),
         ],
         grid=(2,), us=12, limit=24, hbm=[tab, tables],
     )
 
     out_mine, mixed = after(out_mine, mixed)
-    got = lax.all_to_all(mixed, "head", 0, 0)
+    got = [shift(mixed[s], "head", s, 4) for s in range(1, 4)]
     out_other = swap_cores(out_mine)
     own_ids = lax.dynamic_slice_in_dim(
         jnp.concatenate([prior[ROWS - HALO :], token_ids]), head * 256, rows, 0
@@ -599,8 +617,9 @@
             jax.ShapeDtypeStruct((SHORTEN, SHARE, D), bf16),
         ],
         [where],
-        [own_ids[:, None], embedding, got, fine_output, *out_mine, *out_other],
-        [pltpu.SemaphoreType.DMA((4,))], hbm=[shorten_weight],
+        [own_ids[:, None], embedding, *got, fine_output, *out_mine, *out_other],
+        [pltpu.VMEM((rows, SHARE), bf16), pltpu.SemaphoreType.DMA((5,))],
+        hbm=[shorten_weight, mixed[0]],
     )
     blocks = exchange(lambda d: lax.dynamic_index_in_dim(sends, d, 0, keepdims=False), "head", 4)
 
@@ -624,8 +643,7 @@
     )
 
     coarse_output_held, packed = after(coarse_output, packed)
-    co_half = lax.dynamic_slice_in_dim(coarse_output_held, core * 128, 128, 0)
-    co_mine = fetch_rest(coarse_output_held, co_half)
+    co_mine = fetch_rest(coarse_output_held, core)
     turned = lax.all_to_all(packed, "z", 0, 0)
     kv = turned[:, :COARSE_ROWS]
     far = [shift(kv, "core", 1, 2)]

time: 161 us -> 152 us (0.944)
  waiting for transfers between devices: 53.2 us -> 43.5 us
  Pallas kernels: 44.5 us -> 37.5 us
  starting transfers between devices: 44.3 us -> 51.2 us
    all_to_all x1 -> x0, waiting for transfers between devices: 8.65 us -> none  [local(): got = lax.all_to_all(mixed, 'head', 0, 0)]
    ppermute x28 -> x31, starting transfers between devices: 29.2 us -> 37.7 us  [shift(): lax.ppermute(value, axis, [(i, (i + steps) % count) for i in range(count)])]
    pallas_call x13, Pallas kernels: 44.5 us -> 37.5 us  [call(): pl.pallas_call(kernel, out_shape=shapes, in_specs=[smem()] * len(scalars)...]
    all_to_all x1 -> x0, starting transfers between devices: 3.47 us -> none  [local(): got = lax.all_to_all(mixed, 'head', 0, 0)]
    ppermute x2, starting transfers between devices: 1.05 us -> 2.98 us  [fetch_rest(): whole = lax.ppermute(weight, ('core', 'head'), pairs)]
    ppermute x28 -> x31, waiting for transfers between devices: 37.5 us -> 37.4 us  [shift(): lax.ppermute(value, axis, [(i, (i + steps) % count) for i in range(count)])]
  transfers between devices with their start and end apart: 34 -> 36, of which waited for: 21 -> 21; matrix products, arithmetic and copies ran while one was open for 2% -> 2% of each run, Pallas kernels for 19% -> 16%
where the time goes in v11:
time: 152 us
  starting transfers between devices  51.2 us (34%)
  waiting for transfers between devices  43.5 us (29%)
  Pallas kernels  37.5 us (25%)
  blocking collectives  15.7 us (10%)
  local copies, waits for them, and re-layouts  3.13 us (2%)
    ppermute x31, starting transfers between devices, shift(): lax.ppermute(value, axis, [(i, (i + steps) % count) for i in range(count)])  37.7 us
    pallas_call x13, Pallas kernels, call(): pl.pallas_call(kernel, out_shape=shapes, in_specs=[smem()] * len(scalars)...  37.5 us
    ppermute x31, waiting for transfers between devices, shift(): lax.ppermute(value, axis, [(i, (i + steps) % count) for i in range(count)])  37.4 us
    all_to_all x1, blocking collectives, local(): heads_in = lax.all_to_all(wide_sends, ('z', 'head'), 0, 0)  15.7 us
    all_to_all x1, waiting for transfers between devices, local(): turned = lax.all_to_all(packed, 'z', 0, 0)  6.05 us
    ppermute x2, starting transfers between devices, later(): lax.ppermute(value, axis, [(i, i + steps) for i in range(count - steps)])  5.65 us
    all_to_all x1, starting transfers between devices, local(): turned = lax.all_to_all(packed, 'z', 0, 0)  4.86 us
  transfers between devices with their start and end apart: 36, of which 21 were waited for; matrix products, arithmetic and copies ran while one was open for 2% of the time, Pallas kernels for 16%

profile of v11, /device:TPU:6, one launch (start us, length us, event | category | flops | bytes accessed | tf_op | source)
XLA Modules:
  0.0 151.7 jit_solution(2442644536671303650)
XLA Ops:
  0.0 1.9 %collective-permute-start = (s32[1024]{0:T(1024)}, s32[1024]{0:T(1024)S(1)}, u32[]{:S(2)}, u32[]{:S(2)}) collective-permute-start(s32[1024]{0:T(1024)} %param.18), channel_id=1, source_target_pairs={{0,4},{4,8},{8,12},{12,16},{16,20},{20,24},{24,28},{28,32},{32,36}... | collective-permute-start | bytes 12296 | tf_op jit(solution)/shard_map/ppermute | solution.py:49
  1.9 3.7 %collective-permute-start.3 = (s32[1024]{0:T(1024)}, s32[1024]{0:T(1024)S(1)}, u32[]{:S(2)}, u32[]{:S(2)}) collective-permute-start(s32[1024]{0:T(1024)} %param.18), channel_id=1, source_target_pairs={{0,8},{4,12},{8,16},{12,20},{16,24},{20,28},{24,32},{28,36},{32,40... | collective-permute-start | bytes 12296 | tf_op jit(solution)/shard_map/ppermute | solution.py:49
  5.7 1.6 %collective-permute-start.1 = (bf16[256,1024]{1,0:T(8,128)(2,1)}, bf16[256,1024]{1,0:T(8,128)(2,1)S(1)}, u32[]{:S(2)}, u32[]{:S(2)}) collective-permute-start(bf16[256,1024]{1,0:T(8,128)(2,1)} %own_ref.1), channel_id=1, source_target_pairs={{0,1},{1,2},{2,3},{3,0},{4,7},{5,4},{6,5},{7,6},{8,9},{9,10},{10,1... | collective-permute-start | bytes 1572872 | tf_op jit(solution)/shard_map/ppermute | solution.py:536
  7.3 1.7 %constant_dynamic-slice_fusion.1 = bf16[128,1024]{1,0:T(8,128)(2,1)} fusion(bf16[256,1024]{1,0:T(8,128)(2,1)} %own_ref.1, s32[]{:T(128)S(6)} %select_n.54), kind=kLoop, calls=%fused_computation.16 | loop fusion | bytes 524292 | tf_op jit(solution)/shard_map/dynamic_slice | solution.py:537
  9.0 2.9 %collective-permute-start.2 = (bf16[128,1024]{1,0:T(8,128)(2,1)}, bf16[128,1024]{1,0:T(8,128)(2,1)S(1)}, u32[]{:S(2)}, u32[]{:S(2)}) collective-permute-start(bf16[128,1024]{1,0:T(8,128)(2,1)} %constant_dynamic-slice_fusion.1), channel_id=1, source_target_pairs={{0,2},{1,3},{2,0},{3,1},{4,6},{5,7},{6,4},{7,5},{8,10},{9,11},{10,... | collective-permute-start | bytes 786440 | tf_op jit(solution)/shard_map/ppermute | solution.py:45
  11.9 3.2 %fine_tables.1.tab_hbm = bf16[5,256,256]{2,1,0:T(8,128)(2,1)} custom-call(f32[1,1024]{1,0:T(1,128)} %bitcast.35, bf16[256,1024]{1,0:T(8,128)(2,1)} %emb_ref.1, bf16[1024,256]{1,0:T(8,128)(2,1)} %wq_hbm.1, bf16[1024,256]{1,0:T(8,128)(2,1)} %wk_hbm.1, bf16[1024,256]{1,0:T(8,128)(2,1)} %wv_hbm.1), custom_call_target="tpu_custom_call" | custom-call | flops 3000000000 | bytes 6000000 | tf_op jit(solution)/shard_map/fine_tables/pallas_call | solution.py:270
  15.8 11.6 %fine_attention.1 = (bf16[272,256]{1,0:T(8,128)(2,1)}, bf16[272,256]{1,0:T(8,128)(2,1)S(1)}, bf16[272,256]{1,0:T(8,128)(2,1)S(1)}, bf16[272,256]{1,0:T(8,128)(2,1)S(1)}) custom-call(s32[3]{0:T(128)S(1)} %pad_add_fusion.where_ref, s32[16,1]{1,0:T(8,128)S(1)} %copy.20.before_ref, s32[1024,1]{1,0:T(8,128)S(1)} %copy.21.prior_ref, s32[1024,1]{1,0:T(8,128)S(1)} %copy.22.own_ref, ...), custom_call_target="tpu_custom_call" | custom-call | flops 12000000000 | bytes 24000000 | tf_op jit(solution)/shard_map/fine_attention/pallas_call | solution.py:270
  27.5 0.5 collective-permute-start.8
  28.0 0.5 collective-permute-start.4
  28.5 2.3 %collective-permute-start.5 = (bf16[272,256]{1,0:T(8,128)(2,1)S(1)}, bf16[272,256]{1,0:T(8,128)(2,1)S(1)}, u32[]{:S(2)}, u32[]{:S(2)}) collective-permute-start(bf16[272,256]{1,0:T(8,128)(2,1)S(1)} %get-tuple-element.49), channel_id=1, source_target_pairs={{0,2},{1,3},{2,0},{3,1},{4,6},{5,7},{6,4},{7,5},{8,10},{9,11},{10,... | collective-permute-start | bytes 417800 | tf_op jit(solution)/shard_map/ppermute | solution.py:45
  30.8 2.2 %collective-permute-start.6 = (bf16[272,256]{1,0:T(8,128)(2,1)S(1)}, bf16[272,256]{1,0:T(8,128)(2,1)}, u32[]{:S(2)}, u32[]{:S(2)}) collective-permute-start(bf16[272,256]{1,0:T(8,128)(2,1)S(1)} %get-tuple-element.50), channel_id=1, source_target_pairs={{0,3},{1,0},{2,1},{3,2},{4,7},{5,4},{6,5},{7,6},{8,11},{9,8},{10,9... | collective-permute-start | bytes 417800 | tf_op jit(solution)/shard_map/ppermute | solution.py:45
  33.3 4.6 %collective-permute-done.4.g1 = bf16[272,256]{1,0:T(8,128)(2,1)S(1)} collective-permute-done((bf16[272,256]{1,0:T(8,128)(2,1)S(1)}, bf16[272,256]{1,0:T(8,128)(2,1)S(1)}, u32[]{:S(2)}, u32[]{:S(2)}) %collective-permute-start.4) | collective-permute-done | bytes 139296 | tf_op jit(solution)/shard_map/ppermute | solution.py:45
  37.9 0.7 collective-permute-done.6.g3
  38.6 2.9 %fine_rows.1 = (bf16[4,272,256]{2,1,0:T(8,128)(2,1)S(1)}, bf16[4,256,1024]{2,1,0:T(8,128)(2,1)S(1)}) custom-call(s32[3]{0:T(128)S(1)} %pad_add_fusion.where_ref, s32[272,1]{1,0:T(8,128)S(1)} %broadcast_in_dim.28.ids_ref, bf16[256,1024]{1,0:T(8,128)(2,1)S(1)} %copy-done.1, bf16[272,256]{1,0:T(8,128)(2,1)S(1)} %collective-permute-done.4.g1, ...), custom_call_target="tpu_custom_call" | custom-call | flops 2000000000 | bytes 4000000 | tf_op jit(solution)/shard_map/fine_rows/pallas_call | solution.py:270
  41.5 1.8 %collective-permute-start.9 = (bf16[272,256]{1,0:T(8,128)(2,1)S(1)}, bf16[272,256]{1,0:T(8,128)(2,1)S(1)}, u32[]{:S(2)}, u32[]{:S(2)}) collective-permute-start(bf16[272,256]{1,0:T(8,128)(2,1)S(1)} %get-tuple-element.82), channel_id=1, source_target_pairs={{0,1},{1,2},{2,3},{3,0},{4,5},{5,6},{6,7},{7,4},{8,9},{9,10},{10,1... | collective-permute-start | bytes 417800 | tf_op jit(solution)/shard_map/ppermute | solution.py:45
  43.4 2.4 %collective-permute-start.11 = (bf16[272,256]{1,0:T(8,128)(2,1)S(1)}, bf16[272,256]{1,0:T(8,128)(2,1)S(1)}, u32[]{:S(2)}, u32[]{:S(2)}) collective-permute-start(bf16[272,256]{1,0:T(8,128)(2,1)S(1)} %get-tuple-element.81), channel_id=1, source_target_pairs={{0,2},{1,3},{2,0},{3,1},{4,6},{5,7},{6,4},{7,5},{8,10},{9,11},{10,... | collective-permute-start | bytes 417800 | tf_op jit(solution)/shard_map/ppermute | solution.py:45
  45.7 1.3 collective-permute-start.13
  47.0 1.1 collective-permute-done.9.group_ref.b1
  48.1 0.5 short_part.5
  48.6 3.0 %collective-permute-start.10 = (bf16[64,1024]{1,0:T(8,128)(2,1)S(1)}, bf16[64,1024]{1,0:T(8,128)(2,1)S(1)}, u32[]{:S(2)}, u32[]{:S(2)}) collective-permute-start(bf16[64,1024]{1,0:T(8,128)(2,1)S(1)} %short_part.5), channel_id=1, source_target_pairs={{0,3},{1,0},{2,1},{3,2},{4,7},{5,4},{6,5},{7,6},{8,11},{9,8},{10,9... | collective-permute-start | bytes 393224 | tf_op jit(solution)/shard_map/ppermute | solution.py:45
  51.6 0.4 collective-permute-done.11.group_ref.b2
  52.0 0.5 short_part.6
  52.4 1.1 collective-permute-start.12
  53.6 0.5 short_part.7
  54.0 0.6 collective-permute-start.14
  54.7 0.5 short_part.4
  55.2 1.5 %collective-permute-done.10 = bf16[64,1024]{1,0:T(8,128)(2,1)S(1)} collective-permute-done((bf16[64,1024]{1,0:T(8,128)(2,1)S(1)}, bf16[64,1024]{1,0:T(8,128)(2,1)S(1)}, u32[]{:S(2)}, u32[]{:S(2)}) %collective-permute-start.10) | collective-permute-done | bytes 131104 | tf_op jit(solution)/shard_map/ppermute | solution.py:45
  56.7 3.0 %collective-permute-done.12 = bf16[64,1024]{1,0:T(8,128)(2,1)S(1)} collective-permute-done((bf16[64,1024]{1,0:T(8,128)(2,1)S(1)}, bf16[64,1024]{1,0:T(8,128)(2,1)S(1)}, u32[]{:S(2)}, u32[]{:S(2)}) %collective-permute-start.12) | collective-permute-done | bytes 131104 | tf_op jit(solution)/shard_map/ppermute | solution.py:45
  59.7 1.4 collective-permute-done.14
  61.2 1.9 %collective-permute-start.16 = (bf16[64,1024]{1,0:T(8,128)(2,1)S(1)}, bf16[64,1024]{1,0:T(8,128)(2,1)S(1)}, u32[]{:S(2)}, u32[]{:S(2)}) collective-permute-start(bf16[64,1024]{1,0:T(8,128)(2,1)S(1)} %add_convert_fusion.s0), channel_id=1, source_target_pairs={{0,2},{1,3},{2,0},{3,1},{4,6},{5,7},{6,4},{7,5},{8,10},{9,11},{10,... | collective-permute-start | bytes 393224 | tf_op jit(solution)/shard_map/ppermute | solution.py:45
  63.2 2.1 %collective-permute-start.17 = (bf16[64,1024]{1,0:T(8,128)(2,1)S(1)}, bf16[64,1024]{1,0:T(8,128)(2,1)S(1)}, u32[]{:S(2)}, u32[]{:S(2)}) collective-permute-start(bf16[64,1024]{1,0:T(8,128)(2,1)S(1)} %add_convert_fusion.s0), channel_id=1, source_target_pairs={{0,3},{1,0},{2,1},{3,2},{4,7},{5,4},{6,5},{7,6},{8,11},{9,8},{10,9... | collective-permute-start | bytes 393224 | tf_op jit(solution)/shard_map/ppermute | solution.py:45
  65.3 3.5 %collective-permute-done.15.s1 = bf16[64,1024]{1,0:T(8,128)(2,1)S(1)} collective-permute-done((bf16[64,1024]{1,0:T(8,128)(2,1)S(1)}, bf16[64,1024]{1,0:T(8,128)(2,1)S(1)}, u32[]{:S(2)}, u32[]{:S(2)}) %collective-permute-start.15) | collective-permute-done | bytes 131104 | tf_op jit(solution)/shard_map/ppermute | solution.py:45
  68.8 0.9 collective-permute-done.17.s3
  69.7 2.3 %coarse_pack.1 = (bf16[4,384,128]{2,1,0:T(8,128)(2,1)}, bf16[256,1024]{1,0:T(8,128)(2,1)S(1)}) custom-call(s32[3]{0:T(128)S(1)} %pad_add_fusion.where_ref, bf16[64,1024]{1,0:T(8,128)(2,1)S(1)} %add_convert_fusion.s0, bf16[64,1024]{1,0:T(8,128)(2,1)S(1)} %collective-permute-done.15.s1, bf16[64,1024]{1,0:T(8,128)(2,1)S(1)} %collective-permute-done.16.s2, ...), custom_call_target="tpu_custom_call" | custom-call | flops 2000000000 | bytes 4000000 | tf_op jit(solution)/shard_map/coarse_pack/pallas_call | solution.py:270
  72.0 4.9 %all-to-all-start = ((bf16[4,384,128]{2,1,0:T(8,128)(2,1)}), bf16[4,384,128]{2,1,0:T(8,128)(2,1)S(1)}, u32[]{:S(2)}, u32[]{:S(2)}) async-start(bf16[4,384,128]{2,1,0:T(8,128)(2,1)} %get-tuple-element.57), calls=%async_computation | async-start | bytes 786432 | tf_op jit(solution)/shard_map/all_to_all | solution.py:647
  76.9 1.3 collective-permute-start.21
  78.2 6.0 %all-to-all-done.turned_ref = bf16[4,384,128]{2,1,0:T(8,128)(2,1)S(1)} async-done(((bf16[4,384,128]{2,1,0:T(8,128)(2,1)}), bf16[4,384,128]{2,1,0:T(8,128)(2,1)S(1)}, u32[]{:S(2)}, u32[]{:S(2)}) %all-to-all-start) | async-done | bytes 393248 | tf_op jit(solution)/shard_map/all_to_all | solution.py:647
  84.5 2.0 %collective-permute-start.22 = (bf16[128,1024]{1,0:T(8,128)(2,1)S(1)}, bf16[128,1024]{1,0:T(8,128)(2,1)S(1)}, u32[]{:S(2)}, u32[]{:S(2)}) collective-permute-start(bf16[128,1024]{1,0:T(8,128)(2,1)S(1)} %constant_dynamic-slice_fusion), channel_id=1, source_target_pairs={{0,2},{1,3},{2,0},{3,1},{4,6},{5,7},{6,4},{7,5},{8,10},{9,11},{10,... | collective-permute-start | bytes 786440 | tf_op jit(solution)/shard_map/ppermute | solution.py:45
  86.5 1.7 %collective-permute-start.18 = (bf16[4,256,128]{2,1,0:T(8,128)(2,1)S(1)}, bf16[4,256,128]{2,1,0:T(8,128)(2,1)S(1)}, u32[]{:S(2)}, u32[]{:S(2)}) collective-permute-start(bf16[4,256,128]{2,1,0:T(8,128)(2,1)S(1)} %slice.14), channel_id=1, source_target_pairs={{0,16},{8,24},{16,0},{24,8},{1,17},{9,25},{17,1},{25,9},{2,18},{10... | collective-permute-start | bytes 786440 | tf_op jit(solution)/shard_map/ppermute | solution.py:45
  88.2 2.1 %collective-permute-start.19 = (bf16[4,256,128]{2,1,0:T(8,128)(2,1)S(1)}, bf16[4,256,128]{2,1,0:T(8,128)(2,1)S(1)}, u32[]{:S(2)}, u32[]{:S(2)}) collective-permute-start(bf16[4,256,128]{2,1,0:T(8,128)(2,1)S(1)} %slice.14), channel_id=1, source_target_pairs={{0,8},{8,16},{16,24},{24,0},{1,9},{9,17},{17,25},{25,1},{2,10},{10... | collective-permute-start | bytes 786440 | tf_op jit(solution)/shard_map/ppermute | solution.py:45
  90.3 2.1 %coarse_first.1 = (bf16[1024,128]{1,0:T(8,128)(2,1)S(1)}, f32[1024,128]{1,0:T(8,128)S(1)}, f32[1024,128]{1,0:T(8,128)S(1)}, f32[1024,128]{1,0:T(8,128)S(1)}) custom-call(s32[6]{0:T(128)S(1)} %pad_add_fusion.1.flag_ref, bf16[4,384,128]{2,1,0:T(8,128)(2,1)S(1)} %all-to-all-done.turned_ref, bf16[4,256,128]{2,1,0:T(8,128)(2,1)S(1)} %collective-permute-done.23.far_ref), custom_call_target="tpu_custom_call" | custom-call | flops 3000000000 | bytes 6000000 | tf_op jit(solution)/shard_map/coarse_first/pallas_call | solution.py:270
  92.4 2.3 %collective-permute-done.22.refs_8_ = bf16[128,1024]{1,0:T(8,128)(2,1)S(1)} collective-permute-done((bf16[128,1024]{1,0:T(8,128)(2,1)S(1)}, bf16[128,1024]{1,0:T(8,128)(2,1)S(1)}, u32[]{:S(2)}, u32[]{:S(2)}) %collective-permute-start.22) | collective-permute-done | bytes 262176 | tf_op jit(solution)/shard_map/ppermute | solution.py:45
  94.8 2.4 %collective-permute-done.18.refs_0_ = bf16[4,256,128]{2,1,0:T(8,128)(2,1)S(1)} collective-permute-done((bf16[4,256,128]{2,1,0:T(8,128)(2,1)S(1)}, bf16[4,256,128]{2,1,0:T(8,128)(2,1)S(1)}, u32[]{:S(2)}, u32[]{:S(2)}) %collective-permute-start.18) | collective-permute-done | bytes 262176 | tf_op jit(solution)/shard_map/ppermute | solution.py:45
  97.2 2.8 %collective-permute-done.19.refs_0_ = bf16[4,256,128]{2,1,0:T(8,128)(2,1)S(1)} collective-permute-done((bf16[4,256,128]{2,1,0:T(8,128)(2,1)S(1)}, bf16[4,256,128]{2,1,0:T(8,128)(2,1)S(1)}, u32[]{:S(2)}, u32[]{:S(2)}) %collective-permute-start.19) | collective-permute-done | bytes 262176 | tf_op jit(solution)/shard_map/ppermute | solution.py:45
  100.0 2.0 %collective-permute-done.20.refs_2_ = bf16[4,256,128]{2,1,0:T(8,128)(2,1)S(1)} collective-permute-done((bf16[4,256,128]{2,1,0:T(8,128)(2,1)S(1)}, bf16[4,256,128]{2,1,0:T(8,128)(2,1)S(1)}, u32[]{:S(2)}, u32[]{:S(2)}) %collective-permute-start.20) | collective-permute-done | bytes 262176 | tf_op jit(solution)/shard_map/ppermute | solution.py:45
  102.1 0.5 collective-permute-start.26
  102.6 0.5 collective-permute-start.24
  103.1 0.5 collective-permute-done.25.refs_1_
  103.6 0.4 collective-permute-done.26.refs_3_
  104.0 5.0 %coarse_more.1 = (bf16[1024,1024]{1,0:T(8,128)(2,1)S(1)}, bf16[1024,1024]{1,0:T(8,128)(2,1)S(1)}, f32[1024,128]{1,0:T(8,128)S(1)}, f32[1024,128]{1,0:T(8,128)S(1)}, f32[1024,128]{1,0:T(8,128)S(1)}) custom-call(s32[6]{0:T(128)S(1)} %pad_add_fusion.1.flag_ref, bf16[4,256,128]{2,1,0:T(8,128)(2,1)S(1)} %collective-permute-done.19.refs_0_, ...), custom_call_target="tpu_custom_call" | custom-call | flops 6000000000 | bytes 12000000 | tf_op jit(solution)/shard_map/coarse_more/pallas_call | solution.py:270
  109.1 3.0 %coarse_last.1 = (bf16[1024,1024]{1,0:T(8,128)(2,1)S(1)}, bf16[16,128,128]{2,1,0:T(8,128)(2,1)S(1)}) custom-call(s32[6]{0:T(128)S(1)} %pad_add_fusion.1.flag_ref, bf16[4,256,128]{2,1,0:T(8,128)(2,1)S(1)} %collective-permute-done.18.refs_0_, bf16[4,256,128]{2,1,0:T(8,128)(2,1)S(1)} %collective-permute-done.24.refs_1_, ...), custom_call_target="tpu_custom_call" | custom-call | flops 3000000000 | bytes 6000000 | tf_op jit(solution)/shard_map/coarse_last/pallas_call | solution.py:270
  112.1 15.7 %all_to_all.10.heads_ref = bf16[16,128,128]{2,1,0:T(8,128)(2,1)S(1)} all-to-all(bf16[16,128,128]{2,1,0:T(8,128)(2,1)S(1)} %get-tuple-element.72), channel_id=1, replica_groups=mesh['z'=4,'x'=4,'core'=2,'head'=4] {'z','head'}, dimensions={0} | all-to-all | bytes 1048576 | tf_op jit(solution)/shard_map/all_to_all | solution.py:678
  127.8 2.9 %feed.1 = (bf16[4,64,1024]{2,1,0:T(8,128)(2,1)S(1)}, f32[64,1024]{1,0:T(8,128)S(1)}) custom-call(s32[3]{0:T(128)S(1)} %pad_add_fusion.where_ref, bf16[16,128,128]{2,1,0:T(8,128)(2,1)S(1)} %all_to_all.10.heads_ref, bf16[256,1024]{1,0:T(8,128)(2,1)S(1)} %get-tuple-element.73.short_ref, f32[1,1024]{1,0:T(1,128)S(1)} %bitcast.31, ...), custom_call_target="tpu_custom_call" | custom-call | flops 4000000000 | bytes 8000000 | tf_op jit(solution)/shard_map/feed/pallas_call | solution.py:270
  130.7 0.6 collective-permute-start.29
  131.3 1.4 collective-permute-start.30
  132.7 1.5 collective-permute-start.31
  134.2 4.7 %collective-permute-done.29 = bf16[64,1024]{1,0:T(8,128)(2,1)S(1)} collective-permute-done((bf16[64,1024]{1,0:T(8,128)(2,1)S(1)}, bf16[64,1024]{1,0:T(8,128)(2,1)S(1)}, u32[]{:S(2)}, u32[]{:S(2)}) %collective-permute-start.29) | collective-permute-done | bytes 131104 | tf_op jit(solution)/shard_map/ppermute | solution.py:45
  138.9 0.6 collective-permute-done.31
  139.6 1.1 collective-permute-start.32
  140.7 3.0 %collective-permute-start.33 = (bf16[64,1024]{1,0:T(8,128)(2,1)S(1)}, bf16[64,1024]{1,0:T(8,128)(2,1)S(1)}, u32[]{:S(2)}, u32[]{:S(2)}) collective-permute-start(bf16[64,1024]{1,0:T(8,128)(2,1)S(1)} %fusion.3.s0), channel_id=1, source_target_pairs={{0,2},{1,3},{2,0},{3,1},{4,6},{5,7},{6,4},{7,5},{8,10},{9,11},{10,... | collective-permute-start | bytes 393224 | tf_op jit(solution)/shard_map/ppermute | solution.py:45
  144.0 0.5 copy.24
  144.5 2.8 %collective-permute-done.32.s1 = bf16[64,1024]{1,0:T(8,128)(2,1)S(1)} collective-permute-done((bf16[64,1024]{1,0:T(8,128)(2,1)S(1)}, bf16[64,1024]{1,0:T(8,128)(2,1)S(1)}, u32[]{:S(2)}, u32[]{:S(2)}) %collective-permute-start.32) | collective-permute-done | bytes 131104 | tf_op jit(solution)/shard_map/ppermute | solution.py:45
  147.3 1.7 %collective-permute-done.33.s2 = bf16[64,1024]{1,0:T(8,128)(2,1)S(1)} collective-permute-done((bf16[64,1024]{1,0:T(8,128)(2,1)S(1)}, bf16[64,1024]{1,0:T(8,128)(2,1)S(1)}, u32[]{:S(2)}, u32[]{:S(2)}) %collective-permute-start.33) | collective-permute-done | bytes 131104 | tf_op jit(solution)/shard_map/ppermute | solution.py:45
  149.1 2.7 %final.1 = bf16[1024,256]{1,0:T(8,128)(2,1)} custom-call(s32[3]{0:T(128)S(1)} %pad_add_fusion.where_ref, bf16[64,1024]{1,0:T(8,128)(2,1)S(1)} %fusion.3.s0, bf16[64,1024]{1,0:T(8,128)(2,1)S(1)} %collective-permute-done.32.s1, bf16[64,1024]{1,0:T(8,128)(2,1)S(1)} %collective-permute-done.33.s2, bf16[64,1024]{1,0:T(8,128)(2,1)S(1)} %collective-permute-done.34.s3, ...), custom_call_target="tpu_custom_call" | custom-call | flops 2000000000 | bytes 4000000 | tf_op jit(solution)/shard_map/final/pallas_call | solution.py:270
  (62 shorter events, 2.0 us)
Async XLA Ops:
  0.0 15.4 %collective-permute-start = (s32[1024]{0:T(1024)}, s32[1024]{0:T(1024)S(1)}, u32[]{:S(2)}, u32[]{:S(2)}) collective-permute-start(s32[1024]{0:T(1024)} %param.18), channel_id=1, source_target_pairs={{0,4},{4,8},{8,12},{12,16},{16,20},{20,24},{24,28},{28,32},{32,36}... | collective-permute-start | bytes 12296 | tf_op jit(solution)/shard_map/ppermute | solution.py:49
  1.9 13.7 %collective-permute-start.3 = (s32[1024]{0:T(1024)}, s32[1024]{0:T(1024)S(1)}, u32[]{:S(2)}, u32[]{:S(2)}) collective-permute-start(s32[1024]{0:T(1024)} %param.18), channel_id=1, source_target_pairs={{0,8},{4,12},{8,16},{12,20},{16,24},{20,28},{24,32},{28,36},{32,40... | collective-permute-start | bytes 12296 | tf_op jit(solution)/shard_map/ppermute | solution.py:49
  5.7 21.8 %collective-permute-start.1 = (bf16[256,1024]{1,0:T(8,128)(2,1)}, bf16[256,1024]{1,0:T(8,128)(2,1)S(1)}, u32[]{:S(2)}, u32[]{:S(2)}) collective-permute-start(bf16[256,1024]{1,0:T(8,128)(2,1)} %own_ref.1), channel_id=1, source_target_pairs={{0,1},{1,2},{2,3},{3,0},{4,7},{5,4},{6,5},{7,6},{8,9},{9,10},{10,1... | collective-permute-start | bytes 1572872 | tf_op jit(solution)/shard_map/ppermute | solution.py:536
  9.0 18.4 %collective-permute-start.2 = (bf16[128,1024]{1,0:T(8,128)(2,1)}, bf16[128,1024]{1,0:T(8,128)(2,1)S(1)}, u32[]{:S(2)}, u32[]{:S(2)}) collective-permute-start(bf16[128,1024]{1,0:T(8,128)(2,1)} %constant_dynamic-slice_fusion.1), channel_id=1, source_target_pairs={{0,2},{1,3},{2,0},{3,1},{4,6},{5,7},{6,4},{7,5},{8,10},{9,11},{10,... | collective-permute-start | bytes 786440 | tf_op jit(solution)/shard_map/ppermute | solution.py:45
  11.9 3.2 %copy-start.10 = (s32[1024]{0:T(1024)S(1)}, s32[1024]{0:T(1024)}, u32[]{:S(2)}) copy-start(s32[1024]{0:T(1024)} %param.18) | copy-start | bytes 12292
  15.8 22.8 %copy-start = (bf16[256,1024]{1,0:T(8,128)(2,1)S(1)}, bf16[256,1024]{1,0:T(8,128)(2,1)}, u32[]{:S(2)}) copy-start(bf16[256,1024]{1,0:T(8,128)(2,1)} %own_ref.1) | copy-start | bytes 1572868
  15.8 22.8 %copy-start.1 = (bf16[256,1024]{1,0:T(8,128)(2,1)S(1)}, bf16[256,1024]{1,0:T(8,128)(2,1)}, u32[]{:S(2)}) copy-start(bf16[256,1024]{1,0:T(8,128)(2,1)} %emb_ref.1) | copy-start | bytes 1572868
  27.4 11.1 %collective-permute-start.7 = (bf16[256,1024]{1,0:T(8,128)(2,1)S(1)}, bf16[256,1024]{1,0:T(8,128)(2,1)S(1)}, u32[]{:S(2)}, u32[]{:S(2)}) collective-permute-start(bf16[256,1024]{1,0:T(8,128)(2,1)S(1)} %collective-permute-done.1.m1), channel_id=1, source_target_pairs={{0,4},{4,0},{1,5},{5,1},{2,6},{6,2},{3,7},{7,3},{8,12},{12,8},{9,1... | collective-permute-start | bytes 1572872 | tf_op jit(solution)/shard_map/ppermute | solution.py:45
  27.5 11.0 %collective-permute-start.8 = (bf16[128,1024]{1,0:T(8,128)(2,1)S(1)}, bf16[128,1024]{1,0:T(8,128)(2,1)S(1)}, u32[]{:S(2)}, u32[]{:S(2)}) collective-permute-start(bf16[128,1024]{1,0:T(8,128)(2,1)S(1)} %collective-permute-done.2.m2), channel_id=1, source_target_pairs={{0,4},{4,0},{1,5},{5,1},{2,6},{6,2},{3,7},{7,3},{8,12},{12,8},{9,1... | collective-permute-start | bytes 786440 | tf_op jit(solution)/shard_map/ppermute | solution.py:45
  28.0 9.9 %collective-permute-start.4 = (bf16[272,256]{1,0:T(8,128)(2,1)S(1)}, bf16[272,256]{1,0:T(8,128)(2,1)S(1)}, u32[]{:S(2)}, u32[]{:S(2)}) collective-permute-start(bf16[272,256]{1,0:T(8,128)(2,1)S(1)} %get-tuple-element.48), channel_id=1, source_target_pairs={{0,1},{1,2},{2,3},{3,0},{4,5},{5,6},{6,7},{7,4},{8,9},{9,10},{10,1... | collective-permute-start | bytes 417800 | tf_op jit(solution)/shard_map/ppermute | solution.py:45
  28.5 9.4 %collective-permute-start.5 = (bf16[272,256]{1,0:T(8,128)(2,1)S(1)}, bf16[272,256]{1,0:T(8,128)(2,1)S(1)}, u32[]{:S(2)}, u32[]{:S(2)}) collective-permute-start(bf16[272,256]{1,0:T(8,128)(2,1)S(1)} %get-tuple-element.49), channel_id=1, source_target_pairs={{0,2},{1,3},{2,0},{3,1},{4,6},{5,7},{6,4},{7,5},{8,10},{9,11},{10,... | collective-permute-start | bytes 417800 | tf_op jit(solution)/shard_map/ppermute | solution.py:45
  30.8 7.7 %collective-permute-start.6 = (bf16[272,256]{1,0:T(8,128)(2,1)S(1)}, bf16[272,256]{1,0:T(8,128)(2,1)}, u32[]{:S(2)}, u32[]{:S(2)}) collective-permute-start(bf16[272,256]{1,0:T(8,128)(2,1)S(1)} %get-tuple-element.50), channel_id=1, source_target_pairs={{0,3},{1,0},{2,1},{3,2},{4,7},{5,4},{6,5},{7,6},{8,11},{9,8},{10,9... | collective-permute-start | bytes 417800 | tf_op jit(solution)/shard_map/ppermute | solution.py:45
  41.5 6.6 %collective-permute-start.9 = (bf16[272,256]{1,0:T(8,128)(2,1)S(1)}, bf16[272,256]{1,0:T(8,128)(2,1)S(1)}, u32[]{:S(2)}, u32[]{:S(2)}) collective-permute-start(bf16[272,256]{1,0:T(8,128)(2,1)S(1)} %get-tuple-element.82), channel_id=1, source_target_pairs={{0,1},{1,2},{2,3},{3,0},{4,5},{5,6},{6,7},{7,4},{8,9},{9,10},{10,1... | collective-permute-start | bytes 417800 | tf_op jit(solution)/shard_map/ppermute | solution.py:45
  43.4 8.6 %collective-permute-start.11 = (bf16[272,256]{1,0:T(8,128)(2,1)S(1)}, bf16[272,256]{1,0:T(8,128)(2,1)S(1)}, u32[]{:S(2)}, u32[]{:S(2)}) collective-permute-start(bf16[272,256]{1,0:T(8,128)(2,1)S(1)} %get-tuple-element.81), channel_id=1, source_target_pairs={{0,2},{1,3},{2,0},{3,1},{4,6},{5,7},{6,4},{7,5},{8,10},{9,11},{10,... | collective-permute-start | bytes 417800 | tf_op jit(solution)/shard_map/ppermute | solution.py:45
  45.7 7.8 %collective-permute-start.13 = (bf16[272,256]{1,0:T(8,128)(2,1)S(1)}, bf16[272,256]{1,0:T(8,128)(2,1)S(1)}, u32[]{:S(2)}, u32[]{:S(2)}) collective-permute-start(bf16[272,256]{1,0:T(8,128)(2,1)S(1)} %get-tuple-element.80), channel_id=1, source_target_pairs={{0,3},{1,0},{2,1},{3,2},{4,7},{5,4},{6,5},{7,6},{8,11},{9,8},{10,9... | collective-permute-start | bytes 417800 | tf_op jit(solution)/shard_map/ppermute | solution.py:45
  48.6 8.1 %collective-permute-start.10 = (bf16[64,1024]{1,0:T(8,128)(2,1)S(1)}, bf16[64,1024]{1,0:T(8,128)(2,1)S(1)}, u32[]{:S(2)}, u32[]{:S(2)}) collective-permute-start(bf16[64,1024]{1,0:T(8,128)(2,1)S(1)} %short_part.5), channel_id=1, source_target_pairs={{0,3},{1,0},{2,1},{3,2},{4,7},{5,4},{6,5},{7,6},{8,11},{9,8},{10,9... | collective-permute-start | bytes 393224 | tf_op jit(solution)/shard_map/ppermute | solution.py:45
  52.4 7.3 %collective-permute-start.12 = (bf16[64,1024]{1,0:T(8,128)(2,1)S(1)}, bf16[64,1024]{1,0:T(8,128)(2,1)S(1)}, u32[]{:S(2)}, u32[]{:S(2)}) collective-permute-start(bf16[64,1024]{1,0:T(8,128)(2,1)S(1)} %short_part.6), channel_id=1, source_target_pairs={{0,2},{1,3},{2,0},{3,1},{4,6},{5,7},{6,4},{7,5},{8,10},{9,11},{10,... | collective-permute-start | bytes 393224 | tf_op jit(solution)/shard_map/ppermute | solution.py:45
  54.0 7.0 %collective-permute-start.14 = (bf16[64,1024]{1,0:T(8,128)(2,1)S(1)}, bf16[64,1024]{1,0:T(8,128)(2,1)S(1)}, u32[]{:S(2)}, u32[]{:S(2)}) collective-permute-start(bf16[64,1024]{1,0:T(8,128)(2,1)S(1)} %short_part.7), channel_id=1, source_target_pairs={{0,1},{1,2},{2,3},{3,0},{4,5},{5,6},{6,7},{7,4},{8,9},{9,10},{10,1... | collective-permute-start | bytes 393224 | tf_op jit(solution)/shard_map/ppermute | solution.py:45
  54.7 15.0 %copy-start.2 = (bf16[1024,256]{1,0:T(8,128)(2,1)S(1)}, bf16[1024,256]{1,0:T(8,128)(2,1)}, u32[]{:S(2)}) copy-start(bf16[1024,256]{1,0:T(8,128)(2,1)} %wq_ref.1) | copy-start | bytes 1572868
  54.7 15.0 %copy-start.3 = (bf16[1024,256]{1,0:T(8,128)(2,1)S(1)}, bf16[1024,256]{1,0:T(8,128)(2,1)}, u32[]{:S(2)}) copy-start(bf16[1024,256]{1,0:T(8,128)(2,1)} %wk_ref.1) | copy-start | bytes 1572868
  54.7 15.0 %copy-start.4 = (bf16[1024,256]{1,0:T(8,128)(2,1)S(1)}, bf16[1024,256]{1,0:T(8,128)(2,1)}, u32[]{:S(2)}) copy-start(bf16[1024,256]{1,0:T(8,128)(2,1)} %wv_ref.1) | copy-start | bytes 1572868
  54.7 15.0 %copy-start.5 = (f32[1024]{0:T(1024)S(1)}, f32[1024]{0:T(1024)}, u32[]{:S(2)}) copy-start(f32[1024]{0:T(1024)} %param.26) | copy-start | bytes 12292
  54.7 15.0 %copy-start.7 = (f32[576,128]{1,0:T(8,128)S(1)}, f32[576,128]{1,0:T(8,128)}, u32[]{:S(2)}) copy-start(f32[576,128]{1,0:T(8,128)} %constant.90.clone.turn_hbm.turn_ref) | copy-start | bytes 884740
  61.2 7.7 %collective-permute-start.15 = (bf16[64,1024]{1,0:T(8,128)(2,1)S(1)}, bf16[64,1024]{1,0:T(8,128)(2,1)S(1)}, u32[]{:S(2)}, u32[]{:S(2)}) collective-permute-start(bf16[64,1024]{1,0:T(8,128)(2,1)S(1)} %add_convert_fusion.s0), channel_id=1, source_target_pairs={{0,1},{1,2},{2,3},{3,0},{4,5},{5,6},{6,7},{7,4},{8,9},{9,10},{10,1... | collective-permute-start | bytes 393224 | tf_op jit(solution)/shard_map/ppermute | solution.py:45
  61.2 7.6 %collective-permute-start.16 = (bf16[64,1024]{1,0:T(8,128)(2,1)S(1)}, bf16[64,1024]{1,0:T(8,128)(2,1)S(1)}, u32[]{:S(2)}, u32[]{:S(2)}) collective-permute-start(bf16[64,1024]{1,0:T(8,128)(2,1)S(1)} %add_convert_fusion.s0), channel_id=1, source_target_pairs={{0,2},{1,3},{2,0},{3,1},{4,6},{5,7},{6,4},{7,5},{8,10},{9,11},{10,... | collective-permute-start | bytes 393224 | tf_op jit(solution)/shard_map/ppermute | solution.py:45
  63.2 6.5 %collective-permute-start.17 = (bf16[64,1024]{1,0:T(8,128)(2,1)S(1)}, bf16[64,1024]{1,0:T(8,128)(2,1)S(1)}, u32[]{:S(2)}, u32[]{:S(2)}) collective-permute-start(bf16[64,1024]{1,0:T(8,128)(2,1)S(1)} %add_convert_fusion.s0), channel_id=1, source_target_pairs={{0,3},{1,0},{2,1},{3,2},{4,7},{5,4},{6,5},{7,6},{8,11},{9,8},{10,9... | collective-permute-start | bytes 393224 | tf_op jit(solution)/shard_map/ppermute | solution.py:45
  69.7 7.2 %copy-start.9 = (bf16[256,1024]{1,0:T(8,128)(2,1)S(1)}, bf16[256,1024]{1,0:T(8,128)(2,1)}, u32[]{:S(2)}) copy-start(bf16[256,1024]{1,0:T(8,128)(2,1)} %refs_6_.1) | copy-start | bytes 1572868
  72.0 12.2 %all-to-all-start = ((bf16[4,384,128]{2,1,0:T(8,128)(2,1)}), bf16[4,384,128]{2,1,0:T(8,128)(2,1)S(1)}, u32[]{:S(2)}, u32[]{:S(2)}) async-start(bf16[4,384,128]{2,1,0:T(8,128)(2,1)} %get-tuple-element.57), calls=%async_computation | async-start | bytes 786432 | tf_op jit(solution)/shard_map/all_to_all | solution.py:647
  76.9 17.9 %collective-permute-start.21 = (bf16[256,1024]{1,0:T(8,128)(2,1)S(1)}, bf16[256,1024]{1,0:T(8,128)(2,1)S(1)}, u32[]{:S(2)}, u32[]{:S(2)}) collective-permute-start(bf16[256,1024]{1,0:T(8,128)(2,1)S(1)} %copy-done.9), channel_id=1, source_target_pairs={{0,1},{1,2},{2,3},{3,0},{4,7},{5,4},{6,5},{7,6},{8,9},{9,10},{10,1... | collective-permute-start | bytes 1572872 | tf_op jit(solution)/shard_map/ppermute | solution.py:536
  84.3 6.0 %collective-permute-start.23 = (bf16[4,256,128]{2,1,0:T(8,128)(2,1)S(1)}, bf16[4,256,128]{2,1,0:T(8,128)(2,1)S(1)}, u32[]{:S(2)}, u32[]{:S(2)}) collective-permute-start(bf16[4,256,128]{2,1,0:T(8,128)(2,1)S(1)} %slice.14), channel_id=1, source_target_pairs={{0,4},{4,0},{1,5},{5,1},{2,6},{6,2},{3,7},{7,3},{8,12},{12,8},{9,1... | collective-permute-start | bytes 786440 | tf_op jit(solution)/shard_map/ppermute | solution.py:45
  84.5 10.3 %collective-permute-start.22 = (bf16[128,1024]{1,0:T(8,128)(2,1)S(1)}, bf16[128,1024]{1,0:T(8,128)(2,1)S(1)}, u32[]{:S(2)}, u32[]{:S(2)}) collective-permute-start(bf16[128,1024]{1,0:T(8,128)(2,1)S(1)} %constant_dynamic-slice_fusion), channel_id=1, source_target_pairs={{0,2},{1,3},{2,0},{3,1},{4,6},{5,7},{6,4},{7,5},{8,10},{9,11},{10,... | collective-permute-start | bytes 786440 | tf_op jit(solution)/shard_map/ppermute | solution.py:45
  86.5 10.7 %collective-permute-start.18 = (bf16[4,256,128]{2,1,0:T(8,128)(2,1)S(1)}, bf16[4,256,128]{2,1,0:T(8,128)(2,1)S(1)}, u32[]{:S(2)}, u32[]{:S(2)}) collective-permute-start(bf16[4,256,128]{2,1,0:T(8,128)(2,1)S(1)} %slice.14), channel_id=1, source_target_pairs={{0,16},{8,24},{16,0},{24,8},{1,17},{9,25},{17,1},{25,9},{2,18},{10... | collective-permute-start | bytes 786440 | tf_op jit(solution)/shard_map/ppermute | solution.py:45
  88.2 11.8 %collective-permute-start.19 = (bf16[4,256,128]{2,1,0:T(8,128)(2,1)S(1)}, bf16[4,256,128]{2,1,0:T(8,128)(2,1)S(1)}, u32[]{:S(2)}, u32[]{:S(2)}) collective-permute-start(bf16[4,256,128]{2,1,0:T(8,128)(2,1)S(1)} %slice.14), channel_id=1, source_target_pairs={{0,8},{8,16},{16,24},{24,0},{1,9},{9,17},{17,25},{25,1},{2,10},{10... | collective-permute-start | bytes 786440 | tf_op jit(solution)/shard_map/ppermute | solution.py:45
  90.3 11.7 %collective-permute-start.20 = (bf16[4,256,128]{2,1,0:T(8,128)(2,1)S(1)}, bf16[4,256,128]{2,1,0:T(8,128)(2,1)S(1)}, u32[]{:S(2)}, u32[]{:S(2)}) collective-permute-start(bf16[4,256,128]{2,1,0:T(8,128)(2,1)S(1)} %slice.14), channel_id=1, source_target_pairs={{0,24},{8,0},{16,8},{24,16},{1,25},{9,1},{17,9},{25,17},{2,26},{10... | collective-permute-start | bytes 786440 | tf_op jit(solution)/shard_map/ppermute | solution.py:45
  102.1 1.5 %collective-permute-start.25 = (bf16[4,256,128]{2,1,0:T(8,128)(2,1)S(1)}, bf16[4,256,128]{2,1,0:T(8,128)(2,1)S(1)}, u32[]{:S(2)}, u32[]{:S(2)}) collective-permute-start(bf16[4,256,128]{2,1,0:T(8,128)(2,1)S(1)} %collective-permute-done.19.refs_0_), channel_id=1, source_target_pairs={{0,4},{4,0},{1,5},{5,1},{2,6},{6,2},{3,7},{7,3},{8,12},{12,8},{9,1... | collective-permute-start | bytes 786440 | tf_op jit(solution)/shard_map/ppermute | solution.py:45
  102.1 1.9 %collective-permute-start.26 = (bf16[4,256,128]{2,1,0:T(8,128)(2,1)S(1)}, bf16[4,256,128]{2,1,0:T(8,128)(2,1)S(1)}, u32[]{:S(2)}, u32[]{:S(2)}) collective-permute-start(bf16[4,256,128]{2,1,0:T(8,128)(2,1)S(1)} %collective-permute-done.20.refs_2_), channel_id=1, source_target_pairs={{0,4},{4,0},{1,5},{5,1},{2,6},{6,2},{3,7},{7,3},{8,12},{12,8},{9,1... | collective-permute-start | bytes 786440 | tf_op jit(solution)/shard_map/ppermute | solution.py:45
  102.6 6.5 %collective-permute-start.27 = (bf16[256,1024]{1,0:T(8,128)(2,1)S(1)}, bf16[256,1024]{1,0:T(8,128)(2,1)S(1)}, u32[]{:S(2)}, u32[]{:S(2)}) collective-permute-start(bf16[256,1024]{1,0:T(8,128)(2,1)S(1)} %collective-permute-done.21.refs_7_), channel_id=1, source_target_pairs={{0,4},{4,0},{1,5},{5,1},{2,6},{6,2},{3,7},{7,3},{8,12},{12,8},{9,1... | collective-permute-start | bytes 1572872 | tf_op jit(solution)/shard_map/ppermute | solution.py:45
  102.6 6.4 %collective-permute-start.24 = (bf16[4,256,128]{2,1,0:T(8,128)(2,1)S(1)}, bf16[4,256,128]{2,1,0:T(8,128)(2,1)S(1)}, u32[]{:S(2)}, u32[]{:S(2)}) collective-permute-start(bf16[4,256,128]{2,1,0:T(8,128)(2,1)S(1)} %collective-permute-done.18.refs_0_), channel_id=1, source_target_pairs={{0,4},{4,0},{1,5},{5,1},{2,6},{6,2},{3,7},{7,3},{8,12},{12,8},{9,1... | collective-permute-start | bytes 786440 | tf_op jit(solution)/shard_map/ppermute | solution.py:45
  103.1 6.0 %collective-permute-start.28 = (bf16[128,1024]{1,0:T(8,128)(2,1)S(1)}, bf16[128,1024]{1,0:T(8,128)(2,1)S(1)}, u32[]{:S(2)}, u32[]{:S(2)}) collective-permute-start(bf16[128,1024]{1,0:T(8,128)(2,1)S(1)} %collective-permute-done.22.refs_8_), channel_id=1, source_target_pairs={{0,4},{4,0},{1,5},{5,1},{2,6},{6,2},{3,7},{7,3},{8,12},{12,8},{9,1... | collective-permute-start | bytes 786440 | tf_op jit(solution)/shard_map/ppermute | solution.py:45
  109.1 18.7 %copy-start.6 = (f32[1024]{0:T(1024)S(1)}, f32[1024]{0:T(1024)}, u32[]{:S(2)}) copy-start(f32[1024]{0:T(1024)} %param.31) | copy-start | bytes 12292
  127.8 16.2 %copy-start.8 = (bf16[1024,4,256]{2,1,0:T(4,128)(2,1)S(1)}, bf16[1024,4,256]{2,1,0:T(4,128)(2,1)}, u32[]{:S(2)}) copy-start(bf16[1024,4,256]{2,1,0:T(4,128)(2,1)} %param.34) | copy-start | bytes 6291460
  130.7 8.2 %collective-permute-start.29 = (bf16[64,1024]{1,0:T(8,128)(2,1)S(1)}, bf16[64,1024]{1,0:T(8,128)(2,1)S(1)}, u32[]{:S(2)}, u32[]{:S(2)}) collective-permute-start(bf16[64,1024]{1,0:T(8,128)(2,1)S(1)} %get-tuple-element.83), channel_id=1, source_target_pairs={{0,1},{1,2},{2,3},{3,0},{4,5},{5,6},{6,7},{7,4},{8,9},{9,10},{10,1... | collective-permute-start | bytes 393224 | tf_op jit(solution)/shard_map/ppermute | solution.py:45
  131.3 7.6 %collective-permute-start.30 = (bf16[64,1024]{1,0:T(8,128)(2,1)S(1)}, bf16[64,1024]{1,0:T(8,128)(2,1)S(1)}, u32[]{:S(2)}, u32[]{:S(2)}) collective-permute-start(bf16[64,1024]{1,0:T(8,128)(2,1)S(1)} %get-tuple-element.85), channel_id=1, source_target_pairs={{0,2},{1,3},{2,0},{3,1},{4,6},{5,7},{6,4},{7,5},{8,10},{9,11},{10,... | collective-permute-start | bytes 393224 | tf_op jit(solution)/shard_map/ppermute | solution.py:45
  132.7 6.8 %collective-permute-start.31 = (bf16[64,1024]{1,0:T(8,128)(2,1)S(1)}, bf16[64,1024]{1,0:T(8,128)(2,1)S(1)}, u32[]{:S(2)}, u32[]{:S(2)}) collective-permute-start(bf16[64,1024]{1,0:T(8,128)(2,1)S(1)} %get-tuple-element.84), channel_id=1, source_target_pairs={{0,3},{1,0},{2,1},{3,2},{4,7},{5,4},{6,5},{7,6},{8,11},{9,8},{10,9... | collective-permute-start | bytes 393224 | tf_op jit(solution)/shard_map/ppermute | solution.py:45
  139.6 7.7 %collective-permute-start.32 = (bf16[64,1024]{1,0:T(8,128)(2,1)S(1)}, bf16[64,1024]{1,0:T(8,128)(2,1)S(1)}, u32[]{:S(2)}, u32[]{:S(2)}) collective-permute-start(bf16[64,1024]{1,0:T(8,128)(2,1)S(1)} %fusion.3.s0), channel_id=1, source_target_pairs={{0,1},{1,2},{2,3},{3,0},{4,5},{5,6},{6,7},{7,4},{8,9},{9,10},{10,1... | collective-permute-start | bytes 393224 | tf_op jit(solution)/shard_map/ppermute | solution.py:45
  140.7 8.2 %collective-permute-start.33 = (bf16[64,1024]{1,0:T(8,128)(2,1)S(1)}, bf16[64,1024]{1,0:T(8,128)(2,1)S(1)}, u32[]{:S(2)}, u32[]{:S(2)}) collective-permute-start(bf16[64,1024]{1,0:T(8,128)(2,1)S(1)} %fusion.3.s0), channel_id=1, source_target_pairs={{0,2},{1,3},{2,0},{3,1},{4,6},{5,7},{6,4},{7,5},{8,10},{9,11},{10,... | collective-permute-start | bytes 393224 | tf_op jit(solution)/shard_map/ppermute | solution.py:45
  143.8 5.3 %collective-permute-start.34 = (bf16[64,1024]{1,0:T(8,128)(2,1)S(1)}, bf16[64,1024]{1,0:T(8,128)(2,1)S(1)}, u32[]{:S(2)}, u32[]{:S(2)}) collective-permute-start(bf16[64,1024]{1,0:T(8,128)(2,1)S(1)} %fusion.3.s0), channel_id=1, source_target_pairs={{0,3},{1,0},{2,1},{3,2},{4,7},{5,4},{6,5},{7,6},{8,11},{9,8},{10,9... | collective-permute-start | bytes 393224 | tf_op jit(solution)/shard_map/ppermute | solution.py:45

commit v12 on v11

--- a/solution.py
+++ b/solution.py
@@ -404,7 +404,10 @@
         acc_ref[at, :] = acc_ref[at, :] * factor + contrib[:, :128]
 
 
-def coarse_first_kernel(flag_ref, turned_ref, far_ref, q_ref, top_ref, total_ref, acc_ref):
+def coarse_first_kernel(
+    flag_ref, turned_ref, far_ref, up_hbm, up_ref, q_ref, top_ref, total_ref, acc_ref, sems
+):
+    copies = begin_copies([(up_hbm, up_ref)], sems)
     half = COARSE_ROWS // 2
     low_lanes = lax.broadcasted_iota(jnp.int32, (1, 128), 1) < 64
     row = lax.broadcasted_iota(jnp.int32, (256, 256), 0)
@@ -437,6 +440,8 @@
     def _():
         absorb(state, [(z * 256, 256, [far_ref[z]]) for z in range(4)])
 
+    finish_copies(copies)
+
 
 def coarse_more_kernel(which, last, flag_ref, *refs):
     count = 2 * len(which)
@@ -451,7 +456,7 @@
         pairs = place_copies(flag_ref[4], flag_ref[5], own, (m1, m2), (t1, t2), target)
     else:
         pairs = []
-        for a, b in zip(refs[:2], refs[2:4]):
+        for a, b in zip(refs[:1], refs[1:2]):
             for part in range(4):
                 at = pl.ds(part * 256, 256)
                 pairs.append((a.at[at], b.at[at]))
@@ -652,20 +657,21 @@
     flags = ((x_place - steps + 4) % 4 < x_place).astype(jnp.int32) + (steps == 0) * core
     flags = jnp.concatenate([flags, where[1:]])
     wide = jax.ShapeDtypeStruct((1024, 128), f32)
-    q_all, *sums = call(
+    square = jax.ShapeDtypeStruct((D, D), bf16)
+    up_near, q_all, *sums = call(
         coarse_first_kernel, "coarse_first",
-        [jax.ShapeDtypeStruct((1024, 128), bf16), wide, wide, wide], [flags], [turned, far[0]],
-        us=3, limit=24,
+        [square, jax.ShapeDtypeStruct((1024, 128), bf16), wide, wide, wide],
+        [flags], [turned, far[0]], [pltpu.SemaphoreType.DMA((1,))],
+        us=3, limit=24, hbm=[ffn_up],
     )
     near_held, co_held, q_all = lax.optimization_barrier((near, co_mine, q_all))
     far += [shift(part, "core", 1, 2) for part in near_held]
     co_other = swap_cores(co_held)
-    square = jax.ShapeDtypeStruct((D, D), bf16)
-    up_near, down_near, *sums = call(
+    down_near, *sums = call(
         functools.partial(coarse_more_kernel, (1, 3), False), "coarse_more",
-        [square, square, wide, wide, wide],
+        [square, wide, wide, wide],
         [flags], [near[0], far[1], near[2], far[3], q_all, *sums],
-        [pltpu.SemaphoreType.DMA((8,))], us=6, limit=24, hbm=[ffn_up, ffn_down],
+        [pltpu.SemaphoreType.DMA((4,))], us=6, limit=24, hbm=[ffn_down],
     )
     output_near, wide_sends = call(
         functools.partial(coarse_more_kernel, (2,), True), "coarse_last",

time: 152 us -> 152 us (level)
  no operation moved by 1% of the time
where the time goes in v12:
time: 152 us
  starting transfers between devices  51.2 us (34%)
  waiting for transfers between devices  43.3 us (28%)
  Pallas kernels  37.6 us (25%)
  blocking collectives  15.7 us (10%)
  local copies, waits for them, and re-layouts  3.13 us (2%)
    ppermute x31, starting transfers between devices, shift(): lax.ppermute(value, axis, [(i, (i + steps) % count) for i in range(count)])  37.7 us
    pallas_call x13, Pallas kernels, call(): pl.pallas_call(kernel, out_shape=shapes, in_specs=[smem()] * len(scalars)...  37.6 us
    ppermute x31, waiting for transfers between devices, shift(): lax.ppermute(value, axis, [(i, (i + steps) % count) for i in range(count)])  37.3 us
    all_to_all x1, blocking collectives, local(): heads_in = lax.all_to_all(wide_sends, ('z', 'head'), 0, 0)  15.7 us
    all_to_all x1, waiting for transfers between devices, local(): turned = lax.all_to_all(packed, 'z', 0, 0)  6.05 us
    ppermute x2, starting transfers between devices, later(): lax.ppermute(value, axis, [(i, i + steps) for i in range(count - steps)])  5.65 us
    all_to_all x1, starting transfers between devices, local(): turned = lax.all_to_all(packed, 'z', 0, 0)  4.86 us
  transfers between devices with their start and end apart: 36, of which 21 were waited for; matrix products, arithmetic and copies ran while one was open for 2% of the time, Pallas kernels for 16%

profile of v12, /device:TPU:6, one launch (start us, length us, event | category | flops | bytes accessed | tf_op | source)
XLA Modules:
  0.0 151.7 jit_solution(7097296920601067630)
XLA Ops:
  0.0 1.9 %collective-permute-start = (s32[1024]{0:T(1024)}, s32[1024]{0:T(1024)S(1)}, u32[]{:S(2)}, u32[]{:S(2)}) collective-permute-start(s32[1024]{0:T(1024)} %param.18), channel_id=1, source_target_pairs={{0,4},{4,8},{8,12},{12,16},{16,20},{20,24},{24,28},{28,32},{32,36}... | collective-permute-start | bytes 12296 | tf_op jit(solution)/shard_map/ppermute | solution.py:49
  1.9 3.7 %collective-permute-start.3 = (s32[1024]{0:T(1024)}, s32[1024]{0:T(1024)S(1)}, u32[]{:S(2)}, u32[]{:S(2)}) collective-permute-start(s32[1024]{0:T(1024)} %param.18), channel_id=1, source_target_pairs={{0,8},{4,12},{8,16},{12,20},{16,24},{20,28},{24,32},{28,36},{32,40... | collective-permute-start | bytes 12296 | tf_op jit(solution)/shard_map/ppermute | solution.py:49
  5.7 1.6 %collective-permute-start.1 = (bf16[256,1024]{1,0:T(8,128)(2,1)}, bf16[256,1024]{1,0:T(8,128)(2,1)S(1)}, u32[]{:S(2)}, u32[]{:S(2)}) collective-permute-start(bf16[256,1024]{1,0:T(8,128)(2,1)} %own_ref.1), channel_id=1, source_target_pairs={{0,1},{1,2},{2,3},{3,0},{4,7},{5,4},{6,5},{7,6},{8,9},{9,10},{10,1... | collective-permute-start | bytes 1572872 | tf_op jit(solution)/shard_map/ppermute | solution.py:541
  7.3 1.7 %constant_dynamic-slice_fusion.1 = bf16[128,1024]{1,0:T(8,128)(2,1)} fusion(bf16[256,1024]{1,0:T(8,128)(2,1)} %own_ref.1, s32[]{:T(128)S(6)} %select_n.54), kind=kLoop, calls=%fused_computation.16 | loop fusion | bytes 524292 | tf_op jit(solution)/shard_map/dynamic_slice | solution.py:542
  9.0 2.9 %collective-permute-start.2 = (bf16[128,1024]{1,0:T(8,128)(2,1)}, bf16[128,1024]{1,0:T(8,128)(2,1)S(1)}, u32[]{:S(2)}, u32[]{:S(2)}) collective-permute-start(bf16[128,1024]{1,0:T(8,128)(2,1)} %constant_dynamic-slice_fusion.1), channel_id=1, source_target_pairs={{0,2},{1,3},{2,0},{3,1},{4,6},{5,7},{6,4},{7,5},{8,10},{9,11},{10,... | collective-permute-start | bytes 786440 | tf_op jit(solution)/shard_map/ppermute | solution.py:45
  11.9 3.2 %fine_tables.1.tab_hbm = bf16[5,256,256]{2,1,0:T(8,128)(2,1)} custom-call(f32[1,1024]{1,0:T(1,128)} %bitcast.35, bf16[256,1024]{1,0:T(8,128)(2,1)} %emb_ref.1, bf16[1024,256]{1,0:T(8,128)(2,1)} %wq_hbm.1, bf16[1024,256]{1,0:T(8,128)(2,1)} %wk_hbm.1, bf16[1024,256]{1,0:T(8,128)(2,1)} %wv_hbm.1), custom_call_target="tpu_custom_call" | custom-call | flops 3000000000 | bytes 6000000 | tf_op jit(solution)/shard_map/fine_tables/pallas_call | solution.py:270
  15.8 11.6 %fine_attention.1 = (bf16[272,256]{1,0:T(8,128)(2,1)}, bf16[272,256]{1,0:T(8,128)(2,1)S(1)}, bf16[272,256]{1,0:T(8,128)(2,1)S(1)}, bf16[272,256]{1,0:T(8,128)(2,1)S(1)}) custom-call(s32[3]{0:T(128)S(1)} %pad_add_fusion.where_ref, s32[16,1]{1,0:T(8,128)S(1)} %copy.20.before_ref, s32[1024,1]{1,0:T(8,128)S(1)} %copy.21.prior_ref, s32[1024,1]{1,0:T(8,128)S(1)} %copy.22.own_ref, ...), custom_call_target="tpu_custom_call" | custom-call | flops 12000000000 | bytes 24000000 | tf_op jit(solution)/shard_map/fine_attention/pallas_call | solution.py:270
  27.5 0.5 collective-permute-start.8
  28.0 0.5 collective-permute-start.4
  28.5 2.3 %collective-permute-start.5 = (bf16[272,256]{1,0:T(8,128)(2,1)S(1)}, bf16[272,256]{1,0:T(8,128)(2,1)S(1)}, u32[]{:S(2)}, u32[]{:S(2)}) collective-permute-start(bf16[272,256]{1,0:T(8,128)(2,1)S(1)} %get-tuple-element.49), channel_id=1, source_target_pairs={{0,2},{1,3},{2,0},{3,1},{4,6},{5,7},{6,4},{7,5},{8,10},{9,11},{10,... | collective-permute-start | bytes 417800 | tf_op jit(solution)/shard_map/ppermute | solution.py:45
  30.8 2.2 %collective-permute-start.6 = (bf16[272,256]{1,0:T(8,128)(2,1)S(1)}, bf16[272,256]{1,0:T(8,128)(2,1)}, u32[]{:S(2)}, u32[]{:S(2)}) collective-permute-start(bf16[272,256]{1,0:T(8,128)(2,1)S(1)} %get-tuple-element.50), channel_id=1, source_target_pairs={{0,3},{1,0},{2,1},{3,2},{4,7},{5,4},{6,5},{7,6},{8,11},{9,8},{10,9... | collective-permute-start | bytes 417800 | tf_op jit(solution)/shard_map/ppermute | solution.py:45
  33.3 4.6 %collective-permute-done.4.g1 = bf16[272,256]{1,0:T(8,128)(2,1)S(1)} collective-permute-done((bf16[272,256]{1,0:T(8,128)(2,1)S(1)}, bf16[272,256]{1,0:T(8,128)(2,1)S(1)}, u32[]{:S(2)}, u32[]{:S(2)}) %collective-permute-start.4) | collective-permute-done | bytes 139296 | tf_op jit(solution)/shard_map/ppermute | solution.py:45
  37.9 0.7 collective-permute-done.6.g3
  38.6 2.9 %fine_rows.1 = (bf16[4,272,256]{2,1,0:T(8,128)(2,1)S(1)}, bf16[4,256,1024]{2,1,0:T(8,128)(2,1)S(1)}) custom-call(s32[3]{0:T(128)S(1)} %pad_add_fusion.where_ref, s32[272,1]{1,0:T(8,128)S(1)} %broadcast_in_dim.28.ids_ref, bf16[256,1024]{1,0:T(8,128)(2,1)S(1)} %copy-done.1, bf16[272,256]{1,0:T(8,128)(2,1)S(1)} %collective-permute-done.4.g1, ...), custom_call_target="tpu_custom_call" | custom-call | flops 2000000000 | bytes 4000000 | tf_op jit(solution)/shard_map/fine_rows/pallas_call | solution.py:270
  41.5 1.8 %collective-permute-start.9 = (bf16[272,256]{1,0:T(8,128)(2,1)S(1)}, bf16[272,256]{1,0:T(8,128)(2,1)S(1)}, u32[]{:S(2)}, u32[]{:S(2)}) collective-permute-start(bf16[272,256]{1,0:T(8,128)(2,1)S(1)} %get-tuple-element.82), channel_id=1, source_target_pairs={{0,1},{1,2},{2,3},{3,0},{4,5},{5,6},{6,7},{7,4},{8,9},{9,10},{10,1... | collective-permute-start | bytes 417800 | tf_op jit(solution)/shard_map/ppermute | solution.py:45
  43.4 2.4 %collective-permute-start.11 = (bf16[272,256]{1,0:T(8,128)(2,1)S(1)}, bf16[272,256]{1,0:T(8,128)(2,1)S(1)}, u32[]{:S(2)}, u32[]{:S(2)}) collective-permute-start(bf16[272,256]{1,0:T(8,128)(2,1)S(1)} %get-tuple-element.81), channel_id=1, source_target_pairs={{0,2},{1,3},{2,0},{3,1},{4,6},{5,7},{6,4},{7,5},{8,10},{9,11},{10,... | collective-permute-start | bytes 417800 | tf_op jit(solution)/shard_map/ppermute | solution.py:45
  45.7 1.3 collective-permute-start.13
  47.0 1.1 collective-permute-done.9.group_ref.b1
  48.1 0.5 short_part.5
  48.6 3.0 %collective-permute-start.10 = (bf16[64,1024]{1,0:T(8,128)(2,1)S(1)}, bf16[64,1024]{1,0:T(8,128)(2,1)S(1)}, u32[]{:S(2)}, u32[]{:S(2)}) collective-permute-start(bf16[64,1024]{1,0:T(8,128)(2,1)S(1)} %short_part.5), channel_id=1, source_target_pairs={{0,3},{1,0},{2,1},{3,2},{4,7},{5,4},{6,5},{7,6},{8,11},{9,8},{10,9... | collective-permute-start | bytes 393224 | tf_op jit(solution)/shard_map/ppermute | solution.py:45
  51.6 0.4 collective-permute-done.11.group_ref.b2
  52.0 0.5 short_part.6
  52.4 1.1 collective-permute-start.12
  53.6 0.5 short_part.7
  54.0 0.6 collective-permute-start.14
  54.7 0.5 short_part.4
  55.2 1.5 %collective-permute-done.10 = bf16[64,1024]{1,0:T(8,128)(2,1)S(1)} collective-permute-done((bf16[64,1024]{1,0:T(8,128)(2,1)S(1)}, bf16[64,1024]{1,0:T(8,128)(2,1)S(1)}, u32[]{:S(2)}, u32[]{:S(2)}) %collective-permute-start.10) | collective-permute-done | bytes 131104 | tf_op jit(solution)/shard_map/ppermute | solution.py:45
  56.7 3.0 %collective-permute-done.12 = bf16[64,1024]{1,0:T(8,128)(2,1)S(1)} collective-permute-done((bf16[64,1024]{1,0:T(8,128)(2,1)S(1)}, bf16[64,1024]{1,0:T(8,128)(2,1)S(1)}, u32[]{:S(2)}, u32[]{:S(2)}) %collective-permute-start.12) | collective-permute-done | bytes 131104 | tf_op jit(solution)/shard_map/ppermute | solution.py:45
  59.7 1.4 collective-permute-done.14
  61.2 1.9 %collective-permute-start.16 = (bf16[64,1024]{1,0:T(8,128)(2,1)S(1)}, bf16[64,1024]{1,0:T(8,128)(2,1)S(1)}, u32[]{:S(2)}, u32[]{:S(2)}) collective-permute-start(bf16[64,1024]{1,0:T(8,128)(2,1)S(1)} %add_convert_fusion.s0), channel_id=1, source_target_pairs={{0,2},{1,3},{2,0},{3,1},{4,6},{5,7},{6,4},{7,5},{8,10},{9,11},{10,... | collective-permute-start | bytes 393224 | tf_op jit(solution)/shard_map/ppermute | solution.py:45
  63.2 2.1 %collective-permute-start.17 = (bf16[64,1024]{1,0:T(8,128)(2,1)S(1)}, bf16[64,1024]{1,0:T(8,128)(2,1)S(1)}, u32[]{:S(2)}, u32[]{:S(2)}) collective-permute-start(bf16[64,1024]{1,0:T(8,128)(2,1)S(1)} %add_convert_fusion.s0), channel_id=1, source_target_pairs={{0,3},{1,0},{2,1},{3,2},{4,7},{5,4},{6,5},{7,6},{8,11},{9,8},{10,9... | collective-permute-start | bytes 393224 | tf_op jit(solution)/shard_map/ppermute | solution.py:45
  65.3 3.5 %collective-permute-done.15.s1 = bf16[64,1024]{1,0:T(8,128)(2,1)S(1)} collective-permute-done((bf16[64,1024]{1,0:T(8,128)(2,1)S(1)}, bf16[64,1024]{1,0:T(8,128)(2,1)S(1)}, u32[]{:S(2)}, u32[]{:S(2)}) %collective-permute-start.15) | collective-permute-done | bytes 131104 | tf_op jit(solution)/shard_map/ppermute | solution.py:45
  68.8 0.9 collective-permute-done.17.s3
  69.7 2.3 %coarse_pack.1 = (bf16[4,384,128]{2,1,0:T(8,128)(2,1)}, bf16[256,1024]{1,0:T(8,128)(2,1)S(1)}) custom-call(s32[3]{0:T(128)S(1)} %pad_add_fusion.where_ref, bf16[64,1024]{1,0:T(8,128)(2,1)S(1)} %add_convert_fusion.s0, bf16[64,1024]{1,0:T(8,128)(2,1)S(1)} %collective-permute-done.15.s1, bf16[64,1024]{1,0:T(8,128)(2,1)S(1)} %collective-permute-done.16.s2, ...), custom_call_target="tpu_custom_call" | custom-call | flops 2000000000 | bytes 4000000 | tf_op jit(solution)/shard_map/coarse_pack/pallas_call | solution.py:270
  72.0 4.9 %all-to-all-start = ((bf16[4,384,128]{2,1,0:T(8,128)(2,1)}), bf16[4,384,128]{2,1,0:T(8,128)(2,1)S(1)}, u32[]{:S(2)}, u32[]{:S(2)}) async-start(bf16[4,384,128]{2,1,0:T(8,128)(2,1)} %get-tuple-element.57), calls=%async_computation | async-start | bytes 786432 | tf_op jit(solution)/shard_map/all_to_all | solution.py:652
  76.9 1.3 collective-permute-start.21
  78.2 6.0 %all-to-all-done.turned_ref = bf16[4,384,128]{2,1,0:T(8,128)(2,1)S(1)} async-done(((bf16[4,384,128]{2,1,0:T(8,128)(2,1)}), bf16[4,384,128]{2,1,0:T(8,128)(2,1)S(1)}, u32[]{:S(2)}, u32[]{:S(2)}) %all-to-all-start) | async-done | bytes 393248 | tf_op jit(solution)/shard_map/all_to_all | solution.py:652
  84.5 2.0 %collective-permute-start.22 = (bf16[128,1024]{1,0:T(8,128)(2,1)S(1)}, bf16[128,1024]{1,0:T(8,128)(2,1)S(1)}, u32[]{:S(2)}, u32[]{:S(2)}) collective-permute-start(bf16[128,1024]{1,0:T(8,128)(2,1)S(1)} %constant_dynamic-slice_fusion), channel_id=1, source_target_pairs={{0,2},{1,3},{2,0},{3,1},{4,6},{5,7},{6,4},{7,5},{8,10},{9,11},{10,... | collective-permute-start | bytes 786440 | tf_op jit(solution)/shard_map/ppermute | solution.py:45
  86.5 1.7 %collective-permute-start.18 = (bf16[4,256,128]{2,1,0:T(8,128)(2,1)S(1)}, bf16[4,256,128]{2,1,0:T(8,128)(2,1)S(1)}, u32[]{:S(2)}, u32[]{:S(2)}) collective-permute-start(bf16[4,256,128]{2,1,0:T(8,128)(2,1)S(1)} %slice.14), channel_id=1, source_target_pairs={{0,16},{8,24},{16,0},{24,8},{1,17},{9,25},{17,1},{25,9},{2,18},{10... | collective-permute-start | bytes 786440 | tf_op jit(solution)/shard_map/ppermute | solution.py:45
  88.2 2.1 %collective-permute-start.19 = (bf16[4,256,128]{2,1,0:T(8,128)(2,1)S(1)}, bf16[4,256,128]{2,1,0:T(8,128)(2,1)S(1)}, u32[]{:S(2)}, u32[]{:S(2)}) collective-permute-start(bf16[4,256,128]{2,1,0:T(8,128)(2,1)S(1)} %slice.14), channel_id=1, source_target_pairs={{0,8},{8,16},{16,24},{24,0},{1,9},{9,17},{17,25},{25,1},{2,10},{10... | collective-permute-start | bytes 786440 | tf_op jit(solution)/shard_map/ppermute | solution.py:45
  90.3 2.2 %coarse_first.1 = (bf16[1024,1024]{1,0:T(8,128)(2,1)S(1)}, bf16[1024,128]{1,0:T(8,128)(2,1)S(1)}, f32[1024,128]{1,0:T(8,128)S(1)}, f32[1024,128]{1,0:T(8,128)S(1)}, f32[1024,128]{1,0:T(8,128)S(1)}) custom-call(s32[6]{0:T(128)S(1)} %pad_add_fusion.1.flag_ref, bf16[4,384,128]{2,1,0:T(8,128)(2,1)S(1)} %all-to-all-done.turned_ref, ...), custom_call_target="tpu_custom_call" | custom-call | flops 3000000000 | bytes 6000000 | tf_op jit(solution)/shard_map/coarse_first/pallas_call | solution.py:270
  92.6 2.2 %collective-permute-done.22.refs_8_ = bf16[128,1024]{1,0:T(8,128)(2,1)S(1)} collective-permute-done((bf16[128,1024]{1,0:T(8,128)(2,1)S(1)}, bf16[128,1024]{1,0:T(8,128)(2,1)S(1)}, u32[]{:S(2)}, u32[]{:S(2)}) %collective-permute-start.22) | collective-permute-done | bytes 262176 | tf_op jit(solution)/shard_map/ppermute | solution.py:45
  94.8 2.4 %collective-permute-done.18.refs_0_ = bf16[4,256,128]{2,1,0:T(8,128)(2,1)S(1)} collective-permute-done((bf16[4,256,128]{2,1,0:T(8,128)(2,1)S(1)}, bf16[4,256,128]{2,1,0:T(8,128)(2,1)S(1)}, u32[]{:S(2)}, u32[]{:S(2)}) %collective-permute-start.18) | collective-permute-done | bytes 262176 | tf_op jit(solution)/shard_map/ppermute | solution.py:45
  97.2 2.8 %collective-permute-done.19.refs_0_ = bf16[4,256,128]{2,1,0:T(8,128)(2,1)S(1)} collective-permute-done((bf16[4,256,128]{2,1,0:T(8,128)(2,1)S(1)}, bf16[4,256,128]{2,1,0:T(8,128)(2,1)S(1)}, u32[]{:S(2)}, u32[]{:S(2)}) %collective-permute-start.19) | collective-permute-done | bytes 262176 | tf_op jit(solution)/shard_map/ppermute | solution.py:45
  100.0 2.0 %collective-permute-done.20.refs_2_ = bf16[4,256,128]{2,1,0:T(8,128)(2,1)S(1)} collective-permute-done((bf16[4,256,128]{2,1,0:T(8,128)(2,1)S(1)}, bf16[4,256,128]{2,1,0:T(8,128)(2,1)S(1)}, u32[]{:S(2)}, u32[]{:S(2)}) %collective-permute-start.20) | collective-permute-done | bytes 262176 | tf_op jit(solution)/shard_map/ppermute | solution.py:45
  102.1 0.5 collective-permute-start.26
  102.6 0.5 collective-permute-start.24
  103.1 0.5 collective-permute-done.25.refs_1_
  103.6 0.4 collective-permute-done.26.refs_3_
  104.0 5.0 %coarse_more.1 = (bf16[1024,1024]{1,0:T(8,128)(2,1)S(1)}, f32[1024,128]{1,0:T(8,128)S(1)}, f32[1024,128]{1,0:T(8,128)S(1)}, f32[1024,128]{1,0:T(8,128)S(1)}) custom-call(s32[6]{0:T(128)S(1)} %pad_add_fusion.1.flag_ref, bf16[4,256,128]{2,1,0:T(8,128)(2,1)S(1)} %collective-permute-done.19.refs_0_, bf16[4,256,128]{2,1,0:T(8,128)(2,1)S(1)} %collective-permute-done.25.refs_1_, ...), custom_call_target="tpu_custom_call" | custom-call | flops 6000000000 | bytes 12000000 | tf_op jit(solution)/shard_map/coarse_more/pallas_call | solution.py:270
  109.1 3.0 %coarse_last.1 = (bf16[1024,1024]{1,0:T(8,128)(2,1)S(1)}, bf16[16,128,128]{2,1,0:T(8,128)(2,1)S(1)}) custom-call(s32[6]{0:T(128)S(1)} %pad_add_fusion.1.flag_ref, bf16[4,256,128]{2,1,0:T(8,128)(2,1)S(1)} %collective-permute-done.18.refs_0_, bf16[4,256,128]{2,1,0:T(8,128)(2,1)S(1)} %collective-permute-done.24.refs_1_, ...), custom_call_target="tpu_custom_call" | custom-call | flops 3000000000 | bytes 6000000 | tf_op jit(solution)/shard_map/coarse_last/pallas_call | solution.py:270
  112.0 15.7 %all_to_all.10.heads_ref = bf16[16,128,128]{2,1,0:T(8,128)(2,1)S(1)} all-to-all(bf16[16,128,128]{2,1,0:T(8,128)(2,1)S(1)} %get-tuple-element.72), channel_id=1, replica_groups=mesh['z'=4,'x'=4,'core'=2,'head'=4] {'z','head'}, dimensions={0} | all-to-all | bytes 1048576 | tf_op jit(solution)/shard_map/all_to_all | solution.py:684
  127.7 2.9 %feed.1 = (bf16[4,64,1024]{2,1,0:T(8,128)(2,1)S(1)}, f32[64,1024]{1,0:T(8,128)S(1)}) custom-call(s32[3]{0:T(128)S(1)} %pad_add_fusion.where_ref, bf16[16,128,128]{2,1,0:T(8,128)(2,1)S(1)} %all_to_all.10.heads_ref, bf16[256,1024]{1,0:T(8,128)(2,1)S(1)} %get-tuple-element.73.short_ref, f32[1,1024]{1,0:T(1,128)S(1)} %bitcast.31, ...), custom_call_target="tpu_custom_call" | custom-call | flops 4000000000 | bytes 8000000 | tf_op jit(solution)/shard_map/feed/pallas_call | solution.py:270
  130.7 0.6 collective-permute-start.29
  131.3 1.4 collective-permute-start.30
  132.7 1.5 collective-permute-start.31
  134.2 4.7 %collective-permute-done.29 = bf16[64,1024]{1,0:T(8,128)(2,1)S(1)} collective-permute-done((bf16[64,1024]{1,0:T(8,128)(2,1)S(1)}, bf16[64,1024]{1,0:T(8,128)(2,1)S(1)}, u32[]{:S(2)}, u32[]{:S(2)}) %collective-permute-start.29) | collective-permute-done | bytes 131104 | tf_op jit(solution)/shard_map/ppermute | solution.py:45
  138.9 0.6 collective-permute-done.31
  139.6 1.1 collective-permute-start.32
  140.7 3.0 %collective-permute-start.33 = (bf16[64,1024]{1,0:T(8,128)(2,1)S(1)}, bf16[64,1024]{1,0:T(8,128)(2,1)S(1)}, u32[]{:S(2)}, u32[]{:S(2)}) collective-permute-start(bf16[64,1024]{1,0:T(8,128)(2,1)S(1)} %fusion.3.s0), channel_id=1, source_target_pairs={{0,2},{1,3},{2,0},{3,1},{4,6},{5,7},{6,4},{7,5},{8,10},{9,11},{10,... | collective-permute-start | bytes 393224 | tf_op jit(solution)/shard_map/ppermute | solution.py:45
  144.0 0.5 copy.24
  144.5 2.8 %collective-permute-done.32.s1 = bf16[64,1024]{1,0:T(8,128)(2,1)S(1)} collective-permute-done((bf16[64,1024]{1,0:T(8,128)(2,1)S(1)}, bf16[64,1024]{1,0:T(8,128)(2,1)S(1)}, u32[]{:S(2)}, u32[]{:S(2)}) %collective-permute-start.32) | collective-permute-done | bytes 131104 | tf_op jit(solution)/shard_map/ppermute | solution.py:45
  147.2 1.7 %collective-permute-done.33.s2 = bf16[64,1024]{1,0:T(8,128)(2,1)S(1)} collective-permute-done((bf16[64,1024]{1,0:T(8,128)(2,1)S(1)}, bf16[64,1024]{1,0:T(8,128)(2,1)S(1)}, u32[]{:S(2)}, u32[]{:S(2)}) %collective-permute-start.33) | collective-permute-done | bytes 131104 | tf_op jit(solution)/shard_map/ppermute | solution.py:45
  149.0 2.7 %final.1 = bf16[1024,256]{1,0:T(8,128)(2,1)} custom-call(s32[3]{0:T(128)S(1)} %pad_add_fusion.where_ref, bf16[64,1024]{1,0:T(8,128)(2,1)S(1)} %fusion.3.s0, bf16[64,1024]{1,0:T(8,128)(2,1)S(1)} %collective-permute-done.32.s1, bf16[64,1024]{1,0:T(8,128)(2,1)S(1)} %collective-permute-done.33.s2, bf16[64,1024]{1,0:T(8,128)(2,1)S(1)} %collective-permute-done.34.s3, ...), custom_call_target="tpu_custom_call" | custom-call | flops 2000000000 | bytes 4000000 | tf_op jit(solution)/shard_map/final/pallas_call | solution.py:270
  (62 shorter events, 2.0 us)
Async XLA Ops:
  0.0 15.4 %collective-permute-start = (s32[1024]{0:T(1024)}, s32[1024]{0:T(1024)S(1)}, u32[]{:S(2)}, u32[]{:S(2)}) collective-permute-start(s32[1024]{0:T(1024)} %param.18), channel_id=1, source_target_pairs={{0,4},{4,8},{8,12},{12,16},{16,20},{20,24},{24,28},{28,32},{32,36}... | collective-permute-start | bytes 12296 | tf_op jit(solution)/shard_map/ppermute | solution.py:49
  1.9 13.7 %collective-permute-start.3 = (s32[1024]{0:T(1024)}, s32[1024]{0:T(1024)S(1)}, u32[]{:S(2)}, u32[]{:S(2)}) collective-permute-start(s32[1024]{0:T(1024)} %param.18), channel_id=1, source_target_pairs={{0,8},{4,12},{8,16},{12,20},{16,24},{20,28},{24,32},{28,36},{32,40... | collective-permute-start | bytes 12296 | tf_op jit(solution)/shard_map/ppermute | solution.py:49
  5.7 21.8 %collective-permute-start.1 = (bf16[256,1024]{1,0:T(8,128)(2,1)}, bf16[256,1024]{1,0:T(8,128)(2,1)S(1)}, u32[]{:S(2)}, u32[]{:S(2)}) collective-permute-start(bf16[256,1024]{1,0:T(8,128)(2,1)} %own_ref.1), channel_id=1, source_target_pairs={{0,1},{1,2},{2,3},{3,0},{4,7},{5,4},{6,5},{7,6},{8,9},{9,10},{10,1... | collective-permute-start | bytes 1572872 | tf_op jit(solution)/shard_map/ppermute | solution.py:541
  9.0 18.4 %collective-permute-start.2 = (bf16[128,1024]{1,0:T(8,128)(2,1)}, bf16[128,1024]{1,0:T(8,128)(2,1)S(1)}, u32[]{:S(2)}, u32[]{:S(2)}) collective-permute-start(bf16[128,1024]{1,0:T(8,128)(2,1)} %constant_dynamic-slice_fusion.1), channel_id=1, source_target_pairs={{0,2},{1,3},{2,0},{3,1},{4,6},{5,7},{6,4},{7,5},{8,10},{9,11},{10,... | collective-permute-start | bytes 786440 | tf_op jit(solution)/shard_map/ppermute | solution.py:45
  11.9 3.2 %copy-start.10 = (s32[1024]{0:T(1024)S(1)}, s32[1024]{0:T(1024)}, u32[]{:S(2)}) copy-start(s32[1024]{0:T(1024)} %param.18) | copy-start | bytes 12292
  15.8 22.8 %copy-start = (bf16[256,1024]{1,0:T(8,128)(2,1)S(1)}, bf16[256,1024]{1,0:T(8,128)(2,1)}, u32[]{:S(2)}) copy-start(bf16[256,1024]{1,0:T(8,128)(2,1)} %own_ref.1) | copy-start | bytes 1572868
  15.8 22.8 %copy-start.1 = (bf16[256,1024]{1,0:T(8,128)(2,1)S(1)}, bf16[256,1024]{1,0:T(8,128)(2,1)}, u32[]{:S(2)}) copy-start(bf16[256,1024]{1,0:T(8,128)(2,1)} %emb_ref.1) | copy-start | bytes 1572868
  27.4 11.1 %collective-permute-start.7 = (bf16[256,1024]{1,0:T(8,128)(2,1)S(1)}, bf16[256,1024]{1,0:T(8,128)(2,1)S(1)}, u32[]{:S(2)}, u32[]{:S(2)}) collective-permute-start(bf16[256,1024]{1,0:T(8,128)(2,1)S(1)} %collective-permute-done.1.m1), channel_id=1, source_target_pairs={{0,4},{4,0},{1,5},{5,1},{2,6},{6,2},{3,7},{7,3},{8,12},{12,8},{9,1... | collective-permute-start | bytes 1572872 | tf_op jit(solution)/shard_map/ppermute | solution.py:45
  27.5 11.0 %collective-permute-start.8 = (bf16[128,1024]{1,0:T(8,128)(2,1)S(1)}, bf16[128,1024]{1,0:T(8,128)(2,1)S(1)}, u32[]{:S(2)}, u32[]{:S(2)}) collective-permute-start(bf16[128,1024]{1,0:T(8,128)(2,1)S(1)} %collective-permute-done.2.m2), channel_id=1, source_target_pairs={{0,4},{4,0},{1,5},{5,1},{2,6},{6,2},{3,7},{7,3},{8,12},{12,8},{9,1... | collective-permute-start | bytes 786440 | tf_op jit(solution)/shard_map/ppermute | solution.py:45
  28.0 9.9 %collective-permute-start.4 = (bf16[272,256]{1,0:T(8,128)(2,1)S(1)}, bf16[272,256]{1,0:T(8,128)(2,1)S(1)}, u32[]{:S(2)}, u32[]{:S(2)}) collective-permute-start(bf16[272,256]{1,0:T(8,128)(2,1)S(1)} %get-tuple-element.48), channel_id=1, source_target_pairs={{0,1},{1,2},{2,3},{3,0},{4,5},{5,6},{6,7},{7,4},{8,9},{9,10},{10,1... | collective-permute-start | bytes 417800 | tf_op jit(solution)/shard_map/ppermute | solution.py:45
  28.5 9.4 %collective-permute-start.5 = (bf16[272,256]{1,0:T(8,128)(2,1)S(1)}, bf16[272,256]{1,0:T(8,128)(2,1)S(1)}, u32[]{:S(2)}, u32[]{:S(2)}) collective-permute-start(bf16[272,256]{1,0:T(8,128)(2,1)S(1)} %get-tuple-element.49), channel_id=1, source_target_pairs={{0,2},{1,3},{2,0},{3,1},{4,6},{5,7},{6,4},{7,5},{8,10},{9,11},{10,... | collective-permute-start | bytes 417800 | tf_op jit(solution)/shard_map/ppermute | solution.py:45
  30.8 7.7 %collective-permute-start.6 = (bf16[272,256]{1,0:T(8,128)(2,1)S(1)}, bf16[272,256]{1,0:T(8,128)(2,1)}, u32[]{:S(2)}, u32[]{:S(2)}) collective-permute-start(bf16[272,256]{1,0:T(8,128)(2,1)S(1)} %get-tuple-element.50), channel_id=1, source_target_pairs={{0,3},{1,0},{2,1},{3,2},{4,7},{5,4},{6,5},{7,6},{8,11},{9,8},{10,9... | collective-permute-start | bytes 417800 | tf_op jit(solution)/shard_map/ppermute | solution.py:45
  41.5 6.6 %collective-permute-start.9 = (bf16[272,256]{1,0:T(8,128)(2,1)S(1)}, bf16[272,256]{1,0:T(8,128)(2,1)S(1)}, u32[]{:S(2)}, u32[]{:S(2)}) collective-permute-start(bf16[272,256]{1,0:T(8,128)(2,1)S(1)} %get-tuple-element.82), channel_id=1, source_target_pairs={{0,1},{1,2},{2,3},{3,0},{4,5},{5,6},{6,7},{7,4},{8,9},{9,10},{10,1... | collective-permute-start | bytes 417800 | tf_op jit(solution)/shard_map/ppermute | solution.py:45
  43.4 8.6 %collective-permute-start.11 = (bf16[272,256]{1,0:T(8,128)(2,1)S(1)}, bf16[272,256]{1,0:T(8,128)(2,1)S(1)}, u32[]{:S(2)}, u32[]{:S(2)}) collective-permute-start(bf16[272,256]{1,0:T(8,128)(2,1)S(1)} %get-tuple-element.81), channel_id=1, source_target_pairs={{0,2},{1,3},{2,0},{3,1},{4,6},{5,7},{6,4},{7,5},{8,10},{9,11},{10,... | collective-permute-start | bytes 417800 | tf_op jit(solution)/shard_map/ppermute | solution.py:45
  45.7 7.8 %collective-permute-start.13 = (bf16[272,256]{1,0:T(8,128)(2,1)S(1)}, bf16[272,256]{1,0:T(8,128)(2,1)S(1)}, u32[]{:S(2)}, u32[]{:S(2)}) collective-permute-start(bf16[272,256]{1,0:T(8,128)(2,1)S(1)} %get-tuple-element.80), channel_id=1, source_target_pairs={{0,3},{1,0},{2,1},{3,2},{4,7},{5,4},{6,5},{7,6},{8,11},{9,8},{10,9... | collective-permute-start | bytes 417800 | tf_op jit(solution)/shard_map/ppermute | solution.py:45
  48.6 8.1 %collective-permute-start.10 = (bf16[64,1024]{1,0:T(8,128)(2,1)S(1)}, bf16[64,1024]{1,0:T(8,128)(2,1)S(1)}, u32[]{:S(2)}, u32[]{:S(2)}) collective-permute-start(bf16[64,1024]{1,0:T(8,128)(2,1)S(1)} %short_part.5), channel_id=1, source_target_pairs={{0,3},{1,0},{2,1},{3,2},{4,7},{5,4},{6,5},{7,6},{8,11},{9,8},{10,9... | collective-permute-start | bytes 393224 | tf_op jit(solution)/shard_map/ppermute | solution.py:45
  52.4 7.3 %collective-permute-start.12 = (bf16[64,1024]{1,0:T(8,128)(2,1)S(1)}, bf16[64,1024]{1,0:T(8,128)(2,1)S(1)}, u32[]{:S(2)}, u32[]{:S(2)}) collective-permute-start(bf16[64,1024]{1,0:T(8,128)(2,1)S(1)} %short_part.6), channel_id=1, source_target_pairs={{0,2},{1,3},{2,0},{3,1},{4,6},{5,7},{6,4},{7,5},{8,10},{9,11},{10,... | collective-permute-start | bytes 393224 | tf_op jit(solution)/shard_map/ppermute | solution.py:45
  54.0 7.0 %collective-permute-start.14 = (bf16[64,1024]{1,0:T(8,128)(2,1)S(1)}, bf16[64,1024]{1,0:T(8,128)(2,1)S(1)}, u32[]{:S(2)}, u32[]{:S(2)}) collective-permute-start(bf16[64,1024]{1,0:T(8,128)(2,1)S(1)} %short_part.7), channel_id=1, source_target_pairs={{0,1},{1,2},{2,3},{3,0},{4,5},{5,6},{6,7},{7,4},{8,9},{9,10},{10,1... | collective-permute-start | bytes 393224 | tf_op jit(solution)/shard_map/ppermute | solution.py:45
  54.7 15.0 %copy-start.2 = (bf16[1024,256]{1,0:T(8,128)(2,1)S(1)}, bf16[1024,256]{1,0:T(8,128)(2,1)}, u32[]{:S(2)}) copy-start(bf16[1024,256]{1,0:T(8,128)(2,1)} %wq_ref.1) | copy-start | bytes 1572868
  54.7 15.0 %copy-start.3 = (bf16[1024,256]{1,0:T(8,128)(2,1)S(1)}, bf16[1024,256]{1,0:T(8,128)(2,1)}, u32[]{:S(2)}) copy-start(bf16[1024,256]{1,0:T(8,128)(2,1)} %wk_ref.1) | copy-start | bytes 1572868
  54.7 15.0 %copy-start.4 = (bf16[1024,256]{1,0:T(8,128)(2,1)S(1)}, bf16[1024,256]{1,0:T(8,128)(2,1)}, u32[]{:S(2)}) copy-start(bf16[1024,256]{1,0:T(8,128)(2,1)} %wv_ref.1) | copy-start | bytes 1572868
  54.7 15.0 %copy-start.5 = (f32[1024]{0:T(1024)S(1)}, f32[1024]{0:T(1024)}, u32[]{:S(2)}) copy-start(f32[1024]{0:T(1024)} %param.26) | copy-start | bytes 12292
  54.7 15.0 %copy-start.7 = (f32[576,128]{1,0:T(8,128)S(1)}, f32[576,128]{1,0:T(8,128)}, u32[]{:S(2)}) copy-start(f32[576,128]{1,0:T(8,128)} %constant.90.clone.turn_hbm.turn_ref) | copy-start | bytes 884740
  61.2 7.7 %collective-permute-start.15 = (bf16[64,1024]{1,0:T(8,128)(2,1)S(1)}, bf16[64,1024]{1,0:T(8,128)(2,1)S(1)}, u32[]{:S(2)}, u32[]{:S(2)}) collective-permute-start(bf16[64,1024]{1,0:T(8,128)(2,1)S(1)} %add_convert_fusion.s0), channel_id=1, source_target_pairs={{0,1},{1,2},{2,3},{3,0},{4,5},{5,6},{6,7},{7,4},{8,9},{9,10},{10,1... | collective-permute-start | bytes 393224 | tf_op jit(solution)/shard_map/ppermute | solution.py:45
  61.2 7.6 %collective-permute-start.16 = (bf16[64,1024]{1,0:T(8,128)(2,1)S(1)}, bf16[64,1024]{1,0:T(8,128)(2,1)S(1)}, u32[]{:S(2)}, u32[]{:S(2)}) collective-permute-start(bf16[64,1024]{1,0:T(8,128)(2,1)S(1)} %add_convert_fusion.s0), channel_id=1, source_target_pairs={{0,2},{1,3},{2,0},{3,1},{4,6},{5,7},{6,4},{7,5},{8,10},{9,11},{10,... | collective-permute-start | bytes 393224 | tf_op jit(solution)/shard_map/ppermute | solution.py:45
  63.2 6.5 %collective-permute-start.17 = (bf16[64,1024]{1,0:T(8,128)(2,1)S(1)}, bf16[64,1024]{1,0:T(8,128)(2,1)S(1)}, u32[]{:S(2)}, u32[]{:S(2)}) collective-permute-start(bf16[64,1024]{1,0:T(8,128)(2,1)S(1)} %add_convert_fusion.s0), channel_id=1, source_target_pairs={{0,3},{1,0},{2,1},{3,2},{4,7},{5,4},{6,5},{7,6},{8,11},{9,8},{10,9... | collective-permute-start | bytes 393224 | tf_op jit(solution)/shard_map/ppermute | solution.py:45
  69.7 7.2 %copy-start.9 = (bf16[256,1024]{1,0:T(8,128)(2,1)S(1)}, bf16[256,1024]{1,0:T(8,128)(2,1)}, u32[]{:S(2)}) copy-start(bf16[256,1024]{1,0:T(8,128)(2,1)} %refs_6_.1) | copy-start | bytes 1572868
  72.0 12.2 %all-to-all-start = ((bf16[4,384,128]{2,1,0:T(8,128)(2,1)}), bf16[4,384,128]{2,1,0:T(8,128)(2,1)S(1)}, u32[]{:S(2)}, u32[]{:S(2)}) async-start(bf16[4,384,128]{2,1,0:T(8,128)(2,1)} %get-tuple-element.57), calls=%async_computation | async-start | bytes 786432 | tf_op jit(solution)/shard_map/all_to_all | solution.py:652
  76.9 17.9 %collective-permute-start.21 = (bf16[256,1024]{1,0:T(8,128)(2,1)S(1)}, bf16[256,1024]{1,0:T(8,128)(2,1)S(1)}, u32[]{:S(2)}, u32[]{:S(2)}) collective-permute-start(bf16[256,1024]{1,0:T(8,128)(2,1)S(1)} %copy-done.9), channel_id=1, source_target_pairs={{0,1},{1,2},{2,3},{3,0},{4,7},{5,4},{6,5},{7,6},{8,9},{9,10},{10,1... | collective-permute-start | bytes 1572872 | tf_op jit(solution)/shard_map/ppermute | solution.py:541
  84.3 6.0 %collective-permute-start.23 = (bf16[4,256,128]{2,1,0:T(8,128)(2,1)S(1)}, bf16[4,256,128]{2,1,0:T(8,128)(2,1)S(1)}, u32[]{:S(2)}, u32[]{:S(2)}) collective-permute-start(bf16[4,256,128]{2,1,0:T(8,128)(2,1)S(1)} %slice.14), channel_id=1, source_target_pairs={{0,4},{4,0},{1,5},{5,1},{2,6},{6,2},{3,7},{7,3},{8,12},{12,8},{9,1... | collective-permute-start | bytes 786440 | tf_op jit(solution)/shard_map/ppermute | solution.py:45
  84.5 10.3 %collective-permute-start.22 = (bf16[128,1024]{1,0:T(8,128)(2,1)S(1)}, bf16[128,1024]{1,0:T(8,128)(2,1)S(1)}, u32[]{:S(2)}, u32[]{:S(2)}) collective-permute-start(bf16[128,1024]{1,0:T(8,128)(2,1)S(1)} %constant_dynamic-slice_fusion), channel_id=1, source_target_pairs={{0,2},{1,3},{2,0},{3,1},{4,6},{5,7},{6,4},{7,5},{8,10},{9,11},{10,... | collective-permute-start | bytes 786440 | tf_op jit(solution)/shard_map/ppermute | solution.py:45
  86.5 10.7 %collective-permute-start.18 = (bf16[4,256,128]{2,1,0:T(8,128)(2,1)S(1)}, bf16[4,256,128]{2,1,0:T(8,128)(2,1)S(1)}, u32[]{:S(2)}, u32[]{:S(2)}) collective-permute-start(bf16[4,256,128]{2,1,0:T(8,128)(2,1)S(1)} %slice.14), channel_id=1, source_target_pairs={{0,16},{8,24},{16,0},{24,8},{1,17},{9,25},{17,1},{25,9},{2,18},{10... | collective-permute-start | bytes 786440 | tf_op jit(solution)/shard_map/ppermute | solution.py:45
  88.2 11.8 %collective-permute-start.19 = (bf16[4,256,128]{2,1,0:T(8,128)(2,1)S(1)}, bf16[4,256,128]{2,1,0:T(8,128)(2,1)S(1)}, u32[]{:S(2)}, u32[]{:S(2)}) collective-permute-start(bf16[4,256,128]{2,1,0:T(8,128)(2,1)S(1)} %slice.14), channel_id=1, source_target_pairs={{0,8},{8,16},{16,24},{24,0},{1,9},{9,17},{17,25},{25,1},{2,10},{10... | collective-permute-start | bytes 786440 | tf_op jit(solution)/shard_map/ppermute | solution.py:45
  90.3 11.7 %collective-permute-start.20 = (bf16[4,256,128]{2,1,0:T(8,128)(2,1)S(1)}, bf16[4,256,128]{2,1,0:T(8,128)(2,1)S(1)}, u32[]{:S(2)}, u32[]{:S(2)}) collective-permute-start(bf16[4,256,128]{2,1,0:T(8,128)(2,1)S(1)} %slice.14), channel_id=1, source_target_pairs={{0,24},{8,0},{16,8},{24,16},{1,25},{9,1},{17,9},{25,17},{2,26},{10... | collective-permute-start | bytes 786440 | tf_op jit(solution)/shard_map/ppermute | solution.py:45
  102.1 1.5 %collective-permute-start.25 = (bf16[4,256,128]{2,1,0:T(8,128)(2,1)S(1)}, bf16[4,256,128]{2,1,0:T(8,128)(2,1)S(1)}, u32[]{:S(2)}, u32[]{:S(2)}) collective-permute-start(bf16[4,256,128]{2,1,0:T(8,128)(2,1)S(1)} %collective-permute-done.19.refs_0_), channel_id=1, source_target_pairs={{0,4},{4,0},{1,5},{5,1},{2,6},{6,2},{3,7},{7,3},{8,12},{12,8},{9,1... | collective-permute-start | bytes 786440 | tf_op jit(solution)/shard_map/ppermute | solution.py:45
  102.1 1.9 %collective-permute-start.26 = (bf16[4,256,128]{2,1,0:T(8,128)(2,1)S(1)}, bf16[4,256,128]{2,1,0:T(8,128)(2,1)S(1)}, u32[]{:S(2)}, u32[]{:S(2)}) collective-permute-start(bf16[4,256,128]{2,1,0:T(8,128)(2,1)S(1)} %collective-permute-done.20.refs_2_), channel_id=1, source_target_pairs={{0,4},{4,0},{1,5},{5,1},{2,6},{6,2},{3,7},{7,3},{8,12},{12,8},{9,1... | collective-permute-start | bytes 786440 | tf_op jit(solution)/shard_map/ppermute | solution.py:45
  102.6 6.5 %collective-permute-start.27 = (bf16[256,1024]{1,0:T(8,128)(2,1)S(1)}, bf16[256,1024]{1,0:T(8,128)(2,1)S(1)}, u32[]{:S(2)}, u32[]{:S(2)}) collective-permute-start(bf16[256,1024]{1,0:T(8,128)(2,1)S(1)} %collective-permute-done.21.refs_7_), channel_id=1, source_target_pairs={{0,4},{4,0},{1,5},{5,1},{2,6},{6,2},{3,7},{7,3},{8,12},{12,8},{9,1... | collective-permute-start | bytes 1572872 | tf_op jit(solution)/shard_map/ppermute | solution.py:45
  102.6 6.4 %collective-permute-start.24 = (bf16[4,256,128]{2,1,0:T(8,128)(2,1)S(1)}, bf16[4,256,128]{2,1,0:T(8,128)(2,1)S(1)}, u32[]{:S(2)}, u32[]{:S(2)}) collective-permute-start(bf16[4,256,128]{2,1,0:T(8,128)(2,1)S(1)} %collective-permute-done.18.refs_0_), channel_id=1, source_target_pairs={{0,4},{4,0},{1,5},{5,1},{2,6},{6,2},{3,7},{7,3},{8,12},{12,8},{9,1... | collective-permute-start | bytes 786440 | tf_op jit(solution)/shard_map/ppermute | solution.py:45
  103.1 5.9 %collective-permute-start.28 = (bf16[128,1024]{1,0:T(8,128)(2,1)S(1)}, bf16[128,1024]{1,0:T(8,128)(2,1)S(1)}, u32[]{:S(2)}, u32[]{:S(2)}) collective-permute-start(bf16[128,1024]{1,0:T(8,128)(2,1)S(1)} %collective-permute-done.22.refs_8_), channel_id=1, source_target_pairs={{0,4},{4,0},{1,5},{5,1},{2,6},{6,2},{3,7},{7,3},{8,12},{12,8},{9,1... | collective-permute-start | bytes 786440 | tf_op jit(solution)/shard_map/ppermute | solution.py:45
  109.0 18.7 %copy-start.6 = (f32[1024]{0:T(1024)S(1)}, f32[1024]{0:T(1024)}, u32[]{:S(2)}) copy-start(f32[1024]{0:T(1024)} %param.31) | copy-start | bytes 12292
  127.7 16.2 %copy-start.8 = (bf16[1024,4,256]{2,1,0:T(4,128)(2,1)S(1)}, bf16[1024,4,256]{2,1,0:T(4,128)(2,1)}, u32[]{:S(2)}) copy-start(bf16[1024,4,256]{2,1,0:T(4,128)(2,1)} %param.34) | copy-start | bytes 6291460
  130.7 8.2 %collective-permute-start.29 = (bf16[64,1024]{1,0:T(8,128)(2,1)S(1)}, bf16[64,1024]{1,0:T(8,128)(2,1)S(1)}, u32[]{:S(2)}, u32[]{:S(2)}) collective-permute-start(bf16[64,1024]{1,0:T(8,128)(2,1)S(1)} %get-tuple-element.83), channel_id=1, source_target_pairs={{0,1},{1,2},{2,3},{3,0},{4,5},{5,6},{6,7},{7,4},{8,9},{9,10},{10,1... | collective-permute-start | bytes 393224 | tf_op jit(solution)/shard_map/ppermute | solution.py:45
  131.3 7.6 %collective-permute-start.30 = (bf16[64,1024]{1,0:T(8,128)(2,1)S(1)}, bf16[64,1024]{1,0:T(8,128)(2,1)S(1)}, u32[]{:S(2)}, u32[]{:S(2)}) collective-permute-start(bf16[64,1024]{1,0:T(8,128)(2,1)S(1)} %get-tuple-element.85), channel_id=1, source_target_pairs={{0,2},{1,3},{2,0},{3,1},{4,6},{5,7},{6,4},{7,5},{8,10},{9,11},{10,... | collective-permute-start | bytes 393224 | tf_op jit(solution)/shard_map/ppermute | solution.py:45
  132.7 6.8 %collective-permute-start.31 = (bf16[64,1024]{1,0:T(8,128)(2,1)S(1)}, bf16[64,1024]{1,0:T(8,128)(2,1)S(1)}, u32[]{:S(2)}, u32[]{:S(2)}) collective-permute-start(bf16[64,1024]{1,0:T(8,128)(2,1)S(1)} %get-tuple-element.84), channel_id=1, source_target_pairs={{0,3},{1,0},{2,1},{3,2},{4,7},{5,4},{6,5},{7,6},{8,11},{9,8},{10,9... | collective-permute-start | bytes 393224 | tf_op jit(solution)/shard_map/ppermute | solution.py:45
  139.6 7.7 %collective-permute-start.32 = (bf16[64,1024]{1,0:T(8,128)(2,1)S(1)}, bf16[64,1024]{1,0:T(8,128)(2,1)S(1)}, u32[]{:S(2)}, u32[]{:S(2)}) collective-permute-start(bf16[64,1024]{1,0:T(8,128)(2,1)S(1)} %fusion.3.s0), channel_id=1, source_target_pairs={{0,1},{1,2},{2,3},{3,0},{4,5},{5,6},{6,7},{7,4},{8,9},{9,10},{10,1... | collective-permute-start | bytes 393224 | tf_op jit(solution)/shard_map/ppermute | solution.py:45
  140.7 8.2 %collective-permute-start.33 = (bf16[64,1024]{1,0:T(8,128)(2,1)S(1)}, bf16[64,1024]{1,0:T(8,128)(2,1)S(1)}, u32[]{:S(2)}, u32[]{:S(2)}) collective-permute-start(bf16[64,1024]{1,0:T(8,128)(2,1)S(1)} %fusion.3.s0), channel_id=1, source_target_pairs={{0,2},{1,3},{2,0},{3,1},{4,6},{5,7},{6,4},{7,5},{8,10},{9,11},{10,... | collective-permute-start | bytes 393224 | tf_op jit(solution)/shard_map/ppermute | solution.py:45
  143.8 5.3 %collective-permute-start.34 = (bf16[64,1024]{1,0:T(8,128)(2,1)S(1)}, bf16[64,1024]{1,0:T(8,128)(2,1)S(1)}, u32[]{:S(2)}, u32[]{:S(2)}) collective-permute-start(bf16[64,1024]{1,0:T(8,128)(2,1)S(1)} %fusion.3.s0), channel_id=1, source_target_pairs={{0,3},{1,0},{2,1},{3,2},{4,7},{5,4},{6,5},{7,6},{8,11},{9,8},{10,9... | collective-permute-start | bytes 393224 | tf_op jit(solution)/shard_map/ppermute | solution.py:45
